TPU v7x, 256 devices: a whole 4x4x8 slice. The times are simulated.
256 devices in a mesh: row: 16 (over y_lo, z), col: 16 (over x, y_hi, core).
Axes of the slice: x: 4, y: 4 (y_hi: 2, y_lo: 2; y = y_hi * 2 + y_lo), z: 8, core: 2. Of those that a mesh axis runs over, the one named last changes fastest.
Arguments:
- object_field: float32 [2, 2, 4096, 4096], P(None, None, 'row', 'col'), may hold values from -4 to 4
- probe: float32 [2, 128, 128], replicated, may hold values from -6 to 6
- intensity: float32 [16, 128, 128, 128], P('row', 'col'), may hold values from 0 to 2
- offset_row: int32 [16, 128], P('row', 'col'), may hold values from 0 to 255
- offset_col: int32 [16, 128], P('row', 'col'), may hold values from 0 to 255
- live: int32 [16, 16], P('row', 'col'), may hold values from 1 to 8, as said below
Outputs:
- new_object: float32 [2, 2, 4096, 4096], P(None, None, 'row', 'col')
- new_probe: float32 [2, 128, 128], replicated
Inputs may be any that keep to these rules, and one draw needn't show every extreme that they name: Device (a, b) uses its first live[a, b] slots; at least one device uses all 8.
All inputs are finite; a program needn't handle non-finite values.
Results may differ from a plain program's by a relative error of at most 0.0003.
Values sent between devices are 32-bit elements; how exact they have to be, the bound alone decides.
No kernel may reach another device: no remote copies, remote signals or barrier semaphores. Data moves between devices by JAX's collectives and lax.ppermute only.
A program may use at most 64 MiB of HBM per device.

v0:
```python
import math

import jax
import jax.numpy as jnp
from jax import lax
from jax.sharding import PartitionSpec as P

STEP_OBJECT = 0.03
STEP_PROBE = 2.0
FRESNEL_PHASE = 60.0


def with_halo(block, sides, width):
    for axis, dim in sides:
        count = lax.axis_size(axis)
        forward = [(i, i + 1) for i in range(count - 1)]
        backward = [(target, source) for source, target in forward]
        low = lax.ppermute(
            lax.slice_in_dim(block, block.shape[dim] - width, None, axis=dim), axis, forward
        )
        high = lax.ppermute(lax.slice_in_dim(block, 0, width, axis=dim), axis, backward)
        block = jnp.concatenate([low, block, high], axis=dim)
    return block


def make_tables(width):
    index = jnp.arange(width, dtype=jnp.int32)
    product = index[:, None] * index[None, :] % width
    angle = 2.0 * math.pi / width * product.astype(jnp.float32)
    scale = 1.0 / math.sqrt(width)
    four_re = jnp.cos(angle) * scale
    four_im = -jnp.sin(angle) * scale
    freq = jnp.where(index < width // 2, index, index - width).astype(jnp.float32) / width
    phase = -FRESNEL_PHASE * (freq[:, None] ** 2 + freq[None, :] ** 2)
    return (four_re, four_im, jnp.cos(phase), jnp.sin(phase))


def transform(wave_re, wave_im, four_re, four_im):
    high = lax.Precision.HIGHEST
    right_re = jnp.einsum("kab,bc->kac", wave_re, four_re, precision=high) - jnp.einsum(
        "kab,bc->kac", wave_im, four_im, precision=high
    )
    right_im = jnp.einsum("kab,bc->kac", wave_re, four_im, precision=high) + jnp.einsum(
        "kab,bc->kac", wave_im, four_re, precision=high
    )
    out_re = jnp.einsum("ab,kbc->kac", four_re, right_re, precision=high) - jnp.einsum(
        "ab,kbc->kac", four_im, right_im, precision=high
    )
    out_im = jnp.einsum("ab,kbc->kac", four_im, right_re, precision=high) + jnp.einsum(
        "ab,kbc->kac", four_re, right_im, precision=high
    )
    return (out_re, out_im)


def window_grads(windows, probe, measured, active, tabs):
    four_re, four_im, prop_re, prop_im = tabs
    probe_re, probe_im = (probe[0], probe[1])
    first_re, first_im = (windows[:, 0, 0], windows[:, 0, 1])
    second_re, second_im = (windows[:, 1, 0], windows[:, 1, 1])
    wave_re = probe_re * first_re - probe_im * first_im
    wave_im = probe_re * first_im + probe_im * first_re
    spec_re, spec_im = transform(wave_re, wave_im, four_re, four_im)
    spec_re, spec_im = (
        spec_re * prop_re - spec_im * prop_im,
        spec_re * prop_im + spec_im * prop_re,
    )
    mid_re, mid_im = transform(spec_re, spec_im, four_re, -four_im)
    exit_re = mid_re * second_re - mid_im * second_im
    exit_im = mid_re * second_im + mid_im * second_re
    far_re, far_im = transform(exit_re, exit_im, four_re, four_im)
    weight = 2.0 * (far_re * far_re + far_im * far_im - measured) * active[:, None, None]
    chi_re, chi_im = transform(weight * far_re, weight * far_im, four_re, -four_im)
    back_re = second_re * chi_re + second_im * chi_im
    back_im = second_re * chi_im - second_im * chi_re
    grad2_re = mid_re * chi_re + mid_im * chi_im
    grad2_im = mid_re * chi_im - mid_im * chi_re
    spec_re, spec_im = transform(back_re, back_im, four_re, four_im)
    spec_re, spec_im = (
        spec_re * prop_re + spec_im * prop_im,
        spec_im * prop_re - spec_re * prop_im,
    )
    down_re, down_im = transform(spec_re, spec_im, four_re, -four_im)
    grad1_re = probe_re * down_re + probe_im * down_im
    grad1_im = probe_re * down_im - probe_im * down_re
    probe_gre = jnp.sum(first_re * down_re + first_im * down_im, axis=0)
    probe_gim = jnp.sum(first_re * down_im - first_im * down_re, axis=0)
    grads = jnp.stack([jnp.stack([grad1_re, grad1_im], 1), jnp.stack([grad2_re, grad2_im], 1)], 1)
    return (grads, jnp.stack([probe_gre, probe_gim]))


def squeeze_rim(grid, axis, half, tile):
    width = 2 * half
    return jnp.concatenate(
        [
            lax.slice_in_dim(grid, 0, half, axis=axis),
            lax.slice_in_dim(grid, width, tile, axis=axis),
            lax.slice_in_dim(grid, tile + half, tile + width, axis=axis),
        ],
        axis=axis,
    )


def on_device(object_field, probe, intensity, offset_row, offset_col, live):
    tile = object_field.shape[2]
    width = probe.shape[1]
    half = width // 2
    slot_count = offset_row.shape[1]
    extended = with_halo(object_field, (("row", 2), ("col", 3)), half)
    row_start = offset_row[0]
    col_start = offset_col[0]
    active = (jnp.arange(slot_count, dtype=jnp.int32) < live[0, 0]).astype(jnp.float32)
    windows = jax.vmap(
        lambda rstart, cstart: lax.dynamic_slice(
            extended, (jnp.int32(0), jnp.int32(0), rstart, cstart), (2, 2, width, width)
        )
    )(row_start, col_start)
    grads, probe_part = window_grads(windows, probe, intensity[0], active, make_tables(width))

    def add_slot(slot, accum_grad):
        start = (jnp.int32(0), jnp.int32(0), row_start[slot], col_start[slot])
        current = lax.dynamic_slice(accum_grad, start, (2, 2, width, width))
        return lax.dynamic_update_slice(accum_grad, current + grads[slot], start)

    grad_ext = lax.fori_loop(0, slot_count, add_slot, jnp.zeros(extended.shape, jnp.float32))
    row_set = squeeze_rim(grad_ext[:, :, :, half : tile + half], 2, half, tile)
    col_set = squeeze_rim(grad_ext[:, :, half : tile + half, :], 3, half, tile)
    corner_set = squeeze_rim(squeeze_rim(grad_ext, 2, half, tile), 3, half, tile)
    packed = jnp.concatenate([row_set, col_set, corner_set], axis=0)
    returned = with_halo(packed, (("row", 2), ("col", 3)), half)
    from_rows = returned[0:2]
    from_cols = returned[2:4]
    from_corner = returned[4:6]
    inner = grad_ext[:, :, half : tile + half, half : tile + half]
    inner = inner.at[:, :, :half, :].add(from_rows[:, :, :half, half : tile + half])
    inner = inner.at[:, :, tile - half :, :].add(from_rows[:, :, tile + half :, half : tile + half])
    inner = inner.at[:, :, :, :half].add(from_cols[:, :, half : tile + half, :half])
    inner = inner.at[:, :, :, tile - half :].add(from_cols[:, :, half : tile + half, tile + half :])
    inner = inner.at[:, :, :half, :half].add(from_corner[:, :, :half, :half])
    inner = inner.at[:, :, :half, tile - half :].add(from_corner[:, :, :half, tile + half :])
    inner = inner.at[:, :, tile - half :, :half].add(from_corner[:, :, tile + half :, :half])
    inner = inner.at[:, :, tile - half :, tile - half :].add(
        from_corner[:, :, tile + half :, tile + half :]
    )
    probe_total = lax.psum(probe_part, ("row", "col"))
    count_all = slot_count * lax.axis_size("row") * lax.axis_size("col")
    new_object = object_field - STEP_OBJECT * inner
    new_probe = probe - STEP_PROBE / count_all * probe_total
    return (new_object, new_probe)


def solution(mesh):
    placed = (
        P(None, None, "row", "col"),
        P(),
        P("row", "col", None, None),
        P("row", "col"),
        P("row", "col"),
        P("row", "col"),
    )
    return jax.shard_map(
        on_device,
        mesh=mesh,
        in_specs=placed,
        out_specs=(P(None, None, "row", "col"), P()),
        check_vma=False,
    )
```

profile of v0, /device:TPU:1, one launch (start us, length us, event | category | flops | bytes accessed | tf_op | source)
XLA Modules:
  0.0 537.0 jit_solution(3753956804749507980)
XLA Ops:
  7.2 1.6 copy.140
  9.0 1.3 collective-permute-start.1
  10.3 5.0 collective-permute-start
  15.5 7.6 %collective-permute-done.1 = f32[2,2,64,256]{2,3,1,0:T(8,128)S(1)} collective-permute-done((f32[2,2,64,256]{2,3,1,0:T(8,128)S(1)}, f32[2,2,64,256]{2,3,1,0:T(8,128)S(1)}, u32[]{:S(2)}, u32[]{:S(2)}) %collective-permute-start.1) | collective-permute-done | bytes 262176 | tf_op jit(solution)/shard_map/ppermute | solution.py:21
  24.0 1.2 pad_maximum_fusion.12
  25.3 5.3 collective-permute-start.3
  30.6 4.7 collective-permute-start.2
  35.4 2.0 copy.173
  38.6 3.4 collective-permute-done.3
  42.8 3.5 pad_maximum_fusion.1
  46.3 27.8 %while.23 = (s32[]{:T(128)}, f32[2,2,384,384]{2,3,1,0:T(8,128)}, s32[8,4]{0,1:T(4,128)S(1)}, f32[8,2,2,128,128]{3,4,0,2,1:T(8,128)S(1)}, s32[]{:T(128)}) while((s32[]{:T(128)}, f32[2,2,384,384]{2,3,1,0:T(8,128)}, s32[8,4]{0,1:T(4,128)S(1)}, f32[8,2,2,128,128]{3,4,0,2,1:T(8,128)S(1)}, s32[]{:T(128)}) %tuple.110), condition=%wide.while_cond.8, body=%wide.while_body.8.sunk | while | flops 2 | bytes 2097285 | solution.py:113
  46.9 2.4 constant_dynamic-slice_fusion.8
  50.4 2.4 constant_dynamic-slice_fusion.8
  53.8 2.4 constant_dynamic-slice_fusion.8
  57.2 2.4 constant_dynamic-slice_fusion.8
  60.6 2.4 constant_dynamic-slice_fusion.8
  64.0 2.4 constant_dynamic-slice_fusion.8
  67.4 2.4 constant_dynamic-slice_fusion.8
  70.8 2.4 constant_dynamic-slice_fusion.8
  74.1 1.2 fusion.102
  75.3 1.2 fusion.67
  76.5 1.2 convolution_subtract_fusion.11
  79.9 1.2 convolution_add_fusion.11
  83.4 1.2 fusion.30
  84.6 1.4 fusion.29
  86.0 1.2 convolution_subtract_fusion.9
  89.5 1.2 convolution_add_fusion.9
  97.5 1.3 fusion.58
  109.1 1.5 fusion.4
  110.7 1.2 fusion.18
  121.0 1.4 fusion.32
  122.4 1.2 fusion.31
  123.6 1.2 convolution_subtract_fusion.1
  127.1 1.2 convolution_add_fusion.1
  129.5 1.2 fusion.22
  130.8 1.5 pad_maximum_fusion.2
  132.5 77.6 %while.22 = (s32[]{:T(128)}, f32[2,2,384,384]{3,2,1,0:T(8,128)S(1)}, s32[8]{0:T(128)S(1)}, s32[8]{0:T(128)S(1)}, f32[8,2,2,128,128]{3,4,0,2,1:T(8,128)}, /*index=5*/s32[]{:T(128)}, s32[]{:T(128)}, s32[]{:T(128)}) while((s32[]{:T(128)}, f32[2,2,384,384]{3,2,1,0:T(8,128)S(1)}, s32[8]{0:T(128)S(1)}, s32[8]{0:T(128)S(1)}, ...), condition=%wide.region_1.2_spmd, body=%wide.region_0.1_spmd.sunk | while | flops 65544 | bytes 2359497 | solution.py:124
  138.8 3.2 dynamic_update_slice.8
  148.4 3.2 dynamic_update_slice.8
  157.9 3.4 dynamic_update_slice.8
  167.7 3.3 dynamic_update_slice.8
  177.3 3.4 dynamic_update_slice.8
  187.1 3.4 dynamic_update_slice.8
  196.9 3.2 dynamic_update_slice.8
  206.5 3.4 dynamic_update_slice.8
  211.7 3.5 collective-permute-start.4
  215.3 1.3 collective-permute-start.5
  216.6 11.3 %collective-permute-done.4 = f32[6,2,64,256]{3,2,1,0:T(8,128)S(1)} collective-permute-done((f32[6,2,64,256]{3,2,1,0:T(8,128)S(1)}, f32[6,2,64,256]{3,2,1,0:T(8,128)S(1)}, u32[]{:S(2)}, u32[]{:S(2)}) %collective-permute-start.4) | collective-permute-done | bytes 786464 | tf_op jit(solution)/shard_map/ppermute | solution.py:18
  227.8 4.1 collective-permute-done.5
  232.0 2.3 pad_maximum_fusion
  234.2 2.9 fusion.370
  237.2 2.8 copy.199
  240.0 7.6 %collective-permute-start.6 = (f32[6,2,384,64]{2,3,1,0:T(8,128)}, f32[6,2,384,64]{2,3,1,0:T(8,128)}, u32[]{:S(2)}, u32[]{:S(2)}) collective-permute-start(f32[6,2,384,64]{2,3,1,0:T(8,128)} %copy.199), channel_id=1, source_target_pairs={{0,1},{1,2},{2,3},{3,4},{4,5},{5,6},{6,7},{7,8},{8,9},{9,10},{10,1... | collective-permute-start | bytes 3538952 | tf_op jit(solution)/shard_map/ppermute | solution.py:18
  248.4 2.8 copy.201
  251.3 1.9 collective-permute-start.7
  254.8 248.7 %all-reduce.2.cloned.1.call-done = f32[2,128,128]{1,2,0:T(8,128)} async-done(((f32[2,128,128]{1,2,0:T(8,128)}), f32[2,128,128]{1,2,0:T(8,128)}) %all-reduce.2.cloned.1.call-update) | async-done | bytes 131088 | tf_op jit(solution)/shard_map/psum | solution.py:144
  503.6 1.6 multiply_subtract_fusion.3
  505.1 1.7 copy.208
  510.3 2.3 scatter-add.30
  515.3 2.4 scatter-add.31
  517.7 1.2 scatter-add.34
  520.1 1.9 add_select_fusion
  522.1 3.5 scatter-add.35
  526.8 2.0 scatter-add.39
  (190 shorter events, 79.5 us)
Async XLA Ops:
  7.2 8.2 %copy-start.8 = (s32[1,8]{1,0:T(1,128)S(1)}, s32[1,8]{1,0:T(1,128)}, u32[]{:S(2)}) copy-start(s32[1,8]{1,0:T(1,128)} %param.27) | copy-start | bytes 100
  7.2 8.2 %copy-start.9 = (s32[1,8]{1,0:T(1,128)S(1)}, s32[1,8]{1,0:T(1,128)}, u32[]{:S(2)}) copy-start(s32[1,8]{1,0:T(1,128)} %param.28) | copy-start | bytes 100
  7.2 8.3 %copy-start.6 = (f32[2,128,128]{2,1,0:T(8,128)S(1)}, f32[2,128,128]{2,1,0:T(8,128)}, u32[]{:S(2)}) copy-start(f32[2,128,128]{2,1,0:T(8,128)} %param.25) | copy-start | bytes 393220
  7.2 496.4 %all-reduce.2.cloned.1.call-start = ((), (), s32[]{:S(2)}) async-start(), calls=%async_computation | async-start | bytes 262144 | tf_op jit(solution)/shard_map/psum | solution.py:144
  9.0 14.1 %collective-permute-start.1 = (f32[2,2,64,256]{2,3,1,0:T(8,128)S(1)}, f32[2,2,64,256]{2,3,1,0:T(8,128)S(1)}, u32[]{:S(2)}, u32[]{:S(2)}) collective-permute-start(f32[2,2,64,256]{2,3,1,0:T(8,128)S(1)} %get-tuple-element.283), channel_id=1, source_target_pairs={{16,0},{32,16},{48,32},{64,48},{80,64},{96,80},{112,96},{128,112},... | collective-permute-start | bytes 786440 | tf_op jit(solution)/shard_map/ppermute | solution.py:21
  10.3 13.7 %collective-permute-start = (f32[2,2,64,256]{2,3,1,0:T(8,128)S(1)}, f32[2,2,64,256]{2,3,1,0:T(8,128)S(1)}, u32[]{:S(2)}, u32[]{:S(2)}) collective-permute-start(f32[2,2,64,256]{2,3,1,0:T(8,128)S(1)} %get-tuple-element.282), channel_id=1, source_target_pairs={{0,16},{16,32},{32,48},{48,64},{64,80},{80,96},{96,112},{112,128},... | collective-permute-start | bytes 786440 | tf_op jit(solution)/shard_map/ppermute | solution.py:18
  23.1 0.9 copy-start.1
  24.0 1.2 copy-start.2
  25.3 16.7 %collective-permute-start.3 = (f32[2,2,384,64]{2,3,1,0:T(8,128)}, f32[2,2,384,64]{2,3,1,0:T(8,128)}, u32[]{:S(2)}, u32[]{:S(2)}) collective-permute-start(f32[2,2,384,64]{2,3,1,0:T(8,128)} %get-tuple-element.267), channel_id=1, source_target_pairs={{1,0},{2,1},{3,2},{4,3},{5,4},{6,5},{7,6},{8,7},{9,8},{10,9},{11,1... | collective-permute-start | bytes 1179656 | tf_op jit(solution)/shard_map/ppermute | solution.py:21
  30.6 12.2 %collective-permute-start.2 = (f32[2,2,384,64]{2,3,1,0:T(8,128)}, f32[2,2,384,64]{2,3,1,0:T(8,128)}, u32[]{:S(2)}, u32[]{:S(2)}) collective-permute-start(f32[2,2,384,64]{2,3,1,0:T(8,128)} %get-tuple-element.266), channel_id=1, source_target_pairs={{0,1},{1,2},{2,3},{3,4},{4,5},{5,6},{6,7},{7,8},{8,9},{9,10},{10,1... | collective-permute-start | bytes 1179656 | tf_op jit(solution)/shard_map/ppermute | solution.py:18
  96.4 4.8 copy-start.3
  211.7 16.1 %collective-permute-start.4 = (f32[6,2,64,256]{3,2,1,0:T(8,128)S(1)}, f32[6,2,64,256]{3,2,1,0:T(8,128)S(1)}, u32[]{:S(2)}, u32[]{:S(2)}) collective-permute-start(f32[6,2,64,256]{3,2,1,0:T(8,128)S(1)} %get-tuple-element.253), channel_id=1, source_target_pairs={{0,16},{16,32},{32,48},{48,64},{64,80},{80,96},{96,112},{112,128},... | collective-permute-start | bytes 2359304 | tf_op jit(solution)/shard_map/ppermute | solution.py:18
  215.3 16.7 %collective-permute-start.5 = (f32[6,2,64,256]{3,2,1,0:T(8,128)S(1)}, f32[6,2,64,256]{3,2,1,0:T(8,128)S(1)}, u32[]{:S(2)}, u32[]{:S(2)}) collective-permute-start(f32[6,2,64,256]{3,2,1,0:T(8,128)S(1)} %get-tuple-element.252), channel_id=1, source_target_pairs={{16,0},{32,16},{48,32},{64,48},{80,64},{96,80},{112,96},{128,112},... | collective-permute-start | bytes 2359304 | tf_op jit(solution)/shard_map/ppermute | solution.py:21
  227.8 6.4 %copy-start.4 = (f32[6,2,64,256]{3,2,1,0:T(8,128)}, f32[6,2,64,256]{3,2,1,0:T(8,128)S(1)}, u32[]{:S(2)}) copy-start(f32[6,2,64,256]{3,2,1,0:T(8,128)S(1)} %collective-permute-done.4) | copy-start | bytes 2359300
  232.0 2.3 copy-start.5
  237.2 10.4 %copy-start.7 = (f32[2,128,128]{2,1,0:T(8,128)S(1)}, f32[2,128,128]{2,1,0:T(8,128)}, u32[]{:S(2)}) copy-start(f32[2,128,128]{2,1,0:T(8,128)} %param.25) | copy-start | bytes 393220
  237.2 10.6 %copy-start.10 = (s32[4]{0:T(128)S(1)}, s32[4]{0:T(128)}, u32[]{:S(2)}) copy-start(s32[4]{0:T(128)} %constant.288.clone.1) | copy-start | bytes 52
  240.0 268.8 %collective-permute-start.6 = (f32[6,2,384,64]{2,3,1,0:T(8,128)}, f32[6,2,384,64]{2,3,1,0:T(8,128)}, u32[]{:S(2)}, u32[]{:S(2)}) collective-permute-start(f32[6,2,384,64]{2,3,1,0:T(8,128)} %copy.199), channel_id=1, source_target_pairs={{0,1},{1,2},{2,3},{3,4},{4,5},{5,6},{6,7},{7,8},{8,9},{9,10},{10,1... | collective-permute-start | bytes 3538952 | tf_op jit(solution)/shard_map/ppermute | solution.py:18
  251.3 261.3 %collective-permute-start.7 = (f32[6,2,384,64]{2,3,1,0:T(8,128)}, f32[6,2,384,64]{2,3,1,0:T(8,128)}, u32[]{:S(2)}, u32[]{:S(2)}) collective-permute-start(f32[6,2,384,64]{2,3,1,0:T(8,128)} %copy.201), channel_id=1, source_target_pairs={{1,0},{2,1},{3,2},{4,3},{5,4},{6,5},{7,6},{8,7},{9,8},{10,9},{11,1... | collective-permute-start | bytes 3538952 | tf_op jit(solution)/shard_map/ppermute | solution.py:21
  515.3 13.5 %copy-start = (f32[2,2,256,256]{3,2,1,0:T(8,128)S(1)}, f32[2,2,256,256]{3,2,1,0:T(8,128)}, u32[]{:S(2)}) copy-start(f32[2,2,256,256]{3,2,1,0:T(8,128)} %param.24) | copy-start | bytes 3145732
Sparse Core Ops, SparseCore 0:
  254.0 249.5 all-reduce.1
where the time goes:
time: 542 us; the launch traced here: 537 us
  waiting for transfers between devices  277 us (51%)
  local copies, waits for them, and re-layouts  106 us (20%)
  matrix products  56.2 us (10%)
  loops' own time  32.5 us (6%)
  starting transfers between devices  30.7 us (6%)
  other arithmetic  19.2 us (4%)
  between operations  15.8 us (3%)
    psum x1, waiting for transfers between devices, on_device(): probe_total = lax.psum(probe_part, ('row', 'col'))  249 us
    another operation x1, loops' own time, on_device(): lax.fori_loop(0, slot_count, add_slot, jnp.zeros(extended.shape, jnp.floa...  31.7 us
    gather x48, local copies, waits for them, and re-layouts  27 us
    dynamic_update_slice x8, local copies, waits for them, and re-layouts, add_slot(): return lax.dynamic_update_slice(accum_grad, current + grads[slot], start)  26.5 us
    ppermute x4, starting transfers between devices, with_halo(): lax.ppermute(lax.slice_in_dim(block, block.shape[dim] - width, None, axis...  20.9 us
    ppermute x4, waiting for transfers between devices, with_halo(): lax.ppermute(lax.slice_in_dim(block, 0, width, axis=dim), axis, backward)  15.1 us
    ppermute x4, waiting for transfers between devices, with_halo(): lax.ppermute(lax.slice_in_dim(block, block.shape[dim] - width, None, axis...  13 us
  transfers between devices with their start and end apart: 9, of which 7 were waited for; matrix products, arithmetic and copies ran while one was open for 3% of the time, Pallas kernels for 0%

commit v1 on v0

v1 whole, which is shorter than its diff:
```python
import functools
import math

import jax
import jax.numpy as jnp
import ml_dtypes
import numpy as np
from jax import lax
from jax.experimental import pallas as pl
from jax.experimental.pallas import tpu as pltpu
from jax.sharding import PartitionSpec as P

STEP_OBJECT = 0.03
STEP_PROBE = 2.0
FRESNEL_PHASE = 60.0
LANES = 128
BOTH = ("row", "col")
GRANT = 48 * 1024 * 1024


def split_table(table):
    high = table.astype(ml_dtypes.bfloat16)
    low = (table - high.astype(np.float64)).astype(ml_dtypes.bfloat16)
    return high, low


def make_tables(width):
    index = np.arange(width)
    four = np.exp(-2j * math.pi * (np.outer(index, index) % width) / width) / math.sqrt(width)
    freq = np.where(index < width // 2, index, index - width) / width
    hop = np.conj(four) @ np.diag(np.exp(-1j * FRESNEL_PHASE * freq**2)) @ four
    forms = []
    for table in (hop, four):
        forms.append(np.block([[table.real, table.imag], [-table.imag, table.real]]))
        forms.append(np.block([[table.real, -table.imag], [table.imag, table.real]]))
    pairs = [split_table(form) for form in forms]
    return np.stack([np.stack(pair) for pair in pairs])


def split(value):
    high = value.astype(jnp.bfloat16)
    low = (value - high.astype(jnp.float32)).astype(jnp.bfloat16)
    return high, low


def mul3(left, right):
    dot = functools.partial(jnp.dot, preferred_element_type=jnp.float32)
    return dot(left[0], right[0]) + (dot(left[1], right[0]) + dot(left[0], right[1]))


def two_sided(tabs_ref, right, left, real, imag):
    width = real.shape[1]
    field = split(jnp.concatenate([real, imag], axis=1))
    half = mul3(field, (tabs_ref[right, 0], tabs_ref[right, 1]))
    real, imag = half[:, :width], half[:, width:]
    field = jnp.concatenate(
        [
            jnp.concatenate([real[:width], real[width:]], axis=1),
            jnp.concatenate([imag[:width], imag[width:]], axis=1),
        ],
        axis=0,
    )
    full = mul3((tabs_ref[left, 0], tabs_ref[left, 1]), split(field))
    real = jnp.concatenate([full[:width, :width], full[:width, width:]], axis=0)
    imag = jnp.concatenate([full[width:, :width], full[width:, width:]], axis=0)
    return real, imag


def pack_kernel(obj_ref, low_ref, high_ref, *corner_refs):
    half = LANES // 2
    first = lax.broadcasted_iota(jnp.int32, (obj_ref.shape[2], LANES), 1) < half
    tile = obj_ref.shape[2]
    for piece in range(2):
        low = jnp.where(
            first, obj_ref[piece, 0, :, :LANES], pltpu.roll(obj_ref[piece, 1, :, :LANES], half, 1)
        )
        high = jnp.where(
            first, pltpu.roll(obj_ref[piece, 0, :, LANES:], half, 1), obj_ref[piece, 1, :, LANES:]
        )
        low_ref[piece] = low
        high_ref[piece] = high
        corner_refs[0][piece] = low[:half]
        corner_refs[1][piece] = high[:half]
        corner_refs[2][piece] = low[tile - half :]
        corner_refs[3][piece] = high[tile - half :]


def place_window(row_ref, col_ref, slot):
    col = col_ref[0, slot] + LANES // 2
    return row_ref[0, slot], col // LANES, lax.rem(col, LANES)


def step_kernel(
    row_ref, col_ref, live_ref, obj_ref, up_ref, down_ref, low_ref, high_ref,
    ul_ref, uh_ref, dl_ref, dh_ref, probe_ref, measured_ref, tabs_ref,
    new_ref, gup_ref, gdown_ref, glow_ref, ghigh_ref, gul_ref, guh_ref, gdl_ref, gdh_ref, gp_ref,
    ext, grad,
):
    width = probe_ref.shape[1]
    tile = obj_ref.shape[2]
    half = width // 2
    grad[...] = jnp.zeros_like(grad)
    gp_ref[...] = jnp.zeros_like(gp_ref)
    for piece in range(2):
        for part in range(2):
            for block in range(2):
                cols = pl.ds(block * LANES, LANES)
                ext[piece, part, 1 + block, :half] = up_ref[piece, part, :, cols]
                ext[piece, part, 1 + block, half : half + tile] = obj_ref[piece, part, :, cols]
                ext[piece, part, 1 + block, half + tile :] = down_ref[piece, part, :, cols]
            for block, sides in ((0, (ul_ref, low_ref, dl_ref)), (3, (uh_ref, high_ref, dh_ref))):
                for ref, start in zip(sides, (0, half, half + tile)):
                    strip = ref[piece]
                    if (block == 0) == (part == 0):
                        strip = pltpu.roll(strip, half, 1)
                    ext[piece, part, block, start : start + strip.shape[0]] = strip
    lane = lax.broadcasted_iota(jnp.int32, (width, LANES), 1)

    def window(slot, piece):
        row, block, shift = place_window(row_ref, col_ref, slot)
        back = lax.rem(LANES - shift, LANES)
        keep = lane < LANES - shift
        parts = []
        for part in range(2):
            near = pltpu.roll(ext[piece, part, block, pl.ds(row, width), :], back, 1)
            far = pltpu.roll(ext[piece, part, block + 1, pl.ds(row, width), :], back, 1)
            parts.append(jnp.where(keep, near, far))
        return parts

    def deposit(slot, piece, values):
        row, block, shift = place_window(row_ref, col_ref, slot)
        keep = lane >= shift
        for part in range(2):
            value = pltpu.roll(values[part], shift, 1)
            grad[piece, part, block, pl.ds(row, width), :] += jnp.where(keep, value, 0.0)
            grad[piece, part, block + 1, pl.ds(row, width), :] += jnp.where(keep, 0.0, value)

    def pair(index, _):
        slots = (2 * index, 2 * index + 1)
        firsts = [window(slot, 0) for slot in slots]
        seconds = [window(slot, 1) for slot in slots]
        first_re, first_im = (jnp.concatenate([f[p] for f in firsts], axis=0) for p in range(2))
        second_re, second_im = (jnp.concatenate([f[p] for f in seconds], axis=0) for p in range(2))
        probe_re = jnp.concatenate([probe_ref[0], probe_ref[0]], axis=0)
        probe_im = jnp.concatenate([probe_ref[1], probe_ref[1]], axis=0)
        wave_re = probe_re * first_re - probe_im * first_im
        wave_im = probe_re * first_im + probe_im * first_re
        mid_re, mid_im = two_sided(tabs_ref, 0, 1, wave_re, wave_im)
        exit_re = mid_re * second_re - mid_im * second_im
        exit_im = mid_re * second_im + mid_im * second_re
        far_re, far_im = two_sided(tabs_ref, 2, 3, exit_re, exit_im)
        weights = []
        for place, slot in enumerate(slots):
            rows = slice(place * width, (place + 1) * width)
            active = jnp.where(slot < live_ref[0, 0], 2.0, 0.0)
            power = far_re[rows] * far_re[rows] + far_im[rows] * far_im[rows]
            weights.append((power - measured_ref[slot]) * active)
        weight = jnp.concatenate(weights, axis=0)
        chi_re, chi_im = two_sided(tabs_ref, 3, 2, weight * far_re, weight * far_im)
        back_re = second_re * chi_re + second_im * chi_im
        back_im = second_re * chi_im - second_im * chi_re
        grad_re = mid_re * chi_re + mid_im * chi_im
        grad_im = mid_re * chi_im - mid_im * chi_re
        for place, slot in enumerate(slots):
            rows = slice(place * width, (place + 1) * width)
            deposit(slot, 1, (grad_re[rows], grad_im[rows]))
        down_re, down_im = two_sided(tabs_ref, 1, 0, back_re, back_im)
        grad_re = probe_re * down_re + probe_im * down_im
        grad_im = probe_re * down_im - probe_im * down_re
        for place, slot in enumerate(slots):
            rows = slice(place * width, (place + 1) * width)
            deposit(slot, 0, (grad_re[rows], grad_im[rows]))
        sum_re = first_re * down_re + first_im * down_im
        sum_im = first_re * down_im - first_im * down_re
        gp_ref[0] += sum_re[:width] + sum_re[width:]
        gp_ref[1] += sum_im[:width] + sum_im[width:]
        return 0

    lax.fori_loop(0, row_ref.shape[1] // 2, pair, 0)
    lower = lax.broadcasted_iota(jnp.int32, (half, LANES), 1) < half
    inner = lax.broadcasted_iota(jnp.int32, (tile, LANES), 1) < half
    for piece in range(2):
        for part in range(2):
            for block in range(2):
                cols = pl.ds(block * LANES, LANES)
                gup_ref[piece, part, :, cols] = grad[piece, part, 1 + block, :half]
                gdown_ref[piece, part, :, cols] = grad[piece, part, 1 + block, half + tile :]
                new_ref[piece, part, :, cols] = (
                    obj_ref[piece, part, :, cols]
                    - STEP_OBJECT * grad[piece, part, 1 + block, half : half + tile]
                )
        for block, outs in ((0, (gul_ref, glow_ref, gdl_ref)), (3, (guh_ref, ghigh_ref, gdh_ref))):
            for ref, start in zip(outs, (0, half, half + tile)):
                size = ref.shape[1]
                mask = inner if size == tile else lower
                real = grad[piece, 0, block, start : start + size]
                imag = grad[piece, 1, block, start : start + size]
                if block == 0:
                    real = pltpu.roll(real, half, 1)
                else:
                    imag = pltpu.roll(imag, half, 1)
                ref[piece] = jnp.where(mask, real, imag)


def finish_kernel(
    part_ref, up_ref, down_ref, low_ref, high_ref, ul_ref, uh_ref, dl_ref, dh_ref, probe_ref, sum_ref,
    new_ref, newp_ref, *, scale,
):
    tile = part_ref.shape[2]
    half = up_ref.shape[2]
    first = lax.broadcasted_iota(jnp.int32, (half, LANES), 1) < half
    newp_ref[...] = probe_ref[...] - scale * sum_ref[...]
    for piece in range(2):
        for part in range(2):
            for start in range(0, tile, half):
                rows = slice(start, start + half)
                for block in range(2):
                    cols = slice(block * LANES, (block + 1) * LANES)
                    strips = [(low_ref, high_ref)[block][piece, rows]]
                    total = None
                    if start == 0:
                        strips.append((ul_ref, uh_ref)[block][piece])
                        total = up_ref[piece, part, :, cols]
                    if start == tile - half:
                        strips.append((dl_ref, dh_ref)[block][piece])
                        total = down_ref[piece, part, :, cols]
                    strip = strips[0] if len(strips) == 1 else strips[0] + strips[1]
                    if block != part:
                        strip = pltpu.roll(strip, half, 1)
                    strip = jnp.where(first == (block == 0), strip, 0.0)
                    total = strip if total is None else total + strip
                    new_ref[piece, part, rows, cols] = (
                        part_ref[piece, part, rows, cols] - STEP_OBJECT * total
                    )


def vmem(count):
    return [pl.BlockSpec(memory_space=pltpu.VMEM)] * count


def smem(count):
    return [pl.BlockSpec(memory_space=pltpu.SMEM)] * count


def array(*shape):
    return jax.ShapeDtypeStruct(shape, jnp.float32)


def moves(rows, cols, row_step, col_step):
    pairs = []
    for a in range(rows):
        for b in range(cols):
            if 0 <= a + row_step < rows and 0 <= b + col_step < cols:
                pairs.append((a * cols + b, (a + row_step) * cols + b + col_step))
    return pairs


STEPS = ((-1, 0), (1, 0), (0, -1), (0, 1), (-1, -1), (-1, 1), (1, -1), (1, 1))


def exchange(strips):
    rows, cols = lax.axis_size("row"), lax.axis_size("col")
    got = [
        lax.ppermute(strip, BOTH, moves(rows, cols, *step)) for strip, step in zip(strips, STEPS)
    ]
    return [got[1], got[0], got[3], got[2], got[7], got[6], got[5], got[4]]


def swap(value, mask):
    return lax.ppermute(
        value, BOTH, [(i, i ^ mask) for i in range(lax.axis_size("row") * lax.axis_size("col"))]
    )


def on_device(object_field, probe, intensity, offset_row, offset_col, live):
    tile = object_field.shape[2]
    width = probe.shape[1]
    half = width // 2
    params = pltpu.CompilerParams(vmem_limit_bytes=GRANT)
    side, corner, edge = array(2, tile, LANES), array(2, half, LANES), array(2, 2, half, tile)
    packed = pl.pallas_call(
        pack_kernel, out_shape=(side,) * 2 + (corner,) * 4, in_specs=vmem(1),
        out_specs=tuple(vmem(6)), compiler_params=params,
    )(object_field)
    halo = exchange([object_field[:, :, :half], object_field[:, :, tile - half :], *packed])
    tabs = jnp.asarray(make_tables(width))
    count = offset_row.shape[1]
    outs = pl.pallas_call(
        step_kernel,
        out_shape=(array(2, 2, tile, tile), edge, edge, side, side) + (corner,) * 4
        + (array(2, width, width),),
        in_specs=smem(3) + vmem(12),
        out_specs=tuple(vmem(10)),
        scratch_shapes=[pltpu.VMEM((2, 2, 4, tile + width, LANES), jnp.float32)] * 2,
        compiler_params=params,
    )(offset_row, offset_col, live, object_field, *halo, probe, intensity[0], tabs)
    back = exchange(outs[1:9])
    total = outs[9]
    for bit in range(8):
        total = total + swap(total, 1 << bit)
    count_all = count * lax.axis_size("row") * lax.axis_size("col")
    return pl.pallas_call(
        functools.partial(finish_kernel, scale=STEP_PROBE / count_all),
        out_shape=(array(2, 2, tile, tile), array(2, width, width)),
        in_specs=vmem(11), out_specs=tuple(vmem(2)), compiler_params=params,
    )(outs[0], *back, probe, total)


def solution(mesh):
    placed = (
        P(None, None, "row", "col"),
        P(),
        P("row", "col", None, None),
        P("row", "col"),
        P("row", "col"),
        P("row", "col"),
    )
    return jax.shard_map(
        on_device,
        mesh=mesh,
        in_specs=placed,
        out_specs=(P(None, None, "row", "col"), P()),
        check_vma=False,
    )
```

time: 542 us -> 141 us (0.26)
  waiting for transfers between devices: 277 us -> 48.1 us
  local copies, waits for them, and re-layouts: 106 us -> 1.29 us
  matrix products: 56.2 us -> 0 us
  starting transfers between devices: 30.7 us -> 74.5 us
  loops' own time: 32.5 us -> 0 us
  other arithmetic: 19.2 us -> 0.13 us
  Pallas kernels: 0 us -> 15.3 us
  between operations: 15.8 us -> 1.62 us
    psum x1 -> x0, waiting for transfers between devices: 249 us -> none  [on_device(): probe_total = lax.psum(probe_part, ('row', 'col'))]
    dot_general x48 -> x0, matrix products: 56.2 us -> none  [the longest x6 7.21 us: transform(): jnp.einsum('kab,bc->kac', wave_re, four_im, precision=high)]
    ppermute x8 -> x24, starting transfers between devices: 30.7 us -> 74.5 us  [the longest x16 54.7 us: exchange(): lax.ppermute(strip, BOTH, moves(rows, cols, *step))]
    another operation x2 -> x0, loops' own time: 32.5 us -> none  [the longest x1 31.7 us: on_device(): lax.fori_loop(0, slot_count, add_slot, jnp.zeros(extended.shape, jnp.floa...]
    gather x48 -> x0, local copies, waits for them, and re-layouts: 27 us -> none
    dynamic_update_slice x8 -> x0, local copies, waits for them, and re-layouts: 26.5 us -> none  [add_slot(): return lax.dynamic_update_slice(accum_grad, current + grads[slot], start)]
    ppermute x8 -> x24, waiting for transfers between devices: 28.2 us -> 48.1 us  [the longest x16 27.3 us: exchange(): lax.ppermute(strip, BOTH, moves(rows, cols, *step))]
    dynamic_slice x32 -> x0, local copies, waits for them, and re-layouts: 18.3 us -> none  [the longest x16 9.42 us: add_slot(): start = (jnp.int32(0), jnp.int32(0), row_start[slot], col_start[slot])]
  transfers between devices with their start and end apart: 9 -> 24, of which waited for: 7 -> 11; matrix products, arithmetic and copies ran while one was open for 3% -> 0% of each run, Pallas kernels for 0% -> 0%
where the time goes in v1:
time: 141 us
  starting transfers between devices  74.5 us (53%)
  waiting for transfers between devices  48.1 us (34%)
  Pallas kernels  15.3 us (11%)
  between operations  1.62 us (1%)
    ppermute x16, starting transfers between devices, exchange(): lax.ppermute(strip, BOTH, moves(rows, cols, *step))  54.7 us
    ppermute x16, waiting for transfers between devices, exchange(): lax.ppermute(strip, BOTH, moves(rows, cols, *step))  27.3 us
    ppermute x8, waiting for transfers between devices, swap(): lax.ppermute(value, BOTH, [(i, i ^ mask) for i in range(lax.axis_size('ro...  20.8 us
    ppermute x8, starting transfers between devices, swap(): lax.ppermute(value, BOTH, [(i, i ^ mask) for i in range(lax.axis_size('ro...  19.7 us
    pallas_call x1, Pallas kernels, on_device(): pl.pallas_call(step_kernel, out_shape=(array(2, 2, tile, tile), edge, edg...  13.8 us
  transfers between devices with their start and end apart: 24, of which 11 were waited for; matrix products, arithmetic and copies ran while one was open for 0% of the time, Pallas kernels for 0%

profile of v1, /device:TPU:1, one launch (start us, length us, event | category | flops | bytes accessed | tf_op | source)
XLA Modules:
  0.0 140.9 jit_solution(14142698038727798618)
XLA Ops:
  0.6 0.0 copy-start
  0.6 1.2 copy-done
  1.9 0.2 shard_map.86
  2.1 0.0 copy-start.1
  2.1 0.0 copy-start.2
  2.1 7.7 %collective-permute-start.4 = (f32[2,64,128]{2,1,0:T(8,128)S(1)}, f32[2,64,128]{2,1,0:T(8,128)S(1)}, u32[]{:S(2)}, u32[]{:S(2)}) collective-permute-start(f32[2,64,128]{2,1,0:T(8,128)S(1)} %get-tuple-element.20), channel_id=1, source_target_pairs={{0,17},{1,18},{2,19},{3,20},{4,21},{5,22},{6,23},{7,24},{8,25},{9,... | collective-permute-start | bytes 196616 | tf_op jit(solution)/shard_map/ppermute | solution.py:264
  9.8 1.3 collective-permute-start.1
  11.1 4.2 %collective-permute-start = (f32[2,2,64,256]{3,2,1,0:T(8,128)S(1)}, f32[2,2,64,256]{3,2,1,0:T(8,128)S(1)}, u32[]{:S(2)}, u32[]{:S(2)}) collective-permute-start(f32[2,2,64,256]{3,2,1,0:T(8,128)S(1)} %get-tuple-element.35), channel_id=1, source_target_pairs={{0,16},{1,17},{2,18},{3,19},{4,20},{5,21},{6,22},{7,23},{8,24},{9,... | collective-permute-start | bytes 786440 | tf_op jit(solution)/shard_map/ppermute | solution.py:264
  15.3 2.3 %collective-permute-start.2 = (f32[2,256,128]{2,1,0:T(8,128)S(1)}, f32[2,256,128]{2,1,0:T(8,128)S(1)}, u32[]{:S(2)}, u32[]{:S(2)}) collective-permute-start(f32[2,256,128]{2,1,0:T(8,128)S(1)} %get-tuple-element.18), channel_id=1, source_target_pairs={{0,1},{1,2},{2,3},{3,4},{4,5},{5,6},{6,7},{7,8},{8,9},{9,10},{10,1... | collective-permute-start | bytes 786440 | tf_op jit(solution)/shard_map/ppermute | solution.py:264
  17.6 2.1 %collective-permute-start.3 = (f32[2,256,128]{2,1,0:T(8,128)S(1)}, f32[2,256,128]{2,1,0:T(8,128)S(1)}, u32[]{:S(2)}, u32[]{:S(2)}) collective-permute-start(f32[2,256,128]{2,1,0:T(8,128)S(1)} %get-tuple-element.19), channel_id=1, source_target_pairs={{1,0},{2,1},{3,2},{4,3},{5,4},{6,5},{7,6},{8,7},{9,8},{10,9},{11,1... | collective-permute-start | bytes 786440 | tf_op jit(solution)/shard_map/ppermute | solution.py:264
  19.7 0.0 collective-permute-done.4.ul_ref
  19.7 2.8 %collective-permute-start.5 = (f32[2,64,128]{2,1,0:T(8,128)S(1)}, f32[2,64,128]{2,1,0:T(8,128)S(1)}, u32[]{:S(2)}, u32[]{:S(2)}) collective-permute-start(f32[2,64,128]{2,1,0:T(8,128)S(1)} %get-tuple-element.21), channel_id=1, source_target_pairs={{1,16},{2,17},{3,18},{4,19},{5,20},{6,21},{7,22},{8,23},{9,24},{10... | collective-permute-start | bytes 196616 | tf_op jit(solution)/shard_map/ppermute | solution.py:264
  22.5 1.3 collective-permute-done.5.uh_ref
  23.8 1.3 collective-permute-start.6
  25.1 4.3 %collective-permute-done.6.dl_ref = f32[2,64,128]{2,1,0:T(8,128)S(1)} collective-permute-done((f32[2,64,128]{2,1,0:T(8,128)S(1)}, f32[2,64,128]{2,1,0:T(8,128)S(1)}, u32[]{:S(2)}, u32[]{:S(2)}) %collective-permute-start.6) | collective-permute-done | bytes 65568 | tf_op jit(solution)/shard_map/ppermute | solution.py:264
  29.4 1.3 collective-permute-start.7
  31.3 0.0 copy-start.3
  31.3 0.0 copy-start.4
  31.4 11.6 %collective-permute-done.7.dh_ref = f32[2,64,128]{2,1,0:T(8,128)S(1)} collective-permute-done((f32[2,64,128]{2,1,0:T(8,128)S(1)}, f32[2,64,128]{2,1,0:T(8,128)S(1)}, u32[]{:S(2)}, u32[]{:S(2)}) %collective-permute-start.7) | collective-permute-done | bytes 65568 | tf_op jit(solution)/shard_map/ppermute | solution.py:264
  43.0 0.0 collective-permute-done.1.down_ref
  43.0 0.0 collective-permute-done.up_ref
  43.0 0.0 collective-permute-done.2.low_ref
  43.0 0.0 collective-permute-done.3.high_ref
  43.0 0.0 copy-done.1
  43.0 0.0 copy-done.2
  43.0 0.0 copy-done.3
  43.1 0.0 copy-done.4
  43.1 13.8 %shard_map.87 = (f32[2,2,256,256]{3,2,1,0:T(8,128)S(1)}, f32[2,2,64,256]{3,2,1,0:T(8,128)S(1)}, f32[2,2,64,256]{3,2,1,0:T(8,128)S(1)}, f32[2,256,128]{2,1,0:T(8,...) custom-call(s32[1,8]{1,0:T(1,128)S(1)} %copy-done.3, ...), custom_call_target="tpu_custom_call" | custom-call | tf_op jit(solution)/shard_map/pallas_call | solution.py:288
  56.9 0.1 collective-permute-start.16
  57.0 1.3 collective-permute-done.16
  58.3 3.5 %collective-permute-start.17 = (f32[2,128,128]{2,1,0:T(8,128)S(1)}, f32[2,128,128]{2,1,0:T(8,128)S(1)}, u32[]{:S(2)}, u32[]{:S(2)}) collective-permute-start(f32[2,128,128]{2,1,0:T(8,128)S(1)} %add.24), channel_id=1, source_target_pairs={{0,2},{1,3},{2,0},{3,1},{4,6},{5,7},{6,4},{7,5},{8,10},{9,11},{10,... | collective-permute-start | bytes 393224 | tf_op jit(solution)/shard_map/ppermute | solution.py:270
  61.8 3.7 %collective-permute-done.17 = f32[2,128,128]{2,1,0:T(8,128)S(1)} collective-permute-done((f32[2,128,128]{2,1,0:T(8,128)S(1)}, f32[2,128,128]{2,1,0:T(8,128)S(1)}, u32[]{:S(2)}, u32[]{:S(2)}) %collective-permute-start.17) | collective-permute-done | bytes 131104 | tf_op jit(solution)/shard_map/ppermute | solution.py:270
  65.6 1.2 collective-permute-start.18
  66.8 3.2 %collective-permute-done.18 = f32[2,128,128]{2,1,0:T(8,128)S(1)} collective-permute-done((f32[2,128,128]{2,1,0:T(8,128)S(1)}, f32[2,128,128]{2,1,0:T(8,128)S(1)}, u32[]{:S(2)}, u32[]{:S(2)}) %collective-permute-start.18) | collective-permute-done | bytes 131104 | tf_op jit(solution)/shard_map/ppermute | solution.py:270
  70.0 2.2 %collective-permute-start.19 = (f32[2,128,128]{2,1,0:T(8,128)S(1)}, f32[2,128,128]{2,1,0:T(8,128)S(1)}, u32[]{:S(2)}, u32[]{:S(2)}) collective-permute-start(f32[2,128,128]{2,1,0:T(8,128)S(1)} %add.26), channel_id=1, source_target_pairs={{0,8},{1,9},{2,10},{3,11},{4,12},{5,13},{6,14},{7,15},{8,0},{9,1},... | collective-permute-start | bytes 393224 | tf_op jit(solution)/shard_map/ppermute | solution.py:270
  72.2 3.2 %collective-permute-done.19 = f32[2,128,128]{2,1,0:T(8,128)S(1)} collective-permute-done((f32[2,128,128]{2,1,0:T(8,128)S(1)}, f32[2,128,128]{2,1,0:T(8,128)S(1)}, u32[]{:S(2)}, u32[]{:S(2)}) %collective-permute-start.19) | collective-permute-done | bytes 131104 | tf_op jit(solution)/shard_map/ppermute | solution.py:270
  75.4 1.8 %collective-permute-start.20 = (f32[2,128,128]{2,1,0:T(8,128)S(1)}, f32[2,128,128]{2,1,0:T(8,128)S(1)}, u32[]{:S(2)}, u32[]{:S(2)}) collective-permute-start(f32[2,128,128]{2,1,0:T(8,128)S(1)} %add.27), channel_id=1, source_target_pairs={{0,16},{1,17},{2,18},{3,19},{4,20},{5,21},{6,22},{7,23},{8,24},{9,... | collective-permute-start | bytes 393224 | tf_op jit(solution)/shard_map/ppermute | solution.py:270
  77.2 2.4 %collective-permute-done.20 = f32[2,128,128]{2,1,0:T(8,128)S(1)} collective-permute-done((f32[2,128,128]{2,1,0:T(8,128)S(1)}, f32[2,128,128]{2,1,0:T(8,128)S(1)}, u32[]{:S(2)}, u32[]{:S(2)}) %collective-permute-start.20) | collective-permute-done | bytes 131104 | tf_op jit(solution)/shard_map/ppermute | solution.py:270
  79.6 6.8 %collective-permute-start.21 = (f32[2,128,128]{2,1,0:T(8,128)S(1)}, f32[2,128,128]{2,1,0:T(8,128)S(1)}, u32[]{:S(2)}, u32[]{:S(2)}) collective-permute-start(f32[2,128,128]{2,1,0:T(8,128)S(1)} %add.28), channel_id=1, source_target_pairs={{0,32},{1,33},{2,34},{3,35},{4,36},{5,37},{6,38},{7,39},{8,40},{9,... | collective-permute-start | bytes 393224 | tf_op jit(solution)/shard_map/ppermute | solution.py:270
  86.4 2.7 %collective-permute-done.21 = f32[2,128,128]{2,1,0:T(8,128)S(1)} collective-permute-done((f32[2,128,128]{2,1,0:T(8,128)S(1)}, f32[2,128,128]{2,1,0:T(8,128)S(1)}, u32[]{:S(2)}, u32[]{:S(2)}) %collective-permute-start.21) | collective-permute-done | bytes 131104 | tf_op jit(solution)/shard_map/ppermute | solution.py:270
  89.0 1.9 %collective-permute-start.22 = (f32[2,128,128]{2,1,0:T(8,128)S(1)}, f32[2,128,128]{2,1,0:T(8,128)S(1)}, u32[]{:S(2)}, u32[]{:S(2)}) collective-permute-start(f32[2,128,128]{2,1,0:T(8,128)S(1)} %add.29), channel_id=1, source_target_pairs={{0,64},{1,65},{2,66},{3,67},{4,68},{5,69},{6,70},{7,71},{8,72},{9,... | collective-permute-start | bytes 393224 | tf_op jit(solution)/shard_map/ppermute | solution.py:270
  90.9 13.1 %collective-permute-start.12 = (f32[2,64,128]{2,1,0:T(8,128)S(1)}, f32[2,64,128]{2,1,0:T(8,128)S(1)}, u32[]{:S(2)}, u32[]{:S(2)}) collective-permute-start(f32[2,64,128]{2,1,0:T(8,128)S(1)} %get-tuple-element.29), channel_id=1, source_target_pairs={{0,17},{1,18},{2,19},{3,20},{4,21},{5,22},{6,23},{7,24},{8,25},{9,... | collective-permute-start | bytes 196616 | tf_op jit(solution)/shard_map/ppermute | solution.py:264
  104.0 1.3 collective-permute-start.13
  105.3 1.3 collective-permute-start.14
  106.6 7.4 %collective-permute-start.8 = (f32[2,2,64,256]{3,2,1,0:T(8,128)S(1)}, f32[2,2,64,256]{3,2,1,0:T(8,128)S(1)}, u32[]{:S(2)}, u32[]{:S(2)}) collective-permute-start(f32[2,2,64,256]{3,2,1,0:T(8,128)S(1)} %get-tuple-element.25), channel_id=1, source_target_pairs={{0,16},{1,17},{2,18},{3,19},{4,20},{5,21},{6,22},{7,23},{8,24},{9,... | collective-permute-start | bytes 786440 | tf_op jit(solution)/shard_map/ppermute | solution.py:264
  114.0 0.0 collective-permute-done.12.ul_ref
  114.0 1.3 collective-permute-start.9
  115.3 0.0 collective-permute-done.13.uh_ref
  115.3 4.3 %collective-permute-start.10 = (f32[2,256,128]{2,1,0:T(8,128)S(1)}, f32[2,256,128]{2,1,0:T(8,128)S(1)}, u32[]{:S(2)}, u32[]{:S(2)}) collective-permute-start(f32[2,256,128]{2,1,0:T(8,128)S(1)} %get-tuple-element.27), channel_id=1, source_target_pairs={{0,1},{1,2},{2,3},{3,4},{4,5},{5,6},{6,7},{7,8},{8,9},{9,10},{10,1... | collective-permute-start | bytes 786440 | tf_op jit(solution)/shard_map/ppermute | solution.py:264
  119.7 0.0 collective-permute-done.22
  119.7 1.9 %collective-permute-start.11 = (f32[2,256,128]{2,1,0:T(8,128)S(1)}, f32[2,256,128]{2,1,0:T(8,128)S(1)}, u32[]{:S(2)}, u32[]{:S(2)}) collective-permute-start(f32[2,256,128]{2,1,0:T(8,128)S(1)} %get-tuple-element.28), channel_id=1, source_target_pairs={{1,0},{2,1},{3,2},{4,3},{5,4},{6,5},{7,6},{8,7},{9,8},{10,9},{11,1... | collective-permute-start | bytes 786440 | tf_op jit(solution)/shard_map/ppermute | solution.py:264
  121.6 0.0 collective-permute-done.14.dl_ref
  121.6 2.3 %collective-permute-start.23 = (f32[2,128,128]{2,1,0:T(8,128)S(1)}, f32[2,128,128]{2,1,0:T(8,128)S(1)}, u32[]{:S(2)}, u32[]{:S(2)}) collective-permute-start(f32[2,128,128]{2,1,0:T(8,128)S(1)} %add.30), channel_id=1, source_target_pairs={{0,128},{1,129},{2,130},{3,131},{4,132},{5,133},{6,134},{7,135},{8... | collective-permute-start | bytes 393224 | tf_op jit(solution)/shard_map/ppermute | solution.py:270
  123.9 4.3 %collective-permute-done.23 = f32[2,128,128]{2,1,0:T(8,128)S(1)} collective-permute-done((f32[2,128,128]{2,1,0:T(8,128)S(1)}, f32[2,128,128]{2,1,0:T(8,128)S(1)}, u32[]{:S(2)}, u32[]{:S(2)}) %collective-permute-start.23) | collective-permute-done | bytes 131104 | tf_op jit(solution)/shard_map/ppermute | solution.py:270
  128.2 1.3 collective-permute-start.15
  129.5 10.0 %collective-permute-done.15.dh_ref = f32[2,64,128]{2,1,0:T(8,128)S(1)} collective-permute-done((f32[2,64,128]{2,1,0:T(8,128)S(1)}, f32[2,64,128]{2,1,0:T(8,128)S(1)}, u32[]{:S(2)}, u32[]{:S(2)}) %collective-permute-start.15) | collective-permute-done | bytes 65568 | tf_op jit(solution)/shard_map/ppermute | solution.py:264
  139.5 0.0 collective-permute-done.8.up_ref
  139.5 0.0 collective-permute-done.9.down_ref
  139.5 0.0 collective-permute-done.10.low_ref
  139.6 0.0 collective-permute-done.11.high_ref
  139.6 1.3 shard_map.88
  (9 shorter events, 0.2 us)
Async XLA Ops:
  0.6 1.2 copy-start
  2.1 41.0 %copy-start.1 = (f32[1,8,128,128]{3,2,1,0:T(8,128)S(1)}, f32[1,8,128,128]{3,2,1,0:T(8,128)}, u32[]{:S(2)}) copy-start(f32[1,8,128,128]{3,2,1,0:T(8,128)} %param.9) | copy-start | bytes 1572868
  2.1 41.0 %copy-start.2 = (f32[2,128,128]{2,1,0:T(8,128)S(1)}, f32[2,128,128]{2,1,0:T(8,128)}, u32[]{:S(2)}) copy-start(f32[2,128,128]{2,1,0:T(8,128)} %probe_ref.3) | copy-start | bytes 393220
  2.1 17.6 %collective-permute-start.4 = (f32[2,64,128]{2,1,0:T(8,128)S(1)}, f32[2,64,128]{2,1,0:T(8,128)S(1)}, u32[]{:S(2)}, u32[]{:S(2)}) collective-permute-start(f32[2,64,128]{2,1,0:T(8,128)S(1)} %get-tuple-element.20), channel_id=1, source_target_pairs={{0,17},{1,18},{2,19},{3,20},{4,21},{5,22},{6,23},{7,24},{8,25},{9,... | collective-permute-start | bytes 196616 | tf_op jit(solution)/shard_map/ppermute | solution.py:264
  9.8 33.2 %collective-permute-start.1 = (f32[2,2,64,256]{3,2,1,0:T(8,128)S(1)}, f32[2,2,64,256]{3,2,1,0:T(8,128)S(1)}, u32[]{:S(2)}, u32[]{:S(2)}) collective-permute-start(f32[2,2,64,256]{3,2,1,0:T(8,128)S(1)} %get-tuple-element.34), channel_id=1, source_target_pairs={{16,0},{17,1},{18,2},{19,3},{20,4},{21,5},{22,6},{23,7},{24,8},{25... | collective-permute-start | bytes 786440 | tf_op jit(solution)/shard_map/ppermute | solution.py:264
  11.1 31.9 %collective-permute-start = (f32[2,2,64,256]{3,2,1,0:T(8,128)S(1)}, f32[2,2,64,256]{3,2,1,0:T(8,128)S(1)}, u32[]{:S(2)}, u32[]{:S(2)}) collective-permute-start(f32[2,2,64,256]{3,2,1,0:T(8,128)S(1)} %get-tuple-element.35), channel_id=1, source_target_pairs={{0,16},{1,17},{2,18},{3,19},{4,20},{5,21},{6,22},{7,23},{8,24},{9,... | collective-permute-start | bytes 786440 | tf_op jit(solution)/shard_map/ppermute | solution.py:264
  15.3 27.7 %collective-permute-start.2 = (f32[2,256,128]{2,1,0:T(8,128)S(1)}, f32[2,256,128]{2,1,0:T(8,128)S(1)}, u32[]{:S(2)}, u32[]{:S(2)}) collective-permute-start(f32[2,256,128]{2,1,0:T(8,128)S(1)} %get-tuple-element.18), channel_id=1, source_target_pairs={{0,1},{1,2},{2,3},{3,4},{4,5},{5,6},{6,7},{7,8},{8,9},{9,10},{10,1... | collective-permute-start | bytes 786440 | tf_op jit(solution)/shard_map/ppermute | solution.py:264
  17.6 25.4 %collective-permute-start.3 = (f32[2,256,128]{2,1,0:T(8,128)S(1)}, f32[2,256,128]{2,1,0:T(8,128)S(1)}, u32[]{:S(2)}, u32[]{:S(2)}) collective-permute-start(f32[2,256,128]{2,1,0:T(8,128)S(1)} %get-tuple-element.19), channel_id=1, source_target_pairs={{1,0},{2,1},{3,2},{4,3},{5,4},{6,5},{7,6},{8,7},{9,8},{10,9},{11,1... | collective-permute-start | bytes 786440 | tf_op jit(solution)/shard_map/ppermute | solution.py:264
  19.7 4.1 %collective-permute-start.5 = (f32[2,64,128]{2,1,0:T(8,128)S(1)}, f32[2,64,128]{2,1,0:T(8,128)S(1)}, u32[]{:S(2)}, u32[]{:S(2)}) collective-permute-start(f32[2,64,128]{2,1,0:T(8,128)S(1)} %get-tuple-element.21), channel_id=1, source_target_pairs={{1,16},{2,17},{3,18},{4,19},{5,20},{6,21},{7,22},{8,23},{9,24},{10... | collective-permute-start | bytes 196616 | tf_op jit(solution)/shard_map/ppermute | solution.py:264
  23.8 5.6 %collective-permute-start.6 = (f32[2,64,128]{2,1,0:T(8,128)S(1)}, f32[2,64,128]{2,1,0:T(8,128)S(1)}, u32[]{:S(2)}, u32[]{:S(2)}) collective-permute-start(f32[2,64,128]{2,1,0:T(8,128)S(1)} %get-tuple-element.22), channel_id=1, source_target_pairs={{16,1},{17,2},{18,3},{19,4},{20,5},{21,6},{22,7},{23,8},{24,9},{25... | collective-permute-start | bytes 196616 | tf_op jit(solution)/shard_map/ppermute | solution.py:264
  29.4 13.6 %collective-permute-start.7 = (f32[2,64,128]{2,1,0:T(8,128)S(1)}, f32[2,64,128]{2,1,0:T(8,128)S(1)}, u32[]{:S(2)}, u32[]{:S(2)}) collective-permute-start(f32[2,64,128]{2,1,0:T(8,128)S(1)} %get-tuple-element.23), channel_id=1, source_target_pairs={{17,0},{18,1},{19,2},{20,3},{21,4},{22,5},{23,6},{24,7},{25,8},{26... | collective-permute-start | bytes 196616 | tf_op jit(solution)/shard_map/ppermute | solution.py:264
  31.3 11.7 %copy-start.3 = (s32[1,8]{1,0:T(1,128)S(1)}, s32[1,8]{1,0:T(1,128)}, u32[]{:S(2)}) copy-start(s32[1,8]{1,0:T(1,128)} %row_ref.1) | copy-start | bytes 100
  31.3 11.7 %copy-start.4 = (s32[1,8]{1,0:T(1,128)S(1)}, s32[1,8]{1,0:T(1,128)}, u32[]{:S(2)}) copy-start(s32[1,8]{1,0:T(1,128)} %col_ref.1) | copy-start | bytes 100
  56.9 1.4 %collective-permute-start.16 = (f32[2,128,128]{2,1,0:T(8,128)S(1)}, f32[2,128,128]{2,1,0:T(8,128)S(1)}, u32[]{:S(2)}, u32[]{:S(2)}) collective-permute-start(f32[2,128,128]{2,1,0:T(8,128)S(1)} %get-tuple-element.33), channel_id=1, source_target_pairs={{0,1},{1,0},{2,3},{3,2},{4,5},{5,4},{6,7},{7,6},{8,9},{9,8},{10,11... | collective-permute-start | bytes 393224 | tf_op jit(solution)/shard_map/ppermute | solution.py:270
  58.3 7.2 %collective-permute-start.17 = (f32[2,128,128]{2,1,0:T(8,128)S(1)}, f32[2,128,128]{2,1,0:T(8,128)S(1)}, u32[]{:S(2)}, u32[]{:S(2)}) collective-permute-start(f32[2,128,128]{2,1,0:T(8,128)S(1)} %add.24), channel_id=1, source_target_pairs={{0,2},{1,3},{2,0},{3,1},{4,6},{5,7},{6,4},{7,5},{8,10},{9,11},{10,... | collective-permute-start | bytes 393224 | tf_op jit(solution)/shard_map/ppermute | solution.py:270
  65.6 4.4 %collective-permute-start.18 = (f32[2,128,128]{2,1,0:T(8,128)S(1)}, f32[2,128,128]{2,1,0:T(8,128)S(1)}, u32[]{:S(2)}, u32[]{:S(2)}) collective-permute-start(f32[2,128,128]{2,1,0:T(8,128)S(1)} %add.25), channel_id=1, source_target_pairs={{0,4},{1,5},{2,6},{3,7},{4,0},{5,1},{6,2},{7,3},{8,12},{9,13},{10,... | collective-permute-start | bytes 393224 | tf_op jit(solution)/shard_map/ppermute | solution.py:270
  70.0 5.4 %collective-permute-start.19 = (f32[2,128,128]{2,1,0:T(8,128)S(1)}, f32[2,128,128]{2,1,0:T(8,128)S(1)}, u32[]{:S(2)}, u32[]{:S(2)}) collective-permute-start(f32[2,128,128]{2,1,0:T(8,128)S(1)} %add.26), channel_id=1, source_target_pairs={{0,8},{1,9},{2,10},{3,11},{4,12},{5,13},{6,14},{7,15},{8,0},{9,1},... | collective-permute-start | bytes 393224 | tf_op jit(solution)/shard_map/ppermute | solution.py:270
  75.4 4.2 %collective-permute-start.20 = (f32[2,128,128]{2,1,0:T(8,128)S(1)}, f32[2,128,128]{2,1,0:T(8,128)S(1)}, u32[]{:S(2)}, u32[]{:S(2)}) collective-permute-start(f32[2,128,128]{2,1,0:T(8,128)S(1)} %add.27), channel_id=1, source_target_pairs={{0,16},{1,17},{2,18},{3,19},{4,20},{5,21},{6,22},{7,23},{8,24},{9,... | collective-permute-start | bytes 393224 | tf_op jit(solution)/shard_map/ppermute | solution.py:270
  79.6 9.4 %collective-permute-start.21 = (f32[2,128,128]{2,1,0:T(8,128)S(1)}, f32[2,128,128]{2,1,0:T(8,128)S(1)}, u32[]{:S(2)}, u32[]{:S(2)}) collective-permute-start(f32[2,128,128]{2,1,0:T(8,128)S(1)} %add.28), channel_id=1, source_target_pairs={{0,32},{1,33},{2,34},{3,35},{4,36},{5,37},{6,38},{7,39},{8,40},{9,... | collective-permute-start | bytes 393224 | tf_op jit(solution)/shard_map/ppermute | solution.py:270
  89.0 30.6 %collective-permute-start.22 = (f32[2,128,128]{2,1,0:T(8,128)S(1)}, f32[2,128,128]{2,1,0:T(8,128)S(1)}, u32[]{:S(2)}, u32[]{:S(2)}) collective-permute-start(f32[2,128,128]{2,1,0:T(8,128)S(1)} %add.29), channel_id=1, source_target_pairs={{0,64},{1,65},{2,66},{3,67},{4,68},{5,69},{6,70},{7,71},{8,72},{9,... | collective-permute-start | bytes 393224 | tf_op jit(solution)/shard_map/ppermute | solution.py:270
  90.9 23.1 %collective-permute-start.12 = (f32[2,64,128]{2,1,0:T(8,128)S(1)}, f32[2,64,128]{2,1,0:T(8,128)S(1)}, u32[]{:S(2)}, u32[]{:S(2)}) collective-permute-start(f32[2,64,128]{2,1,0:T(8,128)S(1)} %get-tuple-element.29), channel_id=1, source_target_pairs={{0,17},{1,18},{2,19},{3,20},{4,21},{5,22},{6,23},{7,24},{8,25},{9,... | collective-permute-start | bytes 196616 | tf_op jit(solution)/shard_map/ppermute | solution.py:264
  104.0 11.3 %collective-permute-start.13 = (f32[2,64,128]{2,1,0:T(8,128)S(1)}, f32[2,64,128]{2,1,0:T(8,128)S(1)}, u32[]{:S(2)}, u32[]{:S(2)}) collective-permute-start(f32[2,64,128]{2,1,0:T(8,128)S(1)} %get-tuple-element.30), channel_id=1, source_target_pairs={{1,16},{2,17},{3,18},{4,19},{5,20},{6,21},{7,22},{8,23},{9,24},{10... | collective-permute-start | bytes 196616 | tf_op jit(solution)/shard_map/ppermute | solution.py:264
  105.3 16.3 %collective-permute-start.14 = (f32[2,64,128]{2,1,0:T(8,128)S(1)}, f32[2,64,128]{2,1,0:T(8,128)S(1)}, u32[]{:S(2)}, u32[]{:S(2)}) collective-permute-start(f32[2,64,128]{2,1,0:T(8,128)S(1)} %get-tuple-element.31), channel_id=1, source_target_pairs={{16,1},{17,2},{18,3},{19,4},{20,5},{21,6},{22,7},{23,8},{24,9},{25... | collective-permute-start | bytes 196616 | tf_op jit(solution)/shard_map/ppermute | solution.py:264
  106.6 32.9 %collective-permute-start.8 = (f32[2,2,64,256]{3,2,1,0:T(8,128)S(1)}, f32[2,2,64,256]{3,2,1,0:T(8,128)S(1)}, u32[]{:S(2)}, u32[]{:S(2)}) collective-permute-start(f32[2,2,64,256]{3,2,1,0:T(8,128)S(1)} %get-tuple-element.25), channel_id=1, source_target_pairs={{0,16},{1,17},{2,18},{3,19},{4,20},{5,21},{6,22},{7,23},{8,24},{9,... | collective-permute-start | bytes 786440 | tf_op jit(solution)/shard_map/ppermute | solution.py:264
  114.0 25.5 %collective-permute-start.9 = (f32[2,2,64,256]{3,2,1,0:T(8,128)S(1)}, f32[2,2,64,256]{3,2,1,0:T(8,128)S(1)}, u32[]{:S(2)}, u32[]{:S(2)}) collective-permute-start(f32[2,2,64,256]{3,2,1,0:T(8,128)S(1)} %get-tuple-element.26), channel_id=1, source_target_pairs={{16,0},{17,1},{18,2},{19,3},{20,4},{21,5},{22,6},{23,7},{24,8},{25... | collective-permute-start | bytes 786440 | tf_op jit(solution)/shard_map/ppermute | solution.py:264
  115.3 24.2 %collective-permute-start.10 = (f32[2,256,128]{2,1,0:T(8,128)S(1)}, f32[2,256,128]{2,1,0:T(8,128)S(1)}, u32[]{:S(2)}, u32[]{:S(2)}) collective-permute-start(f32[2,256,128]{2,1,0:T(8,128)S(1)} %get-tuple-element.27), channel_id=1, source_target_pairs={{0,1},{1,2},{2,3},{3,4},{4,5},{5,6},{6,7},{7,8},{8,9},{9,10},{10,1... | collective-permute-start | bytes 786440 | tf_op jit(solution)/shard_map/ppermute | solution.py:264
  119.7 19.9 %collective-permute-start.11 = (f32[2,256,128]{2,1,0:T(8,128)S(1)}, f32[2,256,128]{2,1,0:T(8,128)S(1)}, u32[]{:S(2)}, u32[]{:S(2)}) collective-permute-start(f32[2,256,128]{2,1,0:T(8,128)S(1)} %get-tuple-element.28), channel_id=1, source_target_pairs={{1,0},{2,1},{3,2},{4,3},{5,4},{6,5},{7,6},{8,7},{9,8},{10,9},{11,1... | collective-permute-start | bytes 786440 | tf_op jit(solution)/shard_map/ppermute | solution.py:264
  121.6 6.6 %collective-permute-start.23 = (f32[2,128,128]{2,1,0:T(8,128)S(1)}, f32[2,128,128]{2,1,0:T(8,128)S(1)}, u32[]{:S(2)}, u32[]{:S(2)}) collective-permute-start(f32[2,128,128]{2,1,0:T(8,128)S(1)} %add.30), channel_id=1, source_target_pairs={{0,128},{1,129},{2,130},{3,131},{4,132},{5,133},{6,134},{7,135},{8... | collective-permute-start | bytes 393224 | tf_op jit(solution)/shard_map/ppermute | solution.py:270
  128.2 11.3 %collective-permute-start.15 = (f32[2,64,128]{2,1,0:T(8,128)S(1)}, f32[2,64,128]{2,1,0:T(8,128)S(1)}, u32[]{:S(2)}, u32[]{:S(2)}) collective-permute-start(f32[2,64,128]{2,1,0:T(8,128)S(1)} %get-tuple-element.32), channel_id=1, source_target_pairs={{17,0},{18,1},{19,2},{20,3},{21,4},{22,5},{23,6},{24,7},{25,8},{26... | collective-permute-start | bytes 196616 | tf_op jit(solution)/shard_map/ppermute | solution.py:264

commit v2 on v1

--- a/solution.py
+++ b/solution.py
@@ -16,6 +16,7 @@
 LANES = 128
 BOTH = ("row", "col")
 GRANT = 48 * 1024 * 1024
+MASKS = (4, 12, 128, 130, 16, 32, 96)
 
 
 def split_table(table):
@@ -66,23 +67,40 @@
     return real, imag
 
 
-def pack_kernel(obj_ref, low_ref, high_ref, *corner_refs):
+def pack_kernel(obj_ref, low_ref, high_ref):
     half = LANES // 2
     first = lax.broadcasted_iota(jnp.int32, (obj_ref.shape[2], LANES), 1) < half
-    tile = obj_ref.shape[2]
     for piece in range(2):
-        low = jnp.where(
+        low_ref[piece] = jnp.where(
             first, obj_ref[piece, 0, :, :LANES], pltpu.roll(obj_ref[piece, 1, :, :LANES], half, 1)
         )
-        high = jnp.where(
+        high_ref[piece] = jnp.where(
             first, pltpu.roll(obj_ref[piece, 0, :, LANES:], half, 1), obj_ref[piece, 1, :, LANES:]
         )
-        low_ref[piece] = low
-        high_ref[piece] = high
-        corner_refs[0][piece] = low[:half]
-        corner_refs[1][piece] = high[:half]
-        corner_refs[2][piece] = low[tile - half :]
-        corner_refs[3][piece] = high[tile - half :]
+
+
+def rows_kernel(obj_ref, low_ref, high_ref, up_ref, down_ref):
+    half = LANES // 2
+    tile = obj_ref.shape[2]
+    for out, start in ((up_ref, 0), (down_ref, tile - half)):
+        rows = slice(start, start + half)
+        for piece in range(2):
+            for part in range(2):
+                for block in range(2):
+                    cols = slice(block * LANES, (block + 1) * LANES)
+                    out[piece, 2 * part + block] = obj_ref[piece, part, rows, cols]
+            out[piece, 4] = low_ref[piece, rows]
+            out[piece, 5] = high_ref[piece, rows]
+
+
+def fold_kernel(low_ref, high_ref, up_ref, down_ref, low_out, high_out):
+    half = LANES // 2
+    tile = low_ref.shape[1]
+    for ref, out, place in ((low_ref, low_out, 4), (high_ref, high_out, 5)):
+        for piece in range(2):
+            out[piece, :half] = ref[piece, :half] + up_ref[piece, place]
+            out[piece, half : tile - half] = ref[piece, half : tile - half]
+            out[piece, tile - half :] = ref[piece, tile - half :] + down_ref[piece, place]
 
 
 def place_window(row_ref, col_ref, slot):
@@ -91,10 +109,10 @@
 
 
 def step_kernel(
-    row_ref, col_ref, live_ref, obj_ref, up_ref, down_ref, low_ref, high_ref,
-    ul_ref, uh_ref, dl_ref, dh_ref, probe_ref, measured_ref, tabs_ref,
-    new_ref, gup_ref, gdown_ref, glow_ref, ghigh_ref, gul_ref, guh_ref, gdl_ref, gdh_ref, gp_ref,
-    ext, grad,
+    row_ref, col_ref, live_ref, core_ref, obj_ref, up_ref, down_ref, low_ref, high_ref,
+    probe_ref, measured_ref, tabs_ref,
+    new_ref, gup_ref, gdown_ref, glow_ref, ghigh_ref, keep_ref, send_ref,
+    ext, grad, gp_ref,
 ):
     width = probe_ref.shape[1]
     tile = obj_ref.shape[2]
@@ -105,12 +123,13 @@
         for part in range(2):
             for block in range(2):
                 cols = pl.ds(block * LANES, LANES)
-                ext[piece, part, 1 + block, :half] = up_ref[piece, part, :, cols]
+                ext[piece, part, 1 + block, :half] = up_ref[piece, 2 * part + block]
                 ext[piece, part, 1 + block, half : half + tile] = obj_ref[piece, part, :, cols]
-                ext[piece, part, 1 + block, half + tile :] = down_ref[piece, part, :, cols]
-            for block, sides in ((0, (ul_ref, low_ref, dl_ref)), (3, (uh_ref, high_ref, dh_ref))):
-                for ref, start in zip(sides, (0, half, half + tile)):
-                    strip = ref[piece]
+                ext[piece, part, 1 + block, half + tile :] = down_ref[piece, 2 * part + block]
+            for block, side in ((0, low_ref), (3, high_ref)):
+                place = 4 + block // 3
+                strips = (up_ref[piece, place], side[piece], down_ref[piece, place])
+                for strip, start in zip(strips, (0, half, half + tile)):
                     if (block == 0) == (part == 0):
                         strip = pltpu.roll(strip, half, 1)
                     ext[piece, part, block, start : start + strip.shape[0]] = strip
@@ -177,58 +196,60 @@
         return 0
 
     lax.fori_loop(0, row_ref.shape[1] // 2, pair, 0)
-    lower = lax.broadcasted_iota(jnp.int32, (half, LANES), 1) < half
+    first = lax.broadcasted_iota(jnp.int32, (half, LANES), 1) < half
     inner = lax.broadcasted_iota(jnp.int32, (tile, LANES), 1) < half
+    core = core_ref[0, 0]
+    keep_ref[...] = jnp.where(core == 0, gp_ref[0], gp_ref[1])
+    send_ref[...] = jnp.where(core == 0, gp_ref[1], gp_ref[0])
     for piece in range(2):
         for part in range(2):
             for block in range(2):
                 cols = pl.ds(block * LANES, LANES)
-                gup_ref[piece, part, :, cols] = grad[piece, part, 1 + block, :half]
-                gdown_ref[piece, part, :, cols] = grad[piece, part, 1 + block, half + tile :]
+                gup_ref[piece, 2 * part + block] = grad[piece, part, 1 + block, :half]
+                gdown_ref[piece, 2 * part + block] = grad[piece, part, 1 + block, half + tile :]
                 new_ref[piece, part, :, cols] = (
                     obj_ref[piece, part, :, cols]
                     - STEP_OBJECT * grad[piece, part, 1 + block, half : half + tile]
                 )
-        for block, outs in ((0, (gul_ref, glow_ref, gdl_ref)), (3, (guh_ref, ghigh_ref, gdh_ref))):
-            for ref, start in zip(outs, (0, half, half + tile)):
-                size = ref.shape[1]
-                mask = inner if size == tile else lower
+        for block, side in ((0, glow_ref), (3, ghigh_ref)):
+            for start, size in ((0, half), (half, tile), (half + tile, half)):
                 real = grad[piece, 0, block, start : start + size]
                 imag = grad[piece, 1, block, start : start + size]
                 if block == 0:
                     real = pltpu.roll(real, half, 1)
                 else:
                     imag = pltpu.roll(imag, half, 1)
-                ref[piece] = jnp.where(mask, real, imag)
+                strip = jnp.where(inner if size == tile else first, real, imag)
+                if size == tile:
+                    side[piece] = strip
+                else:
+                    (gup_ref if start == 0 else gdown_ref)[piece, 4 + block // 3] = strip
 
 
 def finish_kernel(
-    part_ref, up_ref, down_ref, low_ref, high_ref, ul_ref, uh_ref, dl_ref, dh_ref, probe_ref, sum_ref,
+    core_ref, part_ref, up_ref, down_ref, low_ref, high_ref, probe_ref, mine_ref, other_ref,
     new_ref, newp_ref, *, scale,
 ):
     tile = part_ref.shape[2]
     half = up_ref.shape[2]
     first = lax.broadcasted_iota(jnp.int32, (half, LANES), 1) < half
-    newp_ref[...] = probe_ref[...] - scale * sum_ref[...]
+    core = core_ref[0, 0]
+    newp_ref[0] = probe_ref[0] - scale * jnp.where(core == 0, mine_ref[...], other_ref[...])
+    newp_ref[1] = probe_ref[1] - scale * jnp.where(core == 0, other_ref[...], mine_ref[...])
     for piece in range(2):
         for part in range(2):
             for start in range(0, tile, half):
                 rows = slice(start, start + half)
                 for block in range(2):
                     cols = slice(block * LANES, (block + 1) * LANES)
-                    strips = [(low_ref, high_ref)[block][piece, rows]]
-                    total = None
+                    total = (low_ref, high_ref)[block][piece, rows]
+                    if block != part:
+                        total = pltpu.roll(total, half, 1)
+                    total = jnp.where(first == (block == 0), total, 0.0)
                     if start == 0:
-                        strips.append((ul_ref, uh_ref)[block][piece])
-                        total = up_ref[piece, part, :, cols]
+                        total += up_ref[piece, 2 * part + block]
                     if start == tile - half:
-                        strips.append((dl_ref, dh_ref)[block][piece])
-                        total = down_ref[piece, part, :, cols]
-                    strip = strips[0] if len(strips) == 1 else strips[0] + strips[1]
-                    if block != part:
-                        strip = pltpu.roll(strip, half, 1)
-                    strip = jnp.where(first == (block == 0), strip, 0.0)
-                    total = strip if total is None else total + strip
+                        total += down_ref[piece, 2 * part + block]
                     new_ref[piece, part, rows, cols] = (
                         part_ref[piece, part, rows, cols] - STEP_OBJECT * total
                     )
@@ -255,55 +276,62 @@
     return pairs
 
 
-STEPS = ((-1, 0), (1, 0), (0, -1), (0, 1), (-1, -1), (-1, 1), (1, -1), (1, 1))
-
-
-def exchange(strips):
+def shift(value, row_step, col_step):
     rows, cols = lax.axis_size("row"), lax.axis_size("col")
-    got = [
-        lax.ppermute(strip, BOTH, moves(rows, cols, *step)) for strip, step in zip(strips, STEPS)
-    ]
-    return [got[1], got[0], got[3], got[2], got[7], got[6], got[5], got[4]]
+    return lax.ppermute(value, BOTH, moves(rows, cols, row_step, col_step))
 
 
 def swap(value, mask):
-    return lax.ppermute(
-        value, BOTH, [(i, i ^ mask) for i in range(lax.axis_size("row") * lax.axis_size("col"))]
-    )
+    count = lax.axis_size("row") * lax.axis_size("col")
+    return lax.ppermute(value, BOTH, [(i, i ^ mask) for i in range(count)])
+
+
+def call(kernel, out_shape, scalars, arrays, scratch=()):
+    return pl.pallas_call(
+        kernel, out_shape=tuple(out_shape), in_specs=smem(len(scalars)) + vmem(len(arrays)),
+        out_specs=tuple(vmem(len(out_shape))), scratch_shapes=list(scratch),
+        compiler_params=pltpu.CompilerParams(vmem_limit_bytes=GRANT),
+    )(*scalars, *arrays)
 
 
 def on_device(object_field, probe, intensity, offset_row, offset_col, live):
     tile = object_field.shape[2]
     width = probe.shape[1]
     half = width // 2
-    params = pltpu.CompilerParams(vmem_limit_bytes=GRANT)
-    side, corner, edge = array(2, tile, LANES), array(2, half, LANES), array(2, 2, half, tile)
-    packed = pl.pallas_call(
-        pack_kernel, out_shape=(side,) * 2 + (corner,) * 4, in_specs=vmem(1),
-        out_specs=tuple(vmem(6)), compiler_params=params,
-    )(object_field)
-    halo = exchange([object_field[:, :, :half], object_field[:, :, tile - half :], *packed])
+    side, edge, field = array(2, tile, LANES), array(2, 6, half, LANES), array(2, 2, tile, tile)
+    core = lax.rem(lax.axis_index("col"), 2).astype(jnp.int32).reshape(1, 1)
+    low, high = call(pack_kernel, (side, side), (), (object_field,))
+    low, high = shift(high, 0, 1), shift(low, 0, -1)
+    up, down = call(rows_kernel, (edge, edge), (), (object_field, low, high))
+    up, down = shift(down, 1, 0), shift(up, -1, 0)
     tabs = jnp.asarray(make_tables(width))
     count = offset_row.shape[1]
-    outs = pl.pallas_call(
+    grown = pltpu.VMEM((2, 2, 4, tile + width, LANES), jnp.float32)
+    part, gup, gdown, glow, ghigh, mine, send = call(
         step_kernel,
-        out_shape=(array(2, 2, tile, tile), edge, edge, side, side) + (corner,) * 4
-        + (array(2, width, width),),
-        in_specs=smem(3) + vmem(12),
-        out_specs=tuple(vmem(10)),
-        scratch_shapes=[pltpu.VMEM((2, 2, 4, tile + width, LANES), jnp.float32)] * 2,
-        compiler_params=params,
-    )(offset_row, offset_col, live, object_field, *halo, probe, intensity[0], tabs)
-    back = exchange(outs[1:9])
-    total = outs[9]
-    for bit in range(8):
-        total = total + swap(total, 1 << bit)
+        (field, edge, edge, side, side, array(width, width), array(width, width)),
+        (offset_row, offset_col, live, core),
+        (object_field, up, down, low, high, probe, intensity[0], tabs),
+        (grown, grown, pltpu.VMEM((2, width, width), jnp.float32)),
+    )
+    mine = mine + swap(send, 1)
+    mine, gup, gdown = lax.optimization_barrier((mine, gup, gdown))
+    up, down = shift(gdown, 1, 0), shift(gup, -1, 0)
+    for mask in MASKS[:4]:
+        mine = mine + swap(mine, mask)
+    low, high = call(fold_kernel, (side, side), (), (glow, ghigh, up, down))
+    mine, low, high = lax.optimization_barrier((mine, low, high))
+    low, high = shift(high, 0, 1), shift(low, 0, -1)
+    for mask in MASKS[4:]:
+        mine = mine + swap(mine, mask)
+    other = swap(mine, 1)
     count_all = count * lax.axis_size("row") * lax.axis_size("col")
-    return pl.pallas_call(
+    return call(
         functools.partial(finish_kernel, scale=STEP_PROBE / count_all),
-        out_shape=(array(2, 2, tile, tile), array(2, width, width)),
-        in_specs=vmem(11), out_specs=tuple(vmem(2)), compiler_params=params,
-    )(outs[0], *back, probe, total)
+        (field, array(2, width, width)),
+        (core,),
+        (part, up, down, low, high, probe, mine, other),
+    )
 
 
 def solution(mesh):

time: 141 us -> 102 us (0.72)
  the two profiles are of different devices: /device:TPU:1 before, /device:TPU:7 now
where the time goes in v2:
time: 102 us
  starting transfers between devices  46.6 us (46%)
  waiting for transfers between devices  35.8 us (35%)
  Pallas kernels  16.1 us (16%)
  local copies, waits for them, and re-layouts  1.89 us (2%)
  between operations  1.48 us (1%)
    ppermute x8, starting transfers between devices, shift(): return lax.ppermute(value, BOTH, moves(rows, cols, row_step, col_step))  26 us
    ppermute x9, starting transfers between devices, swap(): return lax.ppermute(value, BOTH, [(i, i ^ mask) for i in range(count)])  20.6 us
    ppermute x9, waiting for transfers between devices, swap(): return lax.ppermute(value, BOTH, [(i, i ^ mask) for i in range(count)])  19.1 us
    ppermute x8, waiting for transfers between devices, shift(): return lax.ppermute(value, BOTH, moves(rows, cols, row_step, col_step))  16.7 us
    pallas_call x5, Pallas kernels, call(): pl.pallas_call(kernel, out_shape=tuple(out_shape), in_specs=smem(len(scal...  16.1 us
  transfers between devices with their start and end apart: 17, of which 12 were waited for; matrix products, arithmetic and copies ran while one was open for 0% of the time, Pallas kernels for 0%

profile of v2, /device:TPU:7, one launch (start us, length us, event | category | flops | bytes accessed | tf_op | source)
XLA Modules:
  0.0 101.9 jit_solution(17914359302334017914)
XLA Ops:
  0.6 0.0 copy-start
  0.6 1.2 %copy-done = f32[2,2,256,256]{3,2,1,0:T(8,128)S(1)} copy-done((f32[2,2,256,256]{3,2,1,0:T(8,128)S(1)}, f32[2,2,256,256]{3,2,1,0:T(8,128)}, u32[]{:S(2)}) %copy-start) | copy-done | bytes 1048600
  1.9 0.0 copy-start.3
  1.9 0.2 shard_map.86
  2.1 0.0 copy-start.1
  2.1 5.5 %collective-permute-start = (f32[2,256,128]{2,1,0:T(8,128)S(1)}, f32[2,256,128]{2,1,0:T(8,128)S(1)}, u32[]{:S(2)}, u32[]{:S(2)}) collective-permute-start(f32[2,256,128]{2,1,0:T(8,128)S(1)} %get-tuple-element.21), channel_id=1, source_target_pairs={{0,1},{1,2},{2,3},{3,4},{4,5},{5,6},{6,7},{7,8},{8,9},{9,10},{10,1... | collective-permute-start | bytes 786440 | tf_op jit(solution)/shard_map/ppermute | solution.py:281
  7.6 0.0 copy-start.2
  7.6 2.1 %collective-permute-start.1 = (f32[2,256,128]{2,1,0:T(8,128)S(1)}, f32[2,256,128]{2,1,0:T(8,128)S(1)}, u32[]{:S(2)}, u32[]{:S(2)}) collective-permute-start(f32[2,256,128]{2,1,0:T(8,128)S(1)} %get-tuple-element.22), channel_id=1, source_target_pairs={{1,0},{2,1},{3,2},{4,3},{5,4},{6,5},{7,6},{8,7},{9,8},{10,9},{11,1... | collective-permute-start | bytes 786440 | tf_op jit(solution)/shard_map/ppermute | solution.py:281
  9.7 1.2 %collective-permute-done.low_ref = f32[2,256,128]{2,1,0:T(8,128)S(1)} collective-permute-done((f32[2,256,128]{2,1,0:T(8,128)S(1)}, f32[2,256,128]{2,1,0:T(8,128)S(1)}, u32[]{:S(2)}, u32[]{:S(2)}) %collective-permute-start) | collective-permute-done | bytes 262176 | tf_op jit(solution)/shard_map/ppermute | solution.py:281
  10.9 6.0 %collective-permute-done.1.high_ref = f32[2,256,128]{2,1,0:T(8,128)S(1)} collective-permute-done((f32[2,256,128]{2,1,0:T(8,128)S(1)}, f32[2,256,128]{2,1,0:T(8,128)S(1)}, u32[]{:S(2)}, u32[]{:S(2)}) %collective-permute-start.1) | collective-permute-done | bytes 262176 | tf_op jit(solution)/shard_map/ppermute | solution.py:281
  16.9 0.8 shard_map.87
  17.7 3.6 %collective-permute-start.2 = (f32[2,6,64,128]{3,2,1,0:T(8,128)}, f32[2,6,64,128]{3,2,1,0:T(8,128)S(1)}, u32[]{:S(2)}, u32[]{:S(2)}) collective-permute-start(f32[2,6,64,128]{3,2,1,0:T(8,128)} %get-tuple-element.23), channel_id=1, source_target_pairs={{0,16},{1,17},{2,18},{3,19},{4,20},{5,21},{6,22},{7,23},{8,24},{9,... | collective-permute-start | bytes 1179656 | tf_op jit(solution)/shard_map/ppermute | solution.py:281
  21.3 1.3 %collective-permute-start.3 = (f32[2,6,64,128]{3,2,1,0:T(8,128)S(1)}, f32[2,6,64,128]{3,2,1,0:T(8,128)S(1)}, u32[]{:S(2)}, u32[]{:S(2)}) collective-permute-start(f32[2,6,64,128]{3,2,1,0:T(8,128)S(1)} %get-tuple-element.24), channel_id=1, source_target_pairs={{16,0},{17,1},{18,2},{19,3},{20,4},{21,5},{22,6},{23,7},{24,8},{25... | collective-permute-start | bytes 1179656 | tf_op jit(solution)/shard_map/ppermute | solution.py:281
  23.2 5.7 %collective-permute-done.2.up_ref = f32[2,6,64,128]{3,2,1,0:T(8,128)S(1)} collective-permute-done((f32[2,6,64,128]{3,2,1,0:T(8,128)}, f32[2,6,64,128]{3,2,1,0:T(8,128)S(1)}, u32[]{:S(2)}, u32[]{:S(2)}) %collective-permute-start.2) | collective-permute-done | bytes 393248 | tf_op jit(solution)/shard_map/ppermute | solution.py:281
  28.9 3.8 %collective-permute-done.3.down_ref = f32[2,6,64,128]{3,2,1,0:T(8,128)S(1)} collective-permute-done((f32[2,6,64,128]{3,2,1,0:T(8,128)S(1)}, f32[2,6,64,128]{3,2,1,0:T(8,128)S(1)}, u32[]{:S(2)}, u32[]{:S(2)}) %collective-permute-start.3) | collective-permute-done | bytes 393248 | tf_op jit(solution)/shard_map/ppermute | solution.py:281
  32.7 0.0 copy-start.4
  32.7 0.0 copy-start.5
  32.7 0.0 copy-done.3
  32.7 0.0 copy-done.1
  32.7 0.0 copy-done.2
  32.7 0.6 copy-done.4
  33.4 0.0 copy-done.5
  33.4 13.7 %shard_map.88 = (f32[2,2,256,256]{3,2,1,0:T(8,128)S(1)}, f32[2,6,64,128]{3,2,1,0:T(8,128)S(1)}, f32[2,6,64,128]{3,2,1,0:T(8,128)S(1)}, f32[2,256,128]{2,1,0:T(8,...) custom-call(s32[1,8]{1,0:T(1,128)S(1)} %copy-done.4, s32[1,8]{1,0:T(1,128)S(1)} %copy-done.5, ...), custom_call_target="tpu_custom_call" | custom-call | tf_op jit(solution)/shard_map/pallas_call | solution.py:290
  47.1 0.1 collective-permute-start.4
  47.2 1.2 %collective-permute-done.4 = f32[128,128]{1,0:T(8,128)S(1)} collective-permute-done((f32[128,128]{1,0:T(8,128)S(1)}, f32[128,128]{1,0:T(8,128)S(1)}, u32[]{:S(2)}, u32[]{:S(2)}) %collective-permute-start.4) | collective-permute-done | bytes 65568 | tf_op jit(solution)/shard_map/ppermute | solution.py:286
  48.5 3.5 %collective-permute-start.5 = (f32[2,6,64,128]{3,2,1,0:T(8,128)S(1)}, f32[2,6,64,128]{3,2,1,0:T(8,128)S(1)}, u32[]{:S(2)}, u32[]{:S(2)}) collective-permute-start(f32[2,6,64,128]{3,2,1,0:T(8,128)S(1)} %get-tuple-element.30), channel_id=1, source_target_pairs={{0,16},{1,17},{2,18},{3,19},{4,20},{5,21},{6,22},{7,23},{8,24},{9,... | collective-permute-start | bytes 1179656 | tf_op jit(solution)/shard_map/ppermute | solution.py:281
  52.0 1.3 %collective-permute-start.6 = (f32[2,6,64,128]{3,2,1,0:T(8,128)S(1)}, f32[2,6,64,128]{3,2,1,0:T(8,128)S(1)}, u32[]{:S(2)}, u32[]{:S(2)}) collective-permute-start(f32[2,6,64,128]{3,2,1,0:T(8,128)S(1)} %get-tuple-element.31), channel_id=1, source_target_pairs={{16,0},{17,1},{18,2},{19,3},{20,4},{21,5},{22,6},{23,7},{24,8},{25... | collective-permute-start | bytes 1179656 | tf_op jit(solution)/shard_map/ppermute | solution.py:281
  53.3 0.6 collective-permute-start.7
  54.0 2.6 %collective-permute-done.7 = f32[128,128]{1,0:T(8,128)S(1)} collective-permute-done((f32[128,128]{1,0:T(8,128)S(1)}, f32[128,128]{1,0:T(8,128)S(1)}, u32[]{:S(2)}, u32[]{:S(2)}) %collective-permute-start.7) | collective-permute-done | bytes 65568 | tf_op jit(solution)/shard_map/ppermute | solution.py:286
  56.5 0.5 collective-permute-start.8
  57.0 4.0 %collective-permute-done.8 = f32[128,128]{1,0:T(8,128)S(1)} collective-permute-done((f32[128,128]{1,0:T(8,128)S(1)}, f32[128,128]{1,0:T(8,128)S(1)}, u32[]{:S(2)}, u32[]{:S(2)}) %collective-permute-start.8) | collective-permute-done | bytes 65568 | tf_op jit(solution)/shard_map/ppermute | solution.py:286
  61.0 6.3 %collective-permute-start.9 = (f32[128,128]{1,0:T(8,128)S(1)}, f32[128,128]{1,0:T(8,128)S(1)}, u32[]{:S(2)}, u32[]{:S(2)}) collective-permute-start(f32[128,128]{1,0:T(8,128)S(1)} %add.26), channel_id=1, source_target_pairs={{0,128},{1,129},{2,130},{3,131},{4,132},{5,133},{6,134},{7,135},{8... | collective-permute-start | bytes 196616 | tf_op jit(solution)/shard_map/ppermute | solution.py:286
  67.3 1.7 %collective-permute-done.9 = f32[128,128]{1,0:T(8,128)S(1)} collective-permute-done((f32[128,128]{1,0:T(8,128)S(1)}, f32[128,128]{1,0:T(8,128)S(1)}, u32[]{:S(2)}, u32[]{:S(2)}) %collective-permute-start.9) | collective-permute-done | bytes 65568 | tf_op jit(solution)/shard_map/ppermute | solution.py:286
  69.0 1.6 %collective-permute-start.10 = (f32[128,128]{1,0:T(8,128)S(1)}, f32[128,128]{1,0:T(8,128)S(1)}, u32[]{:S(2)}, u32[]{:S(2)}) collective-permute-start(f32[128,128]{1,0:T(8,128)S(1)} %add.27), channel_id=1, source_target_pairs={{0,130},{1,131},{2,128},{3,129},{4,134},{5,135},{6,132},{7,133},{8... | collective-permute-start | bytes 196616 | tf_op jit(solution)/shard_map/ppermute | solution.py:286
  70.6 2.8 %collective-permute-done.10 = f32[128,128]{1,0:T(8,128)S(1)} collective-permute-done((f32[128,128]{1,0:T(8,128)S(1)}, f32[128,128]{1,0:T(8,128)S(1)}, u32[]{:S(2)}, u32[]{:S(2)}) %collective-permute-start.10) | collective-permute-done | bytes 65568 | tf_op jit(solution)/shard_map/ppermute | solution.py:286
  73.4 0.0 collective-permute-done.5.up_ref
  73.4 0.0 collective-permute-done.6.down_ref
  73.4 0.1 shard_map.89
  73.5 0.1 collective-permute-start.13
  73.6 6.8 %collective-permute-start.11 = (f32[2,256,128]{2,1,0:T(8,128)S(1)}, f32[2,256,128]{2,1,0:T(8,128)S(1)}, u32[]{:S(2)}, u32[]{:S(2)}) collective-permute-start(f32[2,256,128]{2,1,0:T(8,128)S(1)} %get-tuple-element.37), channel_id=1, source_target_pairs={{0,1},{1,2},{2,3},{3,4},{4,5},{5,6},{6,7},{7,8},{8,9},{9,10},{10,1... | collective-permute-start | bytes 786440 | tf_op jit(solution)/shard_map/ppermute | solution.py:281
  80.4 1.9 %collective-permute-start.12 = (f32[2,256,128]{2,1,0:T(8,128)S(1)}, f32[2,256,128]{2,1,0:T(8,128)S(1)}, u32[]{:S(2)}, u32[]{:S(2)}) collective-permute-start(f32[2,256,128]{2,1,0:T(8,128)S(1)} %get-tuple-element.38), channel_id=1, source_target_pairs={{1,0},{2,1},{3,2},{4,3},{5,4},{6,5},{7,6},{8,7},{9,8},{10,9},{11,1... | collective-permute-start | bytes 786440 | tf_op jit(solution)/shard_map/ppermute | solution.py:281
  82.3 0.0 collective-permute-done.13
  82.4 3.6 %collective-permute-start.14 = (f32[128,128]{1,0:T(8,128)S(1)}, f32[128,128]{1,0:T(8,128)S(1)}, u32[]{:S(2)}, u32[]{:S(2)}) collective-permute-start(f32[128,128]{1,0:T(8,128)S(1)} %add.29), channel_id=1, source_target_pairs={{0,32},{1,33},{2,34},{3,35},{4,36},{5,37},{6,38},{7,39},{8,40},{9,... | collective-permute-start | bytes 196616 | tf_op jit(solution)/shard_map/ppermute | solution.py:286
  86.0 2.4 %collective-permute-done.14 = f32[128,128]{1,0:T(8,128)S(1)} collective-permute-done((f32[128,128]{1,0:T(8,128)S(1)}, f32[128,128]{1,0:T(8,128)S(1)}, u32[]{:S(2)}, u32[]{:S(2)}) %collective-permute-start.14) | collective-permute-done | bytes 65568 | tf_op jit(solution)/shard_map/ppermute | solution.py:286
  88.4 1.7 %collective-permute-start.15 = (f32[128,128]{1,0:T(8,128)S(1)}, f32[128,128]{1,0:T(8,128)S(1)}, u32[]{:S(2)}, u32[]{:S(2)}) collective-permute-start(f32[128,128]{1,0:T(8,128)S(1)} %add.30), channel_id=1, source_target_pairs={{0,96},{1,97},{2,98},{3,99},{4,100},{5,101},{6,102},{7,103},{8,104... | collective-permute-start | bytes 196616 | tf_op jit(solution)/shard_map/ppermute | solution.py:286
  90.1 3.6 %collective-permute-done.15 = f32[128,128]{1,0:T(8,128)S(1)} collective-permute-done((f32[128,128]{1,0:T(8,128)S(1)}, f32[128,128]{1,0:T(8,128)S(1)}, u32[]{:S(2)}, u32[]{:S(2)}) %collective-permute-start.15) | collective-permute-done | bytes 65568 | tf_op jit(solution)/shard_map/ppermute | solution.py:286
  93.7 6.0 %collective-permute-start.16 = (f32[128,128]{1,0:T(8,128)S(1)}, f32[128,128]{1,0:T(8,128)S(1)}, u32[]{:S(2)}, u32[]{:S(2)}) collective-permute-start(f32[128,128]{1,0:T(8,128)S(1)} %add.31.mine_ref), channel_id=1, source_target_pairs={{0,1},{1,0},{2,3},{3,2},{4,5},{5,4},{6,7},{7,6},{8,9},{9,8},{10,11... | collective-permute-start | bytes 196616 | tf_op jit(solution)/shard_map/ppermute | solution.py:286
  99.7 0.0 collective-permute-done.11.low_ref
  99.7 0.0 collective-permute-done.12.high_ref
  99.7 0.9 collective-permute-done.16.other_ref
  100.6 1.3 %shard_map.90 = (f32[2,2,256,256]{3,2,1,0:T(8,128)}, f32[2,128,128]{2,1,0:T(8,128)}) custom-call(s32[1,1]{1,0:T(1,128)} %bitcast.core_ref, f32[2,2,256,256]{3,2,1,0:T(8,128)S(1)} %get-tuple-element.25.part_ref, f32[2,6,64,128]{3,2,1,0:T(8,128)S(1)} %collective-permute-done.5.up_ref, f32[2,6,64,128]{3,2,1,0:T(8,128)S(1)} %collective-permute-done.6.down_ref, ...), custom_call_target="tpu_custom_call" | custom-call | tf_op jit(solution)/shard_map/pallas_call | solution.py:290
  (8 shorter events, 0.1 us)
Async XLA Ops:
  0.6 1.2 %copy-start = (f32[2,2,256,256]{3,2,1,0:T(8,128)S(1)}, f32[2,2,256,256]{3,2,1,0:T(8,128)}, u32[]{:S(2)}) copy-start(f32[2,2,256,256]{3,2,1,0:T(8,128)} %obj_ref.5) | copy-start | bytes 3145732
  1.9 30.9 %copy-start.3 = (f32[2,128,128]{2,1,0:T(8,128)S(1)}, f32[2,128,128]{2,1,0:T(8,128)}, u32[]{:S(2)}) copy-start(f32[2,128,128]{2,1,0:T(8,128)} %probe_ref.3) | copy-start | bytes 393220
  2.1 30.7 %copy-start.1 = (f32[2,2,256,256]{3,2,1,0:T(8,128)S(1)}, f32[2,2,256,256]{3,2,1,0:T(8,128)}, u32[]{:S(2)}) copy-start(f32[2,2,256,256]{3,2,1,0:T(8,128)} %obj_ref.5) | copy-start | bytes 3145732
  2.1 8.8 %collective-permute-start = (f32[2,256,128]{2,1,0:T(8,128)S(1)}, f32[2,256,128]{2,1,0:T(8,128)S(1)}, u32[]{:S(2)}, u32[]{:S(2)}) collective-permute-start(f32[2,256,128]{2,1,0:T(8,128)S(1)} %get-tuple-element.21), channel_id=1, source_target_pairs={{0,1},{1,2},{2,3},{3,4},{4,5},{5,6},{6,7},{7,8},{8,9},{9,10},{10,1... | collective-permute-start | bytes 786440 | tf_op jit(solution)/shard_map/ppermute | solution.py:281
  7.6 25.1 %copy-start.2 = (f32[1,8,128,128]{3,2,1,0:T(8,128)S(1)}, f32[1,8,128,128]{3,2,1,0:T(8,128)}, u32[]{:S(2)}) copy-start(f32[1,8,128,128]{3,2,1,0:T(8,128)} %param.9) | copy-start | bytes 1572868
  7.6 9.3 %collective-permute-start.1 = (f32[2,256,128]{2,1,0:T(8,128)S(1)}, f32[2,256,128]{2,1,0:T(8,128)S(1)}, u32[]{:S(2)}, u32[]{:S(2)}) collective-permute-start(f32[2,256,128]{2,1,0:T(8,128)S(1)} %get-tuple-element.22), channel_id=1, source_target_pairs={{1,0},{2,1},{3,2},{4,3},{5,4},{6,5},{7,6},{8,7},{9,8},{10,9},{11,1... | collective-permute-start | bytes 786440 | tf_op jit(solution)/shard_map/ppermute | solution.py:281
  17.7 11.2 %collective-permute-start.2 = (f32[2,6,64,128]{3,2,1,0:T(8,128)}, f32[2,6,64,128]{3,2,1,0:T(8,128)S(1)}, u32[]{:S(2)}, u32[]{:S(2)}) collective-permute-start(f32[2,6,64,128]{3,2,1,0:T(8,128)} %get-tuple-element.23), channel_id=1, source_target_pairs={{0,16},{1,17},{2,18},{3,19},{4,20},{5,21},{6,22},{7,23},{8,24},{9,... | collective-permute-start | bytes 1179656 | tf_op jit(solution)/shard_map/ppermute | solution.py:281
  21.3 11.4 %collective-permute-start.3 = (f32[2,6,64,128]{3,2,1,0:T(8,128)S(1)}, f32[2,6,64,128]{3,2,1,0:T(8,128)S(1)}, u32[]{:S(2)}, u32[]{:S(2)}) collective-permute-start(f32[2,6,64,128]{3,2,1,0:T(8,128)S(1)} %get-tuple-element.24), channel_id=1, source_target_pairs={{16,0},{17,1},{18,2},{19,3},{20,4},{21,5},{22,6},{23,7},{24,8},{25... | collective-permute-start | bytes 1179656 | tf_op jit(solution)/shard_map/ppermute | solution.py:281
  32.7 0.7 copy-start.4
  32.7 0.7 copy-start.5
  47.1 1.3 %collective-permute-start.4 = (f32[128,128]{1,0:T(8,128)S(1)}, f32[128,128]{1,0:T(8,128)S(1)}, u32[]{:S(2)}, u32[]{:S(2)}) collective-permute-start(f32[128,128]{1,0:T(8,128)S(1)} %get-tuple-element.27), channel_id=1, source_target_pairs={{0,1},{1,0},{2,3},{3,2},{4,5},{5,4},{6,7},{7,6},{8,9},{9,8},{10,11... | collective-permute-start | bytes 196616 | tf_op jit(solution)/shard_map/ppermute | solution.py:286
  48.5 24.9 %collective-permute-start.5 = (f32[2,6,64,128]{3,2,1,0:T(8,128)S(1)}, f32[2,6,64,128]{3,2,1,0:T(8,128)S(1)}, u32[]{:S(2)}, u32[]{:S(2)}) collective-permute-start(f32[2,6,64,128]{3,2,1,0:T(8,128)S(1)} %get-tuple-element.30), channel_id=1, source_target_pairs={{0,16},{1,17},{2,18},{3,19},{4,20},{5,21},{6,22},{7,23},{8,24},{9,... | collective-permute-start | bytes 1179656 | tf_op jit(solution)/shard_map/ppermute | solution.py:281
  52.0 21.4 %collective-permute-start.6 = (f32[2,6,64,128]{3,2,1,0:T(8,128)S(1)}, f32[2,6,64,128]{3,2,1,0:T(8,128)S(1)}, u32[]{:S(2)}, u32[]{:S(2)}) collective-permute-start(f32[2,6,64,128]{3,2,1,0:T(8,128)S(1)} %get-tuple-element.31), channel_id=1, source_target_pairs={{16,0},{17,1},{18,2},{19,3},{20,4},{21,5},{22,6},{23,7},{24,8},{25... | collective-permute-start | bytes 1179656 | tf_op jit(solution)/shard_map/ppermute | solution.py:281
  53.3 3.2 %collective-permute-start.7 = (f32[128,128]{1,0:T(8,128)S(1)}, f32[128,128]{1,0:T(8,128)S(1)}, u32[]{:S(2)}, u32[]{:S(2)}) collective-permute-start(f32[128,128]{1,0:T(8,128)S(1)} %add.24), channel_id=1, source_target_pairs={{0,4},{1,5},{2,6},{3,7},{4,0},{5,1},{6,2},{7,3},{8,12},{9,13},{10,... | collective-permute-start | bytes 196616 | tf_op jit(solution)/shard_map/ppermute | solution.py:286
  56.5 4.4 %collective-permute-start.8 = (f32[128,128]{1,0:T(8,128)S(1)}, f32[128,128]{1,0:T(8,128)S(1)}, u32[]{:S(2)}, u32[]{:S(2)}) collective-permute-start(f32[128,128]{1,0:T(8,128)S(1)} %add.25), channel_id=1, source_target_pairs={{0,12},{1,13},{2,14},{3,15},{4,8},{5,9},{6,10},{7,11},{8,4},{9,5},... | collective-permute-start | bytes 196616 | tf_op jit(solution)/shard_map/ppermute | solution.py:286
  61.0 8.0 %collective-permute-start.9 = (f32[128,128]{1,0:T(8,128)S(1)}, f32[128,128]{1,0:T(8,128)S(1)}, u32[]{:S(2)}, u32[]{:S(2)}) collective-permute-start(f32[128,128]{1,0:T(8,128)S(1)} %add.26), channel_id=1, source_target_pairs={{0,128},{1,129},{2,130},{3,131},{4,132},{5,133},{6,134},{7,135},{8... | collective-permute-start | bytes 196616 | tf_op jit(solution)/shard_map/ppermute | solution.py:286
  69.0 4.4 %collective-permute-start.10 = (f32[128,128]{1,0:T(8,128)S(1)}, f32[128,128]{1,0:T(8,128)S(1)}, u32[]{:S(2)}, u32[]{:S(2)}) collective-permute-start(f32[128,128]{1,0:T(8,128)S(1)} %add.27), channel_id=1, source_target_pairs={{0,130},{1,131},{2,128},{3,129},{4,134},{5,135},{6,132},{7,133},{8... | collective-permute-start | bytes 196616 | tf_op jit(solution)/shard_map/ppermute | solution.py:286
  73.5 8.9 %collective-permute-start.13 = (f32[128,128]{1,0:T(8,128)S(1)}, f32[128,128]{1,0:T(8,128)S(1)}, u32[]{:S(2)}, u32[]{:S(2)}) collective-permute-start(f32[128,128]{1,0:T(8,128)S(1)} %add.28), channel_id=1, source_target_pairs={{0,16},{1,17},{2,18},{3,19},{4,20},{5,21},{6,22},{7,23},{8,24},{9,... | collective-permute-start | bytes 196616 | tf_op jit(solution)/shard_map/ppermute | solution.py:286
  73.6 26.2 %collective-permute-start.11 = (f32[2,256,128]{2,1,0:T(8,128)S(1)}, f32[2,256,128]{2,1,0:T(8,128)S(1)}, u32[]{:S(2)}, u32[]{:S(2)}) collective-permute-start(f32[2,256,128]{2,1,0:T(8,128)S(1)} %get-tuple-element.37), channel_id=1, source_target_pairs={{0,1},{1,2},{2,3},{3,4},{4,5},{5,6},{6,7},{7,8},{8,9},{9,10},{10,1... | collective-permute-start | bytes 786440 | tf_op jit(solution)/shard_map/ppermute | solution.py:281
  80.4 19.3 %collective-permute-start.12 = (f32[2,256,128]{2,1,0:T(8,128)S(1)}, f32[2,256,128]{2,1,0:T(8,128)S(1)}, u32[]{:S(2)}, u32[]{:S(2)}) collective-permute-start(f32[2,256,128]{2,1,0:T(8,128)S(1)} %get-tuple-element.38), channel_id=1, source_target_pairs={{1,0},{2,1},{3,2},{4,3},{5,4},{6,5},{7,6},{8,7},{9,8},{10,9},{11,1... | collective-permute-start | bytes 786440 | tf_op jit(solution)/shard_map/ppermute | solution.py:281
  82.4 6.0 %collective-permute-start.14 = (f32[128,128]{1,0:T(8,128)S(1)}, f32[128,128]{1,0:T(8,128)S(1)}, u32[]{:S(2)}, u32[]{:S(2)}) collective-permute-start(f32[128,128]{1,0:T(8,128)S(1)} %add.29), channel_id=1, source_target_pairs={{0,32},{1,33},{2,34},{3,35},{4,36},{5,37},{6,38},{7,39},{8,40},{9,... | collective-permute-start | bytes 196616 | tf_op jit(solution)/shard_map/ppermute | solution.py:286
  88.4 5.3 %collective-permute-start.15 = (f32[128,128]{1,0:T(8,128)S(1)}, f32[128,128]{1,0:T(8,128)S(1)}, u32[]{:S(2)}, u32[]{:S(2)}) collective-permute-start(f32[128,128]{1,0:T(8,128)S(1)} %add.30), channel_id=1, source_target_pairs={{0,96},{1,97},{2,98},{3,99},{4,100},{5,101},{6,102},{7,103},{8,104... | collective-permute-start | bytes 196616 | tf_op jit(solution)/shard_map/ppermute | solution.py:286
  93.7 6.9 %collective-permute-start.16 = (f32[128,128]{1,0:T(8,128)S(1)}, f32[128,128]{1,0:T(8,128)S(1)}, u32[]{:S(2)}, u32[]{:S(2)}) collective-permute-start(f32[128,128]{1,0:T(8,128)S(1)} %add.31.mine_ref), channel_id=1, source_target_pairs={{0,1},{1,0},{2,3},{3,2},{4,5},{5,4},{6,7},{7,6},{8,9},{9,8},{10,11... | collective-permute-start | bytes 196616 | tf_op jit(solution)/shard_map/ppermute | solution.py:286

commit v3 on v2

v3 whole, which is shorter than its diff:
```python
import functools
import math

import jax
import jax.numpy as jnp
import ml_dtypes
import numpy as np
from jax import lax
from jax.experimental import pallas as pl
from jax.experimental.pallas import tpu as pltpu
from jax.sharding import PartitionSpec as P

STEP_OBJECT = 0.03
STEP_PROBE = 2.0
FRESNEL_PHASE = 60.0
LANES = 128
BOTH = ("row", "col")
GRANT = 48 * 1024 * 1024
MASKS = (4, 12, 128, 130, 16, 32, 96)


def split_table(table):
    high = table.astype(ml_dtypes.bfloat16)
    low = (table - high.astype(np.float64)).astype(ml_dtypes.bfloat16)
    return high, low


def make_tables(width):
    index = np.arange(width)
    four = np.exp(-2j * math.pi * (np.outer(index, index) % width) / width) / math.sqrt(width)
    freq = np.where(index < width // 2, index, index - width) / width
    hop = np.conj(four) @ np.diag(np.exp(-1j * FRESNEL_PHASE * freq**2)) @ four
    forms = []
    for table in (hop, four):
        forms.append(np.block([[table.real, table.imag], [-table.imag, table.real]]))
        forms.append(np.block([[table.real, -table.imag], [table.imag, table.real]]))
    pairs = [split_table(form) for form in forms]
    return np.stack([np.stack(pair) for pair in pairs])


def split(value):
    high = value.astype(jnp.bfloat16)
    low = (value - high.astype(jnp.float32)).astype(jnp.bfloat16)
    return high, low


def mul3(left, right):
    dot = functools.partial(jnp.dot, preferred_element_type=jnp.float32)
    return dot(left[0], right[0]) + (dot(left[1], right[0]) + dot(left[0], right[1]))


def two_sided(tabs_ref, right, left, real, imag):
    width = real.shape[1]
    field = split(jnp.concatenate([real, imag], axis=1))
    half = mul3(field, (tabs_ref[right, 0], tabs_ref[right, 1]))
    real, imag = half[:, :width], half[:, width:]
    field = jnp.concatenate(
        [
            jnp.concatenate([real[:width], real[width:]], axis=1),
            jnp.concatenate([imag[:width], imag[width:]], axis=1),
        ],
        axis=0,
    )
    full = mul3((tabs_ref[left, 0], tabs_ref[left, 1]), split(field))
    real = jnp.concatenate([full[:width, :width], full[:width, width:]], axis=0)
    imag = jnp.concatenate([full[width:, :width], full[width:, width:]], axis=0)
    return real, imag


def columns(piece_ref, first):
    half = LANES // 2
    left = jnp.where(first, piece_ref[0, :, :LANES], pltpu.roll(piece_ref[1, :, :LANES], half, 1))
    right = jnp.where(first, pltpu.roll(piece_ref[0, :, LANES:], half, 1), piece_ref[1, :, LANES:])
    return left, right


def pick(spot_ref, axis, even, odd):
    return jnp.where(spot_ref[0, axis] == 0, even, odd)


def pack_kernel(spot_ref, obj_ref, *outs):
    first = lax.broadcasted_iota(jnp.int32, (obj_ref.shape[2], LANES), 1) < LANES // 2
    for piece in range(2):
        left, right = columns(obj_ref.at[piece], first)
        outs[2 * piece][...] = pick(spot_ref, 1, right, left)
        outs[2 * piece + 1][...] = pick(spot_ref, 1, left, right)


def rows_kernel(spot_ref, obj_ref, cola_ref, colb_ref, rowa_ref, rowb_ref, *, piece):
    half = LANES // 2
    low, high = slice(0, half), slice(obj_ref.shape[2] - half, obj_ref.shape[2])
    for part in range(2):
        for block in range(2):
            cols = slice(block * LANES, (block + 1) * LANES)
            top, bottom = obj_ref[piece, part, low, cols], obj_ref[piece, part, high, cols]
            rowa_ref[2 * part + block] = pick(spot_ref, 0, bottom, top)
            rowb_ref[2 * part + block] = pick(spot_ref, 0, top, bottom)
    for place, east in ((4, False), (5, True)):
        even, odd = (cola_ref, colb_ref) if east else (colb_ref, cola_ref)
        top = pick(spot_ref, 1, even[low], odd[low])
        bottom = pick(spot_ref, 1, even[high], odd[high])
        rowa_ref[place] = pick(spot_ref, 0, bottom, top)
        rowb_ref[place] = pick(spot_ref, 0, top, bottom)


def grow(ext, spot_ref, piece_ref, cola_ref, colb_ref, rowa_ref, rowb_ref):
    half = LANES // 2
    tile = piece_ref.shape[1]
    for part in range(2):
        for block in range(4):
            place = 2 * part + block - 1 if block in (1, 2) else 4 + block // 3
            top = pick(spot_ref, 0, rowb_ref[place], rowa_ref[place])
            bottom = pick(spot_ref, 0, rowa_ref[place], rowb_ref[place])
            if block in (1, 2):
                middle = piece_ref[part, :, (block - 1) * LANES : block * LANES]
            elif block == 0:
                middle = pick(spot_ref, 1, colb_ref[...], cola_ref[...])
            else:
                middle = pick(spot_ref, 1, cola_ref[...], colb_ref[...])
            for strip, start in ((top, 0), (middle, half), (bottom, half + tile)):
                if (block == 0 and part == 0) or (block == 3 and part == 1):
                    strip = pltpu.roll(strip, half, 1)
                ext[part, block, start : start + strip.shape[0]] = strip


def place_window(row_ref, col_ref, slot):
    col = col_ref[0, slot] + LANES // 2
    return row_ref[0, slot], col // LANES, lax.rem(col, LANES)


def window(ext, row_ref, col_ref, slot, width):
    row, block, shift = place_window(row_ref, col_ref, slot)
    back = lax.rem(LANES - shift, LANES)
    keep = lax.broadcasted_iota(jnp.int32, (width, LANES), 1) < LANES - shift
    parts = []
    for part in range(2):
        near = pltpu.roll(ext[part, block, pl.ds(row, width), :], back, 1)
        far = pltpu.roll(ext[part, block + 1, pl.ds(row, width), :], back, 1)
        parts.append(jnp.where(keep, near, far))
    return parts


def windows(ext, row_ref, col_ref, slots, width):
    got = [window(ext, row_ref, col_ref, slot, width) for slot in slots]
    return tuple(jnp.concatenate([g[part] for g in got], axis=0) for part in range(2))


def stacked(ref, slots, part):
    return jnp.concatenate([ref[slot, part] for slot in slots], axis=0)


def store(ref, slots, values):
    width = ref.shape[2]
    for place, slot in enumerate(slots):
        for part in range(2):
            ref[slot, part] = values[part][place * width : (place + 1) * width]


def first_kernel(
    row_ref, col_ref, spot_ref, obj_ref, cola_ref, colb_ref, rowa_ref, rowb_ref, probe_ref, tabs_ref,
    win_ref, mid_ref, ext,
):
    width = probe_ref.shape[1]
    grow(ext, spot_ref, obj_ref.at[0], cola_ref, colb_ref, rowa_ref, rowb_ref)

    def pair(index, _):
        slots = (2 * index, 2 * index + 1)
        first_re, first_im = windows(ext, row_ref, col_ref, slots, width)
        probe_re, probe_im = (jnp.concatenate([probe_ref[p]] * 2, axis=0) for p in range(2))
        wave_re = probe_re * first_re - probe_im * first_im
        wave_im = probe_re * first_im + probe_im * first_re
        store(win_ref, slots, (first_re, first_im))
        store(mid_ref, slots, two_sided(tabs_ref, 0, 1, wave_re, wave_im))
        return 0

    lax.fori_loop(0, row_ref.shape[1] // 2, pair, 0)


def second_kernel(
    row_ref, col_ref, spot_ref, live_ref, obj_ref, cola_ref, colb_ref, rowa_ref, rowb_ref,
    win_ref, mid_ref, measured_ref, tabs_ref,
    grad_ref, down_ref, keep_ref, send_ref,
    ext, sum_ref,
):
    width = win_ref.shape[2]
    grow(ext, spot_ref, obj_ref.at[1], cola_ref, colb_ref, rowa_ref, rowb_ref)
    sum_ref[...] = jnp.zeros_like(sum_ref)

    def pair(index, _):
        slots = (2 * index, 2 * index + 1)
        second_re, second_im = windows(ext, row_ref, col_ref, slots, width)
        mid_re, mid_im = (stacked(mid_ref, slots, part) for part in range(2))
        exit_re = mid_re * second_re - mid_im * second_im
        exit_im = mid_re * second_im + mid_im * second_re
        far_re, far_im = two_sided(tabs_ref, 2, 3, exit_re, exit_im)
        weights = []
        for place, slot in enumerate(slots):
            rows = slice(place * width, (place + 1) * width)
            active = jnp.where(slot < live_ref[0, 0], 2.0, 0.0)
            power = far_re[rows] * far_re[rows] + far_im[rows] * far_im[rows]
            weights.append((power - measured_ref[slot]) * active)
        weight = jnp.concatenate(weights, axis=0)
        chi_re, chi_im = two_sided(tabs_ref, 3, 2, weight * far_re, weight * far_im)
        grad_re = mid_re * chi_re + mid_im * chi_im
        grad_im = mid_re * chi_im - mid_im * chi_re
        store(grad_ref, slots, (grad_re, grad_im))
        back_re = second_re * chi_re + second_im * chi_im
        back_im = second_re * chi_im - second_im * chi_re
        down_re, down_im = two_sided(tabs_ref, 1, 0, back_re, back_im)
        store(down_ref, slots, (down_re, down_im))
        first_re, first_im = (stacked(win_ref, slots, part) for part in range(2))
        sum_re = first_re * down_re + first_im * down_im
        sum_im = first_re * down_im - first_im * down_re
        sum_ref[0] += sum_re[:width] + sum_re[width:]
        sum_ref[1] += sum_im[:width] + sum_im[width:]
        return 0

    lax.fori_loop(0, row_ref.shape[1] // 2, pair, 0)
    keep_ref[...] = pick(spot_ref, 1, sum_ref[0], sum_ref[1])
    send_ref[...] = pick(spot_ref, 1, sum_ref[1], sum_ref[0])


def place_kernel(
    row_ref, col_ref, spot_ref, obj_ref, probe_ref, down_ref, second_ref,
    new_ref, rowa_ref, rowb_ref, left_ref, right_ref,
    grad,
):
    width = probe_ref.shape[1]
    tile = obj_ref.shape[2]
    half = width // 2
    grad[...] = jnp.zeros_like(grad)
    lane = lax.broadcasted_iota(jnp.int32, (width, LANES), 1)

    def deposit(slot, _):
        row, block, shift = place_window(row_ref, col_ref, slot)
        keep = lane >= shift
        probe_re, probe_im = probe_ref[0], probe_ref[1]
        down_re, down_im = down_ref[slot, 0], down_ref[slot, 1]
        values = (
            (probe_re * down_re + probe_im * down_im, probe_re * down_im - probe_im * down_re),
            (second_ref[slot, 0], second_ref[slot, 1]),
        )
        for piece in range(2):
            for part in range(2):
                value = pltpu.roll(values[piece][part], shift, 1)
                grad[piece, part, block, pl.ds(row, width), :] += jnp.where(keep, value, 0.0)
                grad[piece, part, block + 1, pl.ds(row, width), :] += jnp.where(keep, 0.0, value)
        return 0

    lax.fori_loop(0, row_ref.shape[1], deposit, 0)
    first = lax.broadcasted_iota(jnp.int32, (tile + width, LANES), 1) < half
    for piece in range(2):
        for part in range(2):
            for block in range(2):
                cols = slice(block * LANES, (block + 1) * LANES)
                top = grad[piece, part, 1 + block, :half]
                bottom = grad[piece, part, 1 + block, half + tile :]
                rowa_ref[piece, 2 * part + block] = pick(spot_ref, 0, bottom, top)
                rowb_ref[piece, 2 * part + block] = pick(spot_ref, 0, top, bottom)
                new_ref[piece, part, :, cols] = (
                    obj_ref[piece, part, :, cols]
                    - STEP_OBJECT * grad[piece, part, 1 + block, half : half + tile]
                )
        left = jnp.where(first, pltpu.roll(grad[piece, 0, 0], half, 1), grad[piece, 1, 0])
        right = jnp.where(first, grad[piece, 0, 3], pltpu.roll(grad[piece, 1, 3], half, 1))
        for place, strip, ref in ((4, left, left_ref), (5, right, right_ref)):
            top, bottom = strip[:half], strip[half + tile :]
            rowa_ref[piece, place] = pick(spot_ref, 0, bottom, top)
            rowb_ref[piece, place] = pick(spot_ref, 0, top, bottom)
            ref[piece] = strip[half : half + tile]


def fold_kernel(spot_ref, left_ref, right_ref, rowa_ref, rowb_ref, cola_ref, colb_ref):
    half = LANES // 2
    tile = left_ref.shape[1]
    for piece in range(2):
        sides = []
        for ref, place in ((left_ref, 4), (right_ref, 5)):
            a, b = rowa_ref[piece, place], rowb_ref[piece, place]
            sides.append(
                (
                    ref[piece, :half] + pick(spot_ref, 0, b, a),
                    ref[piece, half : tile - half],
                    ref[piece, tile - half :] + pick(spot_ref, 0, a, b),
                )
            )
        for left, right, rows in zip(*sides, (slice(0, half), slice(half, tile - half), slice(tile - half, tile))):
            cola_ref[piece, rows] = pick(spot_ref, 1, right, left)
            colb_ref[piece, rows] = pick(spot_ref, 1, left, right)


def finish_kernel(
    spot_ref, part_ref, rowa_ref, rowb_ref, cola_ref, colb_ref, probe_ref, mine_ref, other_ref,
    new_ref, newp_ref, *, scale,
):
    tile = part_ref.shape[2]
    half = LANES // 2
    first = lax.broadcasted_iota(jnp.int32, (half, LANES), 1) < half
    newp_ref[0] = probe_ref[0] - scale * pick(spot_ref, 1, mine_ref[...], other_ref[...])
    newp_ref[1] = probe_ref[1] - scale * pick(spot_ref, 1, other_ref[...], mine_ref[...])
    for piece in range(2):
        for start in range(0, tile, half):
            rows = slice(start, start + half)
            cola, colb = cola_ref[piece, rows], colb_ref[piece, rows]
            sides = (pick(spot_ref, 1, colb, cola), pick(spot_ref, 1, cola, colb))
            for part in range(2):
                for block in range(2):
                    cols = slice(block * LANES, (block + 1) * LANES)
                    total = sides[block]
                    if block != part:
                        total = pltpu.roll(total, half, 1)
                    total = jnp.where(first == (block == 0), total, 0.0)
                    a, b = rowa_ref[piece, 2 * part + block], rowb_ref[piece, 2 * part + block]
                    if start == 0:
                        total += pick(spot_ref, 0, b, a)
                    if start == tile - half:
                        total += pick(spot_ref, 0, a, b)
                    new_ref[piece, part, rows, cols] = (
                        part_ref[piece, part, rows, cols] - STEP_OBJECT * total
                    )


def vmem(count):
    return [pl.BlockSpec(memory_space=pltpu.VMEM)] * count


def smem(count):
    return [pl.BlockSpec(memory_space=pltpu.SMEM)] * count


def array(*shape):
    return jax.ShapeDtypeStruct(shape, jnp.float32)


def meet(strips, axis):
    rows, cols = lax.axis_size("row"), lax.axis_size("col")
    got = []
    for odd, strip in enumerate(strips):
        pairs = []
        for a in range(rows):
            for b in range(cols):
                c, d = (a, b) if axis else (((a + odd) ^ 1) - odd, b)
                if axis:
                    d = ((b + odd) ^ 1) - odd
                if 0 <= c < rows and 0 <= d < cols:
                    pairs.append((a * cols + b, c * cols + d))
        got.append(lax.ppermute(strip, BOTH, pairs))
    return got


def swap(value, mask):
    count = lax.axis_size("row") * lax.axis_size("col")
    return lax.ppermute(value, BOTH, [(i, i ^ mask) for i in range(count)])


def call(kernel, out_shape, scalars, arrays, scratch=()):
    return pl.pallas_call(
        kernel, out_shape=tuple(out_shape), in_specs=smem(len(scalars)) + vmem(len(arrays)),
        out_specs=tuple(vmem(len(out_shape))), scratch_shapes=list(scratch),
        compiler_params=pltpu.CompilerParams(vmem_limit_bytes=GRANT),
    )(*scalars, *arrays)


def on_device(object_field, probe, intensity, offset_row, offset_col, live):
    tile = object_field.shape[2]
    width = probe.shape[1]
    half = width // 2
    count = offset_row.shape[1]
    side, edge, plane = (tile, LANES), (6, half, LANES), (width, width)
    field, fields = array(2, 2, tile, tile), array(count, 2, width, width)
    spot = jnp.stack([lax.axis_index("row"), lax.axis_index("col")]).astype(jnp.int32) % 2
    spot = spot.reshape(1, 2)
    tabs = jnp.asarray(make_tables(width))
    grown = pltpu.VMEM((2, 4, tile + width, LANES), jnp.float32)
    packed = call(pack_kernel, [array(*side)] * 4, (spot,), (object_field,))
    halos = []
    cols = [meet(packed[2 * piece : 2 * piece + 2], 1) for piece in range(2)]
    for piece in range(2):
        strips = call(
            functools.partial(rows_kernel, piece=piece), [array(*edge)] * 2,
            (spot,), (object_field, *cols[piece]),
        )
        halos.append((*cols[piece], *meet(strips, 0)))
    win, mid = call(
        first_kernel, [fields] * 2, (offset_row, offset_col, spot),
        (object_field, *halos[0], probe, tabs), (grown,),
    )
    grad, down, mine, send = call(
        second_kernel, [fields] * 2 + [array(*plane)] * 2, (offset_row, offset_col, spot, live),
        (object_field, *halos[1], win, mid, intensity[0], tabs),
        (grown, pltpu.VMEM((2, *plane), jnp.float32)),
    )
    part, *strips, left, right = call(
        place_kernel, [field] + [array(2, *edge)] * 2 + [array(2, *side)] * 2,
        (offset_row, offset_col, spot), (object_field, probe, down, grad),
        (pltpu.VMEM((2, 2, 4, tile + width, LANES), jnp.float32),),
    )
    mine = mine + swap(send, 1)
    mine = mine + swap(mine, MASKS[0])
    mine, *strips = lax.optimization_barrier((mine, *strips))
    rows = meet(strips, 0)
    for mask in MASKS[1:4]:
        mine = mine + swap(mine, mask)
    strips = call(fold_kernel, [array(2, *side)] * 2, (spot,), (left, right, *rows))
    mine, *strips = lax.optimization_barrier((mine, *strips))
    cols = meet(strips, 1)
    for mask in MASKS[4:]:
        mine = mine + swap(mine, mask)
    other = swap(mine, 1)
    count_all = count * lax.axis_size("row") * lax.axis_size("col")
    return call(
        functools.partial(finish_kernel, scale=STEP_PROBE / count_all),
        (field, array(2, *plane)),
        (spot,),
        (part, *rows, *cols, probe, mine, other),
    )


def solution(mesh):
    placed = (
        P(None, None, "row", "col"),
        P(),
        P("row", "col", None, None),
        P("row", "col"),
        P("row", "col"),
        P("row", "col"),
    )
    return jax.shard_map(
        on_device,
        mesh=mesh,
        in_specs=placed,
        out_specs=(P(None, None, "row", "col"), P()),
        check_vma=False,
    )
```

time: 102 us -> 92 us (0.902)
  the two profiles are of different devices: /device:TPU:7 before, /device:TPU:1 now
where the time goes in v3:
time: 92 us; the launch traced here: 91.6 us
  starting transfers between devices  48.6 us (53%)
  Pallas kernels  20.8 us (23%)
  waiting for transfers between devices  18.3 us (20%)
  local copies, waits for them, and re-layouts  2.21 us (2%)
  between operations  1.57 us (2%)
    ppermute x12, starting transfers between devices, meet(): got.append(lax.ppermute(strip, BOTH, pairs))  25.3 us
    ppermute x9, starting transfers between devices, swap(): return lax.ppermute(value, BOTH, [(i, i ^ mask) for i in range(count)])  23.3 us
    pallas_call x8, Pallas kernels, call(): pl.pallas_call(kernel, out_shape=tuple(out_shape), in_specs=smem(len(scal...  20.8 us
    ppermute x9, waiting for transfers between devices, swap(): return lax.ppermute(value, BOTH, [(i, i ^ mask) for i in range(count)])  16.4 us
    unnamed x14, local copies, waits for them, and re-layouts  2.21 us
    ppermute x12, waiting for transfers between devices, meet(): got.append(lax.ppermute(strip, BOTH, pairs))  1.87 us
  transfers between devices with their start and end apart: 21, of which 9 were waited for; matrix products, arithmetic and copies ran while one was open for 0% of the time, Pallas kernels for 8%

profile of v3, /device:TPU:1, one launch (start us, length us, event | category | flops | bytes accessed | tf_op | source)
XLA Modules:
  0.0 91.6 jit_solution(2406751334867495521)
XLA Ops:
  0.6 0.1 and_select_fusion.spot_ref
  0.7 0.0 copy-start
  0.7 1.2 %copy-done = f32[2,2,256,256]{3,2,1,0:T(8,128)S(1)} copy-done((f32[2,2,256,256]{3,2,1,0:T(8,128)S(1)}, f32[2,2,256,256]{3,2,1,0:T(8,128)}, u32[]{:S(2)}) %copy-start) | copy-done | bytes 1048600
  1.9 0.7 shard_map.86
  2.7 3.3 %collective-permute-start.4 = (f32[256,128]{1,0:T(8,128)S(1)}, f32[256,128]{1,0:T(8,128)S(1)}, u32[]{:S(2)}, u32[]{:S(2)}) collective-permute-start(f32[256,128]{1,0:T(8,128)S(1)} %get-tuple-element.33), channel_id=1, source_target_pairs={{0,1},{1,0},{2,3},{3,2},{4,5},{5,4},{6,7},{7,6},{8,9},{9,8},{10,11... | collective-permute-start | bytes 393224 | tf_op jit(solution)/shard_map/ppermute | solution.py:347
  6.0 3.0 %collective-permute-start.5 = (f32[256,128]{1,0:T(8,128)S(1)}, f32[256,128]{1,0:T(8,128)S(1)}, u32[]{:S(2)}, u32[]{:S(2)}) collective-permute-start(f32[256,128]{1,0:T(8,128)S(1)} %get-tuple-element.34), channel_id=1, source_target_pairs={{1,2},{2,1},{3,4},{4,3},{5,6},{6,5},{7,8},{8,7},{9,10},{10,9},{11,... | collective-permute-start | bytes 393224 | tf_op jit(solution)/shard_map/ppermute | solution.py:347
  9.0 0.1 collective-permute-start
  9.1 0.0 copy-start.1
  9.1 4.2 %collective-permute-start.1 = (f32[256,128]{1,0:T(8,128)S(1)}, f32[256,128]{1,0:T(8,128)S(1)}, u32[]{:S(2)}, u32[]{:S(2)}) collective-permute-start(f32[256,128]{1,0:T(8,128)S(1)} %get-tuple-element.30), channel_id=1, source_target_pairs={{1,2},{2,1},{3,4},{4,3},{5,6},{6,5},{7,8},{8,7},{9,10},{10,9},{11,... | collective-permute-start | bytes 393224 | tf_op jit(solution)/shard_map/ppermute | solution.py:347
  13.3 0.0 collective-permute-done.4.cola_ref
  13.3 0.5 collective-permute-done.5.colb_ref
  13.8 0.6 shard_map.88
  14.4 0.5 collective-permute-start.6
  14.8 0.0 copy-start.2
  14.8 0.8 collective-permute-start.7
  15.6 0.0 collective-permute-done.cola_ref
  15.7 1.4 %collective-permute-done.1.colb_ref = f32[256,128]{1,0:T(8,128)S(1)} collective-permute-done((f32[256,128]{1,0:T(8,128)S(1)}, f32[256,128]{1,0:T(8,128)S(1)}, u32[]{:S(2)}, u32[]{:S(2)}) %collective-permute-start.1) | collective-permute-done | bytes 131104 | tf_op jit(solution)/shard_map/ppermute | solution.py:347
  17.0 0.6 shard_map.87
  17.6 3.2 %collective-permute-start.2 = (f32[6,64,128]{2,1,0:T(8,128)S(1)}, f32[6,64,128]{2,1,0:T(8,128)S(1)}, u32[]{:S(2)}, u32[]{:S(2)}) collective-permute-start(f32[6,64,128]{2,1,0:T(8,128)S(1)} %get-tuple-element.31), channel_id=1, source_target_pairs={{0,16},{1,17},{2,18},{3,19},{4,20},{5,21},{6,22},{7,23},{8,24},{9,... | collective-permute-start | bytes 589832 | tf_op jit(solution)/shard_map/ppermute | solution.py:347
  20.8 0.0 copy-start.5
  20.8 0.8 collective-permute-start.3
  22.3 0.0 copy-start.4
  22.3 0.0 collective-permute-done.6.rowa_ref
  22.3 0.0 collective-permute-done.7.rowb_ref
  22.3 0.0 copy-done.1
  22.3 0.0 copy-done.2
  22.3 0.0 copy-done.5
  22.4 0.0 copy-done.6
  22.4 4.0 %shard_map.89 = (f32[8,2,128,128]{3,2,1,0:T(8,128)S(1)}, f32[8,2,128,128]{3,2,1,0:T(8,128)S(1)}) custom-call(s32[1,8]{1,0:T(1,128)S(1)} %copy-done.5, s32[1,8]{1,0:T(1,128)S(1)} %copy-done.6, s32[1,2]{1,0:T(1,128)S(1)} %and_select_fusion.spot_ref, f32[2,2,256,256]{3,2,1,0:T(8,128)S(1)} %copy-done, f32[256,128]{1,0:T(8,128)S(1)} %collective-permute-done.4.cola_ref, ...), custom_call_target="tpu_custom_call" | custom-call | tf_op jit(solution)/shard_map/pallas_call | solution.py:357
  26.4 0.0 copy-start.3
  26.4 1.0 %copy-done.3 = f32[8,2,128,128]{3,2,1,0:T(8,128)} copy-done((f32[8,2,128,128]{3,2,1,0:T(8,128)}, f32[8,2,128,128]{3,2,1,0:T(8,128)S(1)}, u32[]{:S(2)}) %copy-start.3) | copy-done | bytes 1048600
  27.3 0.0 collective-permute-done.2.rowa_ref
  27.3 0.0 collective-permute-done.3.rowb_ref
  27.3 0.0 copy-done.4
  27.3 10.2 %shard_map.90 = (f32[8,2,128,128]{3,2,1,0:T(8,128)S(1)}, f32[8,2,128,128]{3,2,1,0:T(8,128)S(1)}, f32[128,128]{1,0:T(8,128)S(1)}, f32[128,128]{1,0:T(8,128)S(1)}) custom-call(s32[1,8]{1,0:T(1,128)S(1)} %copy-done.5, s32[1,8]{1,0:T(1,128)S(1)} %copy-done.6, s32[1,2]{1,0:T(1,128)S(1)} %and_select_fusion.spot_ref, s32[1,1]{1,0:T(1,128)S(6)} %copy.9.live_ref, ...), custom_call_target="tpu_custom_call" | custom-call | tf_op jit(solution)/shard_map/pallas_call | solution.py:357
  37.6 0.1 collective-permute-start.8
  37.7 1.2 %collective-permute-done.8 = f32[128,128]{1,0:T(8,128)S(1)} collective-permute-done((f32[128,128]{1,0:T(8,128)S(1)}, f32[128,128]{1,0:T(8,128)S(1)}, u32[]{:S(2)}, u32[]{:S(2)}) %collective-permute-start.8) | collective-permute-done | bytes 65568 | tf_op jit(solution)/shard_map/ppermute | solution.py:353
  38.9 2.3 %collective-permute-start.9 = (f32[128,128]{1,0:T(8,128)S(1)}, f32[128,128]{1,0:T(8,128)S(1)}, u32[]{:S(2)}, u32[]{:S(2)}) collective-permute-start(f32[128,128]{1,0:T(8,128)S(1)} %add.38), channel_id=1, source_target_pairs={{0,4},{1,5},{2,6},{3,7},{4,0},{5,1},{6,2},{7,3},{8,12},{9,13},{10,... | collective-permute-start | bytes 196616 | tf_op jit(solution)/shard_map/ppermute | solution.py:353
  41.2 2.3 %shard_map.91 = (f32[2,2,256,256]{3,2,1,0:T(8,128)S(1)}, f32[2,6,64,128]{3,2,1,0:T(8,128)S(1)}, f32[2,6,64,128]{3,2,1,0:T(8,128)S(1)}, f32[2,256,128]{2,1,0:T(8,128)S(1)}, f32[2,256,128]{2,1,0:T(8,128)S(1)}) custom-call(s32[1,8]{1,0:T(1,128)S(1)} %copy-done.5, s32[1,8]{1,0:T(1,128)S(1)} %copy-done.6, s32[1,2]{1,0:T(1,128)S(1)} %and_select_fusion.spot_ref, ...), custom_call_target="tpu_custom_call" | custom-call | tf_op jit(solution)/shard_map/pallas_call | solution.py:357
  43.6 0.0 collective-permute-done.9
  43.6 5.2 %collective-permute-start.10 = (f32[2,6,64,128]{3,2,1,0:T(8,128)S(1)}, f32[2,6,64,128]{3,2,1,0:T(8,128)S(1)}, u32[]{:S(2)}, u32[]{:S(2)}) collective-permute-start(f32[2,6,64,128]{3,2,1,0:T(8,128)S(1)} %get-tuple-element.46), channel_id=1, source_target_pairs={{0,16},{1,17},{2,18},{3,19},{4,20},{5,21},{6,22},{7,23},{8,24},{9,... | collective-permute-start | bytes 1179656 | tf_op jit(solution)/shard_map/ppermute | solution.py:347
  48.8 0.7 collective-permute-start.11
  49.5 2.1 %collective-permute-start.12 = (f32[128,128]{1,0:T(8,128)S(1)}, f32[128,128]{1,0:T(8,128)S(1)}, u32[]{:S(2)}, u32[]{:S(2)}) collective-permute-start(f32[128,128]{1,0:T(8,128)S(1)} %add.39), channel_id=1, source_target_pairs={{0,12},{1,13},{2,14},{3,15},{4,8},{5,9},{6,10},{7,11},{8,4},{9,5},... | collective-permute-start | bytes 196616 | tf_op jit(solution)/shard_map/ppermute | solution.py:353
  51.6 2.3 %collective-permute-done.12 = f32[128,128]{1,0:T(8,128)S(1)} collective-permute-done((f32[128,128]{1,0:T(8,128)S(1)}, f32[128,128]{1,0:T(8,128)S(1)}, u32[]{:S(2)}, u32[]{:S(2)}) %collective-permute-start.12) | collective-permute-done | bytes 65568 | tf_op jit(solution)/shard_map/ppermute | solution.py:353
  53.9 6.3 %collective-permute-start.13 = (f32[128,128]{1,0:T(8,128)S(1)}, f32[128,128]{1,0:T(8,128)S(1)}, u32[]{:S(2)}, u32[]{:S(2)}) collective-permute-start(f32[128,128]{1,0:T(8,128)S(1)} %add.40), channel_id=1, source_target_pairs={{0,128},{1,129},{2,130},{3,131},{4,132},{5,133},{6,134},{7,135},{8... | collective-permute-start | bytes 196616 | tf_op jit(solution)/shard_map/ppermute | solution.py:353
  60.2 4.8 %collective-permute-done.13 = f32[128,128]{1,0:T(8,128)S(1)} collective-permute-done((f32[128,128]{1,0:T(8,128)S(1)}, f32[128,128]{1,0:T(8,128)S(1)}, u32[]{:S(2)}, u32[]{:S(2)}) %collective-permute-start.13) | collective-permute-done | bytes 65568 | tf_op jit(solution)/shard_map/ppermute | solution.py:353
  64.9 3.5 %collective-permute-start.14 = (f32[128,128]{1,0:T(8,128)S(1)}, f32[128,128]{1,0:T(8,128)S(1)}, u32[]{:S(2)}, u32[]{:S(2)}) collective-permute-start(f32[128,128]{1,0:T(8,128)S(1)} %add.41), channel_id=1, source_target_pairs={{0,130},{1,131},{2,128},{3,129},{4,134},{5,135},{6,132},{7,133},{8... | collective-permute-start | bytes 196616 | tf_op jit(solution)/shard_map/ppermute | solution.py:353
  68.4 2.0 %collective-permute-done.14 = f32[128,128]{1,0:T(8,128)S(1)} collective-permute-done((f32[128,128]{1,0:T(8,128)S(1)}, f32[128,128]{1,0:T(8,128)S(1)}, u32[]{:S(2)}, u32[]{:S(2)}) %collective-permute-start.14) | collective-permute-done | bytes 65568 | tf_op jit(solution)/shard_map/ppermute | solution.py:353
  70.5 0.0 collective-permute-done.10.rowa_ref
  70.5 0.0 collective-permute-done.11.rowb_ref
  70.5 0.6 shard_map.92
  71.1 0.1 collective-permute-start.17
  71.2 1.1 %collective-permute-start.15 = (f32[2,256,128]{2,1,0:T(8,128)S(1)}, f32[2,256,128]{2,1,0:T(8,128)S(1)}, u32[]{:S(2)}, u32[]{:S(2)}) collective-permute-start(f32[2,256,128]{2,1,0:T(8,128)S(1)} %get-tuple-element.53), channel_id=1, source_target_pairs={{0,1},{1,0},{2,3},{3,2},{4,5},{5,4},{6,7},{7,6},{8,9},{9,8},{10,11... | collective-permute-start | bytes 786440 | tf_op jit(solution)/shard_map/ppermute | solution.py:347
  72.3 2.5 %collective-permute-start.16 = (f32[2,256,128]{2,1,0:T(8,128)S(1)}, f32[2,256,128]{2,1,0:T(8,128)S(1)}, u32[]{:S(2)}, u32[]{:S(2)}) collective-permute-start(f32[2,256,128]{2,1,0:T(8,128)S(1)} %get-tuple-element.54), channel_id=1, source_target_pairs={{1,2},{2,1},{3,4},{4,3},{5,6},{6,5},{7,8},{8,7},{9,10},{10,9},{11,... | collective-permute-start | bytes 786440 | tf_op jit(solution)/shard_map/ppermute | solution.py:347
  74.8 0.0 collective-permute-done.17
  74.9 0.6 collective-permute-start.18
  75.5 3.5 %collective-permute-done.18 = f32[128,128]{1,0:T(8,128)S(1)} collective-permute-done((f32[128,128]{1,0:T(8,128)S(1)}, f32[128,128]{1,0:T(8,128)S(1)}, u32[]{:S(2)}, u32[]{:S(2)}) %collective-permute-start.18) | collective-permute-done | bytes 65568 | tf_op jit(solution)/shard_map/ppermute | solution.py:353
  79.0 5.3 %collective-permute-start.19 = (f32[128,128]{1,0:T(8,128)S(1)}, f32[128,128]{1,0:T(8,128)S(1)}, u32[]{:S(2)}, u32[]{:S(2)}) collective-permute-start(f32[128,128]{1,0:T(8,128)S(1)} %add.44), channel_id=1, source_target_pairs={{0,96},{1,97},{2,98},{3,99},{4,100},{5,101},{6,102},{7,103},{8,104... | collective-permute-start | bytes 196616 | tf_op jit(solution)/shard_map/ppermute | solution.py:353
  84.2 1.8 %collective-permute-done.19 = f32[128,128]{1,0:T(8,128)S(1)} collective-permute-done((f32[128,128]{1,0:T(8,128)S(1)}, f32[128,128]{1,0:T(8,128)S(1)}, u32[]{:S(2)}, u32[]{:S(2)}) %collective-permute-start.19) | collective-permute-done | bytes 65568 | tf_op jit(solution)/shard_map/ppermute | solution.py:353
  86.0 3.0 %collective-permute-start.20 = (f32[128,128]{1,0:T(8,128)S(1)}, f32[128,128]{1,0:T(8,128)S(1)}, u32[]{:S(2)}, u32[]{:S(2)}) collective-permute-start(f32[128,128]{1,0:T(8,128)S(1)} %add.45.mine_ref), channel_id=1, source_target_pairs={{0,1},{1,0},{2,3},{3,2},{4,5},{5,4},{6,7},{7,6},{8,9},{9,8},{10,11... | collective-permute-start | bytes 196616 | tf_op jit(solution)/shard_map/ppermute | solution.py:353
  89.0 0.0 collective-permute-done.15.cola_ref
  89.0 0.0 collective-permute-done.16.colb_ref
  89.0 0.9 collective-permute-done.20.other_ref
  89.9 1.8 %shard_map.93 = (f32[2,2,256,256]{3,2,1,0:T(8,128)}, f32[2,128,128]{2,1,0:T(8,128)}) custom-call(s32[1,2]{1,0:T(1,128)S(1)} %and_select_fusion.spot_ref, f32[2,2,256,256]{3,2,1,0:T(8,128)S(1)} %get-tuple-element.41.part_ref, f32[2,6,64,128]{3,2,1,0:T(8,128)S(1)} %collective-permute-done.10.rowa_ref, f32[2,6,64,128]{3,2,1,0:T(8,128)S(1)} %collective-permute-done.11.rowb_ref, ...), custom_call_target="tpu_custom_call" | custom-call | tf_op jit(solution)/shard_map/pallas_call | solution.py:357
  (9 shorter events, 0.1 us)
Async XLA Ops:
  0.7 1.2 %copy-start = (f32[2,2,256,256]{3,2,1,0:T(8,128)S(1)}, f32[2,2,256,256]{3,2,1,0:T(8,128)}, u32[]{:S(2)}) copy-start(f32[2,2,256,256]{3,2,1,0:T(8,128)} %obj_ref.11) | copy-start | bytes 3145732
  2.7 10.6 %collective-permute-start.4 = (f32[256,128]{1,0:T(8,128)S(1)}, f32[256,128]{1,0:T(8,128)S(1)}, u32[]{:S(2)}, u32[]{:S(2)}) collective-permute-start(f32[256,128]{1,0:T(8,128)S(1)} %get-tuple-element.33), channel_id=1, source_target_pairs={{0,1},{1,0},{2,3},{3,2},{4,5},{5,4},{6,7},{7,6},{8,9},{9,8},{10,11... | collective-permute-start | bytes 393224 | tf_op jit(solution)/shard_map/ppermute | solution.py:347
  6.0 7.8 %collective-permute-start.5 = (f32[256,128]{1,0:T(8,128)S(1)}, f32[256,128]{1,0:T(8,128)S(1)}, u32[]{:S(2)}, u32[]{:S(2)}) collective-permute-start(f32[256,128]{1,0:T(8,128)S(1)} %get-tuple-element.34), channel_id=1, source_target_pairs={{1,2},{2,1},{3,4},{4,3},{5,6},{6,5},{7,8},{8,7},{9,10},{10,9},{11,... | collective-permute-start | bytes 393224 | tf_op jit(solution)/shard_map/ppermute | solution.py:347
  9.0 6.6 %collective-permute-start = (f32[256,128]{1,0:T(8,128)S(1)}, f32[256,128]{1,0:T(8,128)S(1)}, u32[]{:S(2)}, u32[]{:S(2)}) collective-permute-start(f32[256,128]{1,0:T(8,128)S(1)} %get-tuple-element.29), channel_id=1, source_target_pairs={{0,1},{1,0},{2,3},{3,2},{4,5},{5,4},{6,7},{7,6},{8,9},{9,8},{10,11... | collective-permute-start | bytes 393224 | tf_op jit(solution)/shard_map/ppermute | solution.py:347
  9.1 13.2 %copy-start.1 = (bf16[4,2,256,256]{3,2,1,0:T(8,128)(2,1)S(1)}, bf16[4,2,256,256]{3,2,1,0:T(8,128)(2,1)}, u32[]{:S(2)}) copy-start(bf16[4,2,256,256]{3,2,1,0:T(8,128)(2,1)} %constant.24.clone.tabs_ref) | copy-start | bytes 3145732
  9.1 7.9 %collective-permute-start.1 = (f32[256,128]{1,0:T(8,128)S(1)}, f32[256,128]{1,0:T(8,128)S(1)}, u32[]{:S(2)}, u32[]{:S(2)}) collective-permute-start(f32[256,128]{1,0:T(8,128)S(1)} %get-tuple-element.30), channel_id=1, source_target_pairs={{1,2},{2,1},{3,4},{4,3},{5,6},{6,5},{7,8},{8,7},{9,10},{10,9},{11,... | collective-permute-start | bytes 393224 | tf_op jit(solution)/shard_map/ppermute | solution.py:347
  14.4 7.9 %collective-permute-start.6 = (f32[6,64,128]{2,1,0:T(8,128)S(1)}, f32[6,64,128]{2,1,0:T(8,128)S(1)}, u32[]{:S(2)}, u32[]{:S(2)}) collective-permute-start(f32[6,64,128]{2,1,0:T(8,128)S(1)} %get-tuple-element.35), channel_id=1, source_target_pairs={{0,16},{1,17},{2,18},{3,19},{4,20},{5,21},{6,22},{7,23},{8,24},{9,... | collective-permute-start | bytes 589832 | tf_op jit(solution)/shard_map/ppermute | solution.py:347
  14.8 7.5 %copy-start.2 = (f32[2,128,128]{2,1,0:T(8,128)S(1)}, f32[2,128,128]{2,1,0:T(8,128)}, u32[]{:S(2)}) copy-start(f32[2,128,128]{2,1,0:T(8,128)} %probe_ref.5) | copy-start | bytes 393220
  14.8 7.5 %collective-permute-start.7 = (f32[6,64,128]{2,1,0:T(8,128)S(1)}, f32[6,64,128]{2,1,0:T(8,128)S(1)}, u32[]{:S(2)}, u32[]{:S(2)}) collective-permute-start(f32[6,64,128]{2,1,0:T(8,128)S(1)} %get-tuple-element.36), channel_id=1, source_target_pairs={{16,32},{17,33},{18,34},{19,35},{20,36},{21,37},{22,38},{23,39},{2... | collective-permute-start | bytes 589832 | tf_op jit(solution)/shard_map/ppermute | solution.py:347
  17.6 9.7 %collective-permute-start.2 = (f32[6,64,128]{2,1,0:T(8,128)S(1)}, f32[6,64,128]{2,1,0:T(8,128)S(1)}, u32[]{:S(2)}, u32[]{:S(2)}) collective-permute-start(f32[6,64,128]{2,1,0:T(8,128)S(1)} %get-tuple-element.31), channel_id=1, source_target_pairs={{0,16},{1,17},{2,18},{3,19},{4,20},{5,21},{6,22},{7,23},{8,24},{9,... | collective-permute-start | bytes 589832 | tf_op jit(solution)/shard_map/ppermute | solution.py:347
  20.8 1.5 %copy-start.5 = (s32[1,8]{1,0:T(1,128)S(1)}, s32[1,8]{1,0:T(1,128)}, u32[]{:S(2)}) copy-start(s32[1,8]{1,0:T(1,128)} %row_ref.5) | copy-start | bytes 100
  20.8 1.5 %copy-start.6 = (s32[1,8]{1,0:T(1,128)S(1)}, s32[1,8]{1,0:T(1,128)}, u32[]{:S(2)}) copy-start(s32[1,8]{1,0:T(1,128)} %col_ref.5) | copy-start | bytes 100
  20.8 6.5 %collective-permute-start.3 = (f32[6,64,128]{2,1,0:T(8,128)S(1)}, f32[6,64,128]{2,1,0:T(8,128)S(1)}, u32[]{:S(2)}, u32[]{:S(2)}) collective-permute-start(f32[6,64,128]{2,1,0:T(8,128)S(1)} %get-tuple-element.32), channel_id=1, source_target_pairs={{16,32},{17,33},{18,34},{19,35},{20,36},{21,37},{22,38},{23,39},{2... | collective-permute-start | bytes 589832 | tf_op jit(solution)/shard_map/ppermute | solution.py:347
  22.3 5.0 %copy-start.4 = (f32[1,8,128,128]{3,2,1,0:T(8,128)S(1)}, f32[1,8,128,128]{3,2,1,0:T(8,128)}, u32[]{:S(2)}) copy-start(f32[1,8,128,128]{3,2,1,0:T(8,128)} %param.9) | copy-start | bytes 1572868
  26.4 1.0 %copy-start.3 = (f32[8,2,128,128]{3,2,1,0:T(8,128)}, f32[8,2,128,128]{3,2,1,0:T(8,128)S(1)}, u32[]{:S(2)}) copy-start(f32[8,2,128,128]{3,2,1,0:T(8,128)S(1)} %get-tuple-element.38.mid_ref) | copy-start | bytes 3145732
  37.6 1.3 %collective-permute-start.8 = (f32[128,128]{1,0:T(8,128)S(1)}, f32[128,128]{1,0:T(8,128)S(1)}, u32[]{:S(2)}, u32[]{:S(2)}) collective-permute-start(f32[128,128]{1,0:T(8,128)S(1)} %get-tuple-element.43), channel_id=1, source_target_pairs={{0,1},{1,0},{2,3},{3,2},{4,5},{5,4},{6,7},{7,6},{8,9},{9,8},{10,11... | collective-permute-start | bytes 196616 | tf_op jit(solution)/shard_map/ppermute | solution.py:353
  38.9 4.7 %collective-permute-start.9 = (f32[128,128]{1,0:T(8,128)S(1)}, f32[128,128]{1,0:T(8,128)S(1)}, u32[]{:S(2)}, u32[]{:S(2)}) collective-permute-start(f32[128,128]{1,0:T(8,128)S(1)} %add.38), channel_id=1, source_target_pairs={{0,4},{1,5},{2,6},{3,7},{4,0},{5,1},{6,2},{7,3},{8,12},{9,13},{10,... | collective-permute-start | bytes 196616 | tf_op jit(solution)/shard_map/ppermute | solution.py:353
  43.6 26.9 %collective-permute-start.10 = (f32[2,6,64,128]{3,2,1,0:T(8,128)S(1)}, f32[2,6,64,128]{3,2,1,0:T(8,128)S(1)}, u32[]{:S(2)}, u32[]{:S(2)}) collective-permute-start(f32[2,6,64,128]{3,2,1,0:T(8,128)S(1)} %get-tuple-element.46), channel_id=1, source_target_pairs={{0,16},{1,17},{2,18},{3,19},{4,20},{5,21},{6,22},{7,23},{8,24},{9,... | collective-permute-start | bytes 1179656 | tf_op jit(solution)/shard_map/ppermute | solution.py:347
  48.8 21.7 %collective-permute-start.11 = (f32[2,6,64,128]{3,2,1,0:T(8,128)S(1)}, f32[2,6,64,128]{3,2,1,0:T(8,128)S(1)}, u32[]{:S(2)}, u32[]{:S(2)}) collective-permute-start(f32[2,6,64,128]{3,2,1,0:T(8,128)S(1)} %get-tuple-element.47), channel_id=1, source_target_pairs={{16,32},{17,33},{18,34},{19,35},{20,36},{21,37},{22,38},{23,39},{2... | collective-permute-start | bytes 1179656 | tf_op jit(solution)/shard_map/ppermute | solution.py:347
  49.5 4.4 %collective-permute-start.12 = (f32[128,128]{1,0:T(8,128)S(1)}, f32[128,128]{1,0:T(8,128)S(1)}, u32[]{:S(2)}, u32[]{:S(2)}) collective-permute-start(f32[128,128]{1,0:T(8,128)S(1)} %add.39), channel_id=1, source_target_pairs={{0,12},{1,13},{2,14},{3,15},{4,8},{5,9},{6,10},{7,11},{8,4},{9,5},... | collective-permute-start | bytes 196616 | tf_op jit(solution)/shard_map/ppermute | solution.py:353
  53.9 11.0 %collective-permute-start.13 = (f32[128,128]{1,0:T(8,128)S(1)}, f32[128,128]{1,0:T(8,128)S(1)}, u32[]{:S(2)}, u32[]{:S(2)}) collective-permute-start(f32[128,128]{1,0:T(8,128)S(1)} %add.40), channel_id=1, source_target_pairs={{0,128},{1,129},{2,130},{3,131},{4,132},{5,133},{6,134},{7,135},{8... | collective-permute-start | bytes 196616 | tf_op jit(solution)/shard_map/ppermute | solution.py:353
  64.9 5.5 %collective-permute-start.14 = (f32[128,128]{1,0:T(8,128)S(1)}, f32[128,128]{1,0:T(8,128)S(1)}, u32[]{:S(2)}, u32[]{:S(2)}) collective-permute-start(f32[128,128]{1,0:T(8,128)S(1)} %add.41), channel_id=1, source_target_pairs={{0,130},{1,131},{2,128},{3,129},{4,134},{5,135},{6,132},{7,133},{8... | collective-permute-start | bytes 196616 | tf_op jit(solution)/shard_map/ppermute | solution.py:353
  71.1 3.7 %collective-permute-start.17 = (f32[128,128]{1,0:T(8,128)S(1)}, f32[128,128]{1,0:T(8,128)S(1)}, u32[]{:S(2)}, u32[]{:S(2)}) collective-permute-start(f32[128,128]{1,0:T(8,128)S(1)} %add.42), channel_id=1, source_target_pairs={{0,16},{1,17},{2,18},{3,19},{4,20},{5,21},{6,22},{7,23},{8,24},{9,... | collective-permute-start | bytes 196616 | tf_op jit(solution)/shard_map/ppermute | solution.py:353
  71.2 17.8 %collective-permute-start.15 = (f32[2,256,128]{2,1,0:T(8,128)S(1)}, f32[2,256,128]{2,1,0:T(8,128)S(1)}, u32[]{:S(2)}, u32[]{:S(2)}) collective-permute-start(f32[2,256,128]{2,1,0:T(8,128)S(1)} %get-tuple-element.53), channel_id=1, source_target_pairs={{0,1},{1,0},{2,3},{3,2},{4,5},{5,4},{6,7},{7,6},{8,9},{9,8},{10,11... | collective-permute-start | bytes 786440 | tf_op jit(solution)/shard_map/ppermute | solution.py:347
  72.3 16.7 %collective-permute-start.16 = (f32[2,256,128]{2,1,0:T(8,128)S(1)}, f32[2,256,128]{2,1,0:T(8,128)S(1)}, u32[]{:S(2)}, u32[]{:S(2)}) collective-permute-start(f32[2,256,128]{2,1,0:T(8,128)S(1)} %get-tuple-element.54), channel_id=1, source_target_pairs={{1,2},{2,1},{3,4},{4,3},{5,6},{6,5},{7,8},{8,7},{9,10},{10,9},{11,... | collective-permute-start | bytes 786440 | tf_op jit(solution)/shard_map/ppermute | solution.py:347
  74.9 4.1 %collective-permute-start.18 = (f32[128,128]{1,0:T(8,128)S(1)}, f32[128,128]{1,0:T(8,128)S(1)}, u32[]{:S(2)}, u32[]{:S(2)}) collective-permute-start(f32[128,128]{1,0:T(8,128)S(1)} %add.43), channel_id=1, source_target_pairs={{0,32},{1,33},{2,34},{3,35},{4,36},{5,37},{6,38},{7,39},{8,40},{9,... | collective-permute-start | bytes 196616 | tf_op jit(solution)/shard_map/ppermute | solution.py:353
  79.0 7.0 %collective-permute-start.19 = (f32[128,128]{1,0:T(8,128)S(1)}, f32[128,128]{1,0:T(8,128)S(1)}, u32[]{:S(2)}, u32[]{:S(2)}) collective-permute-start(f32[128,128]{1,0:T(8,128)S(1)} %add.44), channel_id=1, source_target_pairs={{0,96},{1,97},{2,98},{3,99},{4,100},{5,101},{6,102},{7,103},{8,104... | collective-permute-start | bytes 196616 | tf_op jit(solution)/shard_map/ppermute | solution.py:353
  86.0 3.9 %collective-permute-start.20 = (f32[128,128]{1,0:T(8,128)S(1)}, f32[128,128]{1,0:T(8,128)S(1)}, u32[]{:S(2)}, u32[]{:S(2)}) collective-permute-start(f32[128,128]{1,0:T(8,128)S(1)} %add.45.mine_ref), channel_id=1, source_target_pairs={{0,1},{1,0},{2,3},{3,2},{4,5},{5,4},{6,7},{7,6},{8,9},{9,8},{10,11... | collective-permute-start | bytes 196616 | tf_op jit(solution)/shard_map/ppermute | solution.py:353

commit v4 on v3

--- a/solution.py
+++ b/solution.py
@@ -15,7 +15,7 @@
 FRESNEL_PHASE = 60.0
 LANES = 128
 BOTH = ("row", "col")
-GRANT = 48 * 1024 * 1024
+GRANT = 16 * 1024 * 1024
 MASKS = (4, 12, 128, 130, 16, 32, 96)
 
 
@@ -75,7 +75,14 @@
 
 
 def pick(spot_ref, axis, even, odd):
-    return jnp.where(spot_ref[0, axis] == 0, even, odd)
+    return jnp.where(lax.rem(spot_ref[0, axis], 2) == 0, even, odd)
+
+
+def beside(spot_ref, axis, a, b):
+    place = spot_ref[0, axis]
+    before = jnp.where(place == 0, 0.0, pick(spot_ref, axis, b, a))
+    after = jnp.where(place == spot_ref[0, 2 + axis] - 1, 0.0, pick(spot_ref, axis, a, b))
+    return before, after
 
 
 def pack_kernel(spot_ref, obj_ref, *outs):
@@ -95,10 +102,9 @@
             top, bottom = obj_ref[piece, part, low, cols], obj_ref[piece, part, high, cols]
             rowa_ref[2 * part + block] = pick(spot_ref, 0, bottom, top)
             rowb_ref[2 * part + block] = pick(spot_ref, 0, top, bottom)
-    for place, east in ((4, False), (5, True)):
-        even, odd = (cola_ref, colb_ref) if east else (colb_ref, cola_ref)
-        top = pick(spot_ref, 1, even[low], odd[low])
-        bottom = pick(spot_ref, 1, even[high], odd[high])
+    tops = beside(spot_ref, 1, cola_ref[low], colb_ref[low])
+    bottoms = beside(spot_ref, 1, cola_ref[high], colb_ref[high])
+    for place, top, bottom in zip((4, 5), tops, bottoms):
         rowa_ref[place] = pick(spot_ref, 0, bottom, top)
         rowb_ref[place] = pick(spot_ref, 0, top, bottom)
 
@@ -106,17 +112,15 @@
 def grow(ext, spot_ref, piece_ref, cola_ref, colb_ref, rowa_ref, rowb_ref):
     half = LANES // 2
     tile = piece_ref.shape[1]
+    sides = beside(spot_ref, 1, cola_ref[...], colb_ref[...])
     for part in range(2):
         for block in range(4):
             place = 2 * part + block - 1 if block in (1, 2) else 4 + block // 3
-            top = pick(spot_ref, 0, rowb_ref[place], rowa_ref[place])
-            bottom = pick(spot_ref, 0, rowa_ref[place], rowb_ref[place])
+            top, bottom = beside(spot_ref, 0, rowa_ref[place], rowb_ref[place])
             if block in (1, 2):
                 middle = piece_ref[part, :, (block - 1) * LANES : block * LANES]
-            elif block == 0:
-                middle = pick(spot_ref, 1, colb_ref[...], cola_ref[...])
             else:
-                middle = pick(spot_ref, 1, cola_ref[...], colb_ref[...])
+                middle = sides[block // 3]
             for strip, start in ((top, 0), (middle, half), (bottom, half + tile)):
                 if (block == 0 and part == 0) or (block == 3 and part == 1):
                     strip = pltpu.roll(strip, half, 1)
@@ -276,12 +280,12 @@
     for piece in range(2):
         sides = []
         for ref, place in ((left_ref, 4), (right_ref, 5)):
-            a, b = rowa_ref[piece, place], rowb_ref[piece, place]
+            top, bottom = beside(spot_ref, 0, rowa_ref[piece, place], rowb_ref[piece, place])
             sides.append(
                 (
-                    ref[piece, :half] + pick(spot_ref, 0, b, a),
+                    ref[piece, :half] + top,
                     ref[piece, half : tile - half],
-                    ref[piece, tile - half :] + pick(spot_ref, 0, a, b),
+                    ref[piece, tile - half :] + bottom,
                 )
             )
         for left, right, rows in zip(*sides, (slice(0, half), slice(half, tile - half), slice(tile - half, tile))):
@@ -301,8 +305,7 @@
     for piece in range(2):
         for start in range(0, tile, half):
             rows = slice(start, start + half)
-            cola, colb = cola_ref[piece, rows], colb_ref[piece, rows]
-            sides = (pick(spot_ref, 1, colb, cola), pick(spot_ref, 1, cola, colb))
+            sides = beside(spot_ref, 1, cola_ref[piece, rows], colb_ref[piece, rows])
             for part in range(2):
                 for block in range(2):
                     cols = slice(block * LANES, (block + 1) * LANES)
@@ -310,11 +313,12 @@
                     if block != part:
                         total = pltpu.roll(total, half, 1)
                     total = jnp.where(first == (block == 0), total, 0.0)
-                    a, b = rowa_ref[piece, 2 * part + block], rowb_ref[piece, 2 * part + block]
+                    place = 2 * part + block
+                    ends = beside(spot_ref, 0, rowa_ref[piece, place], rowb_ref[piece, place])
                     if start == 0:
-                        total += pick(spot_ref, 0, b, a)
+                        total += ends[0]
                     if start == tile - half:
-                        total += pick(spot_ref, 0, a, b)
+                        total += ends[1]
                     new_ref[piece, part, rows, cols] = (
                         part_ref[piece, part, rows, cols] - STEP_OBJECT * total
                     )
@@ -333,17 +337,14 @@
 
 
 def meet(strips, axis):
-    rows, cols = lax.axis_size("row"), lax.axis_size("col")
+    sizes = (lax.axis_size("row"), lax.axis_size("col"))
     got = []
     for odd, strip in enumerate(strips):
         pairs = []
-        for a in range(rows):
-            for b in range(cols):
-                c, d = (a, b) if axis else (((a + odd) ^ 1) - odd, b)
-                if axis:
-                    d = ((b + odd) ^ 1) - odd
-                if 0 <= c < rows and 0 <= d < cols:
-                    pairs.append((a * cols + b, c * cols + d))
+        for spot in np.ndindex(*sizes):
+            other = list(spot)
+            other[axis] = (((spot[axis] + odd) ^ 1) - odd) % sizes[axis]
+            pairs.append((spot[0] * sizes[1] + spot[1], other[0] * sizes[1] + other[1]))
         got.append(lax.ppermute(strip, BOTH, pairs))
     return got
 
@@ -368,8 +369,8 @@
     count = offset_row.shape[1]
     side, edge, plane = (tile, LANES), (6, half, LANES), (width, width)
     field, fields = array(2, 2, tile, tile), array(count, 2, width, width)
-    spot = jnp.stack([lax.axis_index("row"), lax.axis_index("col")]).astype(jnp.int32) % 2
-    spot = spot.reshape(1, 2)
+    place = [lax.axis_index(axis) for axis in BOTH] + [lax.axis_size(axis) for axis in BOTH]
+    spot = jnp.stack([jnp.asarray(entry, jnp.int32) for entry in place]).reshape(1, 4)
     tabs = jnp.asarray(make_tables(width))
     grown = pltpu.VMEM((2, 4, tile + width, LANES), jnp.float32)
     packed = call(pack_kernel, [array(*side)] * 4, (spot,), (object_field,))

time: 92 us -> 85.2 us (0.926)
  starting transfers between devices: 48.6 us -> 37.7 us
  waiting for transfers between devices: 18.3 us -> 24.5 us
  local copies, waits for them, and re-layouts: 2.21 us -> 1.26 us
    ppermute x9, starting transfers between devices: 23.3 us -> 14.9 us  [swap(): return lax.ppermute(value, BOTH, [(i, i ^ mask) for i in range(count)])]
    ppermute x9, waiting for transfers between devices: 16.4 us -> 22.4 us  [swap(): return lax.ppermute(value, BOTH, [(i, i ^ mask) for i in range(count)])]
    ppermute x12, starting transfers between devices: 25.3 us -> 22.9 us  [meet(): got.append(lax.ppermute(strip, BOTH, pairs))]
    unnamed x14 -> x12, local copies, waits for them, and re-layouts: 2.21 us -> 1.26 us
  transfers between devices with their start and end apart: 21 -> 21, of which waited for: 9 -> 9; matrix products, arithmetic and copies ran while one was open for 0% -> 0% of each run, Pallas kernels for 8% -> 9%
where the time goes in v4:
time: 85.2 us; the launch traced here: 85.1 us
  starting transfers between devices  37.7 us (44%)
  waiting for transfers between devices  24.5 us (29%)
  Pallas kernels  19.9 us (23%)
  between operations  1.56 us (2%)
  local copies, waits for them, and re-layouts  1.26 us (1%)
    ppermute x12, starting transfers between devices, meet(): got.append(lax.ppermute(strip, BOTH, pairs))  22.9 us
    ppermute x9, waiting for transfers between devices, swap(): return lax.ppermute(value, BOTH, [(i, i ^ mask) for i in range(count)])  22.4 us
    pallas_call x8, Pallas kernels, call(): pl.pallas_call(kernel, out_shape=tuple(out_shape), in_specs=smem(len(scal...  19.9 us
    ppermute x9, starting transfers between devices, swap(): return lax.ppermute(value, BOTH, [(i, i ^ mask) for i in range(count)])  14.9 us
    ppermute x12, waiting for transfers between devices, meet(): got.append(lax.ppermute(strip, BOTH, pairs))  2.15 us
  transfers between devices with their start and end apart: 21, of which 9 were waited for; matrix products, arithmetic and copies ran while one was open for 0% of the time, Pallas kernels for 9%

profile of v4, /device:TPU:1, one launch (start us, length us, event | category | flops | bytes accessed | tf_op | source)
XLA Modules:
  0.0 85.1 jit_solution(12793666411468900990)
XLA Ops:
  0.6 0.1 add_bitcast_fusion.spot_ref
  0.7 0.0 copy-start
  0.7 1.2 %copy-done = f32[2,2,256,256]{3,2,1,0:T(8,128)S(1)} copy-done((f32[2,2,256,256]{3,2,1,0:T(8,128)S(1)}, f32[2,2,256,256]{3,2,1,0:T(8,128)}, u32[]{:S(2)}) %copy-start) | copy-done | bytes 1048600
  2.0 0.7 shard_map.86
  2.7 3.3 %collective-permute-start.4 = (f32[256,128]{1,0:T(8,128)S(1)}, f32[256,128]{1,0:T(8,128)S(1)}, u32[]{:S(2)}, u32[]{:S(2)}) collective-permute-start(f32[256,128]{1,0:T(8,128)S(1)} %get-tuple-element.33), channel_id=1, source_target_pairs={{0,1},{1,0},{2,3},{3,2},{4,5},{5,4},{6,7},{7,6},{8,9},{9,8},{10,11... | collective-permute-start | bytes 393224 | tf_op jit(solution)/shard_map/ppermute | solution.py:348
  6.0 1.2 %collective-permute-start.5 = (f32[256,128]{1,0:T(8,128)S(1)}, f32[256,128]{1,0:T(8,128)S(1)}, u32[]{:S(2)}, u32[]{:S(2)}) collective-permute-start(f32[256,128]{1,0:T(8,128)S(1)} %get-tuple-element.34), channel_id=1, source_target_pairs={{0,15},{1,2},{2,1},{3,4},{4,3},{5,6},{6,5},{7,8},{8,7},{9,10},{10,... | collective-permute-start | bytes 393224 | tf_op jit(solution)/shard_map/ppermute | solution.py:348
  7.2 2.6 %collective-permute-start = (f32[256,128]{1,0:T(8,128)S(1)}, f32[256,128]{1,0:T(8,128)S(1)}, u32[]{:S(2)}, u32[]{:S(2)}) collective-permute-start(f32[256,128]{1,0:T(8,128)S(1)} %get-tuple-element.29), channel_id=1, source_target_pairs={{0,1},{1,0},{2,3},{3,2},{4,5},{5,4},{6,7},{7,6},{8,9},{9,8},{10,11... | collective-permute-start | bytes 393224 | tf_op jit(solution)/shard_map/ppermute | solution.py:348
  9.8 0.0 copy-start.1
  9.8 0.0 collective-permute-start.1
  9.8 0.0 collective-permute-done.4.cola_ref
  9.8 2.1 %collective-permute-done.5.colb_ref = f32[256,128]{1,0:T(8,128)S(1)} collective-permute-done((f32[256,128]{1,0:T(8,128)S(1)}, f32[256,128]{1,0:T(8,128)S(1)}, u32[]{:S(2)}, u32[]{:S(2)}) %collective-permute-start.5) | collective-permute-done | bytes 131104 | tf_op jit(solution)/shard_map/ppermute | solution.py:348
  11.9 0.6 shard_map.88
  12.5 0.1 collective-permute-start.6
  12.6 0.0 copy-start.2
  12.6 5.6 %collective-permute-start.7 = (f32[6,64,128]{2,1,0:T(8,128)S(1)}, f32[6,64,128]{2,1,0:T(8,128)S(1)}, u32[]{:S(2)}, u32[]{:S(2)}) collective-permute-start(f32[6,64,128]{2,1,0:T(8,128)S(1)} %get-tuple-element.36), channel_id=1, source_target_pairs={{0,240},{1,241},{2,242},{3,243},{4,244},{5,245},{6,246},{7,247},{8... | collective-permute-start | bytes 589832 | tf_op jit(solution)/shard_map/ppermute | solution.py:348
  18.2 0.0 collective-permute-done.cola_ref
  18.2 0.0 collective-permute-done.1.colb_ref
  18.2 0.6 shard_map.87
  18.8 0.1 collective-permute-start.2
  18.9 0.0 copy-start.4
  18.9 0.0 copy-start.5
  18.9 3.9 %collective-permute-start.3 = (f32[6,64,128]{2,1,0:T(8,128)S(1)}, f32[6,64,128]{2,1,0:T(8,128)S(1)}, u32[]{:S(2)}, u32[]{:S(2)}) collective-permute-start(f32[6,64,128]{2,1,0:T(8,128)S(1)} %get-tuple-element.32), channel_id=1, source_target_pairs={{0,240},{1,241},{2,242},{3,243},{4,244},{5,245},{6,246},{7,247},{8... | collective-permute-start | bytes 589832 | tf_op jit(solution)/shard_map/ppermute | solution.py:348
  23.4 0.0 copy-start.3
  23.5 0.0 collective-permute-done.6.rowa_ref
  23.5 0.0 collective-permute-done.7.rowb_ref
  23.5 0.0 copy-done.1
  23.5 0.0 copy-done.2
  23.5 0.0 copy-done.4
  23.5 0.0 copy-done.5
  23.5 4.0 %shard_map.89 = (f32[8,2,128,128]{3,2,1,0:T(8,128)S(1)}, f32[8,2,128,128]{3,2,1,0:T(8,128)S(1)}) custom-call(s32[1,8]{1,0:T(1,128)S(1)} %copy-done.4, s32[1,8]{1,0:T(1,128)S(1)} %copy-done.5, s32[1,4]{1,0:T(1,128)S(1)} %add_bitcast_fusion.spot_ref, f32[2,2,256,256]{3,2,1,0:T(8,128)S(1)} %copy-done, f32[256,128]{1,0:T(8,128)S(1)} %collective-permute-done.4.cola_ref, ...), custom_call_target="tpu_custom_call" | custom-call | tf_op jit(solution)/shard_map/pallas_call | solution.py:358
  27.5 0.0 collective-permute-done.2.rowa_ref
  27.5 0.0 collective-permute-done.3.rowb_ref
  27.5 0.0 copy-done.3
  27.5 9.3 %shard_map.90 = (f32[8,2,128,128]{3,2,1,0:T(8,128)S(1)}, f32[8,2,128,128]{3,2,1,0:T(8,128)S(1)}, f32[128,128]{1,0:T(8,128)S(1)}, f32[128,128]{1,0:T(8,128)S(1)}) custom-call(s32[1,8]{1,0:T(1,128)S(1)} %copy-done.4, s32[1,8]{1,0:T(1,128)S(1)} %copy-done.5, s32[1,4]{1,0:T(1,128)S(1)} %add_bitcast_fusion.spot_ref, s32[1,1]{1,0:T(1,128)S(6)} %copy.9.live_ref, ...), custom_call_target="tpu_custom_call" | custom-call | tf_op jit(solution)/shard_map/pallas_call | solution.py:358
  36.8 2.8 %collective-permute-start.8 = (f32[128,128]{1,0:T(8,128)S(1)}, f32[128,128]{1,0:T(8,128)S(1)}, u32[]{:S(2)}, u32[]{:S(2)}) collective-permute-start(f32[128,128]{1,0:T(8,128)S(1)} %get-tuple-element.43), channel_id=1, source_target_pairs={{0,1},{1,0},{2,3},{3,2},{4,5},{5,4},{6,7},{7,6},{8,9},{9,8},{10,11... | collective-permute-start | bytes 196616 | tf_op jit(solution)/shard_map/ppermute | solution.py:354
  39.6 0.9 %collective-permute-done.8 = f32[128,128]{1,0:T(8,128)S(1)} collective-permute-done((f32[128,128]{1,0:T(8,128)S(1)}, f32[128,128]{1,0:T(8,128)S(1)}, u32[]{:S(2)}, u32[]{:S(2)}) %collective-permute-start.8) | collective-permute-done | bytes 65568 | tf_op jit(solution)/shard_map/ppermute | solution.py:354
  40.5 1.2 %collective-permute-start.9 = (f32[128,128]{1,0:T(8,128)S(1)}, f32[128,128]{1,0:T(8,128)S(1)}, u32[]{:S(2)}, u32[]{:S(2)}) collective-permute-start(f32[128,128]{1,0:T(8,128)S(1)} %add.24), channel_id=1, source_target_pairs={{0,4},{1,5},{2,6},{3,7},{4,0},{5,1},{6,2},{7,3},{8,12},{9,13},{10,... | collective-permute-start | bytes 196616 | tf_op jit(solution)/shard_map/ppermute | solution.py:354
  41.7 2.3 %shard_map.91 = (f32[2,2,256,256]{3,2,1,0:T(8,128)S(1)}, f32[2,6,64,128]{3,2,1,0:T(8,128)S(1)}, f32[2,6,64,128]{3,2,1,0:T(8,128)S(1)}, f32[2,256,128]{2,1,0:T(8,128)S(1)}, f32[2,256,128]{2,1,0:T(8,128)S(1)}) custom-call(s32[1,8]{1,0:T(1,128)S(1)} %copy-done.4, s32[1,8]{1,0:T(1,128)S(1)} %copy-done.5, s32[1,4]{1,0:T(1,128)S(1)} %add_bitcast_fusion.spot_ref, ...), custom_call_target="tpu_custom_call" | custom-call | tf_op jit(solution)/shard_map/pallas_call | solution.py:358
  44.0 0.0 collective-permute-done.9
  44.1 0.1 collective-permute-start.10
  44.2 3.5 %collective-permute-start.11 = (f32[2,6,64,128]{3,2,1,0:T(8,128)S(1)}, f32[2,6,64,128]{3,2,1,0:T(8,128)S(1)}, u32[]{:S(2)}, u32[]{:S(2)}) collective-permute-start(f32[2,6,64,128]{3,2,1,0:T(8,128)S(1)} %get-tuple-element.47), channel_id=1, source_target_pairs={{0,240},{1,241},{2,242},{3,243},{4,244},{5,245},{6,246},{7,247},{8... | collective-permute-start | bytes 1179656 | tf_op jit(solution)/shard_map/ppermute | solution.py:348
  47.6 1.9 %collective-permute-start.12 = (f32[128,128]{1,0:T(8,128)S(1)}, f32[128,128]{1,0:T(8,128)S(1)}, u32[]{:S(2)}, u32[]{:S(2)}) collective-permute-start(f32[128,128]{1,0:T(8,128)S(1)} %add.25), channel_id=1, source_target_pairs={{0,12},{1,13},{2,14},{3,15},{4,8},{5,9},{6,10},{7,11},{8,4},{9,5},... | collective-permute-start | bytes 196616 | tf_op jit(solution)/shard_map/ppermute | solution.py:354
  49.6 2.7 %collective-permute-done.12 = f32[128,128]{1,0:T(8,128)S(1)} collective-permute-done((f32[128,128]{1,0:T(8,128)S(1)}, f32[128,128]{1,0:T(8,128)S(1)}, u32[]{:S(2)}, u32[]{:S(2)}) %collective-permute-start.12) | collective-permute-done | bytes 65568 | tf_op jit(solution)/shard_map/ppermute | solution.py:354
  52.3 0.2 collective-permute-start.13
  52.4 6.4 %collective-permute-done.13 = f32[128,128]{1,0:T(8,128)S(1)} collective-permute-done((f32[128,128]{1,0:T(8,128)S(1)}, f32[128,128]{1,0:T(8,128)S(1)}, u32[]{:S(2)}, u32[]{:S(2)}) %collective-permute-start.13) | collective-permute-done | bytes 65568 | tf_op jit(solution)/shard_map/ppermute | solution.py:354
  58.8 1.3 %collective-permute-start.14 = (f32[128,128]{1,0:T(8,128)S(1)}, f32[128,128]{1,0:T(8,128)S(1)}, u32[]{:S(2)}, u32[]{:S(2)}) collective-permute-start(f32[128,128]{1,0:T(8,128)S(1)} %add.27), channel_id=1, source_target_pairs={{0,130},{1,131},{2,128},{3,129},{4,134},{5,135},{6,132},{7,133},{8... | collective-permute-start | bytes 196616 | tf_op jit(solution)/shard_map/ppermute | solution.py:354
  60.1 3.1 %collective-permute-done.14 = f32[128,128]{1,0:T(8,128)S(1)} collective-permute-done((f32[128,128]{1,0:T(8,128)S(1)}, f32[128,128]{1,0:T(8,128)S(1)}, u32[]{:S(2)}, u32[]{:S(2)}) %collective-permute-start.14) | collective-permute-done | bytes 65568 | tf_op jit(solution)/shard_map/ppermute | solution.py:354
  63.2 0.0 collective-permute-done.10.rowa_ref
  63.2 0.0 collective-permute-done.11.rowb_ref
  63.3 0.6 shard_map.92
  63.9 0.1 collective-permute-start.17
  64.0 1.9 %collective-permute-start.15 = (f32[2,256,128]{2,1,0:T(8,128)S(1)}, f32[2,256,128]{2,1,0:T(8,128)S(1)}, u32[]{:S(2)}, u32[]{:S(2)}) collective-permute-start(f32[2,256,128]{2,1,0:T(8,128)S(1)} %get-tuple-element.53), channel_id=1, source_target_pairs={{0,1},{1,0},{2,3},{3,2},{4,5},{5,4},{6,7},{7,6},{8,9},{9,8},{10,11... | collective-permute-start | bytes 786440 | tf_op jit(solution)/shard_map/ppermute | solution.py:348
  65.9 0.6 collective-permute-start.16
  66.5 0.5 collective-permute-done.17
  67.1 0.1 collective-permute-start.18
  67.2 4.7 %collective-permute-done.18 = f32[128,128]{1,0:T(8,128)S(1)} collective-permute-done((f32[128,128]{1,0:T(8,128)S(1)}, f32[128,128]{1,0:T(8,128)S(1)}, u32[]{:S(2)}, u32[]{:S(2)}) %collective-permute-start.18) | collective-permute-done | bytes 65568 | tf_op jit(solution)/shard_map/ppermute | solution.py:354
  71.9 2.5 %collective-permute-start.19 = (f32[128,128]{1,0:T(8,128)S(1)}, f32[128,128]{1,0:T(8,128)S(1)}, u32[]{:S(2)}, u32[]{:S(2)}) collective-permute-start(f32[128,128]{1,0:T(8,128)S(1)} %add.30), channel_id=1, source_target_pairs={{0,96},{1,97},{2,98},{3,99},{4,100},{5,101},{6,102},{7,103},{8,104... | collective-permute-start | bytes 196616 | tf_op jit(solution)/shard_map/ppermute | solution.py:354
  74.4 3.1 %collective-permute-done.19 = f32[128,128]{1,0:T(8,128)S(1)} collective-permute-done((f32[128,128]{1,0:T(8,128)S(1)}, f32[128,128]{1,0:T(8,128)S(1)}, u32[]{:S(2)}, u32[]{:S(2)}) %collective-permute-start.19) | collective-permute-done | bytes 65568 | tf_op jit(solution)/shard_map/ppermute | solution.py:354
  77.5 4.9 %collective-permute-start.20 = (f32[128,128]{1,0:T(8,128)S(1)}, f32[128,128]{1,0:T(8,128)S(1)}, u32[]{:S(2)}, u32[]{:S(2)}) collective-permute-start(f32[128,128]{1,0:T(8,128)S(1)} %add.31.mine_ref), channel_id=1, source_target_pairs={{0,1},{1,0},{2,3},{3,2},{4,5},{5,4},{6,7},{7,6},{8,9},{9,8},{10,11... | collective-permute-start | bytes 196616 | tf_op jit(solution)/shard_map/ppermute | solution.py:354
  82.4 0.0 collective-permute-done.15.cola_ref
  82.4 0.0 collective-permute-done.16.colb_ref
  82.4 0.9 %collective-permute-done.20.other_ref = f32[128,128]{1,0:T(8,128)S(1)} collective-permute-done((f32[128,128]{1,0:T(8,128)S(1)}, f32[128,128]{1,0:T(8,128)S(1)}, u32[]{:S(2)}, u32[]{:S(2)}) %collective-permute-start.20) | collective-permute-done | bytes 65568 | tf_op jit(solution)/shard_map/ppermute | solution.py:354
  83.3 1.8 %shard_map.93 = (f32[2,2,256,256]{3,2,1,0:T(8,128)}, f32[2,128,128]{2,1,0:T(8,128)}) custom-call(s32[1,4]{1,0:T(1,128)S(1)} %add_bitcast_fusion.spot_ref, f32[2,2,256,256]{3,2,1,0:T(8,128)S(1)} %get-tuple-element.41.part_ref, f32[2,6,64,128]{3,2,1,0:T(8,128)S(1)} %collective-permute-done.10.rowa_ref, f32[2,6,64,128]{3,2,1,0:T(8,128)S(1)} %collective-permute-done.11.rowb_ref, ...), custom_call_target="tpu_custom_call" | custom-call | tf_op jit(solution)/shard_map/pallas_call | solution.py:358
  (9 shorter events, 0.1 us)
Async XLA Ops:
  0.7 1.2 %copy-start = (f32[2,2,256,256]{3,2,1,0:T(8,128)S(1)}, f32[2,2,256,256]{3,2,1,0:T(8,128)}, u32[]{:S(2)}) copy-start(f32[2,2,256,256]{3,2,1,0:T(8,128)} %obj_ref.11) | copy-start | bytes 3145732
  2.7 7.1 %collective-permute-start.4 = (f32[256,128]{1,0:T(8,128)S(1)}, f32[256,128]{1,0:T(8,128)S(1)}, u32[]{:S(2)}, u32[]{:S(2)}) collective-permute-start(f32[256,128]{1,0:T(8,128)S(1)} %get-tuple-element.33), channel_id=1, source_target_pairs={{0,1},{1,0},{2,3},{3,2},{4,5},{5,4},{6,7},{7,6},{8,9},{9,8},{10,11... | collective-permute-start | bytes 393224 | tf_op jit(solution)/shard_map/ppermute | solution.py:348
  6.0 5.9 %collective-permute-start.5 = (f32[256,128]{1,0:T(8,128)S(1)}, f32[256,128]{1,0:T(8,128)S(1)}, u32[]{:S(2)}, u32[]{:S(2)}) collective-permute-start(f32[256,128]{1,0:T(8,128)S(1)} %get-tuple-element.34), channel_id=1, source_target_pairs={{0,15},{1,2},{2,1},{3,4},{4,3},{5,6},{6,5},{7,8},{8,7},{9,10},{10,... | collective-permute-start | bytes 393224 | tf_op jit(solution)/shard_map/ppermute | solution.py:348
  7.2 11.0 %collective-permute-start = (f32[256,128]{1,0:T(8,128)S(1)}, f32[256,128]{1,0:T(8,128)S(1)}, u32[]{:S(2)}, u32[]{:S(2)}) collective-permute-start(f32[256,128]{1,0:T(8,128)S(1)} %get-tuple-element.29), channel_id=1, source_target_pairs={{0,1},{1,0},{2,3},{3,2},{4,5},{5,4},{6,7},{7,6},{8,9},{9,8},{10,11... | collective-permute-start | bytes 393224 | tf_op jit(solution)/shard_map/ppermute | solution.py:348
  9.8 13.7 %copy-start.1 = (bf16[4,2,256,256]{3,2,1,0:T(8,128)(2,1)S(1)}, bf16[4,2,256,256]{3,2,1,0:T(8,128)(2,1)}, u32[]{:S(2)}) copy-start(bf16[4,2,256,256]{3,2,1,0:T(8,128)(2,1)} %constant.11.clone.tabs_ref) | copy-start | bytes 3145732
  9.8 8.4 %collective-permute-start.1 = (f32[256,128]{1,0:T(8,128)S(1)}, f32[256,128]{1,0:T(8,128)S(1)}, u32[]{:S(2)}, u32[]{:S(2)}) collective-permute-start(f32[256,128]{1,0:T(8,128)S(1)} %get-tuple-element.30), channel_id=1, source_target_pairs={{0,15},{1,2},{2,1},{3,4},{4,3},{5,6},{6,5},{7,8},{8,7},{9,10},{10,... | collective-permute-start | bytes 393224 | tf_op jit(solution)/shard_map/ppermute | solution.py:348
  12.5 10.9 %collective-permute-start.6 = (f32[6,64,128]{2,1,0:T(8,128)S(1)}, f32[6,64,128]{2,1,0:T(8,128)S(1)}, u32[]{:S(2)}, u32[]{:S(2)}) collective-permute-start(f32[6,64,128]{2,1,0:T(8,128)S(1)} %get-tuple-element.35), channel_id=1, source_target_pairs={{0,16},{1,17},{2,18},{3,19},{4,20},{5,21},{6,22},{7,23},{8,24},{9,... | collective-permute-start | bytes 589832 | tf_op jit(solution)/shard_map/ppermute | solution.py:348
  12.6 10.9 %copy-start.2 = (f32[2,128,128]{2,1,0:T(8,128)S(1)}, f32[2,128,128]{2,1,0:T(8,128)}, u32[]{:S(2)}) copy-start(f32[2,128,128]{2,1,0:T(8,128)} %probe_ref.5) | copy-start | bytes 393220
  12.6 10.8 %collective-permute-start.7 = (f32[6,64,128]{2,1,0:T(8,128)S(1)}, f32[6,64,128]{2,1,0:T(8,128)S(1)}, u32[]{:S(2)}, u32[]{:S(2)}) collective-permute-start(f32[6,64,128]{2,1,0:T(8,128)S(1)} %get-tuple-element.36), channel_id=1, source_target_pairs={{0,240},{1,241},{2,242},{3,243},{4,244},{5,245},{6,246},{7,247},{8... | collective-permute-start | bytes 589832 | tf_op jit(solution)/shard_map/ppermute | solution.py:348
  18.8 8.7 %collective-permute-start.2 = (f32[6,64,128]{2,1,0:T(8,128)S(1)}, f32[6,64,128]{2,1,0:T(8,128)S(1)}, u32[]{:S(2)}, u32[]{:S(2)}) collective-permute-start(f32[6,64,128]{2,1,0:T(8,128)S(1)} %get-tuple-element.31), channel_id=1, source_target_pairs={{0,16},{1,17},{2,18},{3,19},{4,20},{5,21},{6,22},{7,23},{8,24},{9,... | collective-permute-start | bytes 589832 | tf_op jit(solution)/shard_map/ppermute | solution.py:348
  18.9 4.6 %copy-start.4 = (s32[1,8]{1,0:T(1,128)S(1)}, s32[1,8]{1,0:T(1,128)}, u32[]{:S(2)}) copy-start(s32[1,8]{1,0:T(1,128)} %row_ref.5) | copy-start | bytes 100
  18.9 4.6 %copy-start.5 = (s32[1,8]{1,0:T(1,128)S(1)}, s32[1,8]{1,0:T(1,128)}, u32[]{:S(2)}) copy-start(s32[1,8]{1,0:T(1,128)} %col_ref.5) | copy-start | bytes 100
  18.9 8.6 %collective-permute-start.3 = (f32[6,64,128]{2,1,0:T(8,128)S(1)}, f32[6,64,128]{2,1,0:T(8,128)S(1)}, u32[]{:S(2)}, u32[]{:S(2)}) collective-permute-start(f32[6,64,128]{2,1,0:T(8,128)S(1)} %get-tuple-element.32), channel_id=1, source_target_pairs={{0,240},{1,241},{2,242},{3,243},{4,244},{5,245},{6,246},{7,247},{8... | collective-permute-start | bytes 589832 | tf_op jit(solution)/shard_map/ppermute | solution.py:348
  23.4 4.1 %copy-start.3 = (f32[1,8,128,128]{3,2,1,0:T(8,128)S(1)}, f32[1,8,128,128]{3,2,1,0:T(8,128)}, u32[]{:S(2)}) copy-start(f32[1,8,128,128]{3,2,1,0:T(8,128)} %param.9) | copy-start | bytes 1572868
  36.8 3.7 %collective-permute-start.8 = (f32[128,128]{1,0:T(8,128)S(1)}, f32[128,128]{1,0:T(8,128)S(1)}, u32[]{:S(2)}, u32[]{:S(2)}) collective-permute-start(f32[128,128]{1,0:T(8,128)S(1)} %get-tuple-element.43), channel_id=1, source_target_pairs={{0,1},{1,0},{2,3},{3,2},{4,5},{5,4},{6,7},{7,6},{8,9},{9,8},{10,11... | collective-permute-start | bytes 196616 | tf_op jit(solution)/shard_map/ppermute | solution.py:354
  40.5 3.5 %collective-permute-start.9 = (f32[128,128]{1,0:T(8,128)S(1)}, f32[128,128]{1,0:T(8,128)S(1)}, u32[]{:S(2)}, u32[]{:S(2)}) collective-permute-start(f32[128,128]{1,0:T(8,128)S(1)} %add.24), channel_id=1, source_target_pairs={{0,4},{1,5},{2,6},{3,7},{4,0},{5,1},{6,2},{7,3},{8,12},{9,13},{10,... | collective-permute-start | bytes 196616 | tf_op jit(solution)/shard_map/ppermute | solution.py:354
  44.1 19.2 %collective-permute-start.10 = (f32[2,6,64,128]{3,2,1,0:T(8,128)S(1)}, f32[2,6,64,128]{3,2,1,0:T(8,128)S(1)}, u32[]{:S(2)}, u32[]{:S(2)}) collective-permute-start(f32[2,6,64,128]{3,2,1,0:T(8,128)S(1)} %get-tuple-element.46), channel_id=1, source_target_pairs={{0,16},{1,17},{2,18},{3,19},{4,20},{5,21},{6,22},{7,23},{8,24},{9,... | collective-permute-start | bytes 1179656 | tf_op jit(solution)/shard_map/ppermute | solution.py:348
  44.2 19.1 %collective-permute-start.11 = (f32[2,6,64,128]{3,2,1,0:T(8,128)S(1)}, f32[2,6,64,128]{3,2,1,0:T(8,128)S(1)}, u32[]{:S(2)}, u32[]{:S(2)}) collective-permute-start(f32[2,6,64,128]{3,2,1,0:T(8,128)S(1)} %get-tuple-element.47), channel_id=1, source_target_pairs={{0,240},{1,241},{2,242},{3,243},{4,244},{5,245},{6,246},{7,247},{8... | collective-permute-start | bytes 1179656 | tf_op jit(solution)/shard_map/ppermute | solution.py:348
  47.6 4.6 %collective-permute-start.12 = (f32[128,128]{1,0:T(8,128)S(1)}, f32[128,128]{1,0:T(8,128)S(1)}, u32[]{:S(2)}, u32[]{:S(2)}) collective-permute-start(f32[128,128]{1,0:T(8,128)S(1)} %add.25), channel_id=1, source_target_pairs={{0,12},{1,13},{2,14},{3,15},{4,8},{5,9},{6,10},{7,11},{8,4},{9,5},... | collective-permute-start | bytes 196616 | tf_op jit(solution)/shard_map/ppermute | solution.py:354
  52.3 6.5 %collective-permute-start.13 = (f32[128,128]{1,0:T(8,128)S(1)}, f32[128,128]{1,0:T(8,128)S(1)}, u32[]{:S(2)}, u32[]{:S(2)}) collective-permute-start(f32[128,128]{1,0:T(8,128)S(1)} %add.26), channel_id=1, source_target_pairs={{0,128},{1,129},{2,130},{3,131},{4,132},{5,133},{6,134},{7,135},{8... | collective-permute-start | bytes 196616 | tf_op jit(solution)/shard_map/ppermute | solution.py:354
  58.8 4.4 %collective-permute-start.14 = (f32[128,128]{1,0:T(8,128)S(1)}, f32[128,128]{1,0:T(8,128)S(1)}, u32[]{:S(2)}, u32[]{:S(2)}) collective-permute-start(f32[128,128]{1,0:T(8,128)S(1)} %add.27), channel_id=1, source_target_pairs={{0,130},{1,131},{2,128},{3,129},{4,134},{5,135},{6,132},{7,133},{8... | collective-permute-start | bytes 196616 | tf_op jit(solution)/shard_map/ppermute | solution.py:354
  63.9 3.2 %collective-permute-start.17 = (f32[128,128]{1,0:T(8,128)S(1)}, f32[128,128]{1,0:T(8,128)S(1)}, u32[]{:S(2)}, u32[]{:S(2)}) collective-permute-start(f32[128,128]{1,0:T(8,128)S(1)} %add.28), channel_id=1, source_target_pairs={{0,16},{1,17},{2,18},{3,19},{4,20},{5,21},{6,22},{7,23},{8,24},{9,... | collective-permute-start | bytes 196616 | tf_op jit(solution)/shard_map/ppermute | solution.py:354
  64.0 18.4 %collective-permute-start.15 = (f32[2,256,128]{2,1,0:T(8,128)S(1)}, f32[2,256,128]{2,1,0:T(8,128)S(1)}, u32[]{:S(2)}, u32[]{:S(2)}) collective-permute-start(f32[2,256,128]{2,1,0:T(8,128)S(1)} %get-tuple-element.53), channel_id=1, source_target_pairs={{0,1},{1,0},{2,3},{3,2},{4,5},{5,4},{6,7},{7,6},{8,9},{9,8},{10,11... | collective-permute-start | bytes 786440 | tf_op jit(solution)/shard_map/ppermute | solution.py:348
  65.9 16.5 %collective-permute-start.16 = (f32[2,256,128]{2,1,0:T(8,128)S(1)}, f32[2,256,128]{2,1,0:T(8,128)S(1)}, u32[]{:S(2)}, u32[]{:S(2)}) collective-permute-start(f32[2,256,128]{2,1,0:T(8,128)S(1)} %get-tuple-element.54), channel_id=1, source_target_pairs={{0,15},{1,2},{2,1},{3,4},{4,3},{5,6},{6,5},{7,8},{8,7},{9,10},{10,... | collective-permute-start | bytes 786440 | tf_op jit(solution)/shard_map/ppermute | solution.py:348
  67.1 4.8 %collective-permute-start.18 = (f32[128,128]{1,0:T(8,128)S(1)}, f32[128,128]{1,0:T(8,128)S(1)}, u32[]{:S(2)}, u32[]{:S(2)}) collective-permute-start(f32[128,128]{1,0:T(8,128)S(1)} %add.29), channel_id=1, source_target_pairs={{0,32},{1,33},{2,34},{3,35},{4,36},{5,37},{6,38},{7,39},{8,40},{9,... | collective-permute-start | bytes 196616 | tf_op jit(solution)/shard_map/ppermute | solution.py:354
  71.9 5.6 %collective-permute-start.19 = (f32[128,128]{1,0:T(8,128)S(1)}, f32[128,128]{1,0:T(8,128)S(1)}, u32[]{:S(2)}, u32[]{:S(2)}) collective-permute-start(f32[128,128]{1,0:T(8,128)S(1)} %add.30), channel_id=1, source_target_pairs={{0,96},{1,97},{2,98},{3,99},{4,100},{5,101},{6,102},{7,103},{8,104... | collective-permute-start | bytes 196616 | tf_op jit(solution)/shard_map/ppermute | solution.py:354
  77.5 5.8 %collective-permute-start.20 = (f32[128,128]{1,0:T(8,128)S(1)}, f32[128,128]{1,0:T(8,128)S(1)}, u32[]{:S(2)}, u32[]{:S(2)}) collective-permute-start(f32[128,128]{1,0:T(8,128)S(1)} %add.31.mine_ref), channel_id=1, source_target_pairs={{0,1},{1,0},{2,3},{3,2},{4,5},{5,4},{6,7},{7,6},{8,9},{9,8},{10,11... | collective-permute-start | bytes 196616 | tf_op jit(solution)/shard_map/ppermute | solution.py:354

commit v5 on v4

--- a/solution.py
+++ b/solution.py
@@ -16,7 +16,7 @@
 LANES = 128
 BOTH = ("row", "col")
 GRANT = 16 * 1024 * 1024
-MASKS = (4, 12, 128, 130, 16, 32, 96)
+MASKS = ((4, 16), (12, 32), (128, 96), (130, 128), (16, 130), (32, 4), (96, 12))
 
 
 def split_table(table):
@@ -85,10 +85,15 @@
     return before, after
 
 
-def pack_kernel(spot_ref, obj_ref, *outs):
-    first = lax.broadcasted_iota(jnp.int32, (obj_ref.shape[2], LANES), 1) < LANES // 2
+def pack_kernel(spot_ref, obj_ref, *refs):
+    *outs, held, sems = refs
+    first = lax.broadcasted_iota(jnp.int32, (held.shape[2], LANES), 1) < LANES // 2
+    copies = [pltpu.make_async_copy(obj_ref.at[p], held.at[p], sems.at[p]) for p in range(2)]
+    for copy in copies:
+        copy.start()
     for piece in range(2):
-        left, right = columns(obj_ref.at[piece], first)
+        copies[piece].wait()
+        left, right = columns(held.at[piece], first)
         outs[2 * piece][...] = pick(spot_ref, 1, right, left)
         outs[2 * piece + 1][...] = pick(spot_ref, 1, left, right)
 
@@ -294,14 +299,11 @@
 
 
 def finish_kernel(
-    spot_ref, part_ref, rowa_ref, rowb_ref, cola_ref, colb_ref, probe_ref, mine_ref, other_ref,
-    new_ref, newp_ref, *, scale,
+    spot_ref, part_ref, rowa_ref, rowb_ref, cola_ref, colb_ref, new_ref,
 ):
     tile = part_ref.shape[2]
     half = LANES // 2
     first = lax.broadcasted_iota(jnp.int32, (half, LANES), 1) < half
-    newp_ref[0] = probe_ref[0] - scale * pick(spot_ref, 1, mine_ref[...], other_ref[...])
-    newp_ref[1] = probe_ref[1] - scale * pick(spot_ref, 1, other_ref[...], mine_ref[...])
     for piece in range(2):
         for start in range(0, tile, half):
             rows = slice(start, start + half)
@@ -324,6 +326,11 @@
                     )
 
 
+def probe_kernel(spot_ref, probe_ref, mine_ref, other_ref, newp_ref, *, scale):
+    newp_ref[0] = probe_ref[0] - scale * pick(spot_ref, 1, mine_ref[...], other_ref[...])
+    newp_ref[1] = probe_ref[1] - scale * pick(spot_ref, 1, other_ref[...], mine_ref[...])
+
+
 def vmem(count):
     return [pl.BlockSpec(memory_space=pltpu.VMEM)] * count
 
@@ -349,9 +356,9 @@
     return got
 
 
-def swap(value, mask):
+def swap(value, masks):
     count = lax.axis_size("row") * lax.axis_size("col")
-    return lax.ppermute(value, BOTH, [(i, i ^ mask) for i in range(count)])
+    return lax.ppermute(value, BOTH, [(i, i ^ masks[i % 2]) for i in range(count)])
 
 
 def call(kernel, out_shape, scalars, arrays, scratch=()):
@@ -373,7 +380,12 @@
     spot = jnp.stack([jnp.asarray(entry, jnp.int32) for entry in place]).reshape(1, 4)
     tabs = jnp.asarray(make_tables(width))
     grown = pltpu.VMEM((2, 4, tile + width, LANES), jnp.float32)
-    packed = call(pack_kernel, [array(*side)] * 4, (spot,), (object_field,))
+    packed = pl.pallas_call(
+        pack_kernel, out_shape=tuple([array(*side)] * 4),
+        in_specs=smem(1) + [pl.BlockSpec(memory_space=pltpu.HBM)], out_specs=tuple(vmem(4)),
+        scratch_shapes=[pltpu.VMEM(object_field.shape, jnp.float32), pltpu.SemaphoreType.DMA((2,))],
+        compiler_params=pltpu.CompilerParams(vmem_limit_bytes=GRANT),
+    )(spot, pltpu.with_memory_space_constraint(object_field, pltpu.HBM))
     halos = []
     cols = [meet(packed[2 * piece : 2 * piece + 2], 1) for piece in range(2)]
     for piece in range(2):
@@ -396,7 +408,7 @@
         (offset_row, offset_col, spot), (object_field, probe, down, grad),
         (pltpu.VMEM((2, 2, 4, tile + width, LANES), jnp.float32),),
     )
-    mine = mine + swap(send, 1)
+    mine = mine + swap(send, (1, 1))
     mine = mine + swap(mine, MASKS[0])
     mine, *strips = lax.optimization_barrier((mine, *strips))
     rows = meet(strips, 0)
@@ -407,14 +419,14 @@
     cols = meet(strips, 1)
     for mask in MASKS[4:]:
         mine = mine + swap(mine, mask)
-    other = swap(mine, 1)
+    (new,) = call(finish_kernel, (field,), (spot,), (part, *rows, *cols))
+    other = swap(mine, (1, 1))
     count_all = count * lax.axis_size("row") * lax.axis_size("col")
-    return call(
-        functools.partial(finish_kernel, scale=STEP_PROBE / count_all),
-        (field, array(2, *plane)),
-        (spot,),
-        (part, *rows, *cols, probe, mine, other),
-    )
+    (new_probe,) = call(
+        functools.partial(probe_kernel, scale=STEP_PROBE / count_all), (array(2, *plane),),
+        (spot,), (probe, mine, other),
+    )
+    return new, new_probe
 
 
 def solution(mesh):

time: 85.2 us -> 86.2 us (1.012)
  Pallas kernels: 19.9 us -> 22.2 us
  local copies, waits for them, and re-layouts: 1.26 us -> 0.04 us
    pallas_call x0 -> x1, Pallas kernels: none -> 1.89 us  [on_device(): pl.pallas_call(pack_kernel, out_shape=tuple([array(*side)] * 4), in_specs...]
    unnamed x12, local copies, waits for them, and re-layouts: 1.26 us -> 0.04 us
  transfers between devices with their start and end apart: 21 -> 21, of which waited for: 9 -> 9; matrix products, arithmetic and copies ran while one was open for 0% -> 0% of each run, Pallas kernels for 9% -> 11%
where the time goes in v5:
time: 86.2 us; the launch traced here: 86 us
  starting transfers between devices  37.6 us (44%)
  waiting for transfers between devices  24.5 us (28%)
  Pallas kernels  22.2 us (26%)
  between operations  1.54 us (2%)
    ppermute x12, starting transfers between devices, meet(): got.append(lax.ppermute(strip, BOTH, pairs))  22.4 us
    ppermute x9, waiting for transfers between devices, swap(): lax.ppermute(value, BOTH, [(i, i ^ masks[i % 2]) for i in range(count)])  22.3 us
    pallas_call x8, Pallas kernels, call(): pl.pallas_call(kernel, out_shape=tuple(out_shape), in_specs=smem(len(scal...  20.3 us
    ppermute x9, starting transfers between devices, swap(): lax.ppermute(value, BOTH, [(i, i ^ masks[i % 2]) for i in range(count)])  15.2 us
    ppermute x12, waiting for transfers between devices, meet(): got.append(lax.ppermute(strip, BOTH, pairs))  2.15 us
    pallas_call x1, Pallas kernels, on_device(): pl.pallas_call(pack_kernel, out_shape=tuple([array(*side)] * 4), in_specs...  1.89 us
  transfers between devices with their start and end apart: 21, of which 9 were waited for; matrix products, arithmetic and copies ran while one was open for 0% of the time, Pallas kernels for 11%

profile of v5, /device:TPU:1, one launch (start us, length us, event | category | flops | bytes accessed | tf_op | source)
XLA Modules:
  0.0 86.0 jit_solution(6006807379854637302)
XLA Ops:
  0.6 0.0 copy-start
  0.7 0.1 add_bitcast_fusion.spot_ref
  0.7 1.9 %shard_map.86 = (f32[256,128]{1,0:T(8,128)S(1)}, f32[256,128]{1,0:T(8,128)S(1)}, f32[256,128]{1,0:T(8,128)S(1)}, f32[256,128]{1,0:T(8,128)S(1)}) custom-call(s32[1,4]{1,0:T(1,128)S(1)} %add_bitcast_fusion.spot_ref, f32[2,2,256,256]{3,2,1,0:T(8,128)} %obj_ref.11), custom_call_target="tpu_custom_call" | custom-call | tf_op jit(solution)/shard_map/pallas_call | solution.py:383
  2.6 3.3 %collective-permute-start.4 = (f32[256,128]{1,0:T(8,128)S(1)}, f32[256,128]{1,0:T(8,128)S(1)}, u32[]{:S(2)}, u32[]{:S(2)}) collective-permute-start(f32[256,128]{1,0:T(8,128)S(1)} %get-tuple-element.33), channel_id=1, source_target_pairs={{0,1},{1,0},{2,3},{3,2},{4,5},{5,4},{6,7},{7,6},{8,9},{9,8},{10,11... | collective-permute-start | bytes 393224 | tf_op jit(solution)/shard_map/ppermute | solution.py:355
  6.0 1.2 %collective-permute-start.5 = (f32[256,128]{1,0:T(8,128)S(1)}, f32[256,128]{1,0:T(8,128)S(1)}, u32[]{:S(2)}, u32[]{:S(2)}) collective-permute-start(f32[256,128]{1,0:T(8,128)S(1)} %get-tuple-element.34), channel_id=1, source_target_pairs={{0,15},{1,2},{2,1},{3,4},{4,3},{5,6},{6,5},{7,8},{8,7},{9,10},{10,... | collective-permute-start | bytes 393224 | tf_op jit(solution)/shard_map/ppermute | solution.py:355
  7.1 2.6 %collective-permute-start = (f32[256,128]{1,0:T(8,128)S(1)}, f32[256,128]{1,0:T(8,128)S(1)}, u32[]{:S(2)}, u32[]{:S(2)}) collective-permute-start(f32[256,128]{1,0:T(8,128)S(1)} %get-tuple-element.29), channel_id=1, source_target_pairs={{0,1},{1,0},{2,3},{3,2},{4,5},{5,4},{6,7},{7,6},{8,9},{9,8},{10,11... | collective-permute-start | bytes 393224 | tf_op jit(solution)/shard_map/ppermute | solution.py:355
  9.7 0.0 copy-start.1
  9.7 0.0 collective-permute-start.1
  9.7 0.0 collective-permute-done.4.cola_ref
  9.7 2.1 %collective-permute-done.5.colb_ref = f32[256,128]{1,0:T(8,128)S(1)} collective-permute-done((f32[256,128]{1,0:T(8,128)S(1)}, f32[256,128]{1,0:T(8,128)S(1)}, u32[]{:S(2)}, u32[]{:S(2)}) %collective-permute-start.5) | collective-permute-done | bytes 131104 | tf_op jit(solution)/shard_map/ppermute | solution.py:355
  11.9 0.0 copy-done
  11.9 0.6 shard_map.88
  12.4 0.1 collective-permute-start.6
  12.6 0.0 copy-start.2
  12.6 5.6 %collective-permute-start.7 = (f32[6,64,128]{2,1,0:T(8,128)S(1)}, f32[6,64,128]{2,1,0:T(8,128)S(1)}, u32[]{:S(2)}, u32[]{:S(2)}) collective-permute-start(f32[6,64,128]{2,1,0:T(8,128)S(1)} %get-tuple-element.36), channel_id=1, source_target_pairs={{0,240},{1,241},{2,242},{3,243},{4,244},{5,245},{6,246},{7,247},{8... | collective-permute-start | bytes 589832 | tf_op jit(solution)/shard_map/ppermute | solution.py:355
  18.1 0.0 collective-permute-done.cola_ref
  18.1 0.0 collective-permute-done.1.colb_ref
  18.1 0.6 shard_map.87
  18.7 0.1 collective-permute-start.2
  18.8 0.0 copy-start.4
  18.8 0.0 copy-start.5
  18.8 3.9 %collective-permute-start.3 = (f32[6,64,128]{2,1,0:T(8,128)S(1)}, f32[6,64,128]{2,1,0:T(8,128)S(1)}, u32[]{:S(2)}, u32[]{:S(2)}) collective-permute-start(f32[6,64,128]{2,1,0:T(8,128)S(1)} %get-tuple-element.32), channel_id=1, source_target_pairs={{0,240},{1,241},{2,242},{3,243},{4,244},{5,245},{6,246},{7,247},{8... | collective-permute-start | bytes 589832 | tf_op jit(solution)/shard_map/ppermute | solution.py:355
  23.4 0.0 copy-start.3
  23.4 0.0 collective-permute-done.6.rowa_ref
  23.4 0.0 collective-permute-done.7.rowb_ref
  23.4 0.0 copy-done.1
  23.4 0.0 copy-done.2
  23.4 0.0 copy-done.4
  23.4 0.0 copy-done.5
  23.5 4.0 %shard_map.89 = (f32[8,2,128,128]{3,2,1,0:T(8,128)S(1)}, f32[8,2,128,128]{3,2,1,0:T(8,128)S(1)}) custom-call(s32[1,8]{1,0:T(1,128)S(1)} %copy-done.4, s32[1,8]{1,0:T(1,128)S(1)} %copy-done.5, s32[1,4]{1,0:T(1,128)S(1)} %add_bitcast_fusion.spot_ref, f32[2,2,256,256]{3,2,1,0:T(8,128)S(1)} %copy-done, f32[256,128]{1,0:T(8,128)S(1)} %collective-permute-done.4.cola_ref, ...), custom_call_target="tpu_custom_call" | custom-call | tf_op jit(solution)/shard_map/pallas_call | solution.py:365
  27.4 0.0 collective-permute-done.2.rowa_ref
  27.5 0.0 collective-permute-done.3.rowb_ref
  27.5 0.0 copy-done.3
  27.5 9.3 %shard_map.90 = (f32[8,2,128,128]{3,2,1,0:T(8,128)S(1)}, f32[8,2,128,128]{3,2,1,0:T(8,128)S(1)}, f32[128,128]{1,0:T(8,128)S(1)}, f32[128,128]{1,0:T(8,128)S(1)}) custom-call(s32[1,8]{1,0:T(1,128)S(1)} %copy-done.4, s32[1,8]{1,0:T(1,128)S(1)} %copy-done.5, s32[1,4]{1,0:T(1,128)S(1)} %add_bitcast_fusion.spot_ref, s32[1,1]{1,0:T(1,128)S(6)} %copy.9.live_ref, ...), custom_call_target="tpu_custom_call" | custom-call | tf_op jit(solution)/shard_map/pallas_call | solution.py:365
  36.8 2.8 %collective-permute-start.8 = (f32[128,128]{1,0:T(8,128)S(1)}, f32[128,128]{1,0:T(8,128)S(1)}, u32[]{:S(2)}, u32[]{:S(2)}) collective-permute-start(f32[128,128]{1,0:T(8,128)S(1)} %get-tuple-element.43), channel_id=1, source_target_pairs={{0,1},{1,0},{2,3},{3,2},{4,5},{5,4},{6,7},{7,6},{8,9},{9,8},{10,11... | collective-permute-start | bytes 196616 | tf_op jit(solution)/shard_map/ppermute | solution.py:361
  39.5 0.9 %collective-permute-done.8 = f32[128,128]{1,0:T(8,128)S(1)} collective-permute-done((f32[128,128]{1,0:T(8,128)S(1)}, f32[128,128]{1,0:T(8,128)S(1)}, u32[]{:S(2)}, u32[]{:S(2)}) %collective-permute-start.8) | collective-permute-done | bytes 65568 | tf_op jit(solution)/shard_map/ppermute | solution.py:361
  40.5 0.1 collective-permute-start.9
  40.6 2.3 %shard_map.91 = (f32[2,2,256,256]{3,2,1,0:T(8,128)S(1)}, f32[2,6,64,128]{3,2,1,0:T(8,128)S(1)}, f32[2,6,64,128]{3,2,1,0:T(8,128)S(1)}, f32[2,256,128]{2,1,0:T(8,128)S(1)}, f32[2,256,128]{2,1,0:T(8,128)S(1)}) custom-call(s32[1,8]{1,0:T(1,128)S(1)} %copy-done.4, s32[1,8]{1,0:T(1,128)S(1)} %copy-done.5, s32[1,4]{1,0:T(1,128)S(1)} %add_bitcast_fusion.spot_ref, ...), custom_call_target="tpu_custom_call" | custom-call | tf_op jit(solution)/shard_map/pallas_call | solution.py:365
  42.9 0.8 collective-permute-done.9
  43.7 0.7 collective-permute-start.10
  44.4 2.7 %collective-permute-start.11 = (f32[2,6,64,128]{3,2,1,0:T(8,128)S(1)}, f32[2,6,64,128]{3,2,1,0:T(8,128)S(1)}, u32[]{:S(2)}, u32[]{:S(2)}) collective-permute-start(f32[2,6,64,128]{3,2,1,0:T(8,128)S(1)} %get-tuple-element.47), channel_id=1, source_target_pairs={{0,240},{1,241},{2,242},{3,243},{4,244},{5,245},{6,246},{7,247},{8... | collective-permute-start | bytes 1179656 | tf_op jit(solution)/shard_map/ppermute | solution.py:355
  47.2 0.0 collective-permute-start.12
  47.2 8.6 %collective-permute-done.12 = f32[128,128]{1,0:T(8,128)S(1)} collective-permute-done((f32[128,128]{1,0:T(8,128)S(1)}, f32[128,128]{1,0:T(8,128)S(1)}, u32[]{:S(2)}, u32[]{:S(2)}) %collective-permute-start.12) | collective-permute-done | bytes 65568 | tf_op jit(solution)/shard_map/ppermute | solution.py:361
  55.8 1.9 %collective-permute-start.13 = (f32[128,128]{1,0:T(8,128)S(1)}, f32[128,128]{1,0:T(8,128)S(1)}, u32[]{:S(2)}, u32[]{:S(2)}) collective-permute-start(f32[128,128]{1,0:T(8,128)S(1)} %add.26), channel_id=1, source_target_pairs={{0,128},{1,97},{2,130},{3,99},{4,132},{5,101},{6,134},{7,103},{8,1... | collective-permute-start | bytes 196616 | tf_op jit(solution)/shard_map/ppermute | solution.py:361
  57.6 3.5 %collective-permute-done.13 = f32[128,128]{1,0:T(8,128)S(1)} collective-permute-done((f32[128,128]{1,0:T(8,128)S(1)}, f32[128,128]{1,0:T(8,128)S(1)}, u32[]{:S(2)}, u32[]{:S(2)}) %collective-permute-start.13) | collective-permute-done | bytes 65568 | tf_op jit(solution)/shard_map/ppermute | solution.py:361
  61.1 1.3 %collective-permute-start.14 = (f32[128,128]{1,0:T(8,128)S(1)}, f32[128,128]{1,0:T(8,128)S(1)}, u32[]{:S(2)}, u32[]{:S(2)}) collective-permute-start(f32[128,128]{1,0:T(8,128)S(1)} %add.27), channel_id=1, source_target_pairs={{0,130},{1,129},{2,128},{3,131},{4,134},{5,133},{6,132},{7,135},{8... | collective-permute-start | bytes 196616 | tf_op jit(solution)/shard_map/ppermute | solution.py:361
  62.4 1.9 %collective-permute-done.14 = f32[128,128]{1,0:T(8,128)S(1)} collective-permute-done((f32[128,128]{1,0:T(8,128)S(1)}, f32[128,128]{1,0:T(8,128)S(1)}, u32[]{:S(2)}, u32[]{:S(2)}) %collective-permute-start.14) | collective-permute-done | bytes 65568 | tf_op jit(solution)/shard_map/ppermute | solution.py:361
  64.3 0.0 collective-permute-done.10.rowa_ref
  64.3 0.0 collective-permute-done.11.rowb_ref
  64.3 0.6 shard_map.92
  64.9 1.3 %collective-permute-start.17 = (f32[128,128]{1,0:T(8,128)S(1)}, f32[128,128]{1,0:T(8,128)S(1)}, u32[]{:S(2)}, u32[]{:S(2)}) collective-permute-start(f32[128,128]{1,0:T(8,128)S(1)} %add.28), channel_id=1, source_target_pairs={{0,16},{1,131},{2,18},{3,129},{4,20},{5,135},{6,22},{7,133},{8,24}... | collective-permute-start | bytes 196616 | tf_op jit(solution)/shard_map/ppermute | solution.py:361
  66.3 0.0 collective-permute-start.15
  66.3 2.1 %collective-permute-start.16 = (f32[2,256,128]{2,1,0:T(8,128)S(1)}, f32[2,256,128]{2,1,0:T(8,128)S(1)}, u32[]{:S(2)}, u32[]{:S(2)}) collective-permute-start(f32[2,256,128]{2,1,0:T(8,128)S(1)} %get-tuple-element.54), channel_id=1, source_target_pairs={{0,15},{1,2},{2,1},{3,4},{4,3},{5,6},{6,5},{7,8},{8,7},{9,10},{10,... | collective-permute-start | bytes 786440 | tf_op jit(solution)/shard_map/ppermute | solution.py:355
  68.4 0.9 %collective-permute-done.17 = f32[128,128]{1,0:T(8,128)S(1)} collective-permute-done((f32[128,128]{1,0:T(8,128)S(1)}, f32[128,128]{1,0:T(8,128)S(1)}, u32[]{:S(2)}, u32[]{:S(2)}) %collective-permute-start.17) | collective-permute-done | bytes 65568 | tf_op jit(solution)/shard_map/ppermute | solution.py:361
  69.4 1.3 %collective-permute-start.18 = (f32[128,128]{1,0:T(8,128)S(1)}, f32[128,128]{1,0:T(8,128)S(1)}, u32[]{:S(2)}, u32[]{:S(2)}) collective-permute-start(f32[128,128]{1,0:T(8,128)S(1)} %add.29), channel_id=1, source_target_pairs={{0,32},{1,5},{2,34},{3,7},{4,36},{5,1},{6,38},{7,3},{8,40},{9,13},... | collective-permute-start | bytes 196616 | tf_op jit(solution)/shard_map/ppermute | solution.py:361
  70.7 2.9 %collective-permute-done.18 = f32[128,128]{1,0:T(8,128)S(1)} collective-permute-done((f32[128,128]{1,0:T(8,128)S(1)}, f32[128,128]{1,0:T(8,128)S(1)}, u32[]{:S(2)}, u32[]{:S(2)}) %collective-permute-start.18) | collective-permute-done | bytes 65568 | tf_op jit(solution)/shard_map/ppermute | solution.py:361
  73.6 1.6 %collective-permute-start.19 = (f32[128,128]{1,0:T(8,128)S(1)}, f32[128,128]{1,0:T(8,128)S(1)}, u32[]{:S(2)}, u32[]{:S(2)}) collective-permute-start(f32[128,128]{1,0:T(8,128)S(1)} %add.30), channel_id=1, source_target_pairs={{0,96},{1,13},{2,98},{3,15},{4,100},{5,9},{6,102},{7,11},{8,104},{... | collective-permute-start | bytes 196616 | tf_op jit(solution)/shard_map/ppermute | solution.py:361
  75.2 2.8 %collective-permute-done.19 = f32[128,128]{1,0:T(8,128)S(1)} collective-permute-done((f32[128,128]{1,0:T(8,128)S(1)}, f32[128,128]{1,0:T(8,128)S(1)}, u32[]{:S(2)}, u32[]{:S(2)}) %collective-permute-start.19) | collective-permute-done | bytes 65568 | tf_op jit(solution)/shard_map/ppermute | solution.py:361
  78.0 5.0 %collective-permute-start.20 = (f32[128,128]{1,0:T(8,128)S(1)}, f32[128,128]{1,0:T(8,128)S(1)}, u32[]{:S(2)}, u32[]{:S(2)}) collective-permute-start(f32[128,128]{1,0:T(8,128)S(1)} %add.31.mine_ref), channel_id=1, source_target_pairs={{0,1},{1,0},{2,3},{3,2},{4,5},{5,4},{6,7},{7,6},{8,9},{9,8},{10,11... | collective-permute-start | bytes 196616 | tf_op jit(solution)/shard_map/ppermute | solution.py:361
  83.0 0.0 collective-permute-done.15.cola_ref
  83.1 0.0 collective-permute-done.16.colb_ref
  83.1 1.8 %shard_map.93 = f32[2,2,256,256]{3,2,1,0:T(8,128)} custom-call(s32[1,4]{1,0:T(1,128)S(1)} %add_bitcast_fusion.spot_ref, f32[2,2,256,256]{3,2,1,0:T(8,128)S(1)} %get-tuple-element.41.part_ref, f32[2,6,64,128]{3,2,1,0:T(8,128)S(1)} %collective-permute-done.10.rowa_ref, f32[2,6,64,128]{3,2,1,0:T(8,128)S(1)} %collective-permute-done.11.rowb_ref, ...), custom_call_target="tpu_custom_call" | custom-call | tf_op jit(solution)/shard_map/pallas_call | solution.py:365
  84.8 0.0 collective-permute-done.20.other_ref
  84.8 1.2 %shard_map.94 = f32[2,128,128]{2,1,0:T(8,128)} custom-call(s32[1,4]{1,0:T(1,128)S(1)} %add_bitcast_fusion.spot_ref, f32[2,128,128]{2,1,0:T(8,128)S(1)} %copy-done.2, f32[128,128]{1,0:T(8,128)S(1)} %add.31.mine_ref, f32[128,128]{1,0:T(8,128)S(1)} %collective-permute-done.20.other_ref), custom_call_target="tpu_custom_call" | custom-call | tf_op jit(solution)/shard_map/pallas_call | solution.py:365
  (9 shorter events, 0.1 us)
Async XLA Ops:
  0.6 11.2 %copy-start = (f32[2,2,256,256]{3,2,1,0:T(8,128)S(1)}, f32[2,2,256,256]{3,2,1,0:T(8,128)}, u32[]{:S(2)}) copy-start(f32[2,2,256,256]{3,2,1,0:T(8,128)} %obj_ref.11) | copy-start | bytes 3145732
  2.6 7.1 %collective-permute-start.4 = (f32[256,128]{1,0:T(8,128)S(1)}, f32[256,128]{1,0:T(8,128)S(1)}, u32[]{:S(2)}, u32[]{:S(2)}) collective-permute-start(f32[256,128]{1,0:T(8,128)S(1)} %get-tuple-element.33), channel_id=1, source_target_pairs={{0,1},{1,0},{2,3},{3,2},{4,5},{5,4},{6,7},{7,6},{8,9},{9,8},{10,11... | collective-permute-start | bytes 393224 | tf_op jit(solution)/shard_map/ppermute | solution.py:355
  6.0 5.9 %collective-permute-start.5 = (f32[256,128]{1,0:T(8,128)S(1)}, f32[256,128]{1,0:T(8,128)S(1)}, u32[]{:S(2)}, u32[]{:S(2)}) collective-permute-start(f32[256,128]{1,0:T(8,128)S(1)} %get-tuple-element.34), channel_id=1, source_target_pairs={{0,15},{1,2},{2,1},{3,4},{4,3},{5,6},{6,5},{7,8},{8,7},{9,10},{10,... | collective-permute-start | bytes 393224 | tf_op jit(solution)/shard_map/ppermute | solution.py:355
  7.1 11.0 %collective-permute-start = (f32[256,128]{1,0:T(8,128)S(1)}, f32[256,128]{1,0:T(8,128)S(1)}, u32[]{:S(2)}, u32[]{:S(2)}) collective-permute-start(f32[256,128]{1,0:T(8,128)S(1)} %get-tuple-element.29), channel_id=1, source_target_pairs={{0,1},{1,0},{2,3},{3,2},{4,5},{5,4},{6,7},{7,6},{8,9},{9,8},{10,11... | collective-permute-start | bytes 393224 | tf_op jit(solution)/shard_map/ppermute | solution.py:355
  9.7 13.7 %copy-start.1 = (bf16[4,2,256,256]{3,2,1,0:T(8,128)(2,1)S(1)}, bf16[4,2,256,256]{3,2,1,0:T(8,128)(2,1)}, u32[]{:S(2)}) copy-start(bf16[4,2,256,256]{3,2,1,0:T(8,128)(2,1)} %constant.11.clone.tabs_ref) | copy-start | bytes 3145732
  9.7 8.4 %collective-permute-start.1 = (f32[256,128]{1,0:T(8,128)S(1)}, f32[256,128]{1,0:T(8,128)S(1)}, u32[]{:S(2)}, u32[]{:S(2)}) collective-permute-start(f32[256,128]{1,0:T(8,128)S(1)} %get-tuple-element.30), channel_id=1, source_target_pairs={{0,15},{1,2},{2,1},{3,4},{4,3},{5,6},{6,5},{7,8},{8,7},{9,10},{10,... | collective-permute-start | bytes 393224 | tf_op jit(solution)/shard_map/ppermute | solution.py:355
  12.4 10.9 %collective-permute-start.6 = (f32[6,64,128]{2,1,0:T(8,128)S(1)}, f32[6,64,128]{2,1,0:T(8,128)S(1)}, u32[]{:S(2)}, u32[]{:S(2)}) collective-permute-start(f32[6,64,128]{2,1,0:T(8,128)S(1)} %get-tuple-element.35), channel_id=1, source_target_pairs={{0,16},{1,17},{2,18},{3,19},{4,20},{5,21},{6,22},{7,23},{8,24},{9,... | collective-permute-start | bytes 589832 | tf_op jit(solution)/shard_map/ppermute | solution.py:355
  12.6 10.9 %copy-start.2 = (f32[2,128,128]{2,1,0:T(8,128)S(1)}, f32[2,128,128]{2,1,0:T(8,128)}, u32[]{:S(2)}) copy-start(f32[2,128,128]{2,1,0:T(8,128)} %probe_ref.5) | copy-start | bytes 393220
  12.6 10.8 %collective-permute-start.7 = (f32[6,64,128]{2,1,0:T(8,128)S(1)}, f32[6,64,128]{2,1,0:T(8,128)S(1)}, u32[]{:S(2)}, u32[]{:S(2)}) collective-permute-start(f32[6,64,128]{2,1,0:T(8,128)S(1)} %get-tuple-element.36), channel_id=1, source_target_pairs={{0,240},{1,241},{2,242},{3,243},{4,244},{5,245},{6,246},{7,247},{8... | collective-permute-start | bytes 589832 | tf_op jit(solution)/shard_map/ppermute | solution.py:355
  18.7 8.7 %collective-permute-start.2 = (f32[6,64,128]{2,1,0:T(8,128)S(1)}, f32[6,64,128]{2,1,0:T(8,128)S(1)}, u32[]{:S(2)}, u32[]{:S(2)}) collective-permute-start(f32[6,64,128]{2,1,0:T(8,128)S(1)} %get-tuple-element.31), channel_id=1, source_target_pairs={{0,16},{1,17},{2,18},{3,19},{4,20},{5,21},{6,22},{7,23},{8,24},{9,... | collective-permute-start | bytes 589832 | tf_op jit(solution)/shard_map/ppermute | solution.py:355
  18.8 4.6 %copy-start.4 = (s32[1,8]{1,0:T(1,128)S(1)}, s32[1,8]{1,0:T(1,128)}, u32[]{:S(2)}) copy-start(s32[1,8]{1,0:T(1,128)} %row_ref.5) | copy-start | bytes 100
  18.8 4.6 %copy-start.5 = (s32[1,8]{1,0:T(1,128)S(1)}, s32[1,8]{1,0:T(1,128)}, u32[]{:S(2)}) copy-start(s32[1,8]{1,0:T(1,128)} %col_ref.5) | copy-start | bytes 100
  18.8 8.6 %collective-permute-start.3 = (f32[6,64,128]{2,1,0:T(8,128)S(1)}, f32[6,64,128]{2,1,0:T(8,128)S(1)}, u32[]{:S(2)}, u32[]{:S(2)}) collective-permute-start(f32[6,64,128]{2,1,0:T(8,128)S(1)} %get-tuple-element.32), channel_id=1, source_target_pairs={{0,240},{1,241},{2,242},{3,243},{4,244},{5,245},{6,246},{7,247},{8... | collective-permute-start | bytes 589832 | tf_op jit(solution)/shard_map/ppermute | solution.py:355
  23.4 4.1 %copy-start.3 = (f32[1,8,128,128]{3,2,1,0:T(8,128)S(1)}, f32[1,8,128,128]{3,2,1,0:T(8,128)}, u32[]{:S(2)}) copy-start(f32[1,8,128,128]{3,2,1,0:T(8,128)} %param.9) | copy-start | bytes 1572868
  36.8 3.7 %collective-permute-start.8 = (f32[128,128]{1,0:T(8,128)S(1)}, f32[128,128]{1,0:T(8,128)S(1)}, u32[]{:S(2)}, u32[]{:S(2)}) collective-permute-start(f32[128,128]{1,0:T(8,128)S(1)} %get-tuple-element.43), channel_id=1, source_target_pairs={{0,1},{1,0},{2,3},{3,2},{4,5},{5,4},{6,7},{7,6},{8,9},{9,8},{10,11... | collective-permute-start | bytes 196616 | tf_op jit(solution)/shard_map/ppermute | solution.py:361
  40.5 3.2 %collective-permute-start.9 = (f32[128,128]{1,0:T(8,128)S(1)}, f32[128,128]{1,0:T(8,128)S(1)}, u32[]{:S(2)}, u32[]{:S(2)}) collective-permute-start(f32[128,128]{1,0:T(8,128)S(1)} %add.24), channel_id=1, source_target_pairs={{0,4},{1,17},{2,6},{3,19},{4,0},{5,21},{6,2},{7,23},{8,12},{9,25},... | collective-permute-start | bytes 196616 | tf_op jit(solution)/shard_map/ppermute | solution.py:361
  43.7 20.6 %collective-permute-start.10 = (f32[2,6,64,128]{3,2,1,0:T(8,128)S(1)}, f32[2,6,64,128]{3,2,1,0:T(8,128)S(1)}, u32[]{:S(2)}, u32[]{:S(2)}) collective-permute-start(f32[2,6,64,128]{3,2,1,0:T(8,128)S(1)} %get-tuple-element.46), channel_id=1, source_target_pairs={{0,16},{1,17},{2,18},{3,19},{4,20},{5,21},{6,22},{7,23},{8,24},{9,... | collective-permute-start | bytes 1179656 | tf_op jit(solution)/shard_map/ppermute | solution.py:355
  44.4 19.9 %collective-permute-start.11 = (f32[2,6,64,128]{3,2,1,0:T(8,128)S(1)}, f32[2,6,64,128]{3,2,1,0:T(8,128)S(1)}, u32[]{:S(2)}, u32[]{:S(2)}) collective-permute-start(f32[2,6,64,128]{3,2,1,0:T(8,128)S(1)} %get-tuple-element.47), channel_id=1, source_target_pairs={{0,240},{1,241},{2,242},{3,243},{4,244},{5,245},{6,246},{7,247},{8... | collective-permute-start | bytes 1179656 | tf_op jit(solution)/shard_map/ppermute | solution.py:355
  47.2 8.6 %collective-permute-start.12 = (f32[128,128]{1,0:T(8,128)S(1)}, f32[128,128]{1,0:T(8,128)S(1)}, u32[]{:S(2)}, u32[]{:S(2)}) collective-permute-start(f32[128,128]{1,0:T(8,128)S(1)} %add.25), channel_id=1, source_target_pairs={{0,12},{1,33},{2,14},{3,35},{4,8},{5,37},{6,10},{7,39},{8,4},{9,41... | collective-permute-start | bytes 196616 | tf_op jit(solution)/shard_map/ppermute | solution.py:361
  55.8 5.3 %collective-permute-start.13 = (f32[128,128]{1,0:T(8,128)S(1)}, f32[128,128]{1,0:T(8,128)S(1)}, u32[]{:S(2)}, u32[]{:S(2)}) collective-permute-start(f32[128,128]{1,0:T(8,128)S(1)} %add.26), channel_id=1, source_target_pairs={{0,128},{1,97},{2,130},{3,99},{4,132},{5,101},{6,134},{7,103},{8,1... | collective-permute-start | bytes 196616 | tf_op jit(solution)/shard_map/ppermute | solution.py:361
  61.1 3.2 %collective-permute-start.14 = (f32[128,128]{1,0:T(8,128)S(1)}, f32[128,128]{1,0:T(8,128)S(1)}, u32[]{:S(2)}, u32[]{:S(2)}) collective-permute-start(f32[128,128]{1,0:T(8,128)S(1)} %add.27), channel_id=1, source_target_pairs={{0,130},{1,129},{2,128},{3,131},{4,134},{5,133},{6,132},{7,135},{8... | collective-permute-start | bytes 196616 | tf_op jit(solution)/shard_map/ppermute | solution.py:361
  64.9 4.4 %collective-permute-start.17 = (f32[128,128]{1,0:T(8,128)S(1)}, f32[128,128]{1,0:T(8,128)S(1)}, u32[]{:S(2)}, u32[]{:S(2)}) collective-permute-start(f32[128,128]{1,0:T(8,128)S(1)} %add.28), channel_id=1, source_target_pairs={{0,16},{1,131},{2,18},{3,129},{4,20},{5,135},{6,22},{7,133},{8,24}... | collective-permute-start | bytes 196616 | tf_op jit(solution)/shard_map/ppermute | solution.py:361
  66.3 16.8 %collective-permute-start.15 = (f32[2,256,128]{2,1,0:T(8,128)S(1)}, f32[2,256,128]{2,1,0:T(8,128)S(1)}, u32[]{:S(2)}, u32[]{:S(2)}) collective-permute-start(f32[2,256,128]{2,1,0:T(8,128)S(1)} %get-tuple-element.53), channel_id=1, source_target_pairs={{0,1},{1,0},{2,3},{3,2},{4,5},{5,4},{6,7},{7,6},{8,9},{9,8},{10,11... | collective-permute-start | bytes 786440 | tf_op jit(solution)/shard_map/ppermute | solution.py:355
  66.3 16.8 %collective-permute-start.16 = (f32[2,256,128]{2,1,0:T(8,128)S(1)}, f32[2,256,128]{2,1,0:T(8,128)S(1)}, u32[]{:S(2)}, u32[]{:S(2)}) collective-permute-start(f32[2,256,128]{2,1,0:T(8,128)S(1)} %get-tuple-element.54), channel_id=1, source_target_pairs={{0,15},{1,2},{2,1},{3,4},{4,3},{5,6},{6,5},{7,8},{8,7},{9,10},{10,... | collective-permute-start | bytes 786440 | tf_op jit(solution)/shard_map/ppermute | solution.py:355
  69.4 4.2 %collective-permute-start.18 = (f32[128,128]{1,0:T(8,128)S(1)}, f32[128,128]{1,0:T(8,128)S(1)}, u32[]{:S(2)}, u32[]{:S(2)}) collective-permute-start(f32[128,128]{1,0:T(8,128)S(1)} %add.29), channel_id=1, source_target_pairs={{0,32},{1,5},{2,34},{3,7},{4,36},{5,1},{6,38},{7,3},{8,40},{9,13},... | collective-permute-start | bytes 196616 | tf_op jit(solution)/shard_map/ppermute | solution.py:361
  73.6 4.4 %collective-permute-start.19 = (f32[128,128]{1,0:T(8,128)S(1)}, f32[128,128]{1,0:T(8,128)S(1)}, u32[]{:S(2)}, u32[]{:S(2)}) collective-permute-start(f32[128,128]{1,0:T(8,128)S(1)} %add.30), channel_id=1, source_target_pairs={{0,96},{1,13},{2,98},{3,15},{4,100},{5,9},{6,102},{7,11},{8,104},{... | collective-permute-start | bytes 196616 | tf_op jit(solution)/shard_map/ppermute | solution.py:361
  78.0 6.8 %collective-permute-start.20 = (f32[128,128]{1,0:T(8,128)S(1)}, f32[128,128]{1,0:T(8,128)S(1)}, u32[]{:S(2)}, u32[]{:S(2)}) collective-permute-start(f32[128,128]{1,0:T(8,128)S(1)} %add.31.mine_ref), channel_id=1, source_target_pairs={{0,1},{1,0},{2,3},{3,2},{4,5},{5,4},{6,7},{7,6},{8,9},{9,8},{10,11... | collective-permute-start | bytes 196616 | tf_op jit(solution)/shard_map/ppermute | solution.py:361

commit v6 on v5

--- a/solution.py
+++ b/solution.py
@@ -16,7 +16,7 @@
 LANES = 128
 BOTH = ("row", "col")
 GRANT = 16 * 1024 * 1024
-MASKS = ((4, 16), (12, 32), (128, 96), (130, 128), (16, 130), (32, 4), (96, 12))
+MASKS = ((4, 32), (12, 128), (128, 130), (130, 96), (16, 4), (32, 12), (96, 16))
 
 
 def split_table(table):
@@ -51,20 +51,21 @@
 
 def two_sided(tabs_ref, right, left, real, imag):
     width = real.shape[1]
+    starts = range(0, real.shape[0], width)
     field = split(jnp.concatenate([real, imag], axis=1))
     half = mul3(field, (tabs_ref[right, 0], tabs_ref[right, 1]))
-    real, imag = half[:, :width], half[:, width:]
     field = jnp.concatenate(
         [
-            jnp.concatenate([real[:width], real[width:]], axis=1),
-            jnp.concatenate([imag[:width], imag[width:]], axis=1),
+            jnp.concatenate([half[s : s + width, :width] for s in starts], axis=1),
+            jnp.concatenate([half[s : s + width, width:] for s in starts], axis=1),
         ],
         axis=0,
     )
     full = mul3((tabs_ref[left, 0], tabs_ref[left, 1]), split(field))
-    real = jnp.concatenate([full[:width, :width], full[:width, width:]], axis=0)
-    imag = jnp.concatenate([full[width:, :width], full[width:, width:]], axis=0)
-    return real, imag
+    return tuple(
+        jnp.concatenate([full[part * width : (part + 1) * width, s : s + width] for s in starts], axis=0)
+        for part in range(2)
+    )
 
 
 def columns(piece_ref, first):
@@ -85,47 +86,56 @@
     return before, after
 
 
-def pack_kernel(spot_ref, obj_ref, *refs):
-    *outs, held, sems = refs
-    first = lax.broadcasted_iota(jnp.int32, (held.shape[2], LANES), 1) < LANES // 2
-    copies = [pltpu.make_async_copy(obj_ref.at[p], held.at[p], sems.at[p]) for p in range(2)]
-    for copy in copies:
-        copy.start()
-    for piece in range(2):
-        copies[piece].wait()
-        left, right = columns(held.at[piece], first)
-        outs[2 * piece][...] = pick(spot_ref, 1, right, left)
-        outs[2 * piece + 1][...] = pick(spot_ref, 1, left, right)
-
-
-def rows_kernel(spot_ref, obj_ref, cola_ref, colb_ref, rowa_ref, rowb_ref, *, piece):
-    half = LANES // 2
-    low, high = slice(0, half), slice(obj_ref.shape[2] - half, obj_ref.shape[2])
+def pack_piece(spot_ref, piece_ref, cola_ref, colb_ref, rowa_ref, rowb_ref):
+    half = LANES // 2
+    tile = piece_ref.shape[1]
+    first = lax.broadcasted_iota(jnp.int32, (tile, LANES), 1) < half
+    left, right = columns(piece_ref, first)
+    cola_ref[...] = pick(spot_ref, 1, right, left)
+    colb_ref[...] = pick(spot_ref, 1, left, right)
     for part in range(2):
         for block in range(2):
             cols = slice(block * LANES, (block + 1) * LANES)
-            top, bottom = obj_ref[piece, part, low, cols], obj_ref[piece, part, high, cols]
+            top, bottom = piece_ref[part, :half, cols], piece_ref[part, tile - half :, cols]
             rowa_ref[2 * part + block] = pick(spot_ref, 0, bottom, top)
             rowb_ref[2 * part + block] = pick(spot_ref, 0, top, bottom)
+
+
+def pack_kernel(spot_ref, obj_ref, cola_ref, colb_ref, rowa_ref, rowb_ref, held, sem):
+    copy = pltpu.make_async_copy(obj_ref.at[0], held, sem)
+    copy.start()
+    copy.wait()
+    pack_piece(spot_ref, held, cola_ref, colb_ref, rowa_ref, rowb_ref)
+
+
+def pack_next_kernel(spot_ref, obj_ref, cola_ref, colb_ref, rowa_ref, rowb_ref):
+    pack_piece(spot_ref, obj_ref.at[1], cola_ref, colb_ref, rowa_ref, rowb_ref)
+
+
+def corner_kernel(spot_ref, cola_ref, colb_ref, rowa_ref, rowb_ref):
+    half = LANES // 2
+    low, high = slice(0, half), slice(cola_ref.shape[0] - half, cola_ref.shape[0])
     tops = beside(spot_ref, 1, cola_ref[low], colb_ref[low])
     bottoms = beside(spot_ref, 1, cola_ref[high], colb_ref[high])
-    for place, top, bottom in zip((4, 5), tops, bottoms):
+    for place, (top, bottom) in enumerate(zip(tops, bottoms)):
         rowa_ref[place] = pick(spot_ref, 0, bottom, top)
         rowb_ref[place] = pick(spot_ref, 0, top, bottom)
 
 
-def grow(ext, spot_ref, piece_ref, cola_ref, colb_ref, rowa_ref, rowb_ref):
+def grow(ext, spot_ref, piece_ref, cola_ref, colb_ref, rowa_ref, rowb_ref, cora_ref, corb_ref):
     half = LANES // 2
     tile = piece_ref.shape[1]
     sides = beside(spot_ref, 1, cola_ref[...], colb_ref[...])
     for part in range(2):
         for block in range(4):
-            place = 2 * part + block - 1 if block in (1, 2) else 4 + block // 3
-            top, bottom = beside(spot_ref, 0, rowa_ref[place], rowb_ref[place])
             if block in (1, 2):
+                place = 2 * part + block - 1
+                top, bottom = beside(spot_ref, 0, rowa_ref[place], rowb_ref[place])
                 middle = piece_ref[part, :, (block - 1) * LANES : block * LANES]
             else:
-                middle = sides[block // 3]
+                place = block // 3
+                top, bottom = beside(spot_ref, 0, cora_ref[place], corb_ref[place])
+                middle = sides[place]
             for strip, start in ((top, 0), (middle, half), (bottom, half + tile)):
                 if (block == 0 and part == 0) or (block == 3 and part == 1):
                     strip = pltpu.roll(strip, half, 1)
@@ -166,37 +176,37 @@
 
 
 def first_kernel(
-    row_ref, col_ref, spot_ref, obj_ref, cola_ref, colb_ref, rowa_ref, rowb_ref, probe_ref, tabs_ref,
-    win_ref, mid_ref, ext,
+    row_ref, col_ref, spot_ref, obj_ref, cola_ref, colb_ref, rowa_ref, rowb_ref, cora_ref, corb_ref,
+    probe_ref, tabs_ref, win_ref, mid_ref, ext, *, group,
 ):
     width = probe_ref.shape[1]
-    grow(ext, spot_ref, obj_ref.at[0], cola_ref, colb_ref, rowa_ref, rowb_ref)
-
-    def pair(index, _):
-        slots = (2 * index, 2 * index + 1)
+    grow(ext, spot_ref, obj_ref.at[0], cola_ref, colb_ref, rowa_ref, rowb_ref, cora_ref, corb_ref)
+
+    def some(index, _):
+        slots = [group * index + place for place in range(group)]
         first_re, first_im = windows(ext, row_ref, col_ref, slots, width)
-        probe_re, probe_im = (jnp.concatenate([probe_ref[p]] * 2, axis=0) for p in range(2))
+        probe_re, probe_im = (jnp.concatenate([probe_ref[p]] * group, axis=0) for p in range(2))
         wave_re = probe_re * first_re - probe_im * first_im
         wave_im = probe_re * first_im + probe_im * first_re
         store(win_ref, slots, (first_re, first_im))
         store(mid_ref, slots, two_sided(tabs_ref, 0, 1, wave_re, wave_im))
         return 0
 
-    lax.fori_loop(0, row_ref.shape[1] // 2, pair, 0)
+    lax.fori_loop(0, row_ref.shape[1] // group, some, 0, unroll=True)
 
 
 def second_kernel(
     row_ref, col_ref, spot_ref, live_ref, obj_ref, cola_ref, colb_ref, rowa_ref, rowb_ref,
-    win_ref, mid_ref, measured_ref, tabs_ref,
+    cora_ref, corb_ref, win_ref, mid_ref, measured_ref, tabs_ref,
     grad_ref, down_ref, keep_ref, send_ref,
-    ext, sum_ref,
+    ext, sum_ref, *, group,
 ):
     width = win_ref.shape[2]
-    grow(ext, spot_ref, obj_ref.at[1], cola_ref, colb_ref, rowa_ref, rowb_ref)
+    grow(ext, spot_ref, obj_ref.at[1], cola_ref, colb_ref, rowa_ref, rowb_ref, cora_ref, corb_ref)
     sum_ref[...] = jnp.zeros_like(sum_ref)
 
-    def pair(index, _):
-        slots = (2 * index, 2 * index + 1)
+    def some(index, _):
+        slots = [group * index + place for place in range(group)]
         second_re, second_im = windows(ext, row_ref, col_ref, slots, width)
         mid_re, mid_im = (stacked(mid_ref, slots, part) for part in range(2))
         exit_re = mid_re * second_re - mid_im * second_im
@@ -220,11 +230,14 @@
         first_re, first_im = (stacked(win_ref, slots, part) for part in range(2))
         sum_re = first_re * down_re + first_im * down_im
         sum_im = first_re * down_im - first_im * down_re
-        sum_ref[0] += sum_re[:width] + sum_re[width:]
-        sum_ref[1] += sum_im[:width] + sum_im[width:]
+        for part, value in enumerate((sum_re, sum_im)):
+            total = value[:width]
+            for start in range(width, group * width, width):
+                total += value[start : start + width]
+            sum_ref[part] += total
         return 0
 
-    lax.fori_loop(0, row_ref.shape[1] // 2, pair, 0)
+    lax.fori_loop(0, row_ref.shape[1] // group, some, 0, unroll=True)
     keep_ref[...] = pick(spot_ref, 1, sum_ref[0], sum_ref[1])
     send_ref[...] = pick(spot_ref, 1, sum_ref[1], sum_ref[0])
 
@@ -380,26 +393,30 @@
     spot = jnp.stack([jnp.asarray(entry, jnp.int32) for entry in place]).reshape(1, 4)
     tabs = jnp.asarray(make_tables(width))
     grown = pltpu.VMEM((2, 4, tile + width, LANES), jnp.float32)
-    packed = pl.pallas_call(
-        pack_kernel, out_shape=tuple([array(*side)] * 4),
-        in_specs=smem(1) + [pl.BlockSpec(memory_space=pltpu.HBM)], out_specs=tuple(vmem(4)),
-        scratch_shapes=[pltpu.VMEM(object_field.shape, jnp.float32), pltpu.SemaphoreType.DMA((2,))],
-        compiler_params=pltpu.CompilerParams(vmem_limit_bytes=GRANT),
-    )(spot, pltpu.with_memory_space_constraint(object_field, pltpu.HBM))
-    halos = []
-    cols = [meet(packed[2 * piece : 2 * piece + 2], 1) for piece in range(2)]
-    for piece in range(2):
-        strips = call(
-            functools.partial(rows_kernel, piece=piece), [array(*edge)] * 2,
-            (spot,), (object_field, *cols[piece]),
-        )
-        halos.append((*cols[piece], *meet(strips, 0)))
+    outer, ends = [array(*side)] * 2 + [array(4, half, LANES)] * 2, [array(2, half, LANES)] * 2
+    packed = [
+        pl.pallas_call(
+            pack_kernel, out_shape=tuple(outer),
+            in_specs=smem(1) + [pl.BlockSpec(memory_space=pltpu.HBM)], out_specs=tuple(vmem(4)),
+            scratch_shapes=[pltpu.VMEM((2, tile, tile), jnp.float32), pltpu.SemaphoreType.DMA],
+            compiler_params=pltpu.CompilerParams(vmem_limit_bytes=GRANT),
+        )(spot, pltpu.with_memory_space_constraint(object_field, pltpu.HBM)),
+        call(pack_next_kernel, outer, (spot,), (object_field,)),
+    ]
+    cols = [meet(strips[:2], 1) for strips in packed]
+    rows = meet(packed[0][2:], 0)
+    ends0 = call(corner_kernel, ends, (spot,), cols[0])
+    rows[0], rows[1], *strips = lax.optimization_barrier((*rows, *packed[1][2:]))
+    halos = [(*cols[0], *rows, *meet(ends0, 0))]
+    rows = meet(strips, 0)
+    halos.append((*cols[1], *rows, *meet(call(corner_kernel, ends, (spot,), cols[1]), 0)))
     win, mid = call(
-        first_kernel, [fields] * 2, (offset_row, offset_col, spot),
+        functools.partial(first_kernel, group=2), [fields] * 2, (offset_row, offset_col, spot),
         (object_field, *halos[0], probe, tabs), (grown,),
     )
     grad, down, mine, send = call(
-        second_kernel, [fields] * 2 + [array(*plane)] * 2, (offset_row, offset_col, spot, live),
+        functools.partial(second_kernel, group=count), [fields] * 2 + [array(*plane)] * 2,
+        (offset_row, offset_col, spot, live),
         (object_field, *halos[1], win, mid, intensity[0], tabs),
         (grown, pltpu.VMEM((2, *plane), jnp.float32)),
     )

time: 86.2 us -> 88.2 us (1.023)
  starting transfers between devices: 37.6 us -> 49 us
  waiting for transfers between devices: 24.5 us -> 19.8 us
  Pallas kernels: 22.2 us -> 17.6 us
    ppermute x9, starting transfers between devices: 15.2 us -> 24.9 us  [swap(): lax.ppermute(value, BOTH, [(i, i ^ masks[i % 2]) for i in range(count)])]
    ppermute x9, waiting for transfers between devices: 22.3 us -> 17.6 us  [swap(): lax.ppermute(value, BOTH, [(i, i ^ masks[i % 2]) for i in range(count)])]
    pallas_call x8 -> x9, Pallas kernels: 20.3 us -> 15.8 us  [call(): pl.pallas_call(kernel, out_shape=tuple(out_shape), in_specs=smem(len(scal...]
    ppermute x12 -> x16, starting transfers between devices: 22.4 us -> 24.2 us  [meet(): got.append(lax.ppermute(strip, BOTH, pairs))]
    ppermute x12 -> x16, waiting for transfers between devices: 2.15 us -> 2.14 us  [meet(): got.append(lax.ppermute(strip, BOTH, pairs))]
  transfers between devices with their start and end apart: 21 -> 25, of which waited for: 9 -> 10; matrix products, arithmetic and copies ran while one was open for 0% -> 0% of each run, Pallas kernels for 11% -> 9%
where the time goes in v6:
time: 88.2 us; the launch traced here: 88.1 us
  starting transfers between devices  49 us (56%)
  waiting for transfers between devices  19.8 us (22%)
  Pallas kernels  17.6 us (20%)
  between operations  1.55 us (2%)
    ppermute x9, starting transfers between devices, swap(): lax.ppermute(value, BOTH, [(i, i ^ masks[i % 2]) for i in range(count)])  24.9 us
    ppermute x16, starting transfers between devices, meet(): got.append(lax.ppermute(strip, BOTH, pairs))  24.2 us
    ppermute x9, waiting for transfers between devices, swap(): lax.ppermute(value, BOTH, [(i, i ^ masks[i % 2]) for i in range(count)])  17.6 us
    pallas_call x9, Pallas kernels, call(): pl.pallas_call(kernel, out_shape=tuple(out_shape), in_specs=smem(len(scal...  15.8 us
    ppermute x16, waiting for transfers between devices, meet(): got.append(lax.ppermute(strip, BOTH, pairs))  2.14 us
  transfers between devices with their start and end apart: 25, of which 10 were waited for; matrix products, arithmetic and copies ran while one was open for 0% of the time, Pallas kernels for 9%

profile of v6, /device:TPU:1, one launch (start us, length us, event | category | flops | bytes accessed | tf_op | source)
XLA Modules:
  0.0 88.1 jit_solution(9405815675471240614)
XLA Ops:
  0.6 0.0 copy-start
  0.7 0.1 add_bitcast_fusion.spot_ref
  0.7 1.7 %shard_map.87 = (f32[256,128]{1,0:T(8,128)S(1)}, f32[256,128]{1,0:T(8,128)S(1)}, f32[4,64,128]{2,1,0:T(8,128)S(1)}, f32[4,64,128]{2,1,0:T(8,128)S(1)}) custom-call(s32[1,4]{1,0:T(1,128)S(1)} %add_bitcast_fusion.spot_ref, f32[2,2,256,256]{3,2,1,0:T(8,128)} %obj_ref.9), custom_call_target="tpu_custom_call" | custom-call | tf_op jit(solution)/shard_map/pallas_call | solution.py:398
  2.5 0.0 copy-start.1
  2.5 3.3 %collective-permute-start.8 = (f32[256,128]{1,0:T(8,128)S(1)}, f32[256,128]{1,0:T(8,128)S(1)}, u32[]{:S(2)}, u32[]{:S(2)}) collective-permute-start(f32[256,128]{1,0:T(8,128)S(1)} %get-tuple-element.47), channel_id=1, source_target_pairs={{0,1},{1,0},{2,3},{3,2},{4,5},{5,4},{6,7},{7,6},{8,9},{9,8},{10,11... | collective-permute-start | bytes 393224 | tf_op jit(solution)/shard_map/ppermute | solution.py:368
  5.8 1.2 %collective-permute-start.9 = (f32[256,128]{1,0:T(8,128)S(1)}, f32[256,128]{1,0:T(8,128)S(1)}, u32[]{:S(2)}, u32[]{:S(2)}) collective-permute-start(f32[256,128]{1,0:T(8,128)S(1)} %get-tuple-element.48), channel_id=1, source_target_pairs={{0,15},{1,2},{2,1},{3,4},{4,3},{5,6},{6,5},{7,8},{8,7},{9,10},{10,... | collective-permute-start | bytes 393224 | tf_op jit(solution)/shard_map/ppermute | solution.py:368
  7.0 1.6 %collective-permute-start.2 = (f32[4,64,128]{2,1,0:T(8,128)S(1)}, f32[4,64,128]{2,1,0:T(8,128)S(1)}, u32[]{:S(2)}, u32[]{:S(2)}) collective-permute-start(f32[4,64,128]{2,1,0:T(8,128)S(1)} %get-tuple-element.39), channel_id=1, source_target_pairs={{0,16},{1,17},{2,18},{3,19},{4,20},{5,21},{6,22},{7,23},{8,24},{9,... | collective-permute-start | bytes 393224 | tf_op jit(solution)/shard_map/ppermute | solution.py:368
  8.6 4.8 %collective-permute-start.3 = (f32[4,64,128]{2,1,0:T(8,128)S(1)}, f32[4,64,128]{2,1,0:T(8,128)S(1)}, u32[]{:S(2)}, u32[]{:S(2)}) collective-permute-start(f32[4,64,128]{2,1,0:T(8,128)S(1)} %get-tuple-element.40), channel_id=1, source_target_pairs={{0,240},{1,241},{2,242},{3,243},{4,244},{5,245},{6,246},{7,247},{8... | collective-permute-start | bytes 393224 | tf_op jit(solution)/shard_map/ppermute | solution.py:368
  13.4 0.7 shard_map.86
  14.1 3.3 %collective-permute-start = (f32[256,128]{1,0:T(8,128)S(1)}, f32[256,128]{1,0:T(8,128)S(1)}, u32[]{:S(2)}, u32[]{:S(2)}) collective-permute-start(f32[256,128]{1,0:T(8,128)S(1)} %get-tuple-element.37), channel_id=1, source_target_pairs={{0,1},{1,0},{2,3},{3,2},{4,5},{5,4},{6,7},{7,6},{8,9},{9,8},{10,11... | collective-permute-start | bytes 393224 | tf_op jit(solution)/shard_map/ppermute | solution.py:368
  17.3 0.0 collective-permute-done.8.cola_ref
  17.3 0.0 collective-permute-start.1
  17.3 0.0 collective-permute-done.9.colb_ref
  17.4 0.6 shard_map.89
  17.9 0.1 collective-permute-start.10
  18.0 0.0 collective-permute-done.2.rowa_ref
  18.0 0.0 collective-permute-done.3.rowb_ref
  18.0 1.4 %collective-permute-start.4 = (f32[4,64,128]{2,1,0:T(8,128)S(1)}, f32[4,64,128]{2,1,0:T(8,128)S(1)}, u32[]{:S(2)}, u32[]{:S(2)}) collective-permute-start(f32[4,64,128]{2,1,0:T(8,128)S(1)} %get-tuple-element.43), channel_id=1, source_target_pairs={{0,16},{1,17},{2,18},{3,19},{4,20},{5,21},{6,22},{7,23},{8,24},{9,... | collective-permute-start | bytes 393224 | tf_op jit(solution)/shard_map/ppermute | solution.py:368
  19.5 0.5 collective-permute-start.5
  20.0 0.0 collective-permute-done.cola_ref
  20.0 3.1 %collective-permute-start.11 = (f32[2,64,128]{2,1,0:T(8,128)S(1)}, f32[2,64,128]{2,1,0:T(8,128)S(1)}, u32[]{:S(2)}, u32[]{:S(2)}) collective-permute-start(f32[2,64,128]{2,1,0:T(8,128)S(1)} %get-tuple-element.52), channel_id=1, source_target_pairs={{0,240},{1,241},{2,242},{3,243},{4,244},{5,245},{6,246},{7,247},{8... | collective-permute-start | bytes 196616 | tf_op jit(solution)/shard_map/ppermute | solution.py:368
  23.1 0.2 collective-permute-done.1.colb_ref
  23.2 0.6 shard_map.88
  23.8 0.1 collective-permute-start.6
  23.9 0.0 collective-permute-done.10.cora_ref
  23.9 0.0 copy-start.4
  23.9 0.0 copy-start.5
  23.9 1.4 %collective-permute-start.7 = (f32[2,64,128]{2,1,0:T(8,128)S(1)}, f32[2,64,128]{2,1,0:T(8,128)S(1)}, u32[]{:S(2)}, u32[]{:S(2)}) collective-permute-start(f32[2,64,128]{2,1,0:T(8,128)S(1)} %get-tuple-element.46), channel_id=1, source_target_pairs={{0,240},{1,241},{2,242},{3,243},{4,244},{5,245},{6,246},{7,247},{8... | collective-permute-start | bytes 196616 | tf_op jit(solution)/shard_map/ppermute | solution.py:368
  26.0 0.0 copy-start.3
  26.0 0.1 collective-permute-done.11.corb_ref
  26.1 2.2 %shard_map.90 = (f32[8,2,128,128]{3,2,1,0:T(8,128)S(1)}, f32[8,2,128,128]{3,2,1,0:T(8,128)S(1)}) custom-call(s32[1,8]{1,0:T(1,128)S(1)} %copy-done.4, s32[1,8]{1,0:T(1,128)S(1)} %copy-done.5, s32[1,4]{1,0:T(1,128)S(1)} %add_bitcast_fusion.spot_ref, f32[2,2,256,256]{3,2,1,0:T(8,128)S(1)} %copy-done, f32[256,128]{1,0:T(8,128)S(1)} %collective-permute-done.8.cola_ref, ...), custom_call_target="tpu_custom_call" | custom-call | tf_op jit(solution)/shard_map/pallas_call | solution.py:378
  28.4 0.0 collective-permute-done.6.cora_ref
  28.4 1.8 %collective-permute-done.7.corb_ref = f32[2,64,128]{2,1,0:T(8,128)S(1)} collective-permute-done((f32[2,64,128]{2,1,0:T(8,128)S(1)}, f32[2,64,128]{2,1,0:T(8,128)S(1)}, u32[]{:S(2)}, u32[]{:S(2)}) %collective-permute-start.7) | collective-permute-done | bytes 65568 | tf_op jit(solution)/shard_map/ppermute | solution.py:368
  30.2 0.0 collective-permute-done.4.rowa_ref
  30.2 0.0 collective-permute-done.5.rowb_ref
  30.3 5.9 %shard_map.91 = (f32[8,2,128,128]{3,2,1,0:T(8,128)S(1)}, f32[8,2,128,128]{3,2,1,0:T(8,128)S(1)}, f32[128,128]{1,0:T(8,128)S(1)}, f32[128,128]{1,0:T(8,128)S(1)}) custom-call(s32[1,8]{1,0:T(1,128)S(1)} %copy-done.4, s32[1,8]{1,0:T(1,128)S(1)} %copy-done.5, s32[1,4]{1,0:T(1,128)S(1)} %add_bitcast_fusion.spot_ref, s32[1,1]{1,0:T(1,128)S(6)} %copy.9.live_ref, ...), custom_call_target="tpu_custom_call" | custom-call | tf_op jit(solution)/shard_map/pallas_call | solution.py:378
  36.1 3.3 %collective-permute-start.12 = (f32[128,128]{1,0:T(8,128)S(1)}, f32[128,128]{1,0:T(8,128)S(1)}, u32[]{:S(2)}, u32[]{:S(2)}) collective-permute-start(f32[128,128]{1,0:T(8,128)S(1)} %get-tuple-element.59), channel_id=1, source_target_pairs={{0,1},{1,0},{2,3},{3,2},{4,5},{5,4},{6,7},{7,6},{8,9},{9,8},{10,11... | collective-permute-start | bytes 196616 | tf_op jit(solution)/shard_map/ppermute | solution.py:374
  39.5 0.9 %collective-permute-done.12 = f32[128,128]{1,0:T(8,128)S(1)} collective-permute-done((f32[128,128]{1,0:T(8,128)S(1)}, f32[128,128]{1,0:T(8,128)S(1)}, u32[]{:S(2)}, u32[]{:S(2)}) %collective-permute-start.12) | collective-permute-done | bytes 65568 | tf_op jit(solution)/shard_map/ppermute | solution.py:374
  40.4 0.1 collective-permute-start.13
  40.5 2.3 %shard_map.92 = (f32[2,2,256,256]{3,2,1,0:T(8,128)S(1)}, f32[2,6,64,128]{3,2,1,0:T(8,128)S(1)}, f32[2,6,64,128]{3,2,1,0:T(8,128)S(1)}, f32[2,256,128]{2,1,0:T(8,128)S(1)}, f32[2,256,128]{2,1,0:T(8,128)S(1)}) custom-call(s32[1,8]{1,0:T(1,128)S(1)} %copy-done.4, s32[1,8]{1,0:T(1,128)S(1)} %copy-done.5, s32[1,4]{1,0:T(1,128)S(1)} %add_bitcast_fusion.spot_ref, ...), custom_call_target="tpu_custom_call" | custom-call | tf_op jit(solution)/shard_map/pallas_call | solution.py:378
  42.8 1.7 %collective-permute-done.13 = f32[128,128]{1,0:T(8,128)S(1)} collective-permute-done((f32[128,128]{1,0:T(8,128)S(1)}, f32[128,128]{1,0:T(8,128)S(1)}, u32[]{:S(2)}, u32[]{:S(2)}) %collective-permute-start.13) | collective-permute-done | bytes 65568 | tf_op jit(solution)/shard_map/ppermute | solution.py:374
  44.5 0.1 collective-permute-start.14
  44.6 1.4 %collective-permute-start.15 = (f32[2,6,64,128]{3,2,1,0:T(8,128)S(1)}, f32[2,6,64,128]{3,2,1,0:T(8,128)S(1)}, u32[]{:S(2)}, u32[]{:S(2)}) collective-permute-start(f32[2,6,64,128]{3,2,1,0:T(8,128)S(1)} %get-tuple-element.63), channel_id=1, source_target_pairs={{0,240},{1,241},{2,242},{3,243},{4,244},{5,245},{6,246},{7,247},{8... | collective-permute-start | bytes 1179656 | tf_op jit(solution)/shard_map/ppermute | solution.py:368
  46.1 1.1 %collective-permute-start.16 = (f32[128,128]{1,0:T(8,128)S(1)}, f32[128,128]{1,0:T(8,128)S(1)}, u32[]{:S(2)}, u32[]{:S(2)}) collective-permute-start(f32[128,128]{1,0:T(8,128)S(1)} %add.25), channel_id=1, source_target_pairs={{0,12},{1,129},{2,14},{3,131},{4,8},{5,133},{6,10},{7,135},{8,4},{... | collective-permute-start | bytes 196616 | tf_op jit(solution)/shard_map/ppermute | solution.py:374
  47.1 2.3 %collective-permute-done.16 = f32[128,128]{1,0:T(8,128)S(1)} collective-permute-done((f32[128,128]{1,0:T(8,128)S(1)}, f32[128,128]{1,0:T(8,128)S(1)}, u32[]{:S(2)}, u32[]{:S(2)}) %collective-permute-start.16) | collective-permute-done | bytes 65568 | tf_op jit(solution)/shard_map/ppermute | solution.py:374
  49.5 1.7 %collective-permute-start.17 = (f32[128,128]{1,0:T(8,128)S(1)}, f32[128,128]{1,0:T(8,128)S(1)}, u32[]{:S(2)}, u32[]{:S(2)}) collective-permute-start(f32[128,128]{1,0:T(8,128)S(1)} %add.26), channel_id=1, source_target_pairs={{0,128},{1,131},{2,130},{3,129},{4,132},{5,135},{6,134},{7,133},{8... | collective-permute-start | bytes 196616 | tf_op jit(solution)/shard_map/ppermute | solution.py:374
  51.2 3.0 %collective-permute-done.17 = f32[128,128]{1,0:T(8,128)S(1)} collective-permute-done((f32[128,128]{1,0:T(8,128)S(1)}, f32[128,128]{1,0:T(8,128)S(1)}, u32[]{:S(2)}, u32[]{:S(2)}) %collective-permute-start.17) | collective-permute-done | bytes 65568 | tf_op jit(solution)/shard_map/ppermute | solution.py:374
  54.2 0.8 collective-permute-start.18
  55.0 4.5 %collective-permute-done.18 = f32[128,128]{1,0:T(8,128)S(1)} collective-permute-done((f32[128,128]{1,0:T(8,128)S(1)}, f32[128,128]{1,0:T(8,128)S(1)}, u32[]{:S(2)}, u32[]{:S(2)}) %collective-permute-start.18) | collective-permute-done | bytes 65568 | tf_op jit(solution)/shard_map/ppermute | solution.py:374
  59.5 0.0 collective-permute-done.14.rowa_ref
  59.5 0.0 collective-permute-done.15.rowb_ref
  59.6 0.6 shard_map.93
  60.2 9.4 %collective-permute-start.21 = (f32[128,128]{1,0:T(8,128)S(1)}, f32[128,128]{1,0:T(8,128)S(1)}, u32[]{:S(2)}, u32[]{:S(2)}) collective-permute-start(f32[128,128]{1,0:T(8,128)S(1)} %add.28), channel_id=1, source_target_pairs={{0,16},{1,5},{2,18},{3,7},{4,20},{5,1},{6,22},{7,3},{8,24},{9,13},... | collective-permute-start | bytes 196616 | tf_op jit(solution)/shard_map/ppermute | solution.py:374
  69.6 0.0 collective-permute-start.19
  69.6 1.8 %collective-permute-start.20 = (f32[2,256,128]{2,1,0:T(8,128)S(1)}, f32[2,256,128]{2,1,0:T(8,128)S(1)}, u32[]{:S(2)}, u32[]{:S(2)}) collective-permute-start(f32[2,256,128]{2,1,0:T(8,128)S(1)} %get-tuple-element.70), channel_id=1, source_target_pairs={{0,15},{1,2},{2,1},{3,4},{4,3},{5,6},{6,5},{7,8},{8,7},{9,10},{10,... | collective-permute-start | bytes 786440 | tf_op jit(solution)/shard_map/ppermute | solution.py:368
  71.4 0.0 collective-permute-done.21
  71.4 4.1 %collective-permute-start.22 = (f32[128,128]{1,0:T(8,128)S(1)}, f32[128,128]{1,0:T(8,128)S(1)}, u32[]{:S(2)}, u32[]{:S(2)}) collective-permute-start(f32[128,128]{1,0:T(8,128)S(1)} %add.29), channel_id=1, source_target_pairs={{0,32},{1,13},{2,34},{3,15},{4,36},{5,9},{6,38},{7,11},{8,40},{9,5... | collective-permute-start | bytes 196616 | tf_op jit(solution)/shard_map/ppermute | solution.py:374
  75.5 2.0 %collective-permute-done.22 = f32[128,128]{1,0:T(8,128)S(1)} collective-permute-done((f32[128,128]{1,0:T(8,128)S(1)}, f32[128,128]{1,0:T(8,128)S(1)}, u32[]{:S(2)}, u32[]{:S(2)}) %collective-permute-start.22) | collective-permute-done | bytes 65568 | tf_op jit(solution)/shard_map/ppermute | solution.py:374
  77.5 0.1 collective-permute-start.23
  77.7 3.1 %collective-permute-done.23 = f32[128,128]{1,0:T(8,128)S(1)} collective-permute-done((f32[128,128]{1,0:T(8,128)S(1)}, f32[128,128]{1,0:T(8,128)S(1)}, u32[]{:S(2)}, u32[]{:S(2)}) %collective-permute-start.23) | collective-permute-done | bytes 65568 | tf_op jit(solution)/shard_map/ppermute | solution.py:374
  80.8 4.3 %collective-permute-start.24 = (f32[128,128]{1,0:T(8,128)S(1)}, f32[128,128]{1,0:T(8,128)S(1)}, u32[]{:S(2)}, u32[]{:S(2)}) collective-permute-start(f32[128,128]{1,0:T(8,128)S(1)} %add.31.mine_ref), channel_id=1, source_target_pairs={{0,1},{1,0},{2,3},{3,2},{4,5},{5,4},{6,7},{7,6},{8,9},{9,8},{10,11... | collective-permute-start | bytes 196616 | tf_op jit(solution)/shard_map/ppermute | solution.py:374
  85.1 0.0 collective-permute-done.19.cola_ref
  85.1 1.8 %shard_map.94 = f32[2,2,256,256]{3,2,1,0:T(8,128)} custom-call(s32[1,4]{1,0:T(1,128)S(1)} %add_bitcast_fusion.spot_ref, f32[2,2,256,256]{3,2,1,0:T(8,128)S(1)} %get-tuple-element.57.part_ref, f32[2,6,64,128]{3,2,1,0:T(8,128)S(1)} %collective-permute-done.14.rowa_ref, f32[2,6,64,128]{3,2,1,0:T(8,128)S(1)} %collective-permute-done.15.rowb_ref, ...), custom_call_target="tpu_custom_call" | custom-call | tf_op jit(solution)/shard_map/pallas_call | solution.py:378
  86.9 1.2 %shard_map.95 = f32[2,128,128]{2,1,0:T(8,128)} custom-call(s32[1,4]{1,0:T(1,128)S(1)} %add_bitcast_fusion.spot_ref, f32[2,128,128]{2,1,0:T(8,128)S(1)} %copy-done.2, f32[128,128]{1,0:T(8,128)S(1)} %add.31.mine_ref, f32[128,128]{1,0:T(8,128)S(1)} %collective-permute-done.24.other_ref), custom_call_target="tpu_custom_call" | custom-call | tf_op jit(solution)/shard_map/pallas_call | solution.py:378
  (18 shorter events, 0.1 us)
Async XLA Ops:
  0.6 12.8 %copy-start = (f32[2,2,256,256]{3,2,1,0:T(8,128)S(1)}, f32[2,2,256,256]{3,2,1,0:T(8,128)}, u32[]{:S(2)}) copy-start(f32[2,2,256,256]{3,2,1,0:T(8,128)} %obj_ref.9) | copy-start | bytes 3145732
  2.5 23.6 %copy-start.1 = (bf16[4,2,256,256]{3,2,1,0:T(8,128)(2,1)S(1)}, bf16[4,2,256,256]{3,2,1,0:T(8,128)(2,1)}, u32[]{:S(2)}) copy-start(bf16[4,2,256,256]{3,2,1,0:T(8,128)(2,1)} %constant.11.clone.tabs_ref) | copy-start | bytes 3145732
  2.5 14.8 %collective-permute-start.8 = (f32[256,128]{1,0:T(8,128)S(1)}, f32[256,128]{1,0:T(8,128)S(1)}, u32[]{:S(2)}, u32[]{:S(2)}) collective-permute-start(f32[256,128]{1,0:T(8,128)S(1)} %get-tuple-element.47), channel_id=1, source_target_pairs={{0,1},{1,0},{2,3},{3,2},{4,5},{5,4},{6,7},{7,6},{8,9},{9,8},{10,11... | collective-permute-start | bytes 393224 | tf_op jit(solution)/shard_map/ppermute | solution.py:368
  5.8 11.5 %collective-permute-start.9 = (f32[256,128]{1,0:T(8,128)S(1)}, f32[256,128]{1,0:T(8,128)S(1)}, u32[]{:S(2)}, u32[]{:S(2)}) collective-permute-start(f32[256,128]{1,0:T(8,128)S(1)} %get-tuple-element.48), channel_id=1, source_target_pairs={{0,15},{1,2},{2,1},{3,4},{4,3},{5,6},{6,5},{7,8},{8,7},{9,10},{10,... | collective-permute-start | bytes 393224 | tf_op jit(solution)/shard_map/ppermute | solution.py:368
  7.0 11.0 %collective-permute-start.2 = (f32[4,64,128]{2,1,0:T(8,128)S(1)}, f32[4,64,128]{2,1,0:T(8,128)S(1)}, u32[]{:S(2)}, u32[]{:S(2)}) collective-permute-start(f32[4,64,128]{2,1,0:T(8,128)S(1)} %get-tuple-element.39), channel_id=1, source_target_pairs={{0,16},{1,17},{2,18},{3,19},{4,20},{5,21},{6,22},{7,23},{8,24},{9,... | collective-permute-start | bytes 393224 | tf_op jit(solution)/shard_map/ppermute | solution.py:368
  8.6 9.4 %collective-permute-start.3 = (f32[4,64,128]{2,1,0:T(8,128)S(1)}, f32[4,64,128]{2,1,0:T(8,128)S(1)}, u32[]{:S(2)}, u32[]{:S(2)}) collective-permute-start(f32[4,64,128]{2,1,0:T(8,128)S(1)} %get-tuple-element.40), channel_id=1, source_target_pairs={{0,240},{1,241},{2,242},{3,243},{4,244},{5,245},{6,246},{7,247},{8... | collective-permute-start | bytes 393224 | tf_op jit(solution)/shard_map/ppermute | solution.py:368
  14.1 5.9 %collective-permute-start = (f32[256,128]{1,0:T(8,128)S(1)}, f32[256,128]{1,0:T(8,128)S(1)}, u32[]{:S(2)}, u32[]{:S(2)}) collective-permute-start(f32[256,128]{1,0:T(8,128)S(1)} %get-tuple-element.37), channel_id=1, source_target_pairs={{0,1},{1,0},{2,3},{3,2},{4,5},{5,4},{6,7},{7,6},{8,9},{9,8},{10,11... | collective-permute-start | bytes 393224 | tf_op jit(solution)/shard_map/ppermute | solution.py:368
  17.3 5.9 %collective-permute-start.1 = (f32[256,128]{1,0:T(8,128)S(1)}, f32[256,128]{1,0:T(8,128)S(1)}, u32[]{:S(2)}, u32[]{:S(2)}) collective-permute-start(f32[256,128]{1,0:T(8,128)S(1)} %get-tuple-element.38), channel_id=1, source_target_pairs={{0,15},{1,2},{2,1},{3,4},{4,3},{5,6},{6,5},{7,8},{8,7},{9,10},{10,... | collective-permute-start | bytes 393224 | tf_op jit(solution)/shard_map/ppermute | solution.py:368
  17.9 6.0 %collective-permute-start.10 = (f32[2,64,128]{2,1,0:T(8,128)S(1)}, f32[2,64,128]{2,1,0:T(8,128)S(1)}, u32[]{:S(2)}, u32[]{:S(2)}) collective-permute-start(f32[2,64,128]{2,1,0:T(8,128)S(1)} %get-tuple-element.51), channel_id=1, source_target_pairs={{0,16},{1,17},{2,18},{3,19},{4,20},{5,21},{6,22},{7,23},{8,24},{9,... | collective-permute-start | bytes 196616 | tf_op jit(solution)/shard_map/ppermute | solution.py:368
  18.0 12.2 %collective-permute-start.4 = (f32[4,64,128]{2,1,0:T(8,128)S(1)}, f32[4,64,128]{2,1,0:T(8,128)S(1)}, u32[]{:S(2)}, u32[]{:S(2)}) collective-permute-start(f32[4,64,128]{2,1,0:T(8,128)S(1)} %get-tuple-element.43), channel_id=1, source_target_pairs={{0,16},{1,17},{2,18},{3,19},{4,20},{5,21},{6,22},{7,23},{8,24},{9,... | collective-permute-start | bytes 393224 | tf_op jit(solution)/shard_map/ppermute | solution.py:368
  19.5 10.8 %collective-permute-start.5 = (f32[4,64,128]{2,1,0:T(8,128)S(1)}, f32[4,64,128]{2,1,0:T(8,128)S(1)}, u32[]{:S(2)}, u32[]{:S(2)}) collective-permute-start(f32[4,64,128]{2,1,0:T(8,128)S(1)} %get-tuple-element.44), channel_id=1, source_target_pairs={{0,240},{1,241},{2,242},{3,243},{4,244},{5,245},{6,246},{7,247},{8... | collective-permute-start | bytes 393224 | tf_op jit(solution)/shard_map/ppermute | solution.py:368
  20.0 6.1 %copy-start.2 = (f32[2,128,128]{2,1,0:T(8,128)S(1)}, f32[2,128,128]{2,1,0:T(8,128)}, u32[]{:S(2)}) copy-start(f32[2,128,128]{2,1,0:T(8,128)} %probe_ref.5) | copy-start | bytes 393220
  20.0 6.1 %collective-permute-start.11 = (f32[2,64,128]{2,1,0:T(8,128)S(1)}, f32[2,64,128]{2,1,0:T(8,128)S(1)}, u32[]{:S(2)}, u32[]{:S(2)}) collective-permute-start(f32[2,64,128]{2,1,0:T(8,128)S(1)} %get-tuple-element.52), channel_id=1, source_target_pairs={{0,240},{1,241},{2,242},{3,243},{4,244},{5,245},{6,246},{7,247},{8... | collective-permute-start | bytes 196616 | tf_op jit(solution)/shard_map/ppermute | solution.py:368
  23.8 4.6 %collective-permute-start.6 = (f32[2,64,128]{2,1,0:T(8,128)S(1)}, f32[2,64,128]{2,1,0:T(8,128)S(1)}, u32[]{:S(2)}, u32[]{:S(2)}) collective-permute-start(f32[2,64,128]{2,1,0:T(8,128)S(1)} %get-tuple-element.45), channel_id=1, source_target_pairs={{0,16},{1,17},{2,18},{3,19},{4,20},{5,21},{6,22},{7,23},{8,24},{9,... | collective-permute-start | bytes 196616 | tf_op jit(solution)/shard_map/ppermute | solution.py:368
  23.9 2.2 %copy-start.4 = (s32[1,8]{1,0:T(1,128)S(1)}, s32[1,8]{1,0:T(1,128)}, u32[]{:S(2)}) copy-start(s32[1,8]{1,0:T(1,128)} %row_ref.5) | copy-start | bytes 100
  23.9 2.2 %copy-start.5 = (s32[1,8]{1,0:T(1,128)S(1)}, s32[1,8]{1,0:T(1,128)}, u32[]{:S(2)}) copy-start(s32[1,8]{1,0:T(1,128)} %col_ref.5) | copy-start | bytes 100
  23.9 6.3 %collective-permute-start.7 = (f32[2,64,128]{2,1,0:T(8,128)S(1)}, f32[2,64,128]{2,1,0:T(8,128)S(1)}, u32[]{:S(2)}, u32[]{:S(2)}) collective-permute-start(f32[2,64,128]{2,1,0:T(8,128)S(1)} %get-tuple-element.46), channel_id=1, source_target_pairs={{0,240},{1,241},{2,242},{3,243},{4,244},{5,245},{6,246},{7,247},{8... | collective-permute-start | bytes 196616 | tf_op jit(solution)/shard_map/ppermute | solution.py:368
  26.0 4.2 %copy-start.3 = (f32[1,8,128,128]{3,2,1,0:T(8,128)S(1)}, f32[1,8,128,128]{3,2,1,0:T(8,128)}, u32[]{:S(2)}) copy-start(f32[1,8,128,128]{3,2,1,0:T(8,128)} %param.9) | copy-start | bytes 1572868
  36.1 4.2 %collective-permute-start.12 = (f32[128,128]{1,0:T(8,128)S(1)}, f32[128,128]{1,0:T(8,128)S(1)}, u32[]{:S(2)}, u32[]{:S(2)}) collective-permute-start(f32[128,128]{1,0:T(8,128)S(1)} %get-tuple-element.59), channel_id=1, source_target_pairs={{0,1},{1,0},{2,3},{3,2},{4,5},{5,4},{6,7},{7,6},{8,9},{9,8},{10,11... | collective-permute-start | bytes 196616 | tf_op jit(solution)/shard_map/ppermute | solution.py:374
  40.4 4.1 %collective-permute-start.13 = (f32[128,128]{1,0:T(8,128)S(1)}, f32[128,128]{1,0:T(8,128)S(1)}, u32[]{:S(2)}, u32[]{:S(2)}) collective-permute-start(f32[128,128]{1,0:T(8,128)S(1)} %add.24), channel_id=1, source_target_pairs={{0,4},{1,33},{2,6},{3,35},{4,0},{5,37},{6,2},{7,39},{8,12},{9,41},... | collective-permute-start | bytes 196616 | tf_op jit(solution)/shard_map/ppermute | solution.py:374
  44.5 15.0 %collective-permute-start.14 = (f32[2,6,64,128]{3,2,1,0:T(8,128)S(1)}, f32[2,6,64,128]{3,2,1,0:T(8,128)S(1)}, u32[]{:S(2)}, u32[]{:S(2)}) collective-permute-start(f32[2,6,64,128]{3,2,1,0:T(8,128)S(1)} %get-tuple-element.62), channel_id=1, source_target_pairs={{0,16},{1,17},{2,18},{3,19},{4,20},{5,21},{6,22},{7,23},{8,24},{9,... | collective-permute-start | bytes 1179656 | tf_op jit(solution)/shard_map/ppermute | solution.py:368
  44.6 14.9 %collective-permute-start.15 = (f32[2,6,64,128]{3,2,1,0:T(8,128)S(1)}, f32[2,6,64,128]{3,2,1,0:T(8,128)S(1)}, u32[]{:S(2)}, u32[]{:S(2)}) collective-permute-start(f32[2,6,64,128]{3,2,1,0:T(8,128)S(1)} %get-tuple-element.63), channel_id=1, source_target_pairs={{0,240},{1,241},{2,242},{3,243},{4,244},{5,245},{6,246},{7,247},{8... | collective-permute-start | bytes 1179656 | tf_op jit(solution)/shard_map/ppermute | solution.py:368
  46.1 3.4 %collective-permute-start.16 = (f32[128,128]{1,0:T(8,128)S(1)}, f32[128,128]{1,0:T(8,128)S(1)}, u32[]{:S(2)}, u32[]{:S(2)}) collective-permute-start(f32[128,128]{1,0:T(8,128)S(1)} %add.25), channel_id=1, source_target_pairs={{0,12},{1,129},{2,14},{3,131},{4,8},{5,133},{6,10},{7,135},{8,4},{... | collective-permute-start | bytes 196616 | tf_op jit(solution)/shard_map/ppermute | solution.py:374
  49.5 4.7 %collective-permute-start.17 = (f32[128,128]{1,0:T(8,128)S(1)}, f32[128,128]{1,0:T(8,128)S(1)}, u32[]{:S(2)}, u32[]{:S(2)}) collective-permute-start(f32[128,128]{1,0:T(8,128)S(1)} %add.26), channel_id=1, source_target_pairs={{0,128},{1,131},{2,130},{3,129},{4,132},{5,135},{6,134},{7,133},{8... | collective-permute-start | bytes 196616 | tf_op jit(solution)/shard_map/ppermute | solution.py:374
  54.2 5.3 %collective-permute-start.18 = (f32[128,128]{1,0:T(8,128)S(1)}, f32[128,128]{1,0:T(8,128)S(1)}, u32[]{:S(2)}, u32[]{:S(2)}) collective-permute-start(f32[128,128]{1,0:T(8,128)S(1)} %add.27), channel_id=1, source_target_pairs={{0,130},{1,97},{2,128},{3,99},{4,134},{5,101},{6,132},{7,103},{8,1... | collective-permute-start | bytes 196616 | tf_op jit(solution)/shard_map/ppermute | solution.py:374
  60.2 11.3 %collective-permute-start.21 = (f32[128,128]{1,0:T(8,128)S(1)}, f32[128,128]{1,0:T(8,128)S(1)}, u32[]{:S(2)}, u32[]{:S(2)}) collective-permute-start(f32[128,128]{1,0:T(8,128)S(1)} %add.28), channel_id=1, source_target_pairs={{0,16},{1,5},{2,18},{3,7},{4,20},{5,1},{6,22},{7,3},{8,24},{9,13},... | collective-permute-start | bytes 196616 | tf_op jit(solution)/shard_map/ppermute | solution.py:374
  69.6 15.5 %collective-permute-start.19 = (f32[2,256,128]{2,1,0:T(8,128)S(1)}, f32[2,256,128]{2,1,0:T(8,128)S(1)}, u32[]{:S(2)}, u32[]{:S(2)}) collective-permute-start(f32[2,256,128]{2,1,0:T(8,128)S(1)} %get-tuple-element.69), channel_id=1, source_target_pairs={{0,1},{1,0},{2,3},{3,2},{4,5},{5,4},{6,7},{7,6},{8,9},{9,8},{10,11... | collective-permute-start | bytes 786440 | tf_op jit(solution)/shard_map/ppermute | solution.py:368
  69.6 15.5 %collective-permute-start.20 = (f32[2,256,128]{2,1,0:T(8,128)S(1)}, f32[2,256,128]{2,1,0:T(8,128)S(1)}, u32[]{:S(2)}, u32[]{:S(2)}) collective-permute-start(f32[2,256,128]{2,1,0:T(8,128)S(1)} %get-tuple-element.70), channel_id=1, source_target_pairs={{0,15},{1,2},{2,1},{3,4},{4,3},{5,6},{6,5},{7,8},{8,7},{9,10},{10,... | collective-permute-start | bytes 786440 | tf_op jit(solution)/shard_map/ppermute | solution.py:368
  71.4 6.1 %collective-permute-start.22 = (f32[128,128]{1,0:T(8,128)S(1)}, f32[128,128]{1,0:T(8,128)S(1)}, u32[]{:S(2)}, u32[]{:S(2)}) collective-permute-start(f32[128,128]{1,0:T(8,128)S(1)} %add.29), channel_id=1, source_target_pairs={{0,32},{1,13},{2,34},{3,15},{4,36},{5,9},{6,38},{7,11},{8,40},{9,5... | collective-permute-start | bytes 196616 | tf_op jit(solution)/shard_map/ppermute | solution.py:374
  77.5 3.2 %collective-permute-start.23 = (f32[128,128]{1,0:T(8,128)S(1)}, f32[128,128]{1,0:T(8,128)S(1)}, u32[]{:S(2)}, u32[]{:S(2)}) collective-permute-start(f32[128,128]{1,0:T(8,128)S(1)} %add.30), channel_id=1, source_target_pairs={{0,96},{1,17},{2,98},{3,19},{4,100},{5,21},{6,102},{7,23},{8,104},... | collective-permute-start | bytes 196616 | tf_op jit(solution)/shard_map/ppermute | solution.py:374
  80.8 6.1 %collective-permute-start.24 = (f32[128,128]{1,0:T(8,128)S(1)}, f32[128,128]{1,0:T(8,128)S(1)}, u32[]{:S(2)}, u32[]{:S(2)}) collective-permute-start(f32[128,128]{1,0:T(8,128)S(1)} %add.31.mine_ref), channel_id=1, source_target_pairs={{0,1},{1,0},{2,3},{3,2},{4,5},{5,4},{6,7},{7,6},{8,9},{9,8},{10,11... | collective-permute-start | bytes 196616 | tf_op jit(solution)/shard_map/ppermute | solution.py:374

commit v7 on v6

--- a/solution.py
+++ b/solution.py
@@ -16,7 +16,7 @@
 LANES = 128
 BOTH = ("row", "col")
 GRANT = 16 * 1024 * 1024
-MASKS = ((4, 32), (12, 128), (128, 130), (130, 96), (16, 4), (32, 12), (96, 16))
+MASKS = ((128, 32), (4, 12), (12, 4), (130, 128), (16, 130), (32, 96), (96, 16))
 
 
 def split_table(table):
@@ -86,43 +86,40 @@
     return before, after
 
 
-def pack_piece(spot_ref, piece_ref, cola_ref, colb_ref, rowa_ref, rowb_ref):
-    half = LANES // 2
-    tile = piece_ref.shape[1]
+def pack_kernel(spot_ref, obj_ref, cola_ref, colb_ref, rowa_ref, rowb_ref, held, sems):
+    half = LANES // 2
+    tile = held.shape[2]
     first = lax.broadcasted_iota(jnp.int32, (tile, LANES), 1) < half
-    left, right = columns(piece_ref, first)
-    cola_ref[...] = pick(spot_ref, 1, right, left)
-    colb_ref[...] = pick(spot_ref, 1, left, right)
-    for part in range(2):
-        for block in range(2):
-            cols = slice(block * LANES, (block + 1) * LANES)
-            top, bottom = piece_ref[part, :half, cols], piece_ref[part, tile - half :, cols]
-            rowa_ref[2 * part + block] = pick(spot_ref, 0, bottom, top)
-            rowb_ref[2 * part + block] = pick(spot_ref, 0, top, bottom)
-
-
-def pack_kernel(spot_ref, obj_ref, cola_ref, colb_ref, rowa_ref, rowb_ref, held, sem):
-    copy = pltpu.make_async_copy(obj_ref.at[0], held, sem)
-    copy.start()
-    copy.wait()
-    pack_piece(spot_ref, held, cola_ref, colb_ref, rowa_ref, rowb_ref)
-
-
-def pack_next_kernel(spot_ref, obj_ref, cola_ref, colb_ref, rowa_ref, rowb_ref):
-    pack_piece(spot_ref, obj_ref.at[1], cola_ref, colb_ref, rowa_ref, rowb_ref)
+    copies = [pltpu.make_async_copy(obj_ref.at[p], held.at[p], sems.at[p]) for p in range(2)]
+    for copy in copies:
+        copy.start()
+    for piece in range(2):
+        copies[piece].wait()
+        left, right = columns(held.at[piece], first)
+        cola_ref[piece] = pick(spot_ref, 1, right, left)
+        colb_ref[piece] = pick(spot_ref, 1, left, right)
+        for part in range(2):
+            for block in range(2):
+                cols = slice(block * LANES, (block + 1) * LANES)
+                top = held[piece, part, :half, cols]
+                bottom = held[piece, part, tile - half :, cols]
+                rowa_ref[piece, 2 * part + block] = pick(spot_ref, 0, bottom, top)
+                rowb_ref[piece, 2 * part + block] = pick(spot_ref, 0, top, bottom)
 
 
 def corner_kernel(spot_ref, cola_ref, colb_ref, rowa_ref, rowb_ref):
     half = LANES // 2
-    low, high = slice(0, half), slice(cola_ref.shape[0] - half, cola_ref.shape[0])
-    tops = beside(spot_ref, 1, cola_ref[low], colb_ref[low])
-    bottoms = beside(spot_ref, 1, cola_ref[high], colb_ref[high])
-    for place, (top, bottom) in enumerate(zip(tops, bottoms)):
-        rowa_ref[place] = pick(spot_ref, 0, bottom, top)
-        rowb_ref[place] = pick(spot_ref, 0, top, bottom)
-
-
-def grow(ext, spot_ref, piece_ref, cola_ref, colb_ref, rowa_ref, rowb_ref, cora_ref, corb_ref):
+    low, high = slice(0, half), slice(cola_ref.shape[1] - half, cola_ref.shape[1])
+    for piece in range(2):
+        tops = beside(spot_ref, 1, cola_ref[piece, low], colb_ref[piece, low])
+        bottoms = beside(spot_ref, 1, cola_ref[piece, high], colb_ref[piece, high])
+        for place, (top, bottom) in enumerate(zip(tops, bottoms)):
+            rowa_ref[piece, place] = pick(spot_ref, 0, bottom, top)
+            rowb_ref[piece, place] = pick(spot_ref, 0, top, bottom)
+
+
+def grow(ext, spot_ref, *refs):
+    piece_ref, cola_ref, colb_ref, rowa_ref, rowb_ref, cora_ref, corb_ref = refs
     half = LANES // 2
     tile = piece_ref.shape[1]
     sides = beside(spot_ref, 1, cola_ref[...], colb_ref[...])
@@ -180,7 +177,8 @@
     probe_ref, tabs_ref, win_ref, mid_ref, ext, *, group,
 ):
     width = probe_ref.shape[1]
-    grow(ext, spot_ref, obj_ref.at[0], cola_ref, colb_ref, rowa_ref, rowb_ref, cora_ref, corb_ref)
+    refs = (obj_ref, cola_ref, colb_ref, rowa_ref, rowb_ref, cora_ref, corb_ref)
+    grow(ext, spot_ref, *[ref.at[0] for ref in refs])
 
     def some(index, _):
         slots = [group * index + place for place in range(group)]
@@ -202,7 +200,8 @@
     ext, sum_ref, *, group,
 ):
     width = win_ref.shape[2]
-    grow(ext, spot_ref, obj_ref.at[1], cola_ref, colb_ref, rowa_ref, rowb_ref, cora_ref, corb_ref)
+    refs = (obj_ref, cola_ref, colb_ref, rowa_ref, rowb_ref, cora_ref, corb_ref)
+    grow(ext, spot_ref, *[ref.at[1] for ref in refs])
     sum_ref[...] = jnp.zeros_like(sum_ref)
 
     def some(index, _):
@@ -393,31 +392,23 @@
     spot = jnp.stack([jnp.asarray(entry, jnp.int32) for entry in place]).reshape(1, 4)
     tabs = jnp.asarray(make_tables(width))
     grown = pltpu.VMEM((2, 4, tile + width, LANES), jnp.float32)
-    outer, ends = [array(*side)] * 2 + [array(4, half, LANES)] * 2, [array(2, half, LANES)] * 2
-    packed = [
-        pl.pallas_call(
-            pack_kernel, out_shape=tuple(outer),
-            in_specs=smem(1) + [pl.BlockSpec(memory_space=pltpu.HBM)], out_specs=tuple(vmem(4)),
-            scratch_shapes=[pltpu.VMEM((2, tile, tile), jnp.float32), pltpu.SemaphoreType.DMA],
-            compiler_params=pltpu.CompilerParams(vmem_limit_bytes=GRANT),
-        )(spot, pltpu.with_memory_space_constraint(object_field, pltpu.HBM)),
-        call(pack_next_kernel, outer, (spot,), (object_field,)),
-    ]
-    cols = [meet(strips[:2], 1) for strips in packed]
-    rows = meet(packed[0][2:], 0)
-    ends0 = call(corner_kernel, ends, (spot,), cols[0])
-    rows[0], rows[1], *strips = lax.optimization_barrier((*rows, *packed[1][2:]))
-    halos = [(*cols[0], *rows, *meet(ends0, 0))]
-    rows = meet(strips, 0)
-    halos.append((*cols[1], *rows, *meet(call(corner_kernel, ends, (spot,), cols[1]), 0)))
+    packed = pl.pallas_call(
+        pack_kernel, out_shape=tuple([array(2, *side)] * 2 + [array(2, 4, half, LANES)] * 2),
+        in_specs=smem(1) + [pl.BlockSpec(memory_space=pltpu.HBM)], out_specs=tuple(vmem(4)),
+        scratch_shapes=[pltpu.VMEM((2, 2, tile, tile), jnp.float32), pltpu.SemaphoreType.DMA((2,))],
+        compiler_params=pltpu.CompilerParams(vmem_limit_bytes=GRANT),
+    )(spot, pltpu.with_memory_space_constraint(object_field, pltpu.HBM))
+    cols, rows = meet(packed[:2], 1), meet(packed[2:], 0)
+    corners = meet(call(corner_kernel, [array(2, 2, half, LANES)] * 2, (spot,), cols), 0)
+    halo = (*cols, *rows, *corners)
     win, mid = call(
         functools.partial(first_kernel, group=2), [fields] * 2, (offset_row, offset_col, spot),
-        (object_field, *halos[0], probe, tabs), (grown,),
+        (object_field, *halo, probe, tabs), (grown,),
     )
     grad, down, mine, send = call(
         functools.partial(second_kernel, group=count), [fields] * 2 + [array(*plane)] * 2,
         (offset_row, offset_col, spot, live),
-        (object_field, *halos[1], win, mid, intensity[0], tabs),
+        (object_field, *halo, win, mid, intensity[0], tabs),
         (grown, pltpu.VMEM((2, *plane), jnp.float32)),
     )
     part, *strips, left, right = call(
@@ -427,15 +418,20 @@
     )
     mine = mine + swap(send, (1, 1))
     mine = mine + swap(mine, MASKS[0])
-    mine, *strips = lax.optimization_barrier((mine, *strips))
+    mine, strips[0] = lax.optimization_barrier((mine, strips[0]))
+    mine = mine + swap(mine, MASKS[1])
+    mine, strips[1] = lax.optimization_barrier((mine, strips[1]))
     rows = meet(strips, 0)
-    for mask in MASKS[1:4]:
+    for mask in MASKS[2:4]:
         mine = mine + swap(mine, mask)
+    mine, *rows = lax.optimization_barrier((mine, *rows))
     strips = call(fold_kernel, [array(2, *side)] * 2, (spot,), (left, right, *rows))
+    mine = mine + swap(mine, MASKS[4])
     mine, *strips = lax.optimization_barrier((mine, *strips))
     cols = meet(strips, 1)
-    for mask in MASKS[4:]:
+    for mask in MASKS[5:]:
         mine = mine + swap(mine, mask)
+    mine, *cols = lax.optimization_barrier((mine, *cols))
     (new,) = call(finish_kernel, (field,), (spot,), (part, *rows, *cols))
     other = swap(mine, (1, 1))
     count_all = count * lax.axis_size("row") * lax.axis_size("col")

time: 88.2 us -> 90.4 us (1.025)
  waiting for transfers between devices: 19.8 us -> 33 us
  starting transfers between devices: 49 us -> 37.9 us
  local copies, waits for them, and re-layouts: 0.04 us -> 1.25 us
  Pallas kernels: 17.6 us -> 16.5 us
    ppermute x9, starting transfers between devices: 24.9 us -> 13.7 us  [swap(): lax.ppermute(value, BOTH, [(i, i ^ masks[i % 2]) for i in range(count)])]
    ppermute x16 -> x10, waiting for transfers between devices: 2.14 us -> 9.84 us  [meet(): got.append(lax.ppermute(strip, BOTH, pairs))]
    ppermute x9, waiting for transfers between devices: 17.6 us -> 23.1 us  [swap(): lax.ppermute(value, BOTH, [(i, i ^ masks[i % 2]) for i in range(count)])]
    pallas_call x9 -> x7, Pallas kernels: 15.8 us -> 14.6 us  [call(): pl.pallas_call(kernel, out_shape=tuple(out_shape), in_specs=smem(len(scal...]
    unnamed x12, local copies, waits for them, and re-layouts: 0.04 us -> 1.25 us
    ppermute x16 -> x10, starting transfers between devices: 24.2 us -> 24.2 us  [meet(): got.append(lax.ppermute(strip, BOTH, pairs))]
  transfers between devices with their start and end apart: 25 -> 19, of which waited for: 10 -> 10; matrix products, arithmetic and copies ran while one was open for 0% -> 0% of each run, Pallas kernels for 9% -> 6%
where the time goes in v7:
time: 90.4 us; the launch traced here: 90.2 us
  starting transfers between devices  37.9 us (42%)
  waiting for transfers between devices  33 us (37%)
  Pallas kernels  16.5 us (18%)
  between operations  1.52 us (2%)
  local copies, waits for them, and re-layouts  1.25 us (1%)
    ppermute x10, starting transfers between devices, meet(): got.append(lax.ppermute(strip, BOTH, pairs))  24.2 us
    ppermute x9, waiting for transfers between devices, swap(): lax.ppermute(value, BOTH, [(i, i ^ masks[i % 2]) for i in range(count)])  23.1 us
    pallas_call x7, Pallas kernels, call(): pl.pallas_call(kernel, out_shape=tuple(out_shape), in_specs=smem(len(scal...  14.6 us
    ppermute x9, starting transfers between devices, swap(): lax.ppermute(value, BOTH, [(i, i ^ masks[i % 2]) for i in range(count)])  13.7 us
    ppermute x10, waiting for transfers between devices, meet(): got.append(lax.ppermute(strip, BOTH, pairs))  9.84 us
    pallas_call x1, Pallas kernels, on_device(): pl.pallas_call(pack_kernel, out_shape=tuple([array(2, *side)] * 2 + [arra...  1.91 us
  transfers between devices with their start and end apart: 19, of which 10 were waited for; matrix products, arithmetic and copies ran while one was open for 0% of the time, Pallas kernels for 6%

profile of v7, /device:TPU:1, one launch (start us, length us, event | category | flops | bytes accessed | tf_op | source)
XLA Modules:
  0.0 90.2 jit_solution(3031027479568689436)
XLA Ops:
  0.6 0.0 copy-start
  0.7 0.1 add_bitcast_fusion.spot_ref
  0.7 1.9 %shard_map.86 = (f32[2,256,128]{2,1,0:T(8,128)S(1)}, f32[2,256,128]{2,1,0:T(8,128)S(1)}, f32[2,4,64,128]{3,2,1,0:T(8,128)S(1)}, f32[2,4,64,128]{3,2,1,0:T(8,128)S(1)}) custom-call(s32[1,4]{1,0:T(1,128)S(1)} %add_bitcast_fusion.spot_ref, f32[2,2,256,256]{3,2,1,0:T(8,128)} %obj_ref.7), custom_call_target="tpu_custom_call" | custom-call | tf_op jit(solution)/shard_map/pallas_call | solution.py:395
  2.6 3.3 %collective-permute-start = (f32[2,256,128]{2,1,0:T(8,128)S(1)}, f32[2,256,128]{2,1,0:T(8,128)S(1)}, u32[]{:S(2)}, u32[]{:S(2)}) collective-permute-start(f32[2,256,128]{2,1,0:T(8,128)S(1)} %get-tuple-element.34), channel_id=1, source_target_pairs={{0,1},{1,0},{2,3},{3,2},{4,5},{5,4},{6,7},{7,6},{8,9},{9,8},{10,11... | collective-permute-start | bytes 786440 | tf_op jit(solution)/shard_map/ppermute | solution.py:367
  6.0 1.2 %collective-permute-start.1 = (f32[2,256,128]{2,1,0:T(8,128)S(1)}, f32[2,256,128]{2,1,0:T(8,128)S(1)}, u32[]{:S(2)}, u32[]{:S(2)}) collective-permute-start(f32[2,256,128]{2,1,0:T(8,128)S(1)} %get-tuple-element.35), channel_id=1, source_target_pairs={{0,15},{1,2},{2,1},{3,4},{4,3},{5,6},{6,5},{7,8},{8,7},{9,10},{10,... | collective-permute-start | bytes 786440 | tf_op jit(solution)/shard_map/ppermute | solution.py:367
  7.1 1.6 %collective-permute-start.2 = (f32[2,4,64,128]{3,2,1,0:T(8,128)S(1)}, f32[2,4,64,128]{3,2,1,0:T(8,128)S(1)}, u32[]{:S(2)}, u32[]{:S(2)}) collective-permute-start(f32[2,4,64,128]{3,2,1,0:T(8,128)S(1)} %get-tuple-element.36), channel_id=1, source_target_pairs={{0,16},{1,17},{2,18},{3,19},{4,20},{5,21},{6,22},{7,23},{8,24},{9,... | collective-permute-start | bytes 786440 | tf_op jit(solution)/shard_map/ppermute | solution.py:367
  8.8 0.0 copy-start.2
  8.8 4.8 %collective-permute-start.3 = (f32[2,4,64,128]{3,2,1,0:T(8,128)S(1)}, f32[2,4,64,128]{3,2,1,0:T(8,128)S(1)}, u32[]{:S(2)}, u32[]{:S(2)}) collective-permute-start(f32[2,4,64,128]{3,2,1,0:T(8,128)S(1)} %get-tuple-element.37), channel_id=1, source_target_pairs={{0,240},{1,241},{2,242},{3,243},{4,244},{5,245},{6,246},{7,247},{8... | collective-permute-start | bytes 786440 | tf_op jit(solution)/shard_map/ppermute | solution.py:367
  13.6 0.0 collective-permute-done.cola_ref
  13.6 8.1 %collective-permute-done.1.colb_ref = f32[2,256,128]{2,1,0:T(8,128)S(1)} collective-permute-done((f32[2,256,128]{2,1,0:T(8,128)S(1)}, f32[2,256,128]{2,1,0:T(8,128)S(1)}, u32[]{:S(2)}, u32[]{:S(2)}) %collective-permute-start.1) | collective-permute-done | bytes 262176 | tf_op jit(solution)/shard_map/ppermute | solution.py:367
  21.7 0.6 shard_map.87
  22.3 0.1 collective-permute-start.4
  22.4 0.0 copy-start.4
  22.4 0.0 copy-start.5
  22.4 4.9 %collective-permute-start.5 = (f32[2,2,64,128]{3,2,1,0:T(8,128)S(1)}, f32[2,2,64,128]{3,2,1,0:T(8,128)S(1)}, u32[]{:S(2)}, u32[]{:S(2)}) collective-permute-start(f32[2,2,64,128]{3,2,1,0:T(8,128)S(1)} %get-tuple-element.39), channel_id=1, source_target_pairs={{0,240},{1,241},{2,242},{3,243},{4,244},{5,245},{6,246},{7,247},{8... | collective-permute-start | bytes 393224 | tf_op jit(solution)/shard_map/ppermute | solution.py:367
  28.0 0.0 collective-permute-done.2.rowa_ref
  28.0 0.0 collective-permute-done.3.rowb_ref
  28.0 0.0 collective-permute-done.4.cora_ref
  28.0 1.7 %collective-permute-done.5.corb_ref = f32[2,2,64,128]{3,2,1,0:T(8,128)S(1)} collective-permute-done((f32[2,2,64,128]{3,2,1,0:T(8,128)S(1)}, f32[2,2,64,128]{3,2,1,0:T(8,128)S(1)}, u32[]{:S(2)}, u32[]{:S(2)}) %collective-permute-start.5) | collective-permute-done | bytes 131104 | tf_op jit(solution)/shard_map/ppermute | solution.py:367
  29.7 0.0 copy-done
  29.7 0.0 copy-done.2
  29.7 0.0 copy-done.4
  29.7 0.0 copy-done.5
  29.7 0.0 copy-start.1
  29.7 1.2 %copy-done.1 = bf16[4,2,256,256]{3,2,1,0:T(8,128)(2,1)S(1)} copy-done((bf16[4,2,256,256]{3,2,1,0:T(8,128)(2,1)S(1)}, bf16[4,2,256,256]{3,2,1,0:T(8,128)(2,1)}, u32[]{:S(2)}) %copy-start.1) | copy-done | bytes 1048600
  31.0 0.0 copy-start.3
  31.0 2.2 %shard_map.88 = (f32[8,2,128,128]{3,2,1,0:T(8,128)S(1)}, f32[8,2,128,128]{3,2,1,0:T(8,128)S(1)}) custom-call(s32[1,8]{1,0:T(1,128)S(1)} %copy-done.4, s32[1,8]{1,0:T(1,128)S(1)} %copy-done.5, s32[1,4]{1,0:T(1,128)S(1)} %add_bitcast_fusion.spot_ref, f32[2,2,256,256]{3,2,1,0:T(8,128)S(1)} %copy-done, f32[2,256,128]{2,1,0:T(8,128)S(1)} %collective-permute-done.cola_ref, ...), custom_call_target="tpu_custom_call" | custom-call | tf_op jit(solution)/shard_map/pallas_call | solution.py:377
  33.2 0.0 copy-done.3
  33.2 5.9 %shard_map.89 = (f32[8,2,128,128]{3,2,1,0:T(8,128)S(1)}, f32[8,2,128,128]{3,2,1,0:T(8,128)S(1)}, f32[128,128]{1,0:T(8,128)S(1)}, f32[128,128]{1,0:T(8,128)S(1)}) custom-call(s32[1,8]{1,0:T(1,128)S(1)} %copy-done.4, s32[1,8]{1,0:T(1,128)S(1)} %copy-done.5, s32[1,4]{1,0:T(1,128)S(1)} %add_bitcast_fusion.spot_ref, s32[1,1]{1,0:T(1,128)S(6)} %copy.9.live_ref, ...), custom_call_target="tpu_custom_call" | custom-call | tf_op jit(solution)/shard_map/pallas_call | solution.py:377
  39.1 0.1 collective-permute-start.6
  39.2 1.2 %collective-permute-done.6 = f32[128,128]{1,0:T(8,128)S(1)} collective-permute-done((f32[128,128]{1,0:T(8,128)S(1)}, f32[128,128]{1,0:T(8,128)S(1)}, u32[]{:S(2)}, u32[]{:S(2)}) %collective-permute-start.6) | collective-permute-done | bytes 65568 | tf_op jit(solution)/shard_map/ppermute | solution.py:373
  40.5 0.1 collective-permute-start.7
  40.6 2.3 %shard_map.90 = (f32[2,2,256,256]{3,2,1,0:T(8,128)S(1)}, f32[2,6,64,128]{3,2,1,0:T(8,128)S(1)}, f32[2,6,64,128]{3,2,1,0:T(8,128)S(1)}, f32[2,256,128]{2,1,0:T(8,128)S(1)}, f32[2,256,128]{2,1,0:T(8,128)S(1)}) custom-call(s32[1,8]{1,0:T(1,128)S(1)} %copy-done.4, s32[1,8]{1,0:T(1,128)S(1)} %copy-done.5, s32[1,4]{1,0:T(1,128)S(1)} %add_bitcast_fusion.spot_ref, ...), custom_call_target="tpu_custom_call" | custom-call | tf_op jit(solution)/shard_map/pallas_call | solution.py:377
  42.9 1.7 %collective-permute-done.7 = f32[128,128]{1,0:T(8,128)S(1)} collective-permute-done((f32[128,128]{1,0:T(8,128)S(1)}, f32[128,128]{1,0:T(8,128)S(1)}, u32[]{:S(2)}, u32[]{:S(2)}) %collective-permute-start.7) | collective-permute-done | bytes 65568 | tf_op jit(solution)/shard_map/ppermute | solution.py:373
  44.6 2.6 %collective-permute-start.8 = (f32[128,128]{1,0:T(8,128)S(1)}, f32[128,128]{1,0:T(8,128)S(1)}, u32[]{:S(2)}, u32[]{:S(2)}) collective-permute-start(f32[128,128]{1,0:T(8,128)S(1)} %add.25), channel_id=1, source_target_pairs={{0,4},{1,13},{2,6},{3,15},{4,0},{5,9},{6,2},{7,11},{8,12},{9,5},{1... | collective-permute-start | bytes 196616 | tf_op jit(solution)/shard_map/ppermute | solution.py:373
  47.2 0.0 collective-permute-start.11
  47.2 1.8 %collective-permute-done.8 = f32[128,128]{1,0:T(8,128)S(1)} collective-permute-done((f32[128,128]{1,0:T(8,128)S(1)}, f32[128,128]{1,0:T(8,128)S(1)}, u32[]{:S(2)}, u32[]{:S(2)}) %collective-permute-start.8) | collective-permute-done | bytes 65568 | tf_op jit(solution)/shard_map/ppermute | solution.py:373
  49.0 3.7 %collective-permute-start.12 = (f32[2,6,64,128]{3,2,1,0:T(8,128)S(1)}, f32[2,6,64,128]{3,2,1,0:T(8,128)S(1)}, u32[]{:S(2)}, u32[]{:S(2)}) collective-permute-start(f32[2,6,64,128]{3,2,1,0:T(8,128)S(1)} %get-tuple-element.52), channel_id=1, source_target_pairs={{0,240},{1,241},{2,242},{3,243},{4,244},{5,245},{6,246},{7,247},{8... | collective-permute-start | bytes 1179656 | tf_op jit(solution)/shard_map/ppermute | solution.py:367
  52.7 0.3 collective-permute-start.9
  53.0 3.1 %collective-permute-done.9 = f32[128,128]{1,0:T(8,128)S(1)} collective-permute-done((f32[128,128]{1,0:T(8,128)S(1)}, f32[128,128]{1,0:T(8,128)S(1)}, u32[]{:S(2)}, u32[]{:S(2)}) %collective-permute-start.9) | collective-permute-done | bytes 65568 | tf_op jit(solution)/shard_map/ppermute | solution.py:373
  56.1 0.4 collective-permute-start.10
  56.5 6.3 %collective-permute-done.10 = f32[128,128]{1,0:T(8,128)S(1)} collective-permute-done((f32[128,128]{1,0:T(8,128)S(1)}, f32[128,128]{1,0:T(8,128)S(1)}, u32[]{:S(2)}, u32[]{:S(2)}) %collective-permute-start.10) | collective-permute-done | bytes 65568 | tf_op jit(solution)/shard_map/ppermute | solution.py:373
  62.8 0.0 collective-permute-done.11.rowa_ref
  62.8 0.0 collective-permute-done.12.rowb_ref
  62.8 3.2 %collective-permute-start.13 = (f32[128,128]{1,0:T(8,128)S(1)}, f32[128,128]{1,0:T(8,128)S(1)}, u32[]{:S(2)}, u32[]{:S(2)}) collective-permute-start(f32[128,128]{1,0:T(8,128)S(1)} %add.28), channel_id=1, source_target_pairs={{0,16},{1,131},{2,18},{3,129},{4,20},{5,135},{6,22},{7,133},{8,24}... | collective-permute-start | bytes 196616 | tf_op jit(solution)/shard_map/ppermute | solution.py:373
  66.0 0.6 shard_map.91
  66.6 1.0 %collective-permute-done.13 = f32[128,128]{1,0:T(8,128)S(1)} collective-permute-done((f32[128,128]{1,0:T(8,128)S(1)}, f32[128,128]{1,0:T(8,128)S(1)}, u32[]{:S(2)}, u32[]{:S(2)}) %collective-permute-start.13) | collective-permute-done | bytes 65568 | tf_op jit(solution)/shard_map/ppermute | solution.py:373
  67.7 2.1 %collective-permute-start.16 = (f32[2,256,128]{2,1,0:T(8,128)S(1)}, f32[2,256,128]{2,1,0:T(8,128)S(1)}, u32[]{:S(2)}, u32[]{:S(2)}) collective-permute-start(f32[2,256,128]{2,1,0:T(8,128)S(1)} %get-tuple-element.61), channel_id=1, source_target_pairs={{0,1},{1,0},{2,3},{3,2},{4,5},{5,4},{6,7},{7,6},{8,9},{9,8},{10,11... | collective-permute-start | bytes 786440 | tf_op jit(solution)/shard_map/ppermute | solution.py:367
  69.8 2.5 %collective-permute-start.17 = (f32[2,256,128]{2,1,0:T(8,128)S(1)}, f32[2,256,128]{2,1,0:T(8,128)S(1)}, u32[]{:S(2)}, u32[]{:S(2)}) collective-permute-start(f32[2,256,128]{2,1,0:T(8,128)S(1)} %get-tuple-element.62), channel_id=1, source_target_pairs={{0,15},{1,2},{2,1},{3,4},{4,3},{5,6},{6,5},{7,8},{8,7},{9,10},{10,... | collective-permute-start | bytes 786440 | tf_op jit(solution)/shard_map/ppermute | solution.py:367
  72.3 0.7 collective-permute-start.14
  73.0 4.8 %collective-permute-done.14 = f32[128,128]{1,0:T(8,128)S(1)} collective-permute-done((f32[128,128]{1,0:T(8,128)S(1)}, f32[128,128]{1,0:T(8,128)S(1)}, u32[]{:S(2)}, u32[]{:S(2)}) %collective-permute-start.14) | collective-permute-done | bytes 65568 | tf_op jit(solution)/shard_map/ppermute | solution.py:373
  77.8 0.1 collective-permute-start.15
  77.9 3.1 %collective-permute-done.15 = f32[128,128]{1,0:T(8,128)S(1)} collective-permute-done((f32[128,128]{1,0:T(8,128)S(1)}, f32[128,128]{1,0:T(8,128)S(1)}, u32[]{:S(2)}, u32[]{:S(2)}) %collective-permute-start.15) | collective-permute-done | bytes 65568 | tf_op jit(solution)/shard_map/ppermute | solution.py:373
  81.0 0.0 collective-permute-done.16.cola_ref
  81.0 0.0 collective-permute-done.17.colb_ref
  81.0 6.2 %collective-permute-start.18 = (f32[128,128]{1,0:T(8,128)S(1)}, f32[128,128]{1,0:T(8,128)S(1)}, u32[]{:S(2)}, u32[]{:S(2)}) collective-permute-start(f32[128,128]{1,0:T(8,128)S(1)} %add.31.mine_ref), channel_id=1, source_target_pairs={{0,1},{1,0},{2,3},{3,2},{4,5},{5,4},{6,7},{7,6},{8,9},{9,8},{10,11... | collective-permute-start | bytes 196616 | tf_op jit(solution)/shard_map/ppermute | solution.py:373
  87.2 1.8 %shard_map.92 = f32[2,2,256,256]{3,2,1,0:T(8,128)} custom-call(s32[1,4]{1,0:T(1,128)S(1)} %add_bitcast_fusion.spot_ref, f32[2,2,256,256]{3,2,1,0:T(8,128)S(1)} %get-tuple-element.44.part_ref, f32[2,6,64,128]{3,2,1,0:T(8,128)S(1)} %collective-permute-done.11.rowa_ref, f32[2,6,64,128]{3,2,1,0:T(8,128)S(1)} %collective-permute-done.12.rowb_ref, ...), custom_call_target="tpu_custom_call" | custom-call | tf_op jit(solution)/shard_map/pallas_call | solution.py:377
  89.0 0.0 collective-permute-done.18.other_ref
  89.0 1.2 %shard_map.93 = f32[2,128,128]{2,1,0:T(8,128)} custom-call(s32[1,4]{1,0:T(1,128)S(1)} %add_bitcast_fusion.spot_ref, f32[2,128,128]{2,1,0:T(8,128)S(1)} %copy-done.2, f32[128,128]{1,0:T(8,128)S(1)} %add.31.mine_ref, f32[128,128]{1,0:T(8,128)S(1)} %collective-permute-done.18.other_ref), custom_call_target="tpu_custom_call" | custom-call | tf_op jit(solution)/shard_map/pallas_call | solution.py:377
  (9 shorter events, 0.1 us)
Async XLA Ops:
  0.6 29.1 %copy-start = (f32[2,2,256,256]{3,2,1,0:T(8,128)S(1)}, f32[2,2,256,256]{3,2,1,0:T(8,128)}, u32[]{:S(2)}) copy-start(f32[2,2,256,256]{3,2,1,0:T(8,128)} %obj_ref.7) | copy-start | bytes 3145732
  2.6 10.9 %collective-permute-start = (f32[2,256,128]{2,1,0:T(8,128)S(1)}, f32[2,256,128]{2,1,0:T(8,128)S(1)}, u32[]{:S(2)}, u32[]{:S(2)}) collective-permute-start(f32[2,256,128]{2,1,0:T(8,128)S(1)} %get-tuple-element.34), channel_id=1, source_target_pairs={{0,1},{1,0},{2,3},{3,2},{4,5},{5,4},{6,7},{7,6},{8,9},{9,8},{10,11... | collective-permute-start | bytes 786440 | tf_op jit(solution)/shard_map/ppermute | solution.py:367
  6.0 15.7 %collective-permute-start.1 = (f32[2,256,128]{2,1,0:T(8,128)S(1)}, f32[2,256,128]{2,1,0:T(8,128)S(1)}, u32[]{:S(2)}, u32[]{:S(2)}) collective-permute-start(f32[2,256,128]{2,1,0:T(8,128)S(1)} %get-tuple-element.35), channel_id=1, source_target_pairs={{0,15},{1,2},{2,1},{3,4},{4,3},{5,6},{6,5},{7,8},{8,7},{9,10},{10,... | collective-permute-start | bytes 786440 | tf_op jit(solution)/shard_map/ppermute | solution.py:367
  7.1 20.9 %collective-permute-start.2 = (f32[2,4,64,128]{3,2,1,0:T(8,128)S(1)}, f32[2,4,64,128]{3,2,1,0:T(8,128)S(1)}, u32[]{:S(2)}, u32[]{:S(2)}) collective-permute-start(f32[2,4,64,128]{3,2,1,0:T(8,128)S(1)} %get-tuple-element.36), channel_id=1, source_target_pairs={{0,16},{1,17},{2,18},{3,19},{4,20},{5,21},{6,22},{7,23},{8,24},{9,... | collective-permute-start | bytes 786440 | tf_op jit(solution)/shard_map/ppermute | solution.py:367
  8.8 20.9 %copy-start.2 = (f32[2,128,128]{2,1,0:T(8,128)S(1)}, f32[2,128,128]{2,1,0:T(8,128)}, u32[]{:S(2)}) copy-start(f32[2,128,128]{2,1,0:T(8,128)} %probe_ref.5) | copy-start | bytes 393220
  8.8 19.2 %collective-permute-start.3 = (f32[2,4,64,128]{3,2,1,0:T(8,128)S(1)}, f32[2,4,64,128]{3,2,1,0:T(8,128)S(1)}, u32[]{:S(2)}, u32[]{:S(2)}) collective-permute-start(f32[2,4,64,128]{3,2,1,0:T(8,128)S(1)} %get-tuple-element.37), channel_id=1, source_target_pairs={{0,240},{1,241},{2,242},{3,243},{4,244},{5,245},{6,246},{7,247},{8... | collective-permute-start | bytes 786440 | tf_op jit(solution)/shard_map/ppermute | solution.py:367
  22.3 5.7 %collective-permute-start.4 = (f32[2,2,64,128]{3,2,1,0:T(8,128)S(1)}, f32[2,2,64,128]{3,2,1,0:T(8,128)S(1)}, u32[]{:S(2)}, u32[]{:S(2)}) collective-permute-start(f32[2,2,64,128]{3,2,1,0:T(8,128)S(1)} %get-tuple-element.38), channel_id=1, source_target_pairs={{0,16},{1,17},{2,18},{3,19},{4,20},{5,21},{6,22},{7,23},{8,24},{9,... | collective-permute-start | bytes 393224 | tf_op jit(solution)/shard_map/ppermute | solution.py:367
  22.4 7.3 %copy-start.4 = (s32[1,8]{1,0:T(1,128)S(1)}, s32[1,8]{1,0:T(1,128)}, u32[]{:S(2)}) copy-start(s32[1,8]{1,0:T(1,128)} %row_ref.5) | copy-start | bytes 100
  22.4 7.3 %copy-start.5 = (s32[1,8]{1,0:T(1,128)S(1)}, s32[1,8]{1,0:T(1,128)}, u32[]{:S(2)}) copy-start(s32[1,8]{1,0:T(1,128)} %col_ref.5) | copy-start | bytes 100
  22.4 7.3 %collective-permute-start.5 = (f32[2,2,64,128]{3,2,1,0:T(8,128)S(1)}, f32[2,2,64,128]{3,2,1,0:T(8,128)S(1)}, u32[]{:S(2)}, u32[]{:S(2)}) collective-permute-start(f32[2,2,64,128]{3,2,1,0:T(8,128)S(1)} %get-tuple-element.39), channel_id=1, source_target_pairs={{0,240},{1,241},{2,242},{3,243},{4,244},{5,245},{6,246},{7,247},{8... | collective-permute-start | bytes 393224 | tf_op jit(solution)/shard_map/ppermute | solution.py:367
  29.7 1.2 %copy-start.1 = (bf16[4,2,256,256]{3,2,1,0:T(8,128)(2,1)S(1)}, bf16[4,2,256,256]{3,2,1,0:T(8,128)(2,1)}, u32[]{:S(2)}) copy-start(bf16[4,2,256,256]{3,2,1,0:T(8,128)(2,1)} %constant.11.clone.tabs_ref) | copy-start | bytes 3145732
  31.0 2.3 %copy-start.3 = (f32[1,8,128,128]{3,2,1,0:T(8,128)S(1)}, f32[1,8,128,128]{3,2,1,0:T(8,128)}, u32[]{:S(2)}) copy-start(f32[1,8,128,128]{3,2,1,0:T(8,128)} %param.9) | copy-start | bytes 1572868
  39.1 1.3 %collective-permute-start.6 = (f32[128,128]{1,0:T(8,128)S(1)}, f32[128,128]{1,0:T(8,128)S(1)}, u32[]{:S(2)}, u32[]{:S(2)}) collective-permute-start(f32[128,128]{1,0:T(8,128)S(1)} %get-tuple-element.46), channel_id=1, source_target_pairs={{0,1},{1,0},{2,3},{3,2},{4,5},{5,4},{6,7},{7,6},{8,9},{9,8},{10,11... | collective-permute-start | bytes 196616 | tf_op jit(solution)/shard_map/ppermute | solution.py:373
  40.5 4.1 %collective-permute-start.7 = (f32[128,128]{1,0:T(8,128)S(1)}, f32[128,128]{1,0:T(8,128)S(1)}, u32[]{:S(2)}, u32[]{:S(2)}) collective-permute-start(f32[128,128]{1,0:T(8,128)S(1)} %add.24), channel_id=1, source_target_pairs={{0,128},{1,33},{2,130},{3,35},{4,132},{5,37},{6,134},{7,39},{8,136... | collective-permute-start | bytes 196616 | tf_op jit(solution)/shard_map/ppermute | solution.py:373
  44.6 4.4 %collective-permute-start.8 = (f32[128,128]{1,0:T(8,128)S(1)}, f32[128,128]{1,0:T(8,128)S(1)}, u32[]{:S(2)}, u32[]{:S(2)}) collective-permute-start(f32[128,128]{1,0:T(8,128)S(1)} %add.25), channel_id=1, source_target_pairs={{0,4},{1,13},{2,6},{3,15},{4,0},{5,9},{6,2},{7,11},{8,12},{9,5},{1... | collective-permute-start | bytes 196616 | tf_op jit(solution)/shard_map/ppermute | solution.py:373
  47.2 15.6 %collective-permute-start.11 = (f32[2,6,64,128]{3,2,1,0:T(8,128)S(1)}, f32[2,6,64,128]{3,2,1,0:T(8,128)S(1)}, u32[]{:S(2)}, u32[]{:S(2)}) collective-permute-start(f32[2,6,64,128]{3,2,1,0:T(8,128)S(1)} %get-tuple-element.51), channel_id=1, source_target_pairs={{0,16},{1,17},{2,18},{3,19},{4,20},{5,21},{6,22},{7,23},{8,24},{9,... | collective-permute-start | bytes 1179656 | tf_op jit(solution)/shard_map/ppermute | solution.py:367
  49.0 13.8 %collective-permute-start.12 = (f32[2,6,64,128]{3,2,1,0:T(8,128)S(1)}, f32[2,6,64,128]{3,2,1,0:T(8,128)S(1)}, u32[]{:S(2)}, u32[]{:S(2)}) collective-permute-start(f32[2,6,64,128]{3,2,1,0:T(8,128)S(1)} %get-tuple-element.52), channel_id=1, source_target_pairs={{0,240},{1,241},{2,242},{3,243},{4,244},{5,245},{6,246},{7,247},{8... | collective-permute-start | bytes 1179656 | tf_op jit(solution)/shard_map/ppermute | solution.py:367
  52.7 3.4 %collective-permute-start.9 = (f32[128,128]{1,0:T(8,128)S(1)}, f32[128,128]{1,0:T(8,128)S(1)}, u32[]{:S(2)}, u32[]{:S(2)}) collective-permute-start(f32[128,128]{1,0:T(8,128)S(1)} %add.26), channel_id=1, source_target_pairs={{0,12},{1,5},{2,14},{3,7},{4,8},{5,1},{6,10},{7,3},{8,4},{9,13},{1... | collective-permute-start | bytes 196616 | tf_op jit(solution)/shard_map/ppermute | solution.py:373
  56.1 6.7 %collective-permute-start.10 = (f32[128,128]{1,0:T(8,128)S(1)}, f32[128,128]{1,0:T(8,128)S(1)}, u32[]{:S(2)}, u32[]{:S(2)}) collective-permute-start(f32[128,128]{1,0:T(8,128)S(1)} %add.27), channel_id=1, source_target_pairs={{0,130},{1,129},{2,128},{3,131},{4,134},{5,133},{6,132},{7,135},{8... | collective-permute-start | bytes 196616 | tf_op jit(solution)/shard_map/ppermute | solution.py:373
  62.8 4.8 %collective-permute-start.13 = (f32[128,128]{1,0:T(8,128)S(1)}, f32[128,128]{1,0:T(8,128)S(1)}, u32[]{:S(2)}, u32[]{:S(2)}) collective-permute-start(f32[128,128]{1,0:T(8,128)S(1)} %add.28), channel_id=1, source_target_pairs={{0,16},{1,131},{2,18},{3,129},{4,20},{5,135},{6,22},{7,133},{8,24}... | collective-permute-start | bytes 196616 | tf_op jit(solution)/shard_map/ppermute | solution.py:373
  67.7 13.4 %collective-permute-start.16 = (f32[2,256,128]{2,1,0:T(8,128)S(1)}, f32[2,256,128]{2,1,0:T(8,128)S(1)}, u32[]{:S(2)}, u32[]{:S(2)}) collective-permute-start(f32[2,256,128]{2,1,0:T(8,128)S(1)} %get-tuple-element.61), channel_id=1, source_target_pairs={{0,1},{1,0},{2,3},{3,2},{4,5},{5,4},{6,7},{7,6},{8,9},{9,8},{10,11... | collective-permute-start | bytes 786440 | tf_op jit(solution)/shard_map/ppermute | solution.py:367
  69.8 11.3 %collective-permute-start.17 = (f32[2,256,128]{2,1,0:T(8,128)S(1)}, f32[2,256,128]{2,1,0:T(8,128)S(1)}, u32[]{:S(2)}, u32[]{:S(2)}) collective-permute-start(f32[2,256,128]{2,1,0:T(8,128)S(1)} %get-tuple-element.62), channel_id=1, source_target_pairs={{0,15},{1,2},{2,1},{3,4},{4,3},{5,6},{6,5},{7,8},{8,7},{9,10},{10,... | collective-permute-start | bytes 786440 | tf_op jit(solution)/shard_map/ppermute | solution.py:367
  72.3 5.5 %collective-permute-start.14 = (f32[128,128]{1,0:T(8,128)S(1)}, f32[128,128]{1,0:T(8,128)S(1)}, u32[]{:S(2)}, u32[]{:S(2)}) collective-permute-start(f32[128,128]{1,0:T(8,128)S(1)} %add.29), channel_id=1, source_target_pairs={{0,32},{1,97},{2,34},{3,99},{4,36},{5,101},{6,38},{7,103},{8,40},{... | collective-permute-start | bytes 196616 | tf_op jit(solution)/shard_map/ppermute | solution.py:373
  77.8 3.2 %collective-permute-start.15 = (f32[128,128]{1,0:T(8,128)S(1)}, f32[128,128]{1,0:T(8,128)S(1)}, u32[]{:S(2)}, u32[]{:S(2)}) collective-permute-start(f32[128,128]{1,0:T(8,128)S(1)} %add.30), channel_id=1, source_target_pairs={{0,96},{1,17},{2,98},{3,19},{4,100},{5,21},{6,102},{7,23},{8,104},... | collective-permute-start | bytes 196616 | tf_op jit(solution)/shard_map/ppermute | solution.py:373
  81.0 8.0 %collective-permute-start.18 = (f32[128,128]{1,0:T(8,128)S(1)}, f32[128,128]{1,0:T(8,128)S(1)}, u32[]{:S(2)}, u32[]{:S(2)}) collective-permute-start(f32[128,128]{1,0:T(8,128)S(1)} %add.31.mine_ref), channel_id=1, source_target_pairs={{0,1},{1,0},{2,3},{3,2},{4,5},{5,4},{6,7},{7,6},{8,9},{9,8},{10,11... | collective-permute-start | bytes 196616 | tf_op jit(solution)/shard_map/ppermute | solution.py:373

commit v8 on v5

--- a/solution.py
+++ b/solution.py
@@ -16,7 +16,7 @@
 LANES = 128
 BOTH = ("row", "col")
 GRANT = 16 * 1024 * 1024
-MASKS = ((4, 16), (12, 32), (128, 96), (130, 128), (16, 130), (32, 4), (96, 12))
+MASKS = ((128, 4), (4, 12), (12, 128), (130, 130), (16, 32), (32, 96), (96, 16))
 
 
 def split_table(table):
@@ -51,20 +51,21 @@
 
 def two_sided(tabs_ref, right, left, real, imag):
     width = real.shape[1]
+    starts = range(0, real.shape[0], width)
     field = split(jnp.concatenate([real, imag], axis=1))
     half = mul3(field, (tabs_ref[right, 0], tabs_ref[right, 1]))
-    real, imag = half[:, :width], half[:, width:]
     field = jnp.concatenate(
         [
-            jnp.concatenate([real[:width], real[width:]], axis=1),
-            jnp.concatenate([imag[:width], imag[width:]], axis=1),
+            jnp.concatenate([half[s : s + width, :width] for s in starts], axis=1),
+            jnp.concatenate([half[s : s + width, width:] for s in starts], axis=1),
         ],
         axis=0,
     )
     full = mul3((tabs_ref[left, 0], tabs_ref[left, 1]), split(field))
-    real = jnp.concatenate([full[:width, :width], full[:width, width:]], axis=0)
-    imag = jnp.concatenate([full[width:, :width], full[width:, width:]], axis=0)
-    return real, imag
+    return tuple(
+        jnp.concatenate([full[part * width : (part + 1) * width, s : s + width] for s in starts], axis=0)
+        for part in range(2)
+    )
 
 
 def columns(piece_ref, first):
@@ -167,36 +168,36 @@
 
 def first_kernel(
     row_ref, col_ref, spot_ref, obj_ref, cola_ref, colb_ref, rowa_ref, rowb_ref, probe_ref, tabs_ref,
-    win_ref, mid_ref, ext,
+    win_ref, mid_ref, ext, *, group,
 ):
     width = probe_ref.shape[1]
     grow(ext, spot_ref, obj_ref.at[0], cola_ref, colb_ref, rowa_ref, rowb_ref)
 
-    def pair(index, _):
-        slots = (2 * index, 2 * index + 1)
+    def some(index, _):
+        slots = [group * index + place for place in range(group)]
         first_re, first_im = windows(ext, row_ref, col_ref, slots, width)
-        probe_re, probe_im = (jnp.concatenate([probe_ref[p]] * 2, axis=0) for p in range(2))
+        probe_re, probe_im = (jnp.concatenate([probe_ref[p]] * group, axis=0) for p in range(2))
         wave_re = probe_re * first_re - probe_im * first_im
         wave_im = probe_re * first_im + probe_im * first_re
         store(win_ref, slots, (first_re, first_im))
         store(mid_ref, slots, two_sided(tabs_ref, 0, 1, wave_re, wave_im))
         return 0
 
-    lax.fori_loop(0, row_ref.shape[1] // 2, pair, 0)
+    lax.fori_loop(0, row_ref.shape[1] // group, some, 0, unroll=True)
 
 
 def second_kernel(
     row_ref, col_ref, spot_ref, live_ref, obj_ref, cola_ref, colb_ref, rowa_ref, rowb_ref,
     win_ref, mid_ref, measured_ref, tabs_ref,
     grad_ref, down_ref, keep_ref, send_ref,
-    ext, sum_ref,
+    ext, sum_ref, *, group,
 ):
     width = win_ref.shape[2]
     grow(ext, spot_ref, obj_ref.at[1], cola_ref, colb_ref, rowa_ref, rowb_ref)
     sum_ref[...] = jnp.zeros_like(sum_ref)
 
-    def pair(index, _):
-        slots = (2 * index, 2 * index + 1)
+    def some(index, _):
+        slots = [group * index + place for place in range(group)]
         second_re, second_im = windows(ext, row_ref, col_ref, slots, width)
         mid_re, mid_im = (stacked(mid_ref, slots, part) for part in range(2))
         exit_re = mid_re * second_re - mid_im * second_im
@@ -220,11 +221,14 @@
         first_re, first_im = (stacked(win_ref, slots, part) for part in range(2))
         sum_re = first_re * down_re + first_im * down_im
         sum_im = first_re * down_im - first_im * down_re
-        sum_ref[0] += sum_re[:width] + sum_re[width:]
-        sum_ref[1] += sum_im[:width] + sum_im[width:]
+        for part, value in enumerate((sum_re, sum_im)):
+            total = value[:width]
+            for start in range(width, group * width, width):
+                total += value[start : start + width]
+            sum_ref[part] += total
         return 0
 
-    lax.fori_loop(0, row_ref.shape[1] // 2, pair, 0)
+    lax.fori_loop(0, row_ref.shape[1] // group, some, 0, unroll=True)
     keep_ref[...] = pick(spot_ref, 1, sum_ref[0], sum_ref[1])
     send_ref[...] = pick(spot_ref, 1, sum_ref[1], sum_ref[0])
 
@@ -350,7 +354,9 @@
         pairs = []
         for spot in np.ndindex(*sizes):
             other = list(spot)
-            other[axis] = (((spot[axis] + odd) ^ 1) - odd) % sizes[axis]
+            place = ((spot[axis] + odd) ^ 1) - odd
+            if 0 <= place < sizes[axis]:
+                other[axis] = place
             pairs.append((spot[0] * sizes[1] + spot[1], other[0] * sizes[1] + other[1]))
         got.append(lax.ppermute(strip, BOTH, pairs))
     return got
@@ -395,11 +401,11 @@
         )
         halos.append((*cols[piece], *meet(strips, 0)))
     win, mid = call(
-        first_kernel, [fields] * 2, (offset_row, offset_col, spot),
+        functools.partial(first_kernel, group=2), [fields] * 2, (offset_row, offset_col, spot),
         (object_field, *halos[0], probe, tabs), (grown,),
     )
     grad, down, mine, send = call(
-        second_kernel, [fields] * 2 + [array(*plane)] * 2, (offset_row, offset_col, spot, live),
+        functools.partial(second_kernel, group=count), [fields] * 2 + [array(*plane)] * 2, (offset_row, offset_col, spot, live),
         (object_field, *halos[1], win, mid, intensity[0], tabs),
         (grown, pltpu.VMEM((2, *plane), jnp.float32)),
     )
@@ -414,11 +420,14 @@
     rows = meet(strips, 0)
     for mask in MASKS[1:4]:
         mine = mine + swap(mine, mask)
+    mine, *rows = lax.optimization_barrier((mine, *rows))
     strips = call(fold_kernel, [array(2, *side)] * 2, (spot,), (left, right, *rows))
+    mine = mine + swap(mine, MASKS[4])
     mine, *strips = lax.optimization_barrier((mine, *strips))
     cols = meet(strips, 1)
-    for mask in MASKS[4:]:
+    for mask in MASKS[5:]:
         mine = mine + swap(mine, mask)
+    mine, *cols = lax.optimization_barrier((mine, *cols))
     (new,) = call(finish_kernel, (field,), (spot,), (part, *rows, *cols))
     other = swap(mine, (1, 1))
     count_all = count * lax.axis_size("row") * lax.axis_size("col")

time: 86.2 us -> 89.8 us (1.042)
  the two profiles are of different devices: /device:TPU:1 before, /device:TPU:11 now
where the time goes in v8:
time: 89.8 us; the launch traced here: 89.5 us
  starting transfers between devices  40.2 us (45%)
  waiting for transfers between devices  30.5 us (34%)
  Pallas kernels  17 us (19%)
  between operations  1.62 us (2%)
    ppermute x12, starting transfers between devices, meet(): got.append(lax.ppermute(strip, BOTH, pairs))  31.2 us
    ppermute x9, waiting for transfers between devices, swap(): lax.ppermute(value, BOTH, [(i, i ^ masks[i % 2]) for i in range(count)])  26.8 us
    pallas_call x8, Pallas kernels, call(): pl.pallas_call(kernel, out_shape=tuple(out_shape), in_specs=smem(len(scal...  15.2 us
    ppermute x9, starting transfers between devices, swap(): lax.ppermute(value, BOTH, [(i, i ^ masks[i % 2]) for i in range(count)])  8.98 us
    ppermute x12, waiting for transfers between devices, meet(): got.append(lax.ppermute(strip, BOTH, pairs))  3.64 us
    pallas_call x1, Pallas kernels, on_device(): pl.pallas_call(pack_kernel, out_shape=tuple([array(*side)] * 4), in_specs...  1.89 us
  transfers between devices with their start and end apart: 21, of which 10 were waited for; matrix products, arithmetic and copies ran while one was open for 0% of the time, Pallas kernels for 9%

profile of v8, /device:TPU:11, one launch (start us, length us, event | category | flops | bytes accessed | tf_op | source)
XLA Modules:
  0.0 89.5 jit_solution(2316181603663412451)
XLA Ops:
  0.6 0.0 copy-start
  0.7 0.1 add_bitcast_fusion.spot_ref
  0.7 1.9 %shard_map.86 = (f32[256,128]{1,0:T(8,128)S(1)}, f32[256,128]{1,0:T(8,128)S(1)}, f32[256,128]{1,0:T(8,128)S(1)}, f32[256,128]{1,0:T(8,128)S(1)}) custom-call(s32[1,4]{1,0:T(1,128)S(1)} %add_bitcast_fusion.spot_ref, f32[2,2,256,256]{3,2,1,0:T(8,128)} %obj_ref.11), custom_call_target="tpu_custom_call" | custom-call | tf_op jit(solution)/shard_map/pallas_call | solution.py:389
  2.6 0.8 collective-permute-start.4
  3.4 3.8 %collective-permute-start.5 = (f32[256,128]{1,0:T(8,128)S(1)}, f32[256,128]{1,0:T(8,128)S(1)}, u32[]{:S(2)}, u32[]{:S(2)}) collective-permute-start(f32[256,128]{1,0:T(8,128)S(1)} %get-tuple-element.40), channel_id=1, source_target_pairs={{0,0},{1,2},{2,1},{3,4},{4,3},{5,6},{6,5},{7,8},{8,7},{9,10},{10,9... | collective-permute-start | bytes 393224 | tf_op jit(solution)/shard_map/ppermute | solution.py:361
  7.2 0.5 collective-permute-start
  7.8 0.0 copy-start.1
  7.8 3.8 %collective-permute-start.1 = (f32[256,128]{1,0:T(8,128)S(1)}, f32[256,128]{1,0:T(8,128)S(1)}, u32[]{:S(2)}, u32[]{:S(2)}) collective-permute-start(f32[256,128]{1,0:T(8,128)S(1)} %get-tuple-element.36), channel_id=1, source_target_pairs={{0,0},{1,2},{2,1},{3,4},{4,3},{5,6},{6,5},{7,8},{8,7},{9,10},{10,9... | collective-permute-start | bytes 393224 | tf_op jit(solution)/shard_map/ppermute | solution.py:361
  11.6 0.0 collective-permute-done.4.cola_ref
  11.6 0.9 %collective-permute-done.5.colb_ref = f32[256,128]{1,0:T(8,128)S(1)} collective-permute-done((f32[256,128]{1,0:T(8,128)S(1)}, f32[256,128]{1,0:T(8,128)S(1)}, u32[]{:S(2)}, u32[]{:S(2)}) %collective-permute-start.5) | collective-permute-done | bytes 131104 | tf_op jit(solution)/shard_map/ppermute | solution.py:361
  12.6 0.0 copy-done
  12.6 0.6 shard_map.88
  13.2 1.7 %collective-permute-start.6 = (f32[6,64,128]{2,1,0:T(8,128)S(1)}, f32[6,64,128]{2,1,0:T(8,128)S(1)}, u32[]{:S(2)}, u32[]{:S(2)}) collective-permute-start(f32[6,64,128]{2,1,0:T(8,128)S(1)} %get-tuple-element.41), channel_id=1, source_target_pairs={{0,16},{1,17},{2,18},{3,19},{4,20},{5,21},{6,22},{7,23},{8,24},{9,... | collective-permute-start | bytes 589832 | tf_op jit(solution)/shard_map/ppermute | solution.py:361
  14.9 0.0 copy-start.2
  14.9 6.6 %collective-permute-start.7 = (f32[6,64,128]{2,1,0:T(8,128)S(1)}, f32[6,64,128]{2,1,0:T(8,128)S(1)}, u32[]{:S(2)}, u32[]{:S(2)}) collective-permute-start(f32[6,64,128]{2,1,0:T(8,128)S(1)} %get-tuple-element.42), channel_id=1, source_target_pairs={{0,0},{1,1},{2,2},{3,3},{4,4},{5,5},{6,6},{7,7},{8,8},{9,9},{10,10... | collective-permute-start | bytes 589832 | tf_op jit(solution)/shard_map/ppermute | solution.py:361
  21.5 0.0 collective-permute-done.cola_ref
  21.5 0.0 collective-permute-done.1.colb_ref
  21.5 0.6 shard_map.87
  22.1 0.1 collective-permute-start.2
  22.2 0.0 copy-start.4
  22.2 0.0 copy-start.5
  22.2 4.7 %collective-permute-start.3 = (f32[6,64,128]{2,1,0:T(8,128)S(1)}, f32[6,64,128]{2,1,0:T(8,128)S(1)}, u32[]{:S(2)}, u32[]{:S(2)}) collective-permute-start(f32[6,64,128]{2,1,0:T(8,128)S(1)} %get-tuple-element.38), channel_id=1, source_target_pairs={{0,0},{1,1},{2,2},{3,3},{4,4},{5,5},{6,6},{7,7},{8,8},{9,9},{10,10... | collective-permute-start | bytes 589832 | tf_op jit(solution)/shard_map/ppermute | solution.py:361
  27.5 0.0 copy-start.3
  27.5 0.0 collective-permute-done.6.rowa_ref
  27.6 0.0 collective-permute-done.7.rowb_ref
  27.6 0.0 copy-done.1
  27.6 0.0 copy-done.2
  27.6 0.0 copy-done.4
  27.6 0.0 copy-done.5
  27.6 2.2 %shard_map.89 = (f32[8,2,128,128]{3,2,1,0:T(8,128)S(1)}, f32[8,2,128,128]{3,2,1,0:T(8,128)S(1)}) custom-call(s32[1,8]{1,0:T(1,128)S(1)} %copy-done.4, s32[1,8]{1,0:T(1,128)S(1)} %copy-done.5, s32[1,4]{1,0:T(1,128)S(1)} %add_bitcast_fusion.spot_ref, f32[2,2,256,256]{3,2,1,0:T(8,128)S(1)} %copy-done, f32[256,128]{1,0:T(8,128)S(1)} %collective-permute-done.4.cola_ref, ...), custom_call_target="tpu_custom_call" | custom-call | tf_op jit(solution)/shard_map/pallas_call | solution.py:371
  29.9 0.0 collective-permute-done.2.rowa_ref
  29.9 2.7 %collective-permute-done.3.rowb_ref = f32[6,64,128]{2,1,0:T(8,128)S(1)} collective-permute-done((f32[6,64,128]{2,1,0:T(8,128)S(1)}, f32[6,64,128]{2,1,0:T(8,128)S(1)}, u32[]{:S(2)}, u32[]{:S(2)}) %collective-permute-start.3) | collective-permute-done | bytes 196640 | tf_op jit(solution)/shard_map/ppermute | solution.py:361
  32.6 0.0 copy-done.3
  32.6 5.9 %shard_map.90 = (f32[8,2,128,128]{3,2,1,0:T(8,128)S(1)}, f32[8,2,128,128]{3,2,1,0:T(8,128)S(1)}, f32[128,128]{1,0:T(8,128)S(1)}, f32[128,128]{1,0:T(8,128)S(1)}) custom-call(s32[1,8]{1,0:T(1,128)S(1)} %copy-done.4, s32[1,8]{1,0:T(1,128)S(1)} %copy-done.5, s32[1,4]{1,0:T(1,128)S(1)} %add_bitcast_fusion.spot_ref, s32[1,1]{1,0:T(1,128)S(6)} %copy.9.live_ref, ...), custom_call_target="tpu_custom_call" | custom-call | tf_op jit(solution)/shard_map/pallas_call | solution.py:371
  38.4 1.1 %collective-permute-start.8 = (f32[128,128]{1,0:T(8,128)S(1)}, f32[128,128]{1,0:T(8,128)S(1)}, u32[]{:S(2)}, u32[]{:S(2)}) collective-permute-start(f32[128,128]{1,0:T(8,128)S(1)} %get-tuple-element.49), channel_id=1, source_target_pairs={{0,1},{1,0},{2,3},{3,2},{4,5},{5,4},{6,7},{7,6},{8,9},{9,8},{10,11... | collective-permute-start | bytes 196616 | tf_op jit(solution)/shard_map/ppermute | solution.py:367
  39.5 0.9 %collective-permute-done.8 = f32[128,128]{1,0:T(8,128)S(1)} collective-permute-done((f32[128,128]{1,0:T(8,128)S(1)}, f32[128,128]{1,0:T(8,128)S(1)}, u32[]{:S(2)}, u32[]{:S(2)}) %collective-permute-start.8) | collective-permute-done | bytes 65568 | tf_op jit(solution)/shard_map/ppermute | solution.py:367
  40.4 0.1 collective-permute-start.9
  40.5 2.3 %shard_map.91 = (f32[2,2,256,256]{3,2,1,0:T(8,128)S(1)}, f32[2,6,64,128]{3,2,1,0:T(8,128)S(1)}, f32[2,6,64,128]{3,2,1,0:T(8,128)S(1)}, f32[2,256,128]{2,1,0:T(8,128)S(1)}, f32[2,256,128]{2,1,0:T(8,128)S(1)}) custom-call(s32[1,8]{1,0:T(1,128)S(1)} %copy-done.4, s32[1,8]{1,0:T(1,128)S(1)} %copy-done.5, s32[1,4]{1,0:T(1,128)S(1)} %add_bitcast_fusion.spot_ref, ...), custom_call_target="tpu_custom_call" | custom-call | tf_op jit(solution)/shard_map/pallas_call | solution.py:371
  42.8 0.8 collective-permute-done.9
  43.6 0.1 collective-permute-start.13
  43.8 4.7 %collective-permute-start.14 = (f32[2,6,64,128]{3,2,1,0:T(8,128)S(1)}, f32[2,6,64,128]{3,2,1,0:T(8,128)S(1)}, u32[]{:S(2)}, u32[]{:S(2)}) collective-permute-start(f32[2,6,64,128]{3,2,1,0:T(8,128)S(1)} %get-tuple-element.54), channel_id=1, source_target_pairs={{0,0},{1,1},{2,2},{3,3},{4,4},{5,5},{6,6},{7,7},{8,8},{9,9},{10,10... | collective-permute-start | bytes 1179656 | tf_op jit(solution)/shard_map/ppermute | solution.py:361
  48.4 1.7 %collective-permute-start.10 = (f32[128,128]{1,0:T(8,128)S(1)}, f32[128,128]{1,0:T(8,128)S(1)}, u32[]{:S(2)}, u32[]{:S(2)}) collective-permute-start(f32[128,128]{1,0:T(8,128)S(1)} %add.25), channel_id=1, source_target_pairs={{0,4},{1,13},{2,6},{3,15},{4,0},{5,9},{6,2},{7,11},{8,12},{9,5},{1... | collective-permute-start | bytes 196616 | tf_op jit(solution)/shard_map/ppermute | solution.py:367
  50.1 2.0 %collective-permute-done.10 = f32[128,128]{1,0:T(8,128)S(1)} collective-permute-done((f32[128,128]{1,0:T(8,128)S(1)}, f32[128,128]{1,0:T(8,128)S(1)}, u32[]{:S(2)}, u32[]{:S(2)}) %collective-permute-start.10) | collective-permute-done | bytes 65568 | tf_op jit(solution)/shard_map/ppermute | solution.py:367
  52.1 0.1 collective-permute-start.11
  52.2 7.1 %collective-permute-done.11 = f32[128,128]{1,0:T(8,128)S(1)} collective-permute-done((f32[128,128]{1,0:T(8,128)S(1)}, f32[128,128]{1,0:T(8,128)S(1)}, u32[]{:S(2)}, u32[]{:S(2)}) %collective-permute-start.11) | collective-permute-done | bytes 65568 | tf_op jit(solution)/shard_map/ppermute | solution.py:367
  59.3 0.4 collective-permute-start.12
  59.8 3.9 %collective-permute-done.12 = f32[128,128]{1,0:T(8,128)S(1)} collective-permute-done((f32[128,128]{1,0:T(8,128)S(1)}, f32[128,128]{1,0:T(8,128)S(1)}, u32[]{:S(2)}, u32[]{:S(2)}) %collective-permute-start.12) | collective-permute-done | bytes 65568 | tf_op jit(solution)/shard_map/ppermute | solution.py:367
  63.6 0.0 collective-permute-done.13.rowa_ref
  63.6 0.0 collective-permute-done.14.rowb_ref
  63.6 0.1 collective-permute-start.15
  63.7 0.6 shard_map.92
  64.4 3.5 %collective-permute-done.15 = f32[128,128]{1,0:T(8,128)S(1)} collective-permute-done((f32[128,128]{1,0:T(8,128)S(1)}, f32[128,128]{1,0:T(8,128)S(1)}, u32[]{:S(2)}, u32[]{:S(2)}) %collective-permute-start.15) | collective-permute-done | bytes 65568 | tf_op jit(solution)/shard_map/ppermute | solution.py:367
  67.8 1.4 %collective-permute-start.18 = (f32[2,256,128]{2,1,0:T(8,128)S(1)}, f32[2,256,128]{2,1,0:T(8,128)S(1)}, u32[]{:S(2)}, u32[]{:S(2)}) collective-permute-start(f32[2,256,128]{2,1,0:T(8,128)S(1)} %get-tuple-element.63), channel_id=1, source_target_pairs={{0,1},{1,0},{2,3},{3,2},{4,5},{5,4},{6,7},{7,6},{8,9},{9,8},{10,11... | collective-permute-start | bytes 786440 | tf_op jit(solution)/shard_map/ppermute | solution.py:361
  69.2 3.0 %collective-permute-start.19 = (f32[2,256,128]{2,1,0:T(8,128)S(1)}, f32[2,256,128]{2,1,0:T(8,128)S(1)}, u32[]{:S(2)}, u32[]{:S(2)}) collective-permute-start(f32[2,256,128]{2,1,0:T(8,128)S(1)} %get-tuple-element.64), channel_id=1, source_target_pairs={{0,0},{1,2},{2,1},{3,4},{4,3},{5,6},{6,5},{7,8},{8,7},{9,10},{10,9... | collective-permute-start | bytes 786440 | tf_op jit(solution)/shard_map/ppermute | solution.py:361
  72.2 0.5 collective-permute-start.16
  72.8 5.6 %collective-permute-done.16 = f32[128,128]{1,0:T(8,128)S(1)} collective-permute-done((f32[128,128]{1,0:T(8,128)S(1)}, f32[128,128]{1,0:T(8,128)S(1)}, u32[]{:S(2)}, u32[]{:S(2)}) %collective-permute-start.16) | collective-permute-done | bytes 65568 | tf_op jit(solution)/shard_map/ppermute | solution.py:367
  78.4 0.1 collective-permute-start.17
  78.5 3.1 %collective-permute-done.17 = f32[128,128]{1,0:T(8,128)S(1)} collective-permute-done((f32[128,128]{1,0:T(8,128)S(1)}, f32[128,128]{1,0:T(8,128)S(1)}, u32[]{:S(2)}, u32[]{:S(2)}) %collective-permute-start.17) | collective-permute-done | bytes 65568 | tf_op jit(solution)/shard_map/ppermute | solution.py:367
  81.6 0.0 collective-permute-done.18.cola_ref
  81.6 0.0 collective-permute-done.19.colb_ref
  81.6 4.9 %collective-permute-start.20 = (f32[128,128]{1,0:T(8,128)S(1)}, f32[128,128]{1,0:T(8,128)S(1)}, u32[]{:S(2)}, u32[]{:S(2)}) collective-permute-start(f32[128,128]{1,0:T(8,128)S(1)} %add.31.mine_ref), channel_id=1, source_target_pairs={{0,1},{1,0},{2,3},{3,2},{4,5},{5,4},{6,7},{7,6},{8,9},{9,8},{10,11... | collective-permute-start | bytes 196616 | tf_op jit(solution)/shard_map/ppermute | solution.py:367
  86.5 1.8 %shard_map.93 = f32[2,2,256,256]{3,2,1,0:T(8,128)} custom-call(s32[1,4]{1,0:T(1,128)S(1)} %add_bitcast_fusion.spot_ref, f32[2,2,256,256]{3,2,1,0:T(8,128)S(1)} %get-tuple-element.47.part_ref, f32[2,6,64,128]{3,2,1,0:T(8,128)S(1)} %collective-permute-done.13.rowa_ref, f32[2,6,64,128]{3,2,1,0:T(8,128)S(1)} %collective-permute-done.14.rowb_ref, ...), custom_call_target="tpu_custom_call" | custom-call | tf_op jit(solution)/shard_map/pallas_call | solution.py:371
  88.3 0.0 collective-permute-done.20.other_ref
  88.3 1.2 %shard_map.94 = f32[2,128,128]{2,1,0:T(8,128)} custom-call(s32[1,4]{1,0:T(1,128)S(1)} %add_bitcast_fusion.spot_ref, f32[2,128,128]{2,1,0:T(8,128)S(1)} %copy-done.2, f32[128,128]{1,0:T(8,128)S(1)} %add.31.mine_ref, f32[128,128]{1,0:T(8,128)S(1)} %collective-permute-done.20.other_ref), custom_call_target="tpu_custom_call" | custom-call | tf_op jit(solution)/shard_map/pallas_call | solution.py:371
  (9 shorter events, 0.1 us)
Async XLA Ops:
  0.6 12.0 %copy-start = (f32[2,2,256,256]{3,2,1,0:T(8,128)S(1)}, f32[2,2,256,256]{3,2,1,0:T(8,128)}, u32[]{:S(2)}) copy-start(f32[2,2,256,256]{3,2,1,0:T(8,128)} %obj_ref.11) | copy-start | bytes 3145732
  2.6 9.0 %collective-permute-start.4 = (f32[256,128]{1,0:T(8,128)S(1)}, f32[256,128]{1,0:T(8,128)S(1)}, u32[]{:S(2)}, u32[]{:S(2)}) collective-permute-start(f32[256,128]{1,0:T(8,128)S(1)} %get-tuple-element.39), channel_id=1, source_target_pairs={{0,1},{1,0},{2,3},{3,2},{4,5},{5,4},{6,7},{7,6},{8,9},{9,8},{10,11... | collective-permute-start | bytes 393224 | tf_op jit(solution)/shard_map/ppermute | solution.py:361
  3.4 9.2 %collective-permute-start.5 = (f32[256,128]{1,0:T(8,128)S(1)}, f32[256,128]{1,0:T(8,128)S(1)}, u32[]{:S(2)}, u32[]{:S(2)}) collective-permute-start(f32[256,128]{1,0:T(8,128)S(1)} %get-tuple-element.40), channel_id=1, source_target_pairs={{0,0},{1,2},{2,1},{3,4},{4,3},{5,6},{6,5},{7,8},{8,7},{9,10},{10,9... | collective-permute-start | bytes 393224 | tf_op jit(solution)/shard_map/ppermute | solution.py:361
  7.2 14.3 %collective-permute-start = (f32[256,128]{1,0:T(8,128)S(1)}, f32[256,128]{1,0:T(8,128)S(1)}, u32[]{:S(2)}, u32[]{:S(2)}) collective-permute-start(f32[256,128]{1,0:T(8,128)S(1)} %get-tuple-element.35), channel_id=1, source_target_pairs={{0,1},{1,0},{2,3},{3,2},{4,5},{5,4},{6,7},{7,6},{8,9},{9,8},{10,11... | collective-permute-start | bytes 393224 | tf_op jit(solution)/shard_map/ppermute | solution.py:361
  7.8 19.8 %copy-start.1 = (bf16[4,2,256,256]{3,2,1,0:T(8,128)(2,1)S(1)}, bf16[4,2,256,256]{3,2,1,0:T(8,128)(2,1)}, u32[]{:S(2)}) copy-start(bf16[4,2,256,256]{3,2,1,0:T(8,128)(2,1)} %constant.11.clone.tabs_ref) | copy-start | bytes 3145732
  7.8 13.7 %collective-permute-start.1 = (f32[256,128]{1,0:T(8,128)S(1)}, f32[256,128]{1,0:T(8,128)S(1)}, u32[]{:S(2)}, u32[]{:S(2)}) collective-permute-start(f32[256,128]{1,0:T(8,128)S(1)} %get-tuple-element.36), channel_id=1, source_target_pairs={{0,0},{1,2},{2,1},{3,4},{4,3},{5,6},{6,5},{7,8},{8,7},{9,10},{10,9... | collective-permute-start | bytes 393224 | tf_op jit(solution)/shard_map/ppermute | solution.py:361
  13.2 14.4 %collective-permute-start.6 = (f32[6,64,128]{2,1,0:T(8,128)S(1)}, f32[6,64,128]{2,1,0:T(8,128)S(1)}, u32[]{:S(2)}, u32[]{:S(2)}) collective-permute-start(f32[6,64,128]{2,1,0:T(8,128)S(1)} %get-tuple-element.41), channel_id=1, source_target_pairs={{0,16},{1,17},{2,18},{3,19},{4,20},{5,21},{6,22},{7,23},{8,24},{9,... | collective-permute-start | bytes 589832 | tf_op jit(solution)/shard_map/ppermute | solution.py:361
  14.9 12.7 %copy-start.2 = (f32[2,128,128]{2,1,0:T(8,128)S(1)}, f32[2,128,128]{2,1,0:T(8,128)}, u32[]{:S(2)}) copy-start(f32[2,128,128]{2,1,0:T(8,128)} %probe_ref.5) | copy-start | bytes 393220
  14.9 12.7 %collective-permute-start.7 = (f32[6,64,128]{2,1,0:T(8,128)S(1)}, f32[6,64,128]{2,1,0:T(8,128)S(1)}, u32[]{:S(2)}, u32[]{:S(2)}) collective-permute-start(f32[6,64,128]{2,1,0:T(8,128)S(1)} %get-tuple-element.42), channel_id=1, source_target_pairs={{0,0},{1,1},{2,2},{3,3},{4,4},{5,5},{6,6},{7,7},{8,8},{9,9},{10,10... | collective-permute-start | bytes 589832 | tf_op jit(solution)/shard_map/ppermute | solution.py:361
  22.1 7.8 %collective-permute-start.2 = (f32[6,64,128]{2,1,0:T(8,128)S(1)}, f32[6,64,128]{2,1,0:T(8,128)S(1)}, u32[]{:S(2)}, u32[]{:S(2)}) collective-permute-start(f32[6,64,128]{2,1,0:T(8,128)S(1)} %get-tuple-element.37), channel_id=1, source_target_pairs={{0,16},{1,17},{2,18},{3,19},{4,20},{5,21},{6,22},{7,23},{8,24},{9,... | collective-permute-start | bytes 589832 | tf_op jit(solution)/shard_map/ppermute | solution.py:361
  22.2 5.4 %copy-start.4 = (s32[1,8]{1,0:T(1,128)S(1)}, s32[1,8]{1,0:T(1,128)}, u32[]{:S(2)}) copy-start(s32[1,8]{1,0:T(1,128)} %row_ref.5) | copy-start | bytes 100
  22.2 5.4 %copy-start.5 = (s32[1,8]{1,0:T(1,128)S(1)}, s32[1,8]{1,0:T(1,128)}, u32[]{:S(2)}) copy-start(s32[1,8]{1,0:T(1,128)} %col_ref.5) | copy-start | bytes 100
  22.2 10.3 %collective-permute-start.3 = (f32[6,64,128]{2,1,0:T(8,128)S(1)}, f32[6,64,128]{2,1,0:T(8,128)S(1)}, u32[]{:S(2)}, u32[]{:S(2)}) collective-permute-start(f32[6,64,128]{2,1,0:T(8,128)S(1)} %get-tuple-element.38), channel_id=1, source_target_pairs={{0,0},{1,1},{2,2},{3,3},{4,4},{5,5},{6,6},{7,7},{8,8},{9,9},{10,10... | collective-permute-start | bytes 589832 | tf_op jit(solution)/shard_map/ppermute | solution.py:361
  27.5 5.0 %copy-start.3 = (f32[1,8,128,128]{3,2,1,0:T(8,128)S(1)}, f32[1,8,128,128]{3,2,1,0:T(8,128)}, u32[]{:S(2)}) copy-start(f32[1,8,128,128]{3,2,1,0:T(8,128)} %param.9) | copy-start | bytes 1572868
  38.4 2.0 %collective-permute-start.8 = (f32[128,128]{1,0:T(8,128)S(1)}, f32[128,128]{1,0:T(8,128)S(1)}, u32[]{:S(2)}, u32[]{:S(2)}) collective-permute-start(f32[128,128]{1,0:T(8,128)S(1)} %get-tuple-element.49), channel_id=1, source_target_pairs={{0,1},{1,0},{2,3},{3,2},{4,5},{5,4},{6,7},{7,6},{8,9},{9,8},{10,11... | collective-permute-start | bytes 196616 | tf_op jit(solution)/shard_map/ppermute | solution.py:367
  40.4 3.2 %collective-permute-start.9 = (f32[128,128]{1,0:T(8,128)S(1)}, f32[128,128]{1,0:T(8,128)S(1)}, u32[]{:S(2)}, u32[]{:S(2)}) collective-permute-start(f32[128,128]{1,0:T(8,128)S(1)} %add.24), channel_id=1, source_target_pairs={{0,128},{1,5},{2,130},{3,7},{4,132},{5,1},{6,134},{7,3},{8,136},{9... | collective-permute-start | bytes 196616 | tf_op jit(solution)/shard_map/ppermute | solution.py:367
  43.6 20.0 %collective-permute-start.13 = (f32[2,6,64,128]{3,2,1,0:T(8,128)S(1)}, f32[2,6,64,128]{3,2,1,0:T(8,128)S(1)}, u32[]{:S(2)}, u32[]{:S(2)}) collective-permute-start(f32[2,6,64,128]{3,2,1,0:T(8,128)S(1)} %get-tuple-element.53), channel_id=1, source_target_pairs={{0,16},{1,17},{2,18},{3,19},{4,20},{5,21},{6,22},{7,23},{8,24},{9,... | collective-permute-start | bytes 1179656 | tf_op jit(solution)/shard_map/ppermute | solution.py:361
  43.8 19.9 %collective-permute-start.14 = (f32[2,6,64,128]{3,2,1,0:T(8,128)S(1)}, f32[2,6,64,128]{3,2,1,0:T(8,128)S(1)}, u32[]{:S(2)}, u32[]{:S(2)}) collective-permute-start(f32[2,6,64,128]{3,2,1,0:T(8,128)S(1)} %get-tuple-element.54), channel_id=1, source_target_pairs={{0,0},{1,1},{2,2},{3,3},{4,4},{5,5},{6,6},{7,7},{8,8},{9,9},{10,10... | collective-permute-start | bytes 1179656 | tf_op jit(solution)/shard_map/ppermute | solution.py:361
  48.4 3.7 %collective-permute-start.10 = (f32[128,128]{1,0:T(8,128)S(1)}, f32[128,128]{1,0:T(8,128)S(1)}, u32[]{:S(2)}, u32[]{:S(2)}) collective-permute-start(f32[128,128]{1,0:T(8,128)S(1)} %add.25), channel_id=1, source_target_pairs={{0,4},{1,13},{2,6},{3,15},{4,0},{5,9},{6,2},{7,11},{8,12},{9,5},{1... | collective-permute-start | bytes 196616 | tf_op jit(solution)/shard_map/ppermute | solution.py:367
  52.1 7.2 %collective-permute-start.11 = (f32[128,128]{1,0:T(8,128)S(1)}, f32[128,128]{1,0:T(8,128)S(1)}, u32[]{:S(2)}, u32[]{:S(2)}) collective-permute-start(f32[128,128]{1,0:T(8,128)S(1)} %add.26), channel_id=1, source_target_pairs={{0,12},{1,129},{2,14},{3,131},{4,8},{5,133},{6,10},{7,135},{8,4},{... | collective-permute-start | bytes 196616 | tf_op jit(solution)/shard_map/ppermute | solution.py:367
  59.3 4.3 %collective-permute-start.12 = (f32[128,128]{1,0:T(8,128)S(1)}, f32[128,128]{1,0:T(8,128)S(1)}, u32[]{:S(2)}, u32[]{:S(2)}) collective-permute-start(f32[128,128]{1,0:T(8,128)S(1)} %add.27), channel_id=1, source_target_pairs={{0,130},{1,131},{2,128},{3,129},{4,134},{5,135},{6,132},{7,133},{8... | collective-permute-start | bytes 196616 | tf_op jit(solution)/shard_map/ppermute | solution.py:367
  63.6 4.2 %collective-permute-start.15 = (f32[128,128]{1,0:T(8,128)S(1)}, f32[128,128]{1,0:T(8,128)S(1)}, u32[]{:S(2)}, u32[]{:S(2)}) collective-permute-start(f32[128,128]{1,0:T(8,128)S(1)} %add.28), channel_id=1, source_target_pairs={{0,16},{1,33},{2,18},{3,35},{4,20},{5,37},{6,22},{7,39},{8,24},{9,... | collective-permute-start | bytes 196616 | tf_op jit(solution)/shard_map/ppermute | solution.py:367
  67.8 13.8 %collective-permute-start.18 = (f32[2,256,128]{2,1,0:T(8,128)S(1)}, f32[2,256,128]{2,1,0:T(8,128)S(1)}, u32[]{:S(2)}, u32[]{:S(2)}) collective-permute-start(f32[2,256,128]{2,1,0:T(8,128)S(1)} %get-tuple-element.63), channel_id=1, source_target_pairs={{0,1},{1,0},{2,3},{3,2},{4,5},{5,4},{6,7},{7,6},{8,9},{9,8},{10,11... | collective-permute-start | bytes 786440 | tf_op jit(solution)/shard_map/ppermute | solution.py:361
  69.2 12.4 %collective-permute-start.19 = (f32[2,256,128]{2,1,0:T(8,128)S(1)}, f32[2,256,128]{2,1,0:T(8,128)S(1)}, u32[]{:S(2)}, u32[]{:S(2)}) collective-permute-start(f32[2,256,128]{2,1,0:T(8,128)S(1)} %get-tuple-element.64), channel_id=1, source_target_pairs={{0,0},{1,2},{2,1},{3,4},{4,3},{5,6},{6,5},{7,8},{8,7},{9,10},{10,9... | collective-permute-start | bytes 786440 | tf_op jit(solution)/shard_map/ppermute | solution.py:361
  72.2 6.2 %collective-permute-start.16 = (f32[128,128]{1,0:T(8,128)S(1)}, f32[128,128]{1,0:T(8,128)S(1)}, u32[]{:S(2)}, u32[]{:S(2)}) collective-permute-start(f32[128,128]{1,0:T(8,128)S(1)} %add.29), channel_id=1, source_target_pairs={{0,32},{1,97},{2,34},{3,99},{4,36},{5,101},{6,38},{7,103},{8,40},{... | collective-permute-start | bytes 196616 | tf_op jit(solution)/shard_map/ppermute | solution.py:367
  78.4 3.2 %collective-permute-start.17 = (f32[128,128]{1,0:T(8,128)S(1)}, f32[128,128]{1,0:T(8,128)S(1)}, u32[]{:S(2)}, u32[]{:S(2)}) collective-permute-start(f32[128,128]{1,0:T(8,128)S(1)} %add.30), channel_id=1, source_target_pairs={{0,96},{1,17},{2,98},{3,19},{4,100},{5,21},{6,102},{7,23},{8,104},... | collective-permute-start | bytes 196616 | tf_op jit(solution)/shard_map/ppermute | solution.py:367
  81.6 6.6 %collective-permute-start.20 = (f32[128,128]{1,0:T(8,128)S(1)}, f32[128,128]{1,0:T(8,128)S(1)}, u32[]{:S(2)}, u32[]{:S(2)}) collective-permute-start(f32[128,128]{1,0:T(8,128)S(1)} %add.31.mine_ref), channel_id=1, source_target_pairs={{0,1},{1,0},{2,3},{3,2},{4,5},{5,4},{6,7},{7,6},{8,9},{9,8},{10,11... | collective-permute-start | bytes 196616 | tf_op jit(solution)/shard_map/ppermute | solution.py:367

commit v9 on v8

--- a/solution.py
+++ b/solution.py
@@ -357,6 +357,8 @@
             place = ((spot[axis] + odd) ^ 1) - odd
             if 0 <= place < sizes[axis]:
                 other[axis] = place
+            else:
+                other[1 - axis] ^= 1
             pairs.append((spot[0] * sizes[1] + spot[1], other[0] * sizes[1] + other[1]))
         got.append(lax.ppermute(strip, BOTH, pairs))
     return got

time: 89.8 us -> 80.5 us (0.90)
  the two profiles are of different devices: /device:TPU:11 before, /device:TPU:1 now
where the time goes in v9:
time: 80.5 us; the launch traced here: 80.4 us
  starting transfers between devices  35.6 us (44%)
  waiting for transfers between devices  26 us (32%)
  Pallas kernels  17 us (21%)
  between operations  1.53 us (2%)
    ppermute x9, starting transfers between devices, swap(): lax.ppermute(value, BOTH, [(i, i ^ masks[i % 2]) for i in range(count)])  19.5 us
    ppermute x9, waiting for transfers between devices, swap(): lax.ppermute(value, BOTH, [(i, i ^ masks[i % 2]) for i in range(count)])  19.1 us
    ppermute x12, starting transfers between devices, meet(): got.append(lax.ppermute(strip, BOTH, pairs))  16.1 us
    pallas_call x8, Pallas kernels, call(): pl.pallas_call(kernel, out_shape=tuple(out_shape), in_specs=smem(len(scal...  15.1 us
    ppermute x12, waiting for transfers between devices, meet(): got.append(lax.ppermute(strip, BOTH, pairs))  6.98 us
    pallas_call x1, Pallas kernels, on_device(): pl.pallas_call(pack_kernel, out_shape=tuple([array(*side)] * 4), in_specs...  1.89 us
  transfers between devices with their start and end apart: 21, of which 11 were waited for; matrix products, arithmetic and copies ran while one was open for 0% of the time, Pallas kernels for 10%

profile of v9, /device:TPU:1, one launch (start us, length us, event | category | flops | bytes accessed | tf_op | source)
XLA Modules:
  0.0 80.4 jit_solution(5342162670552541620)
XLA Ops:
  0.6 0.0 copy-start
  0.7 0.1 add_bitcast_fusion.spot_ref
  0.7 1.9 %shard_map.86 = (f32[256,128]{1,0:T(8,128)S(1)}, f32[256,128]{1,0:T(8,128)S(1)}, f32[256,128]{1,0:T(8,128)S(1)}, f32[256,128]{1,0:T(8,128)S(1)}) custom-call(s32[1,4]{1,0:T(1,128)S(1)} %add_bitcast_fusion.spot_ref, f32[2,2,256,256]{3,2,1,0:T(8,128)} %obj_ref.11), custom_call_target="tpu_custom_call" | custom-call | tf_op jit(solution)/shard_map/pallas_call | solution.py:391
  2.6 3.3 %collective-permute-start.4 = (f32[256,128]{1,0:T(8,128)S(1)}, f32[256,128]{1,0:T(8,128)S(1)}, u32[]{:S(2)}, u32[]{:S(2)}) collective-permute-start(f32[256,128]{1,0:T(8,128)S(1)} %get-tuple-element.39), channel_id=1, source_target_pairs={{0,1},{1,0},{2,3},{3,2},{4,5},{5,4},{6,7},{7,6},{8,9},{9,8},{10,11... | collective-permute-start | bytes 393224 | tf_op jit(solution)/shard_map/ppermute | solution.py:363
  6.0 1.2 %collective-permute-start.5 = (f32[256,128]{1,0:T(8,128)S(1)}, f32[256,128]{1,0:T(8,128)S(1)}, u32[]{:S(2)}, u32[]{:S(2)}) collective-permute-start(f32[256,128]{1,0:T(8,128)S(1)} %get-tuple-element.40), channel_id=1, source_target_pairs={{0,16},{1,2},{2,1},{3,4},{4,3},{5,6},{6,5},{7,8},{8,7},{9,10},{10,... | collective-permute-start | bytes 393224 | tf_op jit(solution)/shard_map/ppermute | solution.py:363
  7.1 0.0 collective-permute-start
  7.1 0.0 copy-start.1
  7.1 2.1 %collective-permute-start.1 = (f32[256,128]{1,0:T(8,128)S(1)}, f32[256,128]{1,0:T(8,128)S(1)}, u32[]{:S(2)}, u32[]{:S(2)}) collective-permute-start(f32[256,128]{1,0:T(8,128)S(1)} %get-tuple-element.36), channel_id=1, source_target_pairs={{0,16},{1,2},{2,1},{3,4},{4,3},{5,6},{6,5},{7,8},{8,7},{9,10},{10,... | collective-permute-start | bytes 393224 | tf_op jit(solution)/shard_map/ppermute | solution.py:363
  9.2 0.0 collective-permute-done.4.cola_ref
  9.2 2.6 %collective-permute-done.5.colb_ref = f32[256,128]{1,0:T(8,128)S(1)} collective-permute-done((f32[256,128]{1,0:T(8,128)S(1)}, f32[256,128]{1,0:T(8,128)S(1)}, u32[]{:S(2)}, u32[]{:S(2)}) %collective-permute-start.5) | collective-permute-done | bytes 131104 | tf_op jit(solution)/shard_map/ppermute | solution.py:363
  11.9 0.0 copy-done
  11.9 0.6 shard_map.88
  12.4 0.1 collective-permute-start.6
  12.6 0.0 copy-start.2
  12.6 0.1 collective-permute-start.7
  12.7 0.0 collective-permute-done.cola_ref
  12.7 0.7 collective-permute-done.1.colb_ref
  13.3 0.6 shard_map.87
  13.9 2.5 %collective-permute-start.2 = (f32[6,64,128]{2,1,0:T(8,128)S(1)}, f32[6,64,128]{2,1,0:T(8,128)S(1)}, u32[]{:S(2)}, u32[]{:S(2)}) collective-permute-start(f32[6,64,128]{2,1,0:T(8,128)S(1)} %get-tuple-element.37), channel_id=1, source_target_pairs={{0,16},{1,17},{2,18},{3,19},{4,20},{5,21},{6,22},{7,23},{8,24},{9,... | collective-permute-start | bytes 589832 | tf_op jit(solution)/shard_map/ppermute | solution.py:363
  16.4 0.0 copy-start.4
  16.4 0.0 copy-start.5
  16.4 0.0 collective-permute-start.3
  17.1 0.0 copy-start.3
  17.1 2.3 %collective-permute-done.6.rowa_ref = f32[6,64,128]{2,1,0:T(8,128)S(1)} collective-permute-done((f32[6,64,128]{2,1,0:T(8,128)S(1)}, f32[6,64,128]{2,1,0:T(8,128)S(1)}, u32[]{:S(2)}, u32[]{:S(2)}) %collective-permute-start.6) | collective-permute-done | bytes 196640 | tf_op jit(solution)/shard_map/ppermute | solution.py:363
  19.4 0.0 collective-permute-done.7.rowb_ref
  19.4 0.0 copy-done.1
  19.4 0.0 copy-done.2
  19.4 0.0 copy-done.4
  19.4 0.0 copy-done.5
  19.4 2.2 %shard_map.89 = (f32[8,2,128,128]{3,2,1,0:T(8,128)S(1)}, f32[8,2,128,128]{3,2,1,0:T(8,128)S(1)}) custom-call(s32[1,8]{1,0:T(1,128)S(1)} %copy-done.4, s32[1,8]{1,0:T(1,128)S(1)} %copy-done.5, s32[1,4]{1,0:T(1,128)S(1)} %add_bitcast_fusion.spot_ref, f32[2,2,256,256]{3,2,1,0:T(8,128)S(1)} %copy-done, f32[256,128]{1,0:T(8,128)S(1)} %collective-permute-done.4.cola_ref, ...), custom_call_target="tpu_custom_call" | custom-call | tf_op jit(solution)/shard_map/pallas_call | solution.py:373
  21.6 1.4 %collective-permute-done.2.rowa_ref = f32[6,64,128]{2,1,0:T(8,128)S(1)} collective-permute-done((f32[6,64,128]{2,1,0:T(8,128)S(1)}, f32[6,64,128]{2,1,0:T(8,128)S(1)}, u32[]{:S(2)}, u32[]{:S(2)}) %collective-permute-start.2) | collective-permute-done | bytes 196640 | tf_op jit(solution)/shard_map/ppermute | solution.py:363
  23.0 0.0 collective-permute-done.3.rowb_ref
  23.0 0.0 copy-done.3
  23.0 5.9 %shard_map.90 = (f32[8,2,128,128]{3,2,1,0:T(8,128)S(1)}, f32[8,2,128,128]{3,2,1,0:T(8,128)S(1)}, f32[128,128]{1,0:T(8,128)S(1)}, f32[128,128]{1,0:T(8,128)S(1)}) custom-call(s32[1,8]{1,0:T(1,128)S(1)} %copy-done.4, s32[1,8]{1,0:T(1,128)S(1)} %copy-done.5, s32[1,4]{1,0:T(1,128)S(1)} %add_bitcast_fusion.spot_ref, s32[1,1]{1,0:T(1,128)S(6)} %copy.9.live_ref, ...), custom_call_target="tpu_custom_call" | custom-call | tf_op jit(solution)/shard_map/pallas_call | solution.py:373
  28.9 0.5 collective-permute-start.8
  29.4 0.9 %collective-permute-done.8 = f32[128,128]{1,0:T(8,128)S(1)} collective-permute-done((f32[128,128]{1,0:T(8,128)S(1)}, f32[128,128]{1,0:T(8,128)S(1)}, u32[]{:S(2)}, u32[]{:S(2)}) %collective-permute-start.8) | collective-permute-done | bytes 65568 | tf_op jit(solution)/shard_map/ppermute | solution.py:369
  30.3 2.0 %collective-permute-start.9 = (f32[128,128]{1,0:T(8,128)S(1)}, f32[128,128]{1,0:T(8,128)S(1)}, u32[]{:S(2)}, u32[]{:S(2)}) collective-permute-start(f32[128,128]{1,0:T(8,128)S(1)} %add.24), channel_id=1, source_target_pairs={{0,128},{1,5},{2,130},{3,7},{4,132},{5,1},{6,134},{7,3},{8,136},{9... | collective-permute-start | bytes 196616 | tf_op jit(solution)/shard_map/ppermute | solution.py:369
  32.3 2.3 %shard_map.91 = (f32[2,2,256,256]{3,2,1,0:T(8,128)S(1)}, f32[2,6,64,128]{3,2,1,0:T(8,128)S(1)}, f32[2,6,64,128]{3,2,1,0:T(8,128)S(1)}, f32[2,256,128]{2,1,0:T(8,128)S(1)}, f32[2,256,128]{2,1,0:T(8,128)S(1)}) custom-call(s32[1,8]{1,0:T(1,128)S(1)} %copy-done.4, s32[1,8]{1,0:T(1,128)S(1)} %copy-done.5, s32[1,4]{1,0:T(1,128)S(1)} %add_bitcast_fusion.spot_ref, ...), custom_call_target="tpu_custom_call" | custom-call | tf_op jit(solution)/shard_map/pallas_call | solution.py:373
  34.6 0.0 collective-permute-done.9
  34.6 3.4 %collective-permute-start.13 = (f32[2,6,64,128]{3,2,1,0:T(8,128)S(1)}, f32[2,6,64,128]{3,2,1,0:T(8,128)S(1)}, u32[]{:S(2)}, u32[]{:S(2)}) collective-permute-start(f32[2,6,64,128]{3,2,1,0:T(8,128)S(1)} %get-tuple-element.53), channel_id=1, source_target_pairs={{0,16},{1,17},{2,18},{3,19},{4,20},{5,21},{6,22},{7,23},{8,24},{9,... | collective-permute-start | bytes 1179656 | tf_op jit(solution)/shard_map/ppermute | solution.py:363
  38.0 0.8 collective-permute-start.14
  38.8 3.9 %collective-permute-start.10 = (f32[128,128]{1,0:T(8,128)S(1)}, f32[128,128]{1,0:T(8,128)S(1)}, u32[]{:S(2)}, u32[]{:S(2)}) collective-permute-start(f32[128,128]{1,0:T(8,128)S(1)} %add.25), channel_id=1, source_target_pairs={{0,4},{1,13},{2,6},{3,15},{4,0},{5,9},{6,2},{7,11},{8,12},{9,5},{1... | collective-permute-start | bytes 196616 | tf_op jit(solution)/shard_map/ppermute | solution.py:369
  42.7 1.7 %collective-permute-done.10 = f32[128,128]{1,0:T(8,128)S(1)} collective-permute-done((f32[128,128]{1,0:T(8,128)S(1)}, f32[128,128]{1,0:T(8,128)S(1)}, u32[]{:S(2)}, u32[]{:S(2)}) %collective-permute-start.10) | collective-permute-done | bytes 65568 | tf_op jit(solution)/shard_map/ppermute | solution.py:369
  44.4 4.6 %collective-permute-start.11 = (f32[128,128]{1,0:T(8,128)S(1)}, f32[128,128]{1,0:T(8,128)S(1)}, u32[]{:S(2)}, u32[]{:S(2)}) collective-permute-start(f32[128,128]{1,0:T(8,128)S(1)} %add.26), channel_id=1, source_target_pairs={{0,12},{1,129},{2,14},{3,131},{4,8},{5,133},{6,10},{7,135},{8,4},{... | collective-permute-start | bytes 196616 | tf_op jit(solution)/shard_map/ppermute | solution.py:369
  48.9 3.6 %collective-permute-done.11 = f32[128,128]{1,0:T(8,128)S(1)} collective-permute-done((f32[128,128]{1,0:T(8,128)S(1)}, f32[128,128]{1,0:T(8,128)S(1)}, u32[]{:S(2)}, u32[]{:S(2)}) %collective-permute-start.11) | collective-permute-done | bytes 65568 | tf_op jit(solution)/shard_map/ppermute | solution.py:369
  52.6 3.6 %collective-permute-start.12 = (f32[128,128]{1,0:T(8,128)S(1)}, f32[128,128]{1,0:T(8,128)S(1)}, u32[]{:S(2)}, u32[]{:S(2)}) collective-permute-start(f32[128,128]{1,0:T(8,128)S(1)} %add.27), channel_id=1, source_target_pairs={{0,130},{1,131},{2,128},{3,129},{4,134},{5,135},{6,132},{7,133},{8... | collective-permute-start | bytes 196616 | tf_op jit(solution)/shard_map/ppermute | solution.py:369
  56.2 1.7 %collective-permute-done.12 = f32[128,128]{1,0:T(8,128)S(1)} collective-permute-done((f32[128,128]{1,0:T(8,128)S(1)}, f32[128,128]{1,0:T(8,128)S(1)}, u32[]{:S(2)}, u32[]{:S(2)}) %collective-permute-start.12) | collective-permute-done | bytes 65568 | tf_op jit(solution)/shard_map/ppermute | solution.py:369
  57.8 0.0 collective-permute-done.13.rowa_ref
  57.9 0.0 collective-permute-done.14.rowb_ref
  57.9 0.1 collective-permute-start.15
  58.0 0.6 shard_map.92
  58.6 3.4 %collective-permute-done.15 = f32[128,128]{1,0:T(8,128)S(1)} collective-permute-done((f32[128,128]{1,0:T(8,128)S(1)}, f32[128,128]{1,0:T(8,128)S(1)}, u32[]{:S(2)}, u32[]{:S(2)}) %collective-permute-start.15) | collective-permute-done | bytes 65568 | tf_op jit(solution)/shard_map/ppermute | solution.py:369
  62.0 1.7 %collective-permute-start.18 = (f32[2,256,128]{2,1,0:T(8,128)S(1)}, f32[2,256,128]{2,1,0:T(8,128)S(1)}, u32[]{:S(2)}, u32[]{:S(2)}) collective-permute-start(f32[2,256,128]{2,1,0:T(8,128)S(1)} %get-tuple-element.63), channel_id=1, source_target_pairs={{0,1},{1,0},{2,3},{3,2},{4,5},{5,4},{6,7},{7,6},{8,9},{9,8},{10,11... | collective-permute-start | bytes 786440 | tf_op jit(solution)/shard_map/ppermute | solution.py:363
  63.7 0.9 %collective-permute-start.19 = (f32[2,256,128]{2,1,0:T(8,128)S(1)}, f32[2,256,128]{2,1,0:T(8,128)S(1)}, u32[]{:S(2)}, u32[]{:S(2)}) collective-permute-start(f32[2,256,128]{2,1,0:T(8,128)S(1)} %get-tuple-element.64), channel_id=1, source_target_pairs={{0,16},{1,2},{2,1},{3,4},{4,3},{5,6},{6,5},{7,8},{8,7},{9,10},{10,... | collective-permute-start | bytes 786440 | tf_op jit(solution)/shard_map/ppermute | solution.py:363
  64.6 2.1 %collective-permute-start.16 = (f32[128,128]{1,0:T(8,128)S(1)}, f32[128,128]{1,0:T(8,128)S(1)}, u32[]{:S(2)}, u32[]{:S(2)}) collective-permute-start(f32[128,128]{1,0:T(8,128)S(1)} %add.29), channel_id=1, source_target_pairs={{0,32},{1,97},{2,34},{3,99},{4,36},{5,101},{6,38},{7,103},{8,40},{... | collective-permute-start | bytes 196616 | tf_op jit(solution)/shard_map/ppermute | solution.py:369
  66.7 4.5 %collective-permute-done.16 = f32[128,128]{1,0:T(8,128)S(1)} collective-permute-done((f32[128,128]{1,0:T(8,128)S(1)}, f32[128,128]{1,0:T(8,128)S(1)}, u32[]{:S(2)}, u32[]{:S(2)}) %collective-permute-start.16) | collective-permute-done | bytes 65568 | tf_op jit(solution)/shard_map/ppermute | solution.py:369
  71.2 0.1 collective-permute-start.17
  71.3 3.4 %collective-permute-done.17 = f32[128,128]{1,0:T(8,128)S(1)} collective-permute-done((f32[128,128]{1,0:T(8,128)S(1)}, f32[128,128]{1,0:T(8,128)S(1)}, u32[]{:S(2)}, u32[]{:S(2)}) %collective-permute-start.17) | collective-permute-done | bytes 65568 | tf_op jit(solution)/shard_map/ppermute | solution.py:369
  74.7 0.0 collective-permute-done.18.cola_ref
  74.7 0.0 collective-permute-done.19.colb_ref
  74.7 2.7 %collective-permute-start.20 = (f32[128,128]{1,0:T(8,128)S(1)}, f32[128,128]{1,0:T(8,128)S(1)}, u32[]{:S(2)}, u32[]{:S(2)}) collective-permute-start(f32[128,128]{1,0:T(8,128)S(1)} %add.31.mine_ref), channel_id=1, source_target_pairs={{0,1},{1,0},{2,3},{3,2},{4,5},{5,4},{6,7},{7,6},{8,9},{9,8},{10,11... | collective-permute-start | bytes 196616 | tf_op jit(solution)/shard_map/ppermute | solution.py:369
  77.4 1.8 %shard_map.93 = f32[2,2,256,256]{3,2,1,0:T(8,128)} custom-call(s32[1,4]{1,0:T(1,128)S(1)} %add_bitcast_fusion.spot_ref, f32[2,2,256,256]{3,2,1,0:T(8,128)S(1)} %get-tuple-element.47.part_ref, f32[2,6,64,128]{3,2,1,0:T(8,128)S(1)} %collective-permute-done.13.rowa_ref, f32[2,6,64,128]{3,2,1,0:T(8,128)S(1)} %collective-permute-done.14.rowb_ref, ...), custom_call_target="tpu_custom_call" | custom-call | tf_op jit(solution)/shard_map/pallas_call | solution.py:373
  79.2 0.0 collective-permute-done.20.other_ref
  79.2 1.2 %shard_map.94 = f32[2,128,128]{2,1,0:T(8,128)} custom-call(s32[1,4]{1,0:T(1,128)S(1)} %add_bitcast_fusion.spot_ref, f32[2,128,128]{2,1,0:T(8,128)S(1)} %copy-done.2, f32[128,128]{1,0:T(8,128)S(1)} %add.31.mine_ref, f32[128,128]{1,0:T(8,128)S(1)} %collective-permute-done.20.other_ref), custom_call_target="tpu_custom_call" | custom-call | tf_op jit(solution)/shard_map/pallas_call | solution.py:373
  (9 shorter events, 0.1 us)
Async XLA Ops:
  0.6 11.2 %copy-start = (f32[2,2,256,256]{3,2,1,0:T(8,128)S(1)}, f32[2,2,256,256]{3,2,1,0:T(8,128)}, u32[]{:S(2)}) copy-start(f32[2,2,256,256]{3,2,1,0:T(8,128)} %obj_ref.11) | copy-start | bytes 3145732
  2.6 6.6 %collective-permute-start.4 = (f32[256,128]{1,0:T(8,128)S(1)}, f32[256,128]{1,0:T(8,128)S(1)}, u32[]{:S(2)}, u32[]{:S(2)}) collective-permute-start(f32[256,128]{1,0:T(8,128)S(1)} %get-tuple-element.39), channel_id=1, source_target_pairs={{0,1},{1,0},{2,3},{3,2},{4,5},{5,4},{6,7},{7,6},{8,9},{9,8},{10,11... | collective-permute-start | bytes 393224 | tf_op jit(solution)/shard_map/ppermute | solution.py:363
  6.0 5.9 %collective-permute-start.5 = (f32[256,128]{1,0:T(8,128)S(1)}, f32[256,128]{1,0:T(8,128)S(1)}, u32[]{:S(2)}, u32[]{:S(2)}) collective-permute-start(f32[256,128]{1,0:T(8,128)S(1)} %get-tuple-element.40), channel_id=1, source_target_pairs={{0,16},{1,2},{2,1},{3,4},{4,3},{5,6},{6,5},{7,8},{8,7},{9,10},{10,... | collective-permute-start | bytes 393224 | tf_op jit(solution)/shard_map/ppermute | solution.py:363
  7.1 5.5 %collective-permute-start = (f32[256,128]{1,0:T(8,128)S(1)}, f32[256,128]{1,0:T(8,128)S(1)}, u32[]{:S(2)}, u32[]{:S(2)}) collective-permute-start(f32[256,128]{1,0:T(8,128)S(1)} %get-tuple-element.35), channel_id=1, source_target_pairs={{0,1},{1,0},{2,3},{3,2},{4,5},{5,4},{6,7},{7,6},{8,9},{9,8},{10,11... | collective-permute-start | bytes 393224 | tf_op jit(solution)/shard_map/ppermute | solution.py:363
  7.1 12.2 %copy-start.1 = (bf16[4,2,256,256]{3,2,1,0:T(8,128)(2,1)S(1)}, bf16[4,2,256,256]{3,2,1,0:T(8,128)(2,1)}, u32[]{:S(2)}) copy-start(bf16[4,2,256,256]{3,2,1,0:T(8,128)(2,1)} %constant.11.clone.tabs_ref) | copy-start | bytes 3145732
  7.1 6.2 %collective-permute-start.1 = (f32[256,128]{1,0:T(8,128)S(1)}, f32[256,128]{1,0:T(8,128)S(1)}, u32[]{:S(2)}, u32[]{:S(2)}) collective-permute-start(f32[256,128]{1,0:T(8,128)S(1)} %get-tuple-element.36), channel_id=1, source_target_pairs={{0,16},{1,2},{2,1},{3,4},{4,3},{5,6},{6,5},{7,8},{8,7},{9,10},{10,... | collective-permute-start | bytes 393224 | tf_op jit(solution)/shard_map/ppermute | solution.py:363
  12.4 6.9 %collective-permute-start.6 = (f32[6,64,128]{2,1,0:T(8,128)S(1)}, f32[6,64,128]{2,1,0:T(8,128)S(1)}, u32[]{:S(2)}, u32[]{:S(2)}) collective-permute-start(f32[6,64,128]{2,1,0:T(8,128)S(1)} %get-tuple-element.41), channel_id=1, source_target_pairs={{0,16},{1,17},{2,18},{3,19},{4,20},{5,21},{6,22},{7,23},{8,24},{9,... | collective-permute-start | bytes 589832 | tf_op jit(solution)/shard_map/ppermute | solution.py:363
  12.6 6.8 %copy-start.2 = (f32[2,128,128]{2,1,0:T(8,128)S(1)}, f32[2,128,128]{2,1,0:T(8,128)}, u32[]{:S(2)}) copy-start(f32[2,128,128]{2,1,0:T(8,128)} %probe_ref.5) | copy-start | bytes 393220
  12.6 6.8 %collective-permute-start.7 = (f32[6,64,128]{2,1,0:T(8,128)S(1)}, f32[6,64,128]{2,1,0:T(8,128)S(1)}, u32[]{:S(2)}, u32[]{:S(2)}) collective-permute-start(f32[6,64,128]{2,1,0:T(8,128)S(1)} %get-tuple-element.42), channel_id=1, source_target_pairs={{0,1},{1,0},{2,3},{3,2},{4,5},{5,4},{6,7},{7,6},{8,9},{9,8},{10,11... | collective-permute-start | bytes 589832 | tf_op jit(solution)/shard_map/ppermute | solution.py:363
  13.9 9.1 %collective-permute-start.2 = (f32[6,64,128]{2,1,0:T(8,128)S(1)}, f32[6,64,128]{2,1,0:T(8,128)S(1)}, u32[]{:S(2)}, u32[]{:S(2)}) collective-permute-start(f32[6,64,128]{2,1,0:T(8,128)S(1)} %get-tuple-element.37), channel_id=1, source_target_pairs={{0,16},{1,17},{2,18},{3,19},{4,20},{5,21},{6,22},{7,23},{8,24},{9,... | collective-permute-start | bytes 589832 | tf_op jit(solution)/shard_map/ppermute | solution.py:363
  16.4 3.0 %copy-start.4 = (s32[1,8]{1,0:T(1,128)S(1)}, s32[1,8]{1,0:T(1,128)}, u32[]{:S(2)}) copy-start(s32[1,8]{1,0:T(1,128)} %row_ref.5) | copy-start | bytes 100
  16.4 3.0 %copy-start.5 = (s32[1,8]{1,0:T(1,128)S(1)}, s32[1,8]{1,0:T(1,128)}, u32[]{:S(2)}) copy-start(s32[1,8]{1,0:T(1,128)} %col_ref.5) | copy-start | bytes 100
  16.4 6.6 %collective-permute-start.3 = (f32[6,64,128]{2,1,0:T(8,128)S(1)}, f32[6,64,128]{2,1,0:T(8,128)S(1)}, u32[]{:S(2)}, u32[]{:S(2)}) collective-permute-start(f32[6,64,128]{2,1,0:T(8,128)S(1)} %get-tuple-element.38), channel_id=1, source_target_pairs={{0,1},{1,0},{2,3},{3,2},{4,5},{5,4},{6,7},{7,6},{8,9},{9,8},{10,11... | collective-permute-start | bytes 589832 | tf_op jit(solution)/shard_map/ppermute | solution.py:363
  17.1 6.0 %copy-start.3 = (f32[1,8,128,128]{3,2,1,0:T(8,128)S(1)}, f32[1,8,128,128]{3,2,1,0:T(8,128)}, u32[]{:S(2)}) copy-start(f32[1,8,128,128]{3,2,1,0:T(8,128)} %param.9) | copy-start | bytes 1572868
  28.9 1.4 %collective-permute-start.8 = (f32[128,128]{1,0:T(8,128)S(1)}, f32[128,128]{1,0:T(8,128)S(1)}, u32[]{:S(2)}, u32[]{:S(2)}) collective-permute-start(f32[128,128]{1,0:T(8,128)S(1)} %get-tuple-element.49), channel_id=1, source_target_pairs={{0,1},{1,0},{2,3},{3,2},{4,5},{5,4},{6,7},{7,6},{8,9},{9,8},{10,11... | collective-permute-start | bytes 196616 | tf_op jit(solution)/shard_map/ppermute | solution.py:369
  30.3 4.3 %collective-permute-start.9 = (f32[128,128]{1,0:T(8,128)S(1)}, f32[128,128]{1,0:T(8,128)S(1)}, u32[]{:S(2)}, u32[]{:S(2)}) collective-permute-start(f32[128,128]{1,0:T(8,128)S(1)} %add.24), channel_id=1, source_target_pairs={{0,128},{1,5},{2,130},{3,7},{4,132},{5,1},{6,134},{7,3},{8,136},{9... | collective-permute-start | bytes 196616 | tf_op jit(solution)/shard_map/ppermute | solution.py:369
  34.6 23.3 %collective-permute-start.13 = (f32[2,6,64,128]{3,2,1,0:T(8,128)S(1)}, f32[2,6,64,128]{3,2,1,0:T(8,128)S(1)}, u32[]{:S(2)}, u32[]{:S(2)}) collective-permute-start(f32[2,6,64,128]{3,2,1,0:T(8,128)S(1)} %get-tuple-element.53), channel_id=1, source_target_pairs={{0,16},{1,17},{2,18},{3,19},{4,20},{5,21},{6,22},{7,23},{8,24},{9,... | collective-permute-start | bytes 1179656 | tf_op jit(solution)/shard_map/ppermute | solution.py:363
  38.0 19.8 %collective-permute-start.14 = (f32[2,6,64,128]{3,2,1,0:T(8,128)S(1)}, f32[2,6,64,128]{3,2,1,0:T(8,128)S(1)}, u32[]{:S(2)}, u32[]{:S(2)}) collective-permute-start(f32[2,6,64,128]{3,2,1,0:T(8,128)S(1)} %get-tuple-element.54), channel_id=1, source_target_pairs={{0,1},{1,0},{2,3},{3,2},{4,5},{5,4},{6,7},{7,6},{8,9},{9,8},{10,11... | collective-permute-start | bytes 1179656 | tf_op jit(solution)/shard_map/ppermute | solution.py:363
  38.8 5.5 %collective-permute-start.10 = (f32[128,128]{1,0:T(8,128)S(1)}, f32[128,128]{1,0:T(8,128)S(1)}, u32[]{:S(2)}, u32[]{:S(2)}) collective-permute-start(f32[128,128]{1,0:T(8,128)S(1)} %add.25), channel_id=1, source_target_pairs={{0,4},{1,13},{2,6},{3,15},{4,0},{5,9},{6,2},{7,11},{8,12},{9,5},{1... | collective-permute-start | bytes 196616 | tf_op jit(solution)/shard_map/ppermute | solution.py:369
  44.4 8.2 %collective-permute-start.11 = (f32[128,128]{1,0:T(8,128)S(1)}, f32[128,128]{1,0:T(8,128)S(1)}, u32[]{:S(2)}, u32[]{:S(2)}) collective-permute-start(f32[128,128]{1,0:T(8,128)S(1)} %add.26), channel_id=1, source_target_pairs={{0,12},{1,129},{2,14},{3,131},{4,8},{5,133},{6,10},{7,135},{8,4},{... | collective-permute-start | bytes 196616 | tf_op jit(solution)/shard_map/ppermute | solution.py:369
  52.6 5.3 %collective-permute-start.12 = (f32[128,128]{1,0:T(8,128)S(1)}, f32[128,128]{1,0:T(8,128)S(1)}, u32[]{:S(2)}, u32[]{:S(2)}) collective-permute-start(f32[128,128]{1,0:T(8,128)S(1)} %add.27), channel_id=1, source_target_pairs={{0,130},{1,131},{2,128},{3,129},{4,134},{5,135},{6,132},{7,133},{8... | collective-permute-start | bytes 196616 | tf_op jit(solution)/shard_map/ppermute | solution.py:369
  57.9 4.1 %collective-permute-start.15 = (f32[128,128]{1,0:T(8,128)S(1)}, f32[128,128]{1,0:T(8,128)S(1)}, u32[]{:S(2)}, u32[]{:S(2)}) collective-permute-start(f32[128,128]{1,0:T(8,128)S(1)} %add.28), channel_id=1, source_target_pairs={{0,16},{1,33},{2,18},{3,35},{4,20},{5,37},{6,22},{7,39},{8,24},{9,... | collective-permute-start | bytes 196616 | tf_op jit(solution)/shard_map/ppermute | solution.py:369
  62.0 12.7 %collective-permute-start.18 = (f32[2,256,128]{2,1,0:T(8,128)S(1)}, f32[2,256,128]{2,1,0:T(8,128)S(1)}, u32[]{:S(2)}, u32[]{:S(2)}) collective-permute-start(f32[2,256,128]{2,1,0:T(8,128)S(1)} %get-tuple-element.63), channel_id=1, source_target_pairs={{0,1},{1,0},{2,3},{3,2},{4,5},{5,4},{6,7},{7,6},{8,9},{9,8},{10,11... | collective-permute-start | bytes 786440 | tf_op jit(solution)/shard_map/ppermute | solution.py:363
  63.7 11.0 %collective-permute-start.19 = (f32[2,256,128]{2,1,0:T(8,128)S(1)}, f32[2,256,128]{2,1,0:T(8,128)S(1)}, u32[]{:S(2)}, u32[]{:S(2)}) collective-permute-start(f32[2,256,128]{2,1,0:T(8,128)S(1)} %get-tuple-element.64), channel_id=1, source_target_pairs={{0,16},{1,2},{2,1},{3,4},{4,3},{5,6},{6,5},{7,8},{8,7},{9,10},{10,... | collective-permute-start | bytes 786440 | tf_op jit(solution)/shard_map/ppermute | solution.py:363
  64.6 6.6 %collective-permute-start.16 = (f32[128,128]{1,0:T(8,128)S(1)}, f32[128,128]{1,0:T(8,128)S(1)}, u32[]{:S(2)}, u32[]{:S(2)}) collective-permute-start(f32[128,128]{1,0:T(8,128)S(1)} %add.29), channel_id=1, source_target_pairs={{0,32},{1,97},{2,34},{3,99},{4,36},{5,101},{6,38},{7,103},{8,40},{... | collective-permute-start | bytes 196616 | tf_op jit(solution)/shard_map/ppermute | solution.py:369
  71.2 3.5 %collective-permute-start.17 = (f32[128,128]{1,0:T(8,128)S(1)}, f32[128,128]{1,0:T(8,128)S(1)}, u32[]{:S(2)}, u32[]{:S(2)}) collective-permute-start(f32[128,128]{1,0:T(8,128)S(1)} %add.30), channel_id=1, source_target_pairs={{0,96},{1,17},{2,98},{3,19},{4,100},{5,21},{6,102},{7,23},{8,104},... | collective-permute-start | bytes 196616 | tf_op jit(solution)/shard_map/ppermute | solution.py:369
  74.7 4.5 %collective-permute-start.20 = (f32[128,128]{1,0:T(8,128)S(1)}, f32[128,128]{1,0:T(8,128)S(1)}, u32[]{:S(2)}, u32[]{:S(2)}) collective-permute-start(f32[128,128]{1,0:T(8,128)S(1)} %add.31.mine_ref), channel_id=1, source_target_pairs={{0,1},{1,0},{2,3},{3,2},{4,5},{5,4},{6,7},{7,6},{8,9},{9,8},{10,11... | collective-permute-start | bytes 196616 | tf_op jit(solution)/shard_map/ppermute | solution.py:369

commit v10 on v9

--- a/solution.py
+++ b/solution.py
@@ -16,7 +16,7 @@
 LANES = 128
 BOTH = ("row", "col")
 GRANT = 16 * 1024 * 1024
-MASKS = ((128, 4), (4, 12), (12, 128), (130, 130), (16, 32), (32, 96), (96, 16))
+MASKS = ((128, 130), (4, 12), (12, 4), (130, 128), (16, 32), (32, 96), (96, 16))
 
 
 def split_table(table):
@@ -425,12 +425,12 @@
     mine, *rows = lax.optimization_barrier((mine, *rows))
     strips = call(fold_kernel, [array(2, *side)] * 2, (spot,), (left, right, *rows))
     mine = mine + swap(mine, MASKS[4])
-    mine, *strips = lax.optimization_barrier((mine, *strips))
     cols = meet(strips, 1)
-    for mask in MASKS[5:]:
-        mine = mine + swap(mine, mask)
+    mine = mine + swap(mine, MASKS[5])
     mine, *cols = lax.optimization_barrier((mine, *cols))
     (new,) = call(finish_kernel, (field,), (spot,), (part, *rows, *cols))
+    mine = mine + swap(mine, MASKS[6])
+    mine, new = lax.optimization_barrier((mine, new))
     other = swap(mine, (1, 1))
     count_all = count * lax.axis_size("row") * lax.axis_size("col")
     (new_probe,) = call(

time: 80.5 us -> 82.1 us (1.020)
  starting transfers between devices: 35.6 us -> 39.6 us
  waiting for transfers between devices: 26 us -> 23.5 us
    ppermute x9, starting transfers between devices: 19.5 us -> 25.5 us  [swap(): lax.ppermute(value, BOTH, [(i, i ^ masks[i % 2]) for i in range(count)])]
    ppermute x9, waiting for transfers between devices: 19.1 us -> 16.6 us  [swap(): lax.ppermute(value, BOTH, [(i, i ^ masks[i % 2]) for i in range(count)])]
    ppermute x12, starting transfers between devices: 16.1 us -> 14.2 us  [meet(): got.append(lax.ppermute(strip, BOTH, pairs))]
  transfers between devices with their start and end apart: 21 -> 21, of which waited for: 11 -> 12; matrix products, arithmetic and copies ran while one was open for 0% -> 0% of each run, Pallas kernels for 10% -> 9%
where the time goes in v10:
time: 82.1 us; the launch traced here: 82 us
  starting transfers between devices  39.6 us (48%)
  waiting for transfers between devices  23.5 us (29%)
  Pallas kernels  17.1 us (21%)
  between operations  1.54 us (2%)
    ppermute x9, starting transfers between devices, swap(): lax.ppermute(value, BOTH, [(i, i ^ masks[i % 2]) for i in range(count)])  25.5 us
    ppermute x9, waiting for transfers between devices, swap(): lax.ppermute(value, BOTH, [(i, i ^ masks[i % 2]) for i in range(count)])  16.6 us
    pallas_call x8, Pallas kernels, call(): pl.pallas_call(kernel, out_shape=tuple(out_shape), in_specs=smem(len(scal...  15.2 us
    ppermute x12, starting transfers between devices, meet(): got.append(lax.ppermute(strip, BOTH, pairs))  14.2 us
    ppermute x12, waiting for transfers between devices, meet(): got.append(lax.ppermute(strip, BOTH, pairs))  6.97 us
    pallas_call x1, Pallas kernels, on_device(): pl.pallas_call(pack_kernel, out_shape=tuple([array(*side)] * 4), in_specs...  1.89 us
  transfers between devices with their start and end apart: 21, of which 12 were waited for; matrix products, arithmetic and copies ran while one was open for 0% of the time, Pallas kernels for 9%

profile of v10, /device:TPU:1, one launch (start us, length us, event | category | flops | bytes accessed | tf_op | source)
XLA Modules:
  0.0 82.0 jit_solution(11764960671256643104)
XLA Ops:
  0.6 0.0 copy-start
  0.7 0.1 add_bitcast_fusion.spot_ref
  0.7 1.9 %shard_map.86 = (f32[256,128]{1,0:T(8,128)S(1)}, f32[256,128]{1,0:T(8,128)S(1)}, f32[256,128]{1,0:T(8,128)S(1)}, f32[256,128]{1,0:T(8,128)S(1)}) custom-call(s32[1,4]{1,0:T(1,128)S(1)} %add_bitcast_fusion.spot_ref, f32[2,2,256,256]{3,2,1,0:T(8,128)} %obj_ref.11), custom_call_target="tpu_custom_call" | custom-call | tf_op jit(solution)/shard_map/pallas_call | solution.py:391
  2.6 3.3 %collective-permute-start.4 = (f32[256,128]{1,0:T(8,128)S(1)}, f32[256,128]{1,0:T(8,128)S(1)}, u32[]{:S(2)}, u32[]{:S(2)}) collective-permute-start(f32[256,128]{1,0:T(8,128)S(1)} %get-tuple-element.38), channel_id=1, source_target_pairs={{0,1},{1,0},{2,3},{3,2},{4,5},{5,4},{6,7},{7,6},{8,9},{9,8},{10,11... | collective-permute-start | bytes 393224 | tf_op jit(solution)/shard_map/ppermute | solution.py:363
  6.0 1.2 %collective-permute-start.5 = (f32[256,128]{1,0:T(8,128)S(1)}, f32[256,128]{1,0:T(8,128)S(1)}, u32[]{:S(2)}, u32[]{:S(2)}) collective-permute-start(f32[256,128]{1,0:T(8,128)S(1)} %get-tuple-element.39), channel_id=1, source_target_pairs={{0,16},{1,2},{2,1},{3,4},{4,3},{5,6},{6,5},{7,8},{8,7},{9,10},{10,... | collective-permute-start | bytes 393224 | tf_op jit(solution)/shard_map/ppermute | solution.py:363
  7.1 0.0 collective-permute-start
  7.1 0.0 copy-start.1
  7.1 2.1 %collective-permute-start.1 = (f32[256,128]{1,0:T(8,128)S(1)}, f32[256,128]{1,0:T(8,128)S(1)}, u32[]{:S(2)}, u32[]{:S(2)}) collective-permute-start(f32[256,128]{1,0:T(8,128)S(1)} %get-tuple-element.35), channel_id=1, source_target_pairs={{0,16},{1,2},{2,1},{3,4},{4,3},{5,6},{6,5},{7,8},{8,7},{9,10},{10,... | collective-permute-start | bytes 393224 | tf_op jit(solution)/shard_map/ppermute | solution.py:363
  9.2 0.0 collective-permute-done.4.cola_ref
  9.2 2.6 %collective-permute-done.5.colb_ref = f32[256,128]{1,0:T(8,128)S(1)} collective-permute-done((f32[256,128]{1,0:T(8,128)S(1)}, f32[256,128]{1,0:T(8,128)S(1)}, u32[]{:S(2)}, u32[]{:S(2)}) %collective-permute-start.5) | collective-permute-done | bytes 131104 | tf_op jit(solution)/shard_map/ppermute | solution.py:363
  11.9 0.0 copy-done
  11.9 0.6 shard_map.88
  12.4 0.1 collective-permute-start.6
  12.6 0.0 copy-start.2
  12.6 0.1 collective-permute-start.7
  12.7 0.0 collective-permute-done.cola_ref
  12.7 0.7 collective-permute-done.1.colb_ref
  13.3 0.6 shard_map.87
  13.9 2.5 %collective-permute-start.2 = (f32[6,64,128]{2,1,0:T(8,128)S(1)}, f32[6,64,128]{2,1,0:T(8,128)S(1)}, u32[]{:S(2)}, u32[]{:S(2)}) collective-permute-start(f32[6,64,128]{2,1,0:T(8,128)S(1)} %get-tuple-element.36), channel_id=1, source_target_pairs={{0,16},{1,17},{2,18},{3,19},{4,20},{5,21},{6,22},{7,23},{8,24},{9,... | collective-permute-start | bytes 589832 | tf_op jit(solution)/shard_map/ppermute | solution.py:363
  16.4 0.0 copy-start.4
  16.4 0.0 copy-start.5
  16.4 0.0 collective-permute-start.3
  17.1 0.0 copy-start.3
  17.1 2.3 %collective-permute-done.6.rowa_ref = f32[6,64,128]{2,1,0:T(8,128)S(1)} collective-permute-done((f32[6,64,128]{2,1,0:T(8,128)S(1)}, f32[6,64,128]{2,1,0:T(8,128)S(1)}, u32[]{:S(2)}, u32[]{:S(2)}) %collective-permute-start.6) | collective-permute-done | bytes 196640 | tf_op jit(solution)/shard_map/ppermute | solution.py:363
  19.4 0.0 collective-permute-done.7.rowb_ref
  19.4 0.0 copy-done.1
  19.4 0.0 copy-done.2
  19.4 0.0 copy-done.4
  19.4 0.0 copy-done.5
  19.4 2.2 %shard_map.89 = (f32[8,2,128,128]{3,2,1,0:T(8,128)S(1)}, f32[8,2,128,128]{3,2,1,0:T(8,128)S(1)}) custom-call(s32[1,8]{1,0:T(1,128)S(1)} %copy-done.4, s32[1,8]{1,0:T(1,128)S(1)} %copy-done.5, s32[1,4]{1,0:T(1,128)S(1)} %add_bitcast_fusion.spot_ref, f32[2,2,256,256]{3,2,1,0:T(8,128)S(1)} %copy-done, f32[256,128]{1,0:T(8,128)S(1)} %collective-permute-done.4.cola_ref, ...), custom_call_target="tpu_custom_call" | custom-call | tf_op jit(solution)/shard_map/pallas_call | solution.py:373
  21.7 1.4 %collective-permute-done.2.rowa_ref = f32[6,64,128]{2,1,0:T(8,128)S(1)} collective-permute-done((f32[6,64,128]{2,1,0:T(8,128)S(1)}, f32[6,64,128]{2,1,0:T(8,128)S(1)}, u32[]{:S(2)}, u32[]{:S(2)}) %collective-permute-start.2) | collective-permute-done | bytes 196640 | tf_op jit(solution)/shard_map/ppermute | solution.py:363
  23.0 0.0 collective-permute-done.3.rowb_ref
  23.0 0.0 copy-done.3
  23.0 5.9 %shard_map.90 = (f32[8,2,128,128]{3,2,1,0:T(8,128)S(1)}, f32[8,2,128,128]{3,2,1,0:T(8,128)S(1)}, f32[128,128]{1,0:T(8,128)S(1)}, f32[128,128]{1,0:T(8,128)S(1)}) custom-call(s32[1,8]{1,0:T(1,128)S(1)} %copy-done.4, s32[1,8]{1,0:T(1,128)S(1)} %copy-done.5, s32[1,4]{1,0:T(1,128)S(1)} %add_bitcast_fusion.spot_ref, s32[1,1]{1,0:T(1,128)S(6)} %copy.9.live_ref, ...), custom_call_target="tpu_custom_call" | custom-call | tf_op jit(solution)/shard_map/pallas_call | solution.py:373
  28.9 0.5 collective-permute-start.8
  29.4 0.9 %collective-permute-done.8 = f32[128,128]{1,0:T(8,128)S(1)} collective-permute-done((f32[128,128]{1,0:T(8,128)S(1)}, f32[128,128]{1,0:T(8,128)S(1)}, u32[]{:S(2)}, u32[]{:S(2)}) %collective-permute-start.8) | collective-permute-done | bytes 65568 | tf_op jit(solution)/shard_map/ppermute | solution.py:369
  30.3 8.1 %collective-permute-start.9 = (f32[128,128]{1,0:T(8,128)S(1)}, f32[128,128]{1,0:T(8,128)S(1)}, u32[]{:S(2)}, u32[]{:S(2)}) collective-permute-start(f32[128,128]{1,0:T(8,128)S(1)} %add.24), channel_id=1, source_target_pairs={{0,128},{1,131},{2,130},{3,129},{4,132},{5,135},{6,134},{7,133},{8... | collective-permute-start | bytes 196616 | tf_op jit(solution)/shard_map/ppermute | solution.py:369
  38.4 2.3 %shard_map.91 = (f32[2,2,256,256]{3,2,1,0:T(8,128)S(1)}, f32[2,6,64,128]{3,2,1,0:T(8,128)S(1)}, f32[2,6,64,128]{3,2,1,0:T(8,128)S(1)}, f32[2,256,128]{2,1,0:T(8,128)S(1)}, f32[2,256,128]{2,1,0:T(8,128)S(1)}) custom-call(s32[1,8]{1,0:T(1,128)S(1)} %copy-done.4, s32[1,8]{1,0:T(1,128)S(1)} %copy-done.5, s32[1,4]{1,0:T(1,128)S(1)} %add_bitcast_fusion.spot_ref, ...), custom_call_target="tpu_custom_call" | custom-call | tf_op jit(solution)/shard_map/pallas_call | solution.py:373
  40.7 0.0 collective-permute-done.9
  40.7 0.1 collective-permute-start.13
  40.8 0.1 collective-permute-start.14
  40.9 1.8 %collective-permute-start.10 = (f32[128,128]{1,0:T(8,128)S(1)}, f32[128,128]{1,0:T(8,128)S(1)}, u32[]{:S(2)}, u32[]{:S(2)}) collective-permute-start(f32[128,128]{1,0:T(8,128)S(1)} %add.25), channel_id=1, source_target_pairs={{0,4},{1,13},{2,6},{3,15},{4,0},{5,9},{6,2},{7,11},{8,12},{9,5},{1... | collective-permute-start | bytes 196616 | tf_op jit(solution)/shard_map/ppermute | solution.py:369
  42.7 2.6 %collective-permute-done.10 = f32[128,128]{1,0:T(8,128)S(1)} collective-permute-done((f32[128,128]{1,0:T(8,128)S(1)}, f32[128,128]{1,0:T(8,128)S(1)}, u32[]{:S(2)}, u32[]{:S(2)}) %collective-permute-start.10) | collective-permute-done | bytes 65568 | tf_op jit(solution)/shard_map/ppermute | solution.py:369
  45.4 0.4 collective-permute-start.11
  45.7 2.9 %collective-permute-done.11 = f32[128,128]{1,0:T(8,128)S(1)} collective-permute-done((f32[128,128]{1,0:T(8,128)S(1)}, f32[128,128]{1,0:T(8,128)S(1)}, u32[]{:S(2)}, u32[]{:S(2)}) %collective-permute-start.11) | collective-permute-done | bytes 65568 | tf_op jit(solution)/shard_map/ppermute | solution.py:369
  48.6 4.4 %collective-permute-start.12 = (f32[128,128]{1,0:T(8,128)S(1)}, f32[128,128]{1,0:T(8,128)S(1)}, u32[]{:S(2)}, u32[]{:S(2)}) collective-permute-start(f32[128,128]{1,0:T(8,128)S(1)} %add.27), channel_id=1, source_target_pairs={{0,130},{1,129},{2,128},{3,131},{4,134},{5,133},{6,132},{7,135},{8... | collective-permute-start | bytes 196616 | tf_op jit(solution)/shard_map/ppermute | solution.py:369
  53.0 1.7 %collective-permute-done.12 = f32[128,128]{1,0:T(8,128)S(1)} collective-permute-done((f32[128,128]{1,0:T(8,128)S(1)}, f32[128,128]{1,0:T(8,128)S(1)}, u32[]{:S(2)}, u32[]{:S(2)}) %collective-permute-start.12) | collective-permute-done | bytes 65568 | tf_op jit(solution)/shard_map/ppermute | solution.py:369
  54.7 0.0 collective-permute-done.13.rowa_ref
  54.7 0.0 collective-permute-done.14.rowb_ref
  54.7 0.6 shard_map.92
  55.4 4.6 %collective-permute-start.17 = (f32[2,256,128]{2,1,0:T(8,128)S(1)}, f32[2,256,128]{2,1,0:T(8,128)S(1)}, u32[]{:S(2)}, u32[]{:S(2)}) collective-permute-start(f32[2,256,128]{2,1,0:T(8,128)S(1)} %get-tuple-element.58), channel_id=1, source_target_pairs={{0,1},{1,0},{2,3},{3,2},{4,5},{5,4},{6,7},{7,6},{8,9},{9,8},{10,11... | collective-permute-start | bytes 786440 | tf_op jit(solution)/shard_map/ppermute | solution.py:363
  60.0 0.1 collective-permute-start.18
  60.1 0.7 collective-permute-start.15
  60.8 4.0 %collective-permute-done.15 = f32[128,128]{1,0:T(8,128)S(1)} collective-permute-done((f32[128,128]{1,0:T(8,128)S(1)}, f32[128,128]{1,0:T(8,128)S(1)}, u32[]{:S(2)}, u32[]{:S(2)}) %collective-permute-start.15) | collective-permute-done | bytes 65568 | tf_op jit(solution)/shard_map/ppermute | solution.py:369
  64.8 2.8 %collective-permute-start.16 = (f32[128,128]{1,0:T(8,128)S(1)}, f32[128,128]{1,0:T(8,128)S(1)}, u32[]{:S(2)}, u32[]{:S(2)}) collective-permute-start(f32[128,128]{1,0:T(8,128)S(1)} %add.29), channel_id=1, source_target_pairs={{0,32},{1,97},{2,34},{3,99},{4,36},{5,101},{6,38},{7,103},{8,40},{... | collective-permute-start | bytes 196616 | tf_op jit(solution)/shard_map/ppermute | solution.py:369
  67.6 2.5 %collective-permute-done.16 = f32[128,128]{1,0:T(8,128)S(1)} collective-permute-done((f32[128,128]{1,0:T(8,128)S(1)}, f32[128,128]{1,0:T(8,128)S(1)}, u32[]{:S(2)}, u32[]{:S(2)}) %collective-permute-start.16) | collective-permute-done | bytes 65568 | tf_op jit(solution)/shard_map/ppermute | solution.py:369
  70.1 0.0 collective-permute-done.17.cola_ref
  70.1 0.0 collective-permute-done.18.colb_ref
  70.2 0.4 collective-permute-start.19
  70.5 1.8 %shard_map.93 = f32[2,2,256,256]{3,2,1,0:T(8,128)} custom-call(s32[1,4]{1,0:T(1,128)S(1)} %add_bitcast_fusion.spot_ref, f32[2,2,256,256]{3,2,1,0:T(8,128)S(1)} %get-tuple-element.61.part_ref, f32[2,6,64,128]{3,2,1,0:T(8,128)S(1)} %collective-permute-done.13.rowa_ref, f32[2,6,64,128]{3,2,1,0:T(8,128)S(1)} %collective-permute-done.14.rowb_ref, ...), custom_call_target="tpu_custom_call" | custom-call | tf_op jit(solution)/shard_map/pallas_call | solution.py:373
  72.3 1.1 %collective-permute-done.19 = f32[128,128]{1,0:T(8,128)S(1)} collective-permute-done((f32[128,128]{1,0:T(8,128)S(1)}, f32[128,128]{1,0:T(8,128)S(1)}, u32[]{:S(2)}, u32[]{:S(2)}) %collective-permute-start.19) | collective-permute-done | bytes 65568 | tf_op jit(solution)/shard_map/ppermute | solution.py:369
  73.4 6.5 %collective-permute-start.20 = (f32[128,128]{1,0:T(8,128)S(1)}, f32[128,128]{1,0:T(8,128)S(1)}, u32[]{:S(2)}, u32[]{:S(2)}) collective-permute-start(f32[128,128]{1,0:T(8,128)S(1)} %add.31.mine_ref), channel_id=1, source_target_pairs={{0,1},{1,0},{2,3},{3,2},{4,5},{5,4},{6,7},{7,6},{8,9},{9,8},{10,11... | collective-permute-start | bytes 196616 | tf_op jit(solution)/shard_map/ppermute | solution.py:369
  79.8 0.9 %collective-permute-done.20.other_ref = f32[128,128]{1,0:T(8,128)S(1)} collective-permute-done((f32[128,128]{1,0:T(8,128)S(1)}, f32[128,128]{1,0:T(8,128)S(1)}, u32[]{:S(2)}, u32[]{:S(2)}) %collective-permute-start.20) | collective-permute-done | bytes 65568 | tf_op jit(solution)/shard_map/ppermute | solution.py:369
  80.7 1.2 %shard_map.94 = f32[2,128,128]{2,1,0:T(8,128)} custom-call(s32[1,4]{1,0:T(1,128)S(1)} %add_bitcast_fusion.spot_ref, f32[2,128,128]{2,1,0:T(8,128)S(1)} %copy-done.2, f32[128,128]{1,0:T(8,128)S(1)} %add.31.mine_ref, f32[128,128]{1,0:T(8,128)S(1)} %collective-permute-done.20.other_ref), custom_call_target="tpu_custom_call" | custom-call | tf_op jit(solution)/shard_map/pallas_call | solution.py:373
  (9 shorter events, 0.1 us)
Async XLA Ops:
  0.6 11.2 %copy-start = (f32[2,2,256,256]{3,2,1,0:T(8,128)S(1)}, f32[2,2,256,256]{3,2,1,0:T(8,128)}, u32[]{:S(2)}) copy-start(f32[2,2,256,256]{3,2,1,0:T(8,128)} %obj_ref.11) | copy-start | bytes 3145732
  2.6 6.6 %collective-permute-start.4 = (f32[256,128]{1,0:T(8,128)S(1)}, f32[256,128]{1,0:T(8,128)S(1)}, u32[]{:S(2)}, u32[]{:S(2)}) collective-permute-start(f32[256,128]{1,0:T(8,128)S(1)} %get-tuple-element.38), channel_id=1, source_target_pairs={{0,1},{1,0},{2,3},{3,2},{4,5},{5,4},{6,7},{7,6},{8,9},{9,8},{10,11... | collective-permute-start | bytes 393224 | tf_op jit(solution)/shard_map/ppermute | solution.py:363
  6.0 5.9 %collective-permute-start.5 = (f32[256,128]{1,0:T(8,128)S(1)}, f32[256,128]{1,0:T(8,128)S(1)}, u32[]{:S(2)}, u32[]{:S(2)}) collective-permute-start(f32[256,128]{1,0:T(8,128)S(1)} %get-tuple-element.39), channel_id=1, source_target_pairs={{0,16},{1,2},{2,1},{3,4},{4,3},{5,6},{6,5},{7,8},{8,7},{9,10},{10,... | collective-permute-start | bytes 393224 | tf_op jit(solution)/shard_map/ppermute | solution.py:363
  7.1 5.5 %collective-permute-start = (f32[256,128]{1,0:T(8,128)S(1)}, f32[256,128]{1,0:T(8,128)S(1)}, u32[]{:S(2)}, u32[]{:S(2)}) collective-permute-start(f32[256,128]{1,0:T(8,128)S(1)} %get-tuple-element.34), channel_id=1, source_target_pairs={{0,1},{1,0},{2,3},{3,2},{4,5},{5,4},{6,7},{7,6},{8,9},{9,8},{10,11... | collective-permute-start | bytes 393224 | tf_op jit(solution)/shard_map/ppermute | solution.py:363
  7.1 12.2 %copy-start.1 = (bf16[4,2,256,256]{3,2,1,0:T(8,128)(2,1)S(1)}, bf16[4,2,256,256]{3,2,1,0:T(8,128)(2,1)}, u32[]{:S(2)}) copy-start(bf16[4,2,256,256]{3,2,1,0:T(8,128)(2,1)} %constant.11.clone.tabs_ref) | copy-start | bytes 3145732
  7.1 6.2 %collective-permute-start.1 = (f32[256,128]{1,0:T(8,128)S(1)}, f32[256,128]{1,0:T(8,128)S(1)}, u32[]{:S(2)}, u32[]{:S(2)}) collective-permute-start(f32[256,128]{1,0:T(8,128)S(1)} %get-tuple-element.35), channel_id=1, source_target_pairs={{0,16},{1,2},{2,1},{3,4},{4,3},{5,6},{6,5},{7,8},{8,7},{9,10},{10,... | collective-permute-start | bytes 393224 | tf_op jit(solution)/shard_map/ppermute | solution.py:363
  12.4 6.9 %collective-permute-start.6 = (f32[6,64,128]{2,1,0:T(8,128)S(1)}, f32[6,64,128]{2,1,0:T(8,128)S(1)}, u32[]{:S(2)}, u32[]{:S(2)}) collective-permute-start(f32[6,64,128]{2,1,0:T(8,128)S(1)} %get-tuple-element.40), channel_id=1, source_target_pairs={{0,16},{1,17},{2,18},{3,19},{4,20},{5,21},{6,22},{7,23},{8,24},{9,... | collective-permute-start | bytes 589832 | tf_op jit(solution)/shard_map/ppermute | solution.py:363
  12.6 6.8 %copy-start.2 = (f32[2,128,128]{2,1,0:T(8,128)S(1)}, f32[2,128,128]{2,1,0:T(8,128)}, u32[]{:S(2)}) copy-start(f32[2,128,128]{2,1,0:T(8,128)} %probe_ref.5) | copy-start | bytes 393220
  12.6 6.8 %collective-permute-start.7 = (f32[6,64,128]{2,1,0:T(8,128)S(1)}, f32[6,64,128]{2,1,0:T(8,128)S(1)}, u32[]{:S(2)}, u32[]{:S(2)}) collective-permute-start(f32[6,64,128]{2,1,0:T(8,128)S(1)} %get-tuple-element.41), channel_id=1, source_target_pairs={{0,1},{1,0},{2,3},{3,2},{4,5},{5,4},{6,7},{7,6},{8,9},{9,8},{10,11... | collective-permute-start | bytes 589832 | tf_op jit(solution)/shard_map/ppermute | solution.py:363
  13.9 9.1 %collective-permute-start.2 = (f32[6,64,128]{2,1,0:T(8,128)S(1)}, f32[6,64,128]{2,1,0:T(8,128)S(1)}, u32[]{:S(2)}, u32[]{:S(2)}) collective-permute-start(f32[6,64,128]{2,1,0:T(8,128)S(1)} %get-tuple-element.36), channel_id=1, source_target_pairs={{0,16},{1,17},{2,18},{3,19},{4,20},{5,21},{6,22},{7,23},{8,24},{9,... | collective-permute-start | bytes 589832 | tf_op jit(solution)/shard_map/ppermute | solution.py:363
  16.4 3.0 %copy-start.4 = (s32[1,8]{1,0:T(1,128)S(1)}, s32[1,8]{1,0:T(1,128)}, u32[]{:S(2)}) copy-start(s32[1,8]{1,0:T(1,128)} %row_ref.5) | copy-start | bytes 100
  16.4 3.0 %copy-start.5 = (s32[1,8]{1,0:T(1,128)S(1)}, s32[1,8]{1,0:T(1,128)}, u32[]{:S(2)}) copy-start(s32[1,8]{1,0:T(1,128)} %col_ref.5) | copy-start | bytes 100
  16.4 6.6 %collective-permute-start.3 = (f32[6,64,128]{2,1,0:T(8,128)S(1)}, f32[6,64,128]{2,1,0:T(8,128)S(1)}, u32[]{:S(2)}, u32[]{:S(2)}) collective-permute-start(f32[6,64,128]{2,1,0:T(8,128)S(1)} %get-tuple-element.37), channel_id=1, source_target_pairs={{0,1},{1,0},{2,3},{3,2},{4,5},{5,4},{6,7},{7,6},{8,9},{9,8},{10,11... | collective-permute-start | bytes 589832 | tf_op jit(solution)/shard_map/ppermute | solution.py:363
  17.1 6.0 %copy-start.3 = (f32[1,8,128,128]{3,2,1,0:T(8,128)S(1)}, f32[1,8,128,128]{3,2,1,0:T(8,128)}, u32[]{:S(2)}) copy-start(f32[1,8,128,128]{3,2,1,0:T(8,128)} %param.9) | copy-start | bytes 1572868
  28.9 1.4 %collective-permute-start.8 = (f32[128,128]{1,0:T(8,128)S(1)}, f32[128,128]{1,0:T(8,128)S(1)}, u32[]{:S(2)}, u32[]{:S(2)}) collective-permute-start(f32[128,128]{1,0:T(8,128)S(1)} %get-tuple-element.45), channel_id=1, source_target_pairs={{0,1},{1,0},{2,3},{3,2},{4,5},{5,4},{6,7},{7,6},{8,9},{9,8},{10,11... | collective-permute-start | bytes 196616 | tf_op jit(solution)/shard_map/ppermute | solution.py:369
  30.3 10.4 %collective-permute-start.9 = (f32[128,128]{1,0:T(8,128)S(1)}, f32[128,128]{1,0:T(8,128)S(1)}, u32[]{:S(2)}, u32[]{:S(2)}) collective-permute-start(f32[128,128]{1,0:T(8,128)S(1)} %add.24), channel_id=1, source_target_pairs={{0,128},{1,131},{2,130},{3,129},{4,132},{5,135},{6,134},{7,133},{8... | collective-permute-start | bytes 196616 | tf_op jit(solution)/shard_map/ppermute | solution.py:369
  40.7 14.0 %collective-permute-start.13 = (f32[2,6,64,128]{3,2,1,0:T(8,128)S(1)}, f32[2,6,64,128]{3,2,1,0:T(8,128)S(1)}, u32[]{:S(2)}, u32[]{:S(2)}) collective-permute-start(f32[2,6,64,128]{3,2,1,0:T(8,128)S(1)} %get-tuple-element.51), channel_id=1, source_target_pairs={{0,16},{1,17},{2,18},{3,19},{4,20},{5,21},{6,22},{7,23},{8,24},{9,... | collective-permute-start | bytes 1179656 | tf_op jit(solution)/shard_map/ppermute | solution.py:363
  40.8 13.9 %collective-permute-start.14 = (f32[2,6,64,128]{3,2,1,0:T(8,128)S(1)}, f32[2,6,64,128]{3,2,1,0:T(8,128)S(1)}, u32[]{:S(2)}, u32[]{:S(2)}) collective-permute-start(f32[2,6,64,128]{3,2,1,0:T(8,128)S(1)} %get-tuple-element.52), channel_id=1, source_target_pairs={{0,1},{1,0},{2,3},{3,2},{4,5},{5,4},{6,7},{7,6},{8,9},{9,8},{10,11... | collective-permute-start | bytes 1179656 | tf_op jit(solution)/shard_map/ppermute | solution.py:363
  40.9 4.4 %collective-permute-start.10 = (f32[128,128]{1,0:T(8,128)S(1)}, f32[128,128]{1,0:T(8,128)S(1)}, u32[]{:S(2)}, u32[]{:S(2)}) collective-permute-start(f32[128,128]{1,0:T(8,128)S(1)} %add.25), channel_id=1, source_target_pairs={{0,4},{1,13},{2,6},{3,15},{4,0},{5,9},{6,2},{7,11},{8,12},{9,5},{1... | collective-permute-start | bytes 196616 | tf_op jit(solution)/shard_map/ppermute | solution.py:369
  45.4 3.2 %collective-permute-start.11 = (f32[128,128]{1,0:T(8,128)S(1)}, f32[128,128]{1,0:T(8,128)S(1)}, u32[]{:S(2)}, u32[]{:S(2)}) collective-permute-start(f32[128,128]{1,0:T(8,128)S(1)} %add.26), channel_id=1, source_target_pairs={{0,12},{1,5},{2,14},{3,7},{4,8},{5,1},{6,10},{7,3},{8,4},{9,13},{1... | collective-permute-start | bytes 196616 | tf_op jit(solution)/shard_map/ppermute | solution.py:369
  48.6 6.1 %collective-permute-start.12 = (f32[128,128]{1,0:T(8,128)S(1)}, f32[128,128]{1,0:T(8,128)S(1)}, u32[]{:S(2)}, u32[]{:S(2)}) collective-permute-start(f32[128,128]{1,0:T(8,128)S(1)} %add.27), channel_id=1, source_target_pairs={{0,130},{1,129},{2,128},{3,131},{4,134},{5,133},{6,132},{7,135},{8... | collective-permute-start | bytes 196616 | tf_op jit(solution)/shard_map/ppermute | solution.py:369
  55.4 14.8 %collective-permute-start.17 = (f32[2,256,128]{2,1,0:T(8,128)S(1)}, f32[2,256,128]{2,1,0:T(8,128)S(1)}, u32[]{:S(2)}, u32[]{:S(2)}) collective-permute-start(f32[2,256,128]{2,1,0:T(8,128)S(1)} %get-tuple-element.58), channel_id=1, source_target_pairs={{0,1},{1,0},{2,3},{3,2},{4,5},{5,4},{6,7},{7,6},{8,9},{9,8},{10,11... | collective-permute-start | bytes 786440 | tf_op jit(solution)/shard_map/ppermute | solution.py:363
  60.0 10.2 %collective-permute-start.18 = (f32[2,256,128]{2,1,0:T(8,128)S(1)}, f32[2,256,128]{2,1,0:T(8,128)S(1)}, u32[]{:S(2)}, u32[]{:S(2)}) collective-permute-start(f32[2,256,128]{2,1,0:T(8,128)S(1)} %get-tuple-element.59), channel_id=1, source_target_pairs={{0,16},{1,2},{2,1},{3,4},{4,3},{5,6},{6,5},{7,8},{8,7},{9,10},{10,... | collective-permute-start | bytes 786440 | tf_op jit(solution)/shard_map/ppermute | solution.py:363
  60.1 4.7 %collective-permute-start.15 = (f32[128,128]{1,0:T(8,128)S(1)}, f32[128,128]{1,0:T(8,128)S(1)}, u32[]{:S(2)}, u32[]{:S(2)}) collective-permute-start(f32[128,128]{1,0:T(8,128)S(1)} %add.28), channel_id=1, source_target_pairs={{0,16},{1,33},{2,18},{3,35},{4,20},{5,37},{6,22},{7,39},{8,24},{9,... | collective-permute-start | bytes 196616 | tf_op jit(solution)/shard_map/ppermute | solution.py:369
  64.8 5.3 %collective-permute-start.16 = (f32[128,128]{1,0:T(8,128)S(1)}, f32[128,128]{1,0:T(8,128)S(1)}, u32[]{:S(2)}, u32[]{:S(2)}) collective-permute-start(f32[128,128]{1,0:T(8,128)S(1)} %add.29), channel_id=1, source_target_pairs={{0,32},{1,97},{2,34},{3,99},{4,36},{5,101},{6,38},{7,103},{8,40},{... | collective-permute-start | bytes 196616 | tf_op jit(solution)/shard_map/ppermute | solution.py:369
  70.2 3.2 %collective-permute-start.19 = (f32[128,128]{1,0:T(8,128)S(1)}, f32[128,128]{1,0:T(8,128)S(1)}, u32[]{:S(2)}, u32[]{:S(2)}) collective-permute-start(f32[128,128]{1,0:T(8,128)S(1)} %add.30), channel_id=1, source_target_pairs={{0,96},{1,17},{2,98},{3,19},{4,100},{5,21},{6,102},{7,23},{8,104},... | collective-permute-start | bytes 196616 | tf_op jit(solution)/shard_map/ppermute | solution.py:369
  73.4 7.4 %collective-permute-start.20 = (f32[128,128]{1,0:T(8,128)S(1)}, f32[128,128]{1,0:T(8,128)S(1)}, u32[]{:S(2)}, u32[]{:S(2)}) collective-permute-start(f32[128,128]{1,0:T(8,128)S(1)} %add.31.mine_ref), channel_id=1, source_target_pairs={{0,1},{1,0},{2,3},{3,2},{4,5},{5,4},{6,7},{7,6},{8,9},{9,8},{10,11... | collective-permute-start | bytes 196616 | tf_op jit(solution)/shard_map/ppermute | solution.py:369

commit v11 on v9

--- a/solution.py
+++ b/solution.py
@@ -16,7 +16,7 @@
 LANES = 128
 BOTH = ("row", "col")
 GRANT = 16 * 1024 * 1024
-MASKS = ((128, 4), (4, 12), (12, 128), (130, 130), (16, 32), (32, 96), (96, 16))
+MASKS = ((128, 130), (16, 32), (32, 96), (96, 16), (4, 12), (12, 4), (130, 128))
 
 
 def split_table(table):
@@ -68,10 +68,11 @@
     )
 
 
-def columns(piece_ref, first):
-    half = LANES // 2
-    left = jnp.where(first, piece_ref[0, :, :LANES], pltpu.roll(piece_ref[1, :, :LANES], half, 1))
-    right = jnp.where(first, pltpu.roll(piece_ref[0, :, LANES:], half, 1), piece_ref[1, :, LANES:])
+def pack_sides(real, imag):
+    half = LANES // 2
+    first = lax.broadcasted_iota(jnp.int32, real[0].shape, 1) < half
+    left = jnp.where(first, real[0], pltpu.roll(imag[0], half, 1))
+    right = jnp.where(first, pltpu.roll(real[1], half, 1), imag[1])
     return left, right
 
 
@@ -88,31 +89,43 @@
 
 def pack_kernel(spot_ref, obj_ref, *refs):
     *outs, held, sems = refs
-    first = lax.broadcasted_iota(jnp.int32, (held.shape[2], LANES), 1) < LANES // 2
-    copies = [pltpu.make_async_copy(obj_ref.at[p], held.at[p], sems.at[p]) for p in range(2)]
-    for copy in copies:
-        copy.start()
-    for piece in range(2):
-        copies[piece].wait()
-        left, right = columns(held.at[piece], first)
-        outs[2 * piece][...] = pick(spot_ref, 1, right, left)
-        outs[2 * piece + 1][...] = pick(spot_ref, 1, left, right)
-
-
-def rows_kernel(spot_ref, obj_ref, cola_ref, colb_ref, rowa_ref, rowb_ref, *, piece):
-    half = LANES // 2
-    low, high = slice(0, half), slice(obj_ref.shape[2] - half, obj_ref.shape[2])
-    for part in range(2):
-        for block in range(2):
-            cols = slice(block * LANES, (block + 1) * LANES)
-            top, bottom = obj_ref[piece, part, low, cols], obj_ref[piece, part, high, cols]
-            rowa_ref[2 * part + block] = pick(spot_ref, 0, bottom, top)
-            rowb_ref[2 * part + block] = pick(spot_ref, 0, top, bottom)
-    tops = beside(spot_ref, 1, cola_ref[low], colb_ref[low])
-    bottoms = beside(spot_ref, 1, cola_ref[high], colb_ref[high])
-    for place, top, bottom in zip((4, 5), tops, bottoms):
-        rowa_ref[place] = pick(spot_ref, 0, bottom, top)
-        rowb_ref[place] = pick(spot_ref, 0, top, bottom)
+    half = LANES // 2
+    tile = obj_ref.shape[2]
+    copies = []
+    for piece in range(2):
+        for end, start in enumerate((0, tile - half)):
+            copies.append(
+                pltpu.make_async_copy(
+                    obj_ref.at[piece, :, pl.ds(start, half)], held.at[piece, end], sems.at[piece, end]
+                )
+            )
+            copies[-1].start()
+    for piece in range(2):
+        for copy in copies[2 * piece : 2 * piece + 2]:
+            copy.wait()
+        for part in range(2):
+            for block in range(2):
+                cols = slice(block * LANES, (block + 1) * LANES)
+                top, bottom = held[piece, 0, part, :, cols], held[piece, 1, part, :, cols]
+                outs[2 * piece][2 * part + block] = pick(spot_ref, 0, bottom, top)
+                outs[2 * piece + 1][2 * part + block] = pick(spot_ref, 0, top, bottom)
+
+
+def columns_kernel(spot_ref, obj_ref, rowa_ref, rowb_ref, cola_ref, colb_ref, *, piece):
+    half = LANES // 2
+    tile = obj_ref.shape[2]
+    ends = [beside(spot_ref, 0, rowa_ref[place], rowb_ref[place]) for place in range(4)]
+    for start, size in ((0, half), (half, tile), (half + tile, half)):
+        values = []
+        for place in range(4):
+            cols = slice((place % 2) * LANES, (place % 2 + 1) * LANES)
+            if size == tile:
+                values.append(obj_ref[piece, place // 2, :, cols])
+            else:
+                values.append(ends[place][0 if start == 0 else 1])
+        left, right = pack_sides(values[:2], values[2:])
+        cola_ref[start : start + size] = pick(spot_ref, 1, right, left)
+        colb_ref[start : start + size] = pick(spot_ref, 1, left, right)
 
 
 def grow(ext, spot_ref, piece_ref, cola_ref, colb_ref, rowa_ref, rowb_ref):
@@ -120,17 +133,14 @@
     tile = piece_ref.shape[1]
     sides = beside(spot_ref, 1, cola_ref[...], colb_ref[...])
     for part in range(2):
-        for block in range(4):
-            place = 2 * part + block - 1 if block in (1, 2) else 4 + block // 3
+        for block in range(2):
+            place = 2 * part + block
             top, bottom = beside(spot_ref, 0, rowa_ref[place], rowb_ref[place])
-            if block in (1, 2):
-                middle = piece_ref[part, :, (block - 1) * LANES : block * LANES]
-            else:
-                middle = sides[block // 3]
-            for strip, start in ((top, 0), (middle, half), (bottom, half + tile)):
-                if (block == 0 and part == 0) or (block == 3 and part == 1):
-                    strip = pltpu.roll(strip, half, 1)
-                ext[part, block, start : start + strip.shape[0]] = strip
+            ext[part, 1 + block, :half] = top
+            ext[part, 1 + block, half : half + tile] = piece_ref[part, :, block * LANES : (block + 1) * LANES]
+            ext[part, 1 + block, half + tile :] = bottom
+        ext[part, 0] = pltpu.roll(sides[0], half, 1) if part == 0 else sides[0]
+        ext[part, 3] = sides[1] if part == 0 else pltpu.roll(sides[1], half, 1)
 
 
 def place_window(row_ref, col_ref, slot):
@@ -235,7 +245,7 @@
 
 def place_kernel(
     row_ref, col_ref, spot_ref, obj_ref, probe_ref, down_ref, second_ref,
-    new_ref, rowa_ref, rowb_ref, left_ref, right_ref,
+    new_ref, cola_ref, colb_ref, top_ref, bottom_ref,
     grad,
 ):
     width = probe_ref.shape[1]
@@ -261,45 +271,44 @@
         return 0
 
     lax.fori_loop(0, row_ref.shape[1], deposit, 0)
-    first = lax.broadcasted_iota(jnp.int32, (tile + width, LANES), 1) < half
     for piece in range(2):
         for part in range(2):
             for block in range(2):
                 cols = slice(block * LANES, (block + 1) * LANES)
-                top = grad[piece, part, 1 + block, :half]
-                bottom = grad[piece, part, 1 + block, half + tile :]
-                rowa_ref[piece, 2 * part + block] = pick(spot_ref, 0, bottom, top)
-                rowb_ref[piece, 2 * part + block] = pick(spot_ref, 0, top, bottom)
+                top_ref[piece, 2 * part + block] = grad[piece, part, 1 + block, :half]
+                bottom_ref[piece, 2 * part + block] = grad[piece, part, 1 + block, half + tile :]
                 new_ref[piece, part, :, cols] = (
                     obj_ref[piece, part, :, cols]
                     - STEP_OBJECT * grad[piece, part, 1 + block, half : half + tile]
                 )
+        first = lax.broadcasted_iota(jnp.int32, (tile + width, LANES), 1) < half
         left = jnp.where(first, pltpu.roll(grad[piece, 0, 0], half, 1), grad[piece, 1, 0])
         right = jnp.where(first, grad[piece, 0, 3], pltpu.roll(grad[piece, 1, 3], half, 1))
-        for place, strip, ref in ((4, left, left_ref), (5, right, right_ref)):
-            top, bottom = strip[:half], strip[half + tile :]
-            rowa_ref[piece, place] = pick(spot_ref, 0, bottom, top)
-            rowb_ref[piece, place] = pick(spot_ref, 0, top, bottom)
-            ref[piece] = strip[half : half + tile]
-
-
-def fold_kernel(spot_ref, left_ref, right_ref, rowa_ref, rowb_ref, cola_ref, colb_ref):
-    half = LANES // 2
-    tile = left_ref.shape[1]
-    for piece in range(2):
-        sides = []
-        for ref, place in ((left_ref, 4), (right_ref, 5)):
-            top, bottom = beside(spot_ref, 0, rowa_ref[piece, place], rowb_ref[piece, place])
-            sides.append(
-                (
-                    ref[piece, :half] + top,
-                    ref[piece, half : tile - half],
-                    ref[piece, tile - half :] + bottom,
-                )
-            )
-        for left, right, rows in zip(*sides, (slice(0, half), slice(half, tile - half), slice(tile - half, tile))):
-            cola_ref[piece, rows] = pick(spot_ref, 1, right, left)
-            colb_ref[piece, rows] = pick(spot_ref, 1, left, right)
+        cola_ref[piece] = pick(spot_ref, 1, right, left)
+        colb_ref[piece] = pick(spot_ref, 1, left, right)
+
+
+def unpack_side(strip, part, block):
+    half = LANES // 2
+    first = lax.broadcasted_iota(jnp.int32, strip.shape, 1) < half
+    if block != part:
+        strip = pltpu.roll(strip, half, 1)
+    return jnp.where(first == (block == 0), strip, 0.0)
+
+
+def fold_kernel(spot_ref, top_ref, bottom_ref, cola_ref, colb_ref, rowa_ref, rowb_ref):
+    half = LANES // 2
+    last = cola_ref.shape[1] - half
+    for piece in range(2):
+        uppers = beside(spot_ref, 1, cola_ref[piece, :half], colb_ref[piece, :half])
+        lowers = beside(spot_ref, 1, cola_ref[piece, last:], colb_ref[piece, last:])
+        for part in range(2):
+            for block in range(2):
+                place = 2 * part + block
+                top = top_ref[piece, place] + unpack_side(uppers[block], part, block)
+                bottom = bottom_ref[piece, place] + unpack_side(lowers[block], part, block)
+                rowa_ref[piece, place] = pick(spot_ref, 0, bottom, top)
+                rowb_ref[piece, place] = pick(spot_ref, 0, top, bottom)
 
 
 def finish_kernel(
@@ -307,18 +316,15 @@
 ):
     tile = part_ref.shape[2]
     half = LANES // 2
-    first = lax.broadcasted_iota(jnp.int32, (half, LANES), 1) < half
     for piece in range(2):
         for start in range(0, tile, half):
             rows = slice(start, start + half)
-            sides = beside(spot_ref, 1, cola_ref[piece, rows], colb_ref[piece, rows])
+            strips = slice(half + start, half + start + half)
+            sides = beside(spot_ref, 1, cola_ref[piece, strips], colb_ref[piece, strips])
             for part in range(2):
                 for block in range(2):
                     cols = slice(block * LANES, (block + 1) * LANES)
-                    total = sides[block]
-                    if block != part:
-                        total = pltpu.roll(total, half, 1)
-                    total = jnp.where(first == (block == 0), total, 0.0)
+                    total = unpack_side(sides[block], part, block)
                     place = 2 * part + block
                     ends = beside(spot_ref, 0, rowa_ref[piece, place], rowb_ref[piece, place])
                     if start == 0:
@@ -382,26 +388,26 @@
     width = probe.shape[1]
     half = width // 2
     count = offset_row.shape[1]
-    side, edge, plane = (tile, LANES), (6, half, LANES), (width, width)
+    side, edge, plane = (tile + width, LANES), (4, half, LANES), (width, width)
     field, fields = array(2, 2, tile, tile), array(count, 2, width, width)
     place = [lax.axis_index(axis) for axis in BOTH] + [lax.axis_size(axis) for axis in BOTH]
     spot = jnp.stack([jnp.asarray(entry, jnp.int32) for entry in place]).reshape(1, 4)
     tabs = jnp.asarray(make_tables(width))
     grown = pltpu.VMEM((2, 4, tile + width, LANES), jnp.float32)
     packed = pl.pallas_call(
-        pack_kernel, out_shape=tuple([array(*side)] * 4),
+        pack_kernel, out_shape=tuple([array(*edge)] * 4),
         in_specs=smem(1) + [pl.BlockSpec(memory_space=pltpu.HBM)], out_specs=tuple(vmem(4)),
-        scratch_shapes=[pltpu.VMEM(object_field.shape, jnp.float32), pltpu.SemaphoreType.DMA((2,))],
+        scratch_shapes=[pltpu.VMEM((2, 2, 2, half, tile), jnp.float32), pltpu.SemaphoreType.DMA((2, 2))],
         compiler_params=pltpu.CompilerParams(vmem_limit_bytes=GRANT),
     )(spot, pltpu.with_memory_space_constraint(object_field, pltpu.HBM))
     halos = []
-    cols = [meet(packed[2 * piece : 2 * piece + 2], 1) for piece in range(2)]
+    rows = [meet(packed[2 * piece : 2 * piece + 2], 0) for piece in range(2)]
     for piece in range(2):
         strips = call(
-            functools.partial(rows_kernel, piece=piece), [array(*edge)] * 2,
-            (spot,), (object_field, *cols[piece]),
+            functools.partial(columns_kernel, piece=piece), [array(*side)] * 2,
+            (spot,), (object_field, *rows[piece]),
         )
-        halos.append((*cols[piece], *meet(strips, 0)))
+        halos.append((*meet(strips, 1), *rows[piece]))
     win, mid = call(
         functools.partial(first_kernel, group=2), [fields] * 2, (offset_row, offset_col, spot),
         (object_field, *halos[0], probe, tabs), (grown,),
@@ -411,25 +417,25 @@
         (object_field, *halos[1], win, mid, intensity[0], tabs),
         (grown, pltpu.VMEM((2, *plane), jnp.float32)),
     )
-    part, *strips, left, right = call(
-        place_kernel, [field] + [array(2, *edge)] * 2 + [array(2, *side)] * 2,
+    part, *strips, top, bottom = call(
+        place_kernel, [field] + [array(2, *side)] * 2 + [array(2, *edge)] * 2,
         (offset_row, offset_col, spot), (object_field, probe, down, grad),
         (pltpu.VMEM((2, 2, 4, tile + width, LANES), jnp.float32),),
     )
     mine = mine + swap(send, (1, 1))
     mine = mine + swap(mine, MASKS[0])
     mine, *strips = lax.optimization_barrier((mine, *strips))
-    rows = meet(strips, 0)
+    cols = meet(strips, 1)
     for mask in MASKS[1:4]:
         mine = mine + swap(mine, mask)
-    mine, *rows = lax.optimization_barrier((mine, *rows))
-    strips = call(fold_kernel, [array(2, *side)] * 2, (spot,), (left, right, *rows))
+    mine, *cols = lax.optimization_barrier((mine, *cols))
+    strips = call(fold_kernel, [array(2, *edge)] * 2, (spot,), (top, bottom, *cols))
     mine = mine + swap(mine, MASKS[4])
     mine, *strips = lax.optimization_barrier((mine, *strips))
-    cols = meet(strips, 1)
+    rows = meet(strips, 0)
     for mask in MASKS[5:]:
         mine = mine + swap(mine, mask)
-    mine, *cols = lax.optimization_barrier((mine, *cols))
+    mine, *rows = lax.optimization_barrier((mine, *rows))
     (new,) = call(finish_kernel, (field,), (spot,), (part, *rows, *cols))
     other = swap(mine, (1, 1))
     count_all = count * lax.axis_size("row") * lax.axis_size("col")

time: 80.5 us -> 82.9 us (1.030)
  starting transfers between devices: 35.6 us -> 38.9 us
  waiting for transfers between devices: 26 us -> 24.8 us
    ppermute x12, starting transfers between devices: 16.1 us -> 21.7 us  [meet(): got.append(lax.ppermute(strip, BOTH, pairs))]
    ppermute x9, starting transfers between devices: 19.5 us -> 17.3 us  [swap(): lax.ppermute(value, BOTH, [(i, i ^ masks[i % 2]) for i in range(count)])]
    ppermute x12, waiting for transfers between devices: 6.98 us -> 5.32 us  [meet(): got.append(lax.ppermute(strip, BOTH, pairs))]
  transfers between devices with their start and end apart: 21 -> 21, of which waited for: 11 -> 8; matrix products, arithmetic and copies ran while one was open for 0% -> 0% of each run, Pallas kernels for 10% -> 10%
where the time goes in v11:
time: 82.9 us; the launch traced here: 82.7 us
  starting transfers between devices  38.9 us (47%)
  waiting for transfers between devices  24.8 us (30%)
  Pallas kernels  17.2 us (21%)
  between operations  1.51 us (2%)
    ppermute x12, starting transfers between devices, meet(): got.append(lax.ppermute(strip, BOTH, pairs))  21.7 us
    ppermute x9, waiting for transfers between devices, swap(): lax.ppermute(value, BOTH, [(i, i ^ masks[i % 2]) for i in range(count)])  19.5 us
    ppermute x9, starting transfers between devices, swap(): lax.ppermute(value, BOTH, [(i, i ^ masks[i % 2]) for i in range(count)])  17.3 us
    pallas_call x8, Pallas kernels, call(): pl.pallas_call(kernel, out_shape=tuple(out_shape), in_specs=smem(len(scal...  15.5 us
    ppermute x12, waiting for transfers between devices, meet(): got.append(lax.ppermute(strip, BOTH, pairs))  5.32 us
    pallas_call x1, Pallas kernels, on_device(): pl.pallas_call(pack_kernel, out_shape=tuple([array(*edge)] * 4), in_specs...  1.7 us
  transfers between devices with their start and end apart: 21, of which 8 were waited for; matrix products, arithmetic and copies ran while one was open for 0% of the time, Pallas kernels for 10%

profile of v11, /device:TPU:1, one launch (start us, length us, event | category | flops | bytes accessed | tf_op | source)
XLA Modules:
  0.0 82.7 jit_solution(16427371623515165284)
XLA Ops:
  0.6 0.0 copy-start
  0.7 0.1 add_bitcast_fusion.spot_ref
  0.7 1.7 %shard_map.86 = (f32[4,64,128]{2,1,0:T(8,128)S(1)}, f32[4,64,128]{2,1,0:T(8,128)S(1)}, f32[4,64,128]{2,1,0:T(8,128)S(1)}, f32[4,64,128]{2,1,0:T(8,128)S(1)}) custom-call(s32[1,4]{1,0:T(1,128)S(1)} %add_bitcast_fusion.spot_ref, f32[2,2,256,256]{3,2,1,0:T(8,128)} %obj_ref.11), custom_call_target="tpu_custom_call" | custom-call | tf_op jit(solution)/shard_map/pallas_call | solution.py:397
  2.4 2.6 %collective-permute-start.4 = (f32[4,64,128]{2,1,0:T(8,128)S(1)}, f32[4,64,128]{2,1,0:T(8,128)S(1)}, u32[]{:S(2)}, u32[]{:S(2)}) collective-permute-start(f32[4,64,128]{2,1,0:T(8,128)S(1)} %get-tuple-element.39), channel_id=1, source_target_pairs={{0,16},{1,17},{2,18},{3,19},{4,20},{5,21},{6,22},{7,23},{8,24},{9,... | collective-permute-start | bytes 393224 | tf_op jit(solution)/shard_map/ppermute | solution.py:369
  5.0 1.0 %collective-permute-start.5 = (f32[4,64,128]{2,1,0:T(8,128)S(1)}, f32[4,64,128]{2,1,0:T(8,128)S(1)}, u32[]{:S(2)}, u32[]{:S(2)}) collective-permute-start(f32[4,64,128]{2,1,0:T(8,128)S(1)} %get-tuple-element.40), channel_id=1, source_target_pairs={{0,1},{1,0},{2,3},{3,2},{4,5},{5,4},{6,7},{7,6},{8,9},{9,8},{10,11... | collective-permute-start | bytes 393224 | tf_op jit(solution)/shard_map/ppermute | solution.py:369
  6.0 2.3 %collective-permute-start = (f32[4,64,128]{2,1,0:T(8,128)S(1)}, f32[4,64,128]{2,1,0:T(8,128)S(1)}, u32[]{:S(2)}, u32[]{:S(2)}) collective-permute-start(f32[4,64,128]{2,1,0:T(8,128)S(1)} %get-tuple-element.35), channel_id=1, source_target_pairs={{0,16},{1,17},{2,18},{3,19},{4,20},{5,21},{6,22},{7,23},{8,24},{9,... | collective-permute-start | bytes 393224 | tf_op jit(solution)/shard_map/ppermute | solution.py:369
  8.3 0.0 copy-start.1
  8.3 1.5 %collective-permute-start.1 = (f32[4,64,128]{2,1,0:T(8,128)S(1)}, f32[4,64,128]{2,1,0:T(8,128)S(1)}, u32[]{:S(2)}, u32[]{:S(2)}) collective-permute-start(f32[4,64,128]{2,1,0:T(8,128)S(1)} %get-tuple-element.36), channel_id=1, source_target_pairs={{0,1},{1,0},{2,3},{3,2},{4,5},{5,4},{6,7},{7,6},{8,9},{9,8},{10,11... | collective-permute-start | bytes 393224 | tf_op jit(solution)/shard_map/ppermute | solution.py:369
  9.8 0.0 collective-permute-done.4.rowa_ref
  9.8 0.0 collective-permute-done.5.rowb_ref
  9.8 0.0 copy-done
  9.8 0.7 shard_map.88
  10.5 1.9 %collective-permute-start.6 = (f32[384,128]{1,0:T(8,128)S(1)}, f32[384,128]{1,0:T(8,128)S(1)}, u32[]{:S(2)}, u32[]{:S(2)}) collective-permute-start(f32[384,128]{1,0:T(8,128)S(1)} %get-tuple-element.41), channel_id=1, source_target_pairs={{0,1},{1,0},{2,3},{3,2},{4,5},{5,4},{6,7},{7,6},{8,9},{9,8},{10,11... | collective-permute-start | bytes 589832 | tf_op jit(solution)/shard_map/ppermute | solution.py:369
  12.4 0.0 copy-start.2
  12.4 1.5 %collective-permute-start.7 = (f32[384,128]{1,0:T(8,128)S(1)}, f32[384,128]{1,0:T(8,128)S(1)}, u32[]{:S(2)}, u32[]{:S(2)}) collective-permute-start(f32[384,128]{1,0:T(8,128)S(1)} %get-tuple-element.42), channel_id=1, source_target_pairs={{0,16},{1,2},{2,1},{3,4},{4,3},{5,6},{6,5},{7,8},{8,7},{9,10},{10,... | collective-permute-start | bytes 589832 | tf_op jit(solution)/shard_map/ppermute | solution.py:369
  13.9 0.0 collective-permute-done.rowa_ref
  13.9 0.0 collective-permute-done.1.rowb_ref
  13.9 0.7 shard_map.87
  14.7 1.0 %collective-permute-start.2 = (f32[384,128]{1,0:T(8,128)S(1)}, f32[384,128]{1,0:T(8,128)S(1)}, u32[]{:S(2)}, u32[]{:S(2)}) collective-permute-start(f32[384,128]{1,0:T(8,128)S(1)} %get-tuple-element.37), channel_id=1, source_target_pairs={{0,1},{1,0},{2,3},{3,2},{4,5},{5,4},{6,7},{7,6},{8,9},{9,8},{10,11... | collective-permute-start | bytes 589832 | tf_op jit(solution)/shard_map/ppermute | solution.py:369
  15.7 0.0 copy-start.4
  15.7 0.0 copy-start.5
  15.7 0.9 %collective-permute-start.3 = (f32[384,128]{1,0:T(8,128)S(1)}, f32[384,128]{1,0:T(8,128)S(1)}, u32[]{:S(2)}, u32[]{:S(2)}) collective-permute-start(f32[384,128]{1,0:T(8,128)S(1)} %get-tuple-element.38), channel_id=1, source_target_pairs={{0,16},{1,2},{2,1},{3,4},{4,3},{5,6},{6,5},{7,8},{8,7},{9,10},{10,... | collective-permute-start | bytes 589832 | tf_op jit(solution)/shard_map/ppermute | solution.py:369
  17.3 0.0 copy-start.3
  17.3 0.0 collective-permute-done.6.cola_ref
  17.3 5.3 %collective-permute-done.7.colb_ref = f32[384,128]{1,0:T(8,128)S(1)} collective-permute-done((f32[384,128]{1,0:T(8,128)S(1)}, f32[384,128]{1,0:T(8,128)S(1)}, u32[]{:S(2)}, u32[]{:S(2)}) %collective-permute-start.7) | collective-permute-done | bytes 196640 | tf_op jit(solution)/shard_map/ppermute | solution.py:369
  22.6 0.0 copy-done.1
  22.6 0.0 copy-done.2
  22.6 0.0 copy-done.4
  22.6 0.0 copy-done.5
  22.6 2.2 %shard_map.89 = (f32[8,2,128,128]{3,2,1,0:T(8,128)S(1)}, f32[8,2,128,128]{3,2,1,0:T(8,128)S(1)}) custom-call(s32[1,8]{1,0:T(1,128)S(1)} %copy-done.4, s32[1,8]{1,0:T(1,128)S(1)} %copy-done.5, s32[1,4]{1,0:T(1,128)S(1)} %add_bitcast_fusion.spot_ref, f32[2,2,256,256]{3,2,1,0:T(8,128)S(1)} %copy-done, f32[384,128]{1,0:T(8,128)S(1)} %collective-permute-done.6.cola_ref, ...), custom_call_target="tpu_custom_call" | custom-call | tf_op jit(solution)/shard_map/pallas_call | solution.py:379
  24.9 0.0 collective-permute-done.2.cola_ref
  24.9 0.0 collective-permute-done.3.colb_ref
  24.9 0.0 copy-done.3
  24.9 5.9 %shard_map.90 = (f32[8,2,128,128]{3,2,1,0:T(8,128)S(1)}, f32[8,2,128,128]{3,2,1,0:T(8,128)S(1)}, f32[128,128]{1,0:T(8,128)S(1)}, f32[128,128]{1,0:T(8,128)S(1)}) custom-call(s32[1,8]{1,0:T(1,128)S(1)} %copy-done.4, s32[1,8]{1,0:T(1,128)S(1)} %copy-done.5, s32[1,4]{1,0:T(1,128)S(1)} %add_bitcast_fusion.spot_ref, s32[1,1]{1,0:T(1,128)S(6)} %copy.9.live_ref, ...), custom_call_target="tpu_custom_call" | custom-call | tf_op jit(solution)/shard_map/pallas_call | solution.py:379
  30.8 0.1 collective-permute-start.8
  30.9 1.2 %collective-permute-done.8 = f32[128,128]{1,0:T(8,128)S(1)} collective-permute-done((f32[128,128]{1,0:T(8,128)S(1)}, f32[128,128]{1,0:T(8,128)S(1)}, u32[]{:S(2)}, u32[]{:S(2)}) %collective-permute-start.8) | collective-permute-done | bytes 65568 | tf_op jit(solution)/shard_map/ppermute | solution.py:375
  32.1 6.5 %collective-permute-start.9 = (f32[128,128]{1,0:T(8,128)S(1)}, f32[128,128]{1,0:T(8,128)S(1)}, u32[]{:S(2)}, u32[]{:S(2)}) collective-permute-start(f32[128,128]{1,0:T(8,128)S(1)} %add.24), channel_id=1, source_target_pairs={{0,128},{1,131},{2,130},{3,129},{4,132},{5,135},{6,134},{7,133},{8... | collective-permute-start | bytes 196616 | tf_op jit(solution)/shard_map/ppermute | solution.py:375
  38.7 2.3 %shard_map.91 = (f32[2,2,256,256]{3,2,1,0:T(8,128)S(1)}, f32[2,384,128]{2,1,0:T(8,128)S(1)}, f32[2,384,128]{2,1,0:T(8,128)S(1)}, f32[2,4,64,128]{3,2,1,0:T(8,128)S(1)}, f32[2,4,64,128]{3,2,1,0:T(8,128)S(1)}) custom-call(s32[1,8]{1,0:T(1,128)S(1)} %copy-done.4, s32[1,8]{1,0:T(1,128)S(1)} %copy-done.5, s32[1,4]{1,0:T(1,128)S(1)} %add_bitcast_fusion.spot_ref, ...), custom_call_target="tpu_custom_call" | custom-call | tf_op jit(solution)/shard_map/pallas_call | solution.py:379
  41.0 0.0 collective-permute-done.9
  41.0 0.1 collective-permute-start.13
  41.1 1.8 %collective-permute-start.14 = (f32[2,384,128]{2,1,0:T(8,128)S(1)}, f32[2,384,128]{2,1,0:T(8,128)S(1)}, u32[]{:S(2)}, u32[]{:S(2)}) collective-permute-start(f32[2,384,128]{2,1,0:T(8,128)S(1)} %get-tuple-element.54), channel_id=1, source_target_pairs={{0,16},{1,2},{2,1},{3,4},{4,3},{5,6},{6,5},{7,8},{8,7},{9,10},{10,... | collective-permute-start | bytes 1179656 | tf_op jit(solution)/shard_map/ppermute | solution.py:369
  42.9 0.0 collective-permute-start.10
  42.9 4.7 %collective-permute-done.10 = f32[128,128]{1,0:T(8,128)S(1)} collective-permute-done((f32[128,128]{1,0:T(8,128)S(1)}, f32[128,128]{1,0:T(8,128)S(1)}, u32[]{:S(2)}, u32[]{:S(2)}) %collective-permute-start.10) | collective-permute-done | bytes 65568 | tf_op jit(solution)/shard_map/ppermute | solution.py:375
  47.6 3.5 %collective-permute-start.11 = (f32[128,128]{1,0:T(8,128)S(1)}, f32[128,128]{1,0:T(8,128)S(1)}, u32[]{:S(2)}, u32[]{:S(2)}) collective-permute-start(f32[128,128]{1,0:T(8,128)S(1)} %add.26), channel_id=1, source_target_pairs={{0,32},{1,97},{2,34},{3,99},{4,36},{5,101},{6,38},{7,103},{8,40},{... | collective-permute-start | bytes 196616 | tf_op jit(solution)/shard_map/ppermute | solution.py:375
  51.2 2.2 %collective-permute-done.11 = f32[128,128]{1,0:T(8,128)S(1)} collective-permute-done((f32[128,128]{1,0:T(8,128)S(1)}, f32[128,128]{1,0:T(8,128)S(1)}, u32[]{:S(2)}, u32[]{:S(2)}) %collective-permute-start.11) | collective-permute-done | bytes 65568 | tf_op jit(solution)/shard_map/ppermute | solution.py:375
  53.3 1.9 %collective-permute-start.12 = (f32[128,128]{1,0:T(8,128)S(1)}, f32[128,128]{1,0:T(8,128)S(1)}, u32[]{:S(2)}, u32[]{:S(2)}) collective-permute-start(f32[128,128]{1,0:T(8,128)S(1)} %add.27), channel_id=1, source_target_pairs={{0,96},{1,17},{2,98},{3,19},{4,100},{5,21},{6,102},{7,23},{8,104},... | collective-permute-start | bytes 196616 | tf_op jit(solution)/shard_map/ppermute | solution.py:375
  55.3 1.7 %collective-permute-done.12 = f32[128,128]{1,0:T(8,128)S(1)} collective-permute-done((f32[128,128]{1,0:T(8,128)S(1)}, f32[128,128]{1,0:T(8,128)S(1)}, u32[]{:S(2)}, u32[]{:S(2)}) %collective-permute-start.12) | collective-permute-done | bytes 65568 | tf_op jit(solution)/shard_map/ppermute | solution.py:375
  56.9 0.0 collective-permute-done.13.cola_ref
  56.9 0.0 collective-permute-done.14.colb_ref
  57.0 1.1 %collective-permute-start.15 = (f32[128,128]{1,0:T(8,128)S(1)}, f32[128,128]{1,0:T(8,128)S(1)}, u32[]{:S(2)}, u32[]{:S(2)}) collective-permute-start(f32[128,128]{1,0:T(8,128)S(1)} %add.28), channel_id=1, source_target_pairs={{0,4},{1,13},{2,6},{3,15},{4,0},{5,9},{6,2},{7,11},{8,12},{9,5},{1... | collective-permute-start | bytes 196616 | tf_op jit(solution)/shard_map/ppermute | solution.py:375
  58.0 0.7 shard_map.92
  58.7 2.7 %collective-permute-done.15 = f32[128,128]{1,0:T(8,128)S(1)} collective-permute-done((f32[128,128]{1,0:T(8,128)S(1)}, f32[128,128]{1,0:T(8,128)S(1)}, u32[]{:S(2)}, u32[]{:S(2)}) %collective-permute-start.15) | collective-permute-done | bytes 65568 | tf_op jit(solution)/shard_map/ppermute | solution.py:375
  61.4 1.6 %collective-permute-start.18 = (f32[2,4,64,128]{3,2,1,0:T(8,128)S(1)}, f32[2,4,64,128]{3,2,1,0:T(8,128)S(1)}, u32[]{:S(2)}, u32[]{:S(2)}) collective-permute-start(f32[2,4,64,128]{3,2,1,0:T(8,128)S(1)} %get-tuple-element.63), channel_id=1, source_target_pairs={{0,16},{1,17},{2,18},{3,19},{4,20},{5,21},{6,22},{7,23},{8,24},{9,... | collective-permute-start | bytes 786440 | tf_op jit(solution)/shard_map/ppermute | solution.py:369
  63.0 5.5 %collective-permute-start.19 = (f32[2,4,64,128]{3,2,1,0:T(8,128)S(1)}, f32[2,4,64,128]{3,2,1,0:T(8,128)S(1)}, u32[]{:S(2)}, u32[]{:S(2)}) collective-permute-start(f32[2,4,64,128]{3,2,1,0:T(8,128)S(1)} %get-tuple-element.64), channel_id=1, source_target_pairs={{0,1},{1,0},{2,3},{3,2},{4,5},{5,4},{6,7},{7,6},{8,9},{9,8},{10,11... | collective-permute-start | bytes 786440 | tf_op jit(solution)/shard_map/ppermute | solution.py:369
  68.5 0.4 collective-permute-start.16
  68.9 3.0 %collective-permute-done.16 = f32[128,128]{1,0:T(8,128)S(1)} collective-permute-done((f32[128,128]{1,0:T(8,128)S(1)}, f32[128,128]{1,0:T(8,128)S(1)}, u32[]{:S(2)}, u32[]{:S(2)}) %collective-permute-start.16) | collective-permute-done | bytes 65568 | tf_op jit(solution)/shard_map/ppermute | solution.py:375
  71.9 0.1 collective-permute-start.17
  72.0 4.0 %collective-permute-done.17 = f32[128,128]{1,0:T(8,128)S(1)} collective-permute-done((f32[128,128]{1,0:T(8,128)S(1)}, f32[128,128]{1,0:T(8,128)S(1)}, u32[]{:S(2)}, u32[]{:S(2)}) %collective-permute-start.17) | collective-permute-done | bytes 65568 | tf_op jit(solution)/shard_map/ppermute | solution.py:375
  76.0 0.0 collective-permute-done.18.rowa_ref
  76.0 0.0 collective-permute-done.19.rowb_ref
  76.0 3.6 %collective-permute-start.20 = (f32[128,128]{1,0:T(8,128)S(1)}, f32[128,128]{1,0:T(8,128)S(1)}, u32[]{:S(2)}, u32[]{:S(2)}) collective-permute-start(f32[128,128]{1,0:T(8,128)S(1)} %add.31.mine_ref), channel_id=1, source_target_pairs={{0,1},{1,0},{2,3},{3,2},{4,5},{5,4},{6,7},{7,6},{8,9},{9,8},{10,11... | collective-permute-start | bytes 196616 | tf_op jit(solution)/shard_map/ppermute | solution.py:375
  79.7 1.8 %shard_map.93 = f32[2,2,256,256]{3,2,1,0:T(8,128)} custom-call(s32[1,4]{1,0:T(1,128)S(1)} %add_bitcast_fusion.spot_ref, f32[2,2,256,256]{3,2,1,0:T(8,128)S(1)} %get-tuple-element.47.part_ref, f32[2,4,64,128]{3,2,1,0:T(8,128)S(1)} %collective-permute-done.18.rowa_ref, f32[2,4,64,128]{3,2,1,0:T(8,128)S(1)} %collective-permute-done.19.rowb_ref, ...), custom_call_target="tpu_custom_call" | custom-call | tf_op jit(solution)/shard_map/pallas_call | solution.py:379
  81.4 0.0 collective-permute-done.20.other_ref
  81.4 1.2 %shard_map.94 = f32[2,128,128]{2,1,0:T(8,128)} custom-call(s32[1,4]{1,0:T(1,128)S(1)} %add_bitcast_fusion.spot_ref, f32[2,128,128]{2,1,0:T(8,128)S(1)} %copy-done.2, f32[128,128]{1,0:T(8,128)S(1)} %add.31.mine_ref, f32[128,128]{1,0:T(8,128)S(1)} %collective-permute-done.20.other_ref), custom_call_target="tpu_custom_call" | custom-call | tf_op jit(solution)/shard_map/pallas_call | solution.py:379
  (9 shorter events, 0.1 us)
Async XLA Ops:
  0.6 9.2 %copy-start = (f32[2,2,256,256]{3,2,1,0:T(8,128)S(1)}, f32[2,2,256,256]{3,2,1,0:T(8,128)}, u32[]{:S(2)}) copy-start(f32[2,2,256,256]{3,2,1,0:T(8,128)} %obj_ref.11) | copy-start | bytes 3145732
  2.4 7.3 %collective-permute-start.4 = (f32[4,64,128]{2,1,0:T(8,128)S(1)}, f32[4,64,128]{2,1,0:T(8,128)S(1)}, u32[]{:S(2)}, u32[]{:S(2)}) collective-permute-start(f32[4,64,128]{2,1,0:T(8,128)S(1)} %get-tuple-element.39), channel_id=1, source_target_pairs={{0,16},{1,17},{2,18},{3,19},{4,20},{5,21},{6,22},{7,23},{8,24},{9,... | collective-permute-start | bytes 393224 | tf_op jit(solution)/shard_map/ppermute | solution.py:369
  5.0 4.8 %collective-permute-start.5 = (f32[4,64,128]{2,1,0:T(8,128)S(1)}, f32[4,64,128]{2,1,0:T(8,128)S(1)}, u32[]{:S(2)}, u32[]{:S(2)}) collective-permute-start(f32[4,64,128]{2,1,0:T(8,128)S(1)} %get-tuple-element.40), channel_id=1, source_target_pairs={{0,1},{1,0},{2,3},{3,2},{4,5},{5,4},{6,7},{7,6},{8,9},{9,8},{10,11... | collective-permute-start | bytes 393224 | tf_op jit(solution)/shard_map/ppermute | solution.py:369
  6.0 8.0 %collective-permute-start = (f32[4,64,128]{2,1,0:T(8,128)S(1)}, f32[4,64,128]{2,1,0:T(8,128)S(1)}, u32[]{:S(2)}, u32[]{:S(2)}) collective-permute-start(f32[4,64,128]{2,1,0:T(8,128)S(1)} %get-tuple-element.35), channel_id=1, source_target_pairs={{0,16},{1,17},{2,18},{3,19},{4,20},{5,21},{6,22},{7,23},{8,24},{9,... | collective-permute-start | bytes 393224 | tf_op jit(solution)/shard_map/ppermute | solution.py:369
  8.3 14.3 %copy-start.1 = (bf16[4,2,256,256]{3,2,1,0:T(8,128)(2,1)S(1)}, bf16[4,2,256,256]{3,2,1,0:T(8,128)(2,1)}, u32[]{:S(2)}) copy-start(bf16[4,2,256,256]{3,2,1,0:T(8,128)(2,1)} %constant.11.clone.tabs_ref) | copy-start | bytes 3145732
  8.3 5.7 %collective-permute-start.1 = (f32[4,64,128]{2,1,0:T(8,128)S(1)}, f32[4,64,128]{2,1,0:T(8,128)S(1)}, u32[]{:S(2)}, u32[]{:S(2)}) collective-permute-start(f32[4,64,128]{2,1,0:T(8,128)S(1)} %get-tuple-element.36), channel_id=1, source_target_pairs={{0,1},{1,0},{2,3},{3,2},{4,5},{5,4},{6,7},{7,6},{8,9},{9,8},{10,11... | collective-permute-start | bytes 393224 | tf_op jit(solution)/shard_map/ppermute | solution.py:369
  10.5 6.8 %collective-permute-start.6 = (f32[384,128]{1,0:T(8,128)S(1)}, f32[384,128]{1,0:T(8,128)S(1)}, u32[]{:S(2)}, u32[]{:S(2)}) collective-permute-start(f32[384,128]{1,0:T(8,128)S(1)} %get-tuple-element.41), channel_id=1, source_target_pairs={{0,1},{1,0},{2,3},{3,2},{4,5},{5,4},{6,7},{7,6},{8,9},{9,8},{10,11... | collective-permute-start | bytes 589832 | tf_op jit(solution)/shard_map/ppermute | solution.py:369
  12.4 10.2 %copy-start.2 = (f32[2,128,128]{2,1,0:T(8,128)S(1)}, f32[2,128,128]{2,1,0:T(8,128)}, u32[]{:S(2)}) copy-start(f32[2,128,128]{2,1,0:T(8,128)} %probe_ref.5) | copy-start | bytes 393220
  12.4 10.2 %collective-permute-start.7 = (f32[384,128]{1,0:T(8,128)S(1)}, f32[384,128]{1,0:T(8,128)S(1)}, u32[]{:S(2)}, u32[]{:S(2)}) collective-permute-start(f32[384,128]{1,0:T(8,128)S(1)} %get-tuple-element.42), channel_id=1, source_target_pairs={{0,16},{1,2},{2,1},{3,4},{4,3},{5,6},{6,5},{7,8},{8,7},{9,10},{10,... | collective-permute-start | bytes 589832 | tf_op jit(solution)/shard_map/ppermute | solution.py:369
  14.7 10.2 %collective-permute-start.2 = (f32[384,128]{1,0:T(8,128)S(1)}, f32[384,128]{1,0:T(8,128)S(1)}, u32[]{:S(2)}, u32[]{:S(2)}) collective-permute-start(f32[384,128]{1,0:T(8,128)S(1)} %get-tuple-element.37), channel_id=1, source_target_pairs={{0,1},{1,0},{2,3},{3,2},{4,5},{5,4},{6,7},{7,6},{8,9},{9,8},{10,11... | collective-permute-start | bytes 589832 | tf_op jit(solution)/shard_map/ppermute | solution.py:369
  15.7 6.9 %copy-start.4 = (s32[1,8]{1,0:T(1,128)S(1)}, s32[1,8]{1,0:T(1,128)}, u32[]{:S(2)}) copy-start(s32[1,8]{1,0:T(1,128)} %row_ref.5) | copy-start | bytes 100
  15.7 6.9 %copy-start.5 = (s32[1,8]{1,0:T(1,128)S(1)}, s32[1,8]{1,0:T(1,128)}, u32[]{:S(2)}) copy-start(s32[1,8]{1,0:T(1,128)} %col_ref.5) | copy-start | bytes 100
  15.7 9.2 %collective-permute-start.3 = (f32[384,128]{1,0:T(8,128)S(1)}, f32[384,128]{1,0:T(8,128)S(1)}, u32[]{:S(2)}, u32[]{:S(2)}) collective-permute-start(f32[384,128]{1,0:T(8,128)S(1)} %get-tuple-element.38), channel_id=1, source_target_pairs={{0,16},{1,2},{2,1},{3,4},{4,3},{5,6},{6,5},{7,8},{8,7},{9,10},{10,... | collective-permute-start | bytes 589832 | tf_op jit(solution)/shard_map/ppermute | solution.py:369
  17.3 7.6 %copy-start.3 = (f32[1,8,128,128]{3,2,1,0:T(8,128)S(1)}, f32[1,8,128,128]{3,2,1,0:T(8,128)}, u32[]{:S(2)}) copy-start(f32[1,8,128,128]{3,2,1,0:T(8,128)} %param.9) | copy-start | bytes 1572868
  30.8 1.3 %collective-permute-start.8 = (f32[128,128]{1,0:T(8,128)S(1)}, f32[128,128]{1,0:T(8,128)S(1)}, u32[]{:S(2)}, u32[]{:S(2)}) collective-permute-start(f32[128,128]{1,0:T(8,128)S(1)} %get-tuple-element.49), channel_id=1, source_target_pairs={{0,1},{1,0},{2,3},{3,2},{4,5},{5,4},{6,7},{7,6},{8,9},{9,8},{10,11... | collective-permute-start | bytes 196616 | tf_op jit(solution)/shard_map/ppermute | solution.py:375
  32.1 8.8 %collective-permute-start.9 = (f32[128,128]{1,0:T(8,128)S(1)}, f32[128,128]{1,0:T(8,128)S(1)}, u32[]{:S(2)}, u32[]{:S(2)}) collective-permute-start(f32[128,128]{1,0:T(8,128)S(1)} %add.24), channel_id=1, source_target_pairs={{0,128},{1,131},{2,130},{3,129},{4,132},{5,135},{6,134},{7,133},{8... | collective-permute-start | bytes 196616 | tf_op jit(solution)/shard_map/ppermute | solution.py:375
  41.0 15.9 %collective-permute-start.13 = (f32[2,384,128]{2,1,0:T(8,128)S(1)}, f32[2,384,128]{2,1,0:T(8,128)S(1)}, u32[]{:S(2)}, u32[]{:S(2)}) collective-permute-start(f32[2,384,128]{2,1,0:T(8,128)S(1)} %get-tuple-element.53), channel_id=1, source_target_pairs={{0,1},{1,0},{2,3},{3,2},{4,5},{5,4},{6,7},{7,6},{8,9},{9,8},{10,11... | collective-permute-start | bytes 1179656 | tf_op jit(solution)/shard_map/ppermute | solution.py:369
  41.1 15.8 %collective-permute-start.14 = (f32[2,384,128]{2,1,0:T(8,128)S(1)}, f32[2,384,128]{2,1,0:T(8,128)S(1)}, u32[]{:S(2)}, u32[]{:S(2)}) collective-permute-start(f32[2,384,128]{2,1,0:T(8,128)S(1)} %get-tuple-element.54), channel_id=1, source_target_pairs={{0,16},{1,2},{2,1},{3,4},{4,3},{5,6},{6,5},{7,8},{8,7},{9,10},{10,... | collective-permute-start | bytes 1179656 | tf_op jit(solution)/shard_map/ppermute | solution.py:369
  42.9 4.7 %collective-permute-start.10 = (f32[128,128]{1,0:T(8,128)S(1)}, f32[128,128]{1,0:T(8,128)S(1)}, u32[]{:S(2)}, u32[]{:S(2)}) collective-permute-start(f32[128,128]{1,0:T(8,128)S(1)} %add.25), channel_id=1, source_target_pairs={{0,16},{1,33},{2,18},{3,35},{4,20},{5,37},{6,22},{7,39},{8,24},{9,... | collective-permute-start | bytes 196616 | tf_op jit(solution)/shard_map/ppermute | solution.py:375
  47.6 5.7 %collective-permute-start.11 = (f32[128,128]{1,0:T(8,128)S(1)}, f32[128,128]{1,0:T(8,128)S(1)}, u32[]{:S(2)}, u32[]{:S(2)}) collective-permute-start(f32[128,128]{1,0:T(8,128)S(1)} %add.26), channel_id=1, source_target_pairs={{0,32},{1,97},{2,34},{3,99},{4,36},{5,101},{6,38},{7,103},{8,40},{... | collective-permute-start | bytes 196616 | tf_op jit(solution)/shard_map/ppermute | solution.py:375
  53.3 3.6 %collective-permute-start.12 = (f32[128,128]{1,0:T(8,128)S(1)}, f32[128,128]{1,0:T(8,128)S(1)}, u32[]{:S(2)}, u32[]{:S(2)}) collective-permute-start(f32[128,128]{1,0:T(8,128)S(1)} %add.27), channel_id=1, source_target_pairs={{0,96},{1,17},{2,98},{3,19},{4,100},{5,21},{6,102},{7,23},{8,104},... | collective-permute-start | bytes 196616 | tf_op jit(solution)/shard_map/ppermute | solution.py:375
  57.0 4.4 %collective-permute-start.15 = (f32[128,128]{1,0:T(8,128)S(1)}, f32[128,128]{1,0:T(8,128)S(1)}, u32[]{:S(2)}, u32[]{:S(2)}) collective-permute-start(f32[128,128]{1,0:T(8,128)S(1)} %add.28), channel_id=1, source_target_pairs={{0,4},{1,13},{2,6},{3,15},{4,0},{5,9},{6,2},{7,11},{8,12},{9,5},{1... | collective-permute-start | bytes 196616 | tf_op jit(solution)/shard_map/ppermute | solution.py:375
  61.4 14.6 %collective-permute-start.18 = (f32[2,4,64,128]{3,2,1,0:T(8,128)S(1)}, f32[2,4,64,128]{3,2,1,0:T(8,128)S(1)}, u32[]{:S(2)}, u32[]{:S(2)}) collective-permute-start(f32[2,4,64,128]{3,2,1,0:T(8,128)S(1)} %get-tuple-element.63), channel_id=1, source_target_pairs={{0,16},{1,17},{2,18},{3,19},{4,20},{5,21},{6,22},{7,23},{8,24},{9,... | collective-permute-start | bytes 786440 | tf_op jit(solution)/shard_map/ppermute | solution.py:369
  63.0 13.1 %collective-permute-start.19 = (f32[2,4,64,128]{3,2,1,0:T(8,128)S(1)}, f32[2,4,64,128]{3,2,1,0:T(8,128)S(1)}, u32[]{:S(2)}, u32[]{:S(2)}) collective-permute-start(f32[2,4,64,128]{3,2,1,0:T(8,128)S(1)} %get-tuple-element.64), channel_id=1, source_target_pairs={{0,1},{1,0},{2,3},{3,2},{4,5},{5,4},{6,7},{7,6},{8,9},{9,8},{10,11... | collective-permute-start | bytes 786440 | tf_op jit(solution)/shard_map/ppermute | solution.py:369
  68.5 3.4 %collective-permute-start.16 = (f32[128,128]{1,0:T(8,128)S(1)}, f32[128,128]{1,0:T(8,128)S(1)}, u32[]{:S(2)}, u32[]{:S(2)}) collective-permute-start(f32[128,128]{1,0:T(8,128)S(1)} %add.29), channel_id=1, source_target_pairs={{0,12},{1,5},{2,14},{3,7},{4,8},{5,1},{6,10},{7,3},{8,4},{9,13},{1... | collective-permute-start | bytes 196616 | tf_op jit(solution)/shard_map/ppermute | solution.py:375
  71.9 4.1 %collective-permute-start.17 = (f32[128,128]{1,0:T(8,128)S(1)}, f32[128,128]{1,0:T(8,128)S(1)}, u32[]{:S(2)}, u32[]{:S(2)}) collective-permute-start(f32[128,128]{1,0:T(8,128)S(1)} %add.30), channel_id=1, source_target_pairs={{0,130},{1,129},{2,128},{3,131},{4,134},{5,133},{6,132},{7,135},{8... | collective-permute-start | bytes 196616 | tf_op jit(solution)/shard_map/ppermute | solution.py:375
  76.0 5.4 %collective-permute-start.20 = (f32[128,128]{1,0:T(8,128)S(1)}, f32[128,128]{1,0:T(8,128)S(1)}, u32[]{:S(2)}, u32[]{:S(2)}) collective-permute-start(f32[128,128]{1,0:T(8,128)S(1)} %add.31.mine_ref), channel_id=1, source_target_pairs={{0,1},{1,0},{2,3},{3,2},{4,5},{5,4},{6,7},{7,6},{8,9},{9,8},{10,11... | collective-permute-start | bytes 196616 | tf_op jit(solution)/shard_map/ppermute | solution.py:375

commit v12 on v9

--- a/solution.py
+++ b/solution.py
@@ -75,18 +75,18 @@
     return left, right
 
 
-def pick(spot_ref, axis, even, odd):
-    return jnp.where(lax.rem(spot_ref[0, axis], 2) == 0, even, odd)
-
-
-def beside(spot_ref, axis, a, b):
-    place = spot_ref[0, axis]
-    before = jnp.where(place == 0, 0.0, pick(spot_ref, axis, b, a))
-    after = jnp.where(place == spot_ref[0, 2 + axis] - 1, 0.0, pick(spot_ref, axis, a, b))
+def pick(axis, even, odd):
+    return jnp.where(lax.rem(lax.axis_index(BOTH[axis]), 2) == 0, even, odd)
+
+
+def beside(axis, a, b):
+    place = lax.axis_index(BOTH[axis])
+    before = jnp.where(place == 0, 0.0, pick(axis, b, a))
+    after = jnp.where(place == lax.axis_size(BOTH[axis]) - 1, 0.0, pick(axis, a, b))
     return before, after
 
 
-def pack_kernel(spot_ref, obj_ref, *refs):
+def pack_kernel(obj_ref, *refs):
     *outs, held, sems = refs
     first = lax.broadcasted_iota(jnp.int32, (held.shape[2], LANES), 1) < LANES // 2
     copies = [pltpu.make_async_copy(obj_ref.at[p], held.at[p], sems.at[p]) for p in range(2)]
@@ -95,34 +95,34 @@
     for piece in range(2):
         copies[piece].wait()
         left, right = columns(held.at[piece], first)
-        outs[2 * piece][...] = pick(spot_ref, 1, right, left)
-        outs[2 * piece + 1][...] = pick(spot_ref, 1, left, right)
-
-
-def rows_kernel(spot_ref, obj_ref, cola_ref, colb_ref, rowa_ref, rowb_ref, *, piece):
+        outs[2 * piece][...] = pick(1, right, left)
+        outs[2 * piece + 1][...] = pick(1, left, right)
+
+
+def rows_kernel(obj_ref, cola_ref, colb_ref, rowa_ref, rowb_ref, *, piece):
     half = LANES // 2
     low, high = slice(0, half), slice(obj_ref.shape[2] - half, obj_ref.shape[2])
     for part in range(2):
         for block in range(2):
             cols = slice(block * LANES, (block + 1) * LANES)
             top, bottom = obj_ref[piece, part, low, cols], obj_ref[piece, part, high, cols]
-            rowa_ref[2 * part + block] = pick(spot_ref, 0, bottom, top)
-            rowb_ref[2 * part + block] = pick(spot_ref, 0, top, bottom)
-    tops = beside(spot_ref, 1, cola_ref[low], colb_ref[low])
-    bottoms = beside(spot_ref, 1, cola_ref[high], colb_ref[high])
+            rowa_ref[2 * part + block] = pick(0, bottom, top)
+            rowb_ref[2 * part + block] = pick(0, top, bottom)
+    tops = beside(1, cola_ref[low], colb_ref[low])
+    bottoms = beside(1, cola_ref[high], colb_ref[high])
     for place, top, bottom in zip((4, 5), tops, bottoms):
-        rowa_ref[place] = pick(spot_ref, 0, bottom, top)
-        rowb_ref[place] = pick(spot_ref, 0, top, bottom)
-
-
-def grow(ext, spot_ref, piece_ref, cola_ref, colb_ref, rowa_ref, rowb_ref):
+        rowa_ref[place] = pick(0, bottom, top)
+        rowb_ref[place] = pick(0, top, bottom)
+
+
+def grow(ext, piece_ref, cola_ref, colb_ref, rowa_ref, rowb_ref):
     half = LANES // 2
     tile = piece_ref.shape[1]
-    sides = beside(spot_ref, 1, cola_ref[...], colb_ref[...])
+    sides = beside(1, cola_ref[...], colb_ref[...])
     for part in range(2):
         for block in range(4):
             place = 2 * part + block - 1 if block in (1, 2) else 4 + block // 3
-            top, bottom = beside(spot_ref, 0, rowa_ref[place], rowb_ref[place])
+            top, bottom = beside(0, rowa_ref[place], rowb_ref[place])
             if block in (1, 2):
                 middle = piece_ref[part, :, (block - 1) * LANES : block * LANES]
             else:
@@ -167,11 +167,11 @@
 
 
 def first_kernel(
-    row_ref, col_ref, spot_ref, obj_ref, cola_ref, colb_ref, rowa_ref, rowb_ref, probe_ref, tabs_ref,
+    row_ref, col_ref, obj_ref, cola_ref, colb_ref, rowa_ref, rowb_ref, probe_ref, tabs_ref,
     win_ref, mid_ref, ext, *, group,
 ):
     width = probe_ref.shape[1]
-    grow(ext, spot_ref, obj_ref.at[0], cola_ref, colb_ref, rowa_ref, rowb_ref)
+    grow(ext, obj_ref.at[0], cola_ref, colb_ref, rowa_ref, rowb_ref)
 
     def some(index, _):
         slots = [group * index + place for place in range(group)]
@@ -187,13 +187,13 @@
 
 
 def second_kernel(
-    row_ref, col_ref, spot_ref, live_ref, obj_ref, cola_ref, colb_ref, rowa_ref, rowb_ref,
+    row_ref, col_ref, live_ref, obj_ref, cola_ref, colb_ref, rowa_ref, rowb_ref,
     win_ref, mid_ref, measured_ref, tabs_ref,
     grad_ref, down_ref, keep_ref, send_ref,
     ext, sum_ref, *, group,
 ):
     width = win_ref.shape[2]
-    grow(ext, spot_ref, obj_ref.at[1], cola_ref, colb_ref, rowa_ref, rowb_ref)
+    grow(ext, obj_ref.at[1], cola_ref, colb_ref, rowa_ref, rowb_ref)
     sum_ref[...] = jnp.zeros_like(sum_ref)
 
     def some(index, _):
@@ -229,12 +229,12 @@
         return 0
 
     lax.fori_loop(0, row_ref.shape[1] // group, some, 0, unroll=True)
-    keep_ref[...] = pick(spot_ref, 1, sum_ref[0], sum_ref[1])
-    send_ref[...] = pick(spot_ref, 1, sum_ref[1], sum_ref[0])
+    keep_ref[...] = pick(1, sum_ref[0], sum_ref[1])
+    send_ref[...] = pick(1, sum_ref[1], sum_ref[0])
 
 
 def place_kernel(
-    row_ref, col_ref, spot_ref, obj_ref, probe_ref, down_ref, second_ref,
+    row_ref, col_ref, obj_ref, probe_ref, down_ref, second_ref,
     new_ref, rowa_ref, rowb_ref, left_ref, right_ref,
     grad,
 ):
@@ -268,8 +268,8 @@
                 cols = slice(block * LANES, (block + 1) * LANES)
                 top = grad[piece, part, 1 + block, :half]
                 bottom = grad[piece, part, 1 + block, half + tile :]
-                rowa_ref[piece, 2 * part + block] = pick(spot_ref, 0, bottom, top)
-                rowb_ref[piece, 2 * part + block] = pick(spot_ref, 0, top, bottom)
+                rowa_ref[piece, 2 * part + block] = pick(0, bottom, top)
+                rowb_ref[piece, 2 * part + block] = pick(0, top, bottom)
                 new_ref[piece, part, :, cols] = (
                     obj_ref[piece, part, :, cols]
                     - STEP_OBJECT * grad[piece, part, 1 + block, half : half + tile]
@@ -278,18 +278,18 @@
         right = jnp.where(first, grad[piece, 0, 3], pltpu.roll(grad[piece, 1, 3], half, 1))
         for place, strip, ref in ((4, left, left_ref), (5, right, right_ref)):
             top, bottom = strip[:half], strip[half + tile :]
-            rowa_ref[piece, place] = pick(spot_ref, 0, bottom, top)
-            rowb_ref[piece, place] = pick(spot_ref, 0, top, bottom)
+            rowa_ref[piece, place] = pick(0, bottom, top)
+            rowb_ref[piece, place] = pick(0, top, bottom)
             ref[piece] = strip[half : half + tile]
 
 
-def fold_kernel(spot_ref, left_ref, right_ref, rowa_ref, rowb_ref, cola_ref, colb_ref):
+def fold_kernel(left_ref, right_ref, rowa_ref, rowb_ref, cola_ref, colb_ref):
     half = LANES // 2
     tile = left_ref.shape[1]
     for piece in range(2):
         sides = []
         for ref, place in ((left_ref, 4), (right_ref, 5)):
-            top, bottom = beside(spot_ref, 0, rowa_ref[piece, place], rowb_ref[piece, place])
+            top, bottom = beside(0, rowa_ref[piece, place], rowb_ref[piece, place])
             sides.append(
                 (
                     ref[piece, :half] + top,
@@ -298,12 +298,12 @@
                 )
             )
         for left, right, rows in zip(*sides, (slice(0, half), slice(half, tile - half), slice(tile - half, tile))):
-            cola_ref[piece, rows] = pick(spot_ref, 1, right, left)
-            colb_ref[piece, rows] = pick(spot_ref, 1, left, right)
+            cola_ref[piece, rows] = pick(1, right, left)
+            colb_ref[piece, rows] = pick(1, left, right)
 
 
 def finish_kernel(
-    spot_ref, part_ref, rowa_ref, rowb_ref, cola_ref, colb_ref, new_ref,
+    part_ref, rowa_ref, rowb_ref, cola_ref, colb_ref, new_ref,
 ):
     tile = part_ref.shape[2]
     half = LANES // 2
@@ -311,7 +311,7 @@
     for piece in range(2):
         for start in range(0, tile, half):
             rows = slice(start, start + half)
-            sides = beside(spot_ref, 1, cola_ref[piece, rows], colb_ref[piece, rows])
+            sides = beside(1, cola_ref[piece, rows], colb_ref[piece, rows])
             for part in range(2):
                 for block in range(2):
                     cols = slice(block * LANES, (block + 1) * LANES)
@@ -320,7 +320,7 @@
                         total = pltpu.roll(total, half, 1)
                     total = jnp.where(first == (block == 0), total, 0.0)
                     place = 2 * part + block
-                    ends = beside(spot_ref, 0, rowa_ref[piece, place], rowb_ref[piece, place])
+                    ends = beside(0, rowa_ref[piece, place], rowb_ref[piece, place])
                     if start == 0:
                         total += ends[0]
                     if start == tile - half:
@@ -330,9 +330,9 @@
                     )
 
 
-def probe_kernel(spot_ref, probe_ref, mine_ref, other_ref, newp_ref, *, scale):
-    newp_ref[0] = probe_ref[0] - scale * pick(spot_ref, 1, mine_ref[...], other_ref[...])
-    newp_ref[1] = probe_ref[1] - scale * pick(spot_ref, 1, other_ref[...], mine_ref[...])
+def probe_kernel(probe_ref, mine_ref, other_ref, newp_ref, *, scale):
+    newp_ref[0] = probe_ref[0] - scale * pick(1, mine_ref[...], other_ref[...])
+    newp_ref[1] = probe_ref[1] - scale * pick(1, other_ref[...], mine_ref[...])
 
 
 def vmem(count):
@@ -384,36 +384,34 @@
     count = offset_row.shape[1]
     side, edge, plane = (tile, LANES), (6, half, LANES), (width, width)
     field, fields = array(2, 2, tile, tile), array(count, 2, width, width)
-    place = [lax.axis_index(axis) for axis in BOTH] + [lax.axis_size(axis) for axis in BOTH]
-    spot = jnp.stack([jnp.asarray(entry, jnp.int32) for entry in place]).reshape(1, 4)
     tabs = jnp.asarray(make_tables(width))
     grown = pltpu.VMEM((2, 4, tile + width, LANES), jnp.float32)
     packed = pl.pallas_call(
         pack_kernel, out_shape=tuple([array(*side)] * 4),
-        in_specs=smem(1) + [pl.BlockSpec(memory_space=pltpu.HBM)], out_specs=tuple(vmem(4)),
+        in_specs=[pl.BlockSpec(memory_space=pltpu.HBM)], out_specs=tuple(vmem(4)),
         scratch_shapes=[pltpu.VMEM(object_field.shape, jnp.float32), pltpu.SemaphoreType.DMA((2,))],
         compiler_params=pltpu.CompilerParams(vmem_limit_bytes=GRANT),
-    )(spot, pltpu.with_memory_space_constraint(object_field, pltpu.HBM))
+    )(pltpu.with_memory_space_constraint(object_field, pltpu.HBM))
     halos = []
     cols = [meet(packed[2 * piece : 2 * piece + 2], 1) for piece in range(2)]
     for piece in range(2):
         strips = call(
             functools.partial(rows_kernel, piece=piece), [array(*edge)] * 2,
-            (spot,), (object_field, *cols[piece]),
+            (), (object_field, *cols[piece]),
         )
         halos.append((*cols[piece], *meet(strips, 0)))
     win, mid = call(
-        functools.partial(first_kernel, group=2), [fields] * 2, (offset_row, offset_col, spot),
+        functools.partial(first_kernel, group=2), [fields] * 2, (offset_row, offset_col),
         (object_field, *halos[0], probe, tabs), (grown,),
     )
     grad, down, mine, send = call(
-        functools.partial(second_kernel, group=count), [fields] * 2 + [array(*plane)] * 2, (offset_row, offset_col, spot, live),
+        functools.partial(second_kernel, group=count), [fields] * 2 + [array(*plane)] * 2, (offset_row, offset_col, live),
         (object_field, *halos[1], win, mid, intensity[0], tabs),
         (grown, pltpu.VMEM((2, *plane), jnp.float32)),
     )
     part, *strips, left, right = call(
         place_kernel, [field] + [array(2, *edge)] * 2 + [array(2, *side)] * 2,
-        (offset_row, offset_col, spot), (object_field, probe, down, grad),
+        (offset_row, offset_col), (object_field, probe, down, grad),
         (pltpu.VMEM((2, 2, 4, tile + width, LANES), jnp.float32),),
     )
     mine = mine + swap(send, (1, 1))
@@ -423,19 +421,19 @@
     for mask in MASKS[1:4]:
         mine = mine + swap(mine, mask)
     mine, *rows = lax.optimization_barrier((mine, *rows))
-    strips = call(fold_kernel, [array(2, *side)] * 2, (spot,), (left, right, *rows))
+    strips = call(fold_kernel, [array(2, *side)] * 2, (), (left, right, *rows))
     mine = mine + swap(mine, MASKS[4])
     mine, *strips = lax.optimization_barrier((mine, *strips))
     cols = meet(strips, 1)
     for mask in MASKS[5:]:
         mine = mine + swap(mine, mask)
     mine, *cols = lax.optimization_barrier((mine, *cols))
-    (new,) = call(finish_kernel, (field,), (spot,), (part, *rows, *cols))
+    (new,) = call(finish_kernel, (field,), (), (part, *rows, *cols))
     other = swap(mine, (1, 1))
     count_all = count * lax.axis_size("row") * lax.axis_size("col")
     (new_probe,) = call(
         functools.partial(probe_kernel, scale=STEP_PROBE / count_all), (array(2, *plane),),
-        (spot,), (probe, mine, other),
+        (), (probe, mine, other),
     )
     return new, new_probe
 

time: 80.5 us -> 78.3 us (0.973)
  Pallas kernels: 17 us -> 13.8 us
  starting transfers between devices: 35.6 us -> 37.4 us
    ppermute x9, starting transfers between devices: 19.5 us -> 22.8 us  [swap(): lax.ppermute(value, BOTH, [(i, i ^ masks[i % 2]) for i in range(count)])]
    pallas_call x8, Pallas kernels: 15.1 us -> 12.4 us  [call(): pl.pallas_call(kernel, out_shape=tuple(out_shape), in_specs=smem(len(scal...]
    ppermute x9, waiting for transfers between devices: 19.1 us -> 17.2 us  [swap(): lax.ppermute(value, BOTH, [(i, i ^ masks[i % 2]) for i in range(count)])]
    ppermute x12, starting transfers between devices: 16.1 us -> 14.6 us  [meet(): got.append(lax.ppermute(strip, BOTH, pairs))]
    ppermute x12, waiting for transfers between devices: 6.98 us -> 8.08 us  [meet(): got.append(lax.ppermute(strip, BOTH, pairs))]
  transfers between devices with their start and end apart: 21 -> 21, of which waited for: 11 -> 11; matrix products, arithmetic and copies ran while one was open for 0% -> 0% of each run, Pallas kernels for 10% -> 8%
where the time goes in v12:
time: 78.3 us; the launch traced here: 78.2 us
  starting transfers between devices  37.4 us (48%)
  waiting for transfers between devices  25.3 us (32%)
  Pallas kernels  13.8 us (18%)
  between operations  1.51 us (2%)
    ppermute x9, starting transfers between devices, swap(): lax.ppermute(value, BOTH, [(i, i ^ masks[i % 2]) for i in range(count)])  22.8 us
    ppermute x9, waiting for transfers between devices, swap(): lax.ppermute(value, BOTH, [(i, i ^ masks[i % 2]) for i in range(count)])  17.2 us
    ppermute x12, starting transfers between devices, meet(): got.append(lax.ppermute(strip, BOTH, pairs))  14.6 us
    pallas_call x8, Pallas kernels, call(): pl.pallas_call(kernel, out_shape=tuple(out_shape), in_specs=smem(len(scal...  12.4 us
    ppermute x12, waiting for transfers between devices, meet(): got.append(lax.ppermute(strip, BOTH, pairs))  8.08 us
  transfers between devices with their start and end apart: 21, of which 11 were waited for; matrix products, arithmetic and copies ran while one was open for 0% of the time, Pallas kernels for 8%

profile of v12, /device:TPU:1, one launch (start us, length us, event | category | flops | bytes accessed | tf_op | source)
XLA Modules:
  0.0 78.2 jit_solution(1651283489049450187)
XLA Ops:
  0.6 0.0 copy-start
  0.6 1.4 %shard_map.86 = (f32[256,128]{1,0:T(8,128)S(1)}, f32[256,128]{1,0:T(8,128)S(1)}, f32[256,128]{1,0:T(8,128)S(1)}, f32[256,128]{1,0:T(8,128)S(1)}) custom-call(f32[2,2,256,256]{3,2,1,0:T(8,128)} %obj_ref.11), custom_call_target="tpu_custom_call" | custom-call | tf_op jit(solution)/shard_map/pallas_call | solution.py:389
  2.1 3.3 %collective-permute-start.4 = (f32[256,128]{1,0:T(8,128)S(1)}, f32[256,128]{1,0:T(8,128)S(1)}, u32[]{:S(2)}, u32[]{:S(2)}) collective-permute-start(f32[256,128]{1,0:T(8,128)S(1)} %get-tuple-element.39), channel_id=1, source_target_pairs={{0,1},{1,0},{2,3},{3,2},{4,5},{5,4},{6,7},{7,6},{8,9},{9,8},{10,11... | collective-permute-start | bytes 393224 | tf_op jit(solution)/shard_map/ppermute | solution.py:363
  5.4 1.2 %collective-permute-start.5 = (f32[256,128]{1,0:T(8,128)S(1)}, f32[256,128]{1,0:T(8,128)S(1)}, u32[]{:S(2)}, u32[]{:S(2)}) collective-permute-start(f32[256,128]{1,0:T(8,128)S(1)} %get-tuple-element.40), channel_id=1, source_target_pairs={{0,16},{1,2},{2,1},{3,4},{4,3},{5,6},{6,5},{7,8},{8,7},{9,10},{10,... | collective-permute-start | bytes 393224 | tf_op jit(solution)/shard_map/ppermute | solution.py:363
  6.6 0.0 collective-permute-start
  6.6 0.0 copy-start.1
  6.6 2.1 %collective-permute-start.1 = (f32[256,128]{1,0:T(8,128)S(1)}, f32[256,128]{1,0:T(8,128)S(1)}, u32[]{:S(2)}, u32[]{:S(2)}) collective-permute-start(f32[256,128]{1,0:T(8,128)S(1)} %get-tuple-element.36), channel_id=1, source_target_pairs={{0,16},{1,2},{2,1},{3,4},{4,3},{5,6},{6,5},{7,8},{8,7},{9,10},{10,... | collective-permute-start | bytes 393224 | tf_op jit(solution)/shard_map/ppermute | solution.py:363
  8.7 0.0 collective-permute-done.4.cola_ref
  8.7 2.6 %collective-permute-done.5.colb_ref = f32[256,128]{1,0:T(8,128)S(1)} collective-permute-done((f32[256,128]{1,0:T(8,128)S(1)}, f32[256,128]{1,0:T(8,128)S(1)}, u32[]{:S(2)}, u32[]{:S(2)}) %collective-permute-start.5) | collective-permute-done | bytes 131104 | tf_op jit(solution)/shard_map/ppermute | solution.py:363
  11.3 0.0 copy-done
  11.4 0.1 collective-permute-start.6
  11.5 0.0 copy-start.2
  11.5 0.1 collective-permute-start.7
  11.6 0.0 collective-permute-done.cola_ref
  11.6 1.2 %collective-permute-done.1.colb_ref = f32[256,128]{1,0:T(8,128)S(1)} collective-permute-done((f32[256,128]{1,0:T(8,128)S(1)}, f32[256,128]{1,0:T(8,128)S(1)}, u32[]{:S(2)}, u32[]{:S(2)}) %collective-permute-start.1) | collective-permute-done | bytes 131104 | tf_op jit(solution)/shard_map/ppermute | solution.py:363
  12.8 1.9 %collective-permute-start.2 = (f32[6,64,128]{2,1,0:T(8,128)S(1)}, f32[6,64,128]{2,1,0:T(8,128)S(1)}, u32[]{:S(2)}, u32[]{:S(2)}) collective-permute-start(f32[6,64,128]{2,1,0:T(8,128)S(1)} %get-tuple-element.37), channel_id=1, source_target_pairs={{0,16},{1,17},{2,18},{3,19},{4,20},{5,21},{6,22},{7,23},{8,24},{9,... | collective-permute-start | bytes 589832 | tf_op jit(solution)/shard_map/ppermute | solution.py:363
  14.8 0.0 copy-start.4
  14.8 0.0 copy-start.5
  14.8 0.0 collective-permute-start.3
  15.5 0.0 copy-start.3
  15.5 2.8 %collective-permute-done.6.rowa_ref = f32[6,64,128]{2,1,0:T(8,128)S(1)} collective-permute-done((f32[6,64,128]{2,1,0:T(8,128)S(1)}, f32[6,64,128]{2,1,0:T(8,128)S(1)}, u32[]{:S(2)}, u32[]{:S(2)}) %collective-permute-start.6) | collective-permute-done | bytes 196640 | tf_op jit(solution)/shard_map/ppermute | solution.py:363
  18.3 0.0 collective-permute-done.7.rowb_ref
  18.3 0.0 copy-done.1
  18.3 0.0 copy-done.2
  18.3 0.0 copy-done.4
  18.3 0.0 copy-done.5
  18.3 2.2 %shard_map.89 = (f32[8,2,128,128]{3,2,1,0:T(8,128)S(1)}, f32[8,2,128,128]{3,2,1,0:T(8,128)S(1)}) custom-call(s32[1,8]{1,0:T(1,128)S(1)} %copy-done.4, s32[1,8]{1,0:T(1,128)S(1)} %copy-done.5, f32[2,2,256,256]{3,2,1,0:T(8,128)S(1)} %copy-done, f32[256,128]{1,0:T(8,128)S(1)} %collective-permute-done.4.cola_ref, ...), custom_call_target="tpu_custom_call" | custom-call | tf_op jit(solution)/shard_map/pallas_call | solution.py:373
  20.5 1.4 %collective-permute-done.2.rowa_ref = f32[6,64,128]{2,1,0:T(8,128)S(1)} collective-permute-done((f32[6,64,128]{2,1,0:T(8,128)S(1)}, f32[6,64,128]{2,1,0:T(8,128)S(1)}, u32[]{:S(2)}, u32[]{:S(2)}) %collective-permute-start.2) | collective-permute-done | bytes 196640 | tf_op jit(solution)/shard_map/ppermute | solution.py:363
  21.9 0.0 collective-permute-done.3.rowb_ref
  21.9 0.0 copy-done.3
  21.9 5.8 %shard_map.90 = (f32[8,2,128,128]{3,2,1,0:T(8,128)S(1)}, f32[8,2,128,128]{3,2,1,0:T(8,128)S(1)}, f32[128,128]{1,0:T(8,128)S(1)}, f32[128,128]{1,0:T(8,128)S(1)}) custom-call(s32[1,8]{1,0:T(1,128)S(1)} %copy-done.4, s32[1,8]{1,0:T(1,128)S(1)} %copy-done.5, s32[1,1]{1,0:T(1,128)S(6)} %copy.9.live_ref, f32[2,2,256,256]{3,2,1,0:T(8,128)S(1)} %copy-done, ...), custom_call_target="tpu_custom_call" | custom-call | tf_op jit(solution)/shard_map/pallas_call | solution.py:373
  27.8 0.5 collective-permute-start.8
  28.3 0.9 %collective-permute-done.8 = f32[128,128]{1,0:T(8,128)S(1)} collective-permute-done((f32[128,128]{1,0:T(8,128)S(1)}, f32[128,128]{1,0:T(8,128)S(1)}, u32[]{:S(2)}, u32[]{:S(2)}) %collective-permute-start.8) | collective-permute-done | bytes 65568 | tf_op jit(solution)/shard_map/ppermute | solution.py:369
  29.2 1.9 %collective-permute-start.9 = (f32[128,128]{1,0:T(8,128)S(1)}, f32[128,128]{1,0:T(8,128)S(1)}, u32[]{:S(2)}, u32[]{:S(2)}) collective-permute-start(f32[128,128]{1,0:T(8,128)S(1)} %add.24), channel_id=1, source_target_pairs={{0,128},{1,5},{2,130},{3,7},{4,132},{5,1},{6,134},{7,3},{8,136},{9... | collective-permute-start | bytes 196616 | tf_op jit(solution)/shard_map/ppermute | solution.py:369
  31.1 2.3 %shard_map.91 = (f32[2,2,256,256]{3,2,1,0:T(8,128)S(1)}, f32[2,6,64,128]{3,2,1,0:T(8,128)S(1)}, f32[2,6,64,128]{3,2,1,0:T(8,128)S(1)}, f32[2,256,128]{2,1,0:T(8,128)S(1)}, f32[2,256,128]{2,1,0:T(8,128)S(1)}) custom-call(s32[1,8]{1,0:T(1,128)S(1)} %copy-done.4, s32[1,8]{1,0:T(1,128)S(1)} %copy-done.5, f32[2,2,256,256]{3,2,1,0:T(8,128)S(1)} %copy-done, ...), custom_call_target="tpu_custom_call" | custom-call | tf_op jit(solution)/shard_map/pallas_call | solution.py:373
  33.4 0.0 collective-permute-done.9
  33.5 3.4 %collective-permute-start.13 = (f32[2,6,64,128]{3,2,1,0:T(8,128)S(1)}, f32[2,6,64,128]{3,2,1,0:T(8,128)S(1)}, u32[]{:S(2)}, u32[]{:S(2)}) collective-permute-start(f32[2,6,64,128]{3,2,1,0:T(8,128)S(1)} %get-tuple-element.53), channel_id=1, source_target_pairs={{0,16},{1,17},{2,18},{3,19},{4,20},{5,21},{6,22},{7,23},{8,24},{9,... | collective-permute-start | bytes 1179656 | tf_op jit(solution)/shard_map/ppermute | solution.py:363
  36.9 0.3 collective-permute-start.14
  37.2 4.3 %collective-permute-start.10 = (f32[128,128]{1,0:T(8,128)S(1)}, f32[128,128]{1,0:T(8,128)S(1)}, u32[]{:S(2)}, u32[]{:S(2)}) collective-permute-start(f32[128,128]{1,0:T(8,128)S(1)} %add.25), channel_id=1, source_target_pairs={{0,4},{1,13},{2,6},{3,15},{4,0},{5,9},{6,2},{7,11},{8,12},{9,5},{1... | collective-permute-start | bytes 196616 | tf_op jit(solution)/shard_map/ppermute | solution.py:369
  41.4 1.7 %collective-permute-done.10 = f32[128,128]{1,0:T(8,128)S(1)} collective-permute-done((f32[128,128]{1,0:T(8,128)S(1)}, f32[128,128]{1,0:T(8,128)S(1)}, u32[]{:S(2)}, u32[]{:S(2)}) %collective-permute-start.10) | collective-permute-done | bytes 65568 | tf_op jit(solution)/shard_map/ppermute | solution.py:369
  43.1 4.7 %collective-permute-start.11 = (f32[128,128]{1,0:T(8,128)S(1)}, f32[128,128]{1,0:T(8,128)S(1)}, u32[]{:S(2)}, u32[]{:S(2)}) collective-permute-start(f32[128,128]{1,0:T(8,128)S(1)} %add.26), channel_id=1, source_target_pairs={{0,12},{1,129},{2,14},{3,131},{4,8},{5,133},{6,10},{7,135},{8,4},{... | collective-permute-start | bytes 196616 | tf_op jit(solution)/shard_map/ppermute | solution.py:369
  47.8 3.2 %collective-permute-done.11 = f32[128,128]{1,0:T(8,128)S(1)} collective-permute-done((f32[128,128]{1,0:T(8,128)S(1)}, f32[128,128]{1,0:T(8,128)S(1)}, u32[]{:S(2)}, u32[]{:S(2)}) %collective-permute-start.11) | collective-permute-done | bytes 65568 | tf_op jit(solution)/shard_map/ppermute | solution.py:369
  51.1 3.7 %collective-permute-start.12 = (f32[128,128]{1,0:T(8,128)S(1)}, f32[128,128]{1,0:T(8,128)S(1)}, u32[]{:S(2)}, u32[]{:S(2)}) collective-permute-start(f32[128,128]{1,0:T(8,128)S(1)} %add.27), channel_id=1, source_target_pairs={{0,130},{1,131},{2,128},{3,129},{4,134},{5,135},{6,132},{7,133},{8... | collective-permute-start | bytes 196616 | tf_op jit(solution)/shard_map/ppermute | solution.py:369
  54.7 1.7 %collective-permute-done.12 = f32[128,128]{1,0:T(8,128)S(1)} collective-permute-done((f32[128,128]{1,0:T(8,128)S(1)}, f32[128,128]{1,0:T(8,128)S(1)}, u32[]{:S(2)}, u32[]{:S(2)}) %collective-permute-start.12) | collective-permute-done | bytes 65568 | tf_op jit(solution)/shard_map/ppermute | solution.py:369
  56.4 0.0 collective-permute-done.13.rowa_ref
  56.4 0.0 collective-permute-done.14.rowb_ref
  56.4 0.1 collective-permute-start.15
  56.5 0.1 shard_map.92
  56.6 3.9 %collective-permute-done.15 = f32[128,128]{1,0:T(8,128)S(1)} collective-permute-done((f32[128,128]{1,0:T(8,128)S(1)}, f32[128,128]{1,0:T(8,128)S(1)}, u32[]{:S(2)}, u32[]{:S(2)}) %collective-permute-start.15) | collective-permute-done | bytes 65568 | tf_op jit(solution)/shard_map/ppermute | solution.py:369
  60.5 2.0 %collective-permute-start.18 = (f32[2,256,128]{2,1,0:T(8,128)S(1)}, f32[2,256,128]{2,1,0:T(8,128)S(1)}, u32[]{:S(2)}, u32[]{:S(2)}) collective-permute-start(f32[2,256,128]{2,1,0:T(8,128)S(1)} %get-tuple-element.63), channel_id=1, source_target_pairs={{0,1},{1,0},{2,3},{3,2},{4,5},{5,4},{6,7},{7,6},{8,9},{9,8},{10,11... | collective-permute-start | bytes 786440 | tf_op jit(solution)/shard_map/ppermute | solution.py:363
  62.6 0.1 collective-permute-start.19
  62.7 2.8 %collective-permute-start.16 = (f32[128,128]{1,0:T(8,128)S(1)}, f32[128,128]{1,0:T(8,128)S(1)}, u32[]{:S(2)}, u32[]{:S(2)}) collective-permute-start(f32[128,128]{1,0:T(8,128)S(1)} %add.29), channel_id=1, source_target_pairs={{0,32},{1,97},{2,34},{3,99},{4,36},{5,101},{6,38},{7,103},{8,40},{... | collective-permute-start | bytes 196616 | tf_op jit(solution)/shard_map/ppermute | solution.py:369
  65.6 3.0 %collective-permute-done.16 = f32[128,128]{1,0:T(8,128)S(1)} collective-permute-done((f32[128,128]{1,0:T(8,128)S(1)}, f32[128,128]{1,0:T(8,128)S(1)}, u32[]{:S(2)}, u32[]{:S(2)}) %collective-permute-start.16) | collective-permute-done | bytes 65568 | tf_op jit(solution)/shard_map/ppermute | solution.py:369
  68.6 0.4 collective-permute-start.17
  69.0 2.8 %collective-permute-done.17 = f32[128,128]{1,0:T(8,128)S(1)} collective-permute-done((f32[128,128]{1,0:T(8,128)S(1)}, f32[128,128]{1,0:T(8,128)S(1)}, u32[]{:S(2)}, u32[]{:S(2)}) %collective-permute-start.17) | collective-permute-done | bytes 65568 | tf_op jit(solution)/shard_map/ppermute | solution.py:369
  71.8 0.0 collective-permute-done.18.cola_ref
  71.9 0.0 collective-permute-done.19.colb_ref
  71.9 4.4 %collective-permute-start.20 = (f32[128,128]{1,0:T(8,128)S(1)}, f32[128,128]{1,0:T(8,128)S(1)}, u32[]{:S(2)}, u32[]{:S(2)}) collective-permute-start(f32[128,128]{1,0:T(8,128)S(1)} %add.31.mine_ref), channel_id=1, source_target_pairs={{0,1},{1,0},{2,3},{3,2},{4,5},{5,4},{6,7},{7,6},{8,9},{9,8},{10,11... | collective-permute-start | bytes 196616 | tf_op jit(solution)/shard_map/ppermute | solution.py:369
  76.3 1.2 %shard_map.93 = f32[2,2,256,256]{3,2,1,0:T(8,128)} custom-call(f32[2,2,256,256]{3,2,1,0:T(8,128)S(1)} %get-tuple-element.47.part_ref, f32[2,6,64,128]{3,2,1,0:T(8,128)S(1)} %collective-permute-done.13.rowa_ref, f32[2,6,64,128]{3,2,1,0:T(8,128)S(1)} %collective-permute-done.14.rowb_ref, f32[2,256,128]{2,1,0:T(8,128)S(1)} %collective-permute-done.18.cola_ref, ...), custom_call_target="tpu_custom_call" | custom-call | tf_op jit(solution)/shard_map/pallas_call | solution.py:373
  77.5 0.0 collective-permute-done.20.other_ref
  77.5 0.7 shard_map.94
  (10 shorter events, 0.1 us)
Async XLA Ops:
  0.6 10.7 %copy-start = (f32[2,2,256,256]{3,2,1,0:T(8,128)S(1)}, f32[2,2,256,256]{3,2,1,0:T(8,128)}, u32[]{:S(2)}) copy-start(f32[2,2,256,256]{3,2,1,0:T(8,128)} %obj_ref.11) | copy-start | bytes 3145732
  2.1 6.6 %collective-permute-start.4 = (f32[256,128]{1,0:T(8,128)S(1)}, f32[256,128]{1,0:T(8,128)S(1)}, u32[]{:S(2)}, u32[]{:S(2)}) collective-permute-start(f32[256,128]{1,0:T(8,128)S(1)} %get-tuple-element.39), channel_id=1, source_target_pairs={{0,1},{1,0},{2,3},{3,2},{4,5},{5,4},{6,7},{7,6},{8,9},{9,8},{10,11... | collective-permute-start | bytes 393224 | tf_op jit(solution)/shard_map/ppermute | solution.py:363
  5.4 5.9 %collective-permute-start.5 = (f32[256,128]{1,0:T(8,128)S(1)}, f32[256,128]{1,0:T(8,128)S(1)}, u32[]{:S(2)}, u32[]{:S(2)}) collective-permute-start(f32[256,128]{1,0:T(8,128)S(1)} %get-tuple-element.40), channel_id=1, source_target_pairs={{0,16},{1,2},{2,1},{3,4},{4,3},{5,6},{6,5},{7,8},{8,7},{9,10},{10,... | collective-permute-start | bytes 393224 | tf_op jit(solution)/shard_map/ppermute | solution.py:363
  6.6 5.0 %collective-permute-start = (f32[256,128]{1,0:T(8,128)S(1)}, f32[256,128]{1,0:T(8,128)S(1)}, u32[]{:S(2)}, u32[]{:S(2)}) collective-permute-start(f32[256,128]{1,0:T(8,128)S(1)} %get-tuple-element.35), channel_id=1, source_target_pairs={{0,1},{1,0},{2,3},{3,2},{4,5},{5,4},{6,7},{7,6},{8,9},{9,8},{10,11... | collective-permute-start | bytes 393224 | tf_op jit(solution)/shard_map/ppermute | solution.py:363
  6.6 11.7 %copy-start.1 = (bf16[4,2,256,256]{3,2,1,0:T(8,128)(2,1)S(1)}, bf16[4,2,256,256]{3,2,1,0:T(8,128)(2,1)}, u32[]{:S(2)}) copy-start(bf16[4,2,256,256]{3,2,1,0:T(8,128)(2,1)} %constant.2.clone.tabs_ref) | copy-start | bytes 3145732
  6.6 6.2 %collective-permute-start.1 = (f32[256,128]{1,0:T(8,128)S(1)}, f32[256,128]{1,0:T(8,128)S(1)}, u32[]{:S(2)}, u32[]{:S(2)}) collective-permute-start(f32[256,128]{1,0:T(8,128)S(1)} %get-tuple-element.36), channel_id=1, source_target_pairs={{0,16},{1,2},{2,1},{3,4},{4,3},{5,6},{6,5},{7,8},{8,7},{9,10},{10,... | collective-permute-start | bytes 393224 | tf_op jit(solution)/shard_map/ppermute | solution.py:363
  11.4 6.9 %collective-permute-start.6 = (f32[6,64,128]{2,1,0:T(8,128)S(1)}, f32[6,64,128]{2,1,0:T(8,128)S(1)}, u32[]{:S(2)}, u32[]{:S(2)}) collective-permute-start(f32[6,64,128]{2,1,0:T(8,128)S(1)} %get-tuple-element.41), channel_id=1, source_target_pairs={{0,16},{1,17},{2,18},{3,19},{4,20},{5,21},{6,22},{7,23},{8,24},{9,... | collective-permute-start | bytes 589832 | tf_op jit(solution)/shard_map/ppermute | solution.py:363
  11.5 6.8 %copy-start.2 = (f32[2,128,128]{2,1,0:T(8,128)S(1)}, f32[2,128,128]{2,1,0:T(8,128)}, u32[]{:S(2)}) copy-start(f32[2,128,128]{2,1,0:T(8,128)} %probe_ref.5) | copy-start | bytes 393220
  11.5 6.8 %collective-permute-start.7 = (f32[6,64,128]{2,1,0:T(8,128)S(1)}, f32[6,64,128]{2,1,0:T(8,128)S(1)}, u32[]{:S(2)}, u32[]{:S(2)}) collective-permute-start(f32[6,64,128]{2,1,0:T(8,128)S(1)} %get-tuple-element.42), channel_id=1, source_target_pairs={{0,1},{1,0},{2,3},{3,2},{4,5},{5,4},{6,7},{7,6},{8,9},{9,8},{10,11... | collective-permute-start | bytes 589832 | tf_op jit(solution)/shard_map/ppermute | solution.py:363
  12.8 9.1 %collective-permute-start.2 = (f32[6,64,128]{2,1,0:T(8,128)S(1)}, f32[6,64,128]{2,1,0:T(8,128)S(1)}, u32[]{:S(2)}, u32[]{:S(2)}) collective-permute-start(f32[6,64,128]{2,1,0:T(8,128)S(1)} %get-tuple-element.37), channel_id=1, source_target_pairs={{0,16},{1,17},{2,18},{3,19},{4,20},{5,21},{6,22},{7,23},{8,24},{9,... | collective-permute-start | bytes 589832 | tf_op jit(solution)/shard_map/ppermute | solution.py:363
  14.8 3.5 %copy-start.4 = (s32[1,8]{1,0:T(1,128)S(1)}, s32[1,8]{1,0:T(1,128)}, u32[]{:S(2)}) copy-start(s32[1,8]{1,0:T(1,128)} %row_ref.5) | copy-start | bytes 100
  14.8 3.5 %copy-start.5 = (s32[1,8]{1,0:T(1,128)S(1)}, s32[1,8]{1,0:T(1,128)}, u32[]{:S(2)}) copy-start(s32[1,8]{1,0:T(1,128)} %col_ref.5) | copy-start | bytes 100
  14.8 7.2 %collective-permute-start.3 = (f32[6,64,128]{2,1,0:T(8,128)S(1)}, f32[6,64,128]{2,1,0:T(8,128)S(1)}, u32[]{:S(2)}, u32[]{:S(2)}) collective-permute-start(f32[6,64,128]{2,1,0:T(8,128)S(1)} %get-tuple-element.38), channel_id=1, source_target_pairs={{0,1},{1,0},{2,3},{3,2},{4,5},{5,4},{6,7},{7,6},{8,9},{9,8},{10,11... | collective-permute-start | bytes 589832 | tf_op jit(solution)/shard_map/ppermute | solution.py:363
  15.5 6.5 %copy-start.3 = (f32[1,8,128,128]{3,2,1,0:T(8,128)S(1)}, f32[1,8,128,128]{3,2,1,0:T(8,128)}, u32[]{:S(2)}) copy-start(f32[1,8,128,128]{3,2,1,0:T(8,128)} %param.9) | copy-start | bytes 1572868
  27.8 1.4 %collective-permute-start.8 = (f32[128,128]{1,0:T(8,128)S(1)}, f32[128,128]{1,0:T(8,128)S(1)}, u32[]{:S(2)}, u32[]{:S(2)}) collective-permute-start(f32[128,128]{1,0:T(8,128)S(1)} %get-tuple-element.49), channel_id=1, source_target_pairs={{0,1},{1,0},{2,3},{3,2},{4,5},{5,4},{6,7},{7,6},{8,9},{9,8},{10,11... | collective-permute-start | bytes 196616 | tf_op jit(solution)/shard_map/ppermute | solution.py:369
  29.2 4.2 %collective-permute-start.9 = (f32[128,128]{1,0:T(8,128)S(1)}, f32[128,128]{1,0:T(8,128)S(1)}, u32[]{:S(2)}, u32[]{:S(2)}) collective-permute-start(f32[128,128]{1,0:T(8,128)S(1)} %add.24), channel_id=1, source_target_pairs={{0,128},{1,5},{2,130},{3,7},{4,132},{5,1},{6,134},{7,3},{8,136},{9... | collective-permute-start | bytes 196616 | tf_op jit(solution)/shard_map/ppermute | solution.py:369
  33.5 22.9 %collective-permute-start.13 = (f32[2,6,64,128]{3,2,1,0:T(8,128)S(1)}, f32[2,6,64,128]{3,2,1,0:T(8,128)S(1)}, u32[]{:S(2)}, u32[]{:S(2)}) collective-permute-start(f32[2,6,64,128]{3,2,1,0:T(8,128)S(1)} %get-tuple-element.53), channel_id=1, source_target_pairs={{0,16},{1,17},{2,18},{3,19},{4,20},{5,21},{6,22},{7,23},{8,24},{9,... | collective-permute-start | bytes 1179656 | tf_op jit(solution)/shard_map/ppermute | solution.py:363
  36.9 19.6 %collective-permute-start.14 = (f32[2,6,64,128]{3,2,1,0:T(8,128)S(1)}, f32[2,6,64,128]{3,2,1,0:T(8,128)S(1)}, u32[]{:S(2)}, u32[]{:S(2)}) collective-permute-start(f32[2,6,64,128]{3,2,1,0:T(8,128)S(1)} %get-tuple-element.54), channel_id=1, source_target_pairs={{0,1},{1,0},{2,3},{3,2},{4,5},{5,4},{6,7},{7,6},{8,9},{9,8},{10,11... | collective-permute-start | bytes 1179656 | tf_op jit(solution)/shard_map/ppermute | solution.py:363
  37.2 5.9 %collective-permute-start.10 = (f32[128,128]{1,0:T(8,128)S(1)}, f32[128,128]{1,0:T(8,128)S(1)}, u32[]{:S(2)}, u32[]{:S(2)}) collective-permute-start(f32[128,128]{1,0:T(8,128)S(1)} %add.25), channel_id=1, source_target_pairs={{0,4},{1,13},{2,6},{3,15},{4,0},{5,9},{6,2},{7,11},{8,12},{9,5},{1... | collective-permute-start | bytes 196616 | tf_op jit(solution)/shard_map/ppermute | solution.py:369
  43.1 7.9 %collective-permute-start.11 = (f32[128,128]{1,0:T(8,128)S(1)}, f32[128,128]{1,0:T(8,128)S(1)}, u32[]{:S(2)}, u32[]{:S(2)}) collective-permute-start(f32[128,128]{1,0:T(8,128)S(1)} %add.26), channel_id=1, source_target_pairs={{0,12},{1,129},{2,14},{3,131},{4,8},{5,133},{6,10},{7,135},{8,4},{... | collective-permute-start | bytes 196616 | tf_op jit(solution)/shard_map/ppermute | solution.py:369
  51.1 5.3 %collective-permute-start.12 = (f32[128,128]{1,0:T(8,128)S(1)}, f32[128,128]{1,0:T(8,128)S(1)}, u32[]{:S(2)}, u32[]{:S(2)}) collective-permute-start(f32[128,128]{1,0:T(8,128)S(1)} %add.27), channel_id=1, source_target_pairs={{0,130},{1,131},{2,128},{3,129},{4,134},{5,135},{6,132},{7,133},{8... | collective-permute-start | bytes 196616 | tf_op jit(solution)/shard_map/ppermute | solution.py:369
  56.4 4.1 %collective-permute-start.15 = (f32[128,128]{1,0:T(8,128)S(1)}, f32[128,128]{1,0:T(8,128)S(1)}, u32[]{:S(2)}, u32[]{:S(2)}) collective-permute-start(f32[128,128]{1,0:T(8,128)S(1)} %add.28), channel_id=1, source_target_pairs={{0,16},{1,33},{2,18},{3,35},{4,20},{5,37},{6,22},{7,39},{8,24},{9,... | collective-permute-start | bytes 196616 | tf_op jit(solution)/shard_map/ppermute | solution.py:369
  60.5 11.3 %collective-permute-start.18 = (f32[2,256,128]{2,1,0:T(8,128)S(1)}, f32[2,256,128]{2,1,0:T(8,128)S(1)}, u32[]{:S(2)}, u32[]{:S(2)}) collective-permute-start(f32[2,256,128]{2,1,0:T(8,128)S(1)} %get-tuple-element.63), channel_id=1, source_target_pairs={{0,1},{1,0},{2,3},{3,2},{4,5},{5,4},{6,7},{7,6},{8,9},{9,8},{10,11... | collective-permute-start | bytes 786440 | tf_op jit(solution)/shard_map/ppermute | solution.py:363
  62.6 9.3 %collective-permute-start.19 = (f32[2,256,128]{2,1,0:T(8,128)S(1)}, f32[2,256,128]{2,1,0:T(8,128)S(1)}, u32[]{:S(2)}, u32[]{:S(2)}) collective-permute-start(f32[2,256,128]{2,1,0:T(8,128)S(1)} %get-tuple-element.64), channel_id=1, source_target_pairs={{0,16},{1,2},{2,1},{3,4},{4,3},{5,6},{6,5},{7,8},{8,7},{9,10},{10,... | collective-permute-start | bytes 786440 | tf_op jit(solution)/shard_map/ppermute | solution.py:363
  62.7 5.9 %collective-permute-start.16 = (f32[128,128]{1,0:T(8,128)S(1)}, f32[128,128]{1,0:T(8,128)S(1)}, u32[]{:S(2)}, u32[]{:S(2)}) collective-permute-start(f32[128,128]{1,0:T(8,128)S(1)} %add.29), channel_id=1, source_target_pairs={{0,32},{1,97},{2,34},{3,99},{4,36},{5,101},{6,38},{7,103},{8,40},{... | collective-permute-start | bytes 196616 | tf_op jit(solution)/shard_map/ppermute | solution.py:369
  68.6 3.2 %collective-permute-start.17 = (f32[128,128]{1,0:T(8,128)S(1)}, f32[128,128]{1,0:T(8,128)S(1)}, u32[]{:S(2)}, u32[]{:S(2)}) collective-permute-start(f32[128,128]{1,0:T(8,128)S(1)} %add.30), channel_id=1, source_target_pairs={{0,96},{1,17},{2,98},{3,19},{4,100},{5,21},{6,102},{7,23},{8,104},... | collective-permute-start | bytes 196616 | tf_op jit(solution)/shard_map/ppermute | solution.py:369
  71.9 5.6 %collective-permute-start.20 = (f32[128,128]{1,0:T(8,128)S(1)}, f32[128,128]{1,0:T(8,128)S(1)}, u32[]{:S(2)}, u32[]{:S(2)}) collective-permute-start(f32[128,128]{1,0:T(8,128)S(1)} %add.31.mine_ref), channel_id=1, source_target_pairs={{0,1},{1,0},{2,3},{3,2},{4,5},{5,4},{6,7},{7,6},{8,9},{9,8},{10,11... | collective-permute-start | bytes 196616 | tf_op jit(solution)/shard_map/ppermute | solution.py:369

commit v13 on v12

--- a/solution.py
+++ b/solution.py
@@ -86,20 +86,17 @@
     return before, after
 
 
-def pack_kernel(obj_ref, *refs):
-    *outs, held, sems = refs
-    first = lax.broadcasted_iota(jnp.int32, (held.shape[2], LANES), 1) < LANES // 2
-    copies = [pltpu.make_async_copy(obj_ref.at[p], held.at[p], sems.at[p]) for p in range(2)]
-    for copy in copies:
-        copy.start()
-    for piece in range(2):
-        copies[piece].wait()
-        left, right = columns(held.at[piece], first)
-        outs[2 * piece][...] = pick(1, right, left)
-        outs[2 * piece + 1][...] = pick(1, left, right)
-
-
-def rows_kernel(obj_ref, cola_ref, colb_ref, rowa_ref, rowb_ref, *, piece):
+def pack_kernel(obj_ref, colb_ref, cola_ref, held, sem, *, piece):
+    first = lax.broadcasted_iota(jnp.int32, (held.shape[1], LANES), 1) < LANES // 2
+    copy = pltpu.make_async_copy(obj_ref.at[piece], held, sem)
+    copy.start()
+    copy.wait()
+    left, right = columns(held, first)
+    cola_ref[...] = pick(1, right, left)
+    colb_ref[...] = pick(1, left, right)
+
+
+def rows_kernel(obj_ref, colb_ref, cola_ref, rowb_ref, rowa_ref, *, piece):
     half = LANES // 2
     low, high = slice(0, half), slice(obj_ref.shape[2] - half, obj_ref.shape[2])
     for part in range(2):
@@ -115,7 +112,7 @@
         rowb_ref[place] = pick(0, top, bottom)
 
 
-def grow(ext, piece_ref, cola_ref, colb_ref, rowa_ref, rowb_ref):
+def grow(ext, piece_ref, colb_ref, cola_ref, rowb_ref, rowa_ref):
     half = LANES // 2
     tile = piece_ref.shape[1]
     sides = beside(1, cola_ref[...], colb_ref[...])
@@ -167,11 +164,11 @@
 
 
 def first_kernel(
-    row_ref, col_ref, obj_ref, cola_ref, colb_ref, rowa_ref, rowb_ref, probe_ref, tabs_ref,
+    row_ref, col_ref, obj_ref, colb_ref, cola_ref, rowb_ref, rowa_ref, probe_ref, tabs_ref,
     win_ref, mid_ref, ext, *, group,
 ):
     width = probe_ref.shape[1]
-    grow(ext, obj_ref.at[0], cola_ref, colb_ref, rowa_ref, rowb_ref)
+    grow(ext, obj_ref.at[0], colb_ref, cola_ref, rowb_ref, rowa_ref)
 
     def some(index, _):
         slots = [group * index + place for place in range(group)]
@@ -187,13 +184,13 @@
 
 
 def second_kernel(
-    row_ref, col_ref, live_ref, obj_ref, cola_ref, colb_ref, rowa_ref, rowb_ref,
+    row_ref, col_ref, live_ref, obj_ref, colb_ref, cola_ref, rowb_ref, rowa_ref,
     win_ref, mid_ref, measured_ref, tabs_ref,
     grad_ref, down_ref, keep_ref, send_ref,
     ext, sum_ref, *, group,
 ):
     width = win_ref.shape[2]
-    grow(ext, obj_ref.at[1], cola_ref, colb_ref, rowa_ref, rowb_ref)
+    grow(ext, obj_ref.at[1], colb_ref, cola_ref, rowb_ref, rowa_ref)
     sum_ref[...] = jnp.zeros_like(sum_ref)
 
     def some(index, _):
@@ -235,7 +232,7 @@
 
 def place_kernel(
     row_ref, col_ref, obj_ref, probe_ref, down_ref, second_ref,
-    new_ref, rowa_ref, rowb_ref, left_ref, right_ref,
+    new_ref, rowb_ref, rowa_ref, left_ref, right_ref,
     grad,
 ):
     width = probe_ref.shape[1]
@@ -283,7 +280,7 @@
             ref[piece] = strip[half : half + tile]
 
 
-def fold_kernel(left_ref, right_ref, rowa_ref, rowb_ref, cola_ref, colb_ref):
+def fold_kernel(left_ref, right_ref, rowb_ref, rowa_ref, colb_ref, cola_ref):
     half = LANES // 2
     tile = left_ref.shape[1]
     for piece in range(2):
@@ -303,7 +300,7 @@
 
 
 def finish_kernel(
-    part_ref, rowa_ref, rowb_ref, cola_ref, colb_ref, new_ref,
+    part_ref, rowb_ref, rowa_ref, colb_ref, cola_ref, new_ref,
 ):
     tile = part_ref.shape[2]
     half = LANES // 2
@@ -350,7 +347,7 @@
 def meet(strips, axis):
     sizes = (lax.axis_size("row"), lax.axis_size("col"))
     got = []
-    for odd, strip in enumerate(strips):
+    for odd, strip in zip((1, 0), strips):
         pairs = []
         for spot in np.ndindex(*sizes):
             other = list(spot)
@@ -386,14 +383,17 @@
     field, fields = array(2, 2, tile, tile), array(count, 2, width, width)
     tabs = jnp.asarray(make_tables(width))
     grown = pltpu.VMEM((2, 4, tile + width, LANES), jnp.float32)
-    packed = pl.pallas_call(
-        pack_kernel, out_shape=tuple([array(*side)] * 4),
-        in_specs=[pl.BlockSpec(memory_space=pltpu.HBM)], out_specs=tuple(vmem(4)),
-        scratch_shapes=[pltpu.VMEM(object_field.shape, jnp.float32), pltpu.SemaphoreType.DMA((2,))],
-        compiler_params=pltpu.CompilerParams(vmem_limit_bytes=GRANT),
-    )(pltpu.with_memory_space_constraint(object_field, pltpu.HBM))
+    packed = [
+        pl.pallas_call(
+            functools.partial(pack_kernel, piece=piece), out_shape=tuple([array(*side)] * 2),
+            in_specs=[pl.BlockSpec(memory_space=pltpu.HBM)], out_specs=tuple(vmem(2)),
+            scratch_shapes=[pltpu.VMEM((2, tile, tile), jnp.float32), pltpu.SemaphoreType.DMA],
+            compiler_params=pltpu.CompilerParams(vmem_limit_bytes=GRANT),
+        )(pltpu.with_memory_space_constraint(object_field, pltpu.HBM))
+        for piece in range(2)
+    ]
     halos = []
-    cols = [meet(packed[2 * piece : 2 * piece + 2], 1) for piece in range(2)]
+    cols = [meet(packed[piece], 1) for piece in range(2)]
     for piece in range(2):
         strips = call(
             functools.partial(rows_kernel, piece=piece), [array(*edge)] * 2,

time: 78.3 us -> 84.9 us (1.084)
  starting transfers between devices: 37.4 us -> 45.3 us
  waiting for transfers between devices: 25.3 us -> 22.9 us
  Pallas kernels: 13.8 us -> 14.9 us
    ppermute x12, starting transfers between devices: 14.6 us -> 29.2 us  [meet(): got.append(lax.ppermute(strip, BOTH, pairs))]
    ppermute x9, starting transfers between devices: 22.8 us -> 16.1 us  [swap(): lax.ppermute(value, BOTH, [(i, i ^ masks[i % 2]) for i in range(count)])]
    ppermute x12, waiting for transfers between devices: 8.08 us -> 1.71 us  [meet(): got.append(lax.ppermute(strip, BOTH, pairs))]
    ppermute x9, waiting for transfers between devices: 17.2 us -> 21.2 us  [swap(): lax.ppermute(value, BOTH, [(i, i ^ masks[i % 2]) for i in range(count)])]
    pallas_call x1 -> x2, Pallas kernels: 1.44 us -> 2.46 us  [on_device(): pl.pallas_call(functools.partial(pack_kernel, piece=piece), out_shape=tup...]
  transfers between devices with their start and end apart: 21 -> 21, of which waited for: 11 -> 9; matrix products, arithmetic and copies ran while one was open for 0% -> 0% of each run, Pallas kernels for 8% -> 8%
where the time goes in v13:
time: 84.9 us; the launch traced here: 84.6 us
  starting transfers between devices  45.3 us (53%)
  waiting for transfers between devices  22.9 us (27%)
  Pallas kernels  14.9 us (18%)
  between operations  1.49 us (2%)
    ppermute x12, starting transfers between devices, meet(): got.append(lax.ppermute(strip, BOTH, pairs))  29.2 us
    ppermute x9, waiting for transfers between devices, swap(): lax.ppermute(value, BOTH, [(i, i ^ masks[i % 2]) for i in range(count)])  21.2 us
    ppermute x9, starting transfers between devices, swap(): lax.ppermute(value, BOTH, [(i, i ^ masks[i % 2]) for i in range(count)])  16.1 us
    pallas_call x8, Pallas kernels, call(): pl.pallas_call(kernel, out_shape=tuple(out_shape), in_specs=smem(len(scal...  12.4 us
    pallas_call x2, Pallas kernels, on_device(): pl.pallas_call(functools.partial(pack_kernel, piece=piece), out_shape=tup...  2.46 us
    ppermute x12, waiting for transfers between devices, meet(): got.append(lax.ppermute(strip, BOTH, pairs))  1.71 us
  transfers between devices with their start and end apart: 21, of which 9 were waited for; matrix products, arithmetic and copies ran while one was open for 0% of the time, Pallas kernels for 8%

profile of v13, /device:TPU:1, one launch (start us, length us, event | category | flops | bytes accessed | tf_op | source)
XLA Modules:
  0.0 84.6 jit_solution(7233952213397509711)
XLA Ops:
  0.6 0.0 copy-start
  0.6 1.3 %shard_map.88 = (f32[256,128]{1,0:T(8,128)S(1)}, f32[256,128]{1,0:T(8,128)S(1)}) custom-call(f32[2,2,256,256]{3,2,1,0:T(8,128)} %obj_ref.13), custom_call_target="tpu_custom_call" | custom-call | tf_op jit(solution)/shard_map/pallas_call | solution.py:387
  1.9 4.4 %collective-permute-start.4 = (f32[256,128]{1,0:T(8,128)S(1)}, f32[256,128]{1,0:T(8,128)S(1)}, u32[]{:S(2)}, u32[]{:S(2)}) collective-permute-start(f32[256,128]{1,0:T(8,128)S(1)} %get-tuple-element.39), channel_id=1, source_target_pairs={{0,16},{1,2},{2,1},{3,4},{4,3},{5,6},{6,5},{7,8},{8,7},{9,10},{10,... | collective-permute-start | bytes 393224 | tf_op jit(solution)/shard_map/ppermute | solution.py:360
  6.3 0.0 collective-permute-start.5
  6.3 1.2 %shard_map.86 = (f32[256,128]{1,0:T(8,128)S(1)}, f32[256,128]{1,0:T(8,128)S(1)}) custom-call(f32[2,2,256,256]{3,2,1,0:T(8,128)} %obj_ref.13), custom_call_target="tpu_custom_call" | custom-call | tf_op jit(solution)/shard_map/pallas_call | solution.py:387
  7.5 1.5 %collective-permute-start = (f32[256,128]{1,0:T(8,128)S(1)}, f32[256,128]{1,0:T(8,128)S(1)}, u32[]{:S(2)}, u32[]{:S(2)}) collective-permute-start(f32[256,128]{1,0:T(8,128)S(1)} %get-tuple-element.35), channel_id=1, source_target_pairs={{0,16},{1,2},{2,1},{3,4},{4,3},{5,6},{6,5},{7,8},{8,7},{9,10},{10,... | collective-permute-start | bytes 393224 | tf_op jit(solution)/shard_map/ppermute | solution.py:360
  9.0 0.0 copy-start.1
  9.0 1.0 %collective-permute-start.1 = (f32[256,128]{1,0:T(8,128)S(1)}, f32[256,128]{1,0:T(8,128)S(1)}, u32[]{:S(2)}, u32[]{:S(2)}) collective-permute-start(f32[256,128]{1,0:T(8,128)S(1)} %get-tuple-element.36), channel_id=1, source_target_pairs={{0,1},{1,0},{2,3},{3,2},{4,5},{5,4},{6,7},{7,6},{8,9},{9,8},{10,11... | collective-permute-start | bytes 393224 | tf_op jit(solution)/shard_map/ppermute | solution.py:360
  10.0 0.0 collective-permute-done.4.colb_ref
  10.0 0.0 collective-permute-done.5.cola_ref
  10.0 0.0 copy-done
  10.1 0.3 collective-permute-start.6
  10.4 0.0 copy-start.2
  10.4 3.1 %collective-permute-start.7 = (f32[6,64,128]{2,1,0:T(8,128)S(1)}, f32[6,64,128]{2,1,0:T(8,128)S(1)}, u32[]{:S(2)}, u32[]{:S(2)}) collective-permute-start(f32[6,64,128]{2,1,0:T(8,128)S(1)} %get-tuple-element.42), channel_id=1, source_target_pairs={{0,16},{1,17},{2,18},{3,19},{4,20},{5,21},{6,22},{7,23},{8,24},{9,... | collective-permute-start | bytes 589832 | tf_op jit(solution)/shard_map/ppermute | solution.py:360
  13.5 0.0 collective-permute-done.colb_ref
  13.5 0.0 collective-permute-done.1.cola_ref
  13.5 0.6 collective-permute-start.2
  14.2 0.0 copy-start.4
  14.2 0.0 copy-start.5
  14.2 3.5 %collective-permute-start.3 = (f32[6,64,128]{2,1,0:T(8,128)S(1)}, f32[6,64,128]{2,1,0:T(8,128)S(1)}, u32[]{:S(2)}, u32[]{:S(2)}) collective-permute-start(f32[6,64,128]{2,1,0:T(8,128)S(1)} %get-tuple-element.38), channel_id=1, source_target_pairs={{0,16},{1,17},{2,18},{3,19},{4,20},{5,21},{6,22},{7,23},{8,24},{9,... | collective-permute-start | bytes 589832 | tf_op jit(solution)/shard_map/ppermute | solution.py:360
  18.3 0.0 copy-start.3
  18.3 0.0 collective-permute-done.6.rowb_ref
  18.4 0.1 collective-permute-done.7.rowa_ref
  18.5 0.0 copy-done.1
  18.5 0.0 copy-done.2
  18.5 0.0 copy-done.4
  18.5 0.0 copy-done.5
  18.5 2.2 %shard_map.90 = (f32[8,2,128,128]{3,2,1,0:T(8,128)S(1)}, f32[8,2,128,128]{3,2,1,0:T(8,128)S(1)}) custom-call(s32[1,8]{1,0:T(1,128)S(1)} %copy-done.4, s32[1,8]{1,0:T(1,128)S(1)} %copy-done.5, f32[2,2,256,256]{3,2,1,0:T(8,128)S(1)} %copy-done, f32[256,128]{1,0:T(8,128)S(1)} %collective-permute-done.4.colb_ref, ...), custom_call_target="tpu_custom_call" | custom-call | tf_op jit(solution)/shard_map/pallas_call | solution.py:370
  20.7 0.0 collective-permute-done.2.rowb_ref
  20.8 1.5 %collective-permute-done.3.rowa_ref = f32[6,64,128]{2,1,0:T(8,128)S(1)} collective-permute-done((f32[6,64,128]{2,1,0:T(8,128)S(1)}, f32[6,64,128]{2,1,0:T(8,128)S(1)}, u32[]{:S(2)}, u32[]{:S(2)}) %collective-permute-start.3) | collective-permute-done | bytes 196640 | tf_op jit(solution)/shard_map/ppermute | solution.py:360
  22.2 0.0 copy-done.3
  22.3 5.8 %shard_map.91 = (f32[8,2,128,128]{3,2,1,0:T(8,128)S(1)}, f32[8,2,128,128]{3,2,1,0:T(8,128)S(1)}, f32[128,128]{1,0:T(8,128)S(1)}, f32[128,128]{1,0:T(8,128)S(1)}) custom-call(s32[1,8]{1,0:T(1,128)S(1)} %copy-done.4, s32[1,8]{1,0:T(1,128)S(1)} %copy-done.5, s32[1,1]{1,0:T(1,128)S(6)} %copy.9.live_ref, f32[2,2,256,256]{3,2,1,0:T(8,128)S(1)} %copy-done, ...), custom_call_target="tpu_custom_call" | custom-call | tf_op jit(solution)/shard_map/pallas_call | solution.py:370
  28.1 1.4 %collective-permute-start.8 = (f32[128,128]{1,0:T(8,128)S(1)}, f32[128,128]{1,0:T(8,128)S(1)}, u32[]{:S(2)}, u32[]{:S(2)}) collective-permute-start(f32[128,128]{1,0:T(8,128)S(1)} %get-tuple-element.49), channel_id=1, source_target_pairs={{0,1},{1,0},{2,3},{3,2},{4,5},{5,4},{6,7},{7,6},{8,9},{9,8},{10,11... | collective-permute-start | bytes 196616 | tf_op jit(solution)/shard_map/ppermute | solution.py:366
  29.5 0.9 %collective-permute-done.8 = f32[128,128]{1,0:T(8,128)S(1)} collective-permute-done((f32[128,128]{1,0:T(8,128)S(1)}, f32[128,128]{1,0:T(8,128)S(1)}, u32[]{:S(2)}, u32[]{:S(2)}) %collective-permute-start.8) | collective-permute-done | bytes 65568 | tf_op jit(solution)/shard_map/ppermute | solution.py:366
  30.4 2.2 %collective-permute-start.9 = (f32[128,128]{1,0:T(8,128)S(1)}, f32[128,128]{1,0:T(8,128)S(1)}, u32[]{:S(2)}, u32[]{:S(2)}) collective-permute-start(f32[128,128]{1,0:T(8,128)S(1)} %add.24), channel_id=1, source_target_pairs={{0,128},{1,5},{2,130},{3,7},{4,132},{5,1},{6,134},{7,3},{8,136},{9... | collective-permute-start | bytes 196616 | tf_op jit(solution)/shard_map/ppermute | solution.py:366
  32.6 2.3 %shard_map.92 = (f32[2,2,256,256]{3,2,1,0:T(8,128)S(1)}, f32[2,6,64,128]{3,2,1,0:T(8,128)S(1)}, f32[2,6,64,128]{3,2,1,0:T(8,128)S(1)}, f32[2,256,128]{2,1,0:T(8,128)S(1)}, f32[2,256,128]{2,1,0:T(8,128)S(1)}) custom-call(s32[1,8]{1,0:T(1,128)S(1)} %copy-done.4, s32[1,8]{1,0:T(1,128)S(1)} %copy-done.5, f32[2,2,256,256]{3,2,1,0:T(8,128)S(1)} %copy-done, ...), custom_call_target="tpu_custom_call" | custom-call | tf_op jit(solution)/shard_map/pallas_call | solution.py:370
  34.9 0.0 collective-permute-done.9
  34.9 3.3 %collective-permute-start.13 = (f32[2,6,64,128]{3,2,1,0:T(8,128)S(1)}, f32[2,6,64,128]{3,2,1,0:T(8,128)S(1)}, u32[]{:S(2)}, u32[]{:S(2)}) collective-permute-start(f32[2,6,64,128]{3,2,1,0:T(8,128)S(1)} %get-tuple-element.53), channel_id=1, source_target_pairs={{0,1},{1,0},{2,3},{3,2},{4,5},{5,4},{6,7},{7,6},{8,9},{9,8},{10,11... | collective-permute-start | bytes 1179656 | tf_op jit(solution)/shard_map/ppermute | solution.py:360
  38.2 1.2 %collective-permute-start.14 = (f32[2,6,64,128]{3,2,1,0:T(8,128)S(1)}, f32[2,6,64,128]{3,2,1,0:T(8,128)S(1)}, u32[]{:S(2)}, u32[]{:S(2)}) collective-permute-start(f32[2,6,64,128]{3,2,1,0:T(8,128)S(1)} %get-tuple-element.54), channel_id=1, source_target_pairs={{0,16},{1,17},{2,18},{3,19},{4,20},{5,21},{6,22},{7,23},{8,24},{9,... | collective-permute-start | bytes 1179656 | tf_op jit(solution)/shard_map/ppermute | solution.py:360
  39.4 2.4 %collective-permute-start.10 = (f32[128,128]{1,0:T(8,128)S(1)}, f32[128,128]{1,0:T(8,128)S(1)}, u32[]{:S(2)}, u32[]{:S(2)}) collective-permute-start(f32[128,128]{1,0:T(8,128)S(1)} %add.25), channel_id=1, source_target_pairs={{0,4},{1,13},{2,6},{3,15},{4,0},{5,9},{6,2},{7,11},{8,12},{9,5},{1... | collective-permute-start | bytes 196616 | tf_op jit(solution)/shard_map/ppermute | solution.py:366
  41.9 1.9 %collective-permute-done.10 = f32[128,128]{1,0:T(8,128)S(1)} collective-permute-done((f32[128,128]{1,0:T(8,128)S(1)}, f32[128,128]{1,0:T(8,128)S(1)}, u32[]{:S(2)}, u32[]{:S(2)}) %collective-permute-start.10) | collective-permute-done | bytes 65568 | tf_op jit(solution)/shard_map/ppermute | solution.py:366
  43.8 3.0 %collective-permute-start.11 = (f32[128,128]{1,0:T(8,128)S(1)}, f32[128,128]{1,0:T(8,128)S(1)}, u32[]{:S(2)}, u32[]{:S(2)}) collective-permute-start(f32[128,128]{1,0:T(8,128)S(1)} %add.26), channel_id=1, source_target_pairs={{0,12},{1,129},{2,14},{3,131},{4,8},{5,133},{6,10},{7,135},{8,4},{... | collective-permute-start | bytes 196616 | tf_op jit(solution)/shard_map/ppermute | solution.py:366
  46.7 4.9 %collective-permute-done.11 = f32[128,128]{1,0:T(8,128)S(1)} collective-permute-done((f32[128,128]{1,0:T(8,128)S(1)}, f32[128,128]{1,0:T(8,128)S(1)}, u32[]{:S(2)}, u32[]{:S(2)}) %collective-permute-start.11) | collective-permute-done | bytes 65568 | tf_op jit(solution)/shard_map/ppermute | solution.py:366
  51.7 2.8 %collective-permute-start.12 = (f32[128,128]{1,0:T(8,128)S(1)}, f32[128,128]{1,0:T(8,128)S(1)}, u32[]{:S(2)}, u32[]{:S(2)}) collective-permute-start(f32[128,128]{1,0:T(8,128)S(1)} %add.27), channel_id=1, source_target_pairs={{0,130},{1,131},{2,128},{3,129},{4,134},{5,135},{6,132},{7,133},{8... | collective-permute-start | bytes 196616 | tf_op jit(solution)/shard_map/ppermute | solution.py:366
  54.4 1.7 %collective-permute-done.12 = f32[128,128]{1,0:T(8,128)S(1)} collective-permute-done((f32[128,128]{1,0:T(8,128)S(1)}, f32[128,128]{1,0:T(8,128)S(1)}, u32[]{:S(2)}, u32[]{:S(2)}) %collective-permute-start.12) | collective-permute-done | bytes 65568 | tf_op jit(solution)/shard_map/ppermute | solution.py:366
  56.1 0.0 collective-permute-done.13.rowb_ref
  56.1 0.0 collective-permute-done.14.rowa_ref
  56.1 0.1 collective-permute-start.15
  56.2 0.1 shard_map.93
  56.3 3.9 %collective-permute-done.15 = f32[128,128]{1,0:T(8,128)S(1)} collective-permute-done((f32[128,128]{1,0:T(8,128)S(1)}, f32[128,128]{1,0:T(8,128)S(1)}, u32[]{:S(2)}, u32[]{:S(2)}) %collective-permute-start.15) | collective-permute-done | bytes 65568 | tf_op jit(solution)/shard_map/ppermute | solution.py:366
  60.2 10.1 %collective-permute-start.18 = (f32[2,256,128]{2,1,0:T(8,128)S(1)}, f32[2,256,128]{2,1,0:T(8,128)S(1)}, u32[]{:S(2)}, u32[]{:S(2)}) collective-permute-start(f32[2,256,128]{2,1,0:T(8,128)S(1)} %get-tuple-element.63), channel_id=1, source_target_pairs={{0,16},{1,2},{2,1},{3,4},{4,3},{5,6},{6,5},{7,8},{8,7},{9,10},{10,... | collective-permute-start | bytes 786440 | tf_op jit(solution)/shard_map/ppermute | solution.py:360
  70.3 0.2 collective-permute-start.19
  70.5 1.2 %collective-permute-start.16 = (f32[128,128]{1,0:T(8,128)S(1)}, f32[128,128]{1,0:T(8,128)S(1)}, u32[]{:S(2)}, u32[]{:S(2)}) collective-permute-start(f32[128,128]{1,0:T(8,128)S(1)} %add.29), channel_id=1, source_target_pairs={{0,32},{1,97},{2,34},{3,99},{4,36},{5,101},{6,38},{7,103},{8,40},{... | collective-permute-start | bytes 196616 | tf_op jit(solution)/shard_map/ppermute | solution.py:366
  71.8 5.3 %collective-permute-done.16 = f32[128,128]{1,0:T(8,128)S(1)} collective-permute-done((f32[128,128]{1,0:T(8,128)S(1)}, f32[128,128]{1,0:T(8,128)S(1)}, u32[]{:S(2)}, u32[]{:S(2)}) %collective-permute-start.16) | collective-permute-done | bytes 65568 | tf_op jit(solution)/shard_map/ppermute | solution.py:366
  77.1 0.7 collective-permute-start.17
  77.8 2.5 %collective-permute-done.17 = f32[128,128]{1,0:T(8,128)S(1)} collective-permute-done((f32[128,128]{1,0:T(8,128)S(1)}, f32[128,128]{1,0:T(8,128)S(1)}, u32[]{:S(2)}, u32[]{:S(2)}) %collective-permute-start.17) | collective-permute-done | bytes 65568 | tf_op jit(solution)/shard_map/ppermute | solution.py:366
  80.4 0.0 collective-permute-done.18.colb_ref
  80.4 0.0 collective-permute-done.19.cola_ref
  80.4 2.3 %collective-permute-start.20 = (f32[128,128]{1,0:T(8,128)S(1)}, f32[128,128]{1,0:T(8,128)S(1)}, u32[]{:S(2)}, u32[]{:S(2)}) collective-permute-start(f32[128,128]{1,0:T(8,128)S(1)} %add.31.mine_ref), channel_id=1, source_target_pairs={{0,1},{1,0},{2,3},{3,2},{4,5},{5,4},{6,7},{7,6},{8,9},{9,8},{10,11... | collective-permute-start | bytes 196616 | tf_op jit(solution)/shard_map/ppermute | solution.py:366
  82.7 1.2 %shard_map.94 = f32[2,2,256,256]{3,2,1,0:T(8,128)} custom-call(f32[2,2,256,256]{3,2,1,0:T(8,128)S(1)} %get-tuple-element.47.part_ref, f32[2,6,64,128]{3,2,1,0:T(8,128)S(1)} %collective-permute-done.13.rowb_ref, f32[2,6,64,128]{3,2,1,0:T(8,128)S(1)} %collective-permute-done.14.rowa_ref, f32[2,256,128]{2,1,0:T(8,128)S(1)} %collective-permute-done.18.colb_ref, ...), custom_call_target="tpu_custom_call" | custom-call | tf_op jit(solution)/shard_map/pallas_call | solution.py:370
  83.9 0.0 collective-permute-done.20.other_ref
  83.9 0.7 shard_map.95
  (10 shorter events, 0.2 us)
Async XLA Ops:
  0.6 9.4 %copy-start = (f32[2,2,256,256]{3,2,1,0:T(8,128)S(1)}, f32[2,2,256,256]{3,2,1,0:T(8,128)}, u32[]{:S(2)}) copy-start(f32[2,2,256,256]{3,2,1,0:T(8,128)} %obj_ref.13) | copy-start | bytes 3145732
  1.9 8.1 %collective-permute-start.4 = (f32[256,128]{1,0:T(8,128)S(1)}, f32[256,128]{1,0:T(8,128)S(1)}, u32[]{:S(2)}, u32[]{:S(2)}) collective-permute-start(f32[256,128]{1,0:T(8,128)S(1)} %get-tuple-element.39), channel_id=1, source_target_pairs={{0,16},{1,2},{2,1},{3,4},{4,3},{5,6},{6,5},{7,8},{8,7},{9,10},{10,... | collective-permute-start | bytes 393224 | tf_op jit(solution)/shard_map/ppermute | solution.py:360
  6.3 3.7 %collective-permute-start.5 = (f32[256,128]{1,0:T(8,128)S(1)}, f32[256,128]{1,0:T(8,128)S(1)}, u32[]{:S(2)}, u32[]{:S(2)}) collective-permute-start(f32[256,128]{1,0:T(8,128)S(1)} %get-tuple-element.40), channel_id=1, source_target_pairs={{0,1},{1,0},{2,3},{3,2},{4,5},{5,4},{6,7},{7,6},{8,9},{9,8},{10,11... | collective-permute-start | bytes 393224 | tf_op jit(solution)/shard_map/ppermute | solution.py:360
  7.5 6.0 %collective-permute-start = (f32[256,128]{1,0:T(8,128)S(1)}, f32[256,128]{1,0:T(8,128)S(1)}, u32[]{:S(2)}, u32[]{:S(2)}) collective-permute-start(f32[256,128]{1,0:T(8,128)S(1)} %get-tuple-element.35), channel_id=1, source_target_pairs={{0,16},{1,2},{2,1},{3,4},{4,3},{5,6},{6,5},{7,8},{8,7},{9,10},{10,... | collective-permute-start | bytes 393224 | tf_op jit(solution)/shard_map/ppermute | solution.py:360
  9.0 9.5 %copy-start.1 = (bf16[4,2,256,256]{3,2,1,0:T(8,128)(2,1)S(1)}, bf16[4,2,256,256]{3,2,1,0:T(8,128)(2,1)}, u32[]{:S(2)}) copy-start(bf16[4,2,256,256]{3,2,1,0:T(8,128)(2,1)} %constant.2.clone.tabs_ref) | copy-start | bytes 3145732
  9.0 4.5 %collective-permute-start.1 = (f32[256,128]{1,0:T(8,128)S(1)}, f32[256,128]{1,0:T(8,128)S(1)}, u32[]{:S(2)}, u32[]{:S(2)}) collective-permute-start(f32[256,128]{1,0:T(8,128)S(1)} %get-tuple-element.36), channel_id=1, source_target_pairs={{0,1},{1,0},{2,3},{3,2},{4,5},{5,4},{6,7},{7,6},{8,9},{9,8},{10,11... | collective-permute-start | bytes 393224 | tf_op jit(solution)/shard_map/ppermute | solution.py:360
  10.1 8.3 %collective-permute-start.6 = (f32[6,64,128]{2,1,0:T(8,128)S(1)}, f32[6,64,128]{2,1,0:T(8,128)S(1)}, u32[]{:S(2)}, u32[]{:S(2)}) collective-permute-start(f32[6,64,128]{2,1,0:T(8,128)S(1)} %get-tuple-element.41), channel_id=1, source_target_pairs={{0,1},{1,0},{2,3},{3,2},{4,5},{5,4},{6,7},{7,6},{8,9},{9,8},{10,11... | collective-permute-start | bytes 589832 | tf_op jit(solution)/shard_map/ppermute | solution.py:360
  10.4 8.2 %copy-start.2 = (f32[2,128,128]{2,1,0:T(8,128)S(1)}, f32[2,128,128]{2,1,0:T(8,128)}, u32[]{:S(2)}) copy-start(f32[2,128,128]{2,1,0:T(8,128)} %probe_ref.5) | copy-start | bytes 393220
  10.4 8.1 %collective-permute-start.7 = (f32[6,64,128]{2,1,0:T(8,128)S(1)}, f32[6,64,128]{2,1,0:T(8,128)S(1)}, u32[]{:S(2)}, u32[]{:S(2)}) collective-permute-start(f32[6,64,128]{2,1,0:T(8,128)S(1)} %get-tuple-element.42), channel_id=1, source_target_pairs={{0,16},{1,17},{2,18},{3,19},{4,20},{5,21},{6,22},{7,23},{8,24},{9,... | collective-permute-start | bytes 589832 | tf_op jit(solution)/shard_map/ppermute | solution.py:360
  13.5 7.2 %collective-permute-start.2 = (f32[6,64,128]{2,1,0:T(8,128)S(1)}, f32[6,64,128]{2,1,0:T(8,128)S(1)}, u32[]{:S(2)}, u32[]{:S(2)}) collective-permute-start(f32[6,64,128]{2,1,0:T(8,128)S(1)} %get-tuple-element.37), channel_id=1, source_target_pairs={{0,1},{1,0},{2,3},{3,2},{4,5},{5,4},{6,7},{7,6},{8,9},{9,8},{10,11... | collective-permute-start | bytes 589832 | tf_op jit(solution)/shard_map/ppermute | solution.py:360
  14.2 4.3 %copy-start.4 = (s32[1,8]{1,0:T(1,128)S(1)}, s32[1,8]{1,0:T(1,128)}, u32[]{:S(2)}) copy-start(s32[1,8]{1,0:T(1,128)} %row_ref.5) | copy-start | bytes 100
  14.2 4.3 %copy-start.5 = (s32[1,8]{1,0:T(1,128)S(1)}, s32[1,8]{1,0:T(1,128)}, u32[]{:S(2)}) copy-start(s32[1,8]{1,0:T(1,128)} %col_ref.5) | copy-start | bytes 100
  14.2 8.1 %collective-permute-start.3 = (f32[6,64,128]{2,1,0:T(8,128)S(1)}, f32[6,64,128]{2,1,0:T(8,128)S(1)}, u32[]{:S(2)}, u32[]{:S(2)}) collective-permute-start(f32[6,64,128]{2,1,0:T(8,128)S(1)} %get-tuple-element.38), channel_id=1, source_target_pairs={{0,16},{1,17},{2,18},{3,19},{4,20},{5,21},{6,22},{7,23},{8,24},{9,... | collective-permute-start | bytes 589832 | tf_op jit(solution)/shard_map/ppermute | solution.py:360
  18.3 3.9 %copy-start.3 = (f32[1,8,128,128]{3,2,1,0:T(8,128)S(1)}, f32[1,8,128,128]{3,2,1,0:T(8,128)}, u32[]{:S(2)}) copy-start(f32[1,8,128,128]{3,2,1,0:T(8,128)} %param.9) | copy-start | bytes 1572868
  28.1 2.3 %collective-permute-start.8 = (f32[128,128]{1,0:T(8,128)S(1)}, f32[128,128]{1,0:T(8,128)S(1)}, u32[]{:S(2)}, u32[]{:S(2)}) collective-permute-start(f32[128,128]{1,0:T(8,128)S(1)} %get-tuple-element.49), channel_id=1, source_target_pairs={{0,1},{1,0},{2,3},{3,2},{4,5},{5,4},{6,7},{7,6},{8,9},{9,8},{10,11... | collective-permute-start | bytes 196616 | tf_op jit(solution)/shard_map/ppermute | solution.py:366
  30.4 4.5 %collective-permute-start.9 = (f32[128,128]{1,0:T(8,128)S(1)}, f32[128,128]{1,0:T(8,128)S(1)}, u32[]{:S(2)}, u32[]{:S(2)}) collective-permute-start(f32[128,128]{1,0:T(8,128)S(1)} %add.24), channel_id=1, source_target_pairs={{0,128},{1,5},{2,130},{3,7},{4,132},{5,1},{6,134},{7,3},{8,136},{9... | collective-permute-start | bytes 196616 | tf_op jit(solution)/shard_map/ppermute | solution.py:366
  34.9 21.1 %collective-permute-start.13 = (f32[2,6,64,128]{3,2,1,0:T(8,128)S(1)}, f32[2,6,64,128]{3,2,1,0:T(8,128)S(1)}, u32[]{:S(2)}, u32[]{:S(2)}) collective-permute-start(f32[2,6,64,128]{3,2,1,0:T(8,128)S(1)} %get-tuple-element.53), channel_id=1, source_target_pairs={{0,1},{1,0},{2,3},{3,2},{4,5},{5,4},{6,7},{7,6},{8,9},{9,8},{10,11... | collective-permute-start | bytes 1179656 | tf_op jit(solution)/shard_map/ppermute | solution.py:360
  38.2 17.9 %collective-permute-start.14 = (f32[2,6,64,128]{3,2,1,0:T(8,128)S(1)}, f32[2,6,64,128]{3,2,1,0:T(8,128)S(1)}, u32[]{:S(2)}, u32[]{:S(2)}) collective-permute-start(f32[2,6,64,128]{3,2,1,0:T(8,128)S(1)} %get-tuple-element.54), channel_id=1, source_target_pairs={{0,16},{1,17},{2,18},{3,19},{4,20},{5,21},{6,22},{7,23},{8,24},{9,... | collective-permute-start | bytes 1179656 | tf_op jit(solution)/shard_map/ppermute | solution.py:360
  39.4 4.3 %collective-permute-start.10 = (f32[128,128]{1,0:T(8,128)S(1)}, f32[128,128]{1,0:T(8,128)S(1)}, u32[]{:S(2)}, u32[]{:S(2)}) collective-permute-start(f32[128,128]{1,0:T(8,128)S(1)} %add.25), channel_id=1, source_target_pairs={{0,4},{1,13},{2,6},{3,15},{4,0},{5,9},{6,2},{7,11},{8,12},{9,5},{1... | collective-permute-start | bytes 196616 | tf_op jit(solution)/shard_map/ppermute | solution.py:366
  43.8 7.9 %collective-permute-start.11 = (f32[128,128]{1,0:T(8,128)S(1)}, f32[128,128]{1,0:T(8,128)S(1)}, u32[]{:S(2)}, u32[]{:S(2)}) collective-permute-start(f32[128,128]{1,0:T(8,128)S(1)} %add.26), channel_id=1, source_target_pairs={{0,12},{1,129},{2,14},{3,131},{4,8},{5,133},{6,10},{7,135},{8,4},{... | collective-permute-start | bytes 196616 | tf_op jit(solution)/shard_map/ppermute | solution.py:366
  51.7 4.4 %collective-permute-start.12 = (f32[128,128]{1,0:T(8,128)S(1)}, f32[128,128]{1,0:T(8,128)S(1)}, u32[]{:S(2)}, u32[]{:S(2)}) collective-permute-start(f32[128,128]{1,0:T(8,128)S(1)} %add.27), channel_id=1, source_target_pairs={{0,130},{1,131},{2,128},{3,129},{4,134},{5,135},{6,132},{7,133},{8... | collective-permute-start | bytes 196616 | tf_op jit(solution)/shard_map/ppermute | solution.py:366
  56.1 4.1 %collective-permute-start.15 = (f32[128,128]{1,0:T(8,128)S(1)}, f32[128,128]{1,0:T(8,128)S(1)}, u32[]{:S(2)}, u32[]{:S(2)}) collective-permute-start(f32[128,128]{1,0:T(8,128)S(1)} %add.28), channel_id=1, source_target_pairs={{0,16},{1,33},{2,18},{3,35},{4,20},{5,37},{6,22},{7,39},{8,24},{9,... | collective-permute-start | bytes 196616 | tf_op jit(solution)/shard_map/ppermute | solution.py:366
  60.2 20.1 %collective-permute-start.18 = (f32[2,256,128]{2,1,0:T(8,128)S(1)}, f32[2,256,128]{2,1,0:T(8,128)S(1)}, u32[]{:S(2)}, u32[]{:S(2)}) collective-permute-start(f32[2,256,128]{2,1,0:T(8,128)S(1)} %get-tuple-element.63), channel_id=1, source_target_pairs={{0,16},{1,2},{2,1},{3,4},{4,3},{5,6},{6,5},{7,8},{8,7},{9,10},{10,... | collective-permute-start | bytes 786440 | tf_op jit(solution)/shard_map/ppermute | solution.py:360
  70.3 10.1 %collective-permute-start.19 = (f32[2,256,128]{2,1,0:T(8,128)S(1)}, f32[2,256,128]{2,1,0:T(8,128)S(1)}, u32[]{:S(2)}, u32[]{:S(2)}) collective-permute-start(f32[2,256,128]{2,1,0:T(8,128)S(1)} %get-tuple-element.64), channel_id=1, source_target_pairs={{0,1},{1,0},{2,3},{3,2},{4,5},{5,4},{6,7},{7,6},{8,9},{9,8},{10,11... | collective-permute-start | bytes 786440 | tf_op jit(solution)/shard_map/ppermute | solution.py:360
  70.5 6.6 %collective-permute-start.16 = (f32[128,128]{1,0:T(8,128)S(1)}, f32[128,128]{1,0:T(8,128)S(1)}, u32[]{:S(2)}, u32[]{:S(2)}) collective-permute-start(f32[128,128]{1,0:T(8,128)S(1)} %add.29), channel_id=1, source_target_pairs={{0,32},{1,97},{2,34},{3,99},{4,36},{5,101},{6,38},{7,103},{8,40},{... | collective-permute-start | bytes 196616 | tf_op jit(solution)/shard_map/ppermute | solution.py:366
  77.1 3.2 %collective-permute-start.17 = (f32[128,128]{1,0:T(8,128)S(1)}, f32[128,128]{1,0:T(8,128)S(1)}, u32[]{:S(2)}, u32[]{:S(2)}) collective-permute-start(f32[128,128]{1,0:T(8,128)S(1)} %add.30), channel_id=1, source_target_pairs={{0,96},{1,17},{2,98},{3,19},{4,100},{5,21},{6,102},{7,23},{8,104},... | collective-permute-start | bytes 196616 | tf_op jit(solution)/shard_map/ppermute | solution.py:366
  80.4 3.6 %collective-permute-start.20 = (f32[128,128]{1,0:T(8,128)S(1)}, f32[128,128]{1,0:T(8,128)S(1)}, u32[]{:S(2)}, u32[]{:S(2)}) collective-permute-start(f32[128,128]{1,0:T(8,128)S(1)} %add.31.mine_ref), channel_id=1, source_target_pairs={{0,1},{1,0},{2,3},{3,2},{4,5},{5,4},{6,7},{7,6},{8,9},{9,8},{10,11... | collective-permute-start | bytes 196616 | tf_op jit(solution)/shard_map/ppermute | solution.py:366

commit v14 on v13

--- a/solution.py
+++ b/solution.py
@@ -96,7 +96,7 @@
     colb_ref[...] = pick(1, left, right)
 
 
-def rows_kernel(obj_ref, colb_ref, cola_ref, rowb_ref, rowa_ref, *, piece):
+def rows_kernel(obj_ref, colb_ref, cola_ref, rowa_ref, rowb_ref, *, piece):
     half = LANES // 2
     low, high = slice(0, half), slice(obj_ref.shape[2] - half, obj_ref.shape[2])
     for part in range(2):
@@ -112,7 +112,7 @@
         rowb_ref[place] = pick(0, top, bottom)
 
 
-def grow(ext, piece_ref, colb_ref, cola_ref, rowb_ref, rowa_ref):
+def grow(ext, piece_ref, colb_ref, cola_ref, rowa_ref, rowb_ref):
     half = LANES // 2
     tile = piece_ref.shape[1]
     sides = beside(1, cola_ref[...], colb_ref[...])
@@ -164,11 +164,11 @@
 
 
 def first_kernel(
-    row_ref, col_ref, obj_ref, colb_ref, cola_ref, rowb_ref, rowa_ref, probe_ref, tabs_ref,
+    row_ref, col_ref, obj_ref, colb_ref, cola_ref, rowa_ref, rowb_ref, probe_ref, tabs_ref,
     win_ref, mid_ref, ext, *, group,
 ):
     width = probe_ref.shape[1]
-    grow(ext, obj_ref.at[0], colb_ref, cola_ref, rowb_ref, rowa_ref)
+    grow(ext, obj_ref.at[0], colb_ref, cola_ref, rowa_ref, rowb_ref)
 
     def some(index, _):
         slots = [group * index + place for place in range(group)]
@@ -184,13 +184,13 @@
 
 
 def second_kernel(
-    row_ref, col_ref, live_ref, obj_ref, colb_ref, cola_ref, rowb_ref, rowa_ref,
+    row_ref, col_ref, live_ref, obj_ref, colb_ref, cola_ref, rowa_ref, rowb_ref,
     win_ref, mid_ref, measured_ref, tabs_ref,
     grad_ref, down_ref, keep_ref, send_ref,
     ext, sum_ref, *, group,
 ):
     width = win_ref.shape[2]
-    grow(ext, obj_ref.at[1], colb_ref, cola_ref, rowb_ref, rowa_ref)
+    grow(ext, obj_ref.at[1], colb_ref, cola_ref, rowa_ref, rowb_ref)
     sum_ref[...] = jnp.zeros_like(sum_ref)
 
     def some(index, _):
@@ -232,7 +232,7 @@
 
 def place_kernel(
     row_ref, col_ref, obj_ref, probe_ref, down_ref, second_ref,
-    new_ref, rowb_ref, rowa_ref, left_ref, right_ref,
+    new_ref, rowa_ref, rowb_ref, left_ref, right_ref,
     grad,
 ):
     width = probe_ref.shape[1]
@@ -280,7 +280,7 @@
             ref[piece] = strip[half : half + tile]
 
 
-def fold_kernel(left_ref, right_ref, rowb_ref, rowa_ref, colb_ref, cola_ref):
+def fold_kernel(left_ref, right_ref, rowa_ref, rowb_ref, colb_ref, cola_ref):
     half = LANES // 2
     tile = left_ref.shape[1]
     for piece in range(2):
@@ -300,7 +300,7 @@
 
 
 def finish_kernel(
-    part_ref, rowb_ref, rowa_ref, colb_ref, cola_ref, new_ref,
+    part_ref, rowa_ref, rowb_ref, colb_ref, cola_ref, new_ref,
 ):
     tile = part_ref.shape[2]
     half = LANES // 2
@@ -347,7 +347,7 @@
 def meet(strips, axis):
     sizes = (lax.axis_size("row"), lax.axis_size("col"))
     got = []
-    for odd, strip in zip((1, 0), strips):
+    for odd, strip in zip((axis, 1 - axis), strips):
         pairs = []
         for spot in np.ndindex(*sizes):
             other = list(spot)

time: 84.9 us -> 78.2 us (0.921)
  starting transfers between devices: 45.3 us -> 37.7 us
    ppermute x12, starting transfers between devices: 29.2 us -> 17.6 us  [meet(): got.append(lax.ppermute(strip, BOTH, pairs))]
    ppermute x9, starting transfers between devices: 16.1 us -> 20.1 us  [swap(): lax.ppermute(value, BOTH, [(i, i ^ masks[i % 2]) for i in range(count)])]
    ppermute x12, waiting for transfers between devices: 1.71 us -> 4.3 us  [meet(): got.append(lax.ppermute(strip, BOTH, pairs))]
    ppermute x9, waiting for transfers between devices: 21.2 us -> 19.3 us  [swap(): lax.ppermute(value, BOTH, [(i, i ^ masks[i % 2]) for i in range(count)])]
  transfers between devices with their start and end apart: 21 -> 21, of which waited for: 9 -> 10; matrix products, arithmetic and copies ran while one was open for 0% -> 0% of each run, Pallas kernels for 8% -> 9%
where the time goes in v14:
time: 78.2 us; the launch traced here: 77.7 us
  starting transfers between devices  37.7 us (48%)
  waiting for transfers between devices  23.6 us (30%)
  Pallas kernels  14.8 us (19%)
  between operations  1.49 us (2%)
    ppermute x9, starting transfers between devices, swap(): lax.ppermute(value, BOTH, [(i, i ^ masks[i % 2]) for i in range(count)])  20.1 us
    ppermute x9, waiting for transfers between devices, swap(): lax.ppermute(value, BOTH, [(i, i ^ masks[i % 2]) for i in range(count)])  19.3 us
    ppermute x12, starting transfers between devices, meet(): got.append(lax.ppermute(strip, BOTH, pairs))  17.6 us
    pallas_call x8, Pallas kernels, call(): pl.pallas_call(kernel, out_shape=tuple(out_shape), in_specs=smem(len(scal...  12.4 us
    ppermute x12, waiting for transfers between devices, meet(): got.append(lax.ppermute(strip, BOTH, pairs))  4.3 us
    pallas_call x2, Pallas kernels, on_device(): pl.pallas_call(functools.partial(pack_kernel, piece=piece), out_shape=tup...  2.46 us
  transfers between devices with their start and end apart: 21, of which 10 were waited for; matrix products, arithmetic and copies ran while one was open for 0% of the time, Pallas kernels for 9%

profile of v14, /device:TPU:1, one launch (start us, length us, event | category | flops | bytes accessed | tf_op | source)
XLA Modules:
  0.0 77.7 jit_solution(644945778720628340)
XLA Ops:
  0.6 0.0 copy-start
  0.6 1.3 %shard_map.88 = (f32[256,128]{1,0:T(8,128)S(1)}, f32[256,128]{1,0:T(8,128)S(1)}) custom-call(f32[2,2,256,256]{3,2,1,0:T(8,128)} %obj_ref.13), custom_call_target="tpu_custom_call" | custom-call | tf_op jit(solution)/shard_map/pallas_call | solution.py:387
  1.9 4.4 %collective-permute-start.4 = (f32[256,128]{1,0:T(8,128)S(1)}, f32[256,128]{1,0:T(8,128)S(1)}, u32[]{:S(2)}, u32[]{:S(2)}) collective-permute-start(f32[256,128]{1,0:T(8,128)S(1)} %get-tuple-element.39), channel_id=1, source_target_pairs={{0,16},{1,2},{2,1},{3,4},{4,3},{5,6},{6,5},{7,8},{8,7},{9,10},{10,... | collective-permute-start | bytes 393224 | tf_op jit(solution)/shard_map/ppermute | solution.py:360
  6.3 0.0 collective-permute-start.5
  6.3 1.2 %shard_map.86 = (f32[256,128]{1,0:T(8,128)S(1)}, f32[256,128]{1,0:T(8,128)S(1)}) custom-call(f32[2,2,256,256]{3,2,1,0:T(8,128)} %obj_ref.13), custom_call_target="tpu_custom_call" | custom-call | tf_op jit(solution)/shard_map/pallas_call | solution.py:387
  7.5 1.5 %collective-permute-start = (f32[256,128]{1,0:T(8,128)S(1)}, f32[256,128]{1,0:T(8,128)S(1)}, u32[]{:S(2)}, u32[]{:S(2)}) collective-permute-start(f32[256,128]{1,0:T(8,128)S(1)} %get-tuple-element.35), channel_id=1, source_target_pairs={{0,16},{1,2},{2,1},{3,4},{4,3},{5,6},{6,5},{7,8},{8,7},{9,10},{10,... | collective-permute-start | bytes 393224 | tf_op jit(solution)/shard_map/ppermute | solution.py:360
  9.0 0.0 copy-start.1
  9.0 1.0 %collective-permute-start.1 = (f32[256,128]{1,0:T(8,128)S(1)}, f32[256,128]{1,0:T(8,128)S(1)}, u32[]{:S(2)}, u32[]{:S(2)}) collective-permute-start(f32[256,128]{1,0:T(8,128)S(1)} %get-tuple-element.36), channel_id=1, source_target_pairs={{0,1},{1,0},{2,3},{3,2},{4,5},{5,4},{6,7},{7,6},{8,9},{9,8},{10,11... | collective-permute-start | bytes 393224 | tf_op jit(solution)/shard_map/ppermute | solution.py:360
  10.0 0.0 collective-permute-done.4.colb_ref
  10.0 0.0 collective-permute-done.5.cola_ref
  10.0 0.0 copy-done
  10.1 1.3 %collective-permute-start.6 = (f32[6,64,128]{2,1,0:T(8,128)S(1)}, f32[6,64,128]{2,1,0:T(8,128)S(1)}, u32[]{:S(2)}, u32[]{:S(2)}) collective-permute-start(f32[6,64,128]{2,1,0:T(8,128)S(1)} %get-tuple-element.41), channel_id=1, source_target_pairs={{0,16},{1,17},{2,18},{3,19},{4,20},{5,21},{6,22},{7,23},{8,24},{9,... | collective-permute-start | bytes 589832 | tf_op jit(solution)/shard_map/ppermute | solution.py:360
  11.4 0.0 copy-start.2
  11.4 0.1 collective-permute-start.7
  11.6 1.9 %collective-permute-done.colb_ref = f32[256,128]{1,0:T(8,128)S(1)} collective-permute-done((f32[256,128]{1,0:T(8,128)S(1)}, f32[256,128]{1,0:T(8,128)S(1)}, u32[]{:S(2)}, u32[]{:S(2)}) %collective-permute-start) | collective-permute-done | bytes 131104 | tf_op jit(solution)/shard_map/ppermute | solution.py:360
  13.5 0.0 collective-permute-done.1.cola_ref
  13.5 1.7 %collective-permute-start.2 = (f32[6,64,128]{2,1,0:T(8,128)S(1)}, f32[6,64,128]{2,1,0:T(8,128)S(1)}, u32[]{:S(2)}, u32[]{:S(2)}) collective-permute-start(f32[6,64,128]{2,1,0:T(8,128)S(1)} %get-tuple-element.37), channel_id=1, source_target_pairs={{0,16},{1,17},{2,18},{3,19},{4,20},{5,21},{6,22},{7,23},{8,24},{9,... | collective-permute-start | bytes 589832 | tf_op jit(solution)/shard_map/ppermute | solution.py:360
  15.3 0.0 copy-start.4
  15.3 0.0 copy-start.5
  15.3 0.3 collective-permute-start.3
  16.2 0.0 copy-start.3
  16.2 0.3 collective-permute-done.6.rowa_ref
  16.5 0.0 collective-permute-done.7.rowb_ref
  16.5 0.0 copy-done.1
  16.5 0.0 copy-done.2
  16.5 0.0 copy-done.4
  16.5 0.0 copy-done.5
  16.5 2.2 %shard_map.90 = (f32[8,2,128,128]{3,2,1,0:T(8,128)S(1)}, f32[8,2,128,128]{3,2,1,0:T(8,128)S(1)}) custom-call(s32[1,8]{1,0:T(1,128)S(1)} %copy-done.4, s32[1,8]{1,0:T(1,128)S(1)} %copy-done.5, f32[2,2,256,256]{3,2,1,0:T(8,128)S(1)} %copy-done, f32[256,128]{1,0:T(8,128)S(1)} %collective-permute-done.4.colb_ref, ...), custom_call_target="tpu_custom_call" | custom-call | tf_op jit(solution)/shard_map/pallas_call | solution.py:370
  18.7 2.0 %collective-permute-done.2.rowa_ref = f32[6,64,128]{2,1,0:T(8,128)S(1)} collective-permute-done((f32[6,64,128]{2,1,0:T(8,128)S(1)}, f32[6,64,128]{2,1,0:T(8,128)S(1)}, u32[]{:S(2)}, u32[]{:S(2)}) %collective-permute-start.2) | collective-permute-done | bytes 196640 | tf_op jit(solution)/shard_map/ppermute | solution.py:360
  20.8 0.0 collective-permute-done.3.rowb_ref
  20.8 0.0 copy-done.3
  20.8 5.8 %shard_map.91 = (f32[8,2,128,128]{3,2,1,0:T(8,128)S(1)}, f32[8,2,128,128]{3,2,1,0:T(8,128)S(1)}, f32[128,128]{1,0:T(8,128)S(1)}, f32[128,128]{1,0:T(8,128)S(1)}) custom-call(s32[1,8]{1,0:T(1,128)S(1)} %copy-done.4, s32[1,8]{1,0:T(1,128)S(1)} %copy-done.5, s32[1,1]{1,0:T(1,128)S(6)} %copy.9.live_ref, f32[2,2,256,256]{3,2,1,0:T(8,128)S(1)} %copy-done, ...), custom_call_target="tpu_custom_call" | custom-call | tf_op jit(solution)/shard_map/pallas_call | solution.py:370
  26.6 1.0 %collective-permute-start.8 = (f32[128,128]{1,0:T(8,128)S(1)}, f32[128,128]{1,0:T(8,128)S(1)}, u32[]{:S(2)}, u32[]{:S(2)}) collective-permute-start(f32[128,128]{1,0:T(8,128)S(1)} %get-tuple-element.49), channel_id=1, source_target_pairs={{0,1},{1,0},{2,3},{3,2},{4,5},{5,4},{6,7},{7,6},{8,9},{9,8},{10,11... | collective-permute-start | bytes 196616 | tf_op jit(solution)/shard_map/ppermute | solution.py:366
  27.6 0.9 %collective-permute-done.8 = f32[128,128]{1,0:T(8,128)S(1)} collective-permute-done((f32[128,128]{1,0:T(8,128)S(1)}, f32[128,128]{1,0:T(8,128)S(1)}, u32[]{:S(2)}, u32[]{:S(2)}) %collective-permute-start.8) | collective-permute-done | bytes 65568 | tf_op jit(solution)/shard_map/ppermute | solution.py:366
  28.6 2.3 %collective-permute-start.9 = (f32[128,128]{1,0:T(8,128)S(1)}, f32[128,128]{1,0:T(8,128)S(1)}, u32[]{:S(2)}, u32[]{:S(2)}) collective-permute-start(f32[128,128]{1,0:T(8,128)S(1)} %add.24), channel_id=1, source_target_pairs={{0,128},{1,5},{2,130},{3,7},{4,132},{5,1},{6,134},{7,3},{8,136},{9... | collective-permute-start | bytes 196616 | tf_op jit(solution)/shard_map/ppermute | solution.py:366
  30.9 2.3 %shard_map.92 = (f32[2,2,256,256]{3,2,1,0:T(8,128)S(1)}, f32[2,6,64,128]{3,2,1,0:T(8,128)S(1)}, f32[2,6,64,128]{3,2,1,0:T(8,128)S(1)}, f32[2,256,128]{2,1,0:T(8,128)S(1)}, f32[2,256,128]{2,1,0:T(8,128)S(1)}) custom-call(s32[1,8]{1,0:T(1,128)S(1)} %copy-done.4, s32[1,8]{1,0:T(1,128)S(1)} %copy-done.5, f32[2,2,256,256]{3,2,1,0:T(8,128)S(1)} %copy-done, ...), custom_call_target="tpu_custom_call" | custom-call | tf_op jit(solution)/shard_map/pallas_call | solution.py:370
  33.2 0.0 collective-permute-done.9
  33.2 3.4 %collective-permute-start.13 = (f32[2,6,64,128]{3,2,1,0:T(8,128)S(1)}, f32[2,6,64,128]{3,2,1,0:T(8,128)S(1)}, u32[]{:S(2)}, u32[]{:S(2)}) collective-permute-start(f32[2,6,64,128]{3,2,1,0:T(8,128)S(1)} %get-tuple-element.53), channel_id=1, source_target_pairs={{0,16},{1,17},{2,18},{3,19},{4,20},{5,21},{6,22},{7,23},{8,24},{9,... | collective-permute-start | bytes 1179656 | tf_op jit(solution)/shard_map/ppermute | solution.py:360
  36.6 1.0 %collective-permute-start.14 = (f32[2,6,64,128]{3,2,1,0:T(8,128)S(1)}, f32[2,6,64,128]{3,2,1,0:T(8,128)S(1)}, u32[]{:S(2)}, u32[]{:S(2)}) collective-permute-start(f32[2,6,64,128]{3,2,1,0:T(8,128)S(1)} %get-tuple-element.54), channel_id=1, source_target_pairs={{0,1},{1,0},{2,3},{3,2},{4,5},{5,4},{6,7},{7,6},{8,9},{9,8},{10,11... | collective-permute-start | bytes 1179656 | tf_op jit(solution)/shard_map/ppermute | solution.py:360
  37.6 3.6 %collective-permute-start.10 = (f32[128,128]{1,0:T(8,128)S(1)}, f32[128,128]{1,0:T(8,128)S(1)}, u32[]{:S(2)}, u32[]{:S(2)}) collective-permute-start(f32[128,128]{1,0:T(8,128)S(1)} %add.25), channel_id=1, source_target_pairs={{0,4},{1,13},{2,6},{3,15},{4,0},{5,9},{6,2},{7,11},{8,12},{9,5},{1... | collective-permute-start | bytes 196616 | tf_op jit(solution)/shard_map/ppermute | solution.py:366
  41.2 1.7 %collective-permute-done.10 = f32[128,128]{1,0:T(8,128)S(1)} collective-permute-done((f32[128,128]{1,0:T(8,128)S(1)}, f32[128,128]{1,0:T(8,128)S(1)}, u32[]{:S(2)}, u32[]{:S(2)}) %collective-permute-start.10) | collective-permute-done | bytes 65568 | tf_op jit(solution)/shard_map/ppermute | solution.py:366
  42.9 4.7 %collective-permute-start.11 = (f32[128,128]{1,0:T(8,128)S(1)}, f32[128,128]{1,0:T(8,128)S(1)}, u32[]{:S(2)}, u32[]{:S(2)}) collective-permute-start(f32[128,128]{1,0:T(8,128)S(1)} %add.26), channel_id=1, source_target_pairs={{0,12},{1,129},{2,14},{3,131},{4,8},{5,133},{6,10},{7,135},{8,4},{... | collective-permute-start | bytes 196616 | tf_op jit(solution)/shard_map/ppermute | solution.py:366
  47.6 3.5 %collective-permute-done.11 = f32[128,128]{1,0:T(8,128)S(1)} collective-permute-done((f32[128,128]{1,0:T(8,128)S(1)}, f32[128,128]{1,0:T(8,128)S(1)}, u32[]{:S(2)}, u32[]{:S(2)}) %collective-permute-start.11) | collective-permute-done | bytes 65568 | tf_op jit(solution)/shard_map/ppermute | solution.py:366
  51.0 3.0 %collective-permute-start.12 = (f32[128,128]{1,0:T(8,128)S(1)}, f32[128,128]{1,0:T(8,128)S(1)}, u32[]{:S(2)}, u32[]{:S(2)}) collective-permute-start(f32[128,128]{1,0:T(8,128)S(1)} %add.27), channel_id=1, source_target_pairs={{0,130},{1,131},{2,128},{3,129},{4,134},{5,135},{6,132},{7,133},{8... | collective-permute-start | bytes 196616 | tf_op jit(solution)/shard_map/ppermute | solution.py:366
  54.1 1.7 %collective-permute-done.12 = f32[128,128]{1,0:T(8,128)S(1)} collective-permute-done((f32[128,128]{1,0:T(8,128)S(1)}, f32[128,128]{1,0:T(8,128)S(1)}, u32[]{:S(2)}, u32[]{:S(2)}) %collective-permute-start.12) | collective-permute-done | bytes 65568 | tf_op jit(solution)/shard_map/ppermute | solution.py:366
  55.7 0.0 collective-permute-done.13.rowa_ref
  55.7 0.0 collective-permute-done.14.rowb_ref
  55.8 0.1 collective-permute-start.15
  55.9 0.1 shard_map.93
  55.9 3.9 %collective-permute-done.15 = f32[128,128]{1,0:T(8,128)S(1)} collective-permute-done((f32[128,128]{1,0:T(8,128)S(1)}, f32[128,128]{1,0:T(8,128)S(1)}, u32[]{:S(2)}, u32[]{:S(2)}) %collective-permute-start.15) | collective-permute-done | bytes 65568 | tf_op jit(solution)/shard_map/ppermute | solution.py:366
  59.9 2.8 %collective-permute-start.18 = (f32[2,256,128]{2,1,0:T(8,128)S(1)}, f32[2,256,128]{2,1,0:T(8,128)S(1)}, u32[]{:S(2)}, u32[]{:S(2)}) collective-permute-start(f32[2,256,128]{2,1,0:T(8,128)S(1)} %get-tuple-element.63), channel_id=1, source_target_pairs={{0,16},{1,2},{2,1},{3,4},{4,3},{5,6},{6,5},{7,8},{8,7},{9,10},{10,... | collective-permute-start | bytes 786440 | tf_op jit(solution)/shard_map/ppermute | solution.py:360
  62.7 0.0 collective-permute-start.19
  62.7 2.1 %collective-permute-start.16 = (f32[128,128]{1,0:T(8,128)S(1)}, f32[128,128]{1,0:T(8,128)S(1)}, u32[]{:S(2)}, u32[]{:S(2)}) collective-permute-start(f32[128,128]{1,0:T(8,128)S(1)} %add.29), channel_id=1, source_target_pairs={{0,32},{1,97},{2,34},{3,99},{4,36},{5,101},{6,38},{7,103},{8,40},{... | collective-permute-start | bytes 196616 | tf_op jit(solution)/shard_map/ppermute | solution.py:366
  64.8 4.6 %collective-permute-done.16 = f32[128,128]{1,0:T(8,128)S(1)} collective-permute-done((f32[128,128]{1,0:T(8,128)S(1)}, f32[128,128]{1,0:T(8,128)S(1)}, u32[]{:S(2)}, u32[]{:S(2)}) %collective-permute-start.16) | collective-permute-done | bytes 65568 | tf_op jit(solution)/shard_map/ppermute | solution.py:366
  69.4 0.1 collective-permute-start.17
  69.5 3.1 %collective-permute-done.17 = f32[128,128]{1,0:T(8,128)S(1)} collective-permute-done((f32[128,128]{1,0:T(8,128)S(1)}, f32[128,128]{1,0:T(8,128)S(1)}, u32[]{:S(2)}, u32[]{:S(2)}) %collective-permute-start.17) | collective-permute-done | bytes 65568 | tf_op jit(solution)/shard_map/ppermute | solution.py:366
  72.6 0.0 collective-permute-done.18.colb_ref
  72.6 0.0 collective-permute-done.19.cola_ref
  72.7 3.2 %collective-permute-start.20 = (f32[128,128]{1,0:T(8,128)S(1)}, f32[128,128]{1,0:T(8,128)S(1)}, u32[]{:S(2)}, u32[]{:S(2)}) collective-permute-start(f32[128,128]{1,0:T(8,128)S(1)} %add.31.mine_ref), channel_id=1, source_target_pairs={{0,1},{1,0},{2,3},{3,2},{4,5},{5,4},{6,7},{7,6},{8,9},{9,8},{10,11... | collective-permute-start | bytes 196616 | tf_op jit(solution)/shard_map/ppermute | solution.py:366
  75.8 1.2 %shard_map.94 = f32[2,2,256,256]{3,2,1,0:T(8,128)} custom-call(f32[2,2,256,256]{3,2,1,0:T(8,128)S(1)} %get-tuple-element.47.part_ref, f32[2,6,64,128]{3,2,1,0:T(8,128)S(1)} %collective-permute-done.13.rowa_ref, f32[2,6,64,128]{3,2,1,0:T(8,128)S(1)} %collective-permute-done.14.rowb_ref, f32[2,256,128]{2,1,0:T(8,128)S(1)} %collective-permute-done.18.colb_ref, ...), custom_call_target="tpu_custom_call" | custom-call | tf_op jit(solution)/shard_map/pallas_call | solution.py:370
  77.0 0.0 collective-permute-done.20.other_ref
  77.1 0.7 shard_map.95
  (10 shorter events, 0.2 us)
Async XLA Ops:
  0.6 9.4 %copy-start = (f32[2,2,256,256]{3,2,1,0:T(8,128)S(1)}, f32[2,2,256,256]{3,2,1,0:T(8,128)}, u32[]{:S(2)}) copy-start(f32[2,2,256,256]{3,2,1,0:T(8,128)} %obj_ref.13) | copy-start | bytes 3145732
  1.9 8.1 %collective-permute-start.4 = (f32[256,128]{1,0:T(8,128)S(1)}, f32[256,128]{1,0:T(8,128)S(1)}, u32[]{:S(2)}, u32[]{:S(2)}) collective-permute-start(f32[256,128]{1,0:T(8,128)S(1)} %get-tuple-element.39), channel_id=1, source_target_pairs={{0,16},{1,2},{2,1},{3,4},{4,3},{5,6},{6,5},{7,8},{8,7},{9,10},{10,... | collective-permute-start | bytes 393224 | tf_op jit(solution)/shard_map/ppermute | solution.py:360
  6.3 3.7 %collective-permute-start.5 = (f32[256,128]{1,0:T(8,128)S(1)}, f32[256,128]{1,0:T(8,128)S(1)}, u32[]{:S(2)}, u32[]{:S(2)}) collective-permute-start(f32[256,128]{1,0:T(8,128)S(1)} %get-tuple-element.40), channel_id=1, source_target_pairs={{0,1},{1,0},{2,3},{3,2},{4,5},{5,4},{6,7},{7,6},{8,9},{9,8},{10,11... | collective-permute-start | bytes 393224 | tf_op jit(solution)/shard_map/ppermute | solution.py:360
  7.5 6.0 %collective-permute-start = (f32[256,128]{1,0:T(8,128)S(1)}, f32[256,128]{1,0:T(8,128)S(1)}, u32[]{:S(2)}, u32[]{:S(2)}) collective-permute-start(f32[256,128]{1,0:T(8,128)S(1)} %get-tuple-element.35), channel_id=1, source_target_pairs={{0,16},{1,2},{2,1},{3,4},{4,3},{5,6},{6,5},{7,8},{8,7},{9,10},{10,... | collective-permute-start | bytes 393224 | tf_op jit(solution)/shard_map/ppermute | solution.py:360
  9.0 7.5 %copy-start.1 = (bf16[4,2,256,256]{3,2,1,0:T(8,128)(2,1)S(1)}, bf16[4,2,256,256]{3,2,1,0:T(8,128)(2,1)}, u32[]{:S(2)}) copy-start(bf16[4,2,256,256]{3,2,1,0:T(8,128)(2,1)} %constant.2.clone.tabs_ref) | copy-start | bytes 3145732
  9.0 4.5 %collective-permute-start.1 = (f32[256,128]{1,0:T(8,128)S(1)}, f32[256,128]{1,0:T(8,128)S(1)}, u32[]{:S(2)}, u32[]{:S(2)}) collective-permute-start(f32[256,128]{1,0:T(8,128)S(1)} %get-tuple-element.36), channel_id=1, source_target_pairs={{0,1},{1,0},{2,3},{3,2},{4,5},{5,4},{6,7},{7,6},{8,9},{9,8},{10,11... | collective-permute-start | bytes 393224 | tf_op jit(solution)/shard_map/ppermute | solution.py:360
  10.1 6.4 %collective-permute-start.6 = (f32[6,64,128]{2,1,0:T(8,128)S(1)}, f32[6,64,128]{2,1,0:T(8,128)S(1)}, u32[]{:S(2)}, u32[]{:S(2)}) collective-permute-start(f32[6,64,128]{2,1,0:T(8,128)S(1)} %get-tuple-element.41), channel_id=1, source_target_pairs={{0,16},{1,17},{2,18},{3,19},{4,20},{5,21},{6,22},{7,23},{8,24},{9,... | collective-permute-start | bytes 589832 | tf_op jit(solution)/shard_map/ppermute | solution.py:360
  11.4 5.1 %copy-start.2 = (f32[2,128,128]{2,1,0:T(8,128)S(1)}, f32[2,128,128]{2,1,0:T(8,128)}, u32[]{:S(2)}) copy-start(f32[2,128,128]{2,1,0:T(8,128)} %probe_ref.5) | copy-start | bytes 393220
  11.4 5.1 %collective-permute-start.7 = (f32[6,64,128]{2,1,0:T(8,128)S(1)}, f32[6,64,128]{2,1,0:T(8,128)S(1)}, u32[]{:S(2)}, u32[]{:S(2)}) collective-permute-start(f32[6,64,128]{2,1,0:T(8,128)S(1)} %get-tuple-element.42), channel_id=1, source_target_pairs={{0,1},{1,0},{2,3},{3,2},{4,5},{5,4},{6,7},{7,6},{8,9},{9,8},{10,11... | collective-permute-start | bytes 589832 | tf_op jit(solution)/shard_map/ppermute | solution.py:360
  13.5 7.2 %collective-permute-start.2 = (f32[6,64,128]{2,1,0:T(8,128)S(1)}, f32[6,64,128]{2,1,0:T(8,128)S(1)}, u32[]{:S(2)}, u32[]{:S(2)}) collective-permute-start(f32[6,64,128]{2,1,0:T(8,128)S(1)} %get-tuple-element.37), channel_id=1, source_target_pairs={{0,16},{1,17},{2,18},{3,19},{4,20},{5,21},{6,22},{7,23},{8,24},{9,... | collective-permute-start | bytes 589832 | tf_op jit(solution)/shard_map/ppermute | solution.py:360
  15.3 1.2 %copy-start.4 = (s32[1,8]{1,0:T(1,128)S(1)}, s32[1,8]{1,0:T(1,128)}, u32[]{:S(2)}) copy-start(s32[1,8]{1,0:T(1,128)} %row_ref.5) | copy-start | bytes 100
  15.3 1.3 %copy-start.5 = (s32[1,8]{1,0:T(1,128)S(1)}, s32[1,8]{1,0:T(1,128)}, u32[]{:S(2)}) copy-start(s32[1,8]{1,0:T(1,128)} %col_ref.5) | copy-start | bytes 100
  15.3 5.5 %collective-permute-start.3 = (f32[6,64,128]{2,1,0:T(8,128)S(1)}, f32[6,64,128]{2,1,0:T(8,128)S(1)}, u32[]{:S(2)}, u32[]{:S(2)}) collective-permute-start(f32[6,64,128]{2,1,0:T(8,128)S(1)} %get-tuple-element.38), channel_id=1, source_target_pairs={{0,1},{1,0},{2,3},{3,2},{4,5},{5,4},{6,7},{7,6},{8,9},{9,8},{10,11... | collective-permute-start | bytes 589832 | tf_op jit(solution)/shard_map/ppermute | solution.py:360
  16.2 4.6 %copy-start.3 = (f32[1,8,128,128]{3,2,1,0:T(8,128)S(1)}, f32[1,8,128,128]{3,2,1,0:T(8,128)}, u32[]{:S(2)}) copy-start(f32[1,8,128,128]{3,2,1,0:T(8,128)} %param.9) | copy-start | bytes 1572868
  26.6 1.9 %collective-permute-start.8 = (f32[128,128]{1,0:T(8,128)S(1)}, f32[128,128]{1,0:T(8,128)S(1)}, u32[]{:S(2)}, u32[]{:S(2)}) collective-permute-start(f32[128,128]{1,0:T(8,128)S(1)} %get-tuple-element.49), channel_id=1, source_target_pairs={{0,1},{1,0},{2,3},{3,2},{4,5},{5,4},{6,7},{7,6},{8,9},{9,8},{10,11... | collective-permute-start | bytes 196616 | tf_op jit(solution)/shard_map/ppermute | solution.py:366
  28.6 4.6 %collective-permute-start.9 = (f32[128,128]{1,0:T(8,128)S(1)}, f32[128,128]{1,0:T(8,128)S(1)}, u32[]{:S(2)}, u32[]{:S(2)}) collective-permute-start(f32[128,128]{1,0:T(8,128)S(1)} %add.24), channel_id=1, source_target_pairs={{0,128},{1,5},{2,130},{3,7},{4,132},{5,1},{6,134},{7,3},{8,136},{9... | collective-permute-start | bytes 196616 | tf_op jit(solution)/shard_map/ppermute | solution.py:366
  33.2 22.5 %collective-permute-start.13 = (f32[2,6,64,128]{3,2,1,0:T(8,128)S(1)}, f32[2,6,64,128]{3,2,1,0:T(8,128)S(1)}, u32[]{:S(2)}, u32[]{:S(2)}) collective-permute-start(f32[2,6,64,128]{3,2,1,0:T(8,128)S(1)} %get-tuple-element.53), channel_id=1, source_target_pairs={{0,16},{1,17},{2,18},{3,19},{4,20},{5,21},{6,22},{7,23},{8,24},{9,... | collective-permute-start | bytes 1179656 | tf_op jit(solution)/shard_map/ppermute | solution.py:360
  36.6 19.2 %collective-permute-start.14 = (f32[2,6,64,128]{3,2,1,0:T(8,128)S(1)}, f32[2,6,64,128]{3,2,1,0:T(8,128)S(1)}, u32[]{:S(2)}, u32[]{:S(2)}) collective-permute-start(f32[2,6,64,128]{3,2,1,0:T(8,128)S(1)} %get-tuple-element.54), channel_id=1, source_target_pairs={{0,1},{1,0},{2,3},{3,2},{4,5},{5,4},{6,7},{7,6},{8,9},{9,8},{10,11... | collective-permute-start | bytes 1179656 | tf_op jit(solution)/shard_map/ppermute | solution.py:360
  37.6 5.3 %collective-permute-start.10 = (f32[128,128]{1,0:T(8,128)S(1)}, f32[128,128]{1,0:T(8,128)S(1)}, u32[]{:S(2)}, u32[]{:S(2)}) collective-permute-start(f32[128,128]{1,0:T(8,128)S(1)} %add.25), channel_id=1, source_target_pairs={{0,4},{1,13},{2,6},{3,15},{4,0},{5,9},{6,2},{7,11},{8,12},{9,5},{1... | collective-permute-start | bytes 196616 | tf_op jit(solution)/shard_map/ppermute | solution.py:366
  42.9 8.1 %collective-permute-start.11 = (f32[128,128]{1,0:T(8,128)S(1)}, f32[128,128]{1,0:T(8,128)S(1)}, u32[]{:S(2)}, u32[]{:S(2)}) collective-permute-start(f32[128,128]{1,0:T(8,128)S(1)} %add.26), channel_id=1, source_target_pairs={{0,12},{1,129},{2,14},{3,131},{4,8},{5,133},{6,10},{7,135},{8,4},{... | collective-permute-start | bytes 196616 | tf_op jit(solution)/shard_map/ppermute | solution.py:366
  51.0 4.7 %collective-permute-start.12 = (f32[128,128]{1,0:T(8,128)S(1)}, f32[128,128]{1,0:T(8,128)S(1)}, u32[]{:S(2)}, u32[]{:S(2)}) collective-permute-start(f32[128,128]{1,0:T(8,128)S(1)} %add.27), channel_id=1, source_target_pairs={{0,130},{1,131},{2,128},{3,129},{4,134},{5,135},{6,132},{7,133},{8... | collective-permute-start | bytes 196616 | tf_op jit(solution)/shard_map/ppermute | solution.py:366
  55.8 4.1 %collective-permute-start.15 = (f32[128,128]{1,0:T(8,128)S(1)}, f32[128,128]{1,0:T(8,128)S(1)}, u32[]{:S(2)}, u32[]{:S(2)}) collective-permute-start(f32[128,128]{1,0:T(8,128)S(1)} %add.28), channel_id=1, source_target_pairs={{0,16},{1,33},{2,18},{3,35},{4,20},{5,37},{6,22},{7,39},{8,24},{9,... | collective-permute-start | bytes 196616 | tf_op jit(solution)/shard_map/ppermute | solution.py:366
  59.9 12.8 %collective-permute-start.18 = (f32[2,256,128]{2,1,0:T(8,128)S(1)}, f32[2,256,128]{2,1,0:T(8,128)S(1)}, u32[]{:S(2)}, u32[]{:S(2)}) collective-permute-start(f32[2,256,128]{2,1,0:T(8,128)S(1)} %get-tuple-element.63), channel_id=1, source_target_pairs={{0,16},{1,2},{2,1},{3,4},{4,3},{5,6},{6,5},{7,8},{8,7},{9,10},{10,... | collective-permute-start | bytes 786440 | tf_op jit(solution)/shard_map/ppermute | solution.py:360
  62.7 9.9 %collective-permute-start.19 = (f32[2,256,128]{2,1,0:T(8,128)S(1)}, f32[2,256,128]{2,1,0:T(8,128)S(1)}, u32[]{:S(2)}, u32[]{:S(2)}) collective-permute-start(f32[2,256,128]{2,1,0:T(8,128)S(1)} %get-tuple-element.64), channel_id=1, source_target_pairs={{0,1},{1,0},{2,3},{3,2},{4,5},{5,4},{6,7},{7,6},{8,9},{9,8},{10,11... | collective-permute-start | bytes 786440 | tf_op jit(solution)/shard_map/ppermute | solution.py:360
  62.7 6.7 %collective-permute-start.16 = (f32[128,128]{1,0:T(8,128)S(1)}, f32[128,128]{1,0:T(8,128)S(1)}, u32[]{:S(2)}, u32[]{:S(2)}) collective-permute-start(f32[128,128]{1,0:T(8,128)S(1)} %add.29), channel_id=1, source_target_pairs={{0,32},{1,97},{2,34},{3,99},{4,36},{5,101},{6,38},{7,103},{8,40},{... | collective-permute-start | bytes 196616 | tf_op jit(solution)/shard_map/ppermute | solution.py:366
  69.4 3.2 %collective-permute-start.17 = (f32[128,128]{1,0:T(8,128)S(1)}, f32[128,128]{1,0:T(8,128)S(1)}, u32[]{:S(2)}, u32[]{:S(2)}) collective-permute-start(f32[128,128]{1,0:T(8,128)S(1)} %add.30), channel_id=1, source_target_pairs={{0,96},{1,17},{2,98},{3,19},{4,100},{5,21},{6,102},{7,23},{8,104},... | collective-permute-start | bytes 196616 | tf_op jit(solution)/shard_map/ppermute | solution.py:366
  72.7 4.4 %collective-permute-start.20 = (f32[128,128]{1,0:T(8,128)S(1)}, f32[128,128]{1,0:T(8,128)S(1)}, u32[]{:S(2)}, u32[]{:S(2)}) collective-permute-start(f32[128,128]{1,0:T(8,128)S(1)} %add.31.mine_ref), channel_id=1, source_target_pairs={{0,1},{1,0},{2,3},{3,2},{4,5},{5,4},{6,7},{7,6},{8,9},{9,8},{10,11... | collective-permute-start | bytes 196616 | tf_op jit(solution)/shard_map/ppermute | solution.py:366

commit v15 on v14

--- a/solution.py
+++ b/solution.py
@@ -16,7 +16,7 @@
 LANES = 128
 BOTH = ("row", "col")
 GRANT = 16 * 1024 * 1024
-MASKS = ((128, 4), (4, 12), (12, 128), (130, 130), (16, 32), (32, 96), (96, 16))
+MASKS = ((16, 16), (4, 12), (12, 4), (128, 130), (130, 128), (32, 96), (96, 32))
 
 
 def split_table(table):

time: 78.2 us -> 78.8 us (level)
  starting transfers between devices: 37.7 us -> 39.4 us
  waiting for transfers between devices: 23.6 us -> 22.8 us
    ppermute x12, starting transfers between devices: 17.6 us -> 19.3 us  [meet(): got.append(lax.ppermute(strip, BOTH, pairs))]
where the time goes in v15:
time: 78.8 us; the launch traced here: 78.6 us
  starting transfers between devices  39.4 us (50%)
  waiting for transfers between devices  22.8 us (29%)
  Pallas kernels  14.8 us (19%)
  between operations  1.48 us (2%)
    ppermute x9, starting transfers between devices, swap(): lax.ppermute(value, BOTH, [(i, i ^ masks[i % 2]) for i in range(count)])  20.1 us
    ppermute x12, starting transfers between devices, meet(): got.append(lax.ppermute(strip, BOTH, pairs))  19.3 us
    ppermute x9, waiting for transfers between devices, swap(): lax.ppermute(value, BOTH, [(i, i ^ masks[i % 2]) for i in range(count)])  18.5 us
    pallas_call x8, Pallas kernels, call(): pl.pallas_call(kernel, out_shape=tuple(out_shape), in_specs=smem(len(scal...  12.4 us
    ppermute x12, waiting for transfers between devices, meet(): got.append(lax.ppermute(strip, BOTH, pairs))  4.29 us
    pallas_call x2, Pallas kernels, on_device(): pl.pallas_call(functools.partial(pack_kernel, piece=piece), out_shape=tup...  2.46 us
  transfers between devices with their start and end apart: 21, of which 10 were waited for; matrix products, arithmetic and copies ran while one was open for 0% of the time, Pallas kernels for 9%

profile of v15, /device:TPU:1, one launch (start us, length us, event | category | flops | bytes accessed | tf_op | source)
XLA Modules:
  0.0 78.6 jit_solution(10453991439412632374)
XLA Ops:
  0.6 0.0 copy-start
  0.6 1.3 %shard_map.88 = (f32[256,128]{1,0:T(8,128)S(1)}, f32[256,128]{1,0:T(8,128)S(1)}) custom-call(f32[2,2,256,256]{3,2,1,0:T(8,128)} %obj_ref.13), custom_call_target="tpu_custom_call" | custom-call | tf_op jit(solution)/shard_map/pallas_call | solution.py:387
  1.9 4.4 %collective-permute-start.4 = (f32[256,128]{1,0:T(8,128)S(1)}, f32[256,128]{1,0:T(8,128)S(1)}, u32[]{:S(2)}, u32[]{:S(2)}) collective-permute-start(f32[256,128]{1,0:T(8,128)S(1)} %get-tuple-element.39), channel_id=1, source_target_pairs={{0,16},{1,2},{2,1},{3,4},{4,3},{5,6},{6,5},{7,8},{8,7},{9,10},{10,... | collective-permute-start | bytes 393224 | tf_op jit(solution)/shard_map/ppermute | solution.py:360
  6.3 0.0 collective-permute-start.5
  6.3 1.2 %shard_map.86 = (f32[256,128]{1,0:T(8,128)S(1)}, f32[256,128]{1,0:T(8,128)S(1)}) custom-call(f32[2,2,256,256]{3,2,1,0:T(8,128)} %obj_ref.13), custom_call_target="tpu_custom_call" | custom-call | tf_op jit(solution)/shard_map/pallas_call | solution.py:387
  7.5 1.5 %collective-permute-start = (f32[256,128]{1,0:T(8,128)S(1)}, f32[256,128]{1,0:T(8,128)S(1)}, u32[]{:S(2)}, u32[]{:S(2)}) collective-permute-start(f32[256,128]{1,0:T(8,128)S(1)} %get-tuple-element.35), channel_id=1, source_target_pairs={{0,16},{1,2},{2,1},{3,4},{4,3},{5,6},{6,5},{7,8},{8,7},{9,10},{10,... | collective-permute-start | bytes 393224 | tf_op jit(solution)/shard_map/ppermute | solution.py:360
  9.0 0.0 copy-start.1
  9.0 1.0 %collective-permute-start.1 = (f32[256,128]{1,0:T(8,128)S(1)}, f32[256,128]{1,0:T(8,128)S(1)}, u32[]{:S(2)}, u32[]{:S(2)}) collective-permute-start(f32[256,128]{1,0:T(8,128)S(1)} %get-tuple-element.36), channel_id=1, source_target_pairs={{0,1},{1,0},{2,3},{3,2},{4,5},{5,4},{6,7},{7,6},{8,9},{9,8},{10,11... | collective-permute-start | bytes 393224 | tf_op jit(solution)/shard_map/ppermute | solution.py:360
  10.0 0.0 collective-permute-done.4.colb_ref
  10.0 0.0 collective-permute-done.5.cola_ref
  10.0 0.0 copy-done
  10.1 1.3 %collective-permute-start.6 = (f32[6,64,128]{2,1,0:T(8,128)S(1)}, f32[6,64,128]{2,1,0:T(8,128)S(1)}, u32[]{:S(2)}, u32[]{:S(2)}) collective-permute-start(f32[6,64,128]{2,1,0:T(8,128)S(1)} %get-tuple-element.41), channel_id=1, source_target_pairs={{0,16},{1,17},{2,18},{3,19},{4,20},{5,21},{6,22},{7,23},{8,24},{9,... | collective-permute-start | bytes 589832 | tf_op jit(solution)/shard_map/ppermute | solution.py:360
  11.4 0.0 copy-start.2
  11.4 0.1 collective-permute-start.7
  11.6 1.9 %collective-permute-done.colb_ref = f32[256,128]{1,0:T(8,128)S(1)} collective-permute-done((f32[256,128]{1,0:T(8,128)S(1)}, f32[256,128]{1,0:T(8,128)S(1)}, u32[]{:S(2)}, u32[]{:S(2)}) %collective-permute-start) | collective-permute-done | bytes 131104 | tf_op jit(solution)/shard_map/ppermute | solution.py:360
  13.5 0.0 collective-permute-done.1.cola_ref
  13.5 1.7 %collective-permute-start.2 = (f32[6,64,128]{2,1,0:T(8,128)S(1)}, f32[6,64,128]{2,1,0:T(8,128)S(1)}, u32[]{:S(2)}, u32[]{:S(2)}) collective-permute-start(f32[6,64,128]{2,1,0:T(8,128)S(1)} %get-tuple-element.37), channel_id=1, source_target_pairs={{0,16},{1,17},{2,18},{3,19},{4,20},{5,21},{6,22},{7,23},{8,24},{9,... | collective-permute-start | bytes 589832 | tf_op jit(solution)/shard_map/ppermute | solution.py:360
  15.3 0.0 copy-start.4
  15.3 0.0 copy-start.5
  15.3 0.3 collective-permute-start.3
  16.2 0.0 copy-start.3
  16.2 0.3 collective-permute-done.6.rowa_ref
  16.5 0.0 collective-permute-done.7.rowb_ref
  16.5 0.0 copy-done.1
  16.5 0.0 copy-done.2
  16.5 0.0 copy-done.4
  16.5 0.0 copy-done.5
  16.5 2.2 %shard_map.90 = (f32[8,2,128,128]{3,2,1,0:T(8,128)S(1)}, f32[8,2,128,128]{3,2,1,0:T(8,128)S(1)}) custom-call(s32[1,8]{1,0:T(1,128)S(1)} %copy-done.4, s32[1,8]{1,0:T(1,128)S(1)} %copy-done.5, f32[2,2,256,256]{3,2,1,0:T(8,128)S(1)} %copy-done, f32[256,128]{1,0:T(8,128)S(1)} %collective-permute-done.4.colb_ref, ...), custom_call_target="tpu_custom_call" | custom-call | tf_op jit(solution)/shard_map/pallas_call | solution.py:370
  18.8 2.0 %collective-permute-done.2.rowa_ref = f32[6,64,128]{2,1,0:T(8,128)S(1)} collective-permute-done((f32[6,64,128]{2,1,0:T(8,128)S(1)}, f32[6,64,128]{2,1,0:T(8,128)S(1)}, u32[]{:S(2)}, u32[]{:S(2)}) %collective-permute-start.2) | collective-permute-done | bytes 196640 | tf_op jit(solution)/shard_map/ppermute | solution.py:360
  20.8 0.0 collective-permute-done.3.rowb_ref
  20.8 0.0 copy-done.3
  20.8 5.8 %shard_map.91 = (f32[8,2,128,128]{3,2,1,0:T(8,128)S(1)}, f32[8,2,128,128]{3,2,1,0:T(8,128)S(1)}, f32[128,128]{1,0:T(8,128)S(1)}, f32[128,128]{1,0:T(8,128)S(1)}) custom-call(s32[1,8]{1,0:T(1,128)S(1)} %copy-done.4, s32[1,8]{1,0:T(1,128)S(1)} %copy-done.5, s32[1,1]{1,0:T(1,128)S(6)} %copy.9.live_ref, f32[2,2,256,256]{3,2,1,0:T(8,128)S(1)} %copy-done, ...), custom_call_target="tpu_custom_call" | custom-call | tf_op jit(solution)/shard_map/pallas_call | solution.py:370
  26.6 1.0 %collective-permute-start.8 = (f32[128,128]{1,0:T(8,128)S(1)}, f32[128,128]{1,0:T(8,128)S(1)}, u32[]{:S(2)}, u32[]{:S(2)}) collective-permute-start(f32[128,128]{1,0:T(8,128)S(1)} %get-tuple-element.49), channel_id=1, source_target_pairs={{0,1},{1,0},{2,3},{3,2},{4,5},{5,4},{6,7},{7,6},{8,9},{9,8},{10,11... | collective-permute-start | bytes 196616 | tf_op jit(solution)/shard_map/ppermute | solution.py:366
  27.6 0.9 %collective-permute-done.8 = f32[128,128]{1,0:T(8,128)S(1)} collective-permute-done((f32[128,128]{1,0:T(8,128)S(1)}, f32[128,128]{1,0:T(8,128)S(1)}, u32[]{:S(2)}, u32[]{:S(2)}) %collective-permute-start.8) | collective-permute-done | bytes 65568 | tf_op jit(solution)/shard_map/ppermute | solution.py:366
  28.6 3.3 %collective-permute-start.9 = (f32[128,128]{1,0:T(8,128)S(1)}, f32[128,128]{1,0:T(8,128)S(1)}, u32[]{:S(2)}, u32[]{:S(2)}) collective-permute-start(f32[128,128]{1,0:T(8,128)S(1)} %add.24), channel_id=1, source_target_pairs={{0,16},{1,17},{2,18},{3,19},{4,20},{5,21},{6,22},{7,23},{8,24},{9,... | collective-permute-start | bytes 196616 | tf_op jit(solution)/shard_map/ppermute | solution.py:366
  31.9 2.3 %shard_map.92 = (f32[2,2,256,256]{3,2,1,0:T(8,128)S(1)}, f32[2,6,64,128]{3,2,1,0:T(8,128)S(1)}, f32[2,6,64,128]{3,2,1,0:T(8,128)S(1)}, f32[2,256,128]{2,1,0:T(8,128)S(1)}, f32[2,256,128]{2,1,0:T(8,128)S(1)}) custom-call(s32[1,8]{1,0:T(1,128)S(1)} %copy-done.4, s32[1,8]{1,0:T(1,128)S(1)} %copy-done.5, f32[2,2,256,256]{3,2,1,0:T(8,128)S(1)} %copy-done, ...), custom_call_target="tpu_custom_call" | custom-call | tf_op jit(solution)/shard_map/pallas_call | solution.py:370
  34.2 0.0 collective-permute-done.9
  34.2 0.9 %collective-permute-start.13 = (f32[2,6,64,128]{3,2,1,0:T(8,128)S(1)}, f32[2,6,64,128]{3,2,1,0:T(8,128)S(1)}, u32[]{:S(2)}, u32[]{:S(2)}) collective-permute-start(f32[2,6,64,128]{3,2,1,0:T(8,128)S(1)} %get-tuple-element.53), channel_id=1, source_target_pairs={{0,16},{1,17},{2,18},{3,19},{4,20},{5,21},{6,22},{7,23},{8,24},{9,... | collective-permute-start | bytes 1179656 | tf_op jit(solution)/shard_map/ppermute | solution.py:360
  35.1 1.8 %collective-permute-start.14 = (f32[2,6,64,128]{3,2,1,0:T(8,128)S(1)}, f32[2,6,64,128]{3,2,1,0:T(8,128)S(1)}, u32[]{:S(2)}, u32[]{:S(2)}) collective-permute-start(f32[2,6,64,128]{3,2,1,0:T(8,128)S(1)} %get-tuple-element.54), channel_id=1, source_target_pairs={{0,1},{1,0},{2,3},{3,2},{4,5},{5,4},{6,7},{7,6},{8,9},{9,8},{10,11... | collective-permute-start | bytes 1179656 | tf_op jit(solution)/shard_map/ppermute | solution.py:360
  36.9 3.6 %collective-permute-start.10 = (f32[128,128]{1,0:T(8,128)S(1)}, f32[128,128]{1,0:T(8,128)S(1)}, u32[]{:S(2)}, u32[]{:S(2)}) collective-permute-start(f32[128,128]{1,0:T(8,128)S(1)} %add.25), channel_id=1, source_target_pairs={{0,4},{1,13},{2,6},{3,15},{4,0},{5,9},{6,2},{7,11},{8,12},{9,5},{1... | collective-permute-start | bytes 196616 | tf_op jit(solution)/shard_map/ppermute | solution.py:366
  40.5 1.7 %collective-permute-done.10 = f32[128,128]{1,0:T(8,128)S(1)} collective-permute-done((f32[128,128]{1,0:T(8,128)S(1)}, f32[128,128]{1,0:T(8,128)S(1)}, u32[]{:S(2)}, u32[]{:S(2)}) %collective-permute-start.10) | collective-permute-done | bytes 65568 | tf_op jit(solution)/shard_map/ppermute | solution.py:366
  42.2 0.5 collective-permute-start.11
  42.7 2.8 %collective-permute-done.11 = f32[128,128]{1,0:T(8,128)S(1)} collective-permute-done((f32[128,128]{1,0:T(8,128)S(1)}, f32[128,128]{1,0:T(8,128)S(1)}, u32[]{:S(2)}, u32[]{:S(2)}) %collective-permute-start.11) | collective-permute-done | bytes 65568 | tf_op jit(solution)/shard_map/ppermute | solution.py:366
  45.5 6.5 %collective-permute-start.12 = (f32[128,128]{1,0:T(8,128)S(1)}, f32[128,128]{1,0:T(8,128)S(1)}, u32[]{:S(2)}, u32[]{:S(2)}) collective-permute-start(f32[128,128]{1,0:T(8,128)S(1)} %add.27), channel_id=1, source_target_pairs={{0,128},{1,131},{2,130},{3,129},{4,132},{5,135},{6,134},{7,133},{8... | collective-permute-start | bytes 196616 | tf_op jit(solution)/shard_map/ppermute | solution.py:366
  52.0 1.7 %collective-permute-done.12 = f32[128,128]{1,0:T(8,128)S(1)} collective-permute-done((f32[128,128]{1,0:T(8,128)S(1)}, f32[128,128]{1,0:T(8,128)S(1)}, u32[]{:S(2)}, u32[]{:S(2)}) %collective-permute-start.12) | collective-permute-done | bytes 65568 | tf_op jit(solution)/shard_map/ppermute | solution.py:366
  53.7 0.0 collective-permute-done.13.rowa_ref
  53.7 0.0 collective-permute-done.14.rowb_ref
  53.7 0.7 collective-permute-start.15
  54.3 0.1 shard_map.93
  54.4 2.5 %collective-permute-done.15 = f32[128,128]{1,0:T(8,128)S(1)} collective-permute-done((f32[128,128]{1,0:T(8,128)S(1)}, f32[128,128]{1,0:T(8,128)S(1)}, u32[]{:S(2)}, u32[]{:S(2)}) %collective-permute-start.15) | collective-permute-done | bytes 65568 | tf_op jit(solution)/shard_map/ppermute | solution.py:366
  56.9 6.2 %collective-permute-start.18 = (f32[2,256,128]{2,1,0:T(8,128)S(1)}, f32[2,256,128]{2,1,0:T(8,128)S(1)}, u32[]{:S(2)}, u32[]{:S(2)}) collective-permute-start(f32[2,256,128]{2,1,0:T(8,128)S(1)} %get-tuple-element.63), channel_id=1, source_target_pairs={{0,16},{1,2},{2,1},{3,4},{4,3},{5,6},{6,5},{7,8},{8,7},{9,10},{10,... | collective-permute-start | bytes 786440 | tf_op jit(solution)/shard_map/ppermute | solution.py:360
  63.1 0.0 collective-permute-start.19
  63.1 1.8 %collective-permute-start.16 = (f32[128,128]{1,0:T(8,128)S(1)}, f32[128,128]{1,0:T(8,128)S(1)}, u32[]{:S(2)}, u32[]{:S(2)}) collective-permute-start(f32[128,128]{1,0:T(8,128)S(1)} %add.29), channel_id=1, source_target_pairs={{0,32},{1,97},{2,34},{3,99},{4,36},{5,101},{6,38},{7,103},{8,40},{... | collective-permute-start | bytes 196616 | tf_op jit(solution)/shard_map/ppermute | solution.py:366
  64.9 4.6 %collective-permute-done.16 = f32[128,128]{1,0:T(8,128)S(1)} collective-permute-done((f32[128,128]{1,0:T(8,128)S(1)}, f32[128,128]{1,0:T(8,128)S(1)}, u32[]{:S(2)}, u32[]{:S(2)}) %collective-permute-start.16) | collective-permute-done | bytes 65568 | tf_op jit(solution)/shard_map/ppermute | solution.py:366
  69.5 0.1 collective-permute-start.17
  69.6 4.5 %collective-permute-done.17 = f32[128,128]{1,0:T(8,128)S(1)} collective-permute-done((f32[128,128]{1,0:T(8,128)S(1)}, f32[128,128]{1,0:T(8,128)S(1)}, u32[]{:S(2)}, u32[]{:S(2)}) %collective-permute-start.17) | collective-permute-done | bytes 65568 | tf_op jit(solution)/shard_map/ppermute | solution.py:366
  74.1 0.0 collective-permute-done.18.colb_ref
  74.1 0.0 collective-permute-done.19.cola_ref
  74.1 2.6 %collective-permute-start.20 = (f32[128,128]{1,0:T(8,128)S(1)}, f32[128,128]{1,0:T(8,128)S(1)}, u32[]{:S(2)}, u32[]{:S(2)}) collective-permute-start(f32[128,128]{1,0:T(8,128)S(1)} %add.31.mine_ref), channel_id=1, source_target_pairs={{0,1},{1,0},{2,3},{3,2},{4,5},{5,4},{6,7},{7,6},{8,9},{9,8},{10,11... | collective-permute-start | bytes 196616 | tf_op jit(solution)/shard_map/ppermute | solution.py:366
  76.7 1.2 %shard_map.94 = f32[2,2,256,256]{3,2,1,0:T(8,128)} custom-call(f32[2,2,256,256]{3,2,1,0:T(8,128)S(1)} %get-tuple-element.47.part_ref, f32[2,6,64,128]{3,2,1,0:T(8,128)S(1)} %collective-permute-done.13.rowa_ref, f32[2,6,64,128]{3,2,1,0:T(8,128)S(1)} %collective-permute-done.14.rowb_ref, f32[2,256,128]{2,1,0:T(8,128)S(1)} %collective-permute-done.18.colb_ref, ...), custom_call_target="tpu_custom_call" | custom-call | tf_op jit(solution)/shard_map/pallas_call | solution.py:370
  78.0 0.0 collective-permute-done.20.other_ref
  78.0 0.7 shard_map.95
  (10 shorter events, 0.2 us)
Async XLA Ops:
  0.6 9.4 %copy-start = (f32[2,2,256,256]{3,2,1,0:T(8,128)S(1)}, f32[2,2,256,256]{3,2,1,0:T(8,128)}, u32[]{:S(2)}) copy-start(f32[2,2,256,256]{3,2,1,0:T(8,128)} %obj_ref.13) | copy-start | bytes 3145732
  1.9 8.1 %collective-permute-start.4 = (f32[256,128]{1,0:T(8,128)S(1)}, f32[256,128]{1,0:T(8,128)S(1)}, u32[]{:S(2)}, u32[]{:S(2)}) collective-permute-start(f32[256,128]{1,0:T(8,128)S(1)} %get-tuple-element.39), channel_id=1, source_target_pairs={{0,16},{1,2},{2,1},{3,4},{4,3},{5,6},{6,5},{7,8},{8,7},{9,10},{10,... | collective-permute-start | bytes 393224 | tf_op jit(solution)/shard_map/ppermute | solution.py:360
  6.3 3.7 %collective-permute-start.5 = (f32[256,128]{1,0:T(8,128)S(1)}, f32[256,128]{1,0:T(8,128)S(1)}, u32[]{:S(2)}, u32[]{:S(2)}) collective-permute-start(f32[256,128]{1,0:T(8,128)S(1)} %get-tuple-element.40), channel_id=1, source_target_pairs={{0,1},{1,0},{2,3},{3,2},{4,5},{5,4},{6,7},{7,6},{8,9},{9,8},{10,11... | collective-permute-start | bytes 393224 | tf_op jit(solution)/shard_map/ppermute | solution.py:360
  7.5 6.0 %collective-permute-start = (f32[256,128]{1,0:T(8,128)S(1)}, f32[256,128]{1,0:T(8,128)S(1)}, u32[]{:S(2)}, u32[]{:S(2)}) collective-permute-start(f32[256,128]{1,0:T(8,128)S(1)} %get-tuple-element.35), channel_id=1, source_target_pairs={{0,16},{1,2},{2,1},{3,4},{4,3},{5,6},{6,5},{7,8},{8,7},{9,10},{10,... | collective-permute-start | bytes 393224 | tf_op jit(solution)/shard_map/ppermute | solution.py:360
  9.0 7.5 %copy-start.1 = (bf16[4,2,256,256]{3,2,1,0:T(8,128)(2,1)S(1)}, bf16[4,2,256,256]{3,2,1,0:T(8,128)(2,1)}, u32[]{:S(2)}) copy-start(bf16[4,2,256,256]{3,2,1,0:T(8,128)(2,1)} %constant.2.clone.tabs_ref) | copy-start | bytes 3145732
  9.0 4.5 %collective-permute-start.1 = (f32[256,128]{1,0:T(8,128)S(1)}, f32[256,128]{1,0:T(8,128)S(1)}, u32[]{:S(2)}, u32[]{:S(2)}) collective-permute-start(f32[256,128]{1,0:T(8,128)S(1)} %get-tuple-element.36), channel_id=1, source_target_pairs={{0,1},{1,0},{2,3},{3,2},{4,5},{5,4},{6,7},{7,6},{8,9},{9,8},{10,11... | collective-permute-start | bytes 393224 | tf_op jit(solution)/shard_map/ppermute | solution.py:360
  10.1 6.4 %collective-permute-start.6 = (f32[6,64,128]{2,1,0:T(8,128)S(1)}, f32[6,64,128]{2,1,0:T(8,128)S(1)}, u32[]{:S(2)}, u32[]{:S(2)}) collective-permute-start(f32[6,64,128]{2,1,0:T(8,128)S(1)} %get-tuple-element.41), channel_id=1, source_target_pairs={{0,16},{1,17},{2,18},{3,19},{4,20},{5,21},{6,22},{7,23},{8,24},{9,... | collective-permute-start | bytes 589832 | tf_op jit(solution)/shard_map/ppermute | solution.py:360
  11.4 5.1 %copy-start.2 = (f32[2,128,128]{2,1,0:T(8,128)S(1)}, f32[2,128,128]{2,1,0:T(8,128)}, u32[]{:S(2)}) copy-start(f32[2,128,128]{2,1,0:T(8,128)} %probe_ref.5) | copy-start | bytes 393220
  11.4 5.1 %collective-permute-start.7 = (f32[6,64,128]{2,1,0:T(8,128)S(1)}, f32[6,64,128]{2,1,0:T(8,128)S(1)}, u32[]{:S(2)}, u32[]{:S(2)}) collective-permute-start(f32[6,64,128]{2,1,0:T(8,128)S(1)} %get-tuple-element.42), channel_id=1, source_target_pairs={{0,1},{1,0},{2,3},{3,2},{4,5},{5,4},{6,7},{7,6},{8,9},{9,8},{10,11... | collective-permute-start | bytes 589832 | tf_op jit(solution)/shard_map/ppermute | solution.py:360
  13.5 7.2 %collective-permute-start.2 = (f32[6,64,128]{2,1,0:T(8,128)S(1)}, f32[6,64,128]{2,1,0:T(8,128)S(1)}, u32[]{:S(2)}, u32[]{:S(2)}) collective-permute-start(f32[6,64,128]{2,1,0:T(8,128)S(1)} %get-tuple-element.37), channel_id=1, source_target_pairs={{0,16},{1,17},{2,18},{3,19},{4,20},{5,21},{6,22},{7,23},{8,24},{9,... | collective-permute-start | bytes 589832 | tf_op jit(solution)/shard_map/ppermute | solution.py:360
  15.3 1.2 %copy-start.4 = (s32[1,8]{1,0:T(1,128)S(1)}, s32[1,8]{1,0:T(1,128)}, u32[]{:S(2)}) copy-start(s32[1,8]{1,0:T(1,128)} %row_ref.5) | copy-start | bytes 100
  15.3 1.3 %copy-start.5 = (s32[1,8]{1,0:T(1,128)S(1)}, s32[1,8]{1,0:T(1,128)}, u32[]{:S(2)}) copy-start(s32[1,8]{1,0:T(1,128)} %col_ref.5) | copy-start | bytes 100
  15.3 5.5 %collective-permute-start.3 = (f32[6,64,128]{2,1,0:T(8,128)S(1)}, f32[6,64,128]{2,1,0:T(8,128)S(1)}, u32[]{:S(2)}, u32[]{:S(2)}) collective-permute-start(f32[6,64,128]{2,1,0:T(8,128)S(1)} %get-tuple-element.38), channel_id=1, source_target_pairs={{0,1},{1,0},{2,3},{3,2},{4,5},{5,4},{6,7},{7,6},{8,9},{9,8},{10,11... | collective-permute-start | bytes 589832 | tf_op jit(solution)/shard_map/ppermute | solution.py:360
  16.2 4.6 %copy-start.3 = (f32[1,8,128,128]{3,2,1,0:T(8,128)S(1)}, f32[1,8,128,128]{3,2,1,0:T(8,128)}, u32[]{:S(2)}) copy-start(f32[1,8,128,128]{3,2,1,0:T(8,128)} %param.9) | copy-start | bytes 1572868
  26.6 1.9 %collective-permute-start.8 = (f32[128,128]{1,0:T(8,128)S(1)}, f32[128,128]{1,0:T(8,128)S(1)}, u32[]{:S(2)}, u32[]{:S(2)}) collective-permute-start(f32[128,128]{1,0:T(8,128)S(1)} %get-tuple-element.49), channel_id=1, source_target_pairs={{0,1},{1,0},{2,3},{3,2},{4,5},{5,4},{6,7},{7,6},{8,9},{9,8},{10,11... | collective-permute-start | bytes 196616 | tf_op jit(solution)/shard_map/ppermute | solution.py:366
  28.6 5.6 %collective-permute-start.9 = (f32[128,128]{1,0:T(8,128)S(1)}, f32[128,128]{1,0:T(8,128)S(1)}, u32[]{:S(2)}, u32[]{:S(2)}) collective-permute-start(f32[128,128]{1,0:T(8,128)S(1)} %add.24), channel_id=1, source_target_pairs={{0,16},{1,17},{2,18},{3,19},{4,20},{5,21},{6,22},{7,23},{8,24},{9,... | collective-permute-start | bytes 196616 | tf_op jit(solution)/shard_map/ppermute | solution.py:366
  34.2 19.4 %collective-permute-start.13 = (f32[2,6,64,128]{3,2,1,0:T(8,128)S(1)}, f32[2,6,64,128]{3,2,1,0:T(8,128)S(1)}, u32[]{:S(2)}, u32[]{:S(2)}) collective-permute-start(f32[2,6,64,128]{3,2,1,0:T(8,128)S(1)} %get-tuple-element.53), channel_id=1, source_target_pairs={{0,16},{1,17},{2,18},{3,19},{4,20},{5,21},{6,22},{7,23},{8,24},{9,... | collective-permute-start | bytes 1179656 | tf_op jit(solution)/shard_map/ppermute | solution.py:360
  35.1 18.6 %collective-permute-start.14 = (f32[2,6,64,128]{3,2,1,0:T(8,128)S(1)}, f32[2,6,64,128]{3,2,1,0:T(8,128)S(1)}, u32[]{:S(2)}, u32[]{:S(2)}) collective-permute-start(f32[2,6,64,128]{3,2,1,0:T(8,128)S(1)} %get-tuple-element.54), channel_id=1, source_target_pairs={{0,1},{1,0},{2,3},{3,2},{4,5},{5,4},{6,7},{7,6},{8,9},{9,8},{10,11... | collective-permute-start | bytes 1179656 | tf_op jit(solution)/shard_map/ppermute | solution.py:360
  36.9 5.3 %collective-permute-start.10 = (f32[128,128]{1,0:T(8,128)S(1)}, f32[128,128]{1,0:T(8,128)S(1)}, u32[]{:S(2)}, u32[]{:S(2)}) collective-permute-start(f32[128,128]{1,0:T(8,128)S(1)} %add.25), channel_id=1, source_target_pairs={{0,4},{1,13},{2,6},{3,15},{4,0},{5,9},{6,2},{7,11},{8,12},{9,5},{1... | collective-permute-start | bytes 196616 | tf_op jit(solution)/shard_map/ppermute | solution.py:366
  42.2 3.3 %collective-permute-start.11 = (f32[128,128]{1,0:T(8,128)S(1)}, f32[128,128]{1,0:T(8,128)S(1)}, u32[]{:S(2)}, u32[]{:S(2)}) collective-permute-start(f32[128,128]{1,0:T(8,128)S(1)} %add.26), channel_id=1, source_target_pairs={{0,12},{1,5},{2,14},{3,7},{4,8},{5,1},{6,10},{7,3},{8,4},{9,13},{1... | collective-permute-start | bytes 196616 | tf_op jit(solution)/shard_map/ppermute | solution.py:366
  45.5 8.2 %collective-permute-start.12 = (f32[128,128]{1,0:T(8,128)S(1)}, f32[128,128]{1,0:T(8,128)S(1)}, u32[]{:S(2)}, u32[]{:S(2)}) collective-permute-start(f32[128,128]{1,0:T(8,128)S(1)} %add.27), channel_id=1, source_target_pairs={{0,128},{1,131},{2,130},{3,129},{4,132},{5,135},{6,134},{7,133},{8... | collective-permute-start | bytes 196616 | tf_op jit(solution)/shard_map/ppermute | solution.py:366
  53.7 3.2 %collective-permute-start.15 = (f32[128,128]{1,0:T(8,128)S(1)}, f32[128,128]{1,0:T(8,128)S(1)}, u32[]{:S(2)}, u32[]{:S(2)}) collective-permute-start(f32[128,128]{1,0:T(8,128)S(1)} %add.28), channel_id=1, source_target_pairs={{0,130},{1,129},{2,128},{3,131},{4,134},{5,133},{6,132},{7,135},{8... | collective-permute-start | bytes 196616 | tf_op jit(solution)/shard_map/ppermute | solution.py:366
  56.9 17.2 %collective-permute-start.18 = (f32[2,256,128]{2,1,0:T(8,128)S(1)}, f32[2,256,128]{2,1,0:T(8,128)S(1)}, u32[]{:S(2)}, u32[]{:S(2)}) collective-permute-start(f32[2,256,128]{2,1,0:T(8,128)S(1)} %get-tuple-element.63), channel_id=1, source_target_pairs={{0,16},{1,2},{2,1},{3,4},{4,3},{5,6},{6,5},{7,8},{8,7},{9,10},{10,... | collective-permute-start | bytes 786440 | tf_op jit(solution)/shard_map/ppermute | solution.py:360
  63.1 11.0 %collective-permute-start.19 = (f32[2,256,128]{2,1,0:T(8,128)S(1)}, f32[2,256,128]{2,1,0:T(8,128)S(1)}, u32[]{:S(2)}, u32[]{:S(2)}) collective-permute-start(f32[2,256,128]{2,1,0:T(8,128)S(1)} %get-tuple-element.64), channel_id=1, source_target_pairs={{0,1},{1,0},{2,3},{3,2},{4,5},{5,4},{6,7},{7,6},{8,9},{9,8},{10,11... | collective-permute-start | bytes 786440 | tf_op jit(solution)/shard_map/ppermute | solution.py:360
  63.1 6.4 %collective-permute-start.16 = (f32[128,128]{1,0:T(8,128)S(1)}, f32[128,128]{1,0:T(8,128)S(1)}, u32[]{:S(2)}, u32[]{:S(2)}) collective-permute-start(f32[128,128]{1,0:T(8,128)S(1)} %add.29), channel_id=1, source_target_pairs={{0,32},{1,97},{2,34},{3,99},{4,36},{5,101},{6,38},{7,103},{8,40},{... | collective-permute-start | bytes 196616 | tf_op jit(solution)/shard_map/ppermute | solution.py:366
  69.5 4.6 %collective-permute-start.17 = (f32[128,128]{1,0:T(8,128)S(1)}, f32[128,128]{1,0:T(8,128)S(1)}, u32[]{:S(2)}, u32[]{:S(2)}) collective-permute-start(f32[128,128]{1,0:T(8,128)S(1)} %add.30), channel_id=1, source_target_pairs={{0,96},{1,33},{2,98},{3,35},{4,100},{5,37},{6,102},{7,39},{8,104},... | collective-permute-start | bytes 196616 | tf_op jit(solution)/shard_map/ppermute | solution.py:366
  74.1 3.9 %collective-permute-start.20 = (f32[128,128]{1,0:T(8,128)S(1)}, f32[128,128]{1,0:T(8,128)S(1)}, u32[]{:S(2)}, u32[]{:S(2)}) collective-permute-start(f32[128,128]{1,0:T(8,128)S(1)} %add.31.mine_ref), channel_id=1, source_target_pairs={{0,1},{1,0},{2,3},{3,2},{4,5},{5,4},{6,7},{7,6},{8,9},{9,8},{10,11... | collective-permute-start | bytes 196616 | tf_op jit(solution)/shard_map/ppermute | solution.py:366

commit v16 on v15

--- a/solution.py
+++ b/solution.py
@@ -344,21 +344,26 @@
     return jax.ShapeDtypeStruct(shape, jnp.float32)
 
 
-def meet(strips, axis):
+def meet(strip, axis, odd):
     sizes = (lax.axis_size("row"), lax.axis_size("col"))
-    got = []
-    for odd, strip in zip((axis, 1 - axis), strips):
-        pairs = []
-        for spot in np.ndindex(*sizes):
-            other = list(spot)
-            place = ((spot[axis] + odd) ^ 1) - odd
-            if 0 <= place < sizes[axis]:
-                other[axis] = place
-            else:
-                other[1 - axis] ^= 1
-            pairs.append((spot[0] * sizes[1] + spot[1], other[0] * sizes[1] + other[1]))
-        got.append(lax.ppermute(strip, BOTH, pairs))
-    return got
+    pairs = []
+    for spot in np.ndindex(*sizes):
+        other = list(spot)
+        place = ((spot[axis] + odd) ^ 1) - odd
+        if 0 <= place < sizes[axis]:
+            other[axis] = place
+        else:
+            other[1 - axis] ^= 1
+        pairs.append((spot[0] * sizes[1] + spot[1], other[0] * sizes[1] + other[1]))
+    return lax.ppermute(strip, BOTH, pairs)
+
+
+def meet_rows(strips):
+    return [meet(strips[0], 0, 0), meet(strips[1], 0, 1)]
+
+
+def meet_cols(strips):
+    return [meet(strips[0], 1, 1), meet(strips[1], 1, 0)]
 
 
 def swap(value, masks):
@@ -393,13 +398,13 @@
         for piece in range(2)
     ]
     halos = []
-    cols = [meet(packed[piece], 1) for piece in range(2)]
+    cols = [meet_cols(packed[piece]) for piece in range(2)]
     for piece in range(2):
         strips = call(
             functools.partial(rows_kernel, piece=piece), [array(*edge)] * 2,
             (), (object_field, *cols[piece]),
         )
-        halos.append((*cols[piece], *meet(strips, 0)))
+        halos.append((*cols[piece], *meet_rows(strips)))
     win, mid = call(
         functools.partial(first_kernel, group=2), [fields] * 2, (offset_row, offset_col),
         (object_field, *halos[0], probe, tabs), (grown,),
@@ -416,17 +421,24 @@
     )
     mine = mine + swap(send, (1, 1))
     mine = mine + swap(mine, MASKS[0])
-    mine, *strips = lax.optimization_barrier((mine, *strips))
-    rows = meet(strips, 0)
-    for mask in MASKS[1:4]:
+    rows = [None, None]
+    mine, strips[1] = lax.optimization_barrier((mine, strips[1]))
+    rows[1] = meet(strips[1], 0, 1)
+    mine = mine + swap(mine, MASKS[1])
+    mine, strips[0] = lax.optimization_barrier((mine, strips[0]))
+    rows[0] = meet(strips[0], 0, 0)
+    for mask in MASKS[2:4]:
         mine = mine + swap(mine, mask)
     mine, *rows = lax.optimization_barrier((mine, *rows))
     strips = call(fold_kernel, [array(2, *side)] * 2, (), (left, right, *rows))
     mine = mine + swap(mine, MASKS[4])
+    cols = [None, None]
     mine, *strips = lax.optimization_barrier((mine, *strips))
-    cols = meet(strips, 1)
-    for mask in MASKS[5:]:
-        mine = mine + swap(mine, mask)
+    cols[0] = meet(strips[0], 1, 1)
+    mine = mine + swap(mine, MASKS[5])
+    mine, strips[1] = lax.optimization_barrier((mine, strips[1]))
+    cols[1] = meet(strips[1], 1, 0)
+    mine = mine + swap(mine, MASKS[6])
     mine, *cols = lax.optimization_barrier((mine, *cols))
     (new,) = call(finish_kernel, (field,), (), (part, *rows, *cols))
     other = swap(mine, (1, 1))

time: 78.8 us -> 74 us (0.939)
  waiting for transfers between devices: 22.8 us -> 16.9 us
  starting transfers between devices: 39.4 us -> 40.2 us
    ppermute x9, waiting for transfers between devices: 18.5 us -> 11.4 us  [swap(): lax.ppermute(value, BOTH, [(i, i ^ masks[i % 2]) for i in range(count)])]
    ppermute x9, starting transfers between devices: 20.1 us -> 22.5 us  [swap(): lax.ppermute(value, BOTH, [(i, i ^ masks[i % 2]) for i in range(count)])]
    ppermute x12, starting transfers between devices: 19.3 us -> 17.7 us  [meet(): return lax.ppermute(strip, BOTH, pairs)]
    ppermute x12, waiting for transfers between devices: 4.29 us -> 5.54 us  [meet(): return lax.ppermute(strip, BOTH, pairs)]
  transfers between devices with their start and end apart: 21 -> 21, of which waited for: 10 -> 10; matrix products, arithmetic and copies ran while one was open for 0% -> 0% of each run, Pallas kernels for 9% -> 10%
where the time goes in v16:
time: 74 us; the launch traced here: 73.6 us
  starting transfers between devices  40.2 us (54%)
  waiting for transfers between devices  16.9 us (23%)
  Pallas kernels  14.9 us (20%)
  between operations  1.46 us (2%)
    ppermute x9, starting transfers between devices, swap(): lax.ppermute(value, BOTH, [(i, i ^ masks[i % 2]) for i in range(count)])  22.5 us
    ppermute x12, starting transfers between devices, meet(): return lax.ppermute(strip, BOTH, pairs)  17.7 us
    pallas_call x8, Pallas kernels, call(): pl.pallas_call(kernel, out_shape=tuple(out_shape), in_specs=smem(len(scal...  12.4 us
    ppermute x9, waiting for transfers between devices, swap(): lax.ppermute(value, BOTH, [(i, i ^ masks[i % 2]) for i in range(count)])  11.4 us
    ppermute x12, waiting for transfers between devices, meet(): return lax.ppermute(strip, BOTH, pairs)  5.54 us
    pallas_call x2, Pallas kernels, on_device(): pl.pallas_call(functools.partial(pack_kernel, piece=piece), out_shape=tup...  2.46 us
  transfers between devices with their start and end apart: 21, of which 10 were waited for; matrix products, arithmetic and copies ran while one was open for 0% of the time, Pallas kernels for 10%

profile of v16, /device:TPU:1, one launch (start us, length us, event | category | flops | bytes accessed | tf_op | source)
XLA Modules:
  0.0 73.6 jit_solution(5189098903465614509)
XLA Ops:
  0.6 0.0 copy-start
  0.6 1.3 %shard_map.88 = (f32[256,128]{1,0:T(8,128)S(1)}, f32[256,128]{1,0:T(8,128)S(1)}) custom-call(f32[2,2,256,256]{3,2,1,0:T(8,128)} %obj_ref.13), custom_call_target="tpu_custom_call" | custom-call | tf_op jit(solution)/shard_map/pallas_call | solution.py:392
  1.9 4.4 %collective-permute-start.4 = (f32[256,128]{1,0:T(8,128)S(1)}, f32[256,128]{1,0:T(8,128)S(1)}, u32[]{:S(2)}, u32[]{:S(2)}) collective-permute-start(f32[256,128]{1,0:T(8,128)S(1)} %get-tuple-element.42), channel_id=1, source_target_pairs={{0,16},{1,2},{2,1},{3,4},{4,3},{5,6},{6,5},{7,8},{8,7},{9,10},{10,... | collective-permute-start | bytes 393224 | tf_op jit(solution)/shard_map/ppermute | solution.py:358
  6.3 0.0 collective-permute-start.5
  6.3 1.2 %shard_map.86 = (f32[256,128]{1,0:T(8,128)S(1)}, f32[256,128]{1,0:T(8,128)S(1)}) custom-call(f32[2,2,256,256]{3,2,1,0:T(8,128)} %obj_ref.13), custom_call_target="tpu_custom_call" | custom-call | tf_op jit(solution)/shard_map/pallas_call | solution.py:392
  7.5 1.5 %collective-permute-start = (f32[256,128]{1,0:T(8,128)S(1)}, f32[256,128]{1,0:T(8,128)S(1)}, u32[]{:S(2)}, u32[]{:S(2)}) collective-permute-start(f32[256,128]{1,0:T(8,128)S(1)} %get-tuple-element.38), channel_id=1, source_target_pairs={{0,16},{1,2},{2,1},{3,4},{4,3},{5,6},{6,5},{7,8},{8,7},{9,10},{10,... | collective-permute-start | bytes 393224 | tf_op jit(solution)/shard_map/ppermute | solution.py:358
  9.0 0.0 copy-start.1
  9.0 1.0 %collective-permute-start.1 = (f32[256,128]{1,0:T(8,128)S(1)}, f32[256,128]{1,0:T(8,128)S(1)}, u32[]{:S(2)}, u32[]{:S(2)}) collective-permute-start(f32[256,128]{1,0:T(8,128)S(1)} %get-tuple-element.39), channel_id=1, source_target_pairs={{0,1},{1,0},{2,3},{3,2},{4,5},{5,4},{6,7},{7,6},{8,9},{9,8},{10,11... | collective-permute-start | bytes 393224 | tf_op jit(solution)/shard_map/ppermute | solution.py:358
  10.0 0.0 collective-permute-done.4.colb_ref
  10.0 0.0 collective-permute-done.5.cola_ref
  10.0 0.0 copy-done
  10.1 1.3 %collective-permute-start.6 = (f32[6,64,128]{2,1,0:T(8,128)S(1)}, f32[6,64,128]{2,1,0:T(8,128)S(1)}, u32[]{:S(2)}, u32[]{:S(2)}) collective-permute-start(f32[6,64,128]{2,1,0:T(8,128)S(1)} %get-tuple-element.44), channel_id=1, source_target_pairs={{0,16},{1,17},{2,18},{3,19},{4,20},{5,21},{6,22},{7,23},{8,24},{9,... | collective-permute-start | bytes 589832 | tf_op jit(solution)/shard_map/ppermute | solution.py:358
  11.4 0.0 copy-start.2
  11.4 0.1 collective-permute-start.7
  11.6 1.9 %collective-permute-done.colb_ref = f32[256,128]{1,0:T(8,128)S(1)} collective-permute-done((f32[256,128]{1,0:T(8,128)S(1)}, f32[256,128]{1,0:T(8,128)S(1)}, u32[]{:S(2)}, u32[]{:S(2)}) %collective-permute-start) | collective-permute-done | bytes 131104 | tf_op jit(solution)/shard_map/ppermute | solution.py:358
  13.5 0.0 collective-permute-done.1.cola_ref
  13.5 1.7 %collective-permute-start.2 = (f32[6,64,128]{2,1,0:T(8,128)S(1)}, f32[6,64,128]{2,1,0:T(8,128)S(1)}, u32[]{:S(2)}, u32[]{:S(2)}) collective-permute-start(f32[6,64,128]{2,1,0:T(8,128)S(1)} %get-tuple-element.40), channel_id=1, source_target_pairs={{0,16},{1,17},{2,18},{3,19},{4,20},{5,21},{6,22},{7,23},{8,24},{9,... | collective-permute-start | bytes 589832 | tf_op jit(solution)/shard_map/ppermute | solution.py:358
  15.3 0.0 copy-start.4
  15.3 0.0 copy-start.5
  15.3 0.3 collective-permute-start.3
  16.2 0.0 copy-start.3
  16.2 0.3 collective-permute-done.6.rowa_ref
  16.5 0.0 collective-permute-done.7.rowb_ref
  16.5 0.0 copy-done.1
  16.5 0.0 copy-done.2
  16.5 0.0 copy-done.4
  16.5 0.0 copy-done.5
  16.5 2.2 %shard_map.90 = (f32[8,2,128,128]{3,2,1,0:T(8,128)S(1)}, f32[8,2,128,128]{3,2,1,0:T(8,128)S(1)}) custom-call(s32[1,8]{1,0:T(1,128)S(1)} %copy-done.4, s32[1,8]{1,0:T(1,128)S(1)} %copy-done.5, f32[2,2,256,256]{3,2,1,0:T(8,128)S(1)} %copy-done, f32[256,128]{1,0:T(8,128)S(1)} %collective-permute-done.4.colb_ref, ...), custom_call_target="tpu_custom_call" | custom-call | tf_op jit(solution)/shard_map/pallas_call | solution.py:375
  18.8 2.0 %collective-permute-done.2.rowa_ref = f32[6,64,128]{2,1,0:T(8,128)S(1)} collective-permute-done((f32[6,64,128]{2,1,0:T(8,128)S(1)}, f32[6,64,128]{2,1,0:T(8,128)S(1)}, u32[]{:S(2)}, u32[]{:S(2)}) %collective-permute-start.2) | collective-permute-done | bytes 196640 | tf_op jit(solution)/shard_map/ppermute | solution.py:358
  20.8 0.0 collective-permute-done.3.rowb_ref
  20.8 0.0 copy-done.3
  20.8 5.8 %shard_map.91 = (f32[8,2,128,128]{3,2,1,0:T(8,128)S(1)}, f32[8,2,128,128]{3,2,1,0:T(8,128)S(1)}, f32[128,128]{1,0:T(8,128)S(1)}, f32[128,128]{1,0:T(8,128)S(1)}) custom-call(s32[1,8]{1,0:T(1,128)S(1)} %copy-done.4, s32[1,8]{1,0:T(1,128)S(1)} %copy-done.5, s32[1,1]{1,0:T(1,128)S(6)} %copy.9.live_ref, f32[2,2,256,256]{3,2,1,0:T(8,128)S(1)} %copy-done, ...), custom_call_target="tpu_custom_call" | custom-call | tf_op jit(solution)/shard_map/pallas_call | solution.py:375
  26.7 1.0 %collective-permute-start.8 = (f32[128,128]{1,0:T(8,128)S(1)}, f32[128,128]{1,0:T(8,128)S(1)}, u32[]{:S(2)}, u32[]{:S(2)}) collective-permute-start(f32[128,128]{1,0:T(8,128)S(1)} %get-tuple-element.52), channel_id=1, source_target_pairs={{0,1},{1,0},{2,3},{3,2},{4,5},{5,4},{6,7},{7,6},{8,9},{9,8},{10,11... | collective-permute-start | bytes 196616 | tf_op jit(solution)/shard_map/ppermute | solution.py:371
  27.6 0.9 %collective-permute-done.8 = f32[128,128]{1,0:T(8,128)S(1)} collective-permute-done((f32[128,128]{1,0:T(8,128)S(1)}, f32[128,128]{1,0:T(8,128)S(1)}, u32[]{:S(2)}, u32[]{:S(2)}) %collective-permute-start.8) | collective-permute-done | bytes 65568 | tf_op jit(solution)/shard_map/ppermute | solution.py:371
  28.6 3.3 %collective-permute-start.9 = (f32[128,128]{1,0:T(8,128)S(1)}, f32[128,128]{1,0:T(8,128)S(1)}, u32[]{:S(2)}, u32[]{:S(2)}) collective-permute-start(f32[128,128]{1,0:T(8,128)S(1)} %add.24), channel_id=1, source_target_pairs={{0,16},{1,17},{2,18},{3,19},{4,20},{5,21},{6,22},{7,23},{8,24},{9,... | collective-permute-start | bytes 196616 | tf_op jit(solution)/shard_map/ppermute | solution.py:371
  31.9 2.3 %shard_map.92 = (f32[2,2,256,256]{3,2,1,0:T(8,128)S(1)}, f32[2,6,64,128]{3,2,1,0:T(8,128)S(1)}, f32[2,6,64,128]{3,2,1,0:T(8,128)S(1)}, f32[2,256,128]{2,1,0:T(8,128)S(1)}, f32[2,256,128]{2,1,0:T(8,128)S(1)}) custom-call(s32[1,8]{1,0:T(1,128)S(1)} %copy-done.4, s32[1,8]{1,0:T(1,128)S(1)} %copy-done.5, f32[2,2,256,256]{3,2,1,0:T(8,128)S(1)} %copy-done, ...), custom_call_target="tpu_custom_call" | custom-call | tf_op jit(solution)/shard_map/pallas_call | solution.py:375
  34.2 0.0 collective-permute-done.9
  34.2 3.7 %collective-permute-start.10 = (f32[128,128]{1,0:T(8,128)S(1)}, f32[128,128]{1,0:T(8,128)S(1)}, u32[]{:S(2)}, u32[]{:S(2)}) collective-permute-start(f32[128,128]{1,0:T(8,128)S(1)} %add.25), channel_id=1, source_target_pairs={{0,4},{1,13},{2,6},{3,15},{4,0},{5,9},{6,2},{7,11},{8,12},{9,5},{1... | collective-permute-start | bytes 196616 | tf_op jit(solution)/shard_map/ppermute | solution.py:371
  37.9 0.0 collective-permute-start.14
  37.9 1.7 %collective-permute-done.10 = f32[128,128]{1,0:T(8,128)S(1)} collective-permute-done((f32[128,128]{1,0:T(8,128)S(1)}, f32[128,128]{1,0:T(8,128)S(1)}, u32[]{:S(2)}, u32[]{:S(2)}) %collective-permute-start.10) | collective-permute-done | bytes 65568 | tf_op jit(solution)/shard_map/ppermute | solution.py:371
  39.6 2.0 %collective-permute-start.13 = (f32[2,6,64,128]{3,2,1,0:T(8,128)S(1)}, f32[2,6,64,128]{3,2,1,0:T(8,128)S(1)}, u32[]{:S(2)}, u32[]{:S(2)}) collective-permute-start(f32[2,6,64,128]{3,2,1,0:T(8,128)S(1)} %get-tuple-element.57), channel_id=1, source_target_pairs={{0,16},{1,17},{2,18},{3,19},{4,20},{5,21},{6,22},{7,23},{8,24},{9,... | collective-permute-start | bytes 1179656 | tf_op jit(solution)/shard_map/ppermute | solution.py:358
  41.6 0.0 collective-permute-start.11
  41.6 3.4 %collective-permute-done.11 = f32[128,128]{1,0:T(8,128)S(1)} collective-permute-done((f32[128,128]{1,0:T(8,128)S(1)}, f32[128,128]{1,0:T(8,128)S(1)}, u32[]{:S(2)}, u32[]{:S(2)}) %collective-permute-start.11) | collective-permute-done | bytes 65568 | tf_op jit(solution)/shard_map/ppermute | solution.py:371
  45.0 3.1 %collective-permute-start.12 = (f32[128,128]{1,0:T(8,128)S(1)}, f32[128,128]{1,0:T(8,128)S(1)}, u32[]{:S(2)}, u32[]{:S(2)}) collective-permute-start(f32[128,128]{1,0:T(8,128)S(1)} %add.27), channel_id=1, source_target_pairs={{0,128},{1,131},{2,130},{3,129},{4,132},{5,135},{6,134},{7,133},{8... | collective-permute-start | bytes 196616 | tf_op jit(solution)/shard_map/ppermute | solution.py:371
  48.1 1.7 %collective-permute-done.12 = f32[128,128]{1,0:T(8,128)S(1)} collective-permute-done((f32[128,128]{1,0:T(8,128)S(1)}, f32[128,128]{1,0:T(8,128)S(1)}, u32[]{:S(2)}, u32[]{:S(2)}) %collective-permute-start.12) | collective-permute-done | bytes 65568 | tf_op jit(solution)/shard_map/ppermute | solution.py:371
  49.8 0.0 collective-permute-done.14.rowb_ref
  49.8 1.3 %collective-permute-done.13.rowa_ref = f32[2,6,64,128]{3,2,1,0:T(8,128)S(1)} collective-permute-done((f32[2,6,64,128]{3,2,1,0:T(8,128)S(1)}, f32[2,6,64,128]{3,2,1,0:T(8,128)S(1)}, u32[]{:S(2)}, u32[]{:S(2)}) %collective-permute-start.13) | collective-permute-done | bytes 393248 | tf_op jit(solution)/shard_map/ppermute | solution.py:358
  51.0 3.9 %collective-permute-start.15 = (f32[128,128]{1,0:T(8,128)S(1)}, f32[128,128]{1,0:T(8,128)S(1)}, u32[]{:S(2)}, u32[]{:S(2)}) collective-permute-start(f32[128,128]{1,0:T(8,128)S(1)} %add.28), channel_id=1, source_target_pairs={{0,130},{1,129},{2,128},{3,131},{4,134},{5,133},{6,132},{7,135},{8... | collective-permute-start | bytes 196616 | tf_op jit(solution)/shard_map/ppermute | solution.py:371
  54.9 0.1 shard_map.93
  55.0 1.6 %collective-permute-done.15 = f32[128,128]{1,0:T(8,128)S(1)} collective-permute-done((f32[128,128]{1,0:T(8,128)S(1)}, f32[128,128]{1,0:T(8,128)S(1)}, u32[]{:S(2)}, u32[]{:S(2)}) %collective-permute-start.15) | collective-permute-done | bytes 65568 | tf_op jit(solution)/shard_map/ppermute | solution.py:371
  56.6 3.0 %collective-permute-start.16 = (f32[128,128]{1,0:T(8,128)S(1)}, f32[128,128]{1,0:T(8,128)S(1)}, u32[]{:S(2)}, u32[]{:S(2)}) collective-permute-start(f32[128,128]{1,0:T(8,128)S(1)} %add.29), channel_id=1, source_target_pairs={{0,32},{1,97},{2,34},{3,99},{4,36},{5,101},{6,38},{7,103},{8,40},{... | collective-permute-start | bytes 196616 | tf_op jit(solution)/shard_map/ppermute | solution.py:371
  59.5 2.7 %collective-permute-start.18 = (f32[2,256,128]{2,1,0:T(8,128)S(1)}, f32[2,256,128]{2,1,0:T(8,128)S(1)}, u32[]{:S(2)}, u32[]{:S(2)}) collective-permute-start(f32[2,256,128]{2,1,0:T(8,128)S(1)} %get-tuple-element.69), channel_id=1, source_target_pairs={{0,16},{1,2},{2,1},{3,4},{4,3},{5,6},{6,5},{7,8},{8,7},{9,10},{10,... | collective-permute-start | bytes 786440 | tf_op jit(solution)/shard_map/ppermute | solution.py:358
  62.2 0.0 collective-permute-done.16
  62.3 2.6 %collective-permute-start.19 = (f32[2,256,128]{2,1,0:T(8,128)S(1)}, f32[2,256,128]{2,1,0:T(8,128)S(1)}, u32[]{:S(2)}, u32[]{:S(2)}) collective-permute-start(f32[2,256,128]{2,1,0:T(8,128)S(1)} %get-tuple-element.70), channel_id=1, source_target_pairs={{0,1},{1,0},{2,3},{3,2},{4,5},{5,4},{6,7},{7,6},{8,9},{9,8},{10,11... | collective-permute-start | bytes 786440 | tf_op jit(solution)/shard_map/ppermute | solution.py:358
  64.8 1.8 %collective-permute-start.17 = (f32[128,128]{1,0:T(8,128)S(1)}, f32[128,128]{1,0:T(8,128)S(1)}, u32[]{:S(2)}, u32[]{:S(2)}) collective-permute-start(f32[128,128]{1,0:T(8,128)S(1)} %add.30), channel_id=1, source_target_pairs={{0,96},{1,33},{2,98},{3,35},{4,100},{5,37},{6,102},{7,39},{8,104},... | collective-permute-start | bytes 196616 | tf_op jit(solution)/shard_map/ppermute | solution.py:371
  66.7 2.2 %collective-permute-done.17 = f32[128,128]{1,0:T(8,128)S(1)} collective-permute-done((f32[128,128]{1,0:T(8,128)S(1)}, f32[128,128]{1,0:T(8,128)S(1)}, u32[]{:S(2)}, u32[]{:S(2)}) %collective-permute-start.17) | collective-permute-done | bytes 65568 | tf_op jit(solution)/shard_map/ppermute | solution.py:371
  68.9 0.0 collective-permute-done.18.colb_ref
  68.9 0.0 collective-permute-done.19.cola_ref
  68.9 2.8 %collective-permute-start.20 = (f32[128,128]{1,0:T(8,128)S(1)}, f32[128,128]{1,0:T(8,128)S(1)}, u32[]{:S(2)}, u32[]{:S(2)}) collective-permute-start(f32[128,128]{1,0:T(8,128)S(1)} %add.31.mine_ref), channel_id=1, source_target_pairs={{0,1},{1,0},{2,3},{3,2},{4,5},{5,4},{6,7},{7,6},{8,9},{9,8},{10,11... | collective-permute-start | bytes 196616 | tf_op jit(solution)/shard_map/ppermute | solution.py:371
  71.7 1.2 %shard_map.94 = f32[2,2,256,256]{3,2,1,0:T(8,128)} custom-call(f32[2,2,256,256]{3,2,1,0:T(8,128)S(1)} %get-tuple-element.50.part_ref, f32[2,6,64,128]{3,2,1,0:T(8,128)S(1)} %collective-permute-done.13.rowa_ref, f32[2,6,64,128]{3,2,1,0:T(8,128)S(1)} %collective-permute-done.14.rowb_ref, f32[2,256,128]{2,1,0:T(8,128)S(1)} %collective-permute-done.18.colb_ref, ...), custom_call_target="tpu_custom_call" | custom-call | tf_op jit(solution)/shard_map/pallas_call | solution.py:375
  72.9 0.0 collective-permute-done.20.other_ref
  72.9 0.7 shard_map.95
  (10 shorter events, 0.2 us)
Async XLA Ops:
  0.6 9.4 %copy-start = (f32[2,2,256,256]{3,2,1,0:T(8,128)S(1)}, f32[2,2,256,256]{3,2,1,0:T(8,128)}, u32[]{:S(2)}) copy-start(f32[2,2,256,256]{3,2,1,0:T(8,128)} %obj_ref.13) | copy-start | bytes 3145732
  1.9 8.1 %collective-permute-start.4 = (f32[256,128]{1,0:T(8,128)S(1)}, f32[256,128]{1,0:T(8,128)S(1)}, u32[]{:S(2)}, u32[]{:S(2)}) collective-permute-start(f32[256,128]{1,0:T(8,128)S(1)} %get-tuple-element.42), channel_id=1, source_target_pairs={{0,16},{1,2},{2,1},{3,4},{4,3},{5,6},{6,5},{7,8},{8,7},{9,10},{10,... | collective-permute-start | bytes 393224 | tf_op jit(solution)/shard_map/ppermute | solution.py:358
  6.3 3.7 %collective-permute-start.5 = (f32[256,128]{1,0:T(8,128)S(1)}, f32[256,128]{1,0:T(8,128)S(1)}, u32[]{:S(2)}, u32[]{:S(2)}) collective-permute-start(f32[256,128]{1,0:T(8,128)S(1)} %get-tuple-element.43), channel_id=1, source_target_pairs={{0,1},{1,0},{2,3},{3,2},{4,5},{5,4},{6,7},{7,6},{8,9},{9,8},{10,11... | collective-permute-start | bytes 393224 | tf_op jit(solution)/shard_map/ppermute | solution.py:358
  7.5 6.0 %collective-permute-start = (f32[256,128]{1,0:T(8,128)S(1)}, f32[256,128]{1,0:T(8,128)S(1)}, u32[]{:S(2)}, u32[]{:S(2)}) collective-permute-start(f32[256,128]{1,0:T(8,128)S(1)} %get-tuple-element.38), channel_id=1, source_target_pairs={{0,16},{1,2},{2,1},{3,4},{4,3},{5,6},{6,5},{7,8},{8,7},{9,10},{10,... | collective-permute-start | bytes 393224 | tf_op jit(solution)/shard_map/ppermute | solution.py:358
  9.0 7.5 %copy-start.1 = (bf16[4,2,256,256]{3,2,1,0:T(8,128)(2,1)S(1)}, bf16[4,2,256,256]{3,2,1,0:T(8,128)(2,1)}, u32[]{:S(2)}) copy-start(bf16[4,2,256,256]{3,2,1,0:T(8,128)(2,1)} %constant.2.clone.tabs_ref) | copy-start | bytes 3145732
  9.0 4.5 %collective-permute-start.1 = (f32[256,128]{1,0:T(8,128)S(1)}, f32[256,128]{1,0:T(8,128)S(1)}, u32[]{:S(2)}, u32[]{:S(2)}) collective-permute-start(f32[256,128]{1,0:T(8,128)S(1)} %get-tuple-element.39), channel_id=1, source_target_pairs={{0,1},{1,0},{2,3},{3,2},{4,5},{5,4},{6,7},{7,6},{8,9},{9,8},{10,11... | collective-permute-start | bytes 393224 | tf_op jit(solution)/shard_map/ppermute | solution.py:358
  10.1 6.4 %collective-permute-start.6 = (f32[6,64,128]{2,1,0:T(8,128)S(1)}, f32[6,64,128]{2,1,0:T(8,128)S(1)}, u32[]{:S(2)}, u32[]{:S(2)}) collective-permute-start(f32[6,64,128]{2,1,0:T(8,128)S(1)} %get-tuple-element.44), channel_id=1, source_target_pairs={{0,16},{1,17},{2,18},{3,19},{4,20},{5,21},{6,22},{7,23},{8,24},{9,... | collective-permute-start | bytes 589832 | tf_op jit(solution)/shard_map/ppermute | solution.py:358
  11.4 5.1 %copy-start.2 = (f32[2,128,128]{2,1,0:T(8,128)S(1)}, f32[2,128,128]{2,1,0:T(8,128)}, u32[]{:S(2)}) copy-start(f32[2,128,128]{2,1,0:T(8,128)} %probe_ref.5) | copy-start | bytes 393220
  11.4 5.1 %collective-permute-start.7 = (f32[6,64,128]{2,1,0:T(8,128)S(1)}, f32[6,64,128]{2,1,0:T(8,128)S(1)}, u32[]{:S(2)}, u32[]{:S(2)}) collective-permute-start(f32[6,64,128]{2,1,0:T(8,128)S(1)} %get-tuple-element.45), channel_id=1, source_target_pairs={{0,1},{1,0},{2,3},{3,2},{4,5},{5,4},{6,7},{7,6},{8,9},{9,8},{10,11... | collective-permute-start | bytes 589832 | tf_op jit(solution)/shard_map/ppermute | solution.py:358
  13.5 7.2 %collective-permute-start.2 = (f32[6,64,128]{2,1,0:T(8,128)S(1)}, f32[6,64,128]{2,1,0:T(8,128)S(1)}, u32[]{:S(2)}, u32[]{:S(2)}) collective-permute-start(f32[6,64,128]{2,1,0:T(8,128)S(1)} %get-tuple-element.40), channel_id=1, source_target_pairs={{0,16},{1,17},{2,18},{3,19},{4,20},{5,21},{6,22},{7,23},{8,24},{9,... | collective-permute-start | bytes 589832 | tf_op jit(solution)/shard_map/ppermute | solution.py:358
  15.3 1.2 %copy-start.4 = (s32[1,8]{1,0:T(1,128)S(1)}, s32[1,8]{1,0:T(1,128)}, u32[]{:S(2)}) copy-start(s32[1,8]{1,0:T(1,128)} %row_ref.5) | copy-start | bytes 100
  15.3 1.3 %copy-start.5 = (s32[1,8]{1,0:T(1,128)S(1)}, s32[1,8]{1,0:T(1,128)}, u32[]{:S(2)}) copy-start(s32[1,8]{1,0:T(1,128)} %col_ref.5) | copy-start | bytes 100
  15.3 5.5 %collective-permute-start.3 = (f32[6,64,128]{2,1,0:T(8,128)S(1)}, f32[6,64,128]{2,1,0:T(8,128)S(1)}, u32[]{:S(2)}, u32[]{:S(2)}) collective-permute-start(f32[6,64,128]{2,1,0:T(8,128)S(1)} %get-tuple-element.41), channel_id=1, source_target_pairs={{0,1},{1,0},{2,3},{3,2},{4,5},{5,4},{6,7},{7,6},{8,9},{9,8},{10,11... | collective-permute-start | bytes 589832 | tf_op jit(solution)/shard_map/ppermute | solution.py:358
  16.2 4.6 %copy-start.3 = (f32[1,8,128,128]{3,2,1,0:T(8,128)S(1)}, f32[1,8,128,128]{3,2,1,0:T(8,128)}, u32[]{:S(2)}) copy-start(f32[1,8,128,128]{3,2,1,0:T(8,128)} %param.9) | copy-start | bytes 1572868
  26.7 1.9 %collective-permute-start.8 = (f32[128,128]{1,0:T(8,128)S(1)}, f32[128,128]{1,0:T(8,128)S(1)}, u32[]{:S(2)}, u32[]{:S(2)}) collective-permute-start(f32[128,128]{1,0:T(8,128)S(1)} %get-tuple-element.52), channel_id=1, source_target_pairs={{0,1},{1,0},{2,3},{3,2},{4,5},{5,4},{6,7},{7,6},{8,9},{9,8},{10,11... | collective-permute-start | bytes 196616 | tf_op jit(solution)/shard_map/ppermute | solution.py:371
  28.6 5.6 %collective-permute-start.9 = (f32[128,128]{1,0:T(8,128)S(1)}, f32[128,128]{1,0:T(8,128)S(1)}, u32[]{:S(2)}, u32[]{:S(2)}) collective-permute-start(f32[128,128]{1,0:T(8,128)S(1)} %add.24), channel_id=1, source_target_pairs={{0,16},{1,17},{2,18},{3,19},{4,20},{5,21},{6,22},{7,23},{8,24},{9,... | collective-permute-start | bytes 196616 | tf_op jit(solution)/shard_map/ppermute | solution.py:371
  34.2 5.4 %collective-permute-start.10 = (f32[128,128]{1,0:T(8,128)S(1)}, f32[128,128]{1,0:T(8,128)S(1)}, u32[]{:S(2)}, u32[]{:S(2)}) collective-permute-start(f32[128,128]{1,0:T(8,128)S(1)} %add.25), channel_id=1, source_target_pairs={{0,4},{1,13},{2,6},{3,15},{4,0},{5,9},{6,2},{7,11},{8,12},{9,5},{1... | collective-permute-start | bytes 196616 | tf_op jit(solution)/shard_map/ppermute | solution.py:371
  37.9 11.9 %collective-permute-start.14 = (f32[2,6,64,128]{3,2,1,0:T(8,128)S(1)}, f32[2,6,64,128]{3,2,1,0:T(8,128)S(1)}, u32[]{:S(2)}, u32[]{:S(2)}) collective-permute-start(f32[2,6,64,128]{3,2,1,0:T(8,128)S(1)} %get-tuple-element.58), channel_id=1, source_target_pairs={{0,1},{1,0},{2,3},{3,2},{4,5},{5,4},{6,7},{7,6},{8,9},{9,8},{10,11... | collective-permute-start | bytes 1179656 | tf_op jit(solution)/shard_map/ppermute | solution.py:358
  39.6 11.4 %collective-permute-start.13 = (f32[2,6,64,128]{3,2,1,0:T(8,128)S(1)}, f32[2,6,64,128]{3,2,1,0:T(8,128)S(1)}, u32[]{:S(2)}, u32[]{:S(2)}) collective-permute-start(f32[2,6,64,128]{3,2,1,0:T(8,128)S(1)} %get-tuple-element.57), channel_id=1, source_target_pairs={{0,16},{1,17},{2,18},{3,19},{4,20},{5,21},{6,22},{7,23},{8,24},{9,... | collective-permute-start | bytes 1179656 | tf_op jit(solution)/shard_map/ppermute | solution.py:358
  41.6 3.4 %collective-permute-start.11 = (f32[128,128]{1,0:T(8,128)S(1)}, f32[128,128]{1,0:T(8,128)S(1)}, u32[]{:S(2)}, u32[]{:S(2)}) collective-permute-start(f32[128,128]{1,0:T(8,128)S(1)} %add.26), channel_id=1, source_target_pairs={{0,12},{1,5},{2,14},{3,7},{4,8},{5,1},{6,10},{7,3},{8,4},{9,13},{1... | collective-permute-start | bytes 196616 | tf_op jit(solution)/shard_map/ppermute | solution.py:371
  45.0 4.7 %collective-permute-start.12 = (f32[128,128]{1,0:T(8,128)S(1)}, f32[128,128]{1,0:T(8,128)S(1)}, u32[]{:S(2)}, u32[]{:S(2)}) collective-permute-start(f32[128,128]{1,0:T(8,128)S(1)} %add.27), channel_id=1, source_target_pairs={{0,128},{1,131},{2,130},{3,129},{4,132},{5,135},{6,134},{7,133},{8... | collective-permute-start | bytes 196616 | tf_op jit(solution)/shard_map/ppermute | solution.py:371
  51.0 5.5 %collective-permute-start.15 = (f32[128,128]{1,0:T(8,128)S(1)}, f32[128,128]{1,0:T(8,128)S(1)}, u32[]{:S(2)}, u32[]{:S(2)}) collective-permute-start(f32[128,128]{1,0:T(8,128)S(1)} %add.28), channel_id=1, source_target_pairs={{0,130},{1,129},{2,128},{3,131},{4,134},{5,133},{6,132},{7,135},{8... | collective-permute-start | bytes 196616 | tf_op jit(solution)/shard_map/ppermute | solution.py:371
  56.6 5.7 %collective-permute-start.16 = (f32[128,128]{1,0:T(8,128)S(1)}, f32[128,128]{1,0:T(8,128)S(1)}, u32[]{:S(2)}, u32[]{:S(2)}) collective-permute-start(f32[128,128]{1,0:T(8,128)S(1)} %add.29), channel_id=1, source_target_pairs={{0,32},{1,97},{2,34},{3,99},{4,36},{5,101},{6,38},{7,103},{8,40},{... | collective-permute-start | bytes 196616 | tf_op jit(solution)/shard_map/ppermute | solution.py:371
  59.5 9.4 %collective-permute-start.18 = (f32[2,256,128]{2,1,0:T(8,128)S(1)}, f32[2,256,128]{2,1,0:T(8,128)S(1)}, u32[]{:S(2)}, u32[]{:S(2)}) collective-permute-start(f32[2,256,128]{2,1,0:T(8,128)S(1)} %get-tuple-element.69), channel_id=1, source_target_pairs={{0,16},{1,2},{2,1},{3,4},{4,3},{5,6},{6,5},{7,8},{8,7},{9,10},{10,... | collective-permute-start | bytes 786440 | tf_op jit(solution)/shard_map/ppermute | solution.py:358
  62.3 6.6 %collective-permute-start.19 = (f32[2,256,128]{2,1,0:T(8,128)S(1)}, f32[2,256,128]{2,1,0:T(8,128)S(1)}, u32[]{:S(2)}, u32[]{:S(2)}) collective-permute-start(f32[2,256,128]{2,1,0:T(8,128)S(1)} %get-tuple-element.70), channel_id=1, source_target_pairs={{0,1},{1,0},{2,3},{3,2},{4,5},{5,4},{6,7},{7,6},{8,9},{9,8},{10,11... | collective-permute-start | bytes 786440 | tf_op jit(solution)/shard_map/ppermute | solution.py:358
  64.8 4.0 %collective-permute-start.17 = (f32[128,128]{1,0:T(8,128)S(1)}, f32[128,128]{1,0:T(8,128)S(1)}, u32[]{:S(2)}, u32[]{:S(2)}) collective-permute-start(f32[128,128]{1,0:T(8,128)S(1)} %add.30), channel_id=1, source_target_pairs={{0,96},{1,33},{2,98},{3,35},{4,100},{5,37},{6,102},{7,39},{8,104},... | collective-permute-start | bytes 196616 | tf_op jit(solution)/shard_map/ppermute | solution.py:371
  68.9 4.0 %collective-permute-start.20 = (f32[128,128]{1,0:T(8,128)S(1)}, f32[128,128]{1,0:T(8,128)S(1)}, u32[]{:S(2)}, u32[]{:S(2)}) collective-permute-start(f32[128,128]{1,0:T(8,128)S(1)} %add.31.mine_ref), channel_id=1, source_target_pairs={{0,1},{1,0},{2,3},{3,2},{4,5},{5,4},{6,7},{7,6},{8,9},{9,8},{10,11... | collective-permute-start | bytes 196616 | tf_op jit(solution)/shard_map/ppermute | solution.py:371

commit v17 on v16

--- a/solution.py
+++ b/solution.py
@@ -184,7 +184,7 @@
 
 
 def second_kernel(
-    row_ref, col_ref, live_ref, obj_ref, colb_ref, cola_ref, rowa_ref, rowb_ref,
+    row_ref, col_ref, live_ref, obj_ref, colb_ref, cola_ref, rowb_ref, rowa_ref,
     win_ref, mid_ref, measured_ref, tabs_ref,
     grad_ref, down_ref, keep_ref, send_ref,
     ext, sum_ref, *, group,
@@ -405,13 +405,14 @@
             (), (object_field, *cols[piece]),
         )
         halos.append((*cols[piece], *meet_rows(strips)))
+    *sides, even, odd = halos[1]
     win, mid = call(
         functools.partial(first_kernel, group=2), [fields] * 2, (offset_row, offset_col),
         (object_field, *halos[0], probe, tabs), (grown,),
     )
     grad, down, mine, send = call(
         functools.partial(second_kernel, group=count), [fields] * 2 + [array(*plane)] * 2, (offset_row, offset_col, live),
-        (object_field, *halos[1], win, mid, intensity[0], tabs),
+        (object_field, *sides, odd, even, win, mid, intensity[0], tabs),
         (grown, pltpu.VMEM((2, *plane), jnp.float32)),
     )
     part, *strips, left, right = call(

time: 74 us -> 73.9 us (level)
  waiting for transfers between devices: 16.9 us -> 18.1 us
  starting transfers between devices: 40.2 us -> 39.2 us
    ppermute x9, starting transfers between devices: 22.5 us -> 18.4 us  [swap(): lax.ppermute(value, BOTH, [(i, i ^ masks[i % 2]) for i in range(count)])]
    ppermute x12, starting transfers between devices: 17.7 us -> 20.8 us  [meet(): return lax.ppermute(strip, BOTH, pairs)]
  transfers between devices with their start and end apart: 21 -> 21, of which waited for: 10 -> 9; matrix products, arithmetic and copies ran while one was open for 0% -> 0% of each run, Pallas kernels for 10% -> 10%
where the time goes in v17:
time: 73.9 us; the launch traced here: 73.7 us
  starting transfers between devices  39.2 us (53%)
  waiting for transfers between devices  18.1 us (24%)
  Pallas kernels  14.9 us (20%)
  between operations  1.52 us (2%)
    ppermute x12, starting transfers between devices, meet(): return lax.ppermute(strip, BOTH, pairs)  20.8 us
    ppermute x9, starting transfers between devices, swap(): lax.ppermute(value, BOTH, [(i, i ^ masks[i % 2]) for i in range(count)])  18.4 us
    pallas_call x8, Pallas kernels, call(): pl.pallas_call(kernel, out_shape=tuple(out_shape), in_specs=smem(len(scal...  12.4 us
    ppermute x9, waiting for transfers between devices, swap(): lax.ppermute(value, BOTH, [(i, i ^ masks[i % 2]) for i in range(count)])  12.1 us
    ppermute x12, waiting for transfers between devices, meet(): return lax.ppermute(strip, BOTH, pairs)  6.01 us
    pallas_call x2, Pallas kernels, on_device(): pl.pallas_call(functools.partial(pack_kernel, piece=piece), out_shape=tup...  2.46 us
  transfers between devices with their start and end apart: 21, of which 9 were waited for; matrix products, arithmetic and copies ran while one was open for 0% of the time, Pallas kernels for 10%

profile of v17, /device:TPU:1, one launch (start us, length us, event | category | flops | bytes accessed | tf_op | source)
XLA Modules:
  0.0 73.7 jit_solution(18305747228994090913)
XLA Ops:
  0.6 0.0 copy-start
  0.6 1.3 %shard_map.88 = (f32[256,128]{1,0:T(8,128)S(1)}, f32[256,128]{1,0:T(8,128)S(1)}) custom-call(f32[2,2,256,256]{3,2,1,0:T(8,128)} %obj_ref.13), custom_call_target="tpu_custom_call" | custom-call | tf_op jit(solution)/shard_map/pallas_call | solution.py:392
  1.9 4.4 %collective-permute-start.4 = (f32[256,128]{1,0:T(8,128)S(1)}, f32[256,128]{1,0:T(8,128)S(1)}, u32[]{:S(2)}, u32[]{:S(2)}) collective-permute-start(f32[256,128]{1,0:T(8,128)S(1)} %get-tuple-element.42), channel_id=1, source_target_pairs={{0,16},{1,2},{2,1},{3,4},{4,3},{5,6},{6,5},{7,8},{8,7},{9,10},{10,... | collective-permute-start | bytes 393224 | tf_op jit(solution)/shard_map/ppermute | solution.py:358
  6.3 0.0 collective-permute-start.5
  6.3 1.2 %shard_map.86 = (f32[256,128]{1,0:T(8,128)S(1)}, f32[256,128]{1,0:T(8,128)S(1)}) custom-call(f32[2,2,256,256]{3,2,1,0:T(8,128)} %obj_ref.13), custom_call_target="tpu_custom_call" | custom-call | tf_op jit(solution)/shard_map/pallas_call | solution.py:392
  7.5 1.5 %collective-permute-start = (f32[256,128]{1,0:T(8,128)S(1)}, f32[256,128]{1,0:T(8,128)S(1)}, u32[]{:S(2)}, u32[]{:S(2)}) collective-permute-start(f32[256,128]{1,0:T(8,128)S(1)} %get-tuple-element.38), channel_id=1, source_target_pairs={{0,16},{1,2},{2,1},{3,4},{4,3},{5,6},{6,5},{7,8},{8,7},{9,10},{10,... | collective-permute-start | bytes 393224 | tf_op jit(solution)/shard_map/ppermute | solution.py:358
  9.0 0.0 copy-start.1
  9.0 1.0 %collective-permute-start.1 = (f32[256,128]{1,0:T(8,128)S(1)}, f32[256,128]{1,0:T(8,128)S(1)}, u32[]{:S(2)}, u32[]{:S(2)}) collective-permute-start(f32[256,128]{1,0:T(8,128)S(1)} %get-tuple-element.39), channel_id=1, source_target_pairs={{0,1},{1,0},{2,3},{3,2},{4,5},{5,4},{6,7},{7,6},{8,9},{9,8},{10,11... | collective-permute-start | bytes 393224 | tf_op jit(solution)/shard_map/ppermute | solution.py:358
  10.0 0.0 collective-permute-done.4.colb_ref
  10.0 0.0 collective-permute-done.5.cola_ref
  10.0 0.0 copy-done
  10.1 1.3 %collective-permute-start.6 = (f32[6,64,128]{2,1,0:T(8,128)S(1)}, f32[6,64,128]{2,1,0:T(8,128)S(1)}, u32[]{:S(2)}, u32[]{:S(2)}) collective-permute-start(f32[6,64,128]{2,1,0:T(8,128)S(1)} %get-tuple-element.44), channel_id=1, source_target_pairs={{0,16},{1,17},{2,18},{3,19},{4,20},{5,21},{6,22},{7,23},{8,24},{9,... | collective-permute-start | bytes 589832 | tf_op jit(solution)/shard_map/ppermute | solution.py:358
  11.4 0.0 copy-start.2
  11.4 0.1 collective-permute-start.7
  11.6 1.9 %collective-permute-done.colb_ref = f32[256,128]{1,0:T(8,128)S(1)} collective-permute-done((f32[256,128]{1,0:T(8,128)S(1)}, f32[256,128]{1,0:T(8,128)S(1)}, u32[]{:S(2)}, u32[]{:S(2)}) %collective-permute-start) | collective-permute-done | bytes 131104 | tf_op jit(solution)/shard_map/ppermute | solution.py:358
  13.5 0.0 collective-permute-done.1.cola_ref
  13.5 0.1 collective-permute-start.2
  13.6 0.0 copy-start.4
  13.7 0.0 copy-start.5
  13.7 3.2 %collective-permute-start.3 = (f32[6,64,128]{2,1,0:T(8,128)S(1)}, f32[6,64,128]{2,1,0:T(8,128)S(1)}, u32[]{:S(2)}, u32[]{:S(2)}) collective-permute-start(f32[6,64,128]{2,1,0:T(8,128)S(1)} %get-tuple-element.41), channel_id=1, source_target_pairs={{0,16},{1,17},{2,18},{3,19},{4,20},{5,21},{6,22},{7,23},{8,24},{9,... | collective-permute-start | bytes 589832 | tf_op jit(solution)/shard_map/ppermute | solution.py:358
  17.6 0.0 copy-start.3
  17.6 0.0 collective-permute-done.6.rowa_ref
  17.6 0.0 collective-permute-done.7.rowb_ref
  17.6 0.0 copy-done.1
  17.6 0.0 copy-done.2
  17.6 0.0 copy-done.4
  17.6 0.0 copy-done.5
  17.6 2.2 %shard_map.90 = (f32[8,2,128,128]{3,2,1,0:T(8,128)S(1)}, f32[8,2,128,128]{3,2,1,0:T(8,128)S(1)}) custom-call(s32[1,8]{1,0:T(1,128)S(1)} %copy-done.4, s32[1,8]{1,0:T(1,128)S(1)} %copy-done.5, f32[2,2,256,256]{3,2,1,0:T(8,128)S(1)} %copy-done, f32[256,128]{1,0:T(8,128)S(1)} %collective-permute-done.4.colb_ref, ...), custom_call_target="tpu_custom_call" | custom-call | tf_op jit(solution)/shard_map/pallas_call | solution.py:375
  19.9 0.0 collective-permute-done.2.rowb_ref
  19.9 2.5 %collective-permute-done.3.rowa_ref = f32[6,64,128]{2,1,0:T(8,128)S(1)} collective-permute-done((f32[6,64,128]{2,1,0:T(8,128)S(1)}, f32[6,64,128]{2,1,0:T(8,128)S(1)}, u32[]{:S(2)}, u32[]{:S(2)}) %collective-permute-start.3) | collective-permute-done | bytes 196640 | tf_op jit(solution)/shard_map/ppermute | solution.py:358
  22.3 0.0 copy-done.3
  22.3 5.8 %shard_map.91 = (f32[8,2,128,128]{3,2,1,0:T(8,128)S(1)}, f32[8,2,128,128]{3,2,1,0:T(8,128)S(1)}, f32[128,128]{1,0:T(8,128)S(1)}, f32[128,128]{1,0:T(8,128)S(1)}) custom-call(s32[1,8]{1,0:T(1,128)S(1)} %copy-done.4, s32[1,8]{1,0:T(1,128)S(1)} %copy-done.5, s32[1,1]{1,0:T(1,128)S(6)} %copy.9.live_ref, f32[2,2,256,256]{3,2,1,0:T(8,128)S(1)} %copy-done, ...), custom_call_target="tpu_custom_call" | custom-call | tf_op jit(solution)/shard_map/pallas_call | solution.py:375
  28.2 0.5 collective-permute-start.8
  28.7 0.9 %collective-permute-done.8 = f32[128,128]{1,0:T(8,128)S(1)} collective-permute-done((f32[128,128]{1,0:T(8,128)S(1)}, f32[128,128]{1,0:T(8,128)S(1)}, u32[]{:S(2)}, u32[]{:S(2)}) %collective-permute-start.8) | collective-permute-done | bytes 65568 | tf_op jit(solution)/shard_map/ppermute | solution.py:371
  29.6 2.2 %collective-permute-start.9 = (f32[128,128]{1,0:T(8,128)S(1)}, f32[128,128]{1,0:T(8,128)S(1)}, u32[]{:S(2)}, u32[]{:S(2)}) collective-permute-start(f32[128,128]{1,0:T(8,128)S(1)} %add.24), channel_id=1, source_target_pairs={{0,16},{1,17},{2,18},{3,19},{4,20},{5,21},{6,22},{7,23},{8,24},{9,... | collective-permute-start | bytes 196616 | tf_op jit(solution)/shard_map/ppermute | solution.py:371
  31.9 2.3 %shard_map.92 = (f32[2,2,256,256]{3,2,1,0:T(8,128)S(1)}, f32[2,6,64,128]{3,2,1,0:T(8,128)S(1)}, f32[2,6,64,128]{3,2,1,0:T(8,128)S(1)}, f32[2,256,128]{2,1,0:T(8,128)S(1)}, f32[2,256,128]{2,1,0:T(8,128)S(1)}) custom-call(s32[1,8]{1,0:T(1,128)S(1)} %copy-done.4, s32[1,8]{1,0:T(1,128)S(1)} %copy-done.5, f32[2,2,256,256]{3,2,1,0:T(8,128)S(1)} %copy-done, ...), custom_call_target="tpu_custom_call" | custom-call | tf_op jit(solution)/shard_map/pallas_call | solution.py:375
  34.2 0.0 collective-permute-done.9
  34.2 3.5 %collective-permute-start.10 = (f32[128,128]{1,0:T(8,128)S(1)}, f32[128,128]{1,0:T(8,128)S(1)}, u32[]{:S(2)}, u32[]{:S(2)}) collective-permute-start(f32[128,128]{1,0:T(8,128)S(1)} %add.25), channel_id=1, source_target_pairs={{0,4},{1,13},{2,6},{3,15},{4,0},{5,9},{6,2},{7,11},{8,12},{9,5},{1... | collective-permute-start | bytes 196616 | tf_op jit(solution)/shard_map/ppermute | solution.py:371
  37.7 0.0 collective-permute-start.14
  37.8 1.7 %collective-permute-done.10 = f32[128,128]{1,0:T(8,128)S(1)} collective-permute-done((f32[128,128]{1,0:T(8,128)S(1)}, f32[128,128]{1,0:T(8,128)S(1)}, u32[]{:S(2)}, u32[]{:S(2)}) %collective-permute-start.10) | collective-permute-done | bytes 65568 | tf_op jit(solution)/shard_map/ppermute | solution.py:371
  39.4 2.9 %collective-permute-start.13 = (f32[2,6,64,128]{3,2,1,0:T(8,128)S(1)}, f32[2,6,64,128]{3,2,1,0:T(8,128)S(1)}, u32[]{:S(2)}, u32[]{:S(2)}) collective-permute-start(f32[2,6,64,128]{3,2,1,0:T(8,128)S(1)} %get-tuple-element.57), channel_id=1, source_target_pairs={{0,16},{1,17},{2,18},{3,19},{4,20},{5,21},{6,22},{7,23},{8,24},{9,... | collective-permute-start | bytes 1179656 | tf_op jit(solution)/shard_map/ppermute | solution.py:358
  42.3 0.0 collective-permute-start.11
  42.3 3.4 %collective-permute-done.11 = f32[128,128]{1,0:T(8,128)S(1)} collective-permute-done((f32[128,128]{1,0:T(8,128)S(1)}, f32[128,128]{1,0:T(8,128)S(1)}, u32[]{:S(2)}, u32[]{:S(2)}) %collective-permute-start.11) | collective-permute-done | bytes 65568 | tf_op jit(solution)/shard_map/ppermute | solution.py:371
  45.8 2.4 %collective-permute-start.12 = (f32[128,128]{1,0:T(8,128)S(1)}, f32[128,128]{1,0:T(8,128)S(1)}, u32[]{:S(2)}, u32[]{:S(2)}) collective-permute-start(f32[128,128]{1,0:T(8,128)S(1)} %add.27), channel_id=1, source_target_pairs={{0,128},{1,131},{2,130},{3,129},{4,132},{5,135},{6,134},{7,133},{8... | collective-permute-start | bytes 196616 | tf_op jit(solution)/shard_map/ppermute | solution.py:371
  48.1 2.1 %collective-permute-done.12 = f32[128,128]{1,0:T(8,128)S(1)} collective-permute-done((f32[128,128]{1,0:T(8,128)S(1)}, f32[128,128]{1,0:T(8,128)S(1)}, u32[]{:S(2)}, u32[]{:S(2)}) %collective-permute-start.12) | collective-permute-done | bytes 65568 | tf_op jit(solution)/shard_map/ppermute | solution.py:371
  50.2 0.0 collective-permute-done.14.rowb_ref
  50.2 1.6 %collective-permute-done.13.rowa_ref = f32[2,6,64,128]{3,2,1,0:T(8,128)S(1)} collective-permute-done((f32[2,6,64,128]{3,2,1,0:T(8,128)S(1)}, f32[2,6,64,128]{3,2,1,0:T(8,128)S(1)}, u32[]{:S(2)}, u32[]{:S(2)}) %collective-permute-start.13) | collective-permute-done | bytes 393248 | tf_op jit(solution)/shard_map/ppermute | solution.py:358
  51.8 2.6 %collective-permute-start.15 = (f32[128,128]{1,0:T(8,128)S(1)}, f32[128,128]{1,0:T(8,128)S(1)}, u32[]{:S(2)}, u32[]{:S(2)}) collective-permute-start(f32[128,128]{1,0:T(8,128)S(1)} %add.28), channel_id=1, source_target_pairs={{0,130},{1,129},{2,128},{3,131},{4,134},{5,133},{6,132},{7,135},{8... | collective-permute-start | bytes 196616 | tf_op jit(solution)/shard_map/ppermute | solution.py:371
  54.4 0.1 shard_map.93
  54.5 1.6 %collective-permute-done.15 = f32[128,128]{1,0:T(8,128)S(1)} collective-permute-done((f32[128,128]{1,0:T(8,128)S(1)}, f32[128,128]{1,0:T(8,128)S(1)}, u32[]{:S(2)}, u32[]{:S(2)}) %collective-permute-start.15) | collective-permute-done | bytes 65568 | tf_op jit(solution)/shard_map/ppermute | solution.py:371
  56.1 2.9 %collective-permute-start.16 = (f32[128,128]{1,0:T(8,128)S(1)}, f32[128,128]{1,0:T(8,128)S(1)}, u32[]{:S(2)}, u32[]{:S(2)}) collective-permute-start(f32[128,128]{1,0:T(8,128)S(1)} %add.29), channel_id=1, source_target_pairs={{0,32},{1,97},{2,34},{3,99},{4,36},{5,101},{6,38},{7,103},{8,40},{... | collective-permute-start | bytes 196616 | tf_op jit(solution)/shard_map/ppermute | solution.py:371
  59.0 3.2 %collective-permute-start.18 = (f32[2,256,128]{2,1,0:T(8,128)S(1)}, f32[2,256,128]{2,1,0:T(8,128)S(1)}, u32[]{:S(2)}, u32[]{:S(2)}) collective-permute-start(f32[2,256,128]{2,1,0:T(8,128)S(1)} %get-tuple-element.69), channel_id=1, source_target_pairs={{0,16},{1,2},{2,1},{3,4},{4,3},{5,6},{6,5},{7,8},{8,7},{9,10},{10,... | collective-permute-start | bytes 786440 | tf_op jit(solution)/shard_map/ppermute | solution.py:358
  62.2 0.0 collective-permute-done.16
  62.3 2.9 %collective-permute-start.19 = (f32[2,256,128]{2,1,0:T(8,128)S(1)}, f32[2,256,128]{2,1,0:T(8,128)S(1)}, u32[]{:S(2)}, u32[]{:S(2)}) collective-permute-start(f32[2,256,128]{2,1,0:T(8,128)S(1)} %get-tuple-element.70), channel_id=1, source_target_pairs={{0,1},{1,0},{2,3},{3,2},{4,5},{5,4},{6,7},{7,6},{8,9},{9,8},{10,11... | collective-permute-start | bytes 786440 | tf_op jit(solution)/shard_map/ppermute | solution.py:358
  65.2 1.6 %collective-permute-start.17 = (f32[128,128]{1,0:T(8,128)S(1)}, f32[128,128]{1,0:T(8,128)S(1)}, u32[]{:S(2)}, u32[]{:S(2)}) collective-permute-start(f32[128,128]{1,0:T(8,128)S(1)} %add.30), channel_id=1, source_target_pairs={{0,96},{1,33},{2,98},{3,35},{4,100},{5,37},{6,102},{7,39},{8,104},... | collective-permute-start | bytes 196616 | tf_op jit(solution)/shard_map/ppermute | solution.py:371
  66.7 2.4 %collective-permute-done.17 = f32[128,128]{1,0:T(8,128)S(1)} collective-permute-done((f32[128,128]{1,0:T(8,128)S(1)}, f32[128,128]{1,0:T(8,128)S(1)}, u32[]{:S(2)}, u32[]{:S(2)}) %collective-permute-start.17) | collective-permute-done | bytes 65568 | tf_op jit(solution)/shard_map/ppermute | solution.py:371
  69.2 0.0 collective-permute-done.18.colb_ref
  69.2 0.0 collective-permute-done.19.cola_ref
  69.2 2.6 %collective-permute-start.20 = (f32[128,128]{1,0:T(8,128)S(1)}, f32[128,128]{1,0:T(8,128)S(1)}, u32[]{:S(2)}, u32[]{:S(2)}) collective-permute-start(f32[128,128]{1,0:T(8,128)S(1)} %add.31.mine_ref), channel_id=1, source_target_pairs={{0,1},{1,0},{2,3},{3,2},{4,5},{5,4},{6,7},{7,6},{8,9},{9,8},{10,11... | collective-permute-start | bytes 196616 | tf_op jit(solution)/shard_map/ppermute | solution.py:371
  71.8 1.2 %shard_map.94 = f32[2,2,256,256]{3,2,1,0:T(8,128)} custom-call(f32[2,2,256,256]{3,2,1,0:T(8,128)S(1)} %get-tuple-element.50.part_ref, f32[2,6,64,128]{3,2,1,0:T(8,128)S(1)} %collective-permute-done.13.rowa_ref, f32[2,6,64,128]{3,2,1,0:T(8,128)S(1)} %collective-permute-done.14.rowb_ref, f32[2,256,128]{2,1,0:T(8,128)S(1)} %collective-permute-done.18.colb_ref, ...), custom_call_target="tpu_custom_call" | custom-call | tf_op jit(solution)/shard_map/pallas_call | solution.py:375
  73.0 0.0 collective-permute-done.20.other_ref
  73.0 0.7 shard_map.95
  (10 shorter events, 0.2 us)
Async XLA Ops:
  0.6 9.4 %copy-start = (f32[2,2,256,256]{3,2,1,0:T(8,128)S(1)}, f32[2,2,256,256]{3,2,1,0:T(8,128)}, u32[]{:S(2)}) copy-start(f32[2,2,256,256]{3,2,1,0:T(8,128)} %obj_ref.13) | copy-start | bytes 3145732
  1.9 8.1 %collective-permute-start.4 = (f32[256,128]{1,0:T(8,128)S(1)}, f32[256,128]{1,0:T(8,128)S(1)}, u32[]{:S(2)}, u32[]{:S(2)}) collective-permute-start(f32[256,128]{1,0:T(8,128)S(1)} %get-tuple-element.42), channel_id=1, source_target_pairs={{0,16},{1,2},{2,1},{3,4},{4,3},{5,6},{6,5},{7,8},{8,7},{9,10},{10,... | collective-permute-start | bytes 393224 | tf_op jit(solution)/shard_map/ppermute | solution.py:358
  6.3 3.7 %collective-permute-start.5 = (f32[256,128]{1,0:T(8,128)S(1)}, f32[256,128]{1,0:T(8,128)S(1)}, u32[]{:S(2)}, u32[]{:S(2)}) collective-permute-start(f32[256,128]{1,0:T(8,128)S(1)} %get-tuple-element.43), channel_id=1, source_target_pairs={{0,1},{1,0},{2,3},{3,2},{4,5},{5,4},{6,7},{7,6},{8,9},{9,8},{10,11... | collective-permute-start | bytes 393224 | tf_op jit(solution)/shard_map/ppermute | solution.py:358
  7.5 6.0 %collective-permute-start = (f32[256,128]{1,0:T(8,128)S(1)}, f32[256,128]{1,0:T(8,128)S(1)}, u32[]{:S(2)}, u32[]{:S(2)}) collective-permute-start(f32[256,128]{1,0:T(8,128)S(1)} %get-tuple-element.38), channel_id=1, source_target_pairs={{0,16},{1,2},{2,1},{3,4},{4,3},{5,6},{6,5},{7,8},{8,7},{9,10},{10,... | collective-permute-start | bytes 393224 | tf_op jit(solution)/shard_map/ppermute | solution.py:358
  9.0 8.6 %copy-start.1 = (bf16[4,2,256,256]{3,2,1,0:T(8,128)(2,1)S(1)}, bf16[4,2,256,256]{3,2,1,0:T(8,128)(2,1)}, u32[]{:S(2)}) copy-start(bf16[4,2,256,256]{3,2,1,0:T(8,128)(2,1)} %constant.2.clone.tabs_ref) | copy-start | bytes 3145732
  9.0 4.5 %collective-permute-start.1 = (f32[256,128]{1,0:T(8,128)S(1)}, f32[256,128]{1,0:T(8,128)S(1)}, u32[]{:S(2)}, u32[]{:S(2)}) collective-permute-start(f32[256,128]{1,0:T(8,128)S(1)} %get-tuple-element.39), channel_id=1, source_target_pairs={{0,1},{1,0},{2,3},{3,2},{4,5},{5,4},{6,7},{7,6},{8,9},{9,8},{10,11... | collective-permute-start | bytes 393224 | tf_op jit(solution)/shard_map/ppermute | solution.py:358
  10.1 7.5 %collective-permute-start.6 = (f32[6,64,128]{2,1,0:T(8,128)S(1)}, f32[6,64,128]{2,1,0:T(8,128)S(1)}, u32[]{:S(2)}, u32[]{:S(2)}) collective-permute-start(f32[6,64,128]{2,1,0:T(8,128)S(1)} %get-tuple-element.44), channel_id=1, source_target_pairs={{0,16},{1,17},{2,18},{3,19},{4,20},{5,21},{6,22},{7,23},{8,24},{9,... | collective-permute-start | bytes 589832 | tf_op jit(solution)/shard_map/ppermute | solution.py:358
  11.4 6.2 %copy-start.2 = (f32[2,128,128]{2,1,0:T(8,128)S(1)}, f32[2,128,128]{2,1,0:T(8,128)}, u32[]{:S(2)}) copy-start(f32[2,128,128]{2,1,0:T(8,128)} %probe_ref.5) | copy-start | bytes 393220
  11.4 6.2 %collective-permute-start.7 = (f32[6,64,128]{2,1,0:T(8,128)S(1)}, f32[6,64,128]{2,1,0:T(8,128)S(1)}, u32[]{:S(2)}, u32[]{:S(2)}) collective-permute-start(f32[6,64,128]{2,1,0:T(8,128)S(1)} %get-tuple-element.45), channel_id=1, source_target_pairs={{0,1},{1,0},{2,3},{3,2},{4,5},{5,4},{6,7},{7,6},{8,9},{9,8},{10,11... | collective-permute-start | bytes 589832 | tf_op jit(solution)/shard_map/ppermute | solution.py:358
  13.5 6.3 %collective-permute-start.2 = (f32[6,64,128]{2,1,0:T(8,128)S(1)}, f32[6,64,128]{2,1,0:T(8,128)S(1)}, u32[]{:S(2)}, u32[]{:S(2)}) collective-permute-start(f32[6,64,128]{2,1,0:T(8,128)S(1)} %get-tuple-element.40), channel_id=1, source_target_pairs={{0,1},{1,0},{2,3},{3,2},{4,5},{5,4},{6,7},{7,6},{8,9},{9,8},{10,11... | collective-permute-start | bytes 589832 | tf_op jit(solution)/shard_map/ppermute | solution.py:358
  13.6 4.0 %copy-start.4 = (s32[1,8]{1,0:T(1,128)S(1)}, s32[1,8]{1,0:T(1,128)}, u32[]{:S(2)}) copy-start(s32[1,8]{1,0:T(1,128)} %row_ref.5) | copy-start | bytes 100
  13.7 4.0 %copy-start.5 = (s32[1,8]{1,0:T(1,128)S(1)}, s32[1,8]{1,0:T(1,128)}, u32[]{:S(2)}) copy-start(s32[1,8]{1,0:T(1,128)} %col_ref.5) | copy-start | bytes 100
  13.7 8.7 %collective-permute-start.3 = (f32[6,64,128]{2,1,0:T(8,128)S(1)}, f32[6,64,128]{2,1,0:T(8,128)S(1)}, u32[]{:S(2)}, u32[]{:S(2)}) collective-permute-start(f32[6,64,128]{2,1,0:T(8,128)S(1)} %get-tuple-element.41), channel_id=1, source_target_pairs={{0,16},{1,17},{2,18},{3,19},{4,20},{5,21},{6,22},{7,23},{8,24},{9,... | collective-permute-start | bytes 589832 | tf_op jit(solution)/shard_map/ppermute | solution.py:358
  17.6 4.8 %copy-start.3 = (f32[1,8,128,128]{3,2,1,0:T(8,128)S(1)}, f32[1,8,128,128]{3,2,1,0:T(8,128)}, u32[]{:S(2)}) copy-start(f32[1,8,128,128]{3,2,1,0:T(8,128)} %param.9) | copy-start | bytes 1572868
  28.2 1.4 %collective-permute-start.8 = (f32[128,128]{1,0:T(8,128)S(1)}, f32[128,128]{1,0:T(8,128)S(1)}, u32[]{:S(2)}, u32[]{:S(2)}) collective-permute-start(f32[128,128]{1,0:T(8,128)S(1)} %get-tuple-element.52), channel_id=1, source_target_pairs={{0,1},{1,0},{2,3},{3,2},{4,5},{5,4},{6,7},{7,6},{8,9},{9,8},{10,11... | collective-permute-start | bytes 196616 | tf_op jit(solution)/shard_map/ppermute | solution.py:371
  29.6 4.6 %collective-permute-start.9 = (f32[128,128]{1,0:T(8,128)S(1)}, f32[128,128]{1,0:T(8,128)S(1)}, u32[]{:S(2)}, u32[]{:S(2)}) collective-permute-start(f32[128,128]{1,0:T(8,128)S(1)} %add.24), channel_id=1, source_target_pairs={{0,16},{1,17},{2,18},{3,19},{4,20},{5,21},{6,22},{7,23},{8,24},{9,... | collective-permute-start | bytes 196616 | tf_op jit(solution)/shard_map/ppermute | solution.py:371
  34.2 5.2 %collective-permute-start.10 = (f32[128,128]{1,0:T(8,128)S(1)}, f32[128,128]{1,0:T(8,128)S(1)}, u32[]{:S(2)}, u32[]{:S(2)}) collective-permute-start(f32[128,128]{1,0:T(8,128)S(1)} %add.25), channel_id=1, source_target_pairs={{0,4},{1,13},{2,6},{3,15},{4,0},{5,9},{6,2},{7,11},{8,12},{9,5},{1... | collective-permute-start | bytes 196616 | tf_op jit(solution)/shard_map/ppermute | solution.py:371
  37.7 12.4 %collective-permute-start.14 = (f32[2,6,64,128]{3,2,1,0:T(8,128)S(1)}, f32[2,6,64,128]{3,2,1,0:T(8,128)S(1)}, u32[]{:S(2)}, u32[]{:S(2)}) collective-permute-start(f32[2,6,64,128]{3,2,1,0:T(8,128)S(1)} %get-tuple-element.58), channel_id=1, source_target_pairs={{0,1},{1,0},{2,3},{3,2},{4,5},{5,4},{6,7},{7,6},{8,9},{9,8},{10,11... | collective-permute-start | bytes 1179656 | tf_op jit(solution)/shard_map/ppermute | solution.py:358
  39.4 12.4 %collective-permute-start.13 = (f32[2,6,64,128]{3,2,1,0:T(8,128)S(1)}, f32[2,6,64,128]{3,2,1,0:T(8,128)S(1)}, u32[]{:S(2)}, u32[]{:S(2)}) collective-permute-start(f32[2,6,64,128]{3,2,1,0:T(8,128)S(1)} %get-tuple-element.57), channel_id=1, source_target_pairs={{0,16},{1,17},{2,18},{3,19},{4,20},{5,21},{6,22},{7,23},{8,24},{9,... | collective-permute-start | bytes 1179656 | tf_op jit(solution)/shard_map/ppermute | solution.py:358
  42.3 3.4 %collective-permute-start.11 = (f32[128,128]{1,0:T(8,128)S(1)}, f32[128,128]{1,0:T(8,128)S(1)}, u32[]{:S(2)}, u32[]{:S(2)}) collective-permute-start(f32[128,128]{1,0:T(8,128)S(1)} %add.26), channel_id=1, source_target_pairs={{0,12},{1,5},{2,14},{3,7},{4,8},{5,1},{6,10},{7,3},{8,4},{9,13},{1... | collective-permute-start | bytes 196616 | tf_op jit(solution)/shard_map/ppermute | solution.py:371
  45.8 4.4 %collective-permute-start.12 = (f32[128,128]{1,0:T(8,128)S(1)}, f32[128,128]{1,0:T(8,128)S(1)}, u32[]{:S(2)}, u32[]{:S(2)}) collective-permute-start(f32[128,128]{1,0:T(8,128)S(1)} %add.27), channel_id=1, source_target_pairs={{0,128},{1,131},{2,130},{3,129},{4,132},{5,135},{6,134},{7,133},{8... | collective-permute-start | bytes 196616 | tf_op jit(solution)/shard_map/ppermute | solution.py:371
  51.8 4.3 %collective-permute-start.15 = (f32[128,128]{1,0:T(8,128)S(1)}, f32[128,128]{1,0:T(8,128)S(1)}, u32[]{:S(2)}, u32[]{:S(2)}) collective-permute-start(f32[128,128]{1,0:T(8,128)S(1)} %add.28), channel_id=1, source_target_pairs={{0,130},{1,129},{2,128},{3,131},{4,134},{5,133},{6,132},{7,135},{8... | collective-permute-start | bytes 196616 | tf_op jit(solution)/shard_map/ppermute | solution.py:371
  56.1 6.2 %collective-permute-start.16 = (f32[128,128]{1,0:T(8,128)S(1)}, f32[128,128]{1,0:T(8,128)S(1)}, u32[]{:S(2)}, u32[]{:S(2)}) collective-permute-start(f32[128,128]{1,0:T(8,128)S(1)} %add.29), channel_id=1, source_target_pairs={{0,32},{1,97},{2,34},{3,99},{4,36},{5,101},{6,38},{7,103},{8,40},{... | collective-permute-start | bytes 196616 | tf_op jit(solution)/shard_map/ppermute | solution.py:371
  59.0 10.2 %collective-permute-start.18 = (f32[2,256,128]{2,1,0:T(8,128)S(1)}, f32[2,256,128]{2,1,0:T(8,128)S(1)}, u32[]{:S(2)}, u32[]{:S(2)}) collective-permute-start(f32[2,256,128]{2,1,0:T(8,128)S(1)} %get-tuple-element.69), channel_id=1, source_target_pairs={{0,16},{1,2},{2,1},{3,4},{4,3},{5,6},{6,5},{7,8},{8,7},{9,10},{10,... | collective-permute-start | bytes 786440 | tf_op jit(solution)/shard_map/ppermute | solution.py:358
  62.3 6.9 %collective-permute-start.19 = (f32[2,256,128]{2,1,0:T(8,128)S(1)}, f32[2,256,128]{2,1,0:T(8,128)S(1)}, u32[]{:S(2)}, u32[]{:S(2)}) collective-permute-start(f32[2,256,128]{2,1,0:T(8,128)S(1)} %get-tuple-element.70), channel_id=1, source_target_pairs={{0,1},{1,0},{2,3},{3,2},{4,5},{5,4},{6,7},{7,6},{8,9},{9,8},{10,11... | collective-permute-start | bytes 786440 | tf_op jit(solution)/shard_map/ppermute | solution.py:358
  65.2 4.0 %collective-permute-start.17 = (f32[128,128]{1,0:T(8,128)S(1)}, f32[128,128]{1,0:T(8,128)S(1)}, u32[]{:S(2)}, u32[]{:S(2)}) collective-permute-start(f32[128,128]{1,0:T(8,128)S(1)} %add.30), channel_id=1, source_target_pairs={{0,96},{1,33},{2,98},{3,35},{4,100},{5,37},{6,102},{7,39},{8,104},... | collective-permute-start | bytes 196616 | tf_op jit(solution)/shard_map/ppermute | solution.py:371
  69.2 3.8 %collective-permute-start.20 = (f32[128,128]{1,0:T(8,128)S(1)}, f32[128,128]{1,0:T(8,128)S(1)}, u32[]{:S(2)}, u32[]{:S(2)}) collective-permute-start(f32[128,128]{1,0:T(8,128)S(1)} %add.31.mine_ref), channel_id=1, source_target_pairs={{0,1},{1,0},{2,3},{3,2},{4,5},{5,4},{6,7},{7,6},{8,9},{9,8},{10,11... | collective-permute-start | bytes 196616 | tf_op jit(solution)/shard_map/ppermute | solution.py:371

commit v18 on v17

--- a/solution.py
+++ b/solution.py
@@ -16,7 +16,8 @@
 LANES = 128
 BOTH = ("row", "col")
 GRANT = 16 * 1024 * 1024
-MASKS = ((16, 16), (4, 12), (12, 4), (128, 130), (130, 128), (32, 96), (96, 32))
+MASKS = ((16, 16), (4, 12), (12, 4), (32, 96), (96, 32))
+Y_MASKS = ((128, 130), (130, 128), (2, 2))
 
 
 def split_table(table):
@@ -428,18 +429,18 @@
     mine = mine + swap(mine, MASKS[1])
     mine, strips[0] = lax.optimization_barrier((mine, strips[0]))
     rows[0] = meet(strips[0], 0, 0)
-    for mask in MASKS[2:4]:
-        mine = mine + swap(mine, mask)
+    mine = mine + swap(mine, MASKS[2])
+    along_y = [swap(mine, mask) for mask in Y_MASKS]
+    mine = (mine + along_y[0]) + (along_y[1] + along_y[2])
     mine, *rows = lax.optimization_barrier((mine, *rows))
     strips = call(fold_kernel, [array(2, *side)] * 2, (), (left, right, *rows))
-    mine = mine + swap(mine, MASKS[4])
     cols = [None, None]
     mine, *strips = lax.optimization_barrier((mine, *strips))
     cols[0] = meet(strips[0], 1, 1)
-    mine = mine + swap(mine, MASKS[5])
+    mine = mine + swap(mine, MASKS[3])
     mine, strips[1] = lax.optimization_barrier((mine, strips[1]))
     cols[1] = meet(strips[1], 1, 0)
-    mine = mine + swap(mine, MASKS[6])
+    mine = mine + swap(mine, MASKS[4])
     mine, *cols = lax.optimization_barrier((mine, *cols))
     (new,) = call(finish_kernel, (field,), (), (part, *rows, *cols))
     other = swap(mine, (1, 1))

time: 73.9 us -> 73.2 us (level)
  starting transfers between devices: 39.2 us -> 38.1 us
    ppermute x9 -> x10, waiting for transfers between devices: 12.1 us -> 14 us  [swap(): lax.ppermute(value, BOTH, [(i, i ^ masks[i % 2]) for i in range(count)])]
    ppermute x12, waiting for transfers between devices: 6.01 us -> 4.43 us  [meet(): return lax.ppermute(strip, BOTH, pairs)]
    ppermute x9 -> x10, starting transfers between devices: 18.4 us -> 16.9 us  [swap(): lax.ppermute(value, BOTH, [(i, i ^ masks[i % 2]) for i in range(count)])]
  transfers between devices with their start and end apart: 21 -> 22, of which waited for: 9 -> 9; matrix products, arithmetic and copies ran while one was open for 0% -> 0% of each run, Pallas kernels for 10% -> 10%
where the time goes in v18:
time: 73.2 us; the launch traced here: 73 us
  starting transfers between devices  38.1 us (52%)
  waiting for transfers between devices  18.4 us (25%)
  Pallas kernels  14.9 us (20%)
  between operations  1.53 us (2%)
    ppermute x12, starting transfers between devices, meet(): return lax.ppermute(strip, BOTH, pairs)  21.2 us
    ppermute x10, starting transfers between devices, swap(): lax.ppermute(value, BOTH, [(i, i ^ masks[i % 2]) for i in range(count)])  16.9 us
    ppermute x10, waiting for transfers between devices, swap(): lax.ppermute(value, BOTH, [(i, i ^ masks[i % 2]) for i in range(count)])  14 us
    pallas_call x8, Pallas kernels, call(): pl.pallas_call(kernel, out_shape=tuple(out_shape), in_specs=smem(len(scal...  12.4 us
    ppermute x12, waiting for transfers between devices, meet(): return lax.ppermute(strip, BOTH, pairs)  4.43 us
    pallas_call x2, Pallas kernels, on_device(): pl.pallas_call(functools.partial(pack_kernel, piece=piece), out_shape=tup...  2.46 us
  transfers between devices with their start and end apart: 22, of which 9 were waited for; matrix products, arithmetic and copies ran while one was open for 0% of the time, Pallas kernels for 10%

profile of v18, /device:TPU:1, one launch (start us, length us, event | category | flops | bytes accessed | tf_op | source)
XLA Modules:
  0.0 73.0 jit_solution(11800696095794840002)
XLA Ops:
  0.6 0.0 copy-start
  0.6 1.3 %shard_map.88 = (f32[256,128]{1,0:T(8,128)S(1)}, f32[256,128]{1,0:T(8,128)S(1)}) custom-call(f32[2,2,256,256]{3,2,1,0:T(8,128)} %obj_ref.13), custom_call_target="tpu_custom_call" | custom-call | tf_op jit(solution)/shard_map/pallas_call | solution.py:393
  1.9 4.4 %collective-permute-start.4 = (f32[256,128]{1,0:T(8,128)S(1)}, f32[256,128]{1,0:T(8,128)S(1)}, u32[]{:S(2)}, u32[]{:S(2)}) collective-permute-start(f32[256,128]{1,0:T(8,128)S(1)} %get-tuple-element.42), channel_id=1, source_target_pairs={{0,16},{1,2},{2,1},{3,4},{4,3},{5,6},{6,5},{7,8},{8,7},{9,10},{10,... | collective-permute-start | bytes 393224 | tf_op jit(solution)/shard_map/ppermute | solution.py:359
  6.3 0.0 collective-permute-start.5
  6.3 1.2 %shard_map.86 = (f32[256,128]{1,0:T(8,128)S(1)}, f32[256,128]{1,0:T(8,128)S(1)}) custom-call(f32[2,2,256,256]{3,2,1,0:T(8,128)} %obj_ref.13), custom_call_target="tpu_custom_call" | custom-call | tf_op jit(solution)/shard_map/pallas_call | solution.py:393
  7.5 1.5 %collective-permute-start = (f32[256,128]{1,0:T(8,128)S(1)}, f32[256,128]{1,0:T(8,128)S(1)}, u32[]{:S(2)}, u32[]{:S(2)}) collective-permute-start(f32[256,128]{1,0:T(8,128)S(1)} %get-tuple-element.38), channel_id=1, source_target_pairs={{0,16},{1,2},{2,1},{3,4},{4,3},{5,6},{6,5},{7,8},{8,7},{9,10},{10,... | collective-permute-start | bytes 393224 | tf_op jit(solution)/shard_map/ppermute | solution.py:359
  9.0 0.0 copy-start.1
  9.0 1.0 %collective-permute-start.1 = (f32[256,128]{1,0:T(8,128)S(1)}, f32[256,128]{1,0:T(8,128)S(1)}, u32[]{:S(2)}, u32[]{:S(2)}) collective-permute-start(f32[256,128]{1,0:T(8,128)S(1)} %get-tuple-element.39), channel_id=1, source_target_pairs={{0,1},{1,0},{2,3},{3,2},{4,5},{5,4},{6,7},{7,6},{8,9},{9,8},{10,11... | collective-permute-start | bytes 393224 | tf_op jit(solution)/shard_map/ppermute | solution.py:359
  10.0 0.0 collective-permute-done.4.colb_ref
  10.0 0.0 collective-permute-done.5.cola_ref
  10.0 0.0 copy-done
  10.1 1.3 %collective-permute-start.6 = (f32[6,64,128]{2,1,0:T(8,128)S(1)}, f32[6,64,128]{2,1,0:T(8,128)S(1)}, u32[]{:S(2)}, u32[]{:S(2)}) collective-permute-start(f32[6,64,128]{2,1,0:T(8,128)S(1)} %get-tuple-element.44), channel_id=1, source_target_pairs={{0,16},{1,17},{2,18},{3,19},{4,20},{5,21},{6,22},{7,23},{8,24},{9,... | collective-permute-start | bytes 589832 | tf_op jit(solution)/shard_map/ppermute | solution.py:359
  11.4 0.0 copy-start.2
  11.4 0.1 collective-permute-start.7
  11.6 1.9 %collective-permute-done.colb_ref = f32[256,128]{1,0:T(8,128)S(1)} collective-permute-done((f32[256,128]{1,0:T(8,128)S(1)}, f32[256,128]{1,0:T(8,128)S(1)}, u32[]{:S(2)}, u32[]{:S(2)}) %collective-permute-start) | collective-permute-done | bytes 131104 | tf_op jit(solution)/shard_map/ppermute | solution.py:359
  13.5 0.0 collective-permute-done.1.cola_ref
  13.5 0.1 collective-permute-start.2
  13.6 0.0 copy-start.4
  13.7 0.0 copy-start.5
  13.7 3.2 %collective-permute-start.3 = (f32[6,64,128]{2,1,0:T(8,128)S(1)}, f32[6,64,128]{2,1,0:T(8,128)S(1)}, u32[]{:S(2)}, u32[]{:S(2)}) collective-permute-start(f32[6,64,128]{2,1,0:T(8,128)S(1)} %get-tuple-element.41), channel_id=1, source_target_pairs={{0,16},{1,17},{2,18},{3,19},{4,20},{5,21},{6,22},{7,23},{8,24},{9,... | collective-permute-start | bytes 589832 | tf_op jit(solution)/shard_map/ppermute | solution.py:359
  17.6 0.0 copy-start.3
  17.6 0.0 collective-permute-done.6.rowa_ref
  17.6 0.0 collective-permute-done.7.rowb_ref
  17.6 0.0 copy-done.1
  17.6 0.0 copy-done.2
  17.6 0.0 copy-done.4
  17.6 0.0 copy-done.5
  17.6 2.2 %shard_map.90 = (f32[8,2,128,128]{3,2,1,0:T(8,128)S(1)}, f32[8,2,128,128]{3,2,1,0:T(8,128)S(1)}) custom-call(s32[1,8]{1,0:T(1,128)S(1)} %copy-done.4, s32[1,8]{1,0:T(1,128)S(1)} %copy-done.5, f32[2,2,256,256]{3,2,1,0:T(8,128)S(1)} %copy-done, f32[256,128]{1,0:T(8,128)S(1)} %collective-permute-done.4.colb_ref, ...), custom_call_target="tpu_custom_call" | custom-call | tf_op jit(solution)/shard_map/pallas_call | solution.py:376
  19.9 0.0 collective-permute-done.2.rowb_ref
  19.9 2.5 %collective-permute-done.3.rowa_ref = f32[6,64,128]{2,1,0:T(8,128)S(1)} collective-permute-done((f32[6,64,128]{2,1,0:T(8,128)S(1)}, f32[6,64,128]{2,1,0:T(8,128)S(1)}, u32[]{:S(2)}, u32[]{:S(2)}) %collective-permute-start.3) | collective-permute-done | bytes 196640 | tf_op jit(solution)/shard_map/ppermute | solution.py:359
  22.3 0.0 copy-done.3
  22.3 5.8 %shard_map.91 = (f32[8,2,128,128]{3,2,1,0:T(8,128)S(1)}, f32[8,2,128,128]{3,2,1,0:T(8,128)S(1)}, f32[128,128]{1,0:T(8,128)S(1)}, f32[128,128]{1,0:T(8,128)S(1)}) custom-call(s32[1,8]{1,0:T(1,128)S(1)} %copy-done.4, s32[1,8]{1,0:T(1,128)S(1)} %copy-done.5, s32[1,1]{1,0:T(1,128)S(6)} %copy.9.live_ref, f32[2,2,256,256]{3,2,1,0:T(8,128)S(1)} %copy-done, ...), custom_call_target="tpu_custom_call" | custom-call | tf_op jit(solution)/shard_map/pallas_call | solution.py:376
  28.2 0.5 collective-permute-start.8
  28.7 0.9 %collective-permute-done.8 = f32[128,128]{1,0:T(8,128)S(1)} collective-permute-done((f32[128,128]{1,0:T(8,128)S(1)}, f32[128,128]{1,0:T(8,128)S(1)}, u32[]{:S(2)}, u32[]{:S(2)}) %collective-permute-start.8) | collective-permute-done | bytes 65568 | tf_op jit(solution)/shard_map/ppermute | solution.py:372
  29.6 2.3 %collective-permute-start.9 = (f32[128,128]{1,0:T(8,128)S(1)}, f32[128,128]{1,0:T(8,128)S(1)}, u32[]{:S(2)}, u32[]{:S(2)}) collective-permute-start(f32[128,128]{1,0:T(8,128)S(1)} %add.27), channel_id=1, source_target_pairs={{0,16},{1,17},{2,18},{3,19},{4,20},{5,21},{6,22},{7,23},{8,24},{9,... | collective-permute-start | bytes 196616 | tf_op jit(solution)/shard_map/ppermute | solution.py:372
  31.9 2.3 %shard_map.92 = (f32[2,2,256,256]{3,2,1,0:T(8,128)S(1)}, f32[2,6,64,128]{3,2,1,0:T(8,128)S(1)}, f32[2,6,64,128]{3,2,1,0:T(8,128)S(1)}, f32[2,256,128]{2,1,0:T(8,128)S(1)}, f32[2,256,128]{2,1,0:T(8,128)S(1)}) custom-call(s32[1,8]{1,0:T(1,128)S(1)} %copy-done.4, s32[1,8]{1,0:T(1,128)S(1)} %copy-done.5, f32[2,2,256,256]{3,2,1,0:T(8,128)S(1)} %copy-done, ...), custom_call_target="tpu_custom_call" | custom-call | tf_op jit(solution)/shard_map/pallas_call | solution.py:376
  34.2 0.0 collective-permute-done.9
  34.2 3.5 %collective-permute-start.10 = (f32[128,128]{1,0:T(8,128)S(1)}, f32[128,128]{1,0:T(8,128)S(1)}, u32[]{:S(2)}, u32[]{:S(2)}) collective-permute-start(f32[128,128]{1,0:T(8,128)S(1)} %add.28), channel_id=1, source_target_pairs={{0,4},{1,13},{2,6},{3,15},{4,0},{5,9},{6,2},{7,11},{8,12},{9,5},{1... | collective-permute-start | bytes 196616 | tf_op jit(solution)/shard_map/ppermute | solution.py:372
  37.8 0.0 collective-permute-start.16
  37.8 1.7 %collective-permute-done.10 = f32[128,128]{1,0:T(8,128)S(1)} collective-permute-done((f32[128,128]{1,0:T(8,128)S(1)}, f32[128,128]{1,0:T(8,128)S(1)}, u32[]{:S(2)}, u32[]{:S(2)}) %collective-permute-start.10) | collective-permute-done | bytes 65568 | tf_op jit(solution)/shard_map/ppermute | solution.py:372
  39.4 2.9 %collective-permute-start.15 = (f32[2,6,64,128]{3,2,1,0:T(8,128)S(1)}, f32[2,6,64,128]{3,2,1,0:T(8,128)S(1)}, u32[]{:S(2)}, u32[]{:S(2)}) collective-permute-start(f32[2,6,64,128]{3,2,1,0:T(8,128)S(1)} %get-tuple-element.57), channel_id=1, source_target_pairs={{0,16},{1,17},{2,18},{3,19},{4,20},{5,21},{6,22},{7,23},{8,24},{9,... | collective-permute-start | bytes 1179656 | tf_op jit(solution)/shard_map/ppermute | solution.py:359
  42.3 0.0 collective-permute-start.11
  42.3 3.4 %collective-permute-done.11 = f32[128,128]{1,0:T(8,128)S(1)} collective-permute-done((f32[128,128]{1,0:T(8,128)S(1)}, f32[128,128]{1,0:T(8,128)S(1)}, u32[]{:S(2)}, u32[]{:S(2)}) %collective-permute-start.11) | collective-permute-done | bytes 65568 | tf_op jit(solution)/shard_map/ppermute | solution.py:372
  45.8 0.3 collective-permute-start.14
  46.1 2.6 %collective-permute-start.13 = (f32[128,128]{1,0:T(8,128)S(1)}, f32[128,128]{1,0:T(8,128)S(1)}, u32[]{:S(2)}, u32[]{:S(2)}) collective-permute-start(f32[128,128]{1,0:T(8,128)S(1)} %add.30), channel_id=1, source_target_pairs={{0,130},{1,129},{2,128},{3,131},{4,134},{5,133},{6,132},{7,135},{8... | collective-permute-start | bytes 196616 | tf_op jit(solution)/shard_map/ppermute | solution.py:372
  48.7 1.9 %collective-permute-start.12 = (f32[128,128]{1,0:T(8,128)S(1)}, f32[128,128]{1,0:T(8,128)S(1)}, u32[]{:S(2)}, u32[]{:S(2)}) collective-permute-start(f32[128,128]{1,0:T(8,128)S(1)} %add.30), channel_id=1, source_target_pairs={{0,128},{1,131},{2,130},{3,129},{4,132},{5,135},{6,134},{7,133},{8... | collective-permute-start | bytes 196616 | tf_op jit(solution)/shard_map/ppermute | solution.py:372
  50.6 4.2 %collective-permute-done.14 = f32[128,128]{1,0:T(8,128)S(1)} collective-permute-done((f32[128,128]{1,0:T(8,128)S(1)}, f32[128,128]{1,0:T(8,128)S(1)}, u32[]{:S(2)}, u32[]{:S(2)}) %collective-permute-start.14) | collective-permute-done | bytes 65568 | tf_op jit(solution)/shard_map/ppermute | solution.py:372
  54.8 0.8 %collective-permute-done.13 = f32[128,128]{1,0:T(8,128)S(1)} collective-permute-done((f32[128,128]{1,0:T(8,128)S(1)}, f32[128,128]{1,0:T(8,128)S(1)}, u32[]{:S(2)}, u32[]{:S(2)}) %collective-permute-start.13) | collective-permute-done | bytes 65568 | tf_op jit(solution)/shard_map/ppermute | solution.py:372
  55.6 0.0 collective-permute-done.12
  55.6 0.0 collective-permute-done.16.rowb_ref
  55.6 0.0 collective-permute-done.15.rowa_ref
  55.7 0.1 shard_map.93
  55.7 1.0 %collective-permute-start.17 = (f32[128,128]{1,0:T(8,128)S(1)}, f32[128,128]{1,0:T(8,128)S(1)}, u32[]{:S(2)}, u32[]{:S(2)}) collective-permute-start(f32[128,128]{1,0:T(8,128)S(1)} %add_add_fusion), channel_id=1, source_target_pairs={{0,32},{1,97},{2,34},{3,99},{4,36},{5,101},{6,38},{7,103},{8,40},{... | collective-permute-start | bytes 196616 | tf_op jit(solution)/shard_map/ppermute | solution.py:372
  56.7 4.0 %collective-permute-start.19 = (f32[2,256,128]{2,1,0:T(8,128)S(1)}, f32[2,256,128]{2,1,0:T(8,128)S(1)}, u32[]{:S(2)}, u32[]{:S(2)}) collective-permute-start(f32[2,256,128]{2,1,0:T(8,128)S(1)} %get-tuple-element.69), channel_id=1, source_target_pairs={{0,16},{1,2},{2,1},{3,4},{4,3},{5,6},{6,5},{7,8},{8,7},{9,10},{10,... | collective-permute-start | bytes 786440 | tf_op jit(solution)/shard_map/ppermute | solution.py:359
  60.8 0.4 collective-permute-done.17
  61.2 2.6 %collective-permute-start.20 = (f32[2,256,128]{2,1,0:T(8,128)S(1)}, f32[2,256,128]{2,1,0:T(8,128)S(1)}, u32[]{:S(2)}, u32[]{:S(2)}) collective-permute-start(f32[2,256,128]{2,1,0:T(8,128)S(1)} %get-tuple-element.70), channel_id=1, source_target_pairs={{0,1},{1,0},{2,3},{3,2},{4,5},{5,4},{6,7},{7,6},{8,9},{9,8},{10,11... | collective-permute-start | bytes 786440 | tf_op jit(solution)/shard_map/ppermute | solution.py:359
  63.7 1.4 %collective-permute-start.18 = (f32[128,128]{1,0:T(8,128)S(1)}, f32[128,128]{1,0:T(8,128)S(1)}, u32[]{:S(2)}, u32[]{:S(2)}) collective-permute-start(f32[128,128]{1,0:T(8,128)S(1)} %add.34), channel_id=1, source_target_pairs={{0,96},{1,33},{2,98},{3,35},{4,100},{5,37},{6,102},{7,39},{8,104},... | collective-permute-start | bytes 196616 | tf_op jit(solution)/shard_map/ppermute | solution.py:372
  65.2 2.6 %collective-permute-done.18 = f32[128,128]{1,0:T(8,128)S(1)} collective-permute-done((f32[128,128]{1,0:T(8,128)S(1)}, f32[128,128]{1,0:T(8,128)S(1)}, u32[]{:S(2)}, u32[]{:S(2)}) %collective-permute-start.18) | collective-permute-done | bytes 65568 | tf_op jit(solution)/shard_map/ppermute | solution.py:372
  67.8 0.0 collective-permute-done.19.colb_ref
  67.8 0.0 collective-permute-done.20.cola_ref
  67.8 3.4 %collective-permute-start.21 = (f32[128,128]{1,0:T(8,128)S(1)}, f32[128,128]{1,0:T(8,128)S(1)}, u32[]{:S(2)}, u32[]{:S(2)}) collective-permute-start(f32[128,128]{1,0:T(8,128)S(1)} %add.35.mine_ref), channel_id=1, source_target_pairs={{0,1},{1,0},{2,3},{3,2},{4,5},{5,4},{6,7},{7,6},{8,9},{9,8},{10,11... | collective-permute-start | bytes 196616 | tf_op jit(solution)/shard_map/ppermute | solution.py:372
  71.1 1.2 %shard_map.94 = f32[2,2,256,256]{3,2,1,0:T(8,128)} custom-call(f32[2,2,256,256]{3,2,1,0:T(8,128)S(1)} %get-tuple-element.50.part_ref, f32[2,6,64,128]{3,2,1,0:T(8,128)S(1)} %collective-permute-done.15.rowa_ref, f32[2,6,64,128]{3,2,1,0:T(8,128)S(1)} %collective-permute-done.16.rowb_ref, f32[2,256,128]{2,1,0:T(8,128)S(1)} %collective-permute-done.19.colb_ref, ...), custom_call_target="tpu_custom_call" | custom-call | tf_op jit(solution)/shard_map/pallas_call | solution.py:376
  72.4 0.0 collective-permute-done.21.other_ref
  72.4 0.7 shard_map.95
  (9 shorter events, 0.2 us)
Async XLA Ops:
  0.6 9.4 %copy-start = (f32[2,2,256,256]{3,2,1,0:T(8,128)S(1)}, f32[2,2,256,256]{3,2,1,0:T(8,128)}, u32[]{:S(2)}) copy-start(f32[2,2,256,256]{3,2,1,0:T(8,128)} %obj_ref.13) | copy-start | bytes 3145732
  1.9 8.1 %collective-permute-start.4 = (f32[256,128]{1,0:T(8,128)S(1)}, f32[256,128]{1,0:T(8,128)S(1)}, u32[]{:S(2)}, u32[]{:S(2)}) collective-permute-start(f32[256,128]{1,0:T(8,128)S(1)} %get-tuple-element.42), channel_id=1, source_target_pairs={{0,16},{1,2},{2,1},{3,4},{4,3},{5,6},{6,5},{7,8},{8,7},{9,10},{10,... | collective-permute-start | bytes 393224 | tf_op jit(solution)/shard_map/ppermute | solution.py:359
  6.3 3.7 %collective-permute-start.5 = (f32[256,128]{1,0:T(8,128)S(1)}, f32[256,128]{1,0:T(8,128)S(1)}, u32[]{:S(2)}, u32[]{:S(2)}) collective-permute-start(f32[256,128]{1,0:T(8,128)S(1)} %get-tuple-element.43), channel_id=1, source_target_pairs={{0,1},{1,0},{2,3},{3,2},{4,5},{5,4},{6,7},{7,6},{8,9},{9,8},{10,11... | collective-permute-start | bytes 393224 | tf_op jit(solution)/shard_map/ppermute | solution.py:359
  7.5 6.0 %collective-permute-start = (f32[256,128]{1,0:T(8,128)S(1)}, f32[256,128]{1,0:T(8,128)S(1)}, u32[]{:S(2)}, u32[]{:S(2)}) collective-permute-start(f32[256,128]{1,0:T(8,128)S(1)} %get-tuple-element.38), channel_id=1, source_target_pairs={{0,16},{1,2},{2,1},{3,4},{4,3},{5,6},{6,5},{7,8},{8,7},{9,10},{10,... | collective-permute-start | bytes 393224 | tf_op jit(solution)/shard_map/ppermute | solution.py:359
  9.0 8.6 %copy-start.1 = (bf16[4,2,256,256]{3,2,1,0:T(8,128)(2,1)S(1)}, bf16[4,2,256,256]{3,2,1,0:T(8,128)(2,1)}, u32[]{:S(2)}) copy-start(bf16[4,2,256,256]{3,2,1,0:T(8,128)(2,1)} %constant.2.clone.tabs_ref) | copy-start | bytes 3145732
  9.0 4.5 %collective-permute-start.1 = (f32[256,128]{1,0:T(8,128)S(1)}, f32[256,128]{1,0:T(8,128)S(1)}, u32[]{:S(2)}, u32[]{:S(2)}) collective-permute-start(f32[256,128]{1,0:T(8,128)S(1)} %get-tuple-element.39), channel_id=1, source_target_pairs={{0,1},{1,0},{2,3},{3,2},{4,5},{5,4},{6,7},{7,6},{8,9},{9,8},{10,11... | collective-permute-start | bytes 393224 | tf_op jit(solution)/shard_map/ppermute | solution.py:359
  10.1 7.5 %collective-permute-start.6 = (f32[6,64,128]{2,1,0:T(8,128)S(1)}, f32[6,64,128]{2,1,0:T(8,128)S(1)}, u32[]{:S(2)}, u32[]{:S(2)}) collective-permute-start(f32[6,64,128]{2,1,0:T(8,128)S(1)} %get-tuple-element.44), channel_id=1, source_target_pairs={{0,16},{1,17},{2,18},{3,19},{4,20},{5,21},{6,22},{7,23},{8,24},{9,... | collective-permute-start | bytes 589832 | tf_op jit(solution)/shard_map/ppermute | solution.py:359
  11.4 6.2 %copy-start.2 = (f32[2,128,128]{2,1,0:T(8,128)S(1)}, f32[2,128,128]{2,1,0:T(8,128)}, u32[]{:S(2)}) copy-start(f32[2,128,128]{2,1,0:T(8,128)} %probe_ref.5) | copy-start | bytes 393220
  11.4 6.2 %collective-permute-start.7 = (f32[6,64,128]{2,1,0:T(8,128)S(1)}, f32[6,64,128]{2,1,0:T(8,128)S(1)}, u32[]{:S(2)}, u32[]{:S(2)}) collective-permute-start(f32[6,64,128]{2,1,0:T(8,128)S(1)} %get-tuple-element.45), channel_id=1, source_target_pairs={{0,1},{1,0},{2,3},{3,2},{4,5},{5,4},{6,7},{7,6},{8,9},{9,8},{10,11... | collective-permute-start | bytes 589832 | tf_op jit(solution)/shard_map/ppermute | solution.py:359
  13.5 6.3 %collective-permute-start.2 = (f32[6,64,128]{2,1,0:T(8,128)S(1)}, f32[6,64,128]{2,1,0:T(8,128)S(1)}, u32[]{:S(2)}, u32[]{:S(2)}) collective-permute-start(f32[6,64,128]{2,1,0:T(8,128)S(1)} %get-tuple-element.40), channel_id=1, source_target_pairs={{0,1},{1,0},{2,3},{3,2},{4,5},{5,4},{6,7},{7,6},{8,9},{9,8},{10,11... | collective-permute-start | bytes 589832 | tf_op jit(solution)/shard_map/ppermute | solution.py:359
  13.6 4.0 %copy-start.4 = (s32[1,8]{1,0:T(1,128)S(1)}, s32[1,8]{1,0:T(1,128)}, u32[]{:S(2)}) copy-start(s32[1,8]{1,0:T(1,128)} %row_ref.5) | copy-start | bytes 100
  13.7 4.0 %copy-start.5 = (s32[1,8]{1,0:T(1,128)S(1)}, s32[1,8]{1,0:T(1,128)}, u32[]{:S(2)}) copy-start(s32[1,8]{1,0:T(1,128)} %col_ref.5) | copy-start | bytes 100
  13.7 8.7 %collective-permute-start.3 = (f32[6,64,128]{2,1,0:T(8,128)S(1)}, f32[6,64,128]{2,1,0:T(8,128)S(1)}, u32[]{:S(2)}, u32[]{:S(2)}) collective-permute-start(f32[6,64,128]{2,1,0:T(8,128)S(1)} %get-tuple-element.41), channel_id=1, source_target_pairs={{0,16},{1,17},{2,18},{3,19},{4,20},{5,21},{6,22},{7,23},{8,24},{9,... | collective-permute-start | bytes 589832 | tf_op jit(solution)/shard_map/ppermute | solution.py:359
  17.6 4.8 %copy-start.3 = (f32[1,8,128,128]{3,2,1,0:T(8,128)S(1)}, f32[1,8,128,128]{3,2,1,0:T(8,128)}, u32[]{:S(2)}) copy-start(f32[1,8,128,128]{3,2,1,0:T(8,128)} %param.9) | copy-start | bytes 1572868
  28.2 1.4 %collective-permute-start.8 = (f32[128,128]{1,0:T(8,128)S(1)}, f32[128,128]{1,0:T(8,128)S(1)}, u32[]{:S(2)}, u32[]{:S(2)}) collective-permute-start(f32[128,128]{1,0:T(8,128)S(1)} %get-tuple-element.52), channel_id=1, source_target_pairs={{0,1},{1,0},{2,3},{3,2},{4,5},{5,4},{6,7},{7,6},{8,9},{9,8},{10,11... | collective-permute-start | bytes 196616 | tf_op jit(solution)/shard_map/ppermute | solution.py:372
  29.6 4.6 %collective-permute-start.9 = (f32[128,128]{1,0:T(8,128)S(1)}, f32[128,128]{1,0:T(8,128)S(1)}, u32[]{:S(2)}, u32[]{:S(2)}) collective-permute-start(f32[128,128]{1,0:T(8,128)S(1)} %add.27), channel_id=1, source_target_pairs={{0,16},{1,17},{2,18},{3,19},{4,20},{5,21},{6,22},{7,23},{8,24},{9,... | collective-permute-start | bytes 196616 | tf_op jit(solution)/shard_map/ppermute | solution.py:372
  34.2 5.2 %collective-permute-start.10 = (f32[128,128]{1,0:T(8,128)S(1)}, f32[128,128]{1,0:T(8,128)S(1)}, u32[]{:S(2)}, u32[]{:S(2)}) collective-permute-start(f32[128,128]{1,0:T(8,128)S(1)} %add.28), channel_id=1, source_target_pairs={{0,4},{1,13},{2,6},{3,15},{4,0},{5,9},{6,2},{7,11},{8,12},{9,5},{1... | collective-permute-start | bytes 196616 | tf_op jit(solution)/shard_map/ppermute | solution.py:372
  37.8 17.9 %collective-permute-start.16 = (f32[2,6,64,128]{3,2,1,0:T(8,128)S(1)}, f32[2,6,64,128]{3,2,1,0:T(8,128)S(1)}, u32[]{:S(2)}, u32[]{:S(2)}) collective-permute-start(f32[2,6,64,128]{3,2,1,0:T(8,128)S(1)} %get-tuple-element.58), channel_id=1, source_target_pairs={{0,1},{1,0},{2,3},{3,2},{4,5},{5,4},{6,7},{7,6},{8,9},{9,8},{10,11... | collective-permute-start | bytes 1179656 | tf_op jit(solution)/shard_map/ppermute | solution.py:359
  39.4 16.2 %collective-permute-start.15 = (f32[2,6,64,128]{3,2,1,0:T(8,128)S(1)}, f32[2,6,64,128]{3,2,1,0:T(8,128)S(1)}, u32[]{:S(2)}, u32[]{:S(2)}) collective-permute-start(f32[2,6,64,128]{3,2,1,0:T(8,128)S(1)} %get-tuple-element.57), channel_id=1, source_target_pairs={{0,16},{1,17},{2,18},{3,19},{4,20},{5,21},{6,22},{7,23},{8,24},{9,... | collective-permute-start | bytes 1179656 | tf_op jit(solution)/shard_map/ppermute | solution.py:359
  42.3 3.4 %collective-permute-start.11 = (f32[128,128]{1,0:T(8,128)S(1)}, f32[128,128]{1,0:T(8,128)S(1)}, u32[]{:S(2)}, u32[]{:S(2)}) collective-permute-start(f32[128,128]{1,0:T(8,128)S(1)} %add.29), channel_id=1, source_target_pairs={{0,12},{1,5},{2,14},{3,7},{4,8},{5,1},{6,10},{7,3},{8,4},{9,13},{1... | collective-permute-start | bytes 196616 | tf_op jit(solution)/shard_map/ppermute | solution.py:372
  45.8 9.0 %collective-permute-start.14 = (f32[128,128]{1,0:T(8,128)S(1)}, f32[128,128]{1,0:T(8,128)S(1)}, u32[]{:S(2)}, u32[]{:S(2)}) collective-permute-start(f32[128,128]{1,0:T(8,128)S(1)} %add.30), channel_id=1, source_target_pairs={{0,2},{1,3},{2,0},{3,1},{4,6},{5,7},{6,4},{7,5},{8,10},{9,11},{10,... | collective-permute-start | bytes 196616 | tf_op jit(solution)/shard_map/ppermute | solution.py:372
  46.1 9.5 %collective-permute-start.13 = (f32[128,128]{1,0:T(8,128)S(1)}, f32[128,128]{1,0:T(8,128)S(1)}, u32[]{:S(2)}, u32[]{:S(2)}) collective-permute-start(f32[128,128]{1,0:T(8,128)S(1)} %add.30), channel_id=1, source_target_pairs={{0,130},{1,129},{2,128},{3,131},{4,134},{5,133},{6,132},{7,135},{8... | collective-permute-start | bytes 196616 | tf_op jit(solution)/shard_map/ppermute | solution.py:372
  48.7 6.9 %collective-permute-start.12 = (f32[128,128]{1,0:T(8,128)S(1)}, f32[128,128]{1,0:T(8,128)S(1)}, u32[]{:S(2)}, u32[]{:S(2)}) collective-permute-start(f32[128,128]{1,0:T(8,128)S(1)} %add.30), channel_id=1, source_target_pairs={{0,128},{1,131},{2,130},{3,129},{4,132},{5,135},{6,134},{7,133},{8... | collective-permute-start | bytes 196616 | tf_op jit(solution)/shard_map/ppermute | solution.py:372
  55.7 5.4 %collective-permute-start.17 = (f32[128,128]{1,0:T(8,128)S(1)}, f32[128,128]{1,0:T(8,128)S(1)}, u32[]{:S(2)}, u32[]{:S(2)}) collective-permute-start(f32[128,128]{1,0:T(8,128)S(1)} %add_add_fusion), channel_id=1, source_target_pairs={{0,32},{1,97},{2,34},{3,99},{4,36},{5,101},{6,38},{7,103},{8,40},{... | collective-permute-start | bytes 196616 | tf_op jit(solution)/shard_map/ppermute | solution.py:372
  56.7 11.0 %collective-permute-start.19 = (f32[2,256,128]{2,1,0:T(8,128)S(1)}, f32[2,256,128]{2,1,0:T(8,128)S(1)}, u32[]{:S(2)}, u32[]{:S(2)}) collective-permute-start(f32[2,256,128]{2,1,0:T(8,128)S(1)} %get-tuple-element.69), channel_id=1, source_target_pairs={{0,16},{1,2},{2,1},{3,4},{4,3},{5,6},{6,5},{7,8},{8,7},{9,10},{10,... | collective-permute-start | bytes 786440 | tf_op jit(solution)/shard_map/ppermute | solution.py:359
  61.2 6.6 %collective-permute-start.20 = (f32[2,256,128]{2,1,0:T(8,128)S(1)}, f32[2,256,128]{2,1,0:T(8,128)S(1)}, u32[]{:S(2)}, u32[]{:S(2)}) collective-permute-start(f32[2,256,128]{2,1,0:T(8,128)S(1)} %get-tuple-element.70), channel_id=1, source_target_pairs={{0,1},{1,0},{2,3},{3,2},{4,5},{5,4},{6,7},{7,6},{8,9},{9,8},{10,11... | collective-permute-start | bytes 786440 | tf_op jit(solution)/shard_map/ppermute | solution.py:359
  63.7 4.0 %collective-permute-start.18 = (f32[128,128]{1,0:T(8,128)S(1)}, f32[128,128]{1,0:T(8,128)S(1)}, u32[]{:S(2)}, u32[]{:S(2)}) collective-permute-start(f32[128,128]{1,0:T(8,128)S(1)} %add.34), channel_id=1, source_target_pairs={{0,96},{1,33},{2,98},{3,35},{4,100},{5,37},{6,102},{7,39},{8,104},... | collective-permute-start | bytes 196616 | tf_op jit(solution)/shard_map/ppermute | solution.py:372
  67.8 4.6 %collective-permute-start.21 = (f32[128,128]{1,0:T(8,128)S(1)}, f32[128,128]{1,0:T(8,128)S(1)}, u32[]{:S(2)}, u32[]{:S(2)}) collective-permute-start(f32[128,128]{1,0:T(8,128)S(1)} %add.35.mine_ref), channel_id=1, source_target_pairs={{0,1},{1,0},{2,3},{3,2},{4,5},{5,4},{6,7},{7,6},{8,9},{9,8},{10,11... | collective-permute-start | bytes 196616 | tf_op jit(solution)/shard_map/ppermute | solution.py:372

commit v19 on v18

--- a/solution.py
+++ b/solution.py
@@ -16,7 +16,7 @@
 LANES = 128
 BOTH = ("row", "col")
 GRANT = 16 * 1024 * 1024
-MASKS = ((16, 16), (4, 12), (12, 4), (32, 96), (96, 32))
+MASKS = ((16, 32), (4, 12), (12, 4), (32, 96), (96, 16))
 Y_MASKS = ((128, 130), (130, 128), (2, 2))
 
 

time: 73.2 us -> 73.4 us (level)
    ppermute x12, starting transfers between devices: 21.2 us -> 18.7 us  [meet(): return lax.ppermute(strip, BOTH, pairs)]
    ppermute x10, starting transfers between devices: 16.9 us -> 19.5 us  [swap(): lax.ppermute(value, BOTH, [(i, i ^ masks[i % 2]) for i in range(count)])]
where the time goes in v19:
time: 73.4 us; the launch traced here: 73.3 us
  starting transfers between devices  38.1 us (52%)
  waiting for transfers between devices  18.7 us (25%)
  Pallas kernels  14.9 us (20%)
  between operations  1.53 us (2%)
    ppermute x10, starting transfers between devices, swap(): lax.ppermute(value, BOTH, [(i, i ^ masks[i % 2]) for i in range(count)])  19.5 us
    ppermute x12, starting transfers between devices, meet(): return lax.ppermute(strip, BOTH, pairs)  18.7 us
    ppermute x10, waiting for transfers between devices, swap(): lax.ppermute(value, BOTH, [(i, i ^ masks[i % 2]) for i in range(count)])  14.3 us
    pallas_call x8, Pallas kernels, call(): pl.pallas_call(kernel, out_shape=tuple(out_shape), in_specs=smem(len(scal...  12.4 us
    ppermute x12, waiting for transfers between devices, meet(): return lax.ppermute(strip, BOTH, pairs)  4.43 us
    pallas_call x2, Pallas kernels, on_device(): pl.pallas_call(functools.partial(pack_kernel, piece=piece), out_shape=tup...  2.46 us
  transfers between devices with their start and end apart: 22, of which 9 were waited for; matrix products, arithmetic and copies ran while one was open for 0% of the time, Pallas kernels for 10%

profile of v19, /device:TPU:1, one launch (start us, length us, event | category | flops | bytes accessed | tf_op | source)
XLA Modules:
  0.0 73.3 jit_solution(11705759087964760110)
XLA Ops:
  0.6 0.0 copy-start
  0.6 1.3 %shard_map.88 = (f32[256,128]{1,0:T(8,128)S(1)}, f32[256,128]{1,0:T(8,128)S(1)}) custom-call(f32[2,2,256,256]{3,2,1,0:T(8,128)} %obj_ref.13), custom_call_target="tpu_custom_call" | custom-call | tf_op jit(solution)/shard_map/pallas_call | solution.py:393
  1.9 4.4 %collective-permute-start.4 = (f32[256,128]{1,0:T(8,128)S(1)}, f32[256,128]{1,0:T(8,128)S(1)}, u32[]{:S(2)}, u32[]{:S(2)}) collective-permute-start(f32[256,128]{1,0:T(8,128)S(1)} %get-tuple-element.42), channel_id=1, source_target_pairs={{0,16},{1,2},{2,1},{3,4},{4,3},{5,6},{6,5},{7,8},{8,7},{9,10},{10,... | collective-permute-start | bytes 393224 | tf_op jit(solution)/shard_map/ppermute | solution.py:359
  6.3 0.0 collective-permute-start.5
  6.3 1.2 %shard_map.86 = (f32[256,128]{1,0:T(8,128)S(1)}, f32[256,128]{1,0:T(8,128)S(1)}) custom-call(f32[2,2,256,256]{3,2,1,0:T(8,128)} %obj_ref.13), custom_call_target="tpu_custom_call" | custom-call | tf_op jit(solution)/shard_map/pallas_call | solution.py:393
  7.5 1.5 %collective-permute-start = (f32[256,128]{1,0:T(8,128)S(1)}, f32[256,128]{1,0:T(8,128)S(1)}, u32[]{:S(2)}, u32[]{:S(2)}) collective-permute-start(f32[256,128]{1,0:T(8,128)S(1)} %get-tuple-element.38), channel_id=1, source_target_pairs={{0,16},{1,2},{2,1},{3,4},{4,3},{5,6},{6,5},{7,8},{8,7},{9,10},{10,... | collective-permute-start | bytes 393224 | tf_op jit(solution)/shard_map/ppermute | solution.py:359
  9.0 0.0 copy-start.1
  9.0 1.0 %collective-permute-start.1 = (f32[256,128]{1,0:T(8,128)S(1)}, f32[256,128]{1,0:T(8,128)S(1)}, u32[]{:S(2)}, u32[]{:S(2)}) collective-permute-start(f32[256,128]{1,0:T(8,128)S(1)} %get-tuple-element.39), channel_id=1, source_target_pairs={{0,1},{1,0},{2,3},{3,2},{4,5},{5,4},{6,7},{7,6},{8,9},{9,8},{10,11... | collective-permute-start | bytes 393224 | tf_op jit(solution)/shard_map/ppermute | solution.py:359
  10.0 0.0 collective-permute-done.4.colb_ref
  10.0 0.0 collective-permute-done.5.cola_ref
  10.0 0.0 copy-done
  10.1 1.3 %collective-permute-start.6 = (f32[6,64,128]{2,1,0:T(8,128)S(1)}, f32[6,64,128]{2,1,0:T(8,128)S(1)}, u32[]{:S(2)}, u32[]{:S(2)}) collective-permute-start(f32[6,64,128]{2,1,0:T(8,128)S(1)} %get-tuple-element.44), channel_id=1, source_target_pairs={{0,16},{1,17},{2,18},{3,19},{4,20},{5,21},{6,22},{7,23},{8,24},{9,... | collective-permute-start | bytes 589832 | tf_op jit(solution)/shard_map/ppermute | solution.py:359
  11.4 0.0 copy-start.2
  11.4 0.1 collective-permute-start.7
  11.6 1.9 %collective-permute-done.colb_ref = f32[256,128]{1,0:T(8,128)S(1)} collective-permute-done((f32[256,128]{1,0:T(8,128)S(1)}, f32[256,128]{1,0:T(8,128)S(1)}, u32[]{:S(2)}, u32[]{:S(2)}) %collective-permute-start) | collective-permute-done | bytes 131104 | tf_op jit(solution)/shard_map/ppermute | solution.py:359
  13.5 0.0 collective-permute-done.1.cola_ref
  13.5 0.1 collective-permute-start.2
  13.6 0.0 copy-start.4
  13.7 0.0 copy-start.5
  13.7 3.2 %collective-permute-start.3 = (f32[6,64,128]{2,1,0:T(8,128)S(1)}, f32[6,64,128]{2,1,0:T(8,128)S(1)}, u32[]{:S(2)}, u32[]{:S(2)}) collective-permute-start(f32[6,64,128]{2,1,0:T(8,128)S(1)} %get-tuple-element.41), channel_id=1, source_target_pairs={{0,16},{1,17},{2,18},{3,19},{4,20},{5,21},{6,22},{7,23},{8,24},{9,... | collective-permute-start | bytes 589832 | tf_op jit(solution)/shard_map/ppermute | solution.py:359
  17.6 0.0 copy-start.3
  17.6 0.0 collective-permute-done.6.rowa_ref
  17.6 0.0 collective-permute-done.7.rowb_ref
  17.6 0.0 copy-done.1
  17.6 0.0 copy-done.2
  17.6 0.0 copy-done.4
  17.6 0.0 copy-done.5
  17.6 2.2 %shard_map.90 = (f32[8,2,128,128]{3,2,1,0:T(8,128)S(1)}, f32[8,2,128,128]{3,2,1,0:T(8,128)S(1)}) custom-call(s32[1,8]{1,0:T(1,128)S(1)} %copy-done.4, s32[1,8]{1,0:T(1,128)S(1)} %copy-done.5, f32[2,2,256,256]{3,2,1,0:T(8,128)S(1)} %copy-done, f32[256,128]{1,0:T(8,128)S(1)} %collective-permute-done.4.colb_ref, ...), custom_call_target="tpu_custom_call" | custom-call | tf_op jit(solution)/shard_map/pallas_call | solution.py:376
  19.9 0.0 collective-permute-done.2.rowb_ref
  19.9 2.5 %collective-permute-done.3.rowa_ref = f32[6,64,128]{2,1,0:T(8,128)S(1)} collective-permute-done((f32[6,64,128]{2,1,0:T(8,128)S(1)}, f32[6,64,128]{2,1,0:T(8,128)S(1)}, u32[]{:S(2)}, u32[]{:S(2)}) %collective-permute-start.3) | collective-permute-done | bytes 196640 | tf_op jit(solution)/shard_map/ppermute | solution.py:359
  22.3 0.0 copy-done.3
  22.3 5.8 %shard_map.91 = (f32[8,2,128,128]{3,2,1,0:T(8,128)S(1)}, f32[8,2,128,128]{3,2,1,0:T(8,128)S(1)}, f32[128,128]{1,0:T(8,128)S(1)}, f32[128,128]{1,0:T(8,128)S(1)}) custom-call(s32[1,8]{1,0:T(1,128)S(1)} %copy-done.4, s32[1,8]{1,0:T(1,128)S(1)} %copy-done.5, s32[1,1]{1,0:T(1,128)S(6)} %copy.9.live_ref, f32[2,2,256,256]{3,2,1,0:T(8,128)S(1)} %copy-done, ...), custom_call_target="tpu_custom_call" | custom-call | tf_op jit(solution)/shard_map/pallas_call | solution.py:376
  28.2 0.5 collective-permute-start.8
  28.7 0.9 %collective-permute-done.8 = f32[128,128]{1,0:T(8,128)S(1)} collective-permute-done((f32[128,128]{1,0:T(8,128)S(1)}, f32[128,128]{1,0:T(8,128)S(1)}, u32[]{:S(2)}, u32[]{:S(2)}) %collective-permute-start.8) | collective-permute-done | bytes 65568 | tf_op jit(solution)/shard_map/ppermute | solution.py:372
  29.6 4.5 %collective-permute-start.9 = (f32[128,128]{1,0:T(8,128)S(1)}, f32[128,128]{1,0:T(8,128)S(1)}, u32[]{:S(2)}, u32[]{:S(2)}) collective-permute-start(f32[128,128]{1,0:T(8,128)S(1)} %add.27), channel_id=1, source_target_pairs={{0,16},{1,33},{2,18},{3,35},{4,20},{5,37},{6,22},{7,39},{8,24},{9,... | collective-permute-start | bytes 196616 | tf_op jit(solution)/shard_map/ppermute | solution.py:372
  34.1 2.3 %shard_map.92 = (f32[2,2,256,256]{3,2,1,0:T(8,128)S(1)}, f32[2,6,64,128]{3,2,1,0:T(8,128)S(1)}, f32[2,6,64,128]{3,2,1,0:T(8,128)S(1)}, f32[2,256,128]{2,1,0:T(8,128)S(1)}, f32[2,256,128]{2,1,0:T(8,128)S(1)}) custom-call(s32[1,8]{1,0:T(1,128)S(1)} %copy-done.4, s32[1,8]{1,0:T(1,128)S(1)} %copy-done.5, f32[2,2,256,256]{3,2,1,0:T(8,128)S(1)} %copy-done, ...), custom_call_target="tpu_custom_call" | custom-call | tf_op jit(solution)/shard_map/pallas_call | solution.py:376
  36.4 0.0 collective-permute-done.9
  36.4 4.1 %collective-permute-start.10 = (f32[128,128]{1,0:T(8,128)S(1)}, f32[128,128]{1,0:T(8,128)S(1)}, u32[]{:S(2)}, u32[]{:S(2)}) collective-permute-start(f32[128,128]{1,0:T(8,128)S(1)} %add.28), channel_id=1, source_target_pairs={{0,4},{1,13},{2,6},{3,15},{4,0},{5,9},{6,2},{7,11},{8,12},{9,5},{1... | collective-permute-start | bytes 196616 | tf_op jit(solution)/shard_map/ppermute | solution.py:372
  40.5 0.0 collective-permute-start.16
  40.5 1.7 %collective-permute-done.10 = f32[128,128]{1,0:T(8,128)S(1)} collective-permute-done((f32[128,128]{1,0:T(8,128)S(1)}, f32[128,128]{1,0:T(8,128)S(1)}, u32[]{:S(2)}, u32[]{:S(2)}) %collective-permute-start.10) | collective-permute-done | bytes 65568 | tf_op jit(solution)/shard_map/ppermute | solution.py:372
  42.2 1.5 %collective-permute-start.15 = (f32[2,6,64,128]{3,2,1,0:T(8,128)S(1)}, f32[2,6,64,128]{3,2,1,0:T(8,128)S(1)}, u32[]{:S(2)}, u32[]{:S(2)}) collective-permute-start(f32[2,6,64,128]{3,2,1,0:T(8,128)S(1)} %get-tuple-element.57), channel_id=1, source_target_pairs={{0,16},{1,17},{2,18},{3,19},{4,20},{5,21},{6,22},{7,23},{8,24},{9,... | collective-permute-start | bytes 1179656 | tf_op jit(solution)/shard_map/ppermute | solution.py:359
  43.7 0.4 collective-permute-start.11
  44.1 3.0 %collective-permute-done.11 = f32[128,128]{1,0:T(8,128)S(1)} collective-permute-done((f32[128,128]{1,0:T(8,128)S(1)}, f32[128,128]{1,0:T(8,128)S(1)}, u32[]{:S(2)}, u32[]{:S(2)}) %collective-permute-start.11) | collective-permute-done | bytes 65568 | tf_op jit(solution)/shard_map/ppermute | solution.py:372
  47.1 1.4 %collective-permute-start.14 = (f32[128,128]{1,0:T(8,128)S(1)}, f32[128,128]{1,0:T(8,128)S(1)}, u32[]{:S(2)}, u32[]{:S(2)}) collective-permute-start(f32[128,128]{1,0:T(8,128)S(1)} %add.30), channel_id=1, source_target_pairs={{0,2},{1,3},{2,0},{3,1},{4,6},{5,7},{6,4},{7,5},{8,10},{9,11},{10,... | collective-permute-start | bytes 196616 | tf_op jit(solution)/shard_map/ppermute | solution.py:372
  48.6 0.8 %collective-permute-start.13 = (f32[128,128]{1,0:T(8,128)S(1)}, f32[128,128]{1,0:T(8,128)S(1)}, u32[]{:S(2)}, u32[]{:S(2)}) collective-permute-start(f32[128,128]{1,0:T(8,128)S(1)} %add.30), channel_id=1, source_target_pairs={{0,130},{1,129},{2,128},{3,131},{4,134},{5,133},{6,132},{7,135},{8... | collective-permute-start | bytes 196616 | tf_op jit(solution)/shard_map/ppermute | solution.py:372
  49.4 2.2 %collective-permute-start.12 = (f32[128,128]{1,0:T(8,128)S(1)}, f32[128,128]{1,0:T(8,128)S(1)}, u32[]{:S(2)}, u32[]{:S(2)}) collective-permute-start(f32[128,128]{1,0:T(8,128)S(1)} %add.30), channel_id=1, source_target_pairs={{0,128},{1,131},{2,130},{3,129},{4,132},{5,135},{6,134},{7,133},{8... | collective-permute-start | bytes 196616 | tf_op jit(solution)/shard_map/ppermute | solution.py:372
  51.6 4.3 %collective-permute-done.14 = f32[128,128]{1,0:T(8,128)S(1)} collective-permute-done((f32[128,128]{1,0:T(8,128)S(1)}, f32[128,128]{1,0:T(8,128)S(1)}, u32[]{:S(2)}, u32[]{:S(2)}) %collective-permute-start.14) | collective-permute-done | bytes 65568 | tf_op jit(solution)/shard_map/ppermute | solution.py:372
  55.8 1.4 %collective-permute-done.13 = f32[128,128]{1,0:T(8,128)S(1)} collective-permute-done((f32[128,128]{1,0:T(8,128)S(1)}, f32[128,128]{1,0:T(8,128)S(1)}, u32[]{:S(2)}, u32[]{:S(2)}) %collective-permute-start.13) | collective-permute-done | bytes 65568 | tf_op jit(solution)/shard_map/ppermute | solution.py:372
  57.2 0.0 collective-permute-done.12
  57.3 0.0 collective-permute-done.16.rowb_ref
  57.3 0.0 collective-permute-done.15.rowa_ref
  57.3 0.1 shard_map.93
  57.4 0.4 collective-permute-start.17
  57.7 3.7 %collective-permute-start.19 = (f32[2,256,128]{2,1,0:T(8,128)S(1)}, f32[2,256,128]{2,1,0:T(8,128)S(1)}, u32[]{:S(2)}, u32[]{:S(2)}) collective-permute-start(f32[2,256,128]{2,1,0:T(8,128)S(1)} %get-tuple-element.69), channel_id=1, source_target_pairs={{0,16},{1,2},{2,1},{3,4},{4,3},{5,6},{6,5},{7,8},{8,7},{9,10},{10,... | collective-permute-start | bytes 786440 | tf_op jit(solution)/shard_map/ppermute | solution.py:359
  61.4 1.4 %collective-permute-done.17 = f32[128,128]{1,0:T(8,128)S(1)} collective-permute-done((f32[128,128]{1,0:T(8,128)S(1)}, f32[128,128]{1,0:T(8,128)S(1)}, u32[]{:S(2)}, u32[]{:S(2)}) %collective-permute-start.17) | collective-permute-done | bytes 65568 | tf_op jit(solution)/shard_map/ppermute | solution.py:372
  62.8 1.7 %collective-permute-start.20 = (f32[2,256,128]{2,1,0:T(8,128)S(1)}, f32[2,256,128]{2,1,0:T(8,128)S(1)}, u32[]{:S(2)}, u32[]{:S(2)}) collective-permute-start(f32[2,256,128]{2,1,0:T(8,128)S(1)} %get-tuple-element.70), channel_id=1, source_target_pairs={{0,1},{1,0},{2,3},{3,2},{4,5},{5,4},{6,7},{7,6},{8,9},{9,8},{10,11... | collective-permute-start | bytes 786440 | tf_op jit(solution)/shard_map/ppermute | solution.py:359
  64.5 1.5 %collective-permute-start.18 = (f32[128,128]{1,0:T(8,128)S(1)}, f32[128,128]{1,0:T(8,128)S(1)}, u32[]{:S(2)}, u32[]{:S(2)}) collective-permute-start(f32[128,128]{1,0:T(8,128)S(1)} %add.34), channel_id=1, source_target_pairs={{0,96},{1,17},{2,98},{3,19},{4,100},{5,21},{6,102},{7,23},{8,104},... | collective-permute-start | bytes 196616 | tf_op jit(solution)/shard_map/ppermute | solution.py:372
  66.1 1.7 %collective-permute-done.18 = f32[128,128]{1,0:T(8,128)S(1)} collective-permute-done((f32[128,128]{1,0:T(8,128)S(1)}, f32[128,128]{1,0:T(8,128)S(1)}, u32[]{:S(2)}, u32[]{:S(2)}) %collective-permute-start.18) | collective-permute-done | bytes 65568 | tf_op jit(solution)/shard_map/ppermute | solution.py:372
  67.7 0.0 collective-permute-done.19.colb_ref
  67.8 0.0 collective-permute-done.20.cola_ref
  67.8 3.6 %collective-permute-start.21 = (f32[128,128]{1,0:T(8,128)S(1)}, f32[128,128]{1,0:T(8,128)S(1)}, u32[]{:S(2)}, u32[]{:S(2)}) collective-permute-start(f32[128,128]{1,0:T(8,128)S(1)} %add.35.mine_ref), channel_id=1, source_target_pairs={{0,1},{1,0},{2,3},{3,2},{4,5},{5,4},{6,7},{7,6},{8,9},{9,8},{10,11... | collective-permute-start | bytes 196616 | tf_op jit(solution)/shard_map/ppermute | solution.py:372
  71.4 1.2 %shard_map.94 = f32[2,2,256,256]{3,2,1,0:T(8,128)} custom-call(f32[2,2,256,256]{3,2,1,0:T(8,128)S(1)} %get-tuple-element.50.part_ref, f32[2,6,64,128]{3,2,1,0:T(8,128)S(1)} %collective-permute-done.15.rowa_ref, f32[2,6,64,128]{3,2,1,0:T(8,128)S(1)} %collective-permute-done.16.rowb_ref, f32[2,256,128]{2,1,0:T(8,128)S(1)} %collective-permute-done.19.colb_ref, ...), custom_call_target="tpu_custom_call" | custom-call | tf_op jit(solution)/shard_map/pallas_call | solution.py:376
  72.6 0.0 collective-permute-done.21.other_ref
  72.6 0.7 shard_map.95
  (9 shorter events, 0.2 us)
Async XLA Ops:
  0.6 9.4 %copy-start = (f32[2,2,256,256]{3,2,1,0:T(8,128)S(1)}, f32[2,2,256,256]{3,2,1,0:T(8,128)}, u32[]{:S(2)}) copy-start(f32[2,2,256,256]{3,2,1,0:T(8,128)} %obj_ref.13) | copy-start | bytes 3145732
  1.9 8.1 %collective-permute-start.4 = (f32[256,128]{1,0:T(8,128)S(1)}, f32[256,128]{1,0:T(8,128)S(1)}, u32[]{:S(2)}, u32[]{:S(2)}) collective-permute-start(f32[256,128]{1,0:T(8,128)S(1)} %get-tuple-element.42), channel_id=1, source_target_pairs={{0,16},{1,2},{2,1},{3,4},{4,3},{5,6},{6,5},{7,8},{8,7},{9,10},{10,... | collective-permute-start | bytes 393224 | tf_op jit(solution)/shard_map/ppermute | solution.py:359
  6.3 3.7 %collective-permute-start.5 = (f32[256,128]{1,0:T(8,128)S(1)}, f32[256,128]{1,0:T(8,128)S(1)}, u32[]{:S(2)}, u32[]{:S(2)}) collective-permute-start(f32[256,128]{1,0:T(8,128)S(1)} %get-tuple-element.43), channel_id=1, source_target_pairs={{0,1},{1,0},{2,3},{3,2},{4,5},{5,4},{6,7},{7,6},{8,9},{9,8},{10,11... | collective-permute-start | bytes 393224 | tf_op jit(solution)/shard_map/ppermute | solution.py:359
  7.5 6.0 %collective-permute-start = (f32[256,128]{1,0:T(8,128)S(1)}, f32[256,128]{1,0:T(8,128)S(1)}, u32[]{:S(2)}, u32[]{:S(2)}) collective-permute-start(f32[256,128]{1,0:T(8,128)S(1)} %get-tuple-element.38), channel_id=1, source_target_pairs={{0,16},{1,2},{2,1},{3,4},{4,3},{5,6},{6,5},{7,8},{8,7},{9,10},{10,... | collective-permute-start | bytes 393224 | tf_op jit(solution)/shard_map/ppermute | solution.py:359
  9.0 8.6 %copy-start.1 = (bf16[4,2,256,256]{3,2,1,0:T(8,128)(2,1)S(1)}, bf16[4,2,256,256]{3,2,1,0:T(8,128)(2,1)}, u32[]{:S(2)}) copy-start(bf16[4,2,256,256]{3,2,1,0:T(8,128)(2,1)} %constant.2.clone.tabs_ref) | copy-start | bytes 3145732
  9.0 4.5 %collective-permute-start.1 = (f32[256,128]{1,0:T(8,128)S(1)}, f32[256,128]{1,0:T(8,128)S(1)}, u32[]{:S(2)}, u32[]{:S(2)}) collective-permute-start(f32[256,128]{1,0:T(8,128)S(1)} %get-tuple-element.39), channel_id=1, source_target_pairs={{0,1},{1,0},{2,3},{3,2},{4,5},{5,4},{6,7},{7,6},{8,9},{9,8},{10,11... | collective-permute-start | bytes 393224 | tf_op jit(solution)/shard_map/ppermute | solution.py:359
  10.1 7.5 %collective-permute-start.6 = (f32[6,64,128]{2,1,0:T(8,128)S(1)}, f32[6,64,128]{2,1,0:T(8,128)S(1)}, u32[]{:S(2)}, u32[]{:S(2)}) collective-permute-start(f32[6,64,128]{2,1,0:T(8,128)S(1)} %get-tuple-element.44), channel_id=1, source_target_pairs={{0,16},{1,17},{2,18},{3,19},{4,20},{5,21},{6,22},{7,23},{8,24},{9,... | collective-permute-start | bytes 589832 | tf_op jit(solution)/shard_map/ppermute | solution.py:359
  11.4 6.2 %copy-start.2 = (f32[2,128,128]{2,1,0:T(8,128)S(1)}, f32[2,128,128]{2,1,0:T(8,128)}, u32[]{:S(2)}) copy-start(f32[2,128,128]{2,1,0:T(8,128)} %probe_ref.5) | copy-start | bytes 393220
  11.4 6.2 %collective-permute-start.7 = (f32[6,64,128]{2,1,0:T(8,128)S(1)}, f32[6,64,128]{2,1,0:T(8,128)S(1)}, u32[]{:S(2)}, u32[]{:S(2)}) collective-permute-start(f32[6,64,128]{2,1,0:T(8,128)S(1)} %get-tuple-element.45), channel_id=1, source_target_pairs={{0,1},{1,0},{2,3},{3,2},{4,5},{5,4},{6,7},{7,6},{8,9},{9,8},{10,11... | collective-permute-start | bytes 589832 | tf_op jit(solution)/shard_map/ppermute | solution.py:359
  13.5 6.3 %collective-permute-start.2 = (f32[6,64,128]{2,1,0:T(8,128)S(1)}, f32[6,64,128]{2,1,0:T(8,128)S(1)}, u32[]{:S(2)}, u32[]{:S(2)}) collective-permute-start(f32[6,64,128]{2,1,0:T(8,128)S(1)} %get-tuple-element.40), channel_id=1, source_target_pairs={{0,1},{1,0},{2,3},{3,2},{4,5},{5,4},{6,7},{7,6},{8,9},{9,8},{10,11... | collective-permute-start | bytes 589832 | tf_op jit(solution)/shard_map/ppermute | solution.py:359
  13.6 4.0 %copy-start.4 = (s32[1,8]{1,0:T(1,128)S(1)}, s32[1,8]{1,0:T(1,128)}, u32[]{:S(2)}) copy-start(s32[1,8]{1,0:T(1,128)} %row_ref.5) | copy-start | bytes 100
  13.7 4.0 %copy-start.5 = (s32[1,8]{1,0:T(1,128)S(1)}, s32[1,8]{1,0:T(1,128)}, u32[]{:S(2)}) copy-start(s32[1,8]{1,0:T(1,128)} %col_ref.5) | copy-start | bytes 100
  13.7 8.7 %collective-permute-start.3 = (f32[6,64,128]{2,1,0:T(8,128)S(1)}, f32[6,64,128]{2,1,0:T(8,128)S(1)}, u32[]{:S(2)}, u32[]{:S(2)}) collective-permute-start(f32[6,64,128]{2,1,0:T(8,128)S(1)} %get-tuple-element.41), channel_id=1, source_target_pairs={{0,16},{1,17},{2,18},{3,19},{4,20},{5,21},{6,22},{7,23},{8,24},{9,... | collective-permute-start | bytes 589832 | tf_op jit(solution)/shard_map/ppermute | solution.py:359
  17.6 4.8 %copy-start.3 = (f32[1,8,128,128]{3,2,1,0:T(8,128)S(1)}, f32[1,8,128,128]{3,2,1,0:T(8,128)}, u32[]{:S(2)}) copy-start(f32[1,8,128,128]{3,2,1,0:T(8,128)} %param.9) | copy-start | bytes 1572868
  28.2 1.4 %collective-permute-start.8 = (f32[128,128]{1,0:T(8,128)S(1)}, f32[128,128]{1,0:T(8,128)S(1)}, u32[]{:S(2)}, u32[]{:S(2)}) collective-permute-start(f32[128,128]{1,0:T(8,128)S(1)} %get-tuple-element.52), channel_id=1, source_target_pairs={{0,1},{1,0},{2,3},{3,2},{4,5},{5,4},{6,7},{7,6},{8,9},{9,8},{10,11... | collective-permute-start | bytes 196616 | tf_op jit(solution)/shard_map/ppermute | solution.py:372
  29.6 6.8 %collective-permute-start.9 = (f32[128,128]{1,0:T(8,128)S(1)}, f32[128,128]{1,0:T(8,128)S(1)}, u32[]{:S(2)}, u32[]{:S(2)}) collective-permute-start(f32[128,128]{1,0:T(8,128)S(1)} %add.27), channel_id=1, source_target_pairs={{0,16},{1,33},{2,18},{3,35},{4,20},{5,37},{6,22},{7,39},{8,24},{9,... | collective-permute-start | bytes 196616 | tf_op jit(solution)/shard_map/ppermute | solution.py:372
  36.4 5.7 %collective-permute-start.10 = (f32[128,128]{1,0:T(8,128)S(1)}, f32[128,128]{1,0:T(8,128)S(1)}, u32[]{:S(2)}, u32[]{:S(2)}) collective-permute-start(f32[128,128]{1,0:T(8,128)S(1)} %add.28), channel_id=1, source_target_pairs={{0,4},{1,13},{2,6},{3,15},{4,0},{5,9},{6,2},{7,11},{8,12},{9,5},{1... | collective-permute-start | bytes 196616 | tf_op jit(solution)/shard_map/ppermute | solution.py:372
  40.5 16.8 %collective-permute-start.16 = (f32[2,6,64,128]{3,2,1,0:T(8,128)S(1)}, f32[2,6,64,128]{3,2,1,0:T(8,128)S(1)}, u32[]{:S(2)}, u32[]{:S(2)}) collective-permute-start(f32[2,6,64,128]{3,2,1,0:T(8,128)S(1)} %get-tuple-element.58), channel_id=1, source_target_pairs={{0,1},{1,0},{2,3},{3,2},{4,5},{5,4},{6,7},{7,6},{8,9},{9,8},{10,11... | collective-permute-start | bytes 1179656 | tf_op jit(solution)/shard_map/ppermute | solution.py:359
  42.2 15.1 %collective-permute-start.15 = (f32[2,6,64,128]{3,2,1,0:T(8,128)S(1)}, f32[2,6,64,128]{3,2,1,0:T(8,128)S(1)}, u32[]{:S(2)}, u32[]{:S(2)}) collective-permute-start(f32[2,6,64,128]{3,2,1,0:T(8,128)S(1)} %get-tuple-element.57), channel_id=1, source_target_pairs={{0,16},{1,17},{2,18},{3,19},{4,20},{5,21},{6,22},{7,23},{8,24},{9,... | collective-permute-start | bytes 1179656 | tf_op jit(solution)/shard_map/ppermute | solution.py:359
  43.7 3.4 %collective-permute-start.11 = (f32[128,128]{1,0:T(8,128)S(1)}, f32[128,128]{1,0:T(8,128)S(1)}, u32[]{:S(2)}, u32[]{:S(2)}) collective-permute-start(f32[128,128]{1,0:T(8,128)S(1)} %add.29), channel_id=1, source_target_pairs={{0,12},{1,5},{2,14},{3,7},{4,8},{5,1},{6,10},{7,3},{8,4},{9,13},{1... | collective-permute-start | bytes 196616 | tf_op jit(solution)/shard_map/ppermute | solution.py:372
  47.1 8.7 %collective-permute-start.14 = (f32[128,128]{1,0:T(8,128)S(1)}, f32[128,128]{1,0:T(8,128)S(1)}, u32[]{:S(2)}, u32[]{:S(2)}) collective-permute-start(f32[128,128]{1,0:T(8,128)S(1)} %add.30), channel_id=1, source_target_pairs={{0,2},{1,3},{2,0},{3,1},{4,6},{5,7},{6,4},{7,5},{8,10},{9,11},{10,... | collective-permute-start | bytes 196616 | tf_op jit(solution)/shard_map/ppermute | solution.py:372
  48.6 8.7 %collective-permute-start.13 = (f32[128,128]{1,0:T(8,128)S(1)}, f32[128,128]{1,0:T(8,128)S(1)}, u32[]{:S(2)}, u32[]{:S(2)}) collective-permute-start(f32[128,128]{1,0:T(8,128)S(1)} %add.30), channel_id=1, source_target_pairs={{0,130},{1,129},{2,128},{3,131},{4,134},{5,133},{6,132},{7,135},{8... | collective-permute-start | bytes 196616 | tf_op jit(solution)/shard_map/ppermute | solution.py:372
  49.4 7.9 %collective-permute-start.12 = (f32[128,128]{1,0:T(8,128)S(1)}, f32[128,128]{1,0:T(8,128)S(1)}, u32[]{:S(2)}, u32[]{:S(2)}) collective-permute-start(f32[128,128]{1,0:T(8,128)S(1)} %add.30), channel_id=1, source_target_pairs={{0,128},{1,131},{2,130},{3,129},{4,132},{5,135},{6,134},{7,133},{8... | collective-permute-start | bytes 196616 | tf_op jit(solution)/shard_map/ppermute | solution.py:372
  57.4 5.4 %collective-permute-start.17 = (f32[128,128]{1,0:T(8,128)S(1)}, f32[128,128]{1,0:T(8,128)S(1)}, u32[]{:S(2)}, u32[]{:S(2)}) collective-permute-start(f32[128,128]{1,0:T(8,128)S(1)} %add_add_fusion), channel_id=1, source_target_pairs={{0,32},{1,97},{2,34},{3,99},{4,36},{5,101},{6,38},{7,103},{8,40},{... | collective-permute-start | bytes 196616 | tf_op jit(solution)/shard_map/ppermute | solution.py:372
  57.7 10.0 %collective-permute-start.19 = (f32[2,256,128]{2,1,0:T(8,128)S(1)}, f32[2,256,128]{2,1,0:T(8,128)S(1)}, u32[]{:S(2)}, u32[]{:S(2)}) collective-permute-start(f32[2,256,128]{2,1,0:T(8,128)S(1)} %get-tuple-element.69), channel_id=1, source_target_pairs={{0,16},{1,2},{2,1},{3,4},{4,3},{5,6},{6,5},{7,8},{8,7},{9,10},{10,... | collective-permute-start | bytes 786440 | tf_op jit(solution)/shard_map/ppermute | solution.py:359
  62.8 5.0 %collective-permute-start.20 = (f32[2,256,128]{2,1,0:T(8,128)S(1)}, f32[2,256,128]{2,1,0:T(8,128)S(1)}, u32[]{:S(2)}, u32[]{:S(2)}) collective-permute-start(f32[2,256,128]{2,1,0:T(8,128)S(1)} %get-tuple-element.70), channel_id=1, source_target_pairs={{0,1},{1,0},{2,3},{3,2},{4,5},{5,4},{6,7},{7,6},{8,9},{9,8},{10,11... | collective-permute-start | bytes 786440 | tf_op jit(solution)/shard_map/ppermute | solution.py:359
  64.5 3.2 %collective-permute-start.18 = (f32[128,128]{1,0:T(8,128)S(1)}, f32[128,128]{1,0:T(8,128)S(1)}, u32[]{:S(2)}, u32[]{:S(2)}) collective-permute-start(f32[128,128]{1,0:T(8,128)S(1)} %add.34), channel_id=1, source_target_pairs={{0,96},{1,17},{2,98},{3,19},{4,100},{5,21},{6,102},{7,23},{8,104},... | collective-permute-start | bytes 196616 | tf_op jit(solution)/shard_map/ppermute | solution.py:372
  67.8 4.9 %collective-permute-start.21 = (f32[128,128]{1,0:T(8,128)S(1)}, f32[128,128]{1,0:T(8,128)S(1)}, u32[]{:S(2)}, u32[]{:S(2)}) collective-permute-start(f32[128,128]{1,0:T(8,128)S(1)} %add.35.mine_ref), channel_id=1, source_target_pairs={{0,1},{1,0},{2,3},{3,2},{4,5},{5,4},{6,7},{7,6},{8,9},{9,8},{10,11... | collective-permute-start | bytes 196616 | tf_op jit(solution)/shard_map/ppermute | solution.py:372

commit v20 on v19

--- a/solution.py
+++ b/solution.py
@@ -185,7 +185,7 @@
 
 
 def second_kernel(
-    row_ref, col_ref, live_ref, obj_ref, colb_ref, cola_ref, rowb_ref, rowa_ref,
+    row_ref, col_ref, live_ref, obj_ref, colb_ref, cola_ref, rowa_ref, rowb_ref,
     win_ref, mid_ref, measured_ref, tabs_ref,
     grad_ref, down_ref, keep_ref, send_ref,
     ext, sum_ref, *, group,
@@ -406,14 +406,13 @@
             (), (object_field, *cols[piece]),
         )
         halos.append((*cols[piece], *meet_rows(strips)))
-    *sides, even, odd = halos[1]
     win, mid = call(
         functools.partial(first_kernel, group=2), [fields] * 2, (offset_row, offset_col),
         (object_field, *halos[0], probe, tabs), (grown,),
     )
     grad, down, mine, send = call(
         functools.partial(second_kernel, group=count), [fields] * 2 + [array(*plane)] * 2, (offset_row, offset_col, live),
-        (object_field, *sides, odd, even, win, mid, intensity[0], tabs),
+        (object_field, *halos[1], win, mid, intensity[0], tabs),
         (grown, pltpu.VMEM((2, *plane), jnp.float32)),
     )
     part, *strips, left, right = call(

time: 73.4 us -> 73.9 us (level)
  starting transfers between devices: 38.1 us -> 42 us
  waiting for transfers between devices: 18.7 us -> 15.3 us
    ppermute x10, waiting for transfers between devices: 14.3 us -> 11 us  [swap(): lax.ppermute(value, BOTH, [(i, i ^ masks[i % 2]) for i in range(count)])]
    ppermute x10, starting transfers between devices: 19.5 us -> 22.3 us  [swap(): lax.ppermute(value, BOTH, [(i, i ^ masks[i % 2]) for i in range(count)])]
    ppermute x12, starting transfers between devices: 18.7 us -> 19.7 us  [meet(): return lax.ppermute(strip, BOTH, pairs)]
  transfers between devices with their start and end apart: 22 -> 22, of which waited for: 9 -> 8; matrix products, arithmetic and copies ran while one was open for 0% -> 0% of each run, Pallas kernels for 10% -> 10%
where the time goes in v20:
time: 73.9 us; the launch traced here: 73.7 us
  starting transfers between devices  42 us (57%)
  waiting for transfers between devices  15.3 us (21%)
  Pallas kernels  14.9 us (20%)
  between operations  1.48 us (2%)
    ppermute x10, starting transfers between devices, swap(): lax.ppermute(value, BOTH, [(i, i ^ masks[i % 2]) for i in range(count)])  22.3 us
    ppermute x12, starting transfers between devices, meet(): return lax.ppermute(strip, BOTH, pairs)  19.7 us
    pallas_call x8, Pallas kernels, call(): pl.pallas_call(kernel, out_shape=tuple(out_shape), in_specs=smem(len(scal...  12.4 us
    ppermute x10, waiting for transfers between devices, swap(): lax.ppermute(value, BOTH, [(i, i ^ masks[i % 2]) for i in range(count)])  11 us
    ppermute x12, waiting for transfers between devices, meet(): return lax.ppermute(strip, BOTH, pairs)  4.29 us
    pallas_call x2, Pallas kernels, on_device(): pl.pallas_call(functools.partial(pack_kernel, piece=piece), out_shape=tup...  2.46 us
  transfers between devices with their start and end apart: 22, of which 8 were waited for; matrix products, arithmetic and copies ran while one was open for 0% of the time, Pallas kernels for 10%

profile of v20, /device:TPU:1, one launch (start us, length us, event | category | flops | bytes accessed | tf_op | source)
XLA Modules:
  0.0 73.7 jit_solution(15167880651473607318)
XLA Ops:
  0.6 0.0 copy-start
  0.6 1.3 %shard_map.88 = (f32[256,128]{1,0:T(8,128)S(1)}, f32[256,128]{1,0:T(8,128)S(1)}) custom-call(f32[2,2,256,256]{3,2,1,0:T(8,128)} %obj_ref.13), custom_call_target="tpu_custom_call" | custom-call | tf_op jit(solution)/shard_map/pallas_call | solution.py:393
  1.9 4.4 %collective-permute-start.4 = (f32[256,128]{1,0:T(8,128)S(1)}, f32[256,128]{1,0:T(8,128)S(1)}, u32[]{:S(2)}, u32[]{:S(2)}) collective-permute-start(f32[256,128]{1,0:T(8,128)S(1)} %get-tuple-element.42), channel_id=1, source_target_pairs={{0,16},{1,2},{2,1},{3,4},{4,3},{5,6},{6,5},{7,8},{8,7},{9,10},{10,... | collective-permute-start | bytes 393224 | tf_op jit(solution)/shard_map/ppermute | solution.py:359
  6.3 0.0 collective-permute-start.5
  6.3 1.2 %shard_map.86 = (f32[256,128]{1,0:T(8,128)S(1)}, f32[256,128]{1,0:T(8,128)S(1)}) custom-call(f32[2,2,256,256]{3,2,1,0:T(8,128)} %obj_ref.13), custom_call_target="tpu_custom_call" | custom-call | tf_op jit(solution)/shard_map/pallas_call | solution.py:393
  7.5 1.5 %collective-permute-start = (f32[256,128]{1,0:T(8,128)S(1)}, f32[256,128]{1,0:T(8,128)S(1)}, u32[]{:S(2)}, u32[]{:S(2)}) collective-permute-start(f32[256,128]{1,0:T(8,128)S(1)} %get-tuple-element.38), channel_id=1, source_target_pairs={{0,16},{1,2},{2,1},{3,4},{4,3},{5,6},{6,5},{7,8},{8,7},{9,10},{10,... | collective-permute-start | bytes 393224 | tf_op jit(solution)/shard_map/ppermute | solution.py:359
  9.0 0.0 copy-start.1
  9.0 1.0 %collective-permute-start.1 = (f32[256,128]{1,0:T(8,128)S(1)}, f32[256,128]{1,0:T(8,128)S(1)}, u32[]{:S(2)}, u32[]{:S(2)}) collective-permute-start(f32[256,128]{1,0:T(8,128)S(1)} %get-tuple-element.39), channel_id=1, source_target_pairs={{0,1},{1,0},{2,3},{3,2},{4,5},{5,4},{6,7},{7,6},{8,9},{9,8},{10,11... | collective-permute-start | bytes 393224 | tf_op jit(solution)/shard_map/ppermute | solution.py:359
  10.0 0.0 collective-permute-done.4.colb_ref
  10.0 0.0 collective-permute-done.5.cola_ref
  10.0 0.0 copy-done
  10.1 1.3 %collective-permute-start.6 = (f32[6,64,128]{2,1,0:T(8,128)S(1)}, f32[6,64,128]{2,1,0:T(8,128)S(1)}, u32[]{:S(2)}, u32[]{:S(2)}) collective-permute-start(f32[6,64,128]{2,1,0:T(8,128)S(1)} %get-tuple-element.44), channel_id=1, source_target_pairs={{0,16},{1,17},{2,18},{3,19},{4,20},{5,21},{6,22},{7,23},{8,24},{9,... | collective-permute-start | bytes 589832 | tf_op jit(solution)/shard_map/ppermute | solution.py:359
  11.4 0.0 copy-start.2
  11.4 0.1 collective-permute-start.7
  11.6 1.9 %collective-permute-done.colb_ref = f32[256,128]{1,0:T(8,128)S(1)} collective-permute-done((f32[256,128]{1,0:T(8,128)S(1)}, f32[256,128]{1,0:T(8,128)S(1)}, u32[]{:S(2)}, u32[]{:S(2)}) %collective-permute-start) | collective-permute-done | bytes 131104 | tf_op jit(solution)/shard_map/ppermute | solution.py:359
  13.5 0.0 collective-permute-done.1.cola_ref
  13.5 1.7 %collective-permute-start.2 = (f32[6,64,128]{2,1,0:T(8,128)S(1)}, f32[6,64,128]{2,1,0:T(8,128)S(1)}, u32[]{:S(2)}, u32[]{:S(2)}) collective-permute-start(f32[6,64,128]{2,1,0:T(8,128)S(1)} %get-tuple-element.40), channel_id=1, source_target_pairs={{0,16},{1,17},{2,18},{3,19},{4,20},{5,21},{6,22},{7,23},{8,24},{9,... | collective-permute-start | bytes 589832 | tf_op jit(solution)/shard_map/ppermute | solution.py:359
  15.3 0.0 copy-start.4
  15.3 0.0 copy-start.5
  15.3 0.3 collective-permute-start.3
  16.2 0.0 copy-start.3
  16.2 0.3 collective-permute-done.6.rowa_ref
  16.5 0.0 collective-permute-done.7.rowb_ref
  16.5 0.0 copy-done.1
  16.5 0.0 copy-done.2
  16.5 0.0 copy-done.4
  16.5 0.0 copy-done.5
  16.5 2.2 %shard_map.90 = (f32[8,2,128,128]{3,2,1,0:T(8,128)S(1)}, f32[8,2,128,128]{3,2,1,0:T(8,128)S(1)}) custom-call(s32[1,8]{1,0:T(1,128)S(1)} %copy-done.4, s32[1,8]{1,0:T(1,128)S(1)} %copy-done.5, f32[2,2,256,256]{3,2,1,0:T(8,128)S(1)} %copy-done, f32[256,128]{1,0:T(8,128)S(1)} %collective-permute-done.4.colb_ref, ...), custom_call_target="tpu_custom_call" | custom-call | tf_op jit(solution)/shard_map/pallas_call | solution.py:376
  18.8 2.0 %collective-permute-done.2.rowa_ref = f32[6,64,128]{2,1,0:T(8,128)S(1)} collective-permute-done((f32[6,64,128]{2,1,0:T(8,128)S(1)}, f32[6,64,128]{2,1,0:T(8,128)S(1)}, u32[]{:S(2)}, u32[]{:S(2)}) %collective-permute-start.2) | collective-permute-done | bytes 196640 | tf_op jit(solution)/shard_map/ppermute | solution.py:359
  20.8 0.0 collective-permute-done.3.rowb_ref
  20.8 0.0 copy-done.3
  20.8 5.8 %shard_map.91 = (f32[8,2,128,128]{3,2,1,0:T(8,128)S(1)}, f32[8,2,128,128]{3,2,1,0:T(8,128)S(1)}, f32[128,128]{1,0:T(8,128)S(1)}, f32[128,128]{1,0:T(8,128)S(1)}) custom-call(s32[1,8]{1,0:T(1,128)S(1)} %copy-done.4, s32[1,8]{1,0:T(1,128)S(1)} %copy-done.5, s32[1,1]{1,0:T(1,128)S(6)} %copy.9.live_ref, f32[2,2,256,256]{3,2,1,0:T(8,128)S(1)} %copy-done, ...), custom_call_target="tpu_custom_call" | custom-call | tf_op jit(solution)/shard_map/pallas_call | solution.py:376
  26.6 1.0 %collective-permute-start.8 = (f32[128,128]{1,0:T(8,128)S(1)}, f32[128,128]{1,0:T(8,128)S(1)}, u32[]{:S(2)}, u32[]{:S(2)}) collective-permute-start(f32[128,128]{1,0:T(8,128)S(1)} %get-tuple-element.52), channel_id=1, source_target_pairs={{0,1},{1,0},{2,3},{3,2},{4,5},{5,4},{6,7},{7,6},{8,9},{9,8},{10,11... | collective-permute-start | bytes 196616 | tf_op jit(solution)/shard_map/ppermute | solution.py:372
  27.6 0.9 %collective-permute-done.8 = f32[128,128]{1,0:T(8,128)S(1)} collective-permute-done((f32[128,128]{1,0:T(8,128)S(1)}, f32[128,128]{1,0:T(8,128)S(1)}, u32[]{:S(2)}, u32[]{:S(2)}) %collective-permute-start.8) | collective-permute-done | bytes 65568 | tf_op jit(solution)/shard_map/ppermute | solution.py:372
  28.6 4.5 %collective-permute-start.9 = (f32[128,128]{1,0:T(8,128)S(1)}, f32[128,128]{1,0:T(8,128)S(1)}, u32[]{:S(2)}, u32[]{:S(2)}) collective-permute-start(f32[128,128]{1,0:T(8,128)S(1)} %add.27), channel_id=1, source_target_pairs={{0,16},{1,33},{2,18},{3,35},{4,20},{5,37},{6,22},{7,39},{8,24},{9,... | collective-permute-start | bytes 196616 | tf_op jit(solution)/shard_map/ppermute | solution.py:372
  33.1 2.3 %shard_map.92 = (f32[2,2,256,256]{3,2,1,0:T(8,128)S(1)}, f32[2,6,64,128]{3,2,1,0:T(8,128)S(1)}, f32[2,6,64,128]{3,2,1,0:T(8,128)S(1)}, f32[2,256,128]{2,1,0:T(8,128)S(1)}, f32[2,256,128]{2,1,0:T(8,128)S(1)}) custom-call(s32[1,8]{1,0:T(1,128)S(1)} %copy-done.4, s32[1,8]{1,0:T(1,128)S(1)} %copy-done.5, f32[2,2,256,256]{3,2,1,0:T(8,128)S(1)} %copy-done, ...), custom_call_target="tpu_custom_call" | custom-call | tf_op jit(solution)/shard_map/pallas_call | solution.py:376
  35.4 0.0 collective-permute-done.9
  35.4 3.7 %collective-permute-start.10 = (f32[128,128]{1,0:T(8,128)S(1)}, f32[128,128]{1,0:T(8,128)S(1)}, u32[]{:S(2)}, u32[]{:S(2)}) collective-permute-start(f32[128,128]{1,0:T(8,128)S(1)} %add.28), channel_id=1, source_target_pairs={{0,4},{1,13},{2,6},{3,15},{4,0},{5,9},{6,2},{7,11},{8,12},{9,5},{1... | collective-permute-start | bytes 196616 | tf_op jit(solution)/shard_map/ppermute | solution.py:372
  39.1 0.0 collective-permute-start.16
  39.1 1.7 %collective-permute-done.10 = f32[128,128]{1,0:T(8,128)S(1)} collective-permute-done((f32[128,128]{1,0:T(8,128)S(1)}, f32[128,128]{1,0:T(8,128)S(1)}, u32[]{:S(2)}, u32[]{:S(2)}) %collective-permute-start.10) | collective-permute-done | bytes 65568 | tf_op jit(solution)/shard_map/ppermute | solution.py:372
  40.8 2.2 %collective-permute-start.15 = (f32[2,6,64,128]{3,2,1,0:T(8,128)S(1)}, f32[2,6,64,128]{3,2,1,0:T(8,128)S(1)}, u32[]{:S(2)}, u32[]{:S(2)}) collective-permute-start(f32[2,6,64,128]{3,2,1,0:T(8,128)S(1)} %get-tuple-element.57), channel_id=1, source_target_pairs={{0,16},{1,17},{2,18},{3,19},{4,20},{5,21},{6,22},{7,23},{8,24},{9,... | collective-permute-start | bytes 1179656 | tf_op jit(solution)/shard_map/ppermute | solution.py:359
  43.0 0.4 collective-permute-start.11
  43.4 3.0 %collective-permute-done.11 = f32[128,128]{1,0:T(8,128)S(1)} collective-permute-done((f32[128,128]{1,0:T(8,128)S(1)}, f32[128,128]{1,0:T(8,128)S(1)}, u32[]{:S(2)}, u32[]{:S(2)}) %collective-permute-start.11) | collective-permute-done | bytes 65568 | tf_op jit(solution)/shard_map/ppermute | solution.py:372
  46.4 2.2 %collective-permute-start.14 = (f32[128,128]{1,0:T(8,128)S(1)}, f32[128,128]{1,0:T(8,128)S(1)}, u32[]{:S(2)}, u32[]{:S(2)}) collective-permute-start(f32[128,128]{1,0:T(8,128)S(1)} %add.30), channel_id=1, source_target_pairs={{0,2},{1,3},{2,0},{3,1},{4,6},{5,7},{6,4},{7,5},{8,10},{9,11},{10,... | collective-permute-start | bytes 196616 | tf_op jit(solution)/shard_map/ppermute | solution.py:372
  48.6 1.1 %collective-permute-start.13 = (f32[128,128]{1,0:T(8,128)S(1)}, f32[128,128]{1,0:T(8,128)S(1)}, u32[]{:S(2)}, u32[]{:S(2)}) collective-permute-start(f32[128,128]{1,0:T(8,128)S(1)} %add.30), channel_id=1, source_target_pairs={{0,130},{1,129},{2,128},{3,131},{4,134},{5,133},{6,132},{7,135},{8... | collective-permute-start | bytes 196616 | tf_op jit(solution)/shard_map/ppermute | solution.py:372
  49.7 2.3 %collective-permute-start.12 = (f32[128,128]{1,0:T(8,128)S(1)}, f32[128,128]{1,0:T(8,128)S(1)}, u32[]{:S(2)}, u32[]{:S(2)}) collective-permute-start(f32[128,128]{1,0:T(8,128)S(1)} %add.30), channel_id=1, source_target_pairs={{0,128},{1,131},{2,130},{3,129},{4,132},{5,135},{6,134},{7,133},{8... | collective-permute-start | bytes 196616 | tf_op jit(solution)/shard_map/ppermute | solution.py:372
  52.0 3.8 %collective-permute-done.14 = f32[128,128]{1,0:T(8,128)S(1)} collective-permute-done((f32[128,128]{1,0:T(8,128)S(1)}, f32[128,128]{1,0:T(8,128)S(1)}, u32[]{:S(2)}, u32[]{:S(2)}) %collective-permute-start.14) | collective-permute-done | bytes 65568 | tf_op jit(solution)/shard_map/ppermute | solution.py:372
  55.8 0.0 collective-permute-done.13
  55.8 0.0 collective-permute-done.12
  55.8 0.0 collective-permute-done.16.rowb_ref
  55.8 0.0 collective-permute-done.15.rowa_ref
  55.8 0.1 shard_map.93
  55.9 1.8 %collective-permute-start.17 = (f32[128,128]{1,0:T(8,128)S(1)}, f32[128,128]{1,0:T(8,128)S(1)}, u32[]{:S(2)}, u32[]{:S(2)}) collective-permute-start(f32[128,128]{1,0:T(8,128)S(1)} %add_add_fusion), channel_id=1, source_target_pairs={{0,32},{1,97},{2,34},{3,99},{4,36},{5,101},{6,38},{7,103},{8,40},{... | collective-permute-start | bytes 196616 | tf_op jit(solution)/shard_map/ppermute | solution.py:372
  57.7 3.7 %collective-permute-start.19 = (f32[2,256,128]{2,1,0:T(8,128)S(1)}, f32[2,256,128]{2,1,0:T(8,128)S(1)}, u32[]{:S(2)}, u32[]{:S(2)}) collective-permute-start(f32[2,256,128]{2,1,0:T(8,128)S(1)} %get-tuple-element.69), channel_id=1, source_target_pairs={{0,16},{1,2},{2,1},{3,4},{4,3},{5,6},{6,5},{7,8},{8,7},{9,10},{10,... | collective-permute-start | bytes 786440 | tf_op jit(solution)/shard_map/ppermute | solution.py:359
  61.4 0.0 collective-permute-done.17
  61.4 3.4 %collective-permute-start.20 = (f32[2,256,128]{2,1,0:T(8,128)S(1)}, f32[2,256,128]{2,1,0:T(8,128)S(1)}, u32[]{:S(2)}, u32[]{:S(2)}) collective-permute-start(f32[2,256,128]{2,1,0:T(8,128)S(1)} %get-tuple-element.70), channel_id=1, source_target_pairs={{0,1},{1,0},{2,3},{3,2},{4,5},{5,4},{6,7},{7,6},{8,9},{9,8},{10,11... | collective-permute-start | bytes 786440 | tf_op jit(solution)/shard_map/ppermute | solution.py:359
  64.9 1.5 %collective-permute-start.18 = (f32[128,128]{1,0:T(8,128)S(1)}, f32[128,128]{1,0:T(8,128)S(1)}, u32[]{:S(2)}, u32[]{:S(2)}) collective-permute-start(f32[128,128]{1,0:T(8,128)S(1)} %add.34), channel_id=1, source_target_pairs={{0,96},{1,17},{2,98},{3,19},{4,100},{5,21},{6,102},{7,23},{8,104},... | collective-permute-start | bytes 196616 | tf_op jit(solution)/shard_map/ppermute | solution.py:372
  66.4 1.7 %collective-permute-done.18 = f32[128,128]{1,0:T(8,128)S(1)} collective-permute-done((f32[128,128]{1,0:T(8,128)S(1)}, f32[128,128]{1,0:T(8,128)S(1)}, u32[]{:S(2)}, u32[]{:S(2)}) %collective-permute-start.18) | collective-permute-done | bytes 65568 | tf_op jit(solution)/shard_map/ppermute | solution.py:372
  68.1 0.0 collective-permute-done.19.colb_ref
  68.1 0.0 collective-permute-done.20.cola_ref
  68.1 3.7 %collective-permute-start.21 = (f32[128,128]{1,0:T(8,128)S(1)}, f32[128,128]{1,0:T(8,128)S(1)}, u32[]{:S(2)}, u32[]{:S(2)}) collective-permute-start(f32[128,128]{1,0:T(8,128)S(1)} %add.35.mine_ref), channel_id=1, source_target_pairs={{0,1},{1,0},{2,3},{3,2},{4,5},{5,4},{6,7},{7,6},{8,9},{9,8},{10,11... | collective-permute-start | bytes 196616 | tf_op jit(solution)/shard_map/ppermute | solution.py:372
  71.8 1.2 %shard_map.94 = f32[2,2,256,256]{3,2,1,0:T(8,128)} custom-call(f32[2,2,256,256]{3,2,1,0:T(8,128)S(1)} %get-tuple-element.50.part_ref, f32[2,6,64,128]{3,2,1,0:T(8,128)S(1)} %collective-permute-done.15.rowa_ref, f32[2,6,64,128]{3,2,1,0:T(8,128)S(1)} %collective-permute-done.16.rowb_ref, f32[2,256,128]{2,1,0:T(8,128)S(1)} %collective-permute-done.19.colb_ref, ...), custom_call_target="tpu_custom_call" | custom-call | tf_op jit(solution)/shard_map/pallas_call | solution.py:376
  73.0 0.0 collective-permute-done.21.other_ref
  73.0 0.7 shard_map.95
  (9 shorter events, 0.2 us)
Async XLA Ops:
  0.6 9.4 %copy-start = (f32[2,2,256,256]{3,2,1,0:T(8,128)S(1)}, f32[2,2,256,256]{3,2,1,0:T(8,128)}, u32[]{:S(2)}) copy-start(f32[2,2,256,256]{3,2,1,0:T(8,128)} %obj_ref.13) | copy-start | bytes 3145732
  1.9 8.1 %collective-permute-start.4 = (f32[256,128]{1,0:T(8,128)S(1)}, f32[256,128]{1,0:T(8,128)S(1)}, u32[]{:S(2)}, u32[]{:S(2)}) collective-permute-start(f32[256,128]{1,0:T(8,128)S(1)} %get-tuple-element.42), channel_id=1, source_target_pairs={{0,16},{1,2},{2,1},{3,4},{4,3},{5,6},{6,5},{7,8},{8,7},{9,10},{10,... | collective-permute-start | bytes 393224 | tf_op jit(solution)/shard_map/ppermute | solution.py:359
  6.3 3.7 %collective-permute-start.5 = (f32[256,128]{1,0:T(8,128)S(1)}, f32[256,128]{1,0:T(8,128)S(1)}, u32[]{:S(2)}, u32[]{:S(2)}) collective-permute-start(f32[256,128]{1,0:T(8,128)S(1)} %get-tuple-element.43), channel_id=1, source_target_pairs={{0,1},{1,0},{2,3},{3,2},{4,5},{5,4},{6,7},{7,6},{8,9},{9,8},{10,11... | collective-permute-start | bytes 393224 | tf_op jit(solution)/shard_map/ppermute | solution.py:359
  7.5 6.0 %collective-permute-start = (f32[256,128]{1,0:T(8,128)S(1)}, f32[256,128]{1,0:T(8,128)S(1)}, u32[]{:S(2)}, u32[]{:S(2)}) collective-permute-start(f32[256,128]{1,0:T(8,128)S(1)} %get-tuple-element.38), channel_id=1, source_target_pairs={{0,16},{1,2},{2,1},{3,4},{4,3},{5,6},{6,5},{7,8},{8,7},{9,10},{10,... | collective-permute-start | bytes 393224 | tf_op jit(solution)/shard_map/ppermute | solution.py:359
  9.0 7.5 %copy-start.1 = (bf16[4,2,256,256]{3,2,1,0:T(8,128)(2,1)S(1)}, bf16[4,2,256,256]{3,2,1,0:T(8,128)(2,1)}, u32[]{:S(2)}) copy-start(bf16[4,2,256,256]{3,2,1,0:T(8,128)(2,1)} %constant.2.clone.tabs_ref) | copy-start | bytes 3145732
  9.0 4.5 %collective-permute-start.1 = (f32[256,128]{1,0:T(8,128)S(1)}, f32[256,128]{1,0:T(8,128)S(1)}, u32[]{:S(2)}, u32[]{:S(2)}) collective-permute-start(f32[256,128]{1,0:T(8,128)S(1)} %get-tuple-element.39), channel_id=1, source_target_pairs={{0,1},{1,0},{2,3},{3,2},{4,5},{5,4},{6,7},{7,6},{8,9},{9,8},{10,11... | collective-permute-start | bytes 393224 | tf_op jit(solution)/shard_map/ppermute | solution.py:359
  10.1 6.4 %collective-permute-start.6 = (f32[6,64,128]{2,1,0:T(8,128)S(1)}, f32[6,64,128]{2,1,0:T(8,128)S(1)}, u32[]{:S(2)}, u32[]{:S(2)}) collective-permute-start(f32[6,64,128]{2,1,0:T(8,128)S(1)} %get-tuple-element.44), channel_id=1, source_target_pairs={{0,16},{1,17},{2,18},{3,19},{4,20},{5,21},{6,22},{7,23},{8,24},{9,... | collective-permute-start | bytes 589832 | tf_op jit(solution)/shard_map/ppermute | solution.py:359
  11.4 5.1 %copy-start.2 = (f32[2,128,128]{2,1,0:T(8,128)S(1)}, f32[2,128,128]{2,1,0:T(8,128)}, u32[]{:S(2)}) copy-start(f32[2,128,128]{2,1,0:T(8,128)} %probe_ref.5) | copy-start | bytes 393220
  11.4 5.1 %collective-permute-start.7 = (f32[6,64,128]{2,1,0:T(8,128)S(1)}, f32[6,64,128]{2,1,0:T(8,128)S(1)}, u32[]{:S(2)}, u32[]{:S(2)}) collective-permute-start(f32[6,64,128]{2,1,0:T(8,128)S(1)} %get-tuple-element.45), channel_id=1, source_target_pairs={{0,1},{1,0},{2,3},{3,2},{4,5},{5,4},{6,7},{7,6},{8,9},{9,8},{10,11... | collective-permute-start | bytes 589832 | tf_op jit(solution)/shard_map/ppermute | solution.py:359
  13.5 7.2 %collective-permute-start.2 = (f32[6,64,128]{2,1,0:T(8,128)S(1)}, f32[6,64,128]{2,1,0:T(8,128)S(1)}, u32[]{:S(2)}, u32[]{:S(2)}) collective-permute-start(f32[6,64,128]{2,1,0:T(8,128)S(1)} %get-tuple-element.40), channel_id=1, source_target_pairs={{0,16},{1,17},{2,18},{3,19},{4,20},{5,21},{6,22},{7,23},{8,24},{9,... | collective-permute-start | bytes 589832 | tf_op jit(solution)/shard_map/ppermute | solution.py:359
  15.3 1.2 %copy-start.4 = (s32[1,8]{1,0:T(1,128)S(1)}, s32[1,8]{1,0:T(1,128)}, u32[]{:S(2)}) copy-start(s32[1,8]{1,0:T(1,128)} %row_ref.5) | copy-start | bytes 100
  15.3 1.3 %copy-start.5 = (s32[1,8]{1,0:T(1,128)S(1)}, s32[1,8]{1,0:T(1,128)}, u32[]{:S(2)}) copy-start(s32[1,8]{1,0:T(1,128)} %col_ref.5) | copy-start | bytes 100
  15.3 5.5 %collective-permute-start.3 = (f32[6,64,128]{2,1,0:T(8,128)S(1)}, f32[6,64,128]{2,1,0:T(8,128)S(1)}, u32[]{:S(2)}, u32[]{:S(2)}) collective-permute-start(f32[6,64,128]{2,1,0:T(8,128)S(1)} %get-tuple-element.41), channel_id=1, source_target_pairs={{0,1},{1,0},{2,3},{3,2},{4,5},{5,4},{6,7},{7,6},{8,9},{9,8},{10,11... | collective-permute-start | bytes 589832 | tf_op jit(solution)/shard_map/ppermute | solution.py:359
  16.2 4.6 %copy-start.3 = (f32[1,8,128,128]{3,2,1,0:T(8,128)S(1)}, f32[1,8,128,128]{3,2,1,0:T(8,128)}, u32[]{:S(2)}) copy-start(f32[1,8,128,128]{3,2,1,0:T(8,128)} %param.9) | copy-start | bytes 1572868
  26.6 1.9 %collective-permute-start.8 = (f32[128,128]{1,0:T(8,128)S(1)}, f32[128,128]{1,0:T(8,128)S(1)}, u32[]{:S(2)}, u32[]{:S(2)}) collective-permute-start(f32[128,128]{1,0:T(8,128)S(1)} %get-tuple-element.52), channel_id=1, source_target_pairs={{0,1},{1,0},{2,3},{3,2},{4,5},{5,4},{6,7},{7,6},{8,9},{9,8},{10,11... | collective-permute-start | bytes 196616 | tf_op jit(solution)/shard_map/ppermute | solution.py:372
  28.6 6.8 %collective-permute-start.9 = (f32[128,128]{1,0:T(8,128)S(1)}, f32[128,128]{1,0:T(8,128)S(1)}, u32[]{:S(2)}, u32[]{:S(2)}) collective-permute-start(f32[128,128]{1,0:T(8,128)S(1)} %add.27), channel_id=1, source_target_pairs={{0,16},{1,33},{2,18},{3,35},{4,20},{5,37},{6,22},{7,39},{8,24},{9,... | collective-permute-start | bytes 196616 | tf_op jit(solution)/shard_map/ppermute | solution.py:372
  35.4 5.4 %collective-permute-start.10 = (f32[128,128]{1,0:T(8,128)S(1)}, f32[128,128]{1,0:T(8,128)S(1)}, u32[]{:S(2)}, u32[]{:S(2)}) collective-permute-start(f32[128,128]{1,0:T(8,128)S(1)} %add.28), channel_id=1, source_target_pairs={{0,4},{1,13},{2,6},{3,15},{4,0},{5,9},{6,2},{7,11},{8,12},{9,5},{1... | collective-permute-start | bytes 196616 | tf_op jit(solution)/shard_map/ppermute | solution.py:372
  39.1 16.7 %collective-permute-start.16 = (f32[2,6,64,128]{3,2,1,0:T(8,128)S(1)}, f32[2,6,64,128]{3,2,1,0:T(8,128)S(1)}, u32[]{:S(2)}, u32[]{:S(2)}) collective-permute-start(f32[2,6,64,128]{3,2,1,0:T(8,128)S(1)} %get-tuple-element.58), channel_id=1, source_target_pairs={{0,1},{1,0},{2,3},{3,2},{4,5},{5,4},{6,7},{7,6},{8,9},{9,8},{10,11... | collective-permute-start | bytes 1179656 | tf_op jit(solution)/shard_map/ppermute | solution.py:359
  40.8 15.0 %collective-permute-start.15 = (f32[2,6,64,128]{3,2,1,0:T(8,128)S(1)}, f32[2,6,64,128]{3,2,1,0:T(8,128)S(1)}, u32[]{:S(2)}, u32[]{:S(2)}) collective-permute-start(f32[2,6,64,128]{3,2,1,0:T(8,128)S(1)} %get-tuple-element.57), channel_id=1, source_target_pairs={{0,16},{1,17},{2,18},{3,19},{4,20},{5,21},{6,22},{7,23},{8,24},{9,... | collective-permute-start | bytes 1179656 | tf_op jit(solution)/shard_map/ppermute | solution.py:359
  43.0 3.4 %collective-permute-start.11 = (f32[128,128]{1,0:T(8,128)S(1)}, f32[128,128]{1,0:T(8,128)S(1)}, u32[]{:S(2)}, u32[]{:S(2)}) collective-permute-start(f32[128,128]{1,0:T(8,128)S(1)} %add.29), channel_id=1, source_target_pairs={{0,12},{1,5},{2,14},{3,7},{4,8},{5,1},{6,10},{7,3},{8,4},{9,13},{1... | collective-permute-start | bytes 196616 | tf_op jit(solution)/shard_map/ppermute | solution.py:372
  46.4 9.4 %collective-permute-start.14 = (f32[128,128]{1,0:T(8,128)S(1)}, f32[128,128]{1,0:T(8,128)S(1)}, u32[]{:S(2)}, u32[]{:S(2)}) collective-permute-start(f32[128,128]{1,0:T(8,128)S(1)} %add.30), channel_id=1, source_target_pairs={{0,2},{1,3},{2,0},{3,1},{4,6},{5,7},{6,4},{7,5},{8,10},{9,11},{10,... | collective-permute-start | bytes 196616 | tf_op jit(solution)/shard_map/ppermute | solution.py:372
  48.6 7.2 %collective-permute-start.13 = (f32[128,128]{1,0:T(8,128)S(1)}, f32[128,128]{1,0:T(8,128)S(1)}, u32[]{:S(2)}, u32[]{:S(2)}) collective-permute-start(f32[128,128]{1,0:T(8,128)S(1)} %add.30), channel_id=1, source_target_pairs={{0,130},{1,129},{2,128},{3,131},{4,134},{5,133},{6,132},{7,135},{8... | collective-permute-start | bytes 196616 | tf_op jit(solution)/shard_map/ppermute | solution.py:372
  49.7 6.1 %collective-permute-start.12 = (f32[128,128]{1,0:T(8,128)S(1)}, f32[128,128]{1,0:T(8,128)S(1)}, u32[]{:S(2)}, u32[]{:S(2)}) collective-permute-start(f32[128,128]{1,0:T(8,128)S(1)} %add.30), channel_id=1, source_target_pairs={{0,128},{1,131},{2,130},{3,129},{4,132},{5,135},{6,134},{7,133},{8... | collective-permute-start | bytes 196616 | tf_op jit(solution)/shard_map/ppermute | solution.py:372
  55.9 5.5 %collective-permute-start.17 = (f32[128,128]{1,0:T(8,128)S(1)}, f32[128,128]{1,0:T(8,128)S(1)}, u32[]{:S(2)}, u32[]{:S(2)}) collective-permute-start(f32[128,128]{1,0:T(8,128)S(1)} %add_add_fusion), channel_id=1, source_target_pairs={{0,32},{1,97},{2,34},{3,99},{4,36},{5,101},{6,38},{7,103},{8,40},{... | collective-permute-start | bytes 196616 | tf_op jit(solution)/shard_map/ppermute | solution.py:372
  57.7 10.3 %collective-permute-start.19 = (f32[2,256,128]{2,1,0:T(8,128)S(1)}, f32[2,256,128]{2,1,0:T(8,128)S(1)}, u32[]{:S(2)}, u32[]{:S(2)}) collective-permute-start(f32[2,256,128]{2,1,0:T(8,128)S(1)} %get-tuple-element.69), channel_id=1, source_target_pairs={{0,16},{1,2},{2,1},{3,4},{4,3},{5,6},{6,5},{7,8},{8,7},{9,10},{10,... | collective-permute-start | bytes 786440 | tf_op jit(solution)/shard_map/ppermute | solution.py:359
  61.4 6.7 %collective-permute-start.20 = (f32[2,256,128]{2,1,0:T(8,128)S(1)}, f32[2,256,128]{2,1,0:T(8,128)S(1)}, u32[]{:S(2)}, u32[]{:S(2)}) collective-permute-start(f32[2,256,128]{2,1,0:T(8,128)S(1)} %get-tuple-element.70), channel_id=1, source_target_pairs={{0,1},{1,0},{2,3},{3,2},{4,5},{5,4},{6,7},{7,6},{8,9},{9,8},{10,11... | collective-permute-start | bytes 786440 | tf_op jit(solution)/shard_map/ppermute | solution.py:359
  64.9 3.2 %collective-permute-start.18 = (f32[128,128]{1,0:T(8,128)S(1)}, f32[128,128]{1,0:T(8,128)S(1)}, u32[]{:S(2)}, u32[]{:S(2)}) collective-permute-start(f32[128,128]{1,0:T(8,128)S(1)} %add.34), channel_id=1, source_target_pairs={{0,96},{1,17},{2,98},{3,19},{4,100},{5,21},{6,102},{7,23},{8,104},... | collective-permute-start | bytes 196616 | tf_op jit(solution)/shard_map/ppermute | solution.py:372
  68.1 4.9 %collective-permute-start.21 = (f32[128,128]{1,0:T(8,128)S(1)}, f32[128,128]{1,0:T(8,128)S(1)}, u32[]{:S(2)}, u32[]{:S(2)}) collective-permute-start(f32[128,128]{1,0:T(8,128)S(1)} %add.35.mine_ref), channel_id=1, source_target_pairs={{0,1},{1,0},{2,3},{3,2},{4,5},{5,4},{6,7},{7,6},{8,9},{9,8},{10,11... | collective-permute-start | bytes 196616 | tf_op jit(solution)/shard_map/ppermute | solution.py:372
